TPU v7x, 32 devices: a whole 2x2x4 slice. The times are simulated.
32 devices in a mesh: pair: 8 (over z, x), row: 4 (over y, core).
Axes of the slice: x: 2, y: 2, z: 4, core: 2. Of those that a mesh axis runs over, the one named last changes fastest.
Arguments:
- sector: float32 [8192, 2048], P('row', 'pair'), may hold values from -1.767767 to 1.767767
- block_label: int32 [16], replicated, may hold values from 0 to 15, each once
Outputs:
- rotated: float32 [8192, 2048], P('row', 'pair')
- vectors: float32 [2048, 2048], P('row', 'pair')
- singular: float32 [2048], P('pair')
Inputs may be any that keep to these rules, and one draw needn't show every extreme that they name: `block_label`: each block number appears once.
All inputs are finite; a program needn't handle non-finite values.
Results may differ from a plain program's by a relative error of at most 0.0003.
Values sent between devices are 32-bit elements; how exact they have to be, the bound alone decides.
No kernel may reach another device: no remote copies, remote signals or barrier semaphores. Data moves between devices by JAX's collectives and lax.ppermute only.
A program may use at most 64 MiB of HBM per device.

v0:
```python
import jax
import jax.numpy as jnp
from jax import lax
from jax.sharding import PartitionSpec as P

ROUNDS = 4
NEWTON = 16


highest = lax.Precision.HIGHEST


def from_behind(block, axis, distance):
    devices = range(lax.axis_size(axis))
    route = [(i - distance, i) for i in devices if i - distance in devices]
    return lax.ppermute(block, axis, route)


def rotation_of(gram_matrix):
    size_two = gram_matrix.shape[0]
    diagonal = jnp.diagonal(gram_matrix)
    spread = diagonal[None, :] - diagonal[:, None]
    summed = diagonal[None, :] + diagonal[:, None]
    skewed = (
        gram_matrix
        * spread
        / (spread * spread + 2.0 * gram_matrix * gram_matrix + 0.01 * summed * summed)
    )
    identity = jnp.eye(size_two, dtype=jnp.float32)
    half_step = identity + 0.5 * skewed
    system = identity - 0.25 * jnp.dot(skewed, skewed, precision=highest)
    bound = 1.0 + 0.25 * jnp.sum(skewed * skewed)
    inverse = 2.0 / (1.0 + bound) * identity
    for newton_step in range(NEWTON):
        inverse = jnp.dot(
            inverse, 2.0 * identity - jnp.dot(system, inverse, precision=highest), precision=highest
        )
    return jnp.dot(inverse, jnp.dot(half_step, half_step, precision=highest), precision=highest)


def send_leftward(moving):
    return from_behind(moving, "pair", -1)


def send_rightward(moving):
    return from_behind(moving, "pair", 1)


def per_device(sector, block_label):
    local_rows = sector.shape[0]
    width_pair = sector.shape[1]
    half_width = width_pair // 2
    pair_count = lax.axis_size("pair")
    position = lax.axis_index("pair")
    row_index = lax.axis_index("row")
    vector_rows = pair_count * width_pair // lax.axis_size("row")
    labels = lax.dynamic_slice_in_dim(block_label, 2 * position, 2)
    targets = (
        labels[:, None] * half_width + jnp.arange(half_width, dtype=jnp.int32)[None, :]
    ).reshape(width_pair)
    row_ids = row_index * vector_rows + jnp.arange(vector_rows, dtype=jnp.int32)
    vectors = (row_ids[:, None] == targets[None, :]).astype(jnp.float32)
    stacked = jnp.concatenate([sector, vectors], 0)
    is_first = position == 0
    is_last = position == pair_count - 1
    for sweep_round in range(ROUNDS):
        columns = stacked[:local_rows]
        gram_matrix = lax.psum(jnp.dot(columns.T, columns, precision=highest), "row")
        rotation = rotation_of(gram_matrix)
        if sweep_round == ROUNDS - 1:
            stacked = jnp.dot(stacked, rotation, precision=highest)
        else:
            turned = jnp.dot(stacked, rotation, precision=highest)
            upper_half = turned[:, :half_width]
            lower_half = turned[:, half_width:]
            from_right = send_leftward(lower_half)
            from_left = send_rightward(jnp.where(is_first, lower_half, upper_half))
            new_upper = jnp.where(is_first, upper_half, from_left)
            new_lower = jnp.where(is_last, upper_half, from_right)
            stacked = jnp.concatenate([new_upper, new_lower], 1)
    rotated = stacked[:local_rows]
    vectors_out = stacked[local_rows:]
    squares = lax.psum(jnp.sum(rotated * rotated, axis=0), "row")
    singular = jnp.sqrt(squares + 1e-06)
    return (rotated, vectors_out, singular)


def solution(mesh):
    placed = (P("row", "pair"), P())
    return jax.shard_map(
        per_device,
        mesh=mesh,
        in_specs=placed,
        out_specs=(P("row", "pair"), P("row", "pair"), P("pair")),
        check_vma=False,
    )
```

profile of v0, /device:TPU:0, one launch (start us, length us, event | category | flops | bytes accessed | tf_op | source)
XLA Modules:
  0.0 438.3 jit_solution(17083182142614953925)
XLA Ops:
  7.2 6.4 %fusion.107 = f32[256,256]{1,0:T(8,128)} fusion(f32[2048,256]{1,0:T(8,128)} %param.2), kind=kOutput, calls=%fused_computation.216 | convolution fusion | flops 1610612736 | bytes 2359296 | tf_op jit(solution)/shard_map/dot_general | solution.py:68
  14.2 34.3 %all-reduce.5.cloned.1.call-done = f32[256,256]{1,0:T(8,128)} async-done(((f32[256,256]{1,0:T(8,128)}), f32[256,256]{1,0:T(8,128)}) %all-reduce.5.cloned.1.call-update) | async-done | bytes 262160 | tf_op jit(solution)/shard_map/psum | solution.py:68
  48.5 2.6 gather_fusion
  51.1 0.8 multiply_reduce_fusion.4
  66.8 2.6 fusion
  69.4 1.7 slice_select_fusion.8
  71.1 4.4 %collective-permute-start = (f32[2560,128]{0,1:T(8,128)}, f32[2560,128]{0,1:T(8,128)}, u32[]{:S(2)}, u32[]{:S(2)}) collective-permute-start(f32[2560,128]{0,1:T(8,128)} %get-tuple-element.23), channel_id=1, source_target_pairs={{0,4},{4,8},{8,12},{12,16},{16,20},{20,24},{24,28},{1,5},{5,9},{9,... | collective-permute-start | bytes 3932168 | tf_op jit(solution)/shard_map/ppermute | solution.py:16
  75.6 1.3 collective-permute-start.1
  76.9 52.9 %collective-permute-done = f32[2560,128]{0,1:T(8,128)} collective-permute-done((f32[2560,128]{0,1:T(8,128)}, f32[2560,128]{0,1:T(8,128)}, u32[]{:S(2)}, u32[]{:S(2)}) %collective-permute-start) | collective-permute-done | bytes 1310752 | tf_op jit(solution)/shard_map/ppermute | solution.py:16
  129.8 1.7 slice_select_fusion.7
  131.5 1.1 copy-done.1
  133.0 2.6 fusion.24
  136.1 33.4 %all-reduce.7.cloned.1.call-done = f32[256,256]{1,0:T(8,128)} async-done(((f32[256,256]{1,0:T(8,128)}), f32[256,256]{1,0:T(8,128)}) %all-reduce.7.cloned.1.call-update) | async-done | bytes 262160 | tf_op jit(solution)/shard_map/psum | solution.py:68
  169.5 2.6 gather_fusion.1
  187.6 2.6 fusion.4
  190.4 3.5 collective-permute-start.2
  193.9 1.3 collective-permute-start.3
  195.2 53.6 %collective-permute-done.2 = f32[2560,128]{0,1:T(8,128)S(1)} collective-permute-done((f32[2560,128]{0,1:T(8,128)S(1)}, f32[2560,128]{0,1:T(8,128)S(1)}, u32[]{:S(2)}, u32[]{:S(2)}) %collective-permute-start.2) | collective-permute-done | bytes 1310752 | tf_op jit(solution)/shard_map/ppermute | solution.py:16
  249.0 2.6 fusion.20
  252.1 33.0 %all-reduce.9.cloned.1.call-done = f32[256,256]{1,0:T(8,128)} async-done(((f32[256,256]{1,0:T(8,128)}), f32[256,256]{1,0:T(8,128)}) %all-reduce.9.cloned.1.call-update) | async-done | bytes 262160 | tf_op jit(solution)/shard_map/psum | solution.py:68
  285.0 2.6 gather_fusion.2
  302.9 2.6 fusion.8
  305.7 3.5 collective-permute-start.4
  309.2 1.3 collective-permute-start.5
  310.5 53.6 %collective-permute-done.4 = f32[2560,128]{0,1:T(8,128)S(1)} collective-permute-done((f32[2560,128]{0,1:T(8,128)S(1)}, f32[2560,128]{0,1:T(8,128)S(1)}, u32[]{:S(2)}, u32[]{:S(2)}) %collective-permute-start.4) | collective-permute-done | bytes 1310752 | tf_op jit(solution)/shard_map/ppermute | solution.py:16
  364.3 2.6 fusion.16
  366.9 33.4 %all-reduce.11.cloned.1.call-done = f32[256,256]{1,0:T(8,128)} async-done(((f32[256,256]{1,0:T(8,128)}), f32[256,256]{1,0:T(8,128)}) %all-reduce.11.cloned.1.call-update) | async-done | bytes 262160 | tf_op jit(solution)/shard_map/psum | solution.py:68
  400.4 2.6 gather_fusion.3
  418.2 4.6 %fusion.12 = f32[2560,256]{1,0:T(8,128)S(1)} fusion(f32[256,256]{1,0:T(8,128)S(1)} %fusion.171, f32[2560,128]{0,1:T(8,128)S(1)} %get-tuple-element.14, f32[2560,128]{0,1:T(8,128)S(1)} %get-tuple-element.13), kind=kOutput, calls=%fused_computation.80 | convolution fusion | flops 2013921280 | bytes 5505024 | tf_op jit(solution)/shard_map/dot_general | solution.py:71
  422.8 0.8 slice.59
  423.6 1.6 multiply_reduce_fusion
  425.2 5.7 %psum.39 = f32[256]{0:T(256)S(1)} all-reduce(f32[256]{0:T(256)S(1)} %get-tuple-element.3), channel_id=1, replica_groups=mesh['pair'=8,'row'=4] {'row'}, use_global_device_ids=true, to_apply=%region_9.10 | all-reduce | flops 256 | bytes 2048 | tf_op jit(solution)/shard_map/psum | solution.py:83
  (183 shorter events, 60.3 us)
Async XLA Ops:
  7.2 6.7 %copy-start.9 = (s32[16]{0:T(128)S(1)}, s32[16]{0:T(128)}, u32[]{:S(2)}) copy-start(s32[16]{0:T(128)} %param.3) | copy-start | bytes 196
  7.2 41.3 %all-reduce.5.cloned.1.call-start = ((), (), s32[]{:S(2)}) async-start(), calls=%async_computation | async-start | bytes 524288 | tf_op jit(solution)/shard_map/psum | solution.py:68
  13.6 155.8 %all-reduce.7.cloned.1.call-start = ((), (), s32[]{:S(2)}) async-start(), calls=%async_computation.1 | async-start | bytes 524288 | tf_op jit(solution)/shard_map/psum | solution.py:68
  48.5 2.6 copy-start.5
  65.2 1.6 copy-start
  71.1 58.7 %collective-permute-start = (f32[2560,128]{0,1:T(8,128)}, f32[2560,128]{0,1:T(8,128)}, u32[]{:S(2)}, u32[]{:S(2)}) collective-permute-start(f32[2560,128]{0,1:T(8,128)} %get-tuple-element.23), channel_id=1, source_target_pairs={{0,4},{4,8},{8,12},{12,16},{16,20},{20,24},{24,28},{1,5},{5,9},{9,... | collective-permute-start | bytes 3932168 | tf_op jit(solution)/shard_map/ppermute | solution.py:16
  75.6 54.2 %collective-permute-start.1 = (f32[2560,128]{0,1:T(8,128)}, f32[2560,128]{0,1:T(8,128)}, u32[]{:S(2)}, u32[]{:S(2)}) collective-permute-start(f32[2560,128]{0,1:T(8,128)} %get-tuple-element.24), channel_id=1, source_target_pairs={{4,0},{8,4},{12,8},{16,12},{20,16},{24,20},{28,24},{5,1},{9,5},{13... | collective-permute-start | bytes 3932168 | tf_op jit(solution)/shard_map/ppermute | solution.py:16
  131.5 1.1 copy-start.1
  131.5 1.5 copy-start.3
  135.6 149.4 %all-reduce.9.cloned.1.call-start = ((), (), s32[]{:S(2)}) async-start(), calls=%async_computation.2 | async-start | bytes 524288 | tf_op jit(solution)/shard_map/psum | solution.py:68
  169.5 2.6 copy-start.6
  185.8 1.6 copy-start.4
  186.2 1.4 copy-start.2
  190.4 58.4 %collective-permute-start.2 = (f32[2560,128]{0,1:T(8,128)S(1)}, f32[2560,128]{0,1:T(8,128)S(1)}, u32[]{:S(2)}, u32[]{:S(2)}) collective-permute-start(f32[2560,128]{0,1:T(8,128)S(1)} %get-tuple-element.19), channel_id=1, source_target_pairs={{0,4},{4,8},{8,12},{12,16},{16,20},{20,24},{24,28},{1,5},{5,9},{9,... | collective-permute-start | bytes 3932168 | tf_op jit(solution)/shard_map/ppermute | solution.py:16
  193.9 54.9 %collective-permute-start.3 = (f32[2560,128]{0,1:T(8,128)S(1)}, f32[2560,128]{0,1:T(8,128)S(1)}, u32[]{:S(2)}, u32[]{:S(2)}) collective-permute-start(f32[2560,128]{0,1:T(8,128)S(1)} %get-tuple-element.20), channel_id=1, source_target_pairs={{4,0},{8,4},{12,8},{16,12},{20,16},{24,20},{28,24},{5,1},{9,5},{13... | collective-permute-start | bytes 3932168 | tf_op jit(solution)/shard_map/ppermute | solution.py:16
  251.6 148.8 %all-reduce.11.cloned.1.call-start = ((), (), s32[]{:S(2)}) async-start(), calls=%async_computation.3 | async-start | bytes 524288 | tf_op jit(solution)/shard_map/psum | solution.py:68
  285.0 2.6 copy-start.7
  305.7 58.4 %collective-permute-start.4 = (f32[2560,128]{0,1:T(8,128)S(1)}, f32[2560,128]{0,1:T(8,128)S(1)}, u32[]{:S(2)}, u32[]{:S(2)}) collective-permute-start(f32[2560,128]{0,1:T(8,128)S(1)} %get-tuple-element.15), channel_id=1, source_target_pairs={{0,4},{4,8},{8,12},{12,16},{16,20},{20,24},{24,28},{1,5},{5,9},{9,... | collective-permute-start | bytes 3932168 | tf_op jit(solution)/shard_map/ppermute | solution.py:16
  309.2 54.9 %collective-permute-start.5 = (f32[2560,128]{0,1:T(8,128)S(1)}, f32[2560,128]{0,1:T(8,128)S(1)}, u32[]{:S(2)}, u32[]{:S(2)}) collective-permute-start(f32[2560,128]{0,1:T(8,128)S(1)} %get-tuple-element.16), channel_id=1, source_target_pairs={{4,0},{8,4},{12,8},{16,12},{20,16},{24,20},{28,24},{5,1},{9,5},{13... | collective-permute-start | bytes 3932168 | tf_op jit(solution)/shard_map/ppermute | solution.py:16
  400.4 2.6 copy-start.8
Sparse Core Ops, SparseCore 0:
  13.8 34.6 all-reduce.4
  135.7 33.6 all-reduce.6
  251.7 33.2 all-reduce.8
  367.0 33.2 all-reduce.10
where the time goes:
time: 442 us; the launch traced here: 438 us
  waiting for transfers between devices  294 us (67%)
  matrix products  80.3 us (18%)
  between operations  18.1 us (4%)
  starting transfers between devices  16.4 us (4%)
  local copies, waits for them, and re-layouts  13.6 us (3%)
  other arithmetic  9.97 us (2%)
  blocking collectives  5.73 us (1%)
    ppermute x6, waiting for transfers between devices, from_behind(): return lax.ppermute(block, axis, route)  160 us
    psum x4, waiting for transfers between devices, per_device(): lax.psum(jnp.dot(columns.T, columns, precision=highest), 'row')  134 us
    dot_general x64, matrix products, rotation_of(): jnp.dot(inverse, 2.0 * identity - jnp.dot(system, inverse, precision=high...  24.9 us
    dot_general x64, matrix products, rotation_of(): jnp.dot(system, inverse, precision=highest)  24.2 us
    ppermute x6, starting transfers between devices, from_behind(): return lax.ppermute(block, axis, route)  15.2 us
    dot_general x4, matrix products, per_device(): jnp.dot(columns.T, columns, precision=highest)  14.1 us
    gather x4, local copies, waits for them, and re-layouts, rotation_of(): diagonal = jnp.diagonal(gram_matrix)  10.5 us
  transfers between devices with their start and end apart: 10, of which 7 were waited for; matrix products, arithmetic and copies ran while one was open for 0% of the time, Pallas kernels for 0%

commit v1 on v0

v1 whole, which is shorter than its diff:
```python
import jax
import jax.numpy as jnp
from jax import lax
from jax.experimental import pallas as pl
from jax.experimental.pallas import tpu as pltpu
from jax.sharding import PartitionSpec as P

ROUNDS = 4
NEWTON = 16

highest = lax.Precision.HIGHEST

TARGET = 2.0**-12
BOUNDS = [
    (1.0 + TARGET ** (2.0**-j)) / (1.0 - TARGET ** (2.0**-j)) for j in range(NEWTON)
]

X, CORE, FIRST, LAST, VROW, LABEL = 0, 1, 2, 3, 4, 5


def dot(a, b, precision=highest):
    return lax.dot_general(
        a, b, (((1,), (0,)), ((), ())), precision=precision,
        preferred_element_type=jnp.float32,
    )


def dot_tn(a, b):
    return lax.dot_general(
        a, b, (((0,), (0,)), ((), ())), precision=highest,
        preferred_element_type=jnp.float32,
    )


def shape(*dims):
    return jax.ShapeDtypeStruct(dims, jnp.float32)


def call(body, facts, inputs, outs, scratch=(), limit=24):
    return pl.pallas_call(
        body,
        out_shape=outs,
        in_specs=[pl.BlockSpec(memory_space=pltpu.SMEM)]
        + [pl.BlockSpec(memory_space=pltpu.VMEM)] * len(inputs),
        out_specs=jax.tree.map(
            lambda _: pl.BlockSpec(memory_space=pltpu.VMEM), outs
        ),
        scratch_shapes=list(scratch),
        compiler_params=pltpu.CompilerParams(vmem_limit_bytes=limit << 20),
    )(facts, *inputs)


def first_gram(facts, sector, half):
    rows, width = sector.shape

    def body(f, x_ref, out_ref):
        x = x_ref[...]
        g = dot_tn(x, x)
        out_ref[:half] = g[:half, :half]
        out_ref[half : 2 * half] = g[:half, half:]
        out_ref[2 * half :] = g[half:, half:]

    return call(body, facts, [sector], shape(3 * half, half))


def rotate_of(gram, x_ref, e_ref):
    size = gram.shape[0]
    half = size // 2
    rows = lax.broadcasted_iota(jnp.int32, (size, size), 0)
    cols = lax.broadcasted_iota(jnp.int32, (size, size), 1)
    identity = (rows == cols).astype(jnp.float32)
    only = jnp.where(rows == cols, gram, 0.0)
    g_j = jnp.sum(only, axis=0, keepdims=True)
    g_i = jnp.sum(only, axis=1, keepdims=True)
    spread = g_j - g_i
    summed = g_j + g_i
    skew = gram * spread / (spread * spread + 2.0 * gram * gram + 0.01 * summed * summed)
    bound = 1.0 + 0.25 * jnp.sum(skew * skew)
    steps = jnp.int32(0)
    for limit in BOUNDS:
        steps = steps + (bound > limit).astype(jnp.int32)
    scale = 2.0 / (1.0 + jnp.full((size, size), bound, jnp.float32))
    system = identity - 0.25 * dot(skew, skew)
    residual = identity - scale * system
    x_ref[...] = scale * (identity + residual)
    e_ref[...] = dot(residual, residual)

    def step(_, carry):
        e = e_ref[...]
        x = x_ref[...]
        x_ref[...] = x + dot(x, e)
        e_ref[...] = dot(e, e)
        return carry

    lax.fori_loop(0, jnp.maximum(steps - 1, 0), step, jnp.int32(0))
    x = x_ref[...]
    half_inverse = x + 0.5 * dot(x, skew)
    missing = half_inverse - 0.5 * dot(skew, half_inverse)
    half_inverse = half_inverse + (half_inverse - dot(half_inverse, missing))
    rotation = 2.0 * half_inverse - identity
    turned = dot(gram, rotation)
    upper = dot_tn(rotation[:, :half], turned[:, :half])
    lower = dot_tn(rotation[:, half:], turned[:, half:])
    return rotation, upper, lower


def put_pack(pack_ref, rotation, upper, lower):
    size = rotation.shape[0]
    half = size // 2
    pack_ref[:size] = rotation
    pack_ref[size:, :half] = upper
    pack_ref[size:, half:] = lower


def first_rotation(facts, own, near, far, half):
    size = 2 * half

    def body(f, own_ref, near_ref, far_ref, pack_ref, g_ref, x_ref, e_ref):
        mine = f[X] == f[CORE]
        total = near_ref[...] + jnp.where(mine, own_ref[...], far_ref[...])
        g_ref[:half, :half] = total[:half]
        g_ref[:half, half:] = total[half : 2 * half]
        g_ref[half:, :half] = total[half : 2 * half].T
        g_ref[half:, half:] = total[2 * half :]
        put_pack(pack_ref, *rotate_of(g_ref[...], x_ref, e_ref))

    square = pltpu.VMEM((size, size), jnp.float32)
    return call(
        body, facts, [own, near, far], shape(3 * half, size), [square] * 3
    )


def later_rotation(facts, parts, tails, half):
    size = 2 * half
    top = tails[0].shape[0] - half

    def body(f, *refs):
        own, other_y, other_x, other_xy = [r[...] for r in refs[:4]]
        from_left, kept_left, nat_l, nat_u, from_right, kept_right = [
            r[top:] for r in refs[4:10]
        ]
        pack_ref, g_ref, x_ref, e_ref = refs[10:]
        cross = (own + other_y) + (other_x + other_xy)
        first, last, core = f[FIRST] == 1, f[LAST] == 1, f[CORE] == 0
        up_0 = jnp.where(first, kept_left, from_left)
        low_1 = jnp.where(last, kept_right, from_right)
        g_ref[:half, :half] = jnp.where(core, up_0, nat_u)
        g_ref[:half, half:] = cross
        g_ref[half:, :half] = cross.T
        g_ref[half:, half:] = jnp.where(core, nat_l, low_1)
        put_pack(pack_ref, *rotate_of(g_ref[...], x_ref, e_ref))

    square = pltpu.VMEM((size, size), jnp.float32)
    return call(
        body, facts, parts + tails, shape(3 * half, size), [square] * 3
    )


def two_packs(f, own, other):
    core = f[CORE] == 0
    return jnp.where(core, own, other), jnp.where(core, other, own)


def swapped(flag, matrix, axis):
    half = matrix.shape[axis] // 2
    a = lax.slice_in_dim(matrix, 0, half, axis=axis)
    b = lax.slice_in_dim(matrix, half, 2 * half, axis=axis)
    return jnp.where(flag, lax.concatenate([b, a], axis), matrix)


def blocks_of(f, refs, rows=None):
    vals = [r[...] if rows is None else r[:rows] for r in refs]
    from_left, kept_left, nat_l, nat_u, from_right, kept_right = vals
    up_0 = jnp.where(f[FIRST] == 1, kept_left, from_left)
    low_1 = jnp.where(f[LAST] == 1, kept_right, from_right)
    return up_0, nat_l, nat_u, low_1


def put_turned(f, refs, zero, one, half, swap_natives):
    to_left_ref, nat_l_ref, nat_u_ref, to_right_ref = refs
    to_left_ref[...] = zero[:, half:]
    to_right_ref[...] = one[:, :half]
    nat_u, nat_l = zero[:, :half], one[:, half:]
    if swap_natives:
        even = f[X] == 0
        nat_l, nat_u = jnp.where(even, nat_l, nat_u), jnp.where(even, nat_u, nat_l)
    nat_l_ref[...] = nat_l
    nat_u_ref[...] = nat_u


def turn(facts, packs, kept, got, blocks, half, swap_natives):
    size = 2 * half
    first_round = blocks is None
    inputs = packs + ([kept, got] if first_round else blocks)
    rows = kept.shape[0] if first_round else blocks[0].shape[0]

    def body(f, *refs):
        own, other = refs[0][:size], refs[1][:size]
        turn_0, turn_1 = two_packs(f, own, other)
        turn_0 = swapped(f[FIRST] == 1, turn_0, 1)
        outs = refs[2 + len(inputs) - 2 :]
        if first_round:
            even = f[X] == 0
            mine, theirs = refs[2][...], refs[3][...]
            zero, one = jnp.where(even, mine, theirs), jnp.where(even, theirs, mine)
        else:
            up_0, low_0, up_1, low_1 = blocks_of(f, refs[2:8])
            zero = lax.concatenate([up_0, low_0], 1)
            one = lax.concatenate([up_1, low_1], 1)
        put_turned(f, outs, dot(zero, turn_0), dot(one, turn_1), half, swap_natives)

    return call(body, facts, inputs, (shape(rows, half),) * 4)


def turn_tail(facts, packs, tails, vector_rows, half):
    size = 2 * half
    inputs = packs + (tails or [])

    def body(f, *refs):
        own, other = refs[0][...], refs[1][...]
        pack_0, pack_1 = two_packs(f, own, other)
        pack_0 = swapped(f[FIRST] == 1, pack_0, 1)
        outs = refs[len(inputs) :]
        if tails is None:
            rows = f[VROW] + lax.broadcasted_iota(jnp.int32, (vector_rows, half), 0)
            cols = lax.broadcasted_iota(jnp.int32, (vector_rows, half), 1)
            up_0, low_0, up_1, low_1 = [
                (rows == f[LABEL + k] * half + cols).astype(jnp.float32)
                for k in range(4)
            ]
        else:
            up_0, low_0, up_1, low_1 = blocks_of(f, refs[2:8], vector_rows)
        zero = dot(lax.concatenate([up_0, low_0], 1), pack_0[:size])
        one = dot(lax.concatenate([up_1, low_1], 1), pack_1[:size])
        to_left_ref, nat_l_ref, nat_u_ref, to_right_ref = outs
        for ref, matrix, pack, at in (
            (to_left_ref, zero, pack_0, half),
            (nat_l_ref, one, pack_1, half),
            (nat_u_ref, zero, pack_0, 0),
            (to_right_ref, one, pack_1, 0),
        ):
            ref[:vector_rows] = matrix[:, at : at + half]
            ref[vector_rows:] = pack[size:, at : at + half]

    return call(body, facts, inputs, (shape(vector_rows + half, half),) * 4)


def cross_gram(facts, blocks, half, last_round):
    rows = blocks[0].shape[0]

    def body(f, *refs):
        outs = refs[6:]
        vals = blocks_of(f, refs[:6])
        up_0, low_0, up_1, low_1 = vals
        if last_round:
            even = f[X] == 0
            low_0, up_1 = jnp.where(even, low_0, up_1), jnp.where(even, up_1, low_0)
            outs[2][...] = jnp.where(even, up_0, low_1)
            outs[3][...] = jnp.where(even, low_1, up_0)
        zero, one = dot_tn(up_0, low_0), dot_tn(up_1, low_1)
        core = f[CORE] == 0
        outs[0][...] = jnp.where(core, zero, one)
        outs[1][...] = jnp.where(core, one, zero)

    outs = (shape(half, half),) * 2
    if last_round:
        outs = outs + (shape(rows, half),) * 2
    return call(body, facts, blocks, outs)


def split_vectors(facts, tails, vector_rows, half):
    def body(f, *refs):
        up_0, low_0, up_1, low_1 = blocks_of(f, refs[:6], vector_rows)
        even = f[X] == 0
        keep_ref, send_ref = refs[6:]
        keep_ref[:, :half] = jnp.where(even, up_0, up_1)
        keep_ref[:, half:] = jnp.where(even, low_0, low_1)
        send_ref[:, :half] = jnp.where(even, up_1, up_0)
        send_ref[:, half:] = jnp.where(even, low_1, low_0)

    return call(body, facts, tails, (shape(vector_rows, 2 * half),) * 2)


def finish(facts, packs, moved, native, vectors, half):
    size = 2 * half
    part = moved[0].shape[0]
    vector_part = vectors[0].shape[0]

    def body(f, *refs):
        x = f[X]
        mine = f[CORE] == x
        pack = jnp.where(mine, refs[0][...], refs[1][...])
        rotation = pack[:size]
        turned = swapped(x == 1, rotation, 0)
        moved_keep, moved_got, native_keep, native_got, v_keep, v_got = refs[2:8]
        out_ref, vectors_ref, singular_ref = refs[8:]
        here = pl.multiple_of(x * part, part)
        there = pl.multiple_of((1 - x) * part, part)
        out_ref[pl.ds(here, part)] = dot(
            lax.concatenate([moved_keep[...], native_keep[...]], 1), turned
        )
        out_ref[pl.ds(there, part)] = dot(
            lax.concatenate([moved_got[...], native_got[...]], 1), turned
        )
        here = pl.multiple_of(x * vector_part, vector_part)
        there = pl.multiple_of((1 - x) * vector_part, vector_part)
        vectors_ref[pl.ds(here, vector_part)] = dot(v_keep[...], rotation)
        vectors_ref[pl.ds(there, vector_part)] = dot(v_got[...], rotation)
        rows = lax.broadcasted_iota(jnp.int32, (half, size), 0)
        cols = lax.broadcasted_iota(jnp.int32, (half, size), 1)
        diagonal = (rows == cols) | (rows + half == cols)
        squares = jnp.sum(jnp.where(diagonal, pack[size:], 0.0), axis=0, keepdims=True)
        singular_ref[...] = jnp.sqrt(jnp.maximum(squares, 0.0) + 1e-06)

    return call(
        body,
        facts,
        packs + moved + native + vectors,
        (shape(2 * part, size), shape(2 * vector_part, size), shape(1, size)),
    )


def per_device(sector, block_label):
    local_rows, size = sector.shape
    half = size // 2
    part = local_rows // 2
    pairs = lax.axis_size("pair")
    row_count = lax.axis_size("row")
    vector_rows = pairs * size // row_count // 2
    pair_index = lax.axis_index("pair")
    row_index = lax.axis_index("row")
    x = pair_index % 2
    group = pair_index // 2
    core = row_index % 2

    def permute(block, route):
        moves = [
            (a * row_count + b, c * row_count + d) for (a, b), (c, d) in route
        ]
        return lax.ppermute(block, ("pair", "row"), moves)

    devices = [(p, r) for p in range(pairs) for r in range(row_count)]

    def exchange(block, over_pair, over_row):
        return permute(
            block, [((p ^ over_pair, r ^ over_row), (p, r)) for p, r in devices]
        )

    def shift(block, by):
        return permute(
            block, [((p - by, r), (p, r)) for p, r in devices if 0 <= p - by < pairs]
        )

    def sum_rows(block):
        bit = 4
        while bit < row_count:
            block = block + exchange(block, 0, bit)
            bit *= 2
        return block

    names = jnp.arange(16, dtype=jnp.int32)
    facts = jnp.zeros((16,), jnp.int32)
    for name, value in (
        (X, x),
        (CORE, core),
        (FIRST, group == 0),
        (LAST, group == pairs // 2 - 1),
        (VROW, (row_index * 2 + x) * vector_rows),
    ):
        facts = jnp.where(names == name, value.astype(jnp.int32), facts)
    labels = lax.dynamic_slice_in_dim(block_label, 4 * group, 4)
    facts = lax.dynamic_update_slice_in_dim(facts, labels, LABEL, 0)

    give = lax.dynamic_slice_in_dim(sector, (1 - x) * part, part)
    kept = lax.dynamic_slice_in_dim(sector, x * part, part)
    got = exchange(give, 1, 0)

    own = first_gram(facts, sector, half)
    own = sum_rows(own + exchange(own, 0, 1))
    near = permute(
        own,
        [
            ((p, r ^ 2) if p % 2 == r % 2 else (p ^ 1, r ^ 1), (p, r))
            for p, r in devices
        ],
    )
    far = permute(
        own, [((p ^ 1, r ^ 2), (p, r)) for p, r in devices if p % 2 != r % 2]
    )
    pack = first_rotation(facts, own, near, far, half)

    blocks = tails = None
    for sweep_round in range(ROUNDS - 1):
        packs = [pack, exchange(pack, 0, 1)]
        last_move = sweep_round == ROUNDS - 2
        to_left, nat_l, nat_u, to_right = turn(
            facts, packs, kept, got, blocks, half, last_move
        )
        from_left, from_right = shift(to_right, 2), shift(to_left, -2)
        tail_left, tail_l, tail_u, tail_right = turn_tail(
            facts, packs, tails, vector_rows, half
        )
        tail_from_left, tail_from_right = shift(tail_right, 2), shift(tail_left, -2)
        if last_move:
            native = [nat_l, exchange(nat_u, 1, 0)]
        blocks = [from_left, to_left, nat_l, nat_u, from_right, to_right]
        tails = [tail_from_left, tail_left, tail_l, tail_u, tail_from_right, tail_right]
        grams = cross_gram(facts, blocks, half, last_move)
        own = sum_rows(grams[0] + exchange(grams[1], 0, 1))
        parts = [own, exchange(own, 0, 2), exchange(own, 1, 0), exchange(own, 1, 2)]
        if last_move:
            moved = [grams[2], exchange(grams[3], 1, 0)]
            v_keep, v_give = split_vectors(facts, tails, vector_rows, half)
            vectors = [v_keep, exchange(v_give, 1, 0)]
        pack = later_rotation(facts, parts, tails, half)
    packs = [pack, exchange(pack, 0, 1)]
    rotated, vectors_out, singular = finish(
        facts, packs, moved, native, vectors, half
    )
    return rotated, vectors_out, singular.reshape(size)


def solution(mesh):
    placed = (P("row", "pair"), P())
    return jax.shard_map(
        per_device,
        mesh=mesh,
        in_specs=placed,
        out_specs=(P("row", "pair"), P("row", "pair"), P("pair")),
        check_vma=False,
    )
```

time: 442 us -> 199 us (0.45)
  waiting for transfers between devices: 294 us -> 88.7 us
  matrix products: 80.3 us -> 0 us
  Pallas kernels: 0 us -> 50.5 us
  starting transfers between devices: 16.4 us -> 55.7 us
  between operations: 18.1 us -> 0.98 us
  local copies, waits for them, and re-layouts: 13.6 us -> 2.97 us
  other arithmetic: 9.97 us -> 0.05 us
  blocking collectives: 5.73 us -> 0 us
    psum x4 -> x0, waiting for transfers between devices: 134 us -> none  [per_device(): lax.psum(jnp.dot(columns.T, columns, precision=highest), 'row')]
    dot_general x148 -> x0, matrix products: 80.3 us -> none  [the longest x64 24.9 us: rotation_of(): jnp.dot(inverse, 2.0 * identity - jnp.dot(system, inverse, precision=high...]
    ppermute x6 -> x35, waiting for transfers between devices: 160 us -> 88.7 us  [permute(): return lax.ppermute(block, ('pair', 'row'), moves)]
    pallas_call x0 -> x16, Pallas kernels: none -> 50.5 us  [call(): pl.pallas_call(body, out_shape=outs, in_specs=[pl.BlockSpec(memory_space=...]
    ppermute x6 -> x35, starting transfers between devices: 15.2 us -> 55.7 us  [permute(): return lax.ppermute(block, ('pair', 'row'), moves)]
    gather x4 -> x0, local copies, waits for them, and re-layouts: 10.5 us -> none  [rotation_of(): diagonal = jnp.diagonal(gram_matrix)]
    psum x1 -> x0, blocking collectives: 5.73 us -> none  [per_device(): squares = lax.psum(jnp.sum(rotated * rotated, axis=0), 'row')]
    reduce_sum x5 -> x0, other arithmetic: 4.82 us -> none  [the longest x4 3.26 us: rotation_of(): bound = 1.0 + 0.25 * jnp.sum(skewed * skewed)]
  transfers between devices with their start and end apart: 10 -> 35, of which waited for: 7 -> 21; matrix products, arithmetic and copies ran while one was open for 0% -> 0% of each run, Pallas kernels for 0% -> 13%
where the time goes in v1:
time: 199 us
  waiting for transfers between devices  88.7 us (45%)
  starting transfers between devices  55.7 us (28%)
  Pallas kernels  50.5 us (25%)
  local copies, waits for them, and re-layouts  2.97 us (1%)
    ppermute x35, waiting for transfers between devices, permute(): return lax.ppermute(block, ('pair', 'row'), moves)  88.7 us
    ppermute x35, starting transfers between devices, permute(): return lax.ppermute(block, ('pair', 'row'), moves)  55.7 us
    pallas_call x16, Pallas kernels, call(): pl.pallas_call(body, out_shape=outs, in_specs=[pl.BlockSpec(memory_space=...  50.5 us
  transfers between devices with their start and end apart: 35, of which 21 were waited for; matrix products, arithmetic and copies ran while one was open for 0% of the time, Pallas kernels for 13%

profile of v1, /device:TPU:0, one launch (start us, length us, event | category | flops | bytes accessed | tf_op | source)
XLA Modules:
  0.0 198.9 jit_solution(12153546752795771451)
XLA Ops:
  0.7 2.8 %constant_dynamic-slice_fusion = (f32[1024,256]{1,0:T(8,128)}, f32[1024,256]{1,0:T(8,128)S(1)}) fusion(f32[2048,256]{1,0:T(8,128)} %x_ref.1, s32[]{:T(128)S(6)} %select_n.50, s32[]{:T(128)S(6)} %select_n.49), kind=kLoop, calls=%fused_computation.6 | loop fusion | bytes 4194312 | tf_op jit(solution)/shard_map/dynamic_slice | solution.py:374
  3.5 2.9 %collective-permute-start.4 = (f32[1024,256]{1,0:T(8,128)}, f32[1024,256]{1,0:T(8,128)}, u32[]{:S(2)}, u32[]{:S(2)}) collective-permute-start(f32[1024,256]{1,0:T(8,128)} %get-tuple-element.77), channel_id=1, source_target_pairs={{4,0},{5,1},{6,2},{7,3},{0,4},{1,5},{2,6},{3,7},{12,8},{13,9},{14,... | collective-permute-start | bytes 3145736 | tf_op jit(solution)/shard_map/ppermute | solution.py:340
  6.6 2.6 %shard_map.49 = f32[384,128]{1,0:T(8,128)S(1)} custom-call(s32[16]{0:T(128)S(1)} %constant_dynamic-update-slice_fusion.f, f32[2048,256]{1,0:T(8,128)S(1)} %copy-done), custom_call_target="tpu_custom_call" | custom-call | tf_op jit(solution)/shard_map/pallas_call | solution.py:40
  10.8 3.4 %collective-permute-start.2 = (f32[384,128]{1,0:T(8,128)S(1)}, f32[384,128]{1,0:T(8,128)S(1)}, u32[]{:S(2)}, u32[]{:S(2)}) collective-permute-start(f32[384,128]{1,0:T(8,128)S(1)} %add.36.own_ref), channel_id=1, source_target_pairs={{7,1},{5,3},{2,4},{0,6},{15,9},{13,11},{10,12},{8,14},{23,17},{21,... | collective-permute-start | bytes 589832 | tf_op jit(solution)/shard_map/ppermute | solution.py:340
  14.3 19.0 %collective-permute-done.2.far_ref = f32[384,128]{1,0:T(8,128)S(1)} collective-permute-done((f32[384,128]{1,0:T(8,128)S(1)}, f32[384,128]{1,0:T(8,128)S(1)}, u32[]{:S(2)}, u32[]{:S(2)}) %collective-permute-start.2) | collective-permute-done | bytes 196640 | tf_op jit(solution)/shard_map/ppermute | solution.py:340
  33.3 7.2 %shard_map.50.refs_0_ = f32[384,256]{1,0:T(8,128)S(1)} custom-call(s32[16]{0:T(128)S(1)} %constant_dynamic-update-slice_fusion.f, f32[384,128]{1,0:T(8,128)S(1)} %add.36.own_ref, f32[384,128]{1,0:T(8,128)S(1)} %collective-permute-done.1.near_ref, f32[384,128]{1,0:T(8,128)S(1)} %collective-permute-done.2.far_ref), custom_call_target="tpu_custom_call" | custom-call | tf_op jit(solution)/shard_map/pallas_call | solution.py:40
  42.5 3.3 %shard_map.51 = (f32[1024,128]{1,0:T(8,128)S(1)}, f32[1024,128]{1,0:T(8,128)S(1)}, f32[1024,128]{1,0:T(8,128)S(1)}, f32[1024,128]{1,0:T(8,128)S(1)}) custom-call(s32[16]{0:T(128)S(1)} %constant_dynamic-update-slice_fusion.f, f32[384,256]{1,0:T(8,128)S(1)} %shard_map.50.refs_0_, f32[384,256]{1,0:T(8,128)S(1)} %collective-permute-done.3.refs_1_, ...), custom_call_target="tpu_custom_call" | custom-call | tf_op jit(solution)/shard_map/pallas_call | solution.py:40
  45.8 3.7 %collective-permute-start.5 = (f32[1024,128]{1,0:T(8,128)S(1)}, f32[1024,128]{1,0:T(8,128)S(1)}, u32[]{:S(2)}, u32[]{:S(2)}) collective-permute-start(f32[1024,128]{1,0:T(8,128)S(1)} %get-tuple-element.40.refs_5_.refs_7_), channel_id=1, source_target_pairs={{0,8},{1,9},{2,10},{3,11},{4,12},{5,13},{6,14},{7,15},{8,16},{9,17... | collective-permute-start | bytes 1572872 | tf_op jit(solution)/shard_map/ppermute | solution.py:340
  52.1 4.6 %collective-permute-start.11 = (f32[384,128]{1,0:T(8,128)S(1)}, f32[384,128]{1,0:T(8,128)S(1)}, u32[]{:S(2)}, u32[]{:S(2)}) collective-permute-start(f32[384,128]{1,0:T(8,128)S(1)} %get-tuple-element.46.refs_9_.refs_7_), channel_id=1, source_target_pairs={{0,8},{1,9},{2,10},{3,11},{4,12},{5,13},{6,14},{7,15},{8,16},{9,17... | collective-permute-start | bytes 589832 | tf_op jit(solution)/shard_map/ppermute | solution.py:340
  57.9 3.8 %collective-permute-done.5.refs_0_.refs_2_ = f32[1024,128]{1,0:T(8,128)S(1)} collective-permute-done((f32[1024,128]{1,0:T(8,128)S(1)}, f32[1024,128]{1,0:T(8,128)S(1)}, u32[]{:S(2)}, u32[]{:S(2)}) %collective-permute-start.5) | collective-permute-done | bytes 524320 | tf_op jit(solution)/shard_map/ppermute | solution.py:340
  61.7 4.5 %collective-permute-done.6.refs_4_.refs_6_ = f32[1024,128]{1,0:T(8,128)S(1)} collective-permute-done((f32[1024,128]{1,0:T(8,128)S(1)}, f32[1024,128]{1,0:T(8,128)S(1)}, u32[]{:S(2)}, u32[]{:S(2)}) %collective-permute-start.6) | collective-permute-done | bytes 524320 | tf_op jit(solution)/shard_map/ppermute | solution.py:340
  69.2 3.0 %collective-permute-start.10 = (f32[128,128]{1,0:T(8,128)S(1)}, f32[128,128]{1,0:T(8,128)S(1)}, u32[]{:S(2)}, u32[]{:S(2)}) collective-permute-start(f32[128,128]{1,0:T(8,128)S(1)} %add.39.refs_0_), channel_id=1, source_target_pairs={{6,0},{7,1},{4,2},{5,3},{2,4},{3,5},{0,6},{1,7},{14,8},{15,9},{12,... | collective-permute-start | bytes 196616 | tf_op jit(solution)/shard_map/ppermute | solution.py:340
  74.6 1.9 collective-permute-done.9.refs_2_
  76.6 6.8 %shard_map.54.refs_0_ = f32[384,256]{1,0:T(8,128)S(1)} custom-call(s32[16]{0:T(128)S(1)} %constant_dynamic-update-slice_fusion.f, f32[128,128]{1,0:T(8,128)S(1)} %add.39.refs_0_, f32[128,128]{1,0:T(8,128)S(1)} %collective-permute-done.8.refs_1_, f32[128,128]{1,0:T(8,128)S(1)} %collective-permute-done.9.refs_2_, ...), custom_call_target="tpu_custom_call" | custom-call | tf_op jit(solution)/shard_map/pallas_call | solution.py:40
  85.2 2.5 %shard_map.55 = (f32[1024,128]{1,0:T(8,128)S(1)}, f32[1024,128]{1,0:T(8,128)S(1)}, f32[1024,128]{1,0:T(8,128)S(1)}, f32[1024,128]{1,0:T(8,128)S(1)}) custom-call(s32[16]{0:T(128)S(1)} %constant_dynamic-update-slice_fusion.f, f32[384,256]{1,0:T(8,128)S(1)} %shard_map.54.refs_0_, f32[384,256]{1,0:T(8,128)S(1)} %collective-permute-done.13.refs_1_, ...), custom_call_target="tpu_custom_call" | custom-call | tf_op jit(solution)/shard_map/pallas_call | solution.py:40
  87.7 3.5 %collective-permute-start.14 = (f32[1024,128]{1,0:T(8,128)S(1)}, f32[1024,128]{1,0:T(8,128)S(1)}, u32[]{:S(2)}, u32[]{:S(2)}) collective-permute-start(f32[1024,128]{1,0:T(8,128)S(1)} %get-tuple-element.50.refs_5_.refs_7_), channel_id=1, source_target_pairs={{0,8},{1,9},{2,10},{3,11},{4,12},{5,13},{6,14},{7,15},{8,16},{9,17... | collective-permute-start | bytes 1572872 | tf_op jit(solution)/shard_map/ppermute | solution.py:340
  93.8 4.6 %collective-permute-start.20 = (f32[384,128]{1,0:T(8,128)S(1)}, f32[384,128]{1,0:T(8,128)S(1)}, u32[]{:S(2)}, u32[]{:S(2)}) collective-permute-start(f32[384,128]{1,0:T(8,128)S(1)} %get-tuple-element.56.refs_9_.refs_7_), channel_id=1, source_target_pairs={{0,8},{1,9},{2,10},{3,11},{4,12},{5,13},{6,14},{7,15},{8,16},{9,17... | collective-permute-start | bytes 589832 | tf_op jit(solution)/shard_map/ppermute | solution.py:340
  99.7 3.8 %collective-permute-done.14.refs_0_.refs_2_ = f32[1024,128]{1,0:T(8,128)S(1)} collective-permute-done((f32[1024,128]{1,0:T(8,128)S(1)}, f32[1024,128]{1,0:T(8,128)S(1)}, u32[]{:S(2)}, u32[]{:S(2)}) %collective-permute-start.14) | collective-permute-done | bytes 524320 | tf_op jit(solution)/shard_map/ppermute | solution.py:340
  103.5 4.5 %collective-permute-done.15.refs_4_.refs_6_ = f32[1024,128]{1,0:T(8,128)S(1)} collective-permute-done((f32[1024,128]{1,0:T(8,128)S(1)}, f32[1024,128]{1,0:T(8,128)S(1)}, u32[]{:S(2)}, u32[]{:S(2)}) %collective-permute-start.15) | collective-permute-done | bytes 524320 | tf_op jit(solution)/shard_map/ppermute | solution.py:340
  110.9 2.9 %collective-permute-start.19 = (f32[128,128]{1,0:T(8,128)S(1)}, f32[128,128]{1,0:T(8,128)S(1)}, u32[]{:S(2)}, u32[]{:S(2)}) collective-permute-start(f32[128,128]{1,0:T(8,128)S(1)} %add.40.refs_0_), channel_id=1, source_target_pairs={{6,0},{7,1},{4,2},{5,3},{2,4},{3,5},{0,6},{1,7},{14,8},{15,9},{12,... | collective-permute-start | bytes 196616 | tf_op jit(solution)/shard_map/ppermute | solution.py:340
  118.1 6.0 %shard_map.58.refs_0_ = f32[384,256]{1,0:T(8,128)S(1)} custom-call(s32[16]{0:T(128)S(1)} %constant_dynamic-update-slice_fusion.f, f32[128,128]{1,0:T(8,128)S(1)} %add.40.refs_0_, f32[128,128]{1,0:T(8,128)S(1)} %collective-permute-done.17.refs_1_, f32[128,128]{1,0:T(8,128)S(1)} %collective-permute-done.18.refs_2_, ...), custom_call_target="tpu_custom_call" | custom-call | tf_op jit(solution)/shard_map/pallas_call | solution.py:40
  126.0 2.5 %shard_map.59 = (f32[1024,128]{1,0:T(8,128)S(1)}, f32[1024,128]{1,0:T(8,128)S(1)}, f32[1024,128]{1,0:T(8,128)S(1)}, f32[1024,128]{1,0:T(8,128)S(1)}) custom-call(s32[16]{0:T(128)S(1)} %constant_dynamic-update-slice_fusion.f, f32[384,256]{1,0:T(8,128)S(1)} %shard_map.58.refs_0_, f32[384,256]{1,0:T(8,128)S(1)} %collective-permute-done.22.refs_1_, ...), custom_call_target="tpu_custom_call" | custom-call | tf_op jit(solution)/shard_map/pallas_call | solution.py:40
  128.5 3.7 %collective-permute-start.23 = (f32[1024,128]{1,0:T(8,128)S(1)}, f32[1024,128]{1,0:T(8,128)S(1)}, u32[]{:S(2)}, u32[]{:S(2)}) collective-permute-start(f32[1024,128]{1,0:T(8,128)S(1)} %get-tuple-element.60.refs_5_), channel_id=1, source_target_pairs={{0,8},{1,9},{2,10},{3,11},{4,12},{5,13},{6,14},{7,15},{8,16},{9,17... | collective-permute-start | bytes 1572872 | tf_op jit(solution)/shard_map/ppermute | solution.py:340
  134.8 4.6 %collective-permute-start.29 = (f32[384,128]{1,0:T(8,128)S(1)}, f32[384,128]{1,0:T(8,128)S(1)}, u32[]{:S(2)}, u32[]{:S(2)}) collective-permute-start(f32[384,128]{1,0:T(8,128)S(1)} %get-tuple-element.66.refs_9_.refs_5_), channel_id=1, source_target_pairs={{0,8},{1,9},{2,10},{3,11},{4,12},{5,13},{6,14},{7,15},{8,16},{9,17... | collective-permute-start | bytes 589832 | tf_op jit(solution)/shard_map/ppermute | solution.py:340
  140.6 3.6 %collective-permute-done.23.refs_0_ = f32[1024,128]{1,0:T(8,128)S(1)} collective-permute-done((f32[1024,128]{1,0:T(8,128)S(1)}, f32[1024,128]{1,0:T(8,128)S(1)}, u32[]{:S(2)}, u32[]{:S(2)}) %collective-permute-start.23) | collective-permute-done | bytes 524320 | tf_op jit(solution)/shard_map/ppermute | solution.py:340
  144.2 4.7 %collective-permute-done.24.refs_4_ = f32[1024,128]{1,0:T(8,128)S(1)} collective-permute-done((f32[1024,128]{1,0:T(8,128)S(1)}, f32[1024,128]{1,0:T(8,128)S(1)}, u32[]{:S(2)}, u32[]{:S(2)}) %collective-permute-start.24) | collective-permute-done | bytes 524320 | tf_op jit(solution)/shard_map/ppermute | solution.py:340
  150.7 2.1 %collective-permute-start.33 = (f32[1024,128]{1,0:T(8,128)S(1)}, f32[1024,128]{1,0:T(8,128)S(1)}, u32[]{:S(2)}, u32[]{:S(2)}) collective-permute-start(f32[1024,128]{1,0:T(8,128)S(1)} %get-tuple-element.63.refs_3_), channel_id=1, source_target_pairs={{4,0},{5,1},{6,2},{7,3},{0,4},{1,5},{2,6},{3,7},{12,8},{13,9},{14,... | collective-permute-start | bytes 1572872 | tf_op jit(solution)/shard_map/ppermute | solution.py:340
  152.9 2.2 %collective-permute-start.28 = (f32[128,128]{1,0:T(8,128)S(1)}, f32[128,128]{1,0:T(8,128)S(1)}, u32[]{:S(2)}, u32[]{:S(2)}) collective-permute-start(f32[128,128]{1,0:T(8,128)S(1)} %add.41.refs_0_), channel_id=1, source_target_pairs={{6,0},{7,1},{4,2},{5,3},{2,4},{3,5},{0,6},{1,7},{14,8},{15,9},{12,... | collective-permute-start | bytes 196616 | tf_op jit(solution)/shard_map/ppermute | solution.py:340
  156.5 22.0 %collective-permute-done.28.refs_3_ = f32[128,128]{1,0:T(8,128)S(1)} collective-permute-done((f32[128,128]{1,0:T(8,128)S(1)}, f32[128,128]{1,0:T(8,128)S(1)}, u32[]{:S(2)}, u32[]{:S(2)}) %collective-permute-start.28) | collective-permute-done | bytes 65568 | tf_op jit(solution)/shard_map/ppermute | solution.py:340
  179.4 6.0 %shard_map.62.refs_0_ = f32[384,256]{1,0:T(8,128)S(1)} custom-call(s32[16]{0:T(128)S(1)} %constant_dynamic-update-slice_fusion.f, f32[128,128]{1,0:T(8,128)S(1)} %add.41.refs_0_, f32[128,128]{1,0:T(8,128)S(1)} %collective-permute-done.26.refs_1_, f32[128,128]{1,0:T(8,128)S(1)} %collective-permute-done.27.refs_2_, ...), custom_call_target="tpu_custom_call" | custom-call | tf_op jit(solution)/shard_map/pallas_call | solution.py:40
  187.9 7.0 %collective-permute-done.34.refs_7_ = f32[256,256]{1,0:T(8,128)S(1)} collective-permute-done((f32[256,256]{1,0:T(8,128)S(1)}, f32[256,256]{1,0:T(8,128)S(1)}, u32[]{:S(2)}, u32[]{:S(2)}) %collective-permute-start.34) | collective-permute-done | bytes 262176 | tf_op jit(solution)/shard_map/ppermute | solution.py:340
  194.9 4.1 %shard_map.64 = (f32[2048,256]{1,0:T(8,128)}, f32[512,256]{1,0:T(8,128)}, f32[1,256]{1,0:T(1,128)}) custom-call(s32[16]{0:T(128)S(1)} %constant_dynamic-update-slice_fusion.f, f32[384,256]{1,0:T(8,128)S(1)} %shard_map.62.refs_0_, f32[384,256]{1,0:T(8,128)S(1)} %collective-permute-done.31.refs_1_, f32[1024,128]{1,0:T(8,128)S(1)} %get-tuple-element.70.refs_2_, ...), custom_call_target="tpu_custom_call" | custom-call | tf_op jit(solution)/shard_map/pallas_call | solution.py:40
  (65 shorter events, 38.3 us)
Async XLA Ops:
  3.5 39.0 %collective-permute-start.4 = (f32[1024,256]{1,0:T(8,128)}, f32[1024,256]{1,0:T(8,128)}, u32[]{:S(2)}, u32[]{:S(2)}) collective-permute-start(f32[1024,256]{1,0:T(8,128)} %get-tuple-element.77), channel_id=1, source_target_pairs={{4,0},{5,1},{6,2},{7,3},{0,4},{1,5},{2,6},{3,7},{12,8},{13,9},{14,... | collective-permute-start | bytes 3145736 | tf_op jit(solution)/shard_map/ppermute | solution.py:340
  10.8 22.5 %collective-permute-start.2 = (f32[384,128]{1,0:T(8,128)S(1)}, f32[384,128]{1,0:T(8,128)S(1)}, u32[]{:S(2)}, u32[]{:S(2)}) collective-permute-start(f32[384,128]{1,0:T(8,128)S(1)} %add.36.own_ref), channel_id=1, source_target_pairs={{7,1},{5,3},{2,4},{0,6},{15,9},{13,11},{10,12},{8,14},{23,17},{21,... | collective-permute-start | bytes 589832 | tf_op jit(solution)/shard_map/ppermute | solution.py:340
  14.2 19.1 %collective-permute-start.1 = (f32[384,128]{1,0:T(8,128)S(1)}, f32[384,128]{1,0:T(8,128)S(1)}, u32[]{:S(2)}, u32[]{:S(2)}) collective-permute-start(f32[384,128]{1,0:T(8,128)S(1)} %add.36.own_ref), channel_id=1, source_target_pairs={{2,0},{4,1},{0,2},{6,3},{1,4},{7,5},{3,6},{5,7},{10,8},{12,9},{8,1... | collective-permute-start | bytes 589832 | tf_op jit(solution)/shard_map/ppermute | solution.py:340
  40.5 2.0 %collective-permute-start.3 = (f32[384,256]{1,0:T(8,128)S(1)}, f32[384,256]{1,0:T(8,128)S(1)}, u32[]{:S(2)}, u32[]{:S(2)}) collective-permute-start(f32[384,256]{1,0:T(8,128)S(1)} %shard_map.50.refs_0_), channel_id=1, source_target_pairs={{1,0},{0,1},{3,2},{2,3},{5,4},{4,5},{7,6},{6,7},{9,8},{8,9},{11,10... | collective-permute-start | bytes 1179656 | tf_op jit(solution)/shard_map/ppermute | solution.py:340
  45.8 15.9 %collective-permute-start.5 = (f32[1024,128]{1,0:T(8,128)S(1)}, f32[1024,128]{1,0:T(8,128)S(1)}, u32[]{:S(2)}, u32[]{:S(2)}) collective-permute-start(f32[1024,128]{1,0:T(8,128)S(1)} %get-tuple-element.40.refs_5_.refs_7_), channel_id=1, source_target_pairs={{0,8},{1,9},{2,10},{3,11},{4,12},{5,13},{6,14},{7,15},{8,16},{9,17... | collective-permute-start | bytes 1572872 | tf_op jit(solution)/shard_map/ppermute | solution.py:340
  49.5 16.7 %collective-permute-start.6 = (f32[1024,128]{1,0:T(8,128)S(1)}, f32[1024,128]{1,0:T(8,128)S(1)}, u32[]{:S(2)}, u32[]{:S(2)}) collective-permute-start(f32[1024,128]{1,0:T(8,128)S(1)} %get-tuple-element.41.refs_1_.refs_3_), channel_id=1, source_target_pairs={{8,0},{9,1},{10,2},{11,3},{12,4},{13,5},{14,6},{15,7},{16,8},{17,9... | collective-permute-start | bytes 1572872 | tf_op jit(solution)/shard_map/ppermute | solution.py:340
  52.1 21.6 %collective-permute-start.11 = (f32[384,128]{1,0:T(8,128)S(1)}, f32[384,128]{1,0:T(8,128)S(1)}, u32[]{:S(2)}, u32[]{:S(2)}) collective-permute-start(f32[384,128]{1,0:T(8,128)S(1)} %get-tuple-element.46.refs_9_.refs_7_), channel_id=1, source_target_pairs={{0,8},{1,9},{2,10},{3,11},{4,12},{5,13},{6,14},{7,15},{8,16},{9,17... | collective-permute-start | bytes 589832 | tf_op jit(solution)/shard_map/ppermute | solution.py:340
  56.6 17.1 %collective-permute-start.12 = (f32[384,128]{1,0:T(8,128)S(1)}, f32[384,128]{1,0:T(8,128)S(1)}, u32[]{:S(2)}, u32[]{:S(2)}) collective-permute-start(f32[384,128]{1,0:T(8,128)S(1)} %get-tuple-element.47.refs_5_.refs_3_), channel_id=1, source_target_pairs={{8,0},{9,1},{10,2},{11,3},{12,4},{13,5},{14,6},{15,7},{16,8},{17,9... | collective-permute-start | bytes 589832 | tf_op jit(solution)/shard_map/ppermute | solution.py:340
  69.2 5.4 %collective-permute-start.10 = (f32[128,128]{1,0:T(8,128)S(1)}, f32[128,128]{1,0:T(8,128)S(1)}, u32[]{:S(2)}, u32[]{:S(2)}) collective-permute-start(f32[128,128]{1,0:T(8,128)S(1)} %add.39.refs_0_), channel_id=1, source_target_pairs={{6,0},{7,1},{4,2},{5,3},{2,4},{3,5},{0,6},{1,7},{14,8},{15,9},{12,... | collective-permute-start | bytes 196616 | tf_op jit(solution)/shard_map/ppermute | solution.py:340
  72.2 4.3 %collective-permute-start.9 = (f32[128,128]{1,0:T(8,128)S(1)}, f32[128,128]{1,0:T(8,128)S(1)}, u32[]{:S(2)}, u32[]{:S(2)}) collective-permute-start(f32[128,128]{1,0:T(8,128)S(1)} %add.39.refs_0_), channel_id=1, source_target_pairs={{4,0},{5,1},{6,2},{7,3},{0,4},{1,5},{2,6},{3,7},{12,8},{13,9},{14,... | collective-permute-start | bytes 196616 | tf_op jit(solution)/shard_map/ppermute | solution.py:340
  72.3 4.3 %collective-permute-start.8 = (f32[128,128]{1,0:T(8,128)S(1)}, f32[128,128]{1,0:T(8,128)S(1)}, u32[]{:S(2)}, u32[]{:S(2)}) collective-permute-start(f32[128,128]{1,0:T(8,128)S(1)} %add.39.refs_0_), channel_id=1, source_target_pairs={{2,0},{3,1},{0,2},{1,3},{6,4},{7,5},{4,6},{5,7},{10,8},{11,9},{8,1... | collective-permute-start | bytes 196616 | tf_op jit(solution)/shard_map/ppermute | solution.py:340
  83.4 1.8 collective-permute-start.13
  87.7 15.7 %collective-permute-start.14 = (f32[1024,128]{1,0:T(8,128)S(1)}, f32[1024,128]{1,0:T(8,128)S(1)}, u32[]{:S(2)}, u32[]{:S(2)}) collective-permute-start(f32[1024,128]{1,0:T(8,128)S(1)} %get-tuple-element.50.refs_5_.refs_7_), channel_id=1, source_target_pairs={{0,8},{1,9},{2,10},{3,11},{4,12},{5,13},{6,14},{7,15},{8,16},{9,17... | collective-permute-start | bytes 1572872 | tf_op jit(solution)/shard_map/ppermute | solution.py:340
  91.2 16.7 %collective-permute-start.15 = (f32[1024,128]{1,0:T(8,128)S(1)}, f32[1024,128]{1,0:T(8,128)S(1)}, u32[]{:S(2)}, u32[]{:S(2)}) collective-permute-start(f32[1024,128]{1,0:T(8,128)S(1)} %get-tuple-element.51.refs_1_.refs_3_), channel_id=1, source_target_pairs={{8,0},{9,1},{10,2},{11,3},{12,4},{13,5},{14,6},{15,7},{16,8},{17,9... | collective-permute-start | bytes 1572872 | tf_op jit(solution)/shard_map/ppermute | solution.py:340
  93.8 20.8 %collective-permute-start.20 = (f32[384,128]{1,0:T(8,128)S(1)}, f32[384,128]{1,0:T(8,128)S(1)}, u32[]{:S(2)}, u32[]{:S(2)}) collective-permute-start(f32[384,128]{1,0:T(8,128)S(1)} %get-tuple-element.56.refs_9_.refs_7_), channel_id=1, source_target_pairs={{0,8},{1,9},{2,10},{3,11},{4,12},{5,13},{6,14},{7,15},{8,16},{9,17... | collective-permute-start | bytes 589832 | tf_op jit(solution)/shard_map/ppermute | solution.py:340
  98.4 16.2 %collective-permute-start.21 = (f32[384,128]{1,0:T(8,128)S(1)}, f32[384,128]{1,0:T(8,128)S(1)}, u32[]{:S(2)}, u32[]{:S(2)}) collective-permute-start(f32[384,128]{1,0:T(8,128)S(1)} %get-tuple-element.57.refs_5_.refs_3_), channel_id=1, source_target_pairs={{8,0},{9,1},{10,2},{11,3},{12,4},{13,5},{14,6},{15,7},{16,8},{17,9... | collective-permute-start | bytes 589832 | tf_op jit(solution)/shard_map/ppermute | solution.py:340
  110.9 5.3 %collective-permute-start.19 = (f32[128,128]{1,0:T(8,128)S(1)}, f32[128,128]{1,0:T(8,128)S(1)}, u32[]{:S(2)}, u32[]{:S(2)}) collective-permute-start(f32[128,128]{1,0:T(8,128)S(1)} %add.40.refs_0_), channel_id=1, source_target_pairs={{6,0},{7,1},{4,2},{5,3},{2,4},{3,5},{0,6},{1,7},{14,8},{15,9},{12,... | collective-permute-start | bytes 196616 | tf_op jit(solution)/shard_map/ppermute | solution.py:340
  113.8 4.3 %collective-permute-start.18 = (f32[128,128]{1,0:T(8,128)S(1)}, f32[128,128]{1,0:T(8,128)S(1)}, u32[]{:S(2)}, u32[]{:S(2)}) collective-permute-start(f32[128,128]{1,0:T(8,128)S(1)} %add.40.refs_0_), channel_id=1, source_target_pairs={{4,0},{5,1},{6,2},{7,3},{0,4},{1,5},{2,6},{3,7},{12,8},{13,9},{14,... | collective-permute-start | bytes 196616 | tf_op jit(solution)/shard_map/ppermute | solution.py:340
  113.9 4.3 %collective-permute-start.17 = (f32[128,128]{1,0:T(8,128)S(1)}, f32[128,128]{1,0:T(8,128)S(1)}, u32[]{:S(2)}, u32[]{:S(2)}) collective-permute-start(f32[128,128]{1,0:T(8,128)S(1)} %add.40.refs_0_), channel_id=1, source_target_pairs={{2,0},{3,1},{0,2},{1,3},{6,4},{7,5},{4,6},{5,7},{10,8},{11,9},{8,1... | collective-permute-start | bytes 196616 | tf_op jit(solution)/shard_map/ppermute | solution.py:340
  124.2 1.8 collective-permute-start.22
  128.5 15.7 %collective-permute-start.23 = (f32[1024,128]{1,0:T(8,128)S(1)}, f32[1024,128]{1,0:T(8,128)S(1)}, u32[]{:S(2)}, u32[]{:S(2)}) collective-permute-start(f32[1024,128]{1,0:T(8,128)S(1)} %get-tuple-element.60.refs_5_), channel_id=1, source_target_pairs={{0,8},{1,9},{2,10},{3,11},{4,12},{5,13},{6,14},{7,15},{8,16},{9,17... | collective-permute-start | bytes 1572872 | tf_op jit(solution)/shard_map/ppermute | solution.py:340
  132.2 16.7 %collective-permute-start.24 = (f32[1024,128]{1,0:T(8,128)S(1)}, f32[1024,128]{1,0:T(8,128)S(1)}, u32[]{:S(2)}, u32[]{:S(2)}) collective-permute-start(f32[1024,128]{1,0:T(8,128)S(1)} %get-tuple-element.61.refs_1_), channel_id=1, source_target_pairs={{8,0},{9,1},{10,2},{11,3},{12,4},{13,5},{14,6},{15,7},{16,8},{17,9... | collective-permute-start | bytes 1572872 | tf_op jit(solution)/shard_map/ppermute | solution.py:340
  134.8 20.3 %collective-permute-start.29 = (f32[384,128]{1,0:T(8,128)S(1)}, f32[384,128]{1,0:T(8,128)S(1)}, u32[]{:S(2)}, u32[]{:S(2)}) collective-permute-start(f32[384,128]{1,0:T(8,128)S(1)} %get-tuple-element.66.refs_9_.refs_5_), channel_id=1, source_target_pairs={{0,8},{1,9},{2,10},{3,11},{4,12},{5,13},{6,14},{7,15},{8,16},{9,17... | collective-permute-start | bytes 589832 | tf_op jit(solution)/shard_map/ppermute | solution.py:340
  139.3 15.9 %collective-permute-start.30 = (f32[384,128]{1,0:T(8,128)S(1)}, f32[384,128]{1,0:T(8,128)S(1)}, u32[]{:S(2)}, u32[]{:S(2)}) collective-permute-start(f32[384,128]{1,0:T(8,128)S(1)} %get-tuple-element.67.refs_5_.refs_1_), channel_id=1, source_target_pairs={{8,0},{9,1},{10,2},{11,3},{12,4},{13,5},{14,6},{15,7},{16,8},{17,9... | collective-permute-start | bytes 589832 | tf_op jit(solution)/shard_map/ppermute | solution.py:340
  150.6 2.3 %collective-permute-start.25 = (f32[128,128]{1,0:T(8,128)S(1)}, f32[128,128]{1,0:T(8,128)S(1)}, u32[]{:S(2)}, u32[]{:S(2)}) collective-permute-start(f32[128,128]{1,0:T(8,128)S(1)} %get-tuple-element.65), channel_id=1, source_target_pairs={{1,0},{0,1},{3,2},{2,3},{5,4},{4,5},{7,6},{6,7},{9,8},{8,9},{11,10... | collective-permute-start | bytes 196616 | tf_op jit(solution)/shard_map/ppermute | solution.py:340
  150.7 44.1 %collective-permute-start.33 = (f32[1024,128]{1,0:T(8,128)S(1)}, f32[1024,128]{1,0:T(8,128)S(1)}, u32[]{:S(2)}, u32[]{:S(2)}) collective-permute-start(f32[1024,128]{1,0:T(8,128)S(1)} %get-tuple-element.63.refs_3_), channel_id=1, source_target_pairs={{4,0},{5,1},{6,2},{7,3},{0,4},{1,5},{2,6},{3,7},{12,8},{13,9},{14,... | collective-permute-start | bytes 1572872 | tf_op jit(solution)/shard_map/ppermute | solution.py:340
  152.8 42.1 %collective-permute-start.32 = (f32[1024,128]{1,0:T(8,128)S(1)}, f32[1024,128]{1,0:T(8,128)S(1)}, u32[]{:S(2)}, u32[]{:S(2)}) collective-permute-start(f32[1024,128]{1,0:T(8,128)S(1)} %get-tuple-element.71), channel_id=1, source_target_pairs={{4,0},{5,1},{6,2},{7,3},{0,4},{1,5},{2,6},{3,7},{12,8},{13,9},{14,... | collective-permute-start | bytes 1572872 | tf_op jit(solution)/shard_map/ppermute | solution.py:340
  152.9 25.6 %collective-permute-start.28 = (f32[128,128]{1,0:T(8,128)S(1)}, f32[128,128]{1,0:T(8,128)S(1)}, u32[]{:S(2)}, u32[]{:S(2)}) collective-permute-start(f32[128,128]{1,0:T(8,128)S(1)} %add.41.refs_0_), channel_id=1, source_target_pairs={{6,0},{7,1},{4,2},{5,3},{2,4},{3,5},{0,6},{1,7},{14,8},{15,9},{12,... | collective-permute-start | bytes 196616 | tf_op jit(solution)/shard_map/ppermute | solution.py:340
  155.1 24.2 %collective-permute-start.27 = (f32[128,128]{1,0:T(8,128)S(1)}, f32[128,128]{1,0:T(8,128)S(1)}, u32[]{:S(2)}, u32[]{:S(2)}) collective-permute-start(f32[128,128]{1,0:T(8,128)S(1)} %add.41.refs_0_), channel_id=1, source_target_pairs={{4,0},{5,1},{6,2},{7,3},{0,4},{1,5},{2,6},{3,7},{12,8},{13,9},{14,... | collective-permute-start | bytes 196616 | tf_op jit(solution)/shard_map/ppermute | solution.py:340
  155.2 24.1 %collective-permute-start.26 = (f32[128,128]{1,0:T(8,128)S(1)}, f32[128,128]{1,0:T(8,128)S(1)}, u32[]{:S(2)}, u32[]{:S(2)}) collective-permute-start(f32[128,128]{1,0:T(8,128)S(1)} %add.41.refs_0_), channel_id=1, source_target_pairs={{2,0},{3,1},{0,2},{1,3},{6,4},{7,5},{4,6},{5,7},{10,8},{11,9},{8,1... | collective-permute-start | bytes 196616 | tf_op jit(solution)/shard_map/ppermute | solution.py:340
  185.4 9.5 %collective-permute-start.31 = (f32[384,256]{1,0:T(8,128)S(1)}, f32[384,256]{1,0:T(8,128)S(1)}, u32[]{:S(2)}, u32[]{:S(2)}) collective-permute-start(f32[384,256]{1,0:T(8,128)S(1)} %shard_map.62.refs_0_), channel_id=1, source_target_pairs={{1,0},{0,1},{3,2},{2,3},{5,4},{4,5},{7,6},{6,7},{9,8},{8,9},{11,10... | collective-permute-start | bytes 1179656 | tf_op jit(solution)/shard_map/ppermute | solution.py:340
  186.1 8.8 %collective-permute-start.34 = (f32[256,256]{1,0:T(8,128)S(1)}, f32[256,256]{1,0:T(8,128)S(1)}, u32[]{:S(2)}, u32[]{:S(2)}) collective-permute-start(f32[256,256]{1,0:T(8,128)S(1)} %get-tuple-element.73), channel_id=1, source_target_pairs={{4,0},{5,1},{6,2},{7,3},{0,4},{1,5},{2,6},{3,7},{12,8},{13,9},{14,... | collective-permute-start | bytes 786440 | tf_op jit(solution)/shard_map/ppermute | solution.py:340
  (5 other events, 15.8 us)

commit v2 on v1

v2 whole, which is shorter than its diff:
```python
import jax
import jax.numpy as jnp
from jax import lax
from jax.experimental import pallas as pl
from jax.experimental.pallas import tpu as pltpu
from jax.sharding import PartitionSpec as P

ROUNDS = 4
NEWTON = 16

highest = lax.Precision.HIGHEST

TARGET = 2.0**-12
BOUNDS = [
    (1.0 + TARGET ** (2.0**-j)) / (1.0 - TARGET ** (2.0**-j)) for j in range(NEWTON)
]

X, CORE, FIRST, LAST, VROW, LABEL = 0, 1, 2, 3, 4, 5


def dot(a, b, precision=highest):
    return lax.dot_general(
        a, b, (((1,), (0,)), ((), ())), precision=precision,
        preferred_element_type=jnp.float32,
    )


def split(a):
    high = a.astype(jnp.bfloat16)
    return high, (a - high.astype(jnp.float32)).astype(jnp.bfloat16)


def dot3(a, b):
    a_high, a_low = a if isinstance(a, tuple) else split(a)
    b_high, b_low = b if isinstance(b, tuple) else split(b)
    small = dot(a_high, b_low, None) + dot(a_low, b_high, None)
    return dot(a_high, b_high, None) + small


def dot_tn(a, b):
    return lax.dot_general(
        a, b, (((0,), (0,)), ((), ())), precision=highest,
        preferred_element_type=jnp.float32,
    )


def shape(*dims):
    return jax.ShapeDtypeStruct(dims, jnp.float32)


def call(body, facts, inputs, outs, scratch=(), limit=24):
    return pl.pallas_call(
        body,
        out_shape=outs,
        in_specs=[pl.BlockSpec(memory_space=pltpu.SMEM)]
        + [pl.BlockSpec(memory_space=pltpu.VMEM)] * len(inputs),
        out_specs=jax.tree.map(
            lambda _: pl.BlockSpec(memory_space=pltpu.VMEM), outs
        ),
        scratch_shapes=list(scratch),
        compiler_params=pltpu.CompilerParams(vmem_limit_bytes=limit << 20),
    )(facts, *inputs)


def first_gram(facts, sector, half):
    rows, width = sector.shape
    part = rows // 2

    def body(f, x_ref, out_ref, give_ref):
        x = x_ref[...]
        g = dot_tn(x, x)
        out_ref[:half] = g[:half, :half]
        out_ref[half : 2 * half] = g[:half, half:]
        out_ref[2 * half :] = g[half:, half:]
        there = pl.multiple_of((1 - f[X]) * part, part)
        give_ref[...] = x_ref[pl.ds(there, part)]

    return call(
        body, facts, [sector], (shape(3 * half, half), shape(part, width))
    )


def rotate_of(gram, x_ref, e_ref):
    size = gram.shape[0]
    rows = lax.broadcasted_iota(jnp.int32, (size, size), 0)
    cols = lax.broadcasted_iota(jnp.int32, (size, size), 1)
    identity = (rows == cols).astype(jnp.float32)
    only = jnp.where(rows == cols, gram, 0.0)
    g_j = jnp.sum(only, axis=0, keepdims=True)
    g_i = jnp.sum(only, axis=1, keepdims=True)
    spread = g_j - g_i
    summed = g_j + g_i
    skew = gram * spread / (spread * spread + 2.0 * gram * gram + 0.01 * summed * summed)
    bound = 1.0 + 0.25 * jnp.sum(skew * skew)
    steps = jnp.int32(0)
    for limit in BOUNDS:
        steps = steps + (bound > limit).astype(jnp.int32)
    fixes = 1 + (steps > 7).astype(jnp.int32) + 2 * (steps > 9).astype(jnp.int32)
    scale = 2.0 / (1.0 + jnp.full((size, size), bound, jnp.float32))
    skew_parts = split(skew)
    residual = identity - scale * (identity - 0.25 * dot3(skew_parts, skew_parts))
    x_ref[...] = scale * (identity + residual)
    residual_parts = split(residual)
    e_ref[...] = dot3(residual_parts, residual_parts)

    def step(_, carry):
        e = split(e_ref[...])
        x = x_ref[...]
        x_ref[...] = x + dot3(x, e)
        e_ref[...] = dot3(e, e)
        return carry

    lax.fori_loop(0, jnp.maximum(steps - 1, 0), step, jnp.int32(0))
    x = x_ref[...]
    x_ref[...] = x + 0.5 * dot3(x, skew_parts)

    def fix(_, carry):
        x = x_ref[...]
        x_ref[...] = x + dot3(x, identity - (x - 0.5 * dot(skew, x)))
        return carry

    lax.fori_loop(0, fixes, fix, jnp.int32(0))
    return 2.0 * x_ref[...] - identity


def put_rotation(rotation_ref, gram, x_ref, e_ref, last_round):
    size = gram.shape[0]
    rotation = rotate_of(gram, x_ref, e_ref)
    rotation_ref[:size] = rotation
    if last_round:
        squares = jnp.sum(rotation * dot(gram, rotation), axis=0, keepdims=True)
        rotation_ref[size:] = jnp.broadcast_to(squares, (8, size))


def first_rotation(facts, own, near, far, half):
    size = 2 * half

    def body(f, own_ref, near_ref, far_ref, rotation_ref, g_ref, x_ref, e_ref):
        mine = f[X] == f[CORE]
        total = near_ref[...] + jnp.where(mine, own_ref[...], far_ref[...])
        g_ref[:half, :half] = total[:half]
        g_ref[:half, half:] = total[half : 2 * half]
        g_ref[half:, :half] = total[half : 2 * half].T
        g_ref[half:, half:] = total[2 * half :]
        put_rotation(rotation_ref, g_ref[...], x_ref, e_ref, False)

    square = pltpu.VMEM((size, size), jnp.float32)
    return call(
        body, facts, [own, near, far], (shape(size, size),) * 2, [square] * 2
    )


def later_rotation(facts, parts, tails, half, last_round):
    size = 2 * half
    top = tails[0].shape[0] - half

    def body(f, *refs):
        own, other_y, other_x, other_xy = [r[...] for r in refs[:4]]
        from_left, kept_left, nat_l, nat_u, from_right, kept_right = [
            r[top:] for r in refs[4:10]
        ]
        rotation_ref, g_ref, x_ref, e_ref = refs[10:]
        cross = (own + other_y) + (other_x + other_xy)
        first, last, core = f[FIRST] == 1, f[LAST] == 1, f[CORE] == 0
        up_0 = jnp.where(first, kept_left, from_left)
        low_1 = jnp.where(last, kept_right, from_right)
        g_ref[:half, :half] = jnp.where(core, up_0, nat_u)
        g_ref[:half, half:] = cross
        g_ref[half:, :half] = cross.T
        g_ref[half:, half:] = jnp.where(core, nat_l, low_1)
        put_rotation(rotation_ref, g_ref[...], x_ref, e_ref, last_round)

    square = pltpu.VMEM((size, size), jnp.float32)
    return call(
        body,
        facts,
        parts + tails,
        (shape(size + 8 if last_round else size, size), shape(size, size)),
        [square] * 2,
    )


def turned_gram(facts, gram, rotation):
    size = gram.shape[0]
    half = size // 2

    def body(f, gram_ref, rotation_ref, out_ref):
        rotation = rotation_ref[...]
        turned = dot(gram_ref[...], rotation)
        out_ref[:, :half] = dot_tn(rotation[:, :half], turned[:, :half])
        out_ref[:, half:] = dot_tn(rotation[:, half:], turned[:, half:])

    return call(body, facts, [gram, rotation], shape(half, size))


def two_packs(f, own, other):
    core = f[CORE] == 0
    return jnp.where(core, own, other), jnp.where(core, other, own)


def swapped(flag, matrix, axis):
    half = matrix.shape[axis] // 2
    a = lax.slice_in_dim(matrix, 0, half, axis=axis)
    b = lax.slice_in_dim(matrix, half, 2 * half, axis=axis)
    return jnp.where(flag, lax.concatenate([b, a], axis), matrix)


def blocks_of(f, refs, rows=None):
    vals = [r[...] if rows is None else r[:rows] for r in refs]
    from_left, kept_left, nat_l, nat_u, from_right, kept_right = vals
    up_0 = jnp.where(f[FIRST] == 1, kept_left, from_left)
    low_1 = jnp.where(f[LAST] == 1, kept_right, from_right)
    return up_0, nat_l, nat_u, low_1


def put_turned(f, refs, zero, one, half):
    to_left_ref, nat_l_ref, nat_u_ref, to_right_ref = refs[:4]
    rows = zero.shape[0]
    to_left_ref[:rows] = zero[:, half:]
    to_right_ref[:rows] = one[:, :half]
    nat_u_ref[:rows] = zero[:, :half]
    nat_l_ref[:rows] = one[:, half:]
    if len(refs) > 4:
        refs[4][...] = jnp.where(f[X] == 0, zero[:, :half], one[:, half:])


def turn(facts, packs, kept, got, blocks, half, last_move):
    size = 2 * half
    first_round = blocks is None
    inputs = packs + ([kept, got] if first_round else blocks)
    rows = got.shape[0] if first_round else blocks[0].shape[0]

    def body(f, *refs):
        own, other = refs[0][:size], refs[1][:size]
        turn_0, turn_1 = two_packs(f, own, other)
        turn_0 = swapped(f[FIRST] == 1, turn_0, 1)
        outs = refs[2 + len(inputs) - 2 :]
        if first_round:
            even = f[X] == 0
            here = pl.multiple_of(f[X] * rows, rows)
            mine, theirs = refs[2][pl.ds(here, rows)], refs[3][...]
            zero, one = jnp.where(even, mine, theirs), jnp.where(even, theirs, mine)
        else:
            up_0, low_0, up_1, low_1 = blocks_of(f, refs[2:8])
            zero = lax.concatenate([up_0, low_0], 1)
            one = lax.concatenate([up_1, low_1], 1)
        put_turned(f, outs, dot3(zero, turn_0), dot3(one, turn_1), half)

    return call(body, facts, inputs, (shape(rows, half),) * (5 if last_move else 4))


def turn_tail(facts, packs, grams, tails, vector_rows, half, last_move):
    size = 2 * half
    inputs = packs + grams + (tails or [])

    def body(f, *refs):
        pack_0, pack_1 = two_packs(f, refs[0][...], refs[1][...])
        gram_0, gram_1 = two_packs(f, refs[2][...], refs[3][...])
        pack_0 = swapped(f[FIRST] == 1, pack_0, 1)
        gram_0 = swapped(f[FIRST] == 1, gram_0, 1)
        outs = refs[len(inputs) :]
        if tails is None:
            rows = f[VROW] + lax.broadcasted_iota(jnp.int32, (vector_rows, half), 0)
            cols = lax.broadcasted_iota(jnp.int32, (vector_rows, half), 1)
            up_0, low_0, up_1, low_1 = [
                (rows == f[LABEL + k] * half + cols).astype(jnp.float32)
                for k in range(4)
            ]
        else:
            up_0, low_0, up_1, low_1 = blocks_of(f, refs[4:10], vector_rows)
        zero = dot3(lax.concatenate([up_0, low_0], 1), pack_0)
        one = dot3(lax.concatenate([up_1, low_1], 1), pack_1)
        put_turned(f, outs, zero, one, half)
        outs[0][vector_rows:] = gram_0[:, half:]
        outs[1][vector_rows:] = gram_1[:, half:]
        outs[2][vector_rows:] = gram_0[:, :half]
        outs[3][vector_rows:] = gram_1[:, :half]

    outs = (shape(vector_rows + half, half),) * 4
    if last_move:
        outs = outs + (shape(vector_rows, half),)
    return call(body, facts, inputs, outs)


def cross_gram(facts, blocks, half):
    def body(f, *refs):
        up_0, low_0, up_1, low_1 = blocks_of(f, refs[:6])
        zero, one = dot_tn(up_0, low_0), dot_tn(up_1, low_1)
        core = f[CORE] == 0
        refs[6][...] = jnp.where(core, zero, one)
        refs[7][...] = jnp.where(core, one, zero)

    return call(body, facts, blocks, (shape(half, half),) * 2)


def arrived(f, from_left_ref, kept_left_ref, from_right_ref, kept_right_ref, rows, other):
    up_0 = jnp.where(f[FIRST] == 1, kept_left_ref[rows], from_left_ref[rows])
    low_1 = jnp.where(f[LAST] == 1, kept_right_ref[rows], from_right_ref[rows])
    return jnp.where(f[X] == (1 if other else 0), up_0, low_1)


def ends(refs):
    return refs[0], refs[1], refs[4], refs[5]


def give_top(facts, blocks, rows, half):
    def body(f, *refs):
        refs[4][...] = arrived(f, *refs[:4], slice(0, rows), True)

    return call(body, facts, list(ends(blocks)), shape(rows, half))


def give_rest(facts, blocks, tails, top, vector_rows, half):
    rest = blocks[0].shape[0] - top

    def body(f, *refs):
        refs[8][:rest] = arrived(f, *refs[:4], slice(top, top + rest), True)
        refs[8][rest:] = arrived(f, *refs[4:8], slice(0, vector_rows), True)

    return call(
        body,
        facts,
        list(ends(blocks)) + list(ends(tails)),
        shape(rest + vector_rows, half),
    )


def finish(facts, packs, blocks, tails, got, vector_rows, half):
    size = 2 * half
    part = blocks[0].shape[0]
    top = got[2].shape[0]

    def body(f, *refs):
        x = f[X]
        mine = f[CORE] == x
        pack = jnp.where(mine, refs[0][...], refs[1][...])
        turned = split(swapped(x == 1, pack[:size], 0))
        block_refs, tail_refs = refs[2:8], refs[8:14]
        native_ref, native_tail_ref, top_ref, rest_ref = refs[14:18]
        out_ref, vectors_ref, singular_ref = refs[18:]

        def put(ref, at, rows, moved, native):
            here = pl.ds(pl.multiple_of(at, 8), rows)
            ref[here] = dot3(lax.concatenate([moved, native], 1), turned)

        def own(refs, rows):
            moved = arrived(f, *ends(refs), slice(0, rows), False)
            return moved, jnp.where(x == 0, refs[2][:rows], refs[3][:rows])

        put(out_ref, x * part, part, *own(block_refs, part))
        put(vectors_ref, x * vector_rows, vector_rows, *own(tail_refs, vector_rows))
        put(out_ref, (1 - x) * part, top, top_ref[...], native_ref[:top])
        put(
            out_ref, (1 - x) * part + top, part - top,
            rest_ref[: part - top], native_ref[top:],
        )
        put(
            vectors_ref, (1 - x) * vector_rows, vector_rows,
            rest_ref[part - top :], native_tail_ref[...],
        )
        squares = pack[size : size + 1]
        singular_ref[...] = jnp.sqrt(jnp.maximum(squares, 0.0) + 1e-06)

    return call(
        body,
        facts,
        packs + blocks + tails + got,
        (shape(2 * part, size), shape(2 * vector_rows, size), shape(1, size)),
    )


def per_device(sector, block_label):
    local_rows, size = sector.shape
    half = size // 2
    part = local_rows // 2
    pairs = lax.axis_size("pair")
    row_count = lax.axis_size("row")
    vector_rows = pairs * size // row_count // 2
    pair_index = lax.axis_index("pair")
    row_index = lax.axis_index("row")
    x = pair_index % 2
    group = pair_index // 2
    core = row_index % 2

    def permute(block, route):
        moves = [
            (a * row_count + b, c * row_count + d) for (a, b), (c, d) in route
        ]
        return lax.ppermute(block, ("pair", "row"), moves)

    devices = [(p, r) for p in range(pairs) for r in range(row_count)]

    def exchange(block, over_pair, over_row):
        return permute(
            block, [((p ^ over_pair, r ^ over_row), (p, r)) for p, r in devices]
        )

    def shift(block, by):
        return permute(
            block, [((p - by, r), (p, r)) for p, r in devices if 0 <= p - by < pairs]
        )

    def sum_rows(block):
        bit = 4
        while bit < row_count:
            block = block + exchange(block, 0, bit)
            bit *= 2
        return block

    names = jnp.arange(16, dtype=jnp.int32)
    facts = jnp.zeros((16,), jnp.int32)
    for name, value in (
        (X, x),
        (CORE, core),
        (FIRST, group == 0),
        (LAST, group == pairs // 2 - 1),
        (VROW, (row_index * 2 + x) * vector_rows),
    ):
        facts = jnp.where(names == name, value.astype(jnp.int32), facts)
    labels = lax.dynamic_slice_in_dim(block_label, 4 * group, 4)
    facts = lax.dynamic_update_slice_in_dim(facts, labels, LABEL, 0)

    def after(block, *others):
        return lax.optimization_barrier((block,) + others)[0]

    own, give = first_gram(facts, sector, half)
    own = sum_rows(own + exchange(own, 0, 1))
    near = permute(
        own,
        [
            ((p, r ^ 2) if p % 2 == r % 2 else (p ^ 1, r ^ 1), (p, r))
            for p, r in devices
        ],
    )
    far = permute(
        own, [((p ^ 1, r ^ 2), (p, r)) for p, r in devices if p % 2 != r % 2]
    )
    got = exchange(after(give, near, far), 1, 0)
    rotation, gram = first_rotation(facts, own, near, far, half)

    blocks = tails = None
    for sweep_round in range(ROUNDS - 1):
        packs = [rotation, exchange(rotation, 0, 1)]
        last_move = sweep_round == ROUNDS - 2
        to_left, nat_l, nat_u, to_right, *give = turn(
            facts, packs, sector, got, blocks, half, last_move
        )
        from_left, from_right = shift(to_right, 2), shift(to_left, -2)
        gram = turned_gram(facts, gram, rotation)
        tail_left, tail_l, tail_u, tail_right, *tail_give = turn_tail(
            facts, packs, [gram, exchange(gram, 0, 1)], tails, vector_rows, half,
            last_move,
        )
        tail_from_left, tail_from_right = shift(tail_right, 2), shift(tail_left, -2)
        blocks = [from_left, to_left, nat_l, nat_u, from_right, to_right]
        tails = [tail_from_left, tail_left, tail_l, tail_u, tail_from_right, tail_right]
        if last_move:
            native = exchange(give[0], 1, 0)
            native_tail = exchange(tail_give[0], 1, 0)
            top = part // 2
            top_give = give_top(facts, blocks, top, half)
            *blocks, native, native_tail, top_give = lax.optimization_barrier(
                tuple(blocks) + (native, native_tail, top_give)
            )
            got_top = exchange(top_give, 1, 0)
        grams = cross_gram(facts, blocks, half)
        own = sum_rows(grams[0] + exchange(grams[1], 0, 1))
        parts = [own, exchange(own, 0, 2), exchange(own, 1, 0), exchange(own, 1, 2)]
        if last_move:
            rest = give_rest(facts, blocks, tails, top, vector_rows, half)
            *parts, got_top, rest = lax.optimization_barrier(
                tuple(parts) + (got_top, rest)
            )
            got_rest = exchange(rest, 1, 0)
        rotation, gram = later_rotation(facts, parts, tails, half, last_move)
    packs = [rotation, exchange(rotation, 0, 1)]
    rotated, vectors_out, singular = finish(
        facts, packs, blocks, tails, [native, native_tail, got_top, got_rest],
        vector_rows, half,
    )
    return rotated, vectors_out, singular.reshape(size)


def solution(mesh):
    placed = (P("row", "pair"), P())
    return jax.shard_map(
        per_device,
        mesh=mesh,
        in_specs=placed,
        out_specs=(P("row", "pair"), P("row", "pair"), P("pair")),
        check_vma=False,
    )
```

time: 199 us -> 167 us (0.84)
  waiting for transfers between devices: 88.7 us -> 64.8 us
  Pallas kernels: 50.5 us -> 41.2 us
    ppermute x35 -> x39, waiting for transfers between devices: 88.7 us -> 64.8 us  [permute(): return lax.ppermute(block, ('pair', 'row'), moves)]
    pallas_call x16 -> x20, Pallas kernels: 50.5 us -> 41.2 us  [call(): pl.pallas_call(body, out_shape=outs, in_specs=[pl.BlockSpec(memory_space=...]
    dynamic_slice x1 -> x0, local copies, waits for them, and re-layouts: 2.8 us -> none  [per_device(): give = lax.dynamic_slice_in_dim(sector, (1 - x) * part, part)]
    ppermute x35 -> x39, starting transfers between devices: 55.7 us -> 56.6 us  [permute(): return lax.ppermute(block, ('pair', 'row'), moves)]
  transfers between devices with their start and end apart: 35 -> 39, of which waited for: 21 -> 28; matrix products, arithmetic and copies ran while one was open for 0% -> 0% of each run, Pallas kernels for 13% -> 14%
where the time goes in v2:
time: 167 us; the launch traced here: 166 us
  waiting for transfers between devices  64.8 us (39%)
  starting transfers between devices  56.6 us (34%)
  Pallas kernels  41.2 us (25%)
  local copies, waits for them, and re-layouts  2.4 us (1%)
    ppermute x39, waiting for transfers between devices, permute(): return lax.ppermute(block, ('pair', 'row'), moves)  64.8 us
    ppermute x39, starting transfers between devices, permute(): return lax.ppermute(block, ('pair', 'row'), moves)  56.6 us
    pallas_call x20, Pallas kernels, call(): pl.pallas_call(body, out_shape=outs, in_specs=[pl.BlockSpec(memory_space=...  41.2 us
  transfers between devices with their start and end apart: 39, of which 28 were waited for; matrix products, arithmetic and copies ran while one was open for 0% of the time, Pallas kernels for 14%

profile of v2, /device:TPU:0, one launch (start us, length us, event | category | flops | bytes accessed | tf_op | source)
XLA Modules:
  0.0 166.1 jit_solution(6241917852756483755)
XLA Ops:
  3.1 2.7 %shard_map.49 = (f32[384,128]{1,0:T(8,128)S(1)}, f32[1024,256]{1,0:T(8,128)S(1)}) custom-call(s32[16]{0:T(128)S(1)} %constant_dynamic-update-slice_fusion.f, f32[2048,256]{1,0:T(8,128)S(1)} %copy-done), custom_call_target="tpu_custom_call" | custom-call | tf_op jit(solution)/shard_map/pallas_call | solution.py:52
  7.4 5.7 %collective-permute-start.2 = (f32[384,128]{1,0:T(8,128)S(1)}, f32[384,128]{1,0:T(8,128)S(1)}, u32[]{:S(2)}, u32[]{:S(2)}) collective-permute-start(f32[384,128]{1,0:T(8,128)S(1)} %add.30.own_ref), channel_id=1, source_target_pairs={{7,1},{5,3},{2,4},{0,6},{15,9},{13,11},{10,12},{8,14},{23,17},{21,... | collective-permute-start | bytes 589832 | tf_op jit(solution)/shard_map/ppermute | solution.py:389
  13.7 2.7 %collective-permute-done.2.far_ref = f32[384,128]{1,0:T(8,128)S(1)} collective-permute-done((f32[384,128]{1,0:T(8,128)S(1)}, f32[384,128]{1,0:T(8,128)S(1)}, u32[]{:S(2)}, u32[]{:S(2)}) %collective-permute-start.2) | collective-permute-done | bytes 196640 | tf_op jit(solution)/shard_map/ppermute | solution.py:389
  16.4 2.5 %collective-permute-done.1.near_ref = f32[384,128]{1,0:T(8,128)S(1)} collective-permute-done((f32[384,128]{1,0:T(8,128)S(1)}, f32[384,128]{1,0:T(8,128)S(1)}, u32[]{:S(2)}, u32[]{:S(2)}) %collective-permute-start.1) | collective-permute-done | bytes 196640 | tf_op jit(solution)/shard_map/ppermute | solution.py:389
  19.9 4.4 %shard_map.50 = (f32[256,256]{1,0:T(8,128)S(1)}, f32[256,256]{1,0:T(8,128)S(1)}) custom-call(s32[16]{0:T(128)S(1)} %constant_dynamic-update-slice_fusion.f, f32[384,128]{1,0:T(8,128)S(1)} %add.30.own_ref, f32[384,128]{1,0:T(8,128)S(1)} %collective-permute-done.1.near_ref, f32[384,128]{1,0:T(8,128)S(1)} %collective-permute-done.2.far_ref), custom_call_target="tpu_custom_call" | custom-call | tf_op jit(solution)/shard_map/pallas_call | solution.py:52
  25.9 17.7 %collective-permute-done.4.refs_3_ = f32[1024,256]{1,0:T(8,128)S(1)} collective-permute-done((f32[1024,256]{1,0:T(8,128)S(1)}, f32[1024,256]{1,0:T(8,128)S(1)}, u32[]{:S(2)}, u32[]{:S(2)}) %collective-permute-start.4) | collective-permute-done | bytes 1048608 | tf_op jit(solution)/shard_map/ppermute | solution.py:389
  45.2 3.5 %collective-permute-start.5 = (f32[1024,128]{1,0:T(8,128)S(1)}, f32[1024,128]{1,0:T(8,128)S(1)}, u32[]{:S(2)}, u32[]{:S(2)}) collective-permute-start(f32[1024,128]{1,0:T(8,128)S(1)} %get-tuple-element.67.refs_5_.refs_7_), channel_id=1, source_target_pairs={{0,8},{1,9},{2,10},{3,11},{4,12},{5,13},{6,14},{7,15},{8,16},{9,17... | collective-permute-start | bytes 1572872 | tf_op jit(solution)/shard_map/ppermute | solution.py:389
  54.0 4.6 %collective-permute-start.12 = (f32[384,128]{1,0:T(8,128)S(1)}, f32[384,128]{1,0:T(8,128)S(1)}, u32[]{:S(2)}, u32[]{:S(2)}) collective-permute-start(f32[384,128]{1,0:T(8,128)S(1)} %get-tuple-element.74.refs_9_), channel_id=1, source_target_pairs={{0,8},{1,9},{2,10},{3,11},{4,12},{5,13},{6,14},{7,15},{8,16},{9,17... | collective-permute-start | bytes 589832 | tf_op jit(solution)/shard_map/ppermute | solution.py:389
  59.9 3.0 %collective-permute-done.6.refs_4_.refs_6_ = f32[1024,128]{1,0:T(8,128)S(1)} collective-permute-done((f32[1024,128]{1,0:T(8,128)S(1)}, f32[1024,128]{1,0:T(8,128)S(1)}, u32[]{:S(2)}, u32[]{:S(2)}) %collective-permute-start.6) | collective-permute-done | bytes 524320 | tf_op jit(solution)/shard_map/ppermute | solution.py:389
  62.9 1.7 %shard_map.52 = (f32[128,128]{1,0:T(8,128)S(1)}, f32[128,128]{1,0:T(8,128)S(1)}) custom-call(s32[16]{0:T(128)S(1)} %constant_dynamic-update-slice_fusion.f, f32[1024,128]{1,0:T(8,128)S(1)} %collective-permute-done.5.refs_0_.refs_2_, f32[1024,128]{1,0:T(8,128)S(1)} %get-tuple-element.68.refs_1_.refs_3_, f32[1024,128]{1,0:T(8,128)S(1)} %get-tuple-element.69.refs_2_.refs_4_, ...), custom_call_target="tpu_custom_call" | custom-call | tf_op jit(solution)/shard_map/pallas_call | solution.py:52
  65.9 2.3 %collective-permute-start.10 = (f32[128,128]{1,0:T(8,128)S(1)}, f32[128,128]{1,0:T(8,128)S(1)}, u32[]{:S(2)}, u32[]{:S(2)}) collective-permute-start(f32[128,128]{1,0:T(8,128)S(1)} %add.31.refs_0_), channel_id=1, source_target_pairs={{6,0},{7,1},{4,2},{5,3},{2,4},{3,5},{0,6},{1,7},{14,8},{15,9},{12,... | collective-permute-start | bytes 196616 | tf_op jit(solution)/shard_map/ppermute | solution.py:389
  71.2 1.8 %collective-permute-done.9.refs_2_ = f32[128,128]{1,0:T(8,128)S(1)} collective-permute-done((f32[128,128]{1,0:T(8,128)S(1)}, f32[128,128]{1,0:T(8,128)S(1)}, u32[]{:S(2)}, u32[]{:S(2)}) %collective-permute-start.9) | collective-permute-done | bytes 65568 | tf_op jit(solution)/shard_map/ppermute | solution.py:389
  73.4 4.0 %shard_map.55 = (f32[256,256]{1,0:T(8,128)S(1)}, f32[256,256]{1,0:T(8,128)S(1)}) custom-call(s32[16]{0:T(128)S(1)} %constant_dynamic-update-slice_fusion.f, f32[128,128]{1,0:T(8,128)S(1)} %add.31.refs_0_, f32[128,128]{1,0:T(8,128)S(1)} %collective-permute-done.8.refs_1_, f32[128,128]{1,0:T(8,128)S(1)} %collective-permute-done.9.refs_2_, ...), custom_call_target="tpu_custom_call" | custom-call | tf_op jit(solution)/shard_map/pallas_call | solution.py:52
  80.6 3.5 %collective-permute-start.15 = (f32[1024,128]{1,0:T(8,128)S(1)}, f32[1024,128]{1,0:T(8,128)S(1)}, u32[]{:S(2)}, u32[]{:S(2)}) collective-permute-start(f32[1024,128]{1,0:T(8,128)S(1)} %get-tuple-element.79.refs_5_.refs_7_), channel_id=1, source_target_pairs={{0,8},{1,9},{2,10},{3,11},{4,12},{5,13},{6,14},{7,15},{8,16},{9,17... | collective-permute-start | bytes 1572872 | tf_op jit(solution)/shard_map/ppermute | solution.py:389
  89.6 4.6 %collective-permute-start.22 = (f32[384,128]{1,0:T(8,128)S(1)}, f32[384,128]{1,0:T(8,128)S(1)}, u32[]{:S(2)}, u32[]{:S(2)}) collective-permute-start(f32[384,128]{1,0:T(8,128)S(1)} %get-tuple-element.86.refs_9_), channel_id=1, source_target_pairs={{0,8},{1,9},{2,10},{3,11},{4,12},{5,13},{6,14},{7,15},{8,16},{9,17... | collective-permute-start | bytes 589832 | tf_op jit(solution)/shard_map/ppermute | solution.py:389
  96.3 4.4 %collective-permute-done.16.refs_4_.refs_6_ = f32[1024,128]{1,0:T(8,128)S(1)} collective-permute-done((f32[1024,128]{1,0:T(8,128)S(1)}, f32[1024,128]{1,0:T(8,128)S(1)}, u32[]{:S(2)}, u32[]{:S(2)}) %collective-permute-start.16) | collective-permute-done | bytes 524320 | tf_op jit(solution)/shard_map/ppermute | solution.py:389
  100.7 1.7 %shard_map.57 = (f32[128,128]{1,0:T(8,128)S(1)}, f32[128,128]{1,0:T(8,128)S(1)}) custom-call(s32[16]{0:T(128)S(1)} %constant_dynamic-update-slice_fusion.f, f32[1024,128]{1,0:T(8,128)S(1)} %collective-permute-done.15.refs_0_.refs_2_, f32[1024,128]{1,0:T(8,128)S(1)} %get-tuple-element.80.refs_1_.refs_3_, f32[1024,128]{1,0:T(8,128)S(1)} %get-tuple-element.81.refs_2_.refs_4_, ...), custom_call_target="tpu_custom_call" | custom-call | tf_op jit(solution)/shard_map/pallas_call | solution.py:52
  103.8 2.9 %collective-permute-start.20 = (f32[128,128]{1,0:T(8,128)S(1)}, f32[128,128]{1,0:T(8,128)S(1)}, u32[]{:S(2)}, u32[]{:S(2)}) collective-permute-start(f32[128,128]{1,0:T(8,128)S(1)} %add.32.refs_0_), channel_id=1, source_target_pairs={{6,0},{7,1},{4,2},{5,3},{2,4},{3,5},{0,6},{1,7},{14,8},{15,9},{12,... | collective-permute-start | bytes 196616 | tf_op jit(solution)/shard_map/ppermute | solution.py:389
  107.4 1.7 collective-permute-done.20.refs_3_
  109.1 1.9 %collective-permute-done.19.refs_2_ = f32[128,128]{1,0:T(8,128)S(1)} collective-permute-done((f32[128,128]{1,0:T(8,128)S(1)}, f32[128,128]{1,0:T(8,128)S(1)}, u32[]{:S(2)}, u32[]{:S(2)}) %collective-permute-start.19) | collective-permute-done | bytes 65568 | tf_op jit(solution)/shard_map/ppermute | solution.py:389
  111.0 4.0 %shard_map.60 = (f32[256,256]{1,0:T(8,128)S(1)}, f32[256,256]{1,0:T(8,128)S(1)}) custom-call(s32[16]{0:T(128)S(1)} %constant_dynamic-update-slice_fusion.f, f32[128,128]{1,0:T(8,128)S(1)} %add.32.refs_0_, f32[128,128]{1,0:T(8,128)S(1)} %collective-permute-done.18.refs_1_, f32[128,128]{1,0:T(8,128)S(1)} %collective-permute-done.19.refs_2_, ...), custom_call_target="tpu_custom_call" | custom-call | tf_op jit(solution)/shard_map/pallas_call | solution.py:52
  118.2 3.4 %collective-permute-start.25 = (f32[1024,128]{1,0:T(8,128)S(1)}, f32[1024,128]{1,0:T(8,128)S(1)}, u32[]{:S(2)}, u32[]{:S(2)}) collective-permute-start(f32[1024,128]{1,0:T(8,128)S(1)} %get-tuple-element.103.refs_3_.refs_5_.refs_7_), channel_id=1, source_target_pairs={{0,8},{1,9},{2,10},{3,11},{4,12},{5,13},{6,14},{7,15},{8,16},{9,17... | collective-permute-start | bytes 1572872 | tf_op jit(solution)/shard_map/ppermute | solution.py:389
  122.9 2.1 %collective-permute-start.27 = (f32[1024,128]{1,0:T(8,128)S(1)}, f32[1024,128]{1,0:T(8,128)S(1)}, u32[]{:S(2)}, u32[]{:S(2)}) collective-permute-start(f32[1024,128]{1,0:T(8,128)S(1)} %get-tuple-element.95), channel_id=1, source_target_pairs={{4,0},{5,1},{6,2},{7,3},{0,4},{1,5},{2,6},{3,7},{12,8},{13,9},{14,... | collective-permute-start | bytes 1572872 | tf_op jit(solution)/shard_map/ppermute | solution.py:389
  129.1 4.5 %collective-permute-start.35 = (f32[384,128]{1,0:T(8,128)S(1)}, f32[384,128]{1,0:T(8,128)S(1)}, u32[]{:S(2)}, u32[]{:S(2)}) collective-permute-start(f32[384,128]{1,0:T(8,128)S(1)} %get-tuple-element.107.refs_7_.refs_9_.refs_13_), channel_id=1, source_target_pairs={{0,8},{1,9},{2,10},{3,11},{4,12},{5,13},{6,14},{7,15},{8,16},{9,17... | collective-permute-start | bytes 589832 | tf_op jit(solution)/shard_map/ppermute | solution.py:389
  133.7 3.5 %collective-permute-done.26.refs_2_.refs_4_.refs_6_ = f32[1024,128]{1,0:T(8,128)S(1)} collective-permute-done((f32[1024,128]{1,0:T(8,128)S(1)}, f32[1024,128]{1,0:T(8,128)S(1)}, u32[]{:S(2)}, u32[]{:S(2)}) %collective-permute-start.26) | collective-permute-done | bytes 524320 | tf_op jit(solution)/shard_map/ppermute | solution.py:389
  137.8 1.9 %collective-permute-done.29.refs_15_ = f32[256,128]{1,0:T(8,128)S(1)} collective-permute-done((f32[256,128]{1,0:T(8,128)S(1)}, f32[256,128]{1,0:T(8,128)S(1)}, u32[]{:S(2)}, u32[]{:S(2)}) %collective-permute-start.29) | collective-permute-done | bytes 131104 | tf_op jit(solution)/shard_map/ppermute | solution.py:389
  139.7 1.7 %collective-permute-start.34 = (f32[512,128]{1,0:T(8,128)S(1)}, f32[512,128]{1,0:T(8,128)S(1)}, u32[]{:S(2)}, u32[]{:S(2)}) collective-permute-start(f32[512,128]{1,0:T(8,128)S(1)} %shard_map.64), channel_id=1, source_target_pairs={{4,0},{5,1},{6,2},{7,3},{0,4},{1,5},{2,6},{3,7},{12,8},{13,9},{14,... | collective-permute-start | bytes 786440 | tf_op jit(solution)/shard_map/ppermute | solution.py:389
  142.8 1.7 %shard_map.65 = (f32[128,128]{1,0:T(8,128)S(1)}, f32[128,128]{1,0:T(8,128)S(1)}) custom-call(s32[16]{0:T(128)S(1)} %constant_dynamic-update-slice_fusion.f, f32[1024,128]{1,0:T(8,128)S(1)} %collective-permute-done.25.refs_0_.refs_2_, f32[1024,128]{1,0:T(8,128)S(1)} %get-tuple-element.99.refs_1_.refs_3_, f32[1024,128]{1,0:T(8,128)S(1)} %get-tuple-element.100.refs_2_.refs_4_, ...), custom_call_target="tpu_custom_call" | custom-call | tf_op jit(solution)/shard_map/pallas_call | solution.py:52
  146.4 1.7 %collective-permute-start.32 = (f32[128,128]{1,0:T(8,128)S(1)}, f32[128,128]{1,0:T(8,128)S(1)}, u32[]{:S(2)}, u32[]{:S(2)}) collective-permute-start(f32[128,128]{1,0:T(8,128)S(1)} %add.33.refs_0_), channel_id=1, source_target_pairs={{4,0},{5,1},{6,2},{7,3},{0,4},{1,5},{2,6},{3,7},{12,8},{13,9},{14,... | collective-permute-start | bytes 196616 | tf_op jit(solution)/shard_map/ppermute | solution.py:389
  152.7 4.0 %shard_map.67 = (f32[264,256]{1,0:T(8,128)S(1)}, f32[256,256]{1,0:T(8,128)}) custom-call(s32[16]{0:T(128)S(1)} %constant_dynamic-update-slice_fusion.f, f32[128,128]{1,0:T(8,128)S(1)} %add.33.refs_0_, f32[128,128]{1,0:T(8,128)S(1)} %collective-permute-done.31.refs_1_, f32[128,128]{1,0:T(8,128)S(1)} %collective-permute-done.32.refs_2_, ...), custom_call_target="tpu_custom_call" | custom-call | tf_op jit(solution)/shard_map/pallas_call | solution.py:52
  158.3 4.5 %collective-permute-done.38.refs_17_ = f32[768,128]{1,0:T(8,128)S(1)} collective-permute-done((f32[768,128]{1,0:T(8,128)S(1)}, f32[768,128]{1,0:T(8,128)S(1)}, u32[]{:S(2)}, u32[]{:S(2)}) %collective-permute-start.38) | collective-permute-done | bytes 393248 | tf_op jit(solution)/shard_map/ppermute | solution.py:389
  162.8 3.4 %shard_map.68 = (f32[2048,256]{1,0:T(8,128)}, f32[512,256]{1,0:T(8,128)}, f32[1,256]{1,0:T(1,128)}) custom-call(s32[16]{0:T(128)S(1)} %constant_dynamic-update-slice_fusion.f, f32[264,256]{1,0:T(8,128)S(1)} %get-tuple-element.115.refs_0_, f32[264,256]{1,0:T(8,128)S(1)} %collective-permute-done.37.refs_1_, ...), custom_call_target="tpu_custom_call" | custom-call | tf_op jit(solution)/shard_map/pallas_call | solution.py:52
  (76 shorter events, 51.7 us)
Async XLA Ops:
  7.4 9.0 %collective-permute-start.2 = (f32[384,128]{1,0:T(8,128)S(1)}, f32[384,128]{1,0:T(8,128)S(1)}, u32[]{:S(2)}, u32[]{:S(2)}) collective-permute-start(f32[384,128]{1,0:T(8,128)S(1)} %add.30.own_ref), channel_id=1, source_target_pairs={{7,1},{5,3},{2,4},{0,6},{15,9},{13,11},{10,12},{8,14},{23,17},{21,... | collective-permute-start | bytes 589832 | tf_op jit(solution)/shard_map/ppermute | solution.py:389
  13.1 5.8 %collective-permute-start.1 = (f32[384,128]{1,0:T(8,128)S(1)}, f32[384,128]{1,0:T(8,128)S(1)}, u32[]{:S(2)}, u32[]{:S(2)}) collective-permute-start(f32[384,128]{1,0:T(8,128)S(1)} %add.30.own_ref), channel_id=1, source_target_pairs={{2,0},{4,1},{0,2},{6,3},{1,4},{7,5},{3,6},{5,7},{10,8},{12,9},{8,1... | collective-permute-start | bytes 589832 | tf_op jit(solution)/shard_map/ppermute | solution.py:389
  18.9 24.7 %collective-permute-start.4 = (f32[1024,256]{1,0:T(8,128)S(1)}, f32[1024,256]{1,0:T(8,128)S(1)}, u32[]{:S(2)}, u32[]{:S(2)}) collective-permute-start(f32[1024,256]{1,0:T(8,128)S(1)} %get-tuple-element.66), channel_id=1, source_target_pairs={{4,0},{5,1},{6,2},{7,3},{0,4},{1,5},{2,6},{3,7},{12,8},{13,9},{14,... | collective-permute-start | bytes 3145736 | tf_op jit(solution)/shard_map/ppermute | solution.py:389
  24.3 1.6 collective-permute-start.3
  45.2 14.8 %collective-permute-start.5 = (f32[1024,128]{1,0:T(8,128)S(1)}, f32[1024,128]{1,0:T(8,128)S(1)}, u32[]{:S(2)}, u32[]{:S(2)}) collective-permute-start(f32[1024,128]{1,0:T(8,128)S(1)} %get-tuple-element.67.refs_5_.refs_7_), channel_id=1, source_target_pairs={{0,8},{1,9},{2,10},{3,11},{4,12},{5,13},{6,14},{7,15},{8,16},{9,17... | collective-permute-start | bytes 1572872 | tf_op jit(solution)/shard_map/ppermute | solution.py:389
  48.7 14.2 %collective-permute-start.6 = (f32[1024,128]{1,0:T(8,128)S(1)}, f32[1024,128]{1,0:T(8,128)S(1)}, u32[]{:S(2)}, u32[]{:S(2)}) collective-permute-start(f32[1024,128]{1,0:T(8,128)S(1)} %get-tuple-element.68.refs_1_.refs_3_), channel_id=1, source_target_pairs={{8,0},{9,1},{10,2},{11,3},{12,4},{13,5},{14,6},{15,7},{16,8},{17,9... | collective-permute-start | bytes 1572872 | tf_op jit(solution)/shard_map/ppermute | solution.py:389
  54.0 16.5 %collective-permute-start.12 = (f32[384,128]{1,0:T(8,128)S(1)}, f32[384,128]{1,0:T(8,128)S(1)}, u32[]{:S(2)}, u32[]{:S(2)}) collective-permute-start(f32[384,128]{1,0:T(8,128)S(1)} %get-tuple-element.74.refs_9_), channel_id=1, source_target_pairs={{0,8},{1,9},{2,10},{3,11},{4,12},{5,13},{6,14},{7,15},{8,16},{9,17... | collective-permute-start | bytes 589832 | tf_op jit(solution)/shard_map/ppermute | solution.py:389
  58.6 11.9 %collective-permute-start.13 = (f32[384,128]{1,0:T(8,128)S(1)}, f32[384,128]{1,0:T(8,128)S(1)}, u32[]{:S(2)}, u32[]{:S(2)}) collective-permute-start(f32[384,128]{1,0:T(8,128)S(1)} %get-tuple-element.75.refs_5_), channel_id=1, source_target_pairs={{8,0},{9,1},{10,2},{11,3},{12,4},{13,5},{14,6},{15,7},{16,8},{17,9... | collective-permute-start | bytes 589832 | tf_op jit(solution)/shard_map/ppermute | solution.py:389
  65.9 5.2 %collective-permute-start.10 = (f32[128,128]{1,0:T(8,128)S(1)}, f32[128,128]{1,0:T(8,128)S(1)}, u32[]{:S(2)}, u32[]{:S(2)}) collective-permute-start(f32[128,128]{1,0:T(8,128)S(1)} %add.31.refs_0_), channel_id=1, source_target_pairs={{6,0},{7,1},{4,2},{5,3},{2,4},{3,5},{0,6},{1,7},{14,8},{15,9},{12,... | collective-permute-start | bytes 196616 | tf_op jit(solution)/shard_map/ppermute | solution.py:389
  68.2 4.7 %collective-permute-start.9 = (f32[128,128]{1,0:T(8,128)S(1)}, f32[128,128]{1,0:T(8,128)S(1)}, u32[]{:S(2)}, u32[]{:S(2)}) collective-permute-start(f32[128,128]{1,0:T(8,128)S(1)} %add.31.refs_0_), channel_id=1, source_target_pairs={{4,0},{5,1},{6,2},{7,3},{0,4},{1,5},{2,6},{3,7},{12,8},{13,9},{14,... | collective-permute-start | bytes 196616 | tf_op jit(solution)/shard_map/ppermute | solution.py:389
  69.2 4.3 %collective-permute-start.8 = (f32[128,128]{1,0:T(8,128)S(1)}, f32[128,128]{1,0:T(8,128)S(1)}, u32[]{:S(2)}, u32[]{:S(2)}) collective-permute-start(f32[128,128]{1,0:T(8,128)S(1)} %add.31.refs_0_), channel_id=1, source_target_pairs={{2,0},{3,1},{0,2},{1,3},{6,4},{7,5},{4,6},{5,7},{10,8},{11,9},{8,1... | collective-permute-start | bytes 196616 | tf_op jit(solution)/shard_map/ppermute | solution.py:389
  77.4 1.6 collective-permute-start.14
  80.6 15.7 %collective-permute-start.15 = (f32[1024,128]{1,0:T(8,128)S(1)}, f32[1024,128]{1,0:T(8,128)S(1)}, u32[]{:S(2)}, u32[]{:S(2)}) collective-permute-start(f32[1024,128]{1,0:T(8,128)S(1)} %get-tuple-element.79.refs_5_.refs_7_), channel_id=1, source_target_pairs={{0,8},{1,9},{2,10},{3,11},{4,12},{5,13},{6,14},{7,15},{8,16},{9,17... | collective-permute-start | bytes 1572872 | tf_op jit(solution)/shard_map/ppermute | solution.py:389
  84.1 16.6 %collective-permute-start.16 = (f32[1024,128]{1,0:T(8,128)S(1)}, f32[1024,128]{1,0:T(8,128)S(1)}, u32[]{:S(2)}, u32[]{:S(2)}) collective-permute-start(f32[1024,128]{1,0:T(8,128)S(1)} %get-tuple-element.80.refs_1_.refs_3_), channel_id=1, source_target_pairs={{8,0},{9,1},{10,2},{11,3},{12,4},{13,5},{14,6},{15,7},{16,8},{17,9... | collective-permute-start | bytes 1572872 | tf_op jit(solution)/shard_map/ppermute | solution.py:389
  89.6 17.8 %collective-permute-start.22 = (f32[384,128]{1,0:T(8,128)S(1)}, f32[384,128]{1,0:T(8,128)S(1)}, u32[]{:S(2)}, u32[]{:S(2)}) collective-permute-start(f32[384,128]{1,0:T(8,128)S(1)} %get-tuple-element.86.refs_9_), channel_id=1, source_target_pairs={{0,8},{1,9},{2,10},{3,11},{4,12},{5,13},{6,14},{7,15},{8,16},{9,17... | collective-permute-start | bytes 589832 | tf_op jit(solution)/shard_map/ppermute | solution.py:389
  94.2 13.2 %collective-permute-start.23 = (f32[384,128]{1,0:T(8,128)S(1)}, f32[384,128]{1,0:T(8,128)S(1)}, u32[]{:S(2)}, u32[]{:S(2)}) collective-permute-start(f32[384,128]{1,0:T(8,128)S(1)} %get-tuple-element.87.refs_5_), channel_id=1, source_target_pairs={{8,0},{9,1},{10,2},{11,3},{12,4},{13,5},{14,6},{15,7},{16,8},{17,9... | collective-permute-start | bytes 589832 | tf_op jit(solution)/shard_map/ppermute | solution.py:389
  103.8 5.3 %collective-permute-start.20 = (f32[128,128]{1,0:T(8,128)S(1)}, f32[128,128]{1,0:T(8,128)S(1)}, u32[]{:S(2)}, u32[]{:S(2)}) collective-permute-start(f32[128,128]{1,0:T(8,128)S(1)} %add.32.refs_0_), channel_id=1, source_target_pairs={{6,0},{7,1},{4,2},{5,3},{2,4},{3,5},{0,6},{1,7},{14,8},{15,9},{12,... | collective-permute-start | bytes 196616 | tf_op jit(solution)/shard_map/ppermute | solution.py:389
  106.7 4.3 %collective-permute-start.19 = (f32[128,128]{1,0:T(8,128)S(1)}, f32[128,128]{1,0:T(8,128)S(1)}, u32[]{:S(2)}, u32[]{:S(2)}) collective-permute-start(f32[128,128]{1,0:T(8,128)S(1)} %add.32.refs_0_), channel_id=1, source_target_pairs={{4,0},{5,1},{6,2},{7,3},{0,4},{1,5},{2,6},{3,7},{12,8},{13,9},{14,... | collective-permute-start | bytes 196616 | tf_op jit(solution)/shard_map/ppermute | solution.py:389
  106.7 4.3 %collective-permute-start.18 = (f32[128,128]{1,0:T(8,128)S(1)}, f32[128,128]{1,0:T(8,128)S(1)}, u32[]{:S(2)}, u32[]{:S(2)}) collective-permute-start(f32[128,128]{1,0:T(8,128)S(1)} %add.32.refs_0_), channel_id=1, source_target_pairs={{2,0},{3,1},{0,2},{1,3},{6,4},{7,5},{4,6},{5,7},{10,8},{11,9},{8,1... | collective-permute-start | bytes 196616 | tf_op jit(solution)/shard_map/ppermute | solution.py:389
  115.0 1.6 collective-permute-start.24
  118.2 15.5 %collective-permute-start.25 = (f32[1024,128]{1,0:T(8,128)S(1)}, f32[1024,128]{1,0:T(8,128)S(1)}, u32[]{:S(2)}, u32[]{:S(2)}) collective-permute-start(f32[1024,128]{1,0:T(8,128)S(1)} %get-tuple-element.103.refs_3_.refs_5_.refs_7_), channel_id=1, source_target_pairs={{0,8},{1,9},{2,10},{3,11},{4,12},{5,13},{6,14},{7,15},{8,16},{9,17... | collective-permute-start | bytes 1572872 | tf_op jit(solution)/shard_map/ppermute | solution.py:389
  121.6 15.6 %collective-permute-start.26 = (f32[1024,128]{1,0:T(8,128)S(1)}, f32[1024,128]{1,0:T(8,128)S(1)}, u32[]{:S(2)}, u32[]{:S(2)}) collective-permute-start(f32[1024,128]{1,0:T(8,128)S(1)} %get-tuple-element.99.refs_1_.refs_3_), channel_id=1, source_target_pairs={{8,0},{9,1},{10,2},{11,3},{12,4},{13,5},{14,6},{15,7},{16,8},{17,9... | collective-permute-start | bytes 1572872 | tf_op jit(solution)/shard_map/ppermute | solution.py:389
  122.9 16.8 %collective-permute-start.27 = (f32[1024,128]{1,0:T(8,128)S(1)}, f32[1024,128]{1,0:T(8,128)S(1)}, u32[]{:S(2)}, u32[]{:S(2)}) collective-permute-start(f32[1024,128]{1,0:T(8,128)S(1)} %get-tuple-element.95), channel_id=1, source_target_pairs={{4,0},{5,1},{6,2},{7,3},{0,4},{1,5},{2,6},{3,7},{12,8},{13,9},{14,... | collective-permute-start | bytes 1572872 | tf_op jit(solution)/shard_map/ppermute | solution.py:389
  129.0 10.7 %collective-permute-start.29 = (f32[256,128]{1,0:T(8,128)S(1)}, f32[256,128]{1,0:T(8,128)S(1)}, u32[]{:S(2)}, u32[]{:S(2)}) collective-permute-start(f32[256,128]{1,0:T(8,128)S(1)} %get-tuple-element.97), channel_id=1, source_target_pairs={{4,0},{5,1},{6,2},{7,3},{0,4},{1,5},{2,6},{3,7},{12,8},{13,9},{14,... | collective-permute-start | bytes 393224 | tf_op jit(solution)/shard_map/ppermute | solution.py:389
  129.1 19.0 %collective-permute-start.35 = (f32[384,128]{1,0:T(8,128)S(1)}, f32[384,128]{1,0:T(8,128)S(1)}, u32[]{:S(2)}, u32[]{:S(2)}) collective-permute-start(f32[384,128]{1,0:T(8,128)S(1)} %get-tuple-element.107.refs_7_.refs_9_.refs_13_), channel_id=1, source_target_pairs={{0,8},{1,9},{2,10},{3,11},{4,12},{5,13},{6,14},{7,15},{8,16},{9,17... | collective-permute-start | bytes 589832 | tf_op jit(solution)/shard_map/ppermute | solution.py:389
  139.7 12.7 %collective-permute-start.34 = (f32[512,128]{1,0:T(8,128)S(1)}, f32[512,128]{1,0:T(8,128)S(1)}, u32[]{:S(2)}, u32[]{:S(2)}) collective-permute-start(f32[512,128]{1,0:T(8,128)S(1)} %shard_map.64), channel_id=1, source_target_pairs={{4,0},{5,1},{6,2},{7,3},{0,4},{1,5},{2,6},{3,7},{12,8},{13,9},{14,... | collective-permute-start | bytes 786440 | tf_op jit(solution)/shard_map/ppermute | solution.py:389
  141.5 7.9 %collective-permute-start.36 = (f32[384,128]{1,0:T(8,128)S(1)}, f32[384,128]{1,0:T(8,128)S(1)}, u32[]{:S(2)}, u32[]{:S(2)}) collective-permute-start(f32[384,128]{1,0:T(8,128)S(1)} %get-tuple-element.108.refs_5_.refs_9_), channel_id=1, source_target_pairs={{8,0},{9,1},{10,2},{11,3},{12,4},{13,5},{14,6},{15,7},{16,8},{17,9... | collective-permute-start | bytes 589832 | tf_op jit(solution)/shard_map/ppermute | solution.py:389
  145.8 5.8 %collective-permute-start.33 = (f32[128,128]{1,0:T(8,128)S(1)}, f32[128,128]{1,0:T(8,128)S(1)}, u32[]{:S(2)}, u32[]{:S(2)}) collective-permute-start(f32[128,128]{1,0:T(8,128)S(1)} %add.33.refs_0_), channel_id=1, source_target_pairs={{6,0},{7,1},{4,2},{5,3},{2,4},{3,5},{0,6},{1,7},{14,8},{15,9},{12,... | collective-permute-start | bytes 196616 | tf_op jit(solution)/shard_map/ppermute | solution.py:389
  146.4 5.3 %collective-permute-start.32 = (f32[128,128]{1,0:T(8,128)S(1)}, f32[128,128]{1,0:T(8,128)S(1)}, u32[]{:S(2)}, u32[]{:S(2)}) collective-permute-start(f32[128,128]{1,0:T(8,128)S(1)} %add.33.refs_0_), channel_id=1, source_target_pairs={{4,0},{5,1},{6,2},{7,3},{0,4},{1,5},{2,6},{3,7},{12,8},{13,9},{14,... | collective-permute-start | bytes 196616 | tf_op jit(solution)/shard_map/ppermute | solution.py:389
  148.1 4.3 %collective-permute-start.31 = (f32[128,128]{1,0:T(8,128)S(1)}, f32[128,128]{1,0:T(8,128)S(1)}, u32[]{:S(2)}, u32[]{:S(2)}) collective-permute-start(f32[128,128]{1,0:T(8,128)S(1)} %add.33.refs_0_), channel_id=1, source_target_pairs={{2,0},{3,1},{0,2},{1,3},{6,4},{7,5},{4,6},{5,7},{10,8},{11,9},{8,1... | collective-permute-start | bytes 196616 | tf_op jit(solution)/shard_map/ppermute | solution.py:389
  152.4 10.4 %collective-permute-start.38 = (f32[768,128]{1,0:T(8,128)S(1)}, f32[768,128]{1,0:T(8,128)S(1)}, u32[]{:S(2)}, u32[]{:S(2)}) collective-permute-start(f32[768,128]{1,0:T(8,128)S(1)} %shard_map.66), channel_id=1, source_target_pairs={{4,0},{5,1},{6,2},{7,3},{0,4},{1,5},{2,6},{3,7},{12,8},{13,9},{14,... | collective-permute-start | bytes 1179656 | tf_op jit(solution)/shard_map/ppermute | solution.py:389
  156.7 1.6 collective-permute-start.37
  (9 other events, 51.8 us)

commit v3 on v2

v3 whole, which is shorter than its diff:
```python
import jax
import jax.numpy as jnp
from jax import lax
from jax.experimental import pallas as pl
from jax.experimental.pallas import tpu as pltpu
from jax.sharding import PartitionSpec as P

ROUNDS = 4
NEWTON = 16

highest = lax.Precision.HIGHEST

TARGET = 2.0**-12
BOUNDS = [
    (1.0 + TARGET ** (2.0**-j)) / (1.0 - TARGET ** (2.0**-j)) for j in range(NEWTON)
]

X, CORE, FIRST, LAST, VROW, LABEL, EVEN = 0, 1, 2, 3, 4, 5, 9


def dot(a, b, precision=highest):
    return lax.dot_general(
        a, b, (((1,), (0,)), ((), ())), precision=precision,
        preferred_element_type=jnp.float32,
    )


def split(a):
    high = a.astype(jnp.bfloat16)
    return high, (a - high.astype(jnp.float32)).astype(jnp.bfloat16)


def dot3(a, b):
    a_high, a_low = a if isinstance(a, tuple) else split(a)
    b_high, b_low = b if isinstance(b, tuple) else split(b)
    small = dot(a_high, b_low, None) + dot(a_low, b_high, None)
    return dot(a_high, b_high, None) + small


def dot_tn(a, b):
    return lax.dot_general(
        a, b, (((0,), (0,)), ((), ())), precision=highest,
        preferred_element_type=jnp.float32,
    )


def shape(*dims):
    return jax.ShapeDtypeStruct(dims, jnp.float32)


def call(body, facts, inputs, outs, scratch=(), limit=24):
    return pl.pallas_call(
        body,
        out_shape=outs,
        in_specs=[pl.BlockSpec(memory_space=pltpu.SMEM)]
        + [pl.BlockSpec(memory_space=pltpu.VMEM)] * len(inputs),
        out_specs=jax.tree.map(
            lambda _: pl.BlockSpec(memory_space=pltpu.VMEM), outs
        ),
        scratch_shapes=list(scratch),
        compiler_params=pltpu.CompilerParams(vmem_limit_bytes=limit << 20),
    )(facts, *inputs)


def first_gram(facts, sector, half, top):
    rows, width = sector.shape
    part = rows // 2

    def body(f, x_ref, out_ref, give_ref):
        x = x_ref[...]
        g = dot_tn(x, x)
        out_ref[:half] = g[:half, :half]
        out_ref[half : 2 * half] = g[:half, half:]
        out_ref[2 * half :] = g[half:, half:]
        there = pl.multiple_of((1 - f[X]) * part + top, 8)
        give_ref[...] = x_ref[pl.ds(there, part - top)]

    return call(
        body, facts, [sector], (shape(3 * half, half), shape(part - top, width))
    )


def rotate_of(gram, x_ref, e_ref):
    size = gram.shape[0]
    rows = lax.broadcasted_iota(jnp.int32, (size, size), 0)
    cols = lax.broadcasted_iota(jnp.int32, (size, size), 1)
    identity = (rows == cols).astype(jnp.float32)
    only = jnp.where(rows == cols, gram, 0.0)
    g_j = jnp.sum(only, axis=0, keepdims=True)
    g_i = jnp.sum(only, axis=1, keepdims=True)
    spread = g_j - g_i
    summed = g_j + g_i
    skew = gram * spread / (spread * spread + 2.0 * gram * gram + 0.01 * summed * summed)
    bound = 1.0 + 0.25 * jnp.sum(skew * skew)
    steps = jnp.int32(0)
    for limit in BOUNDS:
        steps = steps + (bound > limit).astype(jnp.int32)
    fixes = 1 + (steps > 7).astype(jnp.int32) + 2 * (steps > 9).astype(jnp.int32)
    scale = 2.0 / (1.0 + jnp.full((size, size), bound, jnp.float32))
    skew_parts = split(skew)
    residual = identity - scale * (identity - 0.25 * dot3(skew_parts, skew_parts))
    x_ref[...] = scale * (identity + residual)
    residual_parts = split(residual)
    e_ref[...] = dot3(residual_parts, residual_parts)

    def step(_, carry):
        e = split(e_ref[...])
        x = x_ref[...]
        x_ref[...] = x + dot3(x, e)
        e_ref[...] = dot3(e, e)
        return carry

    lax.fori_loop(0, jnp.maximum(steps - 1, 0), step, jnp.int32(0))
    x = x_ref[...]
    x_ref[...] = x + 0.5 * dot3(x, skew_parts)

    def fix(_, carry):
        x = x_ref[...]
        x_ref[...] = x + dot3(x, identity - (x - 0.5 * dot(skew, x)))
        return carry

    lax.fori_loop(0, fixes, fix, jnp.int32(0))
    return 2.0 * x_ref[...] - identity


def put_rotation(rotation_ref, gram, x_ref, e_ref, last_round):
    size = gram.shape[0]
    rotation = rotate_of(gram, x_ref, e_ref)
    rotation_ref[:size] = rotation
    if last_round:
        squares = jnp.sum(rotation * dot(gram, rotation), axis=0, keepdims=True)
        rotation_ref[size:] = jnp.broadcast_to(squares, (8, size))


def first_rotation(facts, own, near, far, half):
    size = 2 * half

    def body(f, own_ref, near_ref, far_ref, rotation_ref, g_ref, x_ref, e_ref):
        mine = f[X] == f[CORE]
        total = near_ref[...] + jnp.where(mine, own_ref[...], far_ref[...])
        g_ref[:half, :half] = total[:half]
        g_ref[:half, half:] = total[half : 2 * half]
        g_ref[half:, :half] = total[half : 2 * half].T
        g_ref[half:, half:] = total[2 * half :]
        put_rotation(rotation_ref, g_ref[...], x_ref, e_ref, False)

    square = pltpu.VMEM((size, size), jnp.float32)
    return call(
        body, facts, [own, near, far], (shape(size, size),) * 2, [square] * 2
    )


def later_rotation(facts, parts, diagonals, half, last_round):
    size = 2 * half

    def body(f, *refs):
        own, other_y, other_x, other_xy, foreign, native = [r[...] for r in refs[:6]]
        rotation_ref, g_ref, x_ref, e_ref = refs[6:]
        cross = (own + other_y) + (other_x + other_xy)
        core = f[CORE] == 0
        g_ref[:half, :half] = jnp.where(core, foreign, native)
        g_ref[:half, half:] = cross
        g_ref[half:, :half] = cross.T
        g_ref[half:, half:] = jnp.where(core, native, foreign)
        put_rotation(rotation_ref, g_ref[...], x_ref, e_ref, last_round)

    square = pltpu.VMEM((size, size), jnp.float32)
    return call(
        body,
        facts,
        parts + diagonals,
        (shape(size + 8 if last_round else size, size), shape(size, size)),
        [square] * 2,
    )


def turned_gram(facts, gram, rotation):
    size = gram.shape[0]
    half = size // 2

    def body(f, gram_ref, rotation_ref, leave_ref, stay_ref):
        rotation = rotation_ref[...]
        turned = dot(gram_ref[...], rotation)
        upper = dot_tn(rotation[:, :half], turned[:, :half])
        lower = dot_tn(rotation[:, half:], turned[:, half:])
        lower_leaves = (f[CORE] == 0) & (f[FIRST] == 0)
        leave_ref[...] = jnp.where(lower_leaves, lower, upper)
        stay_ref[...] = jnp.where(lower_leaves, upper, lower)

    return call(body, facts, [gram, rotation], (shape(half, half),) * 2)


def two_packs(f, own, other):
    core = f[CORE] == 0
    return jnp.where(core, own, other), jnp.where(core, other, own)


def swapped(flag, matrix, axis):
    half = matrix.shape[axis] // 2
    a = lax.slice_in_dim(matrix, 0, half, axis=axis)
    b = lax.slice_in_dim(matrix, half, 2 * half, axis=axis)
    return jnp.where(flag, lax.concatenate([b, a], axis), matrix)


def blocks_of(f, got_a, got_b, low_0, up_1):
    even = f[EVEN] == 1
    return (
        jnp.where(even, got_b, got_a), low_0, up_1, jnp.where(even, got_a, got_b)
    )


def put_turned(f, refs, zero, one, half):
    a_ref, b_ref, nat_l_ref, nat_u_ref = refs[:4]
    even = f[EVEN] == 1
    to_left, to_right = zero[:, half:], one[:, :half]
    a_ref[...] = jnp.where(even, to_right, to_left)
    b_ref[...] = jnp.where(even, to_left, to_right)
    nat_l_ref[...] = one[:, half:]
    nat_u_ref[...] = zero[:, :half]
    if len(refs) > 4:
        refs[4][...] = jnp.where(f[X] == 0, zero[:, :half], one[:, half:])


def turns_of(f, own_ref, other_ref):
    size = other_ref.shape[1]
    turn_0, turn_1 = two_packs(f, own_ref[:size], other_ref[:size])
    return swapped(f[FIRST] == 1, turn_0, 1), turn_1


def turn_rows(facts, packs, rows_of, vector_rows, half, own):
    size = 2 * half
    rows = rows_of.shape[0] // 2 if own else rows_of.shape[0]

    def body(f, own_ref, other_ref, x_ref, stay_ref, leave_ref):
        turn_0, turn_1 = turns_of(f, own_ref, other_ref)
        zero = f[X] == (0 if own else 1)
        turn = split(jnp.where(zero, turn_0, swapped(True, turn_1, 1)))
        here = pl.multiple_of(f[X] * rows, 8)
        out = dot3(x_ref[pl.ds(here, rows)] if own else x_ref[...], turn)
        stay_ref[:rows] = out[:, :half]
        leave_ref[:rows] = out[:, half:]
        if vector_rows:
            ids = f[VROW] + lax.broadcasted_iota(jnp.int32, (vector_rows, half), 0)
            cols = lax.broadcasted_iota(jnp.int32, (vector_rows, half), 1)
            position = jnp.where(zero, 0, 2)
            vectors = [
                (ids == f[LABEL + position + k] * half + cols).astype(jnp.float32)
                for k in range(2)
            ]
            out = dot3(lax.concatenate(vectors, 1), turn)
            stay_ref[rows:] = out[:, :half]
            leave_ref[rows:] = out[:, half:]

    return call(
        body, facts, packs + [rows_of], (shape(rows + vector_rows, half),) * 2
    )


def turn(facts, packs, blocks, half, last_move):
    rows = blocks[0].shape[0]

    def body(f, own_ref, other_ref, *refs):
        turn_0, turn_1 = turns_of(f, own_ref, other_ref)
        up_0, low_0, up_1, low_1 = [r[...] for r in refs[:4]]
        zero = dot3(lax.concatenate([up_0, low_0], 1), turn_0)
        one = dot3(lax.concatenate([up_1, low_1], 1), turn_1)
        put_turned(f, refs[4:], zero, one, half)

    outs = (shape(rows, half),) * (5 if last_move else 4)
    return call(body, facts, packs + blocks, outs)


def put_cross(f, refs, zero, one):
    core = f[CORE] == 0
    refs[0][...] = jnp.where(core, zero, one)
    refs[1][...] = jnp.where(core, one, zero)


def first_cross_gram(facts, own, others, part, half):
    rows = own[0].shape[0]
    pieces = len(others)

    def body(f, *refs):
        own_refs = [[r] for r in refs[:3]]
        other_refs = [refs[3 + k : 3 + 3 * pieces : 3] for k in range(3)]
        up_0, low_0, up_1, low_1 = refs[5 + 3 * pieces :]

        def fill(target, sources):
            at = 0
            for ref in sources:
                target[at : at + ref.shape[0]] = ref[...]
                at += ref.shape[0]

        first, last = f[FIRST] == 1, f[LAST] == 1
        for x, near, far in ((0, own_refs, other_refs), (1, other_refs, own_refs)):
            here = f[X] == x

            @pl.when(here)
            def _():
                fill(up_1, near[0])
                fill(low_0, far[0])

            @pl.when(here & first)
            def _():
                fill(up_0, near[1])

            @pl.when(here & ~first)
            def _():
                fill(up_0, far[2])

            @pl.when(here & last)
            def _():
                fill(low_1, far[1])

            @pl.when(here & ~last)
            def _():
                fill(low_1, near[2])

        put_cross(
            f,
            refs[3 + 3 * pieces :],
            dot_tn(up_0[:part], low_0[:part]),
            dot_tn(up_1[:part], low_1[:part]),
        )

    outs = (shape(half, half),) * 2 + (shape(rows, half),) * 4
    return call(body, facts, own + sum(others, []), outs)


def cross_gram(facts, got, natives, part, half):
    rows = got[0].shape[0]

    def body(f, *refs):
        up_0, low_0, up_1, low_1 = blocks_of(f, *[r[...] for r in refs[:4]])
        put_cross(
            f,
            refs[4:],
            dot_tn(up_0[:part], low_0[:part]),
            dot_tn(up_1[:part], low_1[:part]),
        )
        refs[6][...] = up_0
        refs[7][...] = low_1

    outs = (shape(half, half),) * 2 + (shape(rows, half),) * 2
    return call(body, facts, got + natives, outs)


def give(facts, got, start, stop, half):
    def body(f, a_ref, b_ref, out_ref):
        mine = f[X] != f[EVEN]
        out_ref[...] = jnp.where(mine, a_ref[start:stop], b_ref[start:stop])

    return call(body, facts, got, shape(stop - start, half))


def finish(facts, packs, blocks, native, got_top, got_rest, part, half):
    size = 2 * half
    vector_rows = blocks[0].shape[0] - part
    top = got_top.shape[0]

    def body(f, *refs):
        x = f[X]
        mine = f[CORE] == x
        pack = jnp.where(mine, refs[0][...], refs[1][...])
        turned = split(swapped(x == 1, pack[:size], 0))
        native_ref, top_ref, rest_ref = refs[6:9]
        out_ref, vectors_ref, singular_ref = refs[9:]
        up_0, low_0, up_1, low_1 = [r[...] for r in refs[2:6]]

        def product(moved, native):
            return dot3(lax.concatenate([moved, native], 1), turned)

        def put(ref, at, value):
            ref[pl.ds(pl.multiple_of(at, 8), value.shape[0])] = value

        kept = product(jnp.where(x == 0, up_0, low_1), jnp.where(x == 0, low_0, up_1))
        put(out_ref, x * part, kept[:part])
        put(vectors_ref, x * vector_rows, kept[part:])
        there = (1 - x) * part
        put(out_ref, there, product(top_ref[...], native_ref[:top]))
        rest = product(rest_ref[...], native_ref[top:])
        put(out_ref, there + top, rest[: part - top])
        put(vectors_ref, (1 - x) * vector_rows, rest[part - top :])
        squares = pack[size : size + 1]
        singular_ref[...] = jnp.sqrt(jnp.maximum(squares, 0.0) + 1e-06)

    return call(
        body,
        facts,
        packs + blocks + [native, got_top, got_rest],
        (shape(2 * part, size), shape(2 * vector_rows, size), shape(1, size)),
    )


def per_device(sector, block_label):
    local_rows, size = sector.shape
    half = size // 2
    part = local_rows // 2
    pairs = lax.axis_size("pair")
    row_count = lax.axis_size("row")
    vector_rows = pairs * size // row_count // 2
    pair_index = lax.axis_index("pair")
    row_index = lax.axis_index("row")
    x = pair_index % 2
    group = pair_index // 2
    core = row_index % 2

    def permute(block, route):
        moves = [
            (a * row_count + b, c * row_count + d) for (a, b), (c, d) in route
        ]
        return lax.ppermute(block, ("pair", "row"), moves)

    devices = [(p, r) for p in range(pairs) for r in range(row_count)]

    def exchange(block, over_pair, over_row):
        return permute(
            block, [((p ^ over_pair, r ^ over_row), (p, r)) for p, r in devices]
        )

    def shift(block, even_by):
        moves = []
        for p, r in devices:
            source = p - even_by if p % 2 == 0 else p + even_by
            if 0 <= source < pairs:
                moves.append(((source, r), (p, r)))
        return permute(block, moves)

    def swap(block, odd):
        moves = []
        for p, r in devices:
            other = p + 2 if p // 2 % 2 == odd else p - 2
            moves.append(((other if 0 <= other < pairs else p, r), (p, r)))
        return permute(block, moves)

    def pass_diagonal(block):
        moves = []
        for p, r in devices:
            other = p + 2 if r % 2 else p - 2
            inside = 0 <= other < pairs
            moves.append(((other, r ^ 1) if inside else (p, r), (p, r)))
        return permute(block, [((a, b), c) for (a, b), c in moves])

    def sum_rows(block):
        bit = 4
        while bit < row_count:
            block = block + exchange(block, 0, bit)
            bit *= 2
        return block

    names = jnp.arange(16, dtype=jnp.int32)
    facts = jnp.zeros((16,), jnp.int32)
    for name, value in (
        (X, x),
        (CORE, core),
        (FIRST, group == 0),
        (LAST, group == pairs // 2 - 1),
        (VROW, (row_index * 2 + x) * vector_rows),
        (EVEN, group % 2 == 0),
    ):
        facts = jnp.where(names == name, value.astype(jnp.int32), facts)
    labels = lax.dynamic_slice_in_dim(block_label, 4 * group, 4)
    facts = lax.dynamic_update_slice_in_dim(facts, labels, LABEL, 0)

    def together(*arrays):
        return lax.optimization_barrier(arrays)

    top = part * 3 // 8
    got_top = exchange(
        lax.dynamic_slice_in_dim(sector, (1 - x) * part, top), 1, 0
    )
    own, rest = first_gram(facts, sector, half, top)
    own, got_top = together(sum_rows(own + exchange(own, 0, 1)), got_top)
    near = permute(
        own,
        [
            ((p, r ^ 2) if p % 2 == r % 2 else (p ^ 1, r ^ 1), (p, r))
            for p, r in devices
        ],
    )
    far = permute(
        own, [((p ^ 1, r ^ 2), (p, r)) for p, r in devices if p % 2 != r % 2]
    )
    got_rest = exchange(together(rest, own)[0], 1, 0)
    rotation, gram = first_rotation(facts, own, near, far, half)

    for sweep_round in range(ROUNDS - 1):
        packs = [rotation, exchange(rotation, 0, 1)]
        last_move = sweep_round == ROUNDS - 2
        if sweep_round == 0:
            stay, leave = turn_rows(facts, packs, sector, vector_rows, half, True)
            own_rows = [stay, leave, shift(leave, -2)]
            other_rows = []
            for got, below in ((got_top, 0), (got_rest, vector_rows)):
                got, leave = together(got, leave)
                stay, leave = turn_rows(facts, packs, got, below, half, False)
                other_rows.append([stay, leave, shift(leave, 2)])
        else:
            leave_a, leave_b, nat_l, nat_u, *native_give = turn(
                facts, packs, blocks, half, last_move
            )
            got = [swap(leave_a, 0), swap(leave_b, 1)]
        leave, stay = turned_gram(facts, gram, rotation)
        diagonals = [pass_diagonal(leave), exchange(stay, 0, 1)]
        if sweep_round == 0:
            own_rows[2], *diagonals = together(own_rows[2], *diagonals)
            *grams, up_0, nat_l, nat_u, low_1 = first_cross_gram(
                facts, own_rows, other_rows, part, half
            )
        else:
            *got, diagonals[0], diagonals[1] = together(*got, *diagonals)
            if last_move:
                native = exchange(native_give[0], 1, 0)
                top = part // 2
                top_give = give(facts, got, 0, top, half)
                *got, native, top_give = together(*got, native, top_give)
                got_top = exchange(top_give, 1, 0)
            *grams, up_0, low_1 = cross_gram(facts, got, [nat_l, nat_u], part, half)
        blocks = [up_0, nat_l, nat_u, low_1]
        own = sum_rows(grams[0] + exchange(grams[1], 0, 1))
        parts = [own, exchange(own, 0, 2), exchange(own, 1, 0), exchange(own, 1, 2)]
        if last_move:
            rest = give(facts, got, top, part + vector_rows, half)
            *parts, got_top, rest = together(*parts, got_top, rest)
            got_rest = exchange(rest, 1, 0)
        rotation, gram = later_rotation(facts, parts, diagonals, half, last_move)
    packs = [rotation, exchange(rotation, 0, 1)]
    rotated, vectors_out, singular = finish(
        facts, packs, blocks, native, got_top, got_rest, part, half
    )
    return rotated, vectors_out, singular.reshape(size)


def solution(mesh):
    placed = (P("row", "pair"), P())
    return jax.shard_map(
        per_device,
        mesh=mesh,
        in_specs=placed,
        out_specs=(P("row", "pair"), P("row", "pair"), P("pair")),
        check_vma=False,
    )
```

time: 167 us -> 156 us (0.934)
  waiting for transfers between devices: 64.8 us -> 55.4 us
  starting transfers between devices: 56.6 us -> 54.3 us
    ppermute x39 -> x37, waiting for transfers between devices: 64.8 us -> 55.4 us  [permute(): return lax.ppermute(block, ('pair', 'row'), moves)]
    ppermute x39 -> x37, starting transfers between devices: 56.6 us -> 54.3 us  [permute(): return lax.ppermute(block, ('pair', 'row'), moves)]
    pallas_call x20 -> x19, Pallas kernels: 41.2 us -> 40.5 us  [call(): pl.pallas_call(body, out_shape=outs, in_specs=[pl.BlockSpec(memory_space=...]
  transfers between devices with their start and end apart: 39 -> 37, of which waited for: 28 -> 29; matrix products, arithmetic and copies ran while one was open for 0% -> 1% of each run, Pallas kernels for 14% -> 14%
where the time goes in v3:
time: 156 us; the launch traced here: 155 us
  waiting for transfers between devices  55.4 us (36%)
  starting transfers between devices  54.3 us (35%)
  Pallas kernels  40.5 us (26%)
  local copies, waits for them, and re-layouts  3.43 us (2%)
    ppermute x37, waiting for transfers between devices, permute(): return lax.ppermute(block, ('pair', 'row'), moves)  55.4 us
    ppermute x37, starting transfers between devices, permute(): return lax.ppermute(block, ('pair', 'row'), moves)  54.3 us
    pallas_call x19, Pallas kernels, call(): pl.pallas_call(body, out_shape=outs, in_specs=[pl.BlockSpec(memory_space=...  40.5 us
  transfers between devices with their start and end apart: 37, of which 29 were waited for; matrix products, arithmetic and copies ran while one was open for 1% of the time, Pallas kernels for 14%

profile of v3, /device:TPU:0, one launch (start us, length us, event | category | flops | bytes accessed | tf_op | source)
XLA Modules:
  0.0 154.6 jit_solution(9709175789517341180)
XLA Ops:
  1.7 3.0 %collective-permute-start.1 = (f32[384,256]{1,0:T(8,128)S(1)}, f32[384,256]{1,0:T(8,128)S(1)}, u32[]{:S(2)}, u32[]{:S(2)}) collective-permute-start(f32[384,256]{1,0:T(8,128)S(1)} %constant_dynamic-slice_fusion), channel_id=1, source_target_pairs={{4,0},{5,1},{6,2},{7,3},{0,4},{1,5},{2,6},{3,7},{12,8},{13,9},{14,... | collective-permute-start | bytes 1179656 | tf_op jit(solution)/shard_map/ppermute | solution.py:412
  7.1 2.7 %shard_map.49 = (f32[384,128]{1,0:T(8,128)S(1)}, f32[640,256]{1,0:T(8,128)S(1)}) custom-call(s32[16]{0:T(128)S(1)} %constant_dynamic-update-slice_fusion.f, f32[2048,256]{1,0:T(8,128)S(1)} %copy-done), custom_call_target="tpu_custom_call" | custom-call | tf_op jit(solution)/shard_map/pallas_call | solution.py:52
  11.3 2.5 %collective-permute-done.1.x_ref = f32[384,256]{1,0:T(8,128)S(1)} collective-permute-done((f32[384,256]{1,0:T(8,128)S(1)}, f32[384,256]{1,0:T(8,128)S(1)}, u32[]{:S(2)}, u32[]{:S(2)}) %collective-permute-start.1) | collective-permute-done | bytes 393248 | tf_op jit(solution)/shard_map/ppermute | solution.py:412
  13.8 4.6 %collective-permute-start.3 = (f32[384,128]{1,0:T(8,128)S(1)}, f32[384,128]{1,0:T(8,128)S(1)}, u32[]{:S(2)}, u32[]{:S(2)}) collective-permute-start(f32[384,128]{1,0:T(8,128)S(1)} %add.37.own_ref), channel_id=1, source_target_pairs={{7,1},{5,3},{2,4},{0,6},{15,9},{13,11},{10,12},{8,14},{23,17},{21,... | collective-permute-start | bytes 589832 | tf_op jit(solution)/shard_map/ppermute | solution.py:412
  19.0 4.8 %collective-permute-done.3.far_ref = f32[384,128]{1,0:T(8,128)S(1)} collective-permute-done((f32[384,128]{1,0:T(8,128)S(1)}, f32[384,128]{1,0:T(8,128)S(1)}, u32[]{:S(2)}, u32[]{:S(2)}) %collective-permute-start.3) | collective-permute-done | bytes 196640 | tf_op jit(solution)/shard_map/ppermute | solution.py:412
  24.1 4.4 %shard_map.50 = (f32[256,256]{1,0:T(8,128)S(1)}, f32[256,256]{1,0:T(8,128)S(1)}) custom-call(s32[16]{0:T(128)S(1)} %constant_dynamic-update-slice_fusion.f, f32[384,128]{1,0:T(8,128)S(1)} %add.37.own_ref, f32[384,128]{1,0:T(8,128)S(1)} %collective-permute-done.2.near_ref, f32[384,128]{1,0:T(8,128)S(1)} %collective-permute-done.3.far_ref), custom_call_target="tpu_custom_call" | custom-call | tf_op jit(solution)/shard_map/pallas_call | solution.py:52
  33.6 3.1 %collective-permute-done.9.x_ref = f32[640,256]{1,0:T(8,128)S(1)} collective-permute-done((f32[640,256]{1,0:T(8,128)S(1)}, f32[640,256]{1,0:T(8,128)S(1)}, u32[]{:S(2)}, u32[]{:S(2)}) %collective-permute-start.9) | collective-permute-done | bytes 655392 | tf_op jit(solution)/shard_map/ppermute | solution.py:412
  37.8 3.5 %collective-permute-start.10 = (f32[896,128]{1,0:T(8,128)S(1)}, f32[896,128]{1,0:T(8,128)S(1)}, u32[]{:S(2)}, u32[]{:S(2)}) collective-permute-start(f32[896,128]{1,0:T(8,128)S(1)} %get-tuple-element.93.refs_7_), channel_id=1, source_target_pairs={{12,4},{13,5},{14,6},{15,7},{0,8},{1,9},{2,10},{3,11},{20,12},{21,... | collective-permute-start | bytes 1376264 | tf_op jit(solution)/shard_map/ppermute | solution.py:412
  41.3 3.5 %collective-permute-start.8 = (f32[384,128]{1,0:T(8,128)S(1)}, f32[384,128]{1,0:T(8,128)S(1)}, u32[]{:S(2)}, u32[]{:S(2)}) collective-permute-start(f32[384,128]{1,0:T(8,128)S(1)} %get-tuple-element.88.refs_4_), channel_id=1, source_target_pairs={{12,4},{13,5},{14,6},{15,7},{0,8},{1,9},{2,10},{3,11},{20,12},{21,... | collective-permute-start | bytes 589832 | tf_op jit(solution)/shard_map/ppermute | solution.py:412
  47.1 3.0 %collective-permute-start.7 = (f32[128,128]{1,0:T(8,128)S(1)}, f32[128,128]{1,0:T(8,128)S(1)}, u32[]{:S(2)}, u32[]{:S(2)}) collective-permute-start(f32[128,128]{1,0:T(8,128)S(1)} %get-tuple-element.83), channel_id=1, source_target_pairs={{1,0},{0,1},{3,2},{2,3},{5,4},{4,5},{7,6},{6,7},{9,8},{8,9},{11,10... | collective-permute-start | bytes 196616 | tf_op jit(solution)/shard_map/ppermute | solution.py:412
  51.0 5.2 %collective-permute-done.8.refs_5_ = f32[384,128]{1,0:T(8,128)S(1)} collective-permute-done((f32[384,128]{1,0:T(8,128)S(1)}, f32[384,128]{1,0:T(8,128)S(1)}, u32[]{:S(2)}, u32[]{:S(2)}) %collective-permute-start.8) | collective-permute-done | bytes 196640 | tf_op jit(solution)/shard_map/ppermute | solution.py:412
  56.2 1.9 %shard_map.55 = (f32[128,128]{1,0:T(8,128)S(1)}, f32[128,128]{1,0:T(8,128)S(1)}, f32[1280,128]{1,0:T(8,128)S(1)}, f32[1280,128]{1,0:T(8,128)S(1)}, f32[1280,128]{1,0:T(8,128)S(1)}, /*index=5*/f32[1280,128]{1,0:T(8,128)S(1)}) custom-call(s32[16]{0:T(128)S(1)} %constant_dynamic-update-slice_fusion.f, f32[1280,128]{1,0:T(8,128)S(1)} %get-tuple-element.79.refs_0_, ...), custom_call_target="tpu_custom_call" | custom-call | tf_op jit(solution)/shard_map/pallas_call | solution.py:52
  59.4 2.3 %collective-permute-start.14 = (f32[128,128]{1,0:T(8,128)S(1)}, f32[128,128]{1,0:T(8,128)S(1)}, u32[]{:S(2)}, u32[]{:S(2)}) collective-permute-start(f32[128,128]{1,0:T(8,128)S(1)} %add.39.refs_0_), channel_id=1, source_target_pairs={{6,0},{7,1},{4,2},{5,3},{2,4},{3,5},{0,6},{1,7},{14,8},{15,9},{12,... | collective-permute-start | bytes 196616 | tf_op jit(solution)/shard_map/ppermute | solution.py:412
  63.0 2.1 %collective-permute-done.14.refs_3_ = f32[128,128]{1,0:T(8,128)S(1)} collective-permute-done((f32[128,128]{1,0:T(8,128)S(1)}, f32[128,128]{1,0:T(8,128)S(1)}, u32[]{:S(2)}, u32[]{:S(2)}) %collective-permute-start.14) | collective-permute-done | bytes 65568 | tf_op jit(solution)/shard_map/ppermute | solution.py:412
  66.2 4.2 %shard_map.56 = (f32[256,256]{1,0:T(8,128)S(1)}, f32[256,256]{1,0:T(8,128)S(1)}) custom-call(s32[16]{0:T(128)S(1)} %constant_dynamic-update-slice_fusion.f, f32[128,128]{1,0:T(8,128)S(1)} %add.39.refs_0_, f32[128,128]{1,0:T(8,128)S(1)} %collective-permute-done.12.refs_1_, f32[128,128]{1,0:T(8,128)S(1)} %collective-permute-done.13.refs_2_, ...), custom_call_target="tpu_custom_call" | custom-call | tf_op jit(solution)/shard_map/pallas_call | solution.py:52
  71.9 1.8 %shard_map.57 = (f32[1280,128]{1,0:T(8,128)S(1)}, f32[1280,128]{1,0:T(8,128)S(1)}, f32[1280,128]{1,0:T(8,128)S(1)}, f32[1280,128]{1,0:T(8,128)S(1)}) custom-call(s32[16]{0:T(128)S(1)} %constant_dynamic-update-slice_fusion.f, f32[256,256]{1,0:T(8,128)S(1)} %get-tuple-element.98.own_ref.rotation_ref, f32[256,256]{1,0:T(8,128)S(1)} %collective-permute-done.15.other_ref, ...), custom_call_target="tpu_custom_call" | custom-call | tf_op jit(solution)/shard_map/pallas_call | solution.py:52
  73.7 2.3 %collective-permute-start.16 = (f32[1280,128]{1,0:T(8,128)S(1)}, f32[1280,128]{1,0:T(8,128)S(1)}, u32[]{:S(2)}, u32[]{:S(2)}) collective-permute-start(f32[1280,128]{1,0:T(8,128)S(1)} %get-tuple-element.103), channel_id=1, source_target_pairs={{8,0},{9,1},{10,2},{11,3},{12,4},{13,5},{14,6},{15,7},{0,8},{1,9},... | collective-permute-start | bytes 1966088 | tf_op jit(solution)/shard_map/ppermute | solution.py:412
  79.1 5.8 %collective-permute-start.19 = (f32[128,128]{1,0:T(8,128)S(1)}, f32[128,128]{1,0:T(8,128)S(1)}, u32[]{:S(2)}, u32[]{:S(2)}) collective-permute-start(f32[128,128]{1,0:T(8,128)S(1)} %get-tuple-element.107), channel_id=1, source_target_pairs={{1,0},{0,1},{3,2},{2,3},{5,4},{4,5},{7,6},{6,7},{9,8},{8,9},{11,10... | collective-permute-start | bytes 196616 | tf_op jit(solution)/shard_map/ppermute | solution.py:412
  85.8 5.3 %collective-permute-done.16.refs_0_ = f32[1280,128]{1,0:T(8,128)S(1)} collective-permute-done((f32[1280,128]{1,0:T(8,128)S(1)}, f32[1280,128]{1,0:T(8,128)S(1)}, u32[]{:S(2)}, u32[]{:S(2)}) %collective-permute-start.16) | collective-permute-done | bytes 655392 | tf_op jit(solution)/shard_map/ppermute | solution.py:412
  91.1 1.7 %shard_map.59 = (f32[128,128]{1,0:T(8,128)S(1)}, f32[128,128]{1,0:T(8,128)S(1)}, f32[1280,128]{1,0:T(8,128)S(1)}, f32[1280,128]{1,0:T(8,128)S(1)}) custom-call(s32[16]{0:T(128)S(1)} %constant_dynamic-update-slice_fusion.f, f32[1280,128]{1,0:T(8,128)S(1)} %collective-permute-done.16.refs_0_, f32[1280,128]{1,0:T(8,128)S(1)} %collective-permute-done.17.refs_1_, ...), custom_call_target="tpu_custom_call" | custom-call | tf_op jit(solution)/shard_map/pallas_call | solution.py:52
  94.3 1.8 %collective-permute-start.23 = (f32[128,128]{1,0:T(8,128)S(1)}, f32[128,128]{1,0:T(8,128)S(1)}, u32[]{:S(2)}, u32[]{:S(2)}) collective-permute-start(f32[128,128]{1,0:T(8,128)S(1)} %add.40.refs_0_), channel_id=1, source_target_pairs={{6,0},{7,1},{4,2},{5,3},{2,4},{3,5},{0,6},{1,7},{14,8},{15,9},{12,... | collective-permute-start | bytes 196616 | tf_op jit(solution)/shard_map/ppermute | solution.py:412
  97.9 2.1 %collective-permute-done.23.refs_3_ = f32[128,128]{1,0:T(8,128)S(1)} collective-permute-done((f32[128,128]{1,0:T(8,128)S(1)}, f32[128,128]{1,0:T(8,128)S(1)}, u32[]{:S(2)}, u32[]{:S(2)}) %collective-permute-start.23) | collective-permute-done | bytes 65568 | tf_op jit(solution)/shard_map/ppermute | solution.py:412
  101.4 4.0 %shard_map.60 = (f32[256,256]{1,0:T(8,128)S(1)}, f32[256,256]{1,0:T(8,128)S(1)}) custom-call(s32[16]{0:T(128)S(1)} %constant_dynamic-update-slice_fusion.f, f32[128,128]{1,0:T(8,128)S(1)} %add.40.refs_0_, f32[128,128]{1,0:T(8,128)S(1)} %collective-permute-done.21.refs_1_, f32[128,128]{1,0:T(8,128)S(1)} %collective-permute-done.22.refs_2_, ...), custom_call_target="tpu_custom_call" | custom-call | tf_op jit(solution)/shard_map/pallas_call | solution.py:52
  106.9 1.8 %shard_map.61 = (f32[1280,128]{1,0:T(8,128)S(1)}, f32[1280,128]{1,0:T(8,128)S(1)}, f32[1280,128]{1,0:T(8,128)S(1)}, f32[1280,128]{1,0:T(8,128)S(1)}, f32[1280,128]{1,0:T(8,128)S(1)}) custom-call(s32[16]{0:T(128)S(1)} %constant_dynamic-update-slice_fusion.f, f32[256,256]{1,0:T(8,128)S(1)} %get-tuple-element.116.own_ref.rotation_ref, ...), custom_call_target="tpu_custom_call" | custom-call | tf_op jit(solution)/shard_map/pallas_call | solution.py:52
  108.7 4.8 %collective-permute-start.25 = (f32[1280,128]{1,0:T(8,128)S(1)}, f32[1280,128]{1,0:T(8,128)S(1)}, u32[]{:S(2)}, u32[]{:S(2)}) collective-permute-start(f32[1280,128]{1,0:T(8,128)S(1)} %get-tuple-element.119), channel_id=1, source_target_pairs={{8,0},{9,1},{10,2},{11,3},{12,4},{13,5},{14,6},{15,7},{0,8},{1,9},... | collective-permute-start | bytes 1966088 | tf_op jit(solution)/shard_map/ppermute | solution.py:412
  116.7 4.9 %collective-permute-start.28 = (f32[128,128]{1,0:T(8,128)S(1)}, f32[128,128]{1,0:T(8,128)S(1)}, u32[]{:S(2)}, u32[]{:S(2)}) collective-permute-start(f32[128,128]{1,0:T(8,128)S(1)} %get-tuple-element.123), channel_id=1, source_target_pairs={{1,0},{0,1},{3,2},{2,3},{5,4},{4,5},{7,6},{6,7},{9,8},{8,9},{11,10... | collective-permute-start | bytes 196616 | tf_op jit(solution)/shard_map/ppermute | solution.py:412
  122.5 6.1 %collective-permute-done.25.a_ref.refs_0_ = f32[1280,128]{1,0:T(8,128)S(1)} collective-permute-done((f32[1280,128]{1,0:T(8,128)S(1)}, f32[1280,128]{1,0:T(8,128)S(1)}, u32[]{:S(2)}, u32[]{:S(2)}) %collective-permute-start.25) | collective-permute-done | bytes 655392 | tf_op jit(solution)/shard_map/ppermute | solution.py:412
  134.1 2.2 %collective-permute-start.33 = (f32[128,128]{1,0:T(8,128)S(1)}, f32[128,128]{1,0:T(8,128)S(1)}, u32[]{:S(2)}, u32[]{:S(2)}) collective-permute-start(f32[128,128]{1,0:T(8,128)S(1)} %add.41.refs_0_), channel_id=1, source_target_pairs={{6,0},{7,1},{4,2},{5,3},{2,4},{3,5},{0,6},{1,7},{14,8},{15,9},{12,... | collective-permute-start | bytes 196616 | tf_op jit(solution)/shard_map/ppermute | solution.py:412
  138.2 2.6 %collective-permute-done.33.refs_3_ = f32[128,128]{1,0:T(8,128)S(1)} collective-permute-done((f32[128,128]{1,0:T(8,128)S(1)}, f32[128,128]{1,0:T(8,128)S(1)}, u32[]{:S(2)}, u32[]{:S(2)}) %collective-permute-start.33) | collective-permute-done | bytes 65568 | tf_op jit(solution)/shard_map/ppermute | solution.py:412
  142.6 4.0 %shard_map.66 = (f32[264,256]{1,0:T(8,128)S(1)}, f32[256,256]{1,0:T(8,128)}) custom-call(s32[16]{0:T(128)S(1)} %constant_dynamic-update-slice_fusion.f, f32[128,128]{1,0:T(8,128)S(1)} %add.41.refs_0_, f32[128,128]{1,0:T(8,128)S(1)} %collective-permute-done.31.refs_1_, f32[128,128]{1,0:T(8,128)S(1)} %collective-permute-done.32.refs_2_, ...), custom_call_target="tpu_custom_call" | custom-call | tf_op jit(solution)/shard_map/pallas_call | solution.py:52
  148.2 3.1 %collective-permute-done.36.refs_8_ = f32[768,128]{1,0:T(8,128)S(1)} collective-permute-done((f32[768,128]{1,0:T(8,128)S(1)}, f32[768,128]{1,0:T(8,128)S(1)}, u32[]{:S(2)}, u32[]{:S(2)}) %collective-permute-start.36) | collective-permute-done | bytes 393248 | tf_op jit(solution)/shard_map/ppermute | solution.py:412
  151.3 3.3 %shard_map.67 = (f32[2048,256]{1,0:T(8,128)}, f32[512,256]{1,0:T(8,128)}, f32[1,256]{1,0:T(1,128)}) custom-call(s32[16]{0:T(128)S(1)} %constant_dynamic-update-slice_fusion.f, f32[264,256]{1,0:T(8,128)S(1)} %get-tuple-element.140.refs_0_, f32[264,256]{1,0:T(8,128)S(1)} %collective-permute-done.35.refs_1_, f32[1280,128]{1,0:T(8,128)S(1)} %get-tuple-element.141.refs_2_, ...), custom_call_target="tpu_custom_call" | custom-call | tf_op jit(solution)/shard_map/pallas_call | solution.py:52
  (72 shorter events, 45.4 us)
Async XLA Ops:
  1.7 12.1 %collective-permute-start.1 = (f32[384,256]{1,0:T(8,128)S(1)}, f32[384,256]{1,0:T(8,128)S(1)}, u32[]{:S(2)}, u32[]{:S(2)}) collective-permute-start(f32[384,256]{1,0:T(8,128)S(1)} %constant_dynamic-slice_fusion), channel_id=1, source_target_pairs={{4,0},{5,1},{6,2},{7,3},{0,4},{1,5},{2,6},{3,7},{12,8},{13,9},{14,... | collective-permute-start | bytes 1179656 | tf_op jit(solution)/shard_map/ppermute | solution.py:412
  13.8 9.9 %collective-permute-start.3 = (f32[384,128]{1,0:T(8,128)S(1)}, f32[384,128]{1,0:T(8,128)S(1)}, u32[]{:S(2)}, u32[]{:S(2)}) collective-permute-start(f32[384,128]{1,0:T(8,128)S(1)} %add.37.own_ref), channel_id=1, source_target_pairs={{7,1},{5,3},{2,4},{0,6},{15,9},{13,11},{10,12},{8,14},{23,17},{21,... | collective-permute-start | bytes 589832 | tf_op jit(solution)/shard_map/ppermute | solution.py:412
  18.4 5.7 %collective-permute-start.2 = (f32[384,128]{1,0:T(8,128)S(1)}, f32[384,128]{1,0:T(8,128)S(1)}, u32[]{:S(2)}, u32[]{:S(2)}) collective-permute-start(f32[384,128]{1,0:T(8,128)S(1)} %add.37.own_ref), channel_id=1, source_target_pairs={{2,0},{4,1},{0,2},{6,3},{1,4},{7,5},{3,6},{5,7},{10,8},{12,9},{8,1... | collective-permute-start | bytes 589832 | tf_op jit(solution)/shard_map/ppermute | solution.py:412
  19.0 17.7 %collective-permute-start.9 = (f32[640,256]{1,0:T(8,128)S(1)}, f32[640,256]{1,0:T(8,128)S(1)}, u32[]{:S(2)}, u32[]{:S(2)}) collective-permute-start(f32[640,256]{1,0:T(8,128)S(1)} %get-tuple-element.90), channel_id=1, source_target_pairs={{4,0},{5,1},{6,2},{7,3},{0,4},{1,5},{2,6},{3,7},{12,8},{13,9},{14,... | collective-permute-start | bytes 1966088 | tf_op jit(solution)/shard_map/ppermute | solution.py:412
  28.5 1.6 %collective-permute-start.4 = (f32[256,256]{1,0:T(8,128)S(1)}, f32[256,256]{1,0:T(8,128)S(1)}, u32[]{:S(2)}, u32[]{:S(2)}) collective-permute-start(f32[256,256]{1,0:T(8,128)S(1)} %get-tuple-element.78.own_ref.rotation_ref), channel_id=1, source_target_pairs={{1,0},{0,1},{3,2},{2,3},{5,4},{4,5},{7,6},{6,7},{9,8},{8,9},{11,10... | collective-permute-start | bytes 786440 | tf_op jit(solution)/shard_map/ppermute | solution.py:412
  31.4 19.6 %collective-permute-start.5 = (f32[1280,128]{1,0:T(8,128)S(1)}, f32[1280,128]{1,0:T(8,128)S(1)}, u32[]{:S(2)}, u32[]{:S(2)}) collective-permute-start(f32[1280,128]{1,0:T(8,128)S(1)} %get-tuple-element.80.refs_1_), channel_id=1, source_target_pairs={{8,0},{9,1},{10,2},{11,3},{16,8},{17,9},{18,10},{19,11},{4,12},{5,... | collective-permute-start | bytes 1966088 | tf_op jit(solution)/shard_map/ppermute | solution.py:412
  37.8 18.4 %collective-permute-start.10 = (f32[896,128]{1,0:T(8,128)S(1)}, f32[896,128]{1,0:T(8,128)S(1)}, u32[]{:S(2)}, u32[]{:S(2)}) collective-permute-start(f32[896,128]{1,0:T(8,128)S(1)} %get-tuple-element.93.refs_7_), channel_id=1, source_target_pairs={{12,4},{13,5},{14,6},{15,7},{0,8},{1,9},{2,10},{3,11},{20,12},{21,... | collective-permute-start | bytes 1376264 | tf_op jit(solution)/shard_map/ppermute | solution.py:412
  41.3 14.9 %collective-permute-start.8 = (f32[384,128]{1,0:T(8,128)S(1)}, f32[384,128]{1,0:T(8,128)S(1)}, u32[]{:S(2)}, u32[]{:S(2)}) collective-permute-start(f32[384,128]{1,0:T(8,128)S(1)} %get-tuple-element.88.refs_4_), channel_id=1, source_target_pairs={{12,4},{13,5},{14,6},{15,7},{0,8},{1,9},{2,10},{3,11},{20,12},{21,... | collective-permute-start | bytes 589832 | tf_op jit(solution)/shard_map/ppermute | solution.py:412
  46.4 3.7 %collective-permute-start.6 = (f32[128,128]{1,0:T(8,128)S(1)}, f32[128,128]{1,0:T(8,128)S(1)}, u32[]{:S(2)}, u32[]{:S(2)}) collective-permute-start(f32[128,128]{1,0:T(8,128)S(1)} %get-tuple-element.82), channel_id=1, source_target_pairs={{0,0},{8,1},{2,2},{10,3},{4,4},{12,5},{6,6},{14,7},{1,8},{16,9},{3... | collective-permute-start | bytes 196616 | tf_op jit(solution)/shard_map/ppermute | solution.py:412
  47.1 3.9 %collective-permute-start.7 = (f32[128,128]{1,0:T(8,128)S(1)}, f32[128,128]{1,0:T(8,128)S(1)}, u32[]{:S(2)}, u32[]{:S(2)}) collective-permute-start(f32[128,128]{1,0:T(8,128)S(1)} %get-tuple-element.83), channel_id=1, source_target_pairs={{1,0},{0,1},{3,2},{2,3},{5,4},{4,5},{7,6},{6,7},{9,8},{8,9},{11,10... | collective-permute-start | bytes 196616 | tf_op jit(solution)/shard_map/ppermute | solution.py:412
  59.4 5.7 %collective-permute-start.14 = (f32[128,128]{1,0:T(8,128)S(1)}, f32[128,128]{1,0:T(8,128)S(1)}, u32[]{:S(2)}, u32[]{:S(2)}) collective-permute-start(f32[128,128]{1,0:T(8,128)S(1)} %add.39.refs_0_), channel_id=1, source_target_pairs={{6,0},{7,1},{4,2},{5,3},{2,4},{3,5},{0,6},{1,7},{14,8},{15,9},{12,... | collective-permute-start | bytes 196616 | tf_op jit(solution)/shard_map/ppermute | solution.py:412
  61.8 4.3 %collective-permute-start.13 = (f32[128,128]{1,0:T(8,128)S(1)}, f32[128,128]{1,0:T(8,128)S(1)}, u32[]{:S(2)}, u32[]{:S(2)}) collective-permute-start(f32[128,128]{1,0:T(8,128)S(1)} %add.39.refs_0_), channel_id=1, source_target_pairs={{4,0},{5,1},{6,2},{7,3},{0,4},{1,5},{2,6},{3,7},{12,8},{13,9},{14,... | collective-permute-start | bytes 196616 | tf_op jit(solution)/shard_map/ppermute | solution.py:412
  61.8 4.4 %collective-permute-start.12 = (f32[128,128]{1,0:T(8,128)S(1)}, f32[128,128]{1,0:T(8,128)S(1)}, u32[]{:S(2)}, u32[]{:S(2)}) collective-permute-start(f32[128,128]{1,0:T(8,128)S(1)} %add.39.refs_0_), channel_id=1, source_target_pairs={{2,0},{3,1},{0,2},{1,3},{6,4},{7,5},{4,6},{5,7},{10,8},{11,9},{8,1... | collective-permute-start | bytes 196616 | tf_op jit(solution)/shard_map/ppermute | solution.py:412
  70.3 1.6 %collective-permute-start.15 = (f32[256,256]{1,0:T(8,128)S(1)}, f32[256,256]{1,0:T(8,128)S(1)}, u32[]{:S(2)}, u32[]{:S(2)}) collective-permute-start(f32[256,256]{1,0:T(8,128)S(1)} %get-tuple-element.98.own_ref.rotation_ref), channel_id=1, source_target_pairs={{1,0},{0,1},{3,2},{2,3},{5,4},{4,5},{7,6},{6,7},{9,8},{8,9},{11,10... | collective-permute-start | bytes 786440 | tf_op jit(solution)/shard_map/ppermute | solution.py:412
  73.7 17.4 %collective-permute-start.16 = (f32[1280,128]{1,0:T(8,128)S(1)}, f32[1280,128]{1,0:T(8,128)S(1)}, u32[]{:S(2)}, u32[]{:S(2)}) collective-permute-start(f32[1280,128]{1,0:T(8,128)S(1)} %get-tuple-element.103), channel_id=1, source_target_pairs={{8,0},{9,1},{10,2},{11,3},{12,4},{13,5},{14,6},{15,7},{0,8},{1,9},... | collective-permute-start | bytes 1966088 | tf_op jit(solution)/shard_map/ppermute | solution.py:412
  76.0 15.1 %collective-permute-start.17 = (f32[1280,128]{1,0:T(8,128)S(1)}, f32[1280,128]{1,0:T(8,128)S(1)}, u32[]{:S(2)}, u32[]{:S(2)}) collective-permute-start(f32[1280,128]{1,0:T(8,128)S(1)} %get-tuple-element.104), channel_id=1, source_target_pairs={{0,0},{1,1},{2,2},{3,3},{4,4},{5,5},{6,6},{7,7},{16,8},{17,9},{18,... | collective-permute-start | bytes 1966088 | tf_op jit(solution)/shard_map/ppermute | solution.py:412
  78.4 6.5 %collective-permute-start.18 = (f32[128,128]{1,0:T(8,128)S(1)}, f32[128,128]{1,0:T(8,128)S(1)}, u32[]{:S(2)}, u32[]{:S(2)}) collective-permute-start(f32[128,128]{1,0:T(8,128)S(1)} %get-tuple-element.106), channel_id=1, source_target_pairs={{0,0},{8,1},{2,2},{10,3},{4,4},{12,5},{6,6},{14,7},{1,8},{16,9},{3... | collective-permute-start | bytes 196616 | tf_op jit(solution)/shard_map/ppermute | solution.py:412
  79.1 6.7 %collective-permute-start.19 = (f32[128,128]{1,0:T(8,128)S(1)}, f32[128,128]{1,0:T(8,128)S(1)}, u32[]{:S(2)}, u32[]{:S(2)}) collective-permute-start(f32[128,128]{1,0:T(8,128)S(1)} %get-tuple-element.107), channel_id=1, source_target_pairs={{1,0},{0,1},{3,2},{2,3},{5,4},{4,5},{7,6},{6,7},{9,8},{8,9},{11,10... | collective-permute-start | bytes 196616 | tf_op jit(solution)/shard_map/ppermute | solution.py:412
  94.3 5.7 %collective-permute-start.23 = (f32[128,128]{1,0:T(8,128)S(1)}, f32[128,128]{1,0:T(8,128)S(1)}, u32[]{:S(2)}, u32[]{:S(2)}) collective-permute-start(f32[128,128]{1,0:T(8,128)S(1)} %add.40.refs_0_), channel_id=1, source_target_pairs={{6,0},{7,1},{4,2},{5,3},{2,4},{3,5},{0,6},{1,7},{14,8},{15,9},{12,... | collective-permute-start | bytes 196616 | tf_op jit(solution)/shard_map/ppermute | solution.py:412
  96.1 4.8 %collective-permute-start.22 = (f32[128,128]{1,0:T(8,128)S(1)}, f32[128,128]{1,0:T(8,128)S(1)}, u32[]{:S(2)}, u32[]{:S(2)}) collective-permute-start(f32[128,128]{1,0:T(8,128)S(1)} %add.40.refs_0_), channel_id=1, source_target_pairs={{4,0},{5,1},{6,2},{7,3},{0,4},{1,5},{2,6},{3,7},{12,8},{13,9},{14,... | collective-permute-start | bytes 196616 | tf_op jit(solution)/shard_map/ppermute | solution.py:412
  97.1 4.3 %collective-permute-start.21 = (f32[128,128]{1,0:T(8,128)S(1)}, f32[128,128]{1,0:T(8,128)S(1)}, u32[]{:S(2)}, u32[]{:S(2)}) collective-permute-start(f32[128,128]{1,0:T(8,128)S(1)} %add.40.refs_0_), channel_id=1, source_target_pairs={{2,0},{3,1},{0,2},{1,3},{6,4},{7,5},{4,6},{5,7},{10,8},{11,9},{8,1... | collective-permute-start | bytes 196616 | tf_op jit(solution)/shard_map/ppermute | solution.py:412
  108.7 19.9 %collective-permute-start.25 = (f32[1280,128]{1,0:T(8,128)S(1)}, f32[1280,128]{1,0:T(8,128)S(1)}, u32[]{:S(2)}, u32[]{:S(2)}) collective-permute-start(f32[1280,128]{1,0:T(8,128)S(1)} %get-tuple-element.119), channel_id=1, source_target_pairs={{8,0},{9,1},{10,2},{11,3},{12,4},{13,5},{14,6},{15,7},{0,8},{1,9},... | collective-permute-start | bytes 1966088 | tf_op jit(solution)/shard_map/ppermute | solution.py:412
  113.5 15.0 %collective-permute-start.26 = (f32[1280,128]{1,0:T(8,128)S(1)}, f32[1280,128]{1,0:T(8,128)S(1)}, u32[]{:S(2)}, u32[]{:S(2)}) collective-permute-start(f32[1280,128]{1,0:T(8,128)S(1)} %get-tuple-element.120), channel_id=1, source_target_pairs={{0,0},{1,1},{2,2},{3,3},{4,4},{5,5},{6,6},{7,7},{16,8},{17,9},{18,... | collective-permute-start | bytes 1966088 | tf_op jit(solution)/shard_map/ppermute | solution.py:412
  114.2 16.6 %collective-permute-start.29 = (f32[1280,128]{1,0:T(8,128)S(1)}, f32[1280,128]{1,0:T(8,128)S(1)}, u32[]{:S(2)}, u32[]{:S(2)}) collective-permute-start(f32[1280,128]{1,0:T(8,128)S(1)} %get-tuple-element.126), channel_id=1, source_target_pairs={{4,0},{5,1},{6,2},{7,3},{0,4},{1,5},{2,6},{3,7},{12,8},{13,9},{14,... | collective-permute-start | bytes 1966088 | tf_op jit(solution)/shard_map/ppermute | solution.py:412
  116.0 5.6 %collective-permute-start.27 = (f32[128,128]{1,0:T(8,128)S(1)}, f32[128,128]{1,0:T(8,128)S(1)}, u32[]{:S(2)}, u32[]{:S(2)}) collective-permute-start(f32[128,128]{1,0:T(8,128)S(1)} %get-tuple-element.122), channel_id=1, source_target_pairs={{0,0},{8,1},{2,2},{10,3},{4,4},{12,5},{6,6},{14,7},{1,8},{16,9},{3... | collective-permute-start | bytes 196616 | tf_op jit(solution)/shard_map/ppermute | solution.py:412
  116.7 5.8 %collective-permute-start.28 = (f32[128,128]{1,0:T(8,128)S(1)}, f32[128,128]{1,0:T(8,128)S(1)}, u32[]{:S(2)}, u32[]{:S(2)}) collective-permute-start(f32[128,128]{1,0:T(8,128)S(1)} %get-tuple-element.123), channel_id=1, source_target_pairs={{1,0},{0,1},{3,2},{2,3},{5,4},{4,5},{7,6},{6,7},{9,8},{8,9},{11,10... | collective-permute-start | bytes 196616 | tf_op jit(solution)/shard_map/ppermute | solution.py:412
  130.8 10.4 %collective-permute-start.34 = (f32[512,128]{1,0:T(8,128)S(1)}, f32[512,128]{1,0:T(8,128)S(1)}, u32[]{:S(2)}, u32[]{:S(2)}) collective-permute-start(f32[512,128]{1,0:T(8,128)S(1)} %shard_map.63), channel_id=1, source_target_pairs={{4,0},{5,1},{6,2},{7,3},{0,4},{1,5},{2,6},{3,7},{12,8},{13,9},{14,... | collective-permute-start | bytes 786440 | tf_op jit(solution)/shard_map/ppermute | solution.py:412
  134.1 6.7 %collective-permute-start.33 = (f32[128,128]{1,0:T(8,128)S(1)}, f32[128,128]{1,0:T(8,128)S(1)}, u32[]{:S(2)}, u32[]{:S(2)}) collective-permute-start(f32[128,128]{1,0:T(8,128)S(1)} %add.41.refs_0_), channel_id=1, source_target_pairs={{6,0},{7,1},{4,2},{5,3},{2,4},{3,5},{0,6},{1,7},{14,8},{15,9},{12,... | collective-permute-start | bytes 196616 | tf_op jit(solution)/shard_map/ppermute | solution.py:412
  136.3 4.8 %collective-permute-start.32 = (f32[128,128]{1,0:T(8,128)S(1)}, f32[128,128]{1,0:T(8,128)S(1)}, u32[]{:S(2)}, u32[]{:S(2)}) collective-permute-start(f32[128,128]{1,0:T(8,128)S(1)} %add.41.refs_0_), channel_id=1, source_target_pairs={{4,0},{5,1},{6,2},{7,3},{0,4},{1,5},{2,6},{3,7},{12,8},{13,9},{14,... | collective-permute-start | bytes 196616 | tf_op jit(solution)/shard_map/ppermute | solution.py:412
  136.5 4.6 %collective-permute-start.31 = (f32[128,128]{1,0:T(8,128)S(1)}, f32[128,128]{1,0:T(8,128)S(1)}, u32[]{:S(2)}, u32[]{:S(2)}) collective-permute-start(f32[128,128]{1,0:T(8,128)S(1)} %add.41.refs_0_), channel_id=1, source_target_pairs={{2,0},{3,1},{0,2},{1,3},{6,4},{7,5},{4,6},{5,7},{10,8},{11,9},{8,1... | collective-permute-start | bytes 196616 | tf_op jit(solution)/shard_map/ppermute | solution.py:412
  141.2 10.1 %collective-permute-start.36 = (f32[768,128]{1,0:T(8,128)S(1)}, f32[768,128]{1,0:T(8,128)S(1)}, u32[]{:S(2)}, u32[]{:S(2)}) collective-permute-start(f32[768,128]{1,0:T(8,128)S(1)} %shard_map.65), channel_id=1, source_target_pairs={{4,0},{5,1},{6,2},{7,3},{0,4},{1,5},{2,6},{3,7},{12,8},{13,9},{14,... | collective-permute-start | bytes 1179656 | tf_op jit(solution)/shard_map/ppermute | solution.py:412
  146.5 1.6 %collective-permute-start.35 = (f32[264,256]{1,0:T(8,128)S(1)}, f32[264,256]{1,0:T(8,128)S(1)}, u32[]{:S(2)}, u32[]{:S(2)}) collective-permute-start(f32[264,256]{1,0:T(8,128)S(1)} %get-tuple-element.140.refs_0_), channel_id=1, source_target_pairs={{1,0},{0,1},{3,2},{2,3},{5,4},{4,5},{7,6},{6,7},{9,8},{8,9},{11,10... | collective-permute-start | bytes 811016 | tf_op jit(solution)/shard_map/ppermute | solution.py:412
  (7 other events, 31.9 us)

commit v4 on v3

--- a/solution.py
+++ b/solution.py
@@ -11,8 +11,8 @@
 highest = lax.Precision.HIGHEST
 
 TARGET = 2.0**-12
-BOUNDS = [
-    (1.0 + TARGET ** (2.0**-j)) / (1.0 - TARGET ** (2.0**-j)) for j in range(NEWTON)
+REACHES = [
+    (2.0 / (TARGET ** -(2.0**-j) - 1.0)) ** 2 for j in range(NEWTON)
 ]
 
 X, CORE, FIRST, LAST, VROW, LABEL, EVEN = 0, 1, 2, 3, 4, 5, 9
@@ -62,22 +62,15 @@
     )(facts, *inputs)
 
 
-def first_gram(facts, sector, half, top):
-    rows, width = sector.shape
-    part = rows // 2
-
-    def body(f, x_ref, out_ref, give_ref):
+def first_gram(facts, sector, half):
+    def body(f, x_ref, out_ref):
         x = x_ref[...]
         g = dot_tn(x, x)
         out_ref[:half] = g[:half, :half]
         out_ref[half : 2 * half] = g[:half, half:]
         out_ref[2 * half :] = g[half:, half:]
-        there = pl.multiple_of((1 - f[X]) * part + top, 8)
-        give_ref[...] = x_ref[pl.ds(there, part - top)]
-
-    return call(
-        body, facts, [sector], (shape(3 * half, half), shape(part - top, width))
-    )
+
+    return call(body, facts, [sector], shape(3 * half, half))
 
 
 def rotate_of(gram, x_ref, e_ref):
@@ -91,14 +84,17 @@
     spread = g_j - g_i
     summed = g_j + g_i
     skew = gram * spread / (spread * spread + 2.0 * gram * gram + 0.01 * summed * summed)
-    bound = 1.0 + 0.25 * jnp.sum(skew * skew)
+    skew_parts = split(skew)
+    square = dot3(skew_parts, skew_parts)
+    whole = 0.25 * jnp.sum(skew * skew)
+    paired = 0.03125 * jnp.sum(square * square) * 1.001
+    reach = jnp.minimum(whole * whole, paired)
     steps = jnp.int32(0)
-    for limit in BOUNDS:
-        steps = steps + (bound > limit).astype(jnp.int32)
+    for limit in REACHES:
+        steps = steps + (reach > limit).astype(jnp.int32)
     fixes = 1 + (steps > 7).astype(jnp.int32) + 2 * (steps > 9).astype(jnp.int32)
-    scale = 2.0 / (1.0 + jnp.full((size, size), bound, jnp.float32))
-    skew_parts = split(skew)
-    residual = identity - scale * (identity - 0.25 * dot3(skew_parts, skew_parts))
+    scale = 2.0 / (2.0 + jnp.sqrt(jnp.full((size, size), reach, jnp.float32)))
+    residual = identity - scale * (identity - 0.25 * square)
     x_ref[...] = scale * (identity + residual)
     residual_parts = split(residual)
     e_ref[...] = dot3(residual_parts, residual_parts)
@@ -132,12 +128,11 @@
         rotation_ref[size:] = jnp.broadcast_to(squares, (8, size))
 
 
-def first_rotation(facts, own, near, far, half):
+def first_rotation(facts, own, other_y, half):
     size = 2 * half
 
-    def body(f, own_ref, near_ref, far_ref, rotation_ref, g_ref, x_ref, e_ref):
-        mine = f[X] == f[CORE]
-        total = near_ref[...] + jnp.where(mine, own_ref[...], far_ref[...])
+    def body(f, own_ref, other_ref, rotation_ref, g_ref, x_ref, e_ref):
+        total = own_ref[...] + other_ref[...]
         g_ref[:half, :half] = total[:half]
         g_ref[:half, half:] = total[half : 2 * half]
         g_ref[half:, :half] = total[half : 2 * half].T
@@ -145,9 +140,7 @@
         put_rotation(rotation_ref, g_ref[...], x_ref, e_ref, False)
 
     square = pltpu.VMEM((size, size), jnp.float32)
-    return call(
-        body, facts, [own, near, far], (shape(size, size),) * 2, [square] * 2
-    )
+    return call(body, facts, [own, other_y], (shape(size, size),) * 2, [square] * 2)
 
 
 def later_rotation(facts, parts, diagonals, half, last_round):
@@ -174,7 +167,7 @@
     )
 
 
-def turned_gram(facts, gram, rotation):
+def turned_gram(facts, gram, rotation, position):
     size = gram.shape[0]
     half = size // 2
 
@@ -183,7 +176,7 @@
         turned = dot(gram_ref[...], rotation)
         upper = dot_tn(rotation[:, :half], turned[:, :half])
         lower = dot_tn(rotation[:, half:], turned[:, half:])
-        lower_leaves = (f[CORE] == 0) & (f[FIRST] == 0)
+        lower_leaves = (f[position] == 0) & (f[FIRST] == 0)
         leave_ref[...] = jnp.where(lower_leaves, lower, upper)
         stay_ref[...] = jnp.where(lower_leaves, upper, lower)
 
@@ -227,32 +220,30 @@
     return swapped(f[FIRST] == 1, turn_0, 1), turn_1
 
 
-def turn_rows(facts, packs, rows_of, vector_rows, half, own):
-    size = 2 * half
+def turn_rows(facts, rotation, rows_of, vector_rows, half, own):
     rows = rows_of.shape[0] // 2 if own else rows_of.shape[0]
 
-    def body(f, own_ref, other_ref, x_ref, stay_ref, leave_ref):
-        turn_0, turn_1 = turns_of(f, own_ref, other_ref)
+    def body(f, rotation_ref, x_ref, stay_ref, leave_ref):
         zero = f[X] == (0 if own else 1)
-        turn = split(jnp.where(zero, turn_0, swapped(True, turn_1, 1)))
+        upper_leaves = jnp.where(zero, f[FIRST], 1) == 1
+        turn = split(swapped(upper_leaves, rotation_ref[...], 1))
         here = pl.multiple_of(f[X] * rows, 8)
         out = dot3(x_ref[pl.ds(here, rows)] if own else x_ref[...], turn)
         stay_ref[:rows] = out[:, :half]
         leave_ref[:rows] = out[:, half:]
-        if vector_rows:
-            ids = f[VROW] + lax.broadcasted_iota(jnp.int32, (vector_rows, half), 0)
-            cols = lax.broadcasted_iota(jnp.int32, (vector_rows, half), 1)
-            position = jnp.where(zero, 0, 2)
-            vectors = [
-                (ids == f[LABEL + position + k] * half + cols).astype(jnp.float32)
-                for k in range(2)
-            ]
-            out = dot3(lax.concatenate(vectors, 1), turn)
-            stay_ref[rows:] = out[:, :half]
-            leave_ref[rows:] = out[:, half:]
+        ids = f[VROW] + lax.broadcasted_iota(jnp.int32, (vector_rows, half), 0)
+        cols = lax.broadcasted_iota(jnp.int32, (vector_rows, half), 1)
+        position = jnp.where(zero, 0, 2)
+        vectors = [
+            (ids == f[LABEL + position + k] * half + cols).astype(jnp.float32)
+            for k in range(2)
+        ]
+        out = dot3(lax.concatenate(vectors, 1), turn)
+        stay_ref[rows:] = out[:, :half]
+        leave_ref[rows:] = out[:, half:]
 
     return call(
-        body, facts, packs + [rows_of], (shape(rows + vector_rows, half),) * 2
+        body, facts, [rotation, rows_of], (shape(rows + vector_rows, half),) * 2
     )
 
 
@@ -276,55 +267,45 @@
     refs[1][...] = jnp.where(core, one, zero)
 
 
-def first_cross_gram(facts, own, others, part, half):
+def first_cross_gram(facts, own, other, part, half):
     rows = own[0].shape[0]
-    pieces = len(others)
 
     def body(f, *refs):
-        own_refs = [[r] for r in refs[:3]]
-        other_refs = [refs[3 + k : 3 + 3 * pieces : 3] for k in range(3)]
-        up_0, low_0, up_1, low_1 = refs[5 + 3 * pieces :]
-
-        def fill(target, sources):
-            at = 0
-            for ref in sources:
-                target[at : at + ref.shape[0]] = ref[...]
-                at += ref.shape[0]
-
+        up_0, low_0, up_1, low_1 = refs[8:]
         first, last = f[FIRST] == 1, f[LAST] == 1
-        for x, near, far in ((0, own_refs, other_refs), (1, other_refs, own_refs)):
+        for x, near, far in ((0, refs[:3], refs[3:6]), (1, refs[3:6], refs[:3])):
             here = f[X] == x
 
             @pl.when(here)
             def _():
-                fill(up_1, near[0])
-                fill(low_0, far[0])
+                up_1[...] = near[0][...]
+                low_0[...] = far[0][...]
 
             @pl.when(here & first)
             def _():
-                fill(up_0, near[1])
+                up_0[...] = near[1][...]
 
             @pl.when(here & ~first)
             def _():
-                fill(up_0, far[2])
+                up_0[...] = far[2][...]
 
             @pl.when(here & last)
             def _():
-                fill(low_1, far[1])
+                low_1[...] = far[1][...]
 
             @pl.when(here & ~last)
             def _():
-                fill(low_1, near[2])
+                low_1[...] = near[2][...]
 
         put_cross(
             f,
-            refs[3 + 3 * pieces :],
+            refs[6:],
             dot_tn(up_0[:part], low_0[:part]),
             dot_tn(up_1[:part], low_1[:part]),
         )
 
     outs = (shape(half, half),) * 2 + (shape(rows, half),) * 4
-    return call(body, facts, own + sum(others, []), outs)
+    return call(body, facts, own + other, outs)
 
 
 def cross_gram(facts, got, natives, part, half):
@@ -440,6 +421,19 @@
             inside = 0 <= other < pairs
             moves.append(((other, r ^ 1) if inside else (p, r), (p, r)))
         return permute(block, [((a, b), c) for (a, b), c in moves])
+
+    def first_diagonal(block, leaves):
+        moves = []
+        for p, r in devices:
+            c, even = r % 2, p - p % 2
+            if leaves:
+                source = even - 1 if c == 0 else even + 2
+                if not 0 <= source < pairs:
+                    source = even + c
+            else:
+                source = even + 1 - c
+            moves.append(((source, r - c + p % 2), (p, r)))
+        return permute(block, moves)
 
     def sum_rows(block):
         bit = 4
@@ -465,43 +459,31 @@
     def together(*arrays):
         return lax.optimization_barrier(arrays)
 
-    top = part * 3 // 8
-    got_top = exchange(
-        lax.dynamic_slice_in_dim(sector, (1 - x) * part, top), 1, 0
-    )
-    own, rest = first_gram(facts, sector, half, top)
-    own, got_top = together(sum_rows(own + exchange(own, 0, 1)), got_top)
-    near = permute(
-        own,
-        [
-            ((p, r ^ 2) if p % 2 == r % 2 else (p ^ 1, r ^ 1), (p, r))
-            for p, r in devices
-        ],
-    )
-    far = permute(
-        own, [((p ^ 1, r ^ 2), (p, r)) for p, r in devices if p % 2 != r % 2]
-    )
-    got_rest = exchange(together(rest, own)[0], 1, 0)
-    rotation, gram = first_rotation(facts, own, near, far, half)
+    got = exchange(lax.dynamic_slice_in_dim(sector, (1 - x) * part, part), 1, 0)
+    own = first_gram(facts, sector, half)
+    own = sum_rows(own + exchange(own, 0, 1))
+    rotation, gram = first_rotation(facts, own, exchange(own, 0, 2), half)
 
     for sweep_round in range(ROUNDS - 1):
-        packs = [rotation, exchange(rotation, 0, 1)]
         last_move = sweep_round == ROUNDS - 2
         if sweep_round == 0:
-            stay, leave = turn_rows(facts, packs, sector, vector_rows, half, True)
+            stay, leave = turn_rows(facts, rotation, sector, vector_rows, half, True)
             own_rows = [stay, leave, shift(leave, -2)]
-            other_rows = []
-            for got, below in ((got_top, 0), (got_rest, vector_rows)):
-                got, leave = together(got, leave)
-                stay, leave = turn_rows(facts, packs, got, below, half, False)
-                other_rows.append([stay, leave, shift(leave, 2)])
+            leave, stay = turned_gram(facts, gram, rotation, X)
+            diagonals = [first_diagonal(leave, True), first_diagonal(stay, False)]
+            other_rotation = exchange(rotation, 1, 0)
+            stay, leave = turn_rows(
+                facts, other_rotation, got, vector_rows, half, False
+            )
+            other_rows = [stay, leave, shift(leave, 2)]
         else:
+            packs = [rotation, exchange(rotation, 0, 1)]
             leave_a, leave_b, nat_l, nat_u, *native_give = turn(
                 facts, packs, blocks, half, last_move
             )
             got = [swap(leave_a, 0), swap(leave_b, 1)]
-        leave, stay = turned_gram(facts, gram, rotation)
-        diagonals = [pass_diagonal(leave), exchange(stay, 0, 1)]
+            leave, stay = turned_gram(facts, gram, rotation, CORE)
+            diagonals = [pass_diagonal(leave), exchange(stay, 0, 1)]
         if sweep_round == 0:
             own_rows[2], *diagonals = together(own_rows[2], *diagonals)
             *grams, up_0, nat_l, nat_u, low_1 = first_cross_gram(

time: 156 us -> 151 us (0.968)
  waiting for transfers between devices: 55.4 us -> 64.6 us
  starting transfers between devices: 54.3 us -> 46 us
  Pallas kernels: 40.5 us -> 36.5 us
    ppermute x37 -> x34, waiting for transfers between devices: 55.4 us -> 64.6 us  [permute(): return lax.ppermute(block, ('pair', 'row'), moves)]
    ppermute x37 -> x34, starting transfers between devices: 54.3 us -> 46 us  [permute(): return lax.ppermute(block, ('pair', 'row'), moves)]
    pallas_call x19 -> x18, Pallas kernels: 40.5 us -> 36.5 us  [call(): pl.pallas_call(body, out_shape=outs, in_specs=[pl.BlockSpec(memory_space=...]
    unnamed x4, local copies, waits for them, and re-layouts: 1.59 us -> 0.01 us
  transfers between devices with their start and end apart: 37 -> 34, of which waited for: 29 -> 25; matrix products, arithmetic and copies ran while one was open for 1% -> 0% of each run, Pallas kernels for 14% -> 13%
where the time goes in v4:
time: 151 us
  waiting for transfers between devices  64.6 us (43%)
  starting transfers between devices  46 us (30%)
  Pallas kernels  36.5 us (24%)
  local copies, waits for them, and re-layouts  2.57 us (2%)
    ppermute x34, waiting for transfers between devices, permute(): return lax.ppermute(block, ('pair', 'row'), moves)  64.6 us
    ppermute x34, starting transfers between devices, permute(): return lax.ppermute(block, ('pair', 'row'), moves)  46 us
    pallas_call x18, Pallas kernels, call(): pl.pallas_call(body, out_shape=outs, in_specs=[pl.BlockSpec(memory_space=...  36.5 us
  transfers between devices with their start and end apart: 34, of which 25 were waited for; matrix products, arithmetic and copies ran while one was open for 0% of the time, Pallas kernels for 13%

profile of v4, /device:TPU:0, one launch (start us, length us, event | category | flops | bytes accessed | tf_op | source)
XLA Modules:
  0.0 150.6 jit_solution(2096790834925613253)
XLA Ops:
  0.7 2.4 %constant_dynamic-slice_fusion = f32[1024,256]{1,0:T(8,128)} fusion(f32[2048,256]{1,0:T(8,128)} %x_ref.3, s32[]{:T(128)S(6)} %select_n.55), kind=kLoop, calls=%fused_computation.7 | loop fusion | bytes 2097156 | tf_op jit(solution)/shard_map/dynamic_slice | solution.py:462
  3.1 2.9 %collective-permute-start.6 = (f32[1024,256]{1,0:T(8,128)}, f32[1024,256]{1,0:T(8,128)S(1)}, u32[]{:S(2)}, u32[]{:S(2)}) collective-permute-start(f32[1024,256]{1,0:T(8,128)} %constant_dynamic-slice_fusion), channel_id=1, source_target_pairs={{4,0},{5,1},{6,2},{7,3},{0,4},{1,5},{2,6},{3,7},{12,8},{13,9},{14,... | collective-permute-start | bytes 3145736 | tf_op jit(solution)/shard_map/ppermute | solution.py:393
  6.2 2.6 %shard_map.49 = f32[384,128]{1,0:T(8,128)S(1)} custom-call(s32[16]{0:T(128)S(1)} %constant_dynamic-update-slice_fusion.f, f32[2048,256]{1,0:T(8,128)S(1)} %copy-done), custom_call_target="tpu_custom_call" | custom-call | tf_op jit(solution)/shard_map/pallas_call | solution.py:52
  12.0 5.4 %collective-permute-done.1.other_ref = f32[384,128]{1,0:T(8,128)S(1)} collective-permute-done((f32[384,128]{1,0:T(8,128)S(1)}, f32[384,128]{1,0:T(8,128)S(1)}, u32[]{:S(2)}, u32[]{:S(2)}) %collective-permute-start.1) | collective-permute-done | bytes 196640 | tf_op jit(solution)/shard_map/ppermute | solution.py:393
  17.4 3.4 %shard_map.50 = (f32[256,256]{1,0:T(8,128)S(1)}, f32[256,256]{1,0:T(8,128)S(1)}) custom-call(s32[16]{0:T(128)S(1)} %constant_dynamic-update-slice_fusion.f, f32[384,128]{1,0:T(8,128)S(1)} %add.37.own_ref, f32[384,128]{1,0:T(8,128)S(1)} %collective-permute-done.1.other_ref), custom_call_target="tpu_custom_call" | custom-call | tf_op jit(solution)/shard_map/pallas_call | solution.py:52
  23.7 11.3 %collective-permute-done.5.rotation_ref = f32[256,256]{1,0:T(8,128)S(1)} collective-permute-done((f32[256,256]{1,0:T(8,128)S(1)}, f32[256,256]{1,0:T(8,128)S(1)}, u32[]{:S(2)}, u32[]{:S(2)}) %collective-permute-start.5) | collective-permute-done | bytes 262176 | tf_op jit(solution)/shard_map/ppermute | solution.py:393
  36.2 3.8 %collective-permute-start.7 = (f32[1280,128]{1,0:T(8,128)S(1)}, f32[1280,128]{1,0:T(8,128)S(1)}, u32[]{:S(2)}, u32[]{:S(2)}) collective-permute-start(f32[1280,128]{1,0:T(8,128)S(1)} %get-tuple-element.75.refs_4_), channel_id=1, source_target_pairs={{12,4},{13,5},{14,6},{15,7},{0,8},{1,9},{2,10},{3,11},{20,12},{21,... | collective-permute-start | bytes 1966088 | tf_op jit(solution)/shard_map/ppermute | solution.py:393
  43.0 5.9 %collective-permute-done.4.refs_5_ = f32[128,128]{1,0:T(8,128)S(1)} collective-permute-done((f32[128,128]{1,0:T(8,128)S(1)}, f32[128,128]{1,0:T(8,128)S(1)}, u32[]{:S(2)}, u32[]{:S(2)}) %collective-permute-start.4) | collective-permute-done | bytes 65568 | tf_op jit(solution)/shard_map/ppermute | solution.py:393
  48.8 4.2 %collective-permute-done.7.refs_5_ = f32[1280,128]{1,0:T(8,128)S(1)} collective-permute-done((f32[1280,128]{1,0:T(8,128)S(1)}, f32[1280,128]{1,0:T(8,128)S(1)}, u32[]{:S(2)}, u32[]{:S(2)}) %collective-permute-start.7) | collective-permute-done | bytes 655392 | tf_op jit(solution)/shard_map/ppermute | solution.py:393
  53.1 1.9 %shard_map.54 = (f32[128,128]{1,0:T(8,128)S(1)}, f32[128,128]{1,0:T(8,128)S(1)}, f32[1280,128]{1,0:T(8,128)S(1)}, f32[1280,128]{1,0:T(8,128)S(1)}, f32[1280,128]{1,0:T(8,128)S(1)}, /*index=5*/f32[1280,128]{1,0:T(8,128)S(1)}) custom-call(s32[16]{0:T(128)S(1)} %constant_dynamic-update-slice_fusion.f, f32[1280,128]{1,0:T(8,128)S(1)} %get-tuple-element.68.refs_0_, ...), custom_call_target="tpu_custom_call" | custom-call | tf_op jit(solution)/shard_map/pallas_call | solution.py:52
  56.3 3.4 %collective-permute-start.11 = (f32[128,128]{1,0:T(8,128)S(1)}, f32[128,128]{1,0:T(8,128)S(1)}, u32[]{:S(2)}, u32[]{:S(2)}) collective-permute-start(f32[128,128]{1,0:T(8,128)S(1)} %add.39.refs_0_), channel_id=1, source_target_pairs={{6,0},{7,1},{4,2},{5,3},{2,4},{3,5},{0,6},{1,7},{14,8},{15,9},{12,... | collective-permute-start | bytes 196616 | tf_op jit(solution)/shard_map/ppermute | solution.py:393
  60.3 1.8 %collective-permute-done.11.refs_3_ = f32[128,128]{1,0:T(8,128)S(1)} collective-permute-done((f32[128,128]{1,0:T(8,128)S(1)}, f32[128,128]{1,0:T(8,128)S(1)}, u32[]{:S(2)}, u32[]{:S(2)}) %collective-permute-start.11) | collective-permute-done | bytes 65568 | tf_op jit(solution)/shard_map/ppermute | solution.py:393
  62.1 1.9 %collective-permute-done.10.refs_2_ = f32[128,128]{1,0:T(8,128)S(1)} collective-permute-done((f32[128,128]{1,0:T(8,128)S(1)}, f32[128,128]{1,0:T(8,128)S(1)}, u32[]{:S(2)}, u32[]{:S(2)}) %collective-permute-start.10) | collective-permute-done | bytes 65568 | tf_op jit(solution)/shard_map/ppermute | solution.py:393
  64.0 3.4 %shard_map.55 = (f32[256,256]{1,0:T(8,128)S(1)}, f32[256,256]{1,0:T(8,128)S(1)}) custom-call(s32[16]{0:T(128)S(1)} %constant_dynamic-update-slice_fusion.f, f32[128,128]{1,0:T(8,128)S(1)} %add.39.refs_0_, f32[128,128]{1,0:T(8,128)S(1)} %collective-permute-done.9.refs_1_, f32[128,128]{1,0:T(8,128)S(1)} %collective-permute-done.10.refs_2_, ...), custom_call_target="tpu_custom_call" | custom-call | tf_op jit(solution)/shard_map/pallas_call | solution.py:52
  69.0 1.8 %shard_map.56 = (f32[1280,128]{1,0:T(8,128)S(1)}, f32[1280,128]{1,0:T(8,128)S(1)}, f32[1280,128]{1,0:T(8,128)S(1)}, f32[1280,128]{1,0:T(8,128)S(1)}) custom-call(s32[16]{0:T(128)S(1)} %constant_dynamic-update-slice_fusion.f, f32[256,256]{1,0:T(8,128)S(1)} %get-tuple-element.80.own_ref.rotation_ref, f32[256,256]{1,0:T(8,128)S(1)} %collective-permute-done.12.other_ref, ...), custom_call_target="tpu_custom_call" | custom-call | tf_op jit(solution)/shard_map/pallas_call | solution.py:52
  70.8 2.2 %collective-permute-start.13 = (f32[1280,128]{1,0:T(8,128)S(1)}, f32[1280,128]{1,0:T(8,128)S(1)}, u32[]{:S(2)}, u32[]{:S(2)}) collective-permute-start(f32[1280,128]{1,0:T(8,128)S(1)} %get-tuple-element.85), channel_id=1, source_target_pairs={{8,0},{9,1},{10,2},{11,3},{12,4},{13,5},{14,6},{15,7},{0,8},{1,9},... | collective-permute-start | bytes 1966088 | tf_op jit(solution)/shard_map/ppermute | solution.py:393
  76.1 5.8 %collective-permute-start.16 = (f32[128,128]{1,0:T(8,128)S(1)}, f32[128,128]{1,0:T(8,128)S(1)}, u32[]{:S(2)}, u32[]{:S(2)}) collective-permute-start(f32[128,128]{1,0:T(8,128)S(1)} %get-tuple-element.89), channel_id=1, source_target_pairs={{1,0},{0,1},{3,2},{2,3},{5,4},{4,5},{7,6},{6,7},{9,8},{8,9},{11,10... | collective-permute-start | bytes 196616 | tf_op jit(solution)/shard_map/ppermute | solution.py:393
  82.8 5.2 %collective-permute-done.13.refs_0_ = f32[1280,128]{1,0:T(8,128)S(1)} collective-permute-done((f32[1280,128]{1,0:T(8,128)S(1)}, f32[1280,128]{1,0:T(8,128)S(1)}, u32[]{:S(2)}, u32[]{:S(2)}) %collective-permute-start.13) | collective-permute-done | bytes 655392 | tf_op jit(solution)/shard_map/ppermute | solution.py:393
  88.0 1.7 %shard_map.58 = (f32[128,128]{1,0:T(8,128)S(1)}, f32[128,128]{1,0:T(8,128)S(1)}, f32[1280,128]{1,0:T(8,128)S(1)}, f32[1280,128]{1,0:T(8,128)S(1)}) custom-call(s32[16]{0:T(128)S(1)} %constant_dynamic-update-slice_fusion.f, f32[1280,128]{1,0:T(8,128)S(1)} %collective-permute-done.13.refs_0_, f32[1280,128]{1,0:T(8,128)S(1)} %collective-permute-done.14.refs_1_, ...), custom_call_target="tpu_custom_call" | custom-call | tf_op jit(solution)/shard_map/pallas_call | solution.py:52
  91.2 1.9 %collective-permute-start.20 = (f32[128,128]{1,0:T(8,128)S(1)}, f32[128,128]{1,0:T(8,128)S(1)}, u32[]{:S(2)}, u32[]{:S(2)}) collective-permute-start(f32[128,128]{1,0:T(8,128)S(1)} %add.40.refs_0_), channel_id=1, source_target_pairs={{6,0},{7,1},{4,2},{5,3},{2,4},{3,5},{0,6},{1,7},{14,8},{15,9},{12,... | collective-permute-start | bytes 196616 | tf_op jit(solution)/shard_map/ppermute | solution.py:393
  94.8 1.8 %collective-permute-done.20.refs_3_ = f32[128,128]{1,0:T(8,128)S(1)} collective-permute-done((f32[128,128]{1,0:T(8,128)S(1)}, f32[128,128]{1,0:T(8,128)S(1)}, u32[]{:S(2)}, u32[]{:S(2)}) %collective-permute-start.20) | collective-permute-done | bytes 65568 | tf_op jit(solution)/shard_map/ppermute | solution.py:393
  97.9 3.0 %shard_map.59 = (f32[256,256]{1,0:T(8,128)S(1)}, f32[256,256]{1,0:T(8,128)S(1)}) custom-call(s32[16]{0:T(128)S(1)} %constant_dynamic-update-slice_fusion.f, f32[128,128]{1,0:T(8,128)S(1)} %add.40.refs_0_, f32[128,128]{1,0:T(8,128)S(1)} %collective-permute-done.18.refs_1_, f32[128,128]{1,0:T(8,128)S(1)} %collective-permute-done.19.refs_2_, ...), custom_call_target="tpu_custom_call" | custom-call | tf_op jit(solution)/shard_map/pallas_call | solution.py:52
  102.6 1.8 %shard_map.60 = (f32[1280,128]{1,0:T(8,128)S(1)}, f32[1280,128]{1,0:T(8,128)S(1)}, f32[1280,128]{1,0:T(8,128)S(1)}, f32[1280,128]{1,0:T(8,128)S(1)}, f32[1280,128]{1,0:T(8,128)S(1)}) custom-call(s32[16]{0:T(128)S(1)} %constant_dynamic-update-slice_fusion.f, f32[256,256]{1,0:T(8,128)S(1)} %get-tuple-element.98.own_ref.rotation_ref, ...), custom_call_target="tpu_custom_call" | custom-call | tf_op jit(solution)/shard_map/pallas_call | solution.py:52
  104.4 4.8 %collective-permute-start.22 = (f32[1280,128]{1,0:T(8,128)S(1)}, f32[1280,128]{1,0:T(8,128)S(1)}, u32[]{:S(2)}, u32[]{:S(2)}) collective-permute-start(f32[1280,128]{1,0:T(8,128)S(1)} %get-tuple-element.101), channel_id=1, source_target_pairs={{8,0},{9,1},{10,2},{11,3},{12,4},{13,5},{14,6},{15,7},{0,8},{1,9},... | collective-permute-start | bytes 1966088 | tf_op jit(solution)/shard_map/ppermute | solution.py:393
  112.8 4.5 %collective-permute-start.25 = (f32[128,128]{1,0:T(8,128)S(1)}, f32[128,128]{1,0:T(8,128)S(1)}, u32[]{:S(2)}, u32[]{:S(2)}) collective-permute-start(f32[128,128]{1,0:T(8,128)S(1)} %get-tuple-element.105), channel_id=1, source_target_pairs={{1,0},{0,1},{3,2},{2,3},{5,4},{4,5},{7,6},{6,7},{9,8},{8,9},{11,10... | collective-permute-start | bytes 196616 | tf_op jit(solution)/shard_map/ppermute | solution.py:393
  118.2 6.0 %collective-permute-done.22.a_ref.refs_0_ = f32[1280,128]{1,0:T(8,128)S(1)} collective-permute-done((f32[1280,128]{1,0:T(8,128)S(1)}, f32[1280,128]{1,0:T(8,128)S(1)}, u32[]{:S(2)}, u32[]{:S(2)}) %collective-permute-start.22) | collective-permute-done | bytes 655392 | tf_op jit(solution)/shard_map/ppermute | solution.py:393
  127.0 1.7 %shard_map.63 = (f32[128,128]{1,0:T(8,128)S(1)}, f32[128,128]{1,0:T(8,128)S(1)}, f32[1280,128]{1,0:T(8,128)S(1)}, f32[1280,128]{1,0:T(8,128)S(1)}) custom-call(s32[16]{0:T(128)S(1)} %constant_dynamic-update-slice_fusion.f, f32[1280,128]{1,0:T(8,128)S(1)} %collective-permute-done.22.a_ref.refs_0_, f32[1280,128]{1,0:T(8,128)S(1)} %collective-permute-done.23.b_ref.refs_1_, ...), custom_call_target="tpu_custom_call" | custom-call | tf_op jit(solution)/shard_map/pallas_call | solution.py:52
  130.0 2.1 %collective-permute-start.30 = (f32[128,128]{1,0:T(8,128)S(1)}, f32[128,128]{1,0:T(8,128)S(1)}, u32[]{:S(2)}, u32[]{:S(2)}) collective-permute-start(f32[128,128]{1,0:T(8,128)S(1)} %add.41.refs_0_), channel_id=1, source_target_pairs={{6,0},{7,1},{4,2},{5,3},{2,4},{3,5},{0,6},{1,7},{14,8},{15,9},{12,... | collective-permute-start | bytes 196616 | tf_op jit(solution)/shard_map/ppermute | solution.py:393
  134.1 2.4 %collective-permute-done.30.refs_3_ = f32[128,128]{1,0:T(8,128)S(1)} collective-permute-done((f32[128,128]{1,0:T(8,128)S(1)}, f32[128,128]{1,0:T(8,128)S(1)}, u32[]{:S(2)}, u32[]{:S(2)}) %collective-permute-start.30) | collective-permute-done | bytes 65568 | tf_op jit(solution)/shard_map/ppermute | solution.py:393
  138.4 3.4 %shard_map.65 = (f32[264,256]{1,0:T(8,128)S(1)}, f32[256,256]{1,0:T(8,128)}) custom-call(s32[16]{0:T(128)S(1)} %constant_dynamic-update-slice_fusion.f, f32[128,128]{1,0:T(8,128)S(1)} %add.41.refs_0_, f32[128,128]{1,0:T(8,128)S(1)} %collective-permute-done.28.refs_1_, f32[128,128]{1,0:T(8,128)S(1)} %collective-permute-done.29.refs_2_, ...), custom_call_target="tpu_custom_call" | custom-call | tf_op jit(solution)/shard_map/pallas_call | solution.py:52
  143.4 3.9 %collective-permute-done.33.refs_8_ = f32[768,128]{1,0:T(8,128)S(1)} collective-permute-done((f32[768,128]{1,0:T(8,128)S(1)}, f32[768,128]{1,0:T(8,128)S(1)}, u32[]{:S(2)}, u32[]{:S(2)}) %collective-permute-start.33) | collective-permute-done | bytes 393248 | tf_op jit(solution)/shard_map/ppermute | solution.py:393
  147.4 3.3 %shard_map.66 = (f32[2048,256]{1,0:T(8,128)}, f32[512,256]{1,0:T(8,128)}, f32[1,256]{1,0:T(1,128)}) custom-call(s32[16]{0:T(128)S(1)} %constant_dynamic-update-slice_fusion.f, f32[264,256]{1,0:T(8,128)S(1)} %get-tuple-element.122.refs_0_, f32[264,256]{1,0:T(8,128)S(1)} %collective-permute-done.32.refs_1_, f32[1280,128]{1,0:T(8,128)S(1)} %get-tuple-element.123.refs_2_, ...), custom_call_target="tpu_custom_call" | custom-call | tf_op jit(solution)/shard_map/pallas_call | solution.py:52
  (65 shorter events, 38.1 us)
Async XLA Ops:
  3.1 31.9 %collective-permute-start.6 = (f32[1024,256]{1,0:T(8,128)}, f32[1024,256]{1,0:T(8,128)S(1)}, u32[]{:S(2)}, u32[]{:S(2)}) collective-permute-start(f32[1024,256]{1,0:T(8,128)} %constant_dynamic-slice_fusion), channel_id=1, source_target_pairs={{4,0},{5,1},{6,2},{7,3},{0,4},{1,5},{2,6},{3,7},{12,8},{13,9},{14,... | collective-permute-start | bytes 3145736 | tf_op jit(solution)/shard_map/ppermute | solution.py:393
  8.8 1.5 %collective-permute-start = (f32[384,128]{1,0:T(8,128)S(1)}, f32[384,128]{1,0:T(8,128)S(1)}, u32[]{:S(2)}, u32[]{:S(2)}) collective-permute-start(f32[384,128]{1,0:T(8,128)S(1)} %shard_map.49), channel_id=1, source_target_pairs={{1,0},{0,1},{3,2},{2,3},{5,4},{4,5},{7,6},{6,7},{9,8},{8,9},{11,10... | collective-permute-start | bytes 589832 | tf_op jit(solution)/shard_map/ppermute | solution.py:393
  10.4 7.0 %collective-permute-start.1 = (f32[384,128]{1,0:T(8,128)S(1)}, f32[384,128]{1,0:T(8,128)S(1)}, u32[]{:S(2)}, u32[]{:S(2)}) collective-permute-start(f32[384,128]{1,0:T(8,128)S(1)} %add.37.own_ref), channel_id=1, source_target_pairs={{2,0},{3,1},{0,2},{1,3},{6,4},{7,5},{4,6},{5,7},{10,8},{11,9},{8,1... | collective-permute-start | bytes 589832 | tf_op jit(solution)/shard_map/ppermute | solution.py:393
  20.8 14.2 %collective-permute-start.5 = (f32[256,256]{1,0:T(8,128)S(1)}, f32[256,256]{1,0:T(8,128)S(1)}, u32[]{:S(2)}, u32[]{:S(2)}) collective-permute-start(f32[256,256]{1,0:T(8,128)S(1)} %get-tuple-element.67.rotation_ref), channel_id=1, source_target_pairs={{4,0},{5,1},{6,2},{7,3},{0,4},{1,5},{2,6},{3,7},{12,8},{13,9},{14,... | collective-permute-start | bytes 786440 | tf_op jit(solution)/shard_map/ppermute | solution.py:393
  22.4 26.4 %collective-permute-start.2 = (f32[1280,128]{1,0:T(8,128)S(1)}, f32[1280,128]{1,0:T(8,128)S(1)}, u32[]{:S(2)}, u32[]{:S(2)}) collective-permute-start(f32[1280,128]{1,0:T(8,128)S(1)} %get-tuple-element.69.refs_1_), channel_id=1, source_target_pairs={{8,0},{9,1},{10,2},{11,3},{16,8},{17,9},{18,10},{19,11},{4,12},{5,... | collective-permute-start | bytes 1966088 | tf_op jit(solution)/shard_map/ppermute | solution.py:393
  36.2 16.8 %collective-permute-start.7 = (f32[1280,128]{1,0:T(8,128)S(1)}, f32[1280,128]{1,0:T(8,128)S(1)}, u32[]{:S(2)}, u32[]{:S(2)}) collective-permute-start(f32[1280,128]{1,0:T(8,128)S(1)} %get-tuple-element.75.refs_4_), channel_id=1, source_target_pairs={{12,4},{13,5},{14,6},{15,7},{0,8},{1,9},{2,10},{3,11},{20,12},{21,... | collective-permute-start | bytes 1966088 | tf_op jit(solution)/shard_map/ppermute | solution.py:393
  42.3 6.5 %collective-permute-start.4 = (f32[128,128]{1,0:T(8,128)S(1)}, f32[128,128]{1,0:T(8,128)S(1)}, u32[]{:S(2)}, u32[]{:S(2)}) collective-permute-start(f32[128,128]{1,0:T(8,128)S(1)} %get-tuple-element.72), channel_id=1, source_target_pairs={{4,0},{0,1},{6,2},{2,3},{5,4},{1,5},{7,6},{3,7},{12,8},{8,9},{14,1... | collective-permute-start | bytes 196616 | tf_op jit(solution)/shard_map/ppermute | solution.py:393
  54.9 1.3 collective-permute-start.8
  56.3 5.8 %collective-permute-start.11 = (f32[128,128]{1,0:T(8,128)S(1)}, f32[128,128]{1,0:T(8,128)S(1)}, u32[]{:S(2)}, u32[]{:S(2)}) collective-permute-start(f32[128,128]{1,0:T(8,128)S(1)} %add.39.refs_0_), channel_id=1, source_target_pairs={{6,0},{7,1},{4,2},{5,3},{2,4},{3,5},{0,6},{1,7},{14,8},{15,9},{12,... | collective-permute-start | bytes 196616 | tf_op jit(solution)/shard_map/ppermute | solution.py:393
  59.7 4.3 %collective-permute-start.10 = (f32[128,128]{1,0:T(8,128)S(1)}, f32[128,128]{1,0:T(8,128)S(1)}, u32[]{:S(2)}, u32[]{:S(2)}) collective-permute-start(f32[128,128]{1,0:T(8,128)S(1)} %add.39.refs_0_), channel_id=1, source_target_pairs={{4,0},{5,1},{6,2},{7,3},{0,4},{1,5},{2,6},{3,7},{12,8},{13,9},{14,... | collective-permute-start | bytes 196616 | tf_op jit(solution)/shard_map/ppermute | solution.py:393
  59.7 4.3 %collective-permute-start.9 = (f32[128,128]{1,0:T(8,128)S(1)}, f32[128,128]{1,0:T(8,128)S(1)}, u32[]{:S(2)}, u32[]{:S(2)}) collective-permute-start(f32[128,128]{1,0:T(8,128)S(1)} %add.39.refs_0_), channel_id=1, source_target_pairs={{2,0},{3,1},{0,2},{1,3},{6,4},{7,5},{4,6},{5,7},{10,8},{11,9},{8,1... | collective-permute-start | bytes 196616 | tf_op jit(solution)/shard_map/ppermute | solution.py:393
  67.4 1.6 %collective-permute-start.12 = (f32[256,256]{1,0:T(8,128)S(1)}, f32[256,256]{1,0:T(8,128)S(1)}, u32[]{:S(2)}, u32[]{:S(2)}) collective-permute-start(f32[256,256]{1,0:T(8,128)S(1)} %get-tuple-element.80.own_ref.rotation_ref), channel_id=1, source_target_pairs={{1,0},{0,1},{3,2},{2,3},{5,4},{4,5},{7,6},{6,7},{9,8},{8,9},{11,10... | collective-permute-start | bytes 786440 | tf_op jit(solution)/shard_map/ppermute | solution.py:393
  70.8 17.2 %collective-permute-start.13 = (f32[1280,128]{1,0:T(8,128)S(1)}, f32[1280,128]{1,0:T(8,128)S(1)}, u32[]{:S(2)}, u32[]{:S(2)}) collective-permute-start(f32[1280,128]{1,0:T(8,128)S(1)} %get-tuple-element.85), channel_id=1, source_target_pairs={{8,0},{9,1},{10,2},{11,3},{12,4},{13,5},{14,6},{15,7},{0,8},{1,9},... | collective-permute-start | bytes 1966088 | tf_op jit(solution)/shard_map/ppermute | solution.py:393
  73.0 15.1 %collective-permute-start.14 = (f32[1280,128]{1,0:T(8,128)S(1)}, f32[1280,128]{1,0:T(8,128)S(1)}, u32[]{:S(2)}, u32[]{:S(2)}) collective-permute-start(f32[1280,128]{1,0:T(8,128)S(1)} %get-tuple-element.86), channel_id=1, source_target_pairs={{0,0},{1,1},{2,2},{3,3},{4,4},{5,5},{6,6},{7,7},{16,8},{17,9},{18,... | collective-permute-start | bytes 1966088 | tf_op jit(solution)/shard_map/ppermute | solution.py:393
  75.5 6.5 %collective-permute-start.15 = (f32[128,128]{1,0:T(8,128)S(1)}, f32[128,128]{1,0:T(8,128)S(1)}, u32[]{:S(2)}, u32[]{:S(2)}) collective-permute-start(f32[128,128]{1,0:T(8,128)S(1)} %get-tuple-element.88), channel_id=1, source_target_pairs={{0,0},{8,1},{2,2},{10,3},{4,4},{12,5},{6,6},{14,7},{1,8},{16,9},{3... | collective-permute-start | bytes 196616 | tf_op jit(solution)/shard_map/ppermute | solution.py:393
  76.1 6.7 %collective-permute-start.16 = (f32[128,128]{1,0:T(8,128)S(1)}, f32[128,128]{1,0:T(8,128)S(1)}, u32[]{:S(2)}, u32[]{:S(2)}) collective-permute-start(f32[128,128]{1,0:T(8,128)S(1)} %get-tuple-element.89), channel_id=1, source_target_pairs={{1,0},{0,1},{3,2},{2,3},{5,4},{4,5},{7,6},{6,7},{9,8},{8,9},{11,10... | collective-permute-start | bytes 196616 | tf_op jit(solution)/shard_map/ppermute | solution.py:393
  89.7 1.5 collective-permute-start.17
  91.2 5.4 %collective-permute-start.20 = (f32[128,128]{1,0:T(8,128)S(1)}, f32[128,128]{1,0:T(8,128)S(1)}, u32[]{:S(2)}, u32[]{:S(2)}) collective-permute-start(f32[128,128]{1,0:T(8,128)S(1)} %add.40.refs_0_), channel_id=1, source_target_pairs={{6,0},{7,1},{4,2},{5,3},{2,4},{3,5},{0,6},{1,7},{14,8},{15,9},{12,... | collective-permute-start | bytes 196616 | tf_op jit(solution)/shard_map/ppermute | solution.py:393
  93.1 4.3 %collective-permute-start.19 = (f32[128,128]{1,0:T(8,128)S(1)}, f32[128,128]{1,0:T(8,128)S(1)}, u32[]{:S(2)}, u32[]{:S(2)}) collective-permute-start(f32[128,128]{1,0:T(8,128)S(1)} %add.40.refs_0_), channel_id=1, source_target_pairs={{4,0},{5,1},{6,2},{7,3},{0,4},{1,5},{2,6},{3,7},{12,8},{13,9},{14,... | collective-permute-start | bytes 196616 | tf_op jit(solution)/shard_map/ppermute | solution.py:393
  93.4 4.5 %collective-permute-start.18 = (f32[128,128]{1,0:T(8,128)S(1)}, f32[128,128]{1,0:T(8,128)S(1)}, u32[]{:S(2)}, u32[]{:S(2)}) collective-permute-start(f32[128,128]{1,0:T(8,128)S(1)} %add.40.refs_0_), channel_id=1, source_target_pairs={{2,0},{3,1},{0,2},{1,3},{6,4},{7,5},{4,6},{5,7},{10,8},{11,9},{8,1... | collective-permute-start | bytes 196616 | tf_op jit(solution)/shard_map/ppermute | solution.py:393
  101.0 1.6 %collective-permute-start.21 = (f32[256,256]{1,0:T(8,128)S(1)}, f32[256,256]{1,0:T(8,128)S(1)}, u32[]{:S(2)}, u32[]{:S(2)}) collective-permute-start(f32[256,256]{1,0:T(8,128)S(1)} %get-tuple-element.98.own_ref.rotation_ref), channel_id=1, source_target_pairs={{1,0},{0,1},{3,2},{2,3},{5,4},{4,5},{7,6},{6,7},{9,8},{8,9},{11,10... | collective-permute-start | bytes 786440 | tf_op jit(solution)/shard_map/ppermute | solution.py:393
  104.4 19.9 %collective-permute-start.22 = (f32[1280,128]{1,0:T(8,128)S(1)}, f32[1280,128]{1,0:T(8,128)S(1)}, u32[]{:S(2)}, u32[]{:S(2)}) collective-permute-start(f32[1280,128]{1,0:T(8,128)S(1)} %get-tuple-element.101), channel_id=1, source_target_pairs={{8,0},{9,1},{10,2},{11,3},{12,4},{13,5},{14,6},{15,7},{0,8},{1,9},... | collective-permute-start | bytes 1966088 | tf_op jit(solution)/shard_map/ppermute | solution.py:393
  109.2 15.0 %collective-permute-start.23 = (f32[1280,128]{1,0:T(8,128)S(1)}, f32[1280,128]{1,0:T(8,128)S(1)}, u32[]{:S(2)}, u32[]{:S(2)}) collective-permute-start(f32[1280,128]{1,0:T(8,128)S(1)} %get-tuple-element.102), channel_id=1, source_target_pairs={{0,0},{1,1},{2,2},{3,3},{4,4},{5,5},{6,6},{7,7},{16,8},{17,9},{18,... | collective-permute-start | bytes 1966088 | tf_op jit(solution)/shard_map/ppermute | solution.py:393
  109.9 16.6 %collective-permute-start.26 = (f32[1280,128]{1,0:T(8,128)S(1)}, f32[1280,128]{1,0:T(8,128)S(1)}, u32[]{:S(2)}, u32[]{:S(2)}) collective-permute-start(f32[1280,128]{1,0:T(8,128)S(1)} %get-tuple-element.108), channel_id=1, source_target_pairs={{4,0},{5,1},{6,2},{7,3},{0,4},{1,5},{2,6},{3,7},{12,8},{13,9},{14,... | collective-permute-start | bytes 1966088 | tf_op jit(solution)/shard_map/ppermute | solution.py:393
  112.1 5.2 %collective-permute-start.24 = (f32[128,128]{1,0:T(8,128)S(1)}, f32[128,128]{1,0:T(8,128)S(1)}, u32[]{:S(2)}, u32[]{:S(2)}) collective-permute-start(f32[128,128]{1,0:T(8,128)S(1)} %get-tuple-element.104), channel_id=1, source_target_pairs={{0,0},{8,1},{2,2},{10,3},{4,4},{12,5},{6,6},{14,7},{1,8},{16,9},{3... | collective-permute-start | bytes 196616 | tf_op jit(solution)/shard_map/ppermute | solution.py:393
  112.8 5.4 %collective-permute-start.25 = (f32[128,128]{1,0:T(8,128)S(1)}, f32[128,128]{1,0:T(8,128)S(1)}, u32[]{:S(2)}, u32[]{:S(2)}) collective-permute-start(f32[128,128]{1,0:T(8,128)S(1)} %get-tuple-element.105), channel_id=1, source_target_pairs={{1,0},{0,1},{3,2},{2,3},{5,4},{4,5},{7,6},{6,7},{9,8},{8,9},{11,10... | collective-permute-start | bytes 196616 | tf_op jit(solution)/shard_map/ppermute | solution.py:393
  126.4 10.7 %collective-permute-start.31 = (f32[512,128]{1,0:T(8,128)S(1)}, f32[512,128]{1,0:T(8,128)S(1)}, u32[]{:S(2)}, u32[]{:S(2)}) collective-permute-start(f32[512,128]{1,0:T(8,128)S(1)} %shard_map.62), channel_id=1, source_target_pairs={{4,0},{5,1},{6,2},{7,3},{0,4},{1,5},{2,6},{3,7},{12,8},{13,9},{14,... | collective-permute-start | bytes 786440 | tf_op jit(solution)/shard_map/ppermute | solution.py:393
  130.0 6.6 %collective-permute-start.30 = (f32[128,128]{1,0:T(8,128)S(1)}, f32[128,128]{1,0:T(8,128)S(1)}, u32[]{:S(2)}, u32[]{:S(2)}) collective-permute-start(f32[128,128]{1,0:T(8,128)S(1)} %add.41.refs_0_), channel_id=1, source_target_pairs={{6,0},{7,1},{4,2},{5,3},{2,4},{3,5},{0,6},{1,7},{14,8},{15,9},{12,... | collective-permute-start | bytes 196616 | tf_op jit(solution)/shard_map/ppermute | solution.py:393
  132.1 4.6 %collective-permute-start.29 = (f32[128,128]{1,0:T(8,128)S(1)}, f32[128,128]{1,0:T(8,128)S(1)}, u32[]{:S(2)}, u32[]{:S(2)}) collective-permute-start(f32[128,128]{1,0:T(8,128)S(1)} %add.41.refs_0_), channel_id=1, source_target_pairs={{4,0},{5,1},{6,2},{7,3},{0,4},{1,5},{2,6},{3,7},{12,8},{13,9},{14,... | collective-permute-start | bytes 196616 | tf_op jit(solution)/shard_map/ppermute | solution.py:393
  132.6 4.5 %collective-permute-start.28 = (f32[128,128]{1,0:T(8,128)S(1)}, f32[128,128]{1,0:T(8,128)S(1)}, u32[]{:S(2)}, u32[]{:S(2)}) collective-permute-start(f32[128,128]{1,0:T(8,128)S(1)} %add.41.refs_0_), channel_id=1, source_target_pairs={{2,0},{3,1},{0,2},{1,3},{6,4},{7,5},{4,6},{5,7},{10,8},{11,9},{8,1... | collective-permute-start | bytes 196616 | tf_op jit(solution)/shard_map/ppermute | solution.py:393
  137.1 10.3 %collective-permute-start.33 = (f32[768,128]{1,0:T(8,128)S(1)}, f32[768,128]{1,0:T(8,128)S(1)}, u32[]{:S(2)}, u32[]{:S(2)}) collective-permute-start(f32[768,128]{1,0:T(8,128)S(1)} %shard_map.64), channel_id=1, source_target_pairs={{4,0},{5,1},{6,2},{7,3},{0,4},{1,5},{2,6},{3,7},{12,8},{13,9},{14,... | collective-permute-start | bytes 1179656 | tf_op jit(solution)/shard_map/ppermute | solution.py:393
  141.8 1.6 %collective-permute-start.32 = (f32[264,256]{1,0:T(8,128)S(1)}, f32[264,256]{1,0:T(8,128)S(1)}, u32[]{:S(2)}, u32[]{:S(2)}) collective-permute-start(f32[264,256]{1,0:T(8,128)S(1)} %get-tuple-element.122.refs_0_), channel_id=1, source_target_pairs={{1,0},{0,1},{3,2},{2,3},{5,4},{4,5},{7,6},{6,7},{9,8},{8,9},{11,10... | collective-permute-start | bytes 811016 | tf_op jit(solution)/shard_map/ppermute | solution.py:393
  (4 other events, 13.6 us)

commit v5 on v4

--- a/solution.py
+++ b/solution.py
@@ -203,15 +203,13 @@
 
 
 def put_turned(f, refs, zero, one, half):
-    a_ref, b_ref, nat_l_ref, nat_u_ref = refs[:4]
+    a_ref, b_ref, nat_l_ref, nat_u_ref = refs
     even = f[EVEN] == 1
     to_left, to_right = zero[:, half:], one[:, :half]
     a_ref[...] = jnp.where(even, to_right, to_left)
     b_ref[...] = jnp.where(even, to_left, to_right)
     nat_l_ref[...] = one[:, half:]
     nat_u_ref[...] = zero[:, :half]
-    if len(refs) > 4:
-        refs[4][...] = jnp.where(f[X] == 0, zero[:, :half], one[:, half:])
 
 
 def turns_of(f, own_ref, other_ref):
@@ -220,45 +218,65 @@
     return swapped(f[FIRST] == 1, turn_0, 1), turn_1
 
 
-def turn_rows(facts, rotation, rows_of, vector_rows, half, own):
+def turn_rows(facts, rotation, rows_of, half, own):
     rows = rows_of.shape[0] // 2 if own else rows_of.shape[0]
 
     def body(f, rotation_ref, x_ref, stay_ref, leave_ref):
         zero = f[X] == (0 if own else 1)
         upper_leaves = jnp.where(zero, f[FIRST], 1) == 1
-        turn = split(swapped(upper_leaves, rotation_ref[...], 1))
+        turn = swapped(upper_leaves, rotation_ref[...], 1)
         here = pl.multiple_of(f[X] * rows, 8)
         out = dot3(x_ref[pl.ds(here, rows)] if own else x_ref[...], turn)
-        stay_ref[:rows] = out[:, :half]
-        leave_ref[:rows] = out[:, half:]
+        stay_ref[...] = out[:, :half]
+        leave_ref[...] = out[:, half:]
+
+    return call(body, facts, [rotation, rows_of], (shape(rows, half),) * 2)
+
+
+def first_vectors(facts, rotation, other_rotation, vector_rows, half):
+    def body(f, own_ref, other_ref, *refs):
+        even = f[X] == 0
+        own, other = own_ref[...], other_ref[...]
+        turn_0 = swapped(f[FIRST] == 1, jnp.where(even, own, other), 1)
+        turn_1 = jnp.where(even, other, own)
         ids = f[VROW] + lax.broadcasted_iota(jnp.int32, (vector_rows, half), 0)
         cols = lax.broadcasted_iota(jnp.int32, (vector_rows, half), 1)
-        position = jnp.where(zero, 0, 2)
-        vectors = [
-            (ids == f[LABEL + position + k] * half + cols).astype(jnp.float32)
-            for k in range(2)
+        up_0, low_0, up_1, low_1 = [
+            (ids == f[LABEL + k] * half + cols).astype(jnp.float32) for k in range(4)
         ]
-        out = dot3(lax.concatenate(vectors, 1), turn)
-        stay_ref[rows:] = out[:, :half]
-        leave_ref[rows:] = out[:, half:]
+        zero = dot3(lax.concatenate([up_0, low_0], 1), turn_0)
+        one = dot3(lax.concatenate([up_1, low_1], 1), turn_1)
+        put_turned(f, refs, zero, one, half)
 
     return call(
-        body, facts, [rotation, rows_of], (shape(rows + vector_rows, half),) * 2
-    )
-
-
-def turn(facts, packs, blocks, half, last_move):
-    rows = blocks[0].shape[0]
+        body, facts, [rotation, other_rotation], (shape(vector_rows, half),) * 4
+    )
+
+
+def turn(facts, packs, blocks, vectors, half, last_move):
+    part, vector_rows = blocks[0].shape[0], vectors[0].shape[0]
 
     def body(f, own_ref, other_ref, *refs):
         turn_0, turn_1 = turns_of(f, own_ref, other_ref)
-        up_0, low_0, up_1, low_1 = [r[...] for r in refs[:4]]
-        zero = dot3(lax.concatenate([up_0, low_0], 1), turn_0)
-        one = dot3(lax.concatenate([up_1, low_1], 1), turn_1)
-        put_turned(f, refs[4:], zero, one, half)
-
-    outs = (shape(rows, half),) * (5 if last_move else 4)
-    return call(body, facts, packs + blocks, outs)
+        turn_0, turn_1 = split(turn_0), split(turn_1)
+        columns = [r[...] for r in refs[:4]]
+        rows = blocks_of(f, *[r[...] for r in refs[4:8]])
+        at = 0
+        for (up_0, low_0, up_1, low_1), outs in (
+            (columns, refs[8:12]), (rows, refs[12:16])
+        ):
+            zero = dot3(lax.concatenate([up_0, low_0], 1), turn_0)
+            one = dot3(lax.concatenate([up_1, low_1], 1), turn_1)
+            put_turned(f, outs, zero, one, half)
+            if last_move:
+                given = jnp.where(f[X] == 0, zero[:, :half], one[:, half:])
+                refs[16][at : at + given.shape[0]] = given
+                at += given.shape[0]
+
+    outs = (shape(part, half),) * 4 + (shape(vector_rows, half),) * 4
+    if last_move:
+        outs = outs + (shape(part + vector_rows, half),)
+    return call(body, facts, packs + blocks + vectors, outs)
 
 
 def put_cross(f, refs, zero, one):
@@ -267,7 +285,7 @@
     refs[1][...] = jnp.where(core, one, zero)
 
 
-def first_cross_gram(facts, own, other, part, half):
+def first_cross_gram(facts, own, other, half):
     rows = own[0].shape[0]
 
     def body(f, *refs):
@@ -300,25 +318,20 @@
         put_cross(
             f,
             refs[6:],
-            dot_tn(up_0[:part], low_0[:part]),
-            dot_tn(up_1[:part], low_1[:part]),
+            dot_tn(up_0[...], low_0[...]),
+            dot_tn(up_1[...], low_1[...]),
         )
 
     outs = (shape(half, half),) * 2 + (shape(rows, half),) * 4
     return call(body, facts, own + other, outs)
 
 
-def cross_gram(facts, got, natives, part, half):
+def cross_gram(facts, got, natives, half):
     rows = got[0].shape[0]
 
     def body(f, *refs):
         up_0, low_0, up_1, low_1 = blocks_of(f, *[r[...] for r in refs[:4]])
-        put_cross(
-            f,
-            refs[4:],
-            dot_tn(up_0[:part], low_0[:part]),
-            dot_tn(up_1[:part], low_1[:part]),
-        )
+        put_cross(f, refs[4:], dot_tn(up_0, low_0), dot_tn(up_1, low_1))
         refs[6][...] = up_0
         refs[7][...] = low_1
 
@@ -326,17 +339,27 @@
     return call(body, facts, got + natives, outs)
 
 
-def give(facts, got, start, stop, half):
-    def body(f, a_ref, b_ref, out_ref):
+def give(facts, pieces, half):
+    total = sum(stop - start for _, start, stop in pieces)
+
+    def body(f, *refs):
         mine = f[X] != f[EVEN]
-        out_ref[...] = jnp.where(mine, a_ref[start:stop], b_ref[start:stop])
-
-    return call(body, facts, got, shape(stop - start, half))
-
-
-def finish(facts, packs, blocks, native, got_top, got_rest, part, half):
+        at = 0
+        for k, (_, start, stop) in enumerate(pieces):
+            a_ref, b_ref = refs[2 * k : 2 * k + 2]
+            refs[-1][at : at + stop - start] = jnp.where(
+                mine, a_ref[start:stop], b_ref[start:stop]
+            )
+            at += stop - start
+
+    return call(
+        body, facts, sum([list(got) for got, _, _ in pieces], []), shape(total, half)
+    )
+
+
+def finish(facts, packs, blocks, vectors, native, got_top, got_rest, half):
     size = 2 * half
-    vector_rows = blocks[0].shape[0] - part
+    part, vector_rows = blocks[0].shape[0], vectors[0].shape[0]
     top = got_top.shape[0]
 
     def body(f, *refs):
@@ -344,19 +367,23 @@
         mine = f[CORE] == x
         pack = jnp.where(mine, refs[0][...], refs[1][...])
         turned = split(swapped(x == 1, pack[:size], 0))
-        native_ref, top_ref, rest_ref = refs[6:9]
-        out_ref, vectors_ref, singular_ref = refs[9:]
-        up_0, low_0, up_1, low_1 = [r[...] for r in refs[2:6]]
+        native_ref, top_ref, rest_ref = refs[10:13]
+        out_ref, vectors_ref, singular_ref = refs[13:]
 
         def product(moved, native):
             return dot3(lax.concatenate([moved, native], 1), turned)
 
+        def own(up_0, low_0, up_1, low_1):
+            return product(
+                jnp.where(x == 0, up_0, low_1), jnp.where(x == 0, low_0, up_1)
+            )
+
         def put(ref, at, value):
             ref[pl.ds(pl.multiple_of(at, 8), value.shape[0])] = value
 
-        kept = product(jnp.where(x == 0, up_0, low_1), jnp.where(x == 0, low_0, up_1))
-        put(out_ref, x * part, kept[:part])
-        put(vectors_ref, x * vector_rows, kept[part:])
+        put(out_ref, x * part, own(*[r[...] for r in refs[2:6]]))
+        rows = blocks_of(f, *[r[...] for r in refs[6:10]])
+        put(vectors_ref, x * vector_rows, own(*rows))
         there = (1 - x) * part
         put(out_ref, there, product(top_ref[...], native_ref[:top]))
         rest = product(rest_ref[...], native_ref[top:])
@@ -368,7 +395,7 @@
     return call(
         body,
         facts,
-        packs + blocks + [native, got_top, got_rest],
+        packs + blocks + vectors + [native, got_top, got_rest],
         (shape(2 * part, size), shape(2 * vector_rows, size), shape(1, size)),
     )
 
@@ -467,48 +494,53 @@
     for sweep_round in range(ROUNDS - 1):
         last_move = sweep_round == ROUNDS - 2
         if sweep_round == 0:
-            stay, leave = turn_rows(facts, rotation, sector, vector_rows, half, True)
+            stay, leave = turn_rows(facts, rotation, sector, half, True)
             own_rows = [stay, leave, shift(leave, -2)]
             leave, stay = turned_gram(facts, gram, rotation, X)
             diagonals = [first_diagonal(leave, True), first_diagonal(stay, False)]
             other_rotation = exchange(rotation, 1, 0)
-            stay, leave = turn_rows(
-                facts, other_rotation, got, vector_rows, half, False
+            stay, leave = turn_rows(facts, other_rotation, got, half, False)
+            other_rows = [stay, leave, shift(leave, 2)]
+            vectors = first_vectors(
+                facts, rotation, other_rotation, vector_rows, half
             )
-            other_rows = [stay, leave, shift(leave, 2)]
+            own_rows[2], *diagonals = together(own_rows[2], *diagonals)
+            *grams, up_0, nat_l, nat_u, low_1 = first_cross_gram(
+                facts, own_rows, other_rows, half
+            )
         else:
             packs = [rotation, exchange(rotation, 0, 1)]
-            leave_a, leave_b, nat_l, nat_u, *native_give = turn(
-                facts, packs, blocks, half, last_move
+            leave_a, leave_b, nat_l, nat_u, *vectors = turn(
+                facts, packs, blocks, vectors, half, last_move
             )
             got = [swap(leave_a, 0), swap(leave_b, 1)]
             leave, stay = turned_gram(facts, gram, rotation, CORE)
             diagonals = [pass_diagonal(leave), exchange(stay, 0, 1)]
-        if sweep_round == 0:
-            own_rows[2], *diagonals = together(own_rows[2], *diagonals)
-            *grams, up_0, nat_l, nat_u, low_1 = first_cross_gram(
-                facts, own_rows, other_rows, part, half
-            )
-        else:
             *got, diagonals[0], diagonals[1] = together(*got, *diagonals)
             if last_move:
-                native = exchange(native_give[0], 1, 0)
+                native = exchange(vectors.pop(), 1, 0)
                 top = part // 2
-                top_give = give(facts, got, 0, top, half)
+                top_give = give(facts, [(got, 0, top)], half)
                 *got, native, top_give = together(*got, native, top_give)
                 got_top = exchange(top_give, 1, 0)
-            *grams, up_0, low_1 = cross_gram(facts, got, [nat_l, nat_u], part, half)
+            *grams, up_0, low_1 = cross_gram(facts, got, [nat_l, nat_u], half)
         blocks = [up_0, nat_l, nat_u, low_1]
+        vector_a, vector_b, *kept = vectors
+        vectors = [swap(vector_a, 0), swap(vector_b, 1)] + kept
+        grams[1], vectors[0], vectors[1] = together(grams[1], *vectors[:2])
         own = sum_rows(grams[0] + exchange(grams[1], 0, 1))
+        if last_move:
+            rest = give(
+                facts, [(got, top, part), (vectors[:2], 0, vector_rows)], half
+            )
         parts = [own, exchange(own, 0, 2), exchange(own, 1, 0), exchange(own, 1, 2)]
         if last_move:
-            rest = give(facts, got, top, part + vector_rows, half)
-            *parts, got_top, rest = together(*parts, got_top, rest)
+            parts[2], parts[3], got_top, rest = together(*parts[2:], got_top, rest)
             got_rest = exchange(rest, 1, 0)
         rotation, gram = later_rotation(facts, parts, diagonals, half, last_move)
     packs = [rotation, exchange(rotation, 0, 1)]
     rotated, vectors_out, singular = finish(
-        facts, packs, blocks, native, got_top, got_rest, part, half
+        facts, packs, blocks, vectors, native, got_top, got_rest, half
     )
     return rotated, vectors_out, singular.reshape(size)
 

time: 151 us -> 150 us (level)
  waiting for transfers between devices: 64.6 us -> 44.4 us
  starting transfers between devices: 46 us -> 64.1 us
    ppermute x34 -> x40, waiting for transfers between devices: 64.6 us -> 44.4 us  [permute(): return lax.ppermute(block, ('pair', 'row'), moves)]
    ppermute x34 -> x40, starting transfers between devices: 46 us -> 64.1 us  [permute(): return lax.ppermute(block, ('pair', 'row'), moves)]
    pallas_call x18 -> x19, Pallas kernels: 36.5 us -> 37.2 us  [call(): pl.pallas_call(body, out_shape=outs, in_specs=[pl.BlockSpec(memory_space=...]
  transfers between devices with their start and end apart: 34 -> 40, of which waited for: 25 -> 20; matrix products, arithmetic and copies ran while one was open for 0% -> 0% of each run, Pallas kernels for 13% -> 16%
where the time goes in v5:
time: 150 us; the launch traced here: 149 us
  starting transfers between devices  64.1 us (43%)
  waiting for transfers between devices  44.4 us (30%)
  Pallas kernels  37.2 us (25%)
  local copies, waits for them, and re-layouts  2.57 us (2%)
    ppermute x40, starting transfers between devices, permute(): return lax.ppermute(block, ('pair', 'row'), moves)  64.1 us
    ppermute x40, waiting for transfers between devices, permute(): return lax.ppermute(block, ('pair', 'row'), moves)  44.4 us
    pallas_call x19, Pallas kernels, call(): pl.pallas_call(body, out_shape=outs, in_specs=[pl.BlockSpec(memory_space=...  37.2 us
  transfers between devices with their start and end apart: 40, of which 20 were waited for; matrix products, arithmetic and copies ran while one was open for 0% of the time, Pallas kernels for 16%

profile of v5, /device:TPU:0, one launch (start us, length us, event | category | flops | bytes accessed | tf_op | source)
XLA Modules:
  0.0 149.4 jit_solution(16787519421759649726)
XLA Ops:
  0.7 2.4 %constant_dynamic-slice_fusion = f32[1024,256]{1,0:T(8,128)} fusion(f32[2048,256]{1,0:T(8,128)} %x_ref.3, s32[]{:T(128)S(6)} %select_n.55), kind=kLoop, calls=%fused_computation.7 | loop fusion | bytes 2097156 | tf_op jit(solution)/shard_map/dynamic_slice | solution.py:489
  3.1 2.9 %collective-permute-start.6 = (f32[1024,256]{1,0:T(8,128)}, f32[1024,256]{1,0:T(8,128)S(1)}, u32[]{:S(2)}, u32[]{:S(2)}) collective-permute-start(f32[1024,256]{1,0:T(8,128)} %constant_dynamic-slice_fusion), channel_id=1, source_target_pairs={{4,0},{5,1},{6,2},{7,3},{0,4},{1,5},{2,6},{3,7},{12,8},{13,9},{14,... | collective-permute-start | bytes 3145736 | tf_op jit(solution)/shard_map/ppermute | solution.py:420
  6.2 2.6 %shard_map.49 = f32[384,128]{1,0:T(8,128)S(1)} custom-call(s32[16]{0:T(128)S(1)} %constant_dynamic-update-slice_fusion.f, f32[2048,256]{1,0:T(8,128)S(1)} %copy-done), custom_call_target="tpu_custom_call" | custom-call | tf_op jit(solution)/shard_map/pallas_call | solution.py:52
  12.0 5.4 %collective-permute-done.1.other_ref = f32[384,128]{1,0:T(8,128)S(1)} collective-permute-done((f32[384,128]{1,0:T(8,128)S(1)}, f32[384,128]{1,0:T(8,128)S(1)}, u32[]{:S(2)}, u32[]{:S(2)}) %collective-permute-start.1) | collective-permute-done | bytes 196640 | tf_op jit(solution)/shard_map/ppermute | solution.py:420
  17.4 3.4 %shard_map.50 = (f32[256,256]{1,0:T(8,128)S(1)}, f32[256,256]{1,0:T(8,128)S(1)}) custom-call(s32[16]{0:T(128)S(1)} %constant_dynamic-update-slice_fusion.f, f32[384,128]{1,0:T(8,128)S(1)} %add.37.own_ref, f32[384,128]{1,0:T(8,128)S(1)} %collective-permute-done.1.other_ref), custom_call_target="tpu_custom_call" | custom-call | tf_op jit(solution)/shard_map/pallas_call | solution.py:52
  23.6 11.4 %collective-permute-done.5.rotation_ref.other_ref = f32[256,256]{1,0:T(8,128)S(1)} collective-permute-done((f32[256,256]{1,0:T(8,128)S(1)}, f32[256,256]{1,0:T(8,128)S(1)}, u32[]{:S(2)}, u32[]{:S(2)}) %collective-permute-start.5) | collective-permute-done | bytes 262176 | tf_op jit(solution)/shard_map/ppermute | solution.py:420
  36.1 3.8 %collective-permute-start.7 = (f32[1024,128]{1,0:T(8,128)S(1)}, f32[1024,128]{1,0:T(8,128)S(1)}, u32[]{:S(2)}, u32[]{:S(2)}) collective-permute-start(f32[1024,128]{1,0:T(8,128)S(1)} %get-tuple-element.94.refs_4_), channel_id=1, source_target_pairs={{12,4},{13,5},{14,6},{15,7},{0,8},{1,9},{2,10},{3,11},{20,12},{21,... | collective-permute-start | bytes 1572872 | tf_op jit(solution)/shard_map/ppermute | solution.py:420
  43.2 2.9 %collective-permute-start.8 = (f32[256,128]{1,0:T(8,128)S(1)}, f32[256,128]{1,0:T(8,128)S(1)}, u32[]{:S(2)}, u32[]{:S(2)}) collective-permute-start(f32[256,128]{1,0:T(8,128)S(1)} %get-tuple-element.97), channel_id=1, source_target_pairs={{8,0},{9,1},{10,2},{11,3},{12,4},{13,5},{14,6},{15,7},{0,8},{1,9},... | collective-permute-start | bytes 393224 | tf_op jit(solution)/shard_map/ppermute | solution.py:420
  47.8 4.3 %collective-permute-done.4.refs_5_ = f32[128,128]{1,0:T(8,128)S(1)} collective-permute-done((f32[128,128]{1,0:T(8,128)S(1)}, f32[128,128]{1,0:T(8,128)S(1)}, u32[]{:S(2)}, u32[]{:S(2)}) %collective-permute-start.4) | collective-permute-done | bytes 65568 | tf_op jit(solution)/shard_map/ppermute | solution.py:420
  52.1 1.8 %shard_map.54 = (f32[128,128]{1,0:T(8,128)S(1)}, f32[128,128]{1,0:T(8,128)S(1)}, f32[1024,128]{1,0:T(8,128)S(1)}, f32[1024,128]{1,0:T(8,128)S(1)}, f32[1024,128]{1,0:T(8,128)S(1)}, /*index=5*/f32[1024,128]{1,0:T(8,128)S(1)}) custom-call(s32[16]{0:T(128)S(1)} %constant_dynamic-update-slice_fusion.f, f32[1024,128]{1,0:T(8,128)S(1)} %get-tuple-element.87.refs_0_, ...), custom_call_target="tpu_custom_call" | custom-call | tf_op jit(solution)/shard_map/pallas_call | solution.py:52
  55.3 2.9 %collective-permute-start.13 = (f32[128,128]{1,0:T(8,128)S(1)}, f32[128,128]{1,0:T(8,128)S(1)}, u32[]{:S(2)}, u32[]{:S(2)}) collective-permute-start(f32[128,128]{1,0:T(8,128)S(1)} %add.39.refs_0_), channel_id=1, source_target_pairs={{6,0},{7,1},{4,2},{5,3},{2,4},{3,5},{0,6},{1,7},{14,8},{15,9},{12,... | collective-permute-start | bytes 196616 | tf_op jit(solution)/shard_map/ppermute | solution.py:420
  58.8 1.8 %collective-permute-done.13.refs_3_ = f32[128,128]{1,0:T(8,128)S(1)} collective-permute-done((f32[128,128]{1,0:T(8,128)S(1)}, f32[128,128]{1,0:T(8,128)S(1)}, u32[]{:S(2)}, u32[]{:S(2)}) %collective-permute-start.13) | collective-permute-done | bytes 65568 | tf_op jit(solution)/shard_map/ppermute | solution.py:420
  60.6 1.9 %collective-permute-done.12.refs_2_ = f32[128,128]{1,0:T(8,128)S(1)} collective-permute-done((f32[128,128]{1,0:T(8,128)S(1)}, f32[128,128]{1,0:T(8,128)S(1)}, u32[]{:S(2)}, u32[]{:S(2)}) %collective-permute-start.12) | collective-permute-done | bytes 65568 | tf_op jit(solution)/shard_map/ppermute | solution.py:420
  62.6 3.4 %shard_map.56 = (f32[256,256]{1,0:T(8,128)S(1)}, f32[256,256]{1,0:T(8,128)S(1)}) custom-call(s32[16]{0:T(128)S(1)} %constant_dynamic-update-slice_fusion.f, f32[128,128]{1,0:T(8,128)S(1)} %add.39.refs_0_, f32[128,128]{1,0:T(8,128)S(1)} %collective-permute-done.11.refs_1_, f32[128,128]{1,0:T(8,128)S(1)} %collective-permute-done.12.refs_2_, ...), custom_call_target="tpu_custom_call" | custom-call | tf_op jit(solution)/shard_map/pallas_call | solution.py:52
  67.6 1.8 %shard_map.57 = (f32[1024,128]{1,0:T(8,128)S(1)}, f32[1024,128]{1,0:T(8,128)S(1)}, f32[1024,128]{1,0:T(8,128)S(1)}, f32[1024,128]{1,0:T(8,128)S(1)}, f32[256,128...) custom-call(s32[16]{0:T(128)S(1)} %constant_dynamic-update-slice_fusion.f, ...), custom_call_target="tpu_custom_call" | custom-call | tf_op jit(solution)/shard_map/pallas_call | solution.py:52
  69.4 2.4 %collective-permute-start.15 = (f32[1024,128]{1,0:T(8,128)S(1)}, f32[1024,128]{1,0:T(8,128)S(1)}, u32[]{:S(2)}, u32[]{:S(2)}) collective-permute-start(f32[1024,128]{1,0:T(8,128)S(1)} %get-tuple-element.111), channel_id=1, source_target_pairs={{8,0},{9,1},{10,2},{11,3},{12,4},{13,5},{14,6},{15,7},{0,8},{1,9},... | collective-permute-start | bytes 1572872 | tf_op jit(solution)/shard_map/ppermute | solution.py:420
  75.0 5.3 %collective-permute-start.19 = (f32[256,128]{1,0:T(8,128)S(1)}, f32[256,128]{1,0:T(8,128)S(1)}, u32[]{:S(2)}, u32[]{:S(2)}) collective-permute-start(f32[256,128]{1,0:T(8,128)S(1)} %get-tuple-element.122), channel_id=1, source_target_pairs={{8,0},{9,1},{10,2},{11,3},{12,4},{13,5},{14,6},{15,7},{0,8},{1,9},... | collective-permute-start | bytes 393224 | tf_op jit(solution)/shard_map/ppermute | solution.py:420
  81.0 4.8 %collective-permute-start.18 = (f32[128,128]{1,0:T(8,128)S(1)}, f32[128,128]{1,0:T(8,128)S(1)}, u32[]{:S(2)}, u32[]{:S(2)}) collective-permute-start(f32[128,128]{1,0:T(8,128)S(1)} %get-tuple-element.115), channel_id=1, source_target_pairs={{1,0},{0,1},{3,2},{2,3},{5,4},{4,5},{7,6},{6,7},{9,8},{8,9},{11,10... | collective-permute-start | bytes 196616 | tf_op jit(solution)/shard_map/ppermute | solution.py:420
  86.7 1.7 %shard_map.59 = (f32[128,128]{1,0:T(8,128)S(1)}, f32[128,128]{1,0:T(8,128)S(1)}, f32[1024,128]{1,0:T(8,128)S(1)}, f32[1024,128]{1,0:T(8,128)S(1)}) custom-call(s32[16]{0:T(128)S(1)} %constant_dynamic-update-slice_fusion.f, f32[1024,128]{1,0:T(8,128)S(1)} %collective-permute-done.15.refs_0_, f32[1024,128]{1,0:T(8,128)S(1)} %collective-permute-done.16.refs_1_, ...), custom_call_target="tpu_custom_call" | custom-call | tf_op jit(solution)/shard_map/pallas_call | solution.py:52
  89.7 1.7 %collective-permute-start.24 = (f32[128,128]{1,0:T(8,128)S(1)}, f32[128,128]{1,0:T(8,128)S(1)}, u32[]{:S(2)}, u32[]{:S(2)}) collective-permute-start(f32[128,128]{1,0:T(8,128)S(1)} %add.40.refs_0_), channel_id=1, source_target_pairs={{6,0},{7,1},{4,2},{5,3},{2,4},{3,5},{0,6},{1,7},{14,8},{15,9},{12,... | collective-permute-start | bytes 196616 | tf_op jit(solution)/shard_map/ppermute | solution.py:420
  93.2 2.0 %collective-permute-done.24.refs_3_ = f32[128,128]{1,0:T(8,128)S(1)} collective-permute-done((f32[128,128]{1,0:T(8,128)S(1)}, f32[128,128]{1,0:T(8,128)S(1)}, u32[]{:S(2)}, u32[]{:S(2)}) %collective-permute-start.24) | collective-permute-done | bytes 65568 | tf_op jit(solution)/shard_map/ppermute | solution.py:420
  96.4 3.0 %shard_map.60 = (f32[256,256]{1,0:T(8,128)S(1)}, f32[256,256]{1,0:T(8,128)S(1)}) custom-call(s32[16]{0:T(128)S(1)} %constant_dynamic-update-slice_fusion.f, f32[128,128]{1,0:T(8,128)S(1)} %add.40.refs_0_, f32[128,128]{1,0:T(8,128)S(1)} %collective-permute-done.22.refs_1_, f32[128,128]{1,0:T(8,128)S(1)} %collective-permute-done.23.refs_2_, ...), custom_call_target="tpu_custom_call" | custom-call | tf_op jit(solution)/shard_map/pallas_call | solution.py:52
  101.1 1.8 %shard_map.61 = (f32[1024,128]{1,0:T(8,128)S(1)}, f32[1024,128]{1,0:T(8,128)S(1)}, f32[1024,128]{1,0:T(8,128)S(1)}, f32[1024,128]{1,0:T(8,128)S(1)}, f32[256,128...) custom-call(s32[16]{0:T(128)S(1)} %constant_dynamic-update-slice_fus, ...), custom_call_target="tpu_custom_call" | custom-call | tf_op jit(solution)/shard_map/pallas_call | solution.py:52
  104.4 3.6 %collective-permute-start.26 = (f32[1024,128]{1,0:T(8,128)S(1)}, f32[1024,128]{1,0:T(8,128)S(1)}, u32[]{:S(2)}, u32[]{:S(2)}) collective-permute-start(f32[1024,128]{1,0:T(8,128)S(1)} %get-tuple-element.134), channel_id=1, source_target_pairs={{8,0},{9,1},{10,2},{11,3},{12,4},{13,5},{14,6},{15,7},{0,8},{1,9},... | collective-permute-start | bytes 1572872 | tf_op jit(solution)/shard_map/ppermute | solution.py:420
  111.0 2.9 %collective-permute-start.29 = (f32[128,128]{1,0:T(8,128)S(1)}, f32[128,128]{1,0:T(8,128)S(1)}, u32[]{:S(2)}, u32[]{:S(2)}) collective-permute-start(f32[128,128]{1,0:T(8,128)S(1)} %get-tuple-element.138), channel_id=1, source_target_pairs={{1,0},{0,1},{3,2},{2,3},{5,4},{4,5},{7,6},{6,7},{9,8},{8,9},{11,10... | collective-permute-start | bytes 196616 | tf_op jit(solution)/shard_map/ppermute | solution.py:420
  114.0 8.1 %collective-permute-start.31 = (f32[256,128]{1,0:T(8,128)S(1)}, f32[256,128]{1,0:T(8,128)S(1)}, u32[]{:S(2)}, u32[]{:S(2)}) collective-permute-start(f32[256,128]{1,0:T(8,128)S(1)} %get-tuple-element.148), channel_id=1, source_target_pairs={{8,0},{9,1},{10,2},{11,3},{12,4},{13,5},{14,6},{15,7},{0,8},{1,9},... | collective-permute-start | bytes 393224 | tf_op jit(solution)/shard_map/ppermute | solution.py:420
  124.8 1.7 %shard_map.64 = (f32[128,128]{1,0:T(8,128)S(1)}, f32[128,128]{1,0:T(8,128)S(1)}, f32[1024,128]{1,0:T(8,128)S(1)}, f32[1024,128]{1,0:T(8,128)S(1)}) custom-call(s32[16]{0:T(128)S(1)} %constant_dynamic-update-slice_fusion.f, f32[1024,128]{1,0:T(8,128)S(1)} %collective-permute-done.26.refs_0_, f32[1024,128]{1,0:T(8,128)S(1)} %collective-permute-done.27.refs_1_, ...), custom_call_target="tpu_custom_call" | custom-call | tf_op jit(solution)/shard_map/pallas_call | solution.py:52
  126.5 1.6 %collective-permute-start.33 = (f32[128,128]{1,0:T(8,128)S(1)}, f32[128,128]{1,0:T(8,128)S(1)}, u32[]{:S(2)}, u32[]{:S(2)}) collective-permute-start(f32[128,128]{1,0:T(8,128)S(1)} %get-tuple-element.150), channel_id=1, source_target_pairs={{1,0},{0,1},{3,2},{2,3},{5,4},{4,5},{7,6},{6,7},{9,8},{8,9},{11,10... | collective-permute-start | bytes 196616 | tf_op jit(solution)/shard_map/ppermute | solution.py:420
  132.3 2.8 %collective-permute-done.36.refs_3_ = f32[128,128]{1,0:T(8,128)S(1)} collective-permute-done((f32[128,128]{1,0:T(8,128)S(1)}, f32[128,128]{1,0:T(8,128)S(1)}, u32[]{:S(2)}, u32[]{:S(2)}) %collective-permute-start.36) | collective-permute-done | bytes 65568 | tf_op jit(solution)/shard_map/ppermute | solution.py:420
  137.9 3.2 %collective-permute-done.34.refs_1_ = f32[128,128]{1,0:T(8,128)S(1)} collective-permute-done((f32[128,128]{1,0:T(8,128)S(1)}, f32[128,128]{1,0:T(8,128)S(1)}, u32[]{:S(2)}, u32[]{:S(2)}) %collective-permute-start.34) | collective-permute-done | bytes 65568 | tf_op jit(solution)/shard_map/ppermute | solution.py:420
  141.1 3.4 %shard_map.66 = (f32[264,256]{1,0:T(8,128)S(1)}, f32[256,256]{1,0:T(8,128)}) custom-call(s32[16]{0:T(128)S(1)} %constant_dynamic-update-slice_fusion.f, f32[128,128]{1,0:T(8,128)S(1)} %add.41.refs_0_, f32[128,128]{1,0:T(8,128)S(1)} %collective-permute-done.34.refs_1_, f32[128,128]{1,0:T(8,128)S(1)} %collective-permute-done.35.refs_2_, ...), custom_call_target="tpu_custom_call" | custom-call | tf_op jit(solution)/shard_map/pallas_call | solution.py:52
  146.2 3.2 %shard_map.67 = (f32[2048,256]{1,0:T(8,128)}, f32[512,256]{1,0:T(8,128)}, f32[1,256]{1,0:T(1,128)}) custom-call(s32[16]{0:T(128)S(1)} %constant_dynamic-update-slice_fusion.f, f32[264,256]{1,0:T(8,128)S(1)} %get-tuple-element.158.refs_0_, f32[264,256]{1,0:T(8,128)S(1)} %collective-permute-done.38.refs_1_, f32[1024,128]{1,0:T(8,128)S(1)} %get-tuple-element.159.refs_2_, ...), custom_call_target="tpu_custom_call" | custom-call | tf_op jit(solution)/shard_map/pallas_call | solution.py:52
  (78 shorter events, 42.3 us)
Async XLA Ops:
  3.1 31.9 %collective-permute-start.6 = (f32[1024,256]{1,0:T(8,128)}, f32[1024,256]{1,0:T(8,128)S(1)}, u32[]{:S(2)}, u32[]{:S(2)}) collective-permute-start(f32[1024,256]{1,0:T(8,128)} %constant_dynamic-slice_fusion), channel_id=1, source_target_pairs={{4,0},{5,1},{6,2},{7,3},{0,4},{1,5},{2,6},{3,7},{12,8},{13,9},{14,... | collective-permute-start | bytes 3145736 | tf_op jit(solution)/shard_map/ppermute | solution.py:420
  10.4 7.0 %collective-permute-start.1 = (f32[384,128]{1,0:T(8,128)S(1)}, f32[384,128]{1,0:T(8,128)S(1)}, u32[]{:S(2)}, u32[]{:S(2)}) collective-permute-start(f32[384,128]{1,0:T(8,128)S(1)} %add.37.own_ref), channel_id=1, source_target_pairs={{2,0},{3,1},{0,2},{1,3},{6,4},{7,5},{4,6},{5,7},{10,8},{11,9},{8,1... | collective-permute-start | bytes 589832 | tf_op jit(solution)/shard_map/ppermute | solution.py:420
  20.8 14.2 %collective-permute-start.5 = (f32[256,256]{1,0:T(8,128)S(1)}, f32[256,256]{1,0:T(8,128)S(1)}, u32[]{:S(2)}, u32[]{:S(2)}) collective-permute-start(f32[256,256]{1,0:T(8,128)S(1)} %get-tuple-element.86.rotation_ref.own_ref), channel_id=1, source_target_pairs={{4,0},{5,1},{6,2},{7,3},{0,4},{1,5},{2,6},{3,7},{12,8},{13,9},{14,... | collective-permute-start | bytes 786440 | tf_op jit(solution)/shard_map/ppermute | solution.py:420
  22.3 29.7 %collective-permute-start.2 = (f32[1024,128]{1,0:T(8,128)S(1)}, f32[1024,128]{1,0:T(8,128)S(1)}, u32[]{:S(2)}, u32[]{:S(2)}) collective-permute-start(f32[1024,128]{1,0:T(8,128)S(1)} %get-tuple-element.88.refs_1_), channel_id=1, source_target_pairs={{8,0},{9,1},{10,2},{11,3},{16,8},{17,9},{18,10},{19,11},{4,12},{5,... | collective-permute-start | bytes 1572872 | tf_op jit(solution)/shard_map/ppermute | solution.py:420
  36.1 15.9 %collective-permute-start.7 = (f32[1024,128]{1,0:T(8,128)S(1)}, f32[1024,128]{1,0:T(8,128)S(1)}, u32[]{:S(2)}, u32[]{:S(2)}) collective-permute-start(f32[1024,128]{1,0:T(8,128)S(1)} %get-tuple-element.94.refs_4_), channel_id=1, source_target_pairs={{12,4},{13,5},{14,6},{15,7},{0,8},{1,9},{2,10},{3,11},{20,12},{21,... | collective-permute-start | bytes 1572872 | tf_op jit(solution)/shard_map/ppermute | solution.py:420
  41.6 5.2 %collective-permute-start.3 = (f32[128,128]{1,0:T(8,128)S(1)}, f32[128,128]{1,0:T(8,128)S(1)}, u32[]{:S(2)}, u32[]{:S(2)}) collective-permute-start(f32[128,128]{1,0:T(8,128)S(1)} %get-tuple-element.90), channel_id=1, source_target_pairs={{0,0},{8,1},{2,2},{10,3},{1,4},{9,5},{3,6},{11,7},{4,8},{16,9},{6,... | collective-permute-start | bytes 196616 | tf_op jit(solution)/shard_map/ppermute | solution.py:420
  43.2 10.7 %collective-permute-start.8 = (f32[256,128]{1,0:T(8,128)S(1)}, f32[256,128]{1,0:T(8,128)S(1)}, u32[]{:S(2)}, u32[]{:S(2)}) collective-permute-start(f32[256,128]{1,0:T(8,128)S(1)} %get-tuple-element.97), channel_id=1, source_target_pairs={{8,0},{9,1},{10,2},{11,3},{12,4},{13,5},{14,6},{15,7},{0,8},{1,9},... | collective-permute-start | bytes 393224 | tf_op jit(solution)/shard_map/ppermute | solution.py:420
  46.1 7.8 %collective-permute-start.9 = (f32[256,128]{1,0:T(8,128)S(1)}, f32[256,128]{1,0:T(8,128)S(1)}, u32[]{:S(2)}, u32[]{:S(2)}) collective-permute-start(f32[256,128]{1,0:T(8,128)S(1)} %get-tuple-element.98), channel_id=1, source_target_pairs={{0,0},{1,1},{2,2},{3,3},{4,4},{5,5},{6,6},{7,7},{16,8},{17,9},{18,... | collective-permute-start | bytes 393224 | tf_op jit(solution)/shard_map/ppermute | solution.py:420
  46.8 5.3 %collective-permute-start.4 = (f32[128,128]{1,0:T(8,128)S(1)}, f32[128,128]{1,0:T(8,128)S(1)}, u32[]{:S(2)}, u32[]{:S(2)}) collective-permute-start(f32[128,128]{1,0:T(8,128)S(1)} %get-tuple-element.91), channel_id=1, source_target_pairs={{4,0},{0,1},{6,2},{2,3},{5,4},{1,5},{7,6},{3,7},{12,8},{8,9},{14,1... | collective-permute-start | bytes 196616 | tf_op jit(solution)/shard_map/ppermute | solution.py:420
  55.3 5.3 %collective-permute-start.13 = (f32[128,128]{1,0:T(8,128)S(1)}, f32[128,128]{1,0:T(8,128)S(1)}, u32[]{:S(2)}, u32[]{:S(2)}) collective-permute-start(f32[128,128]{1,0:T(8,128)S(1)} %add.39.refs_0_), channel_id=1, source_target_pairs={{6,0},{7,1},{4,2},{5,3},{2,4},{3,5},{0,6},{1,7},{14,8},{15,9},{12,... | collective-permute-start | bytes 196616 | tf_op jit(solution)/shard_map/ppermute | solution.py:420
  58.2 4.3 %collective-permute-start.12 = (f32[128,128]{1,0:T(8,128)S(1)}, f32[128,128]{1,0:T(8,128)S(1)}, u32[]{:S(2)}, u32[]{:S(2)}) collective-permute-start(f32[128,128]{1,0:T(8,128)S(1)} %add.39.refs_0_), channel_id=1, source_target_pairs={{4,0},{5,1},{6,2},{7,3},{0,4},{1,5},{2,6},{3,7},{12,8},{13,9},{14,... | collective-permute-start | bytes 196616 | tf_op jit(solution)/shard_map/ppermute | solution.py:420
  58.3 4.3 %collective-permute-start.11 = (f32[128,128]{1,0:T(8,128)S(1)}, f32[128,128]{1,0:T(8,128)S(1)}, u32[]{:S(2)}, u32[]{:S(2)}) collective-permute-start(f32[128,128]{1,0:T(8,128)S(1)} %add.39.refs_0_), channel_id=1, source_target_pairs={{2,0},{3,1},{0,2},{1,3},{6,4},{7,5},{4,6},{5,7},{10,8},{11,9},{8,1... | collective-permute-start | bytes 196616 | tf_op jit(solution)/shard_map/ppermute | solution.py:420
  69.4 17.3 %collective-permute-start.15 = (f32[1024,128]{1,0:T(8,128)S(1)}, f32[1024,128]{1,0:T(8,128)S(1)}, u32[]{:S(2)}, u32[]{:S(2)}) collective-permute-start(f32[1024,128]{1,0:T(8,128)S(1)} %get-tuple-element.111), channel_id=1, source_target_pairs={{8,0},{9,1},{10,2},{11,3},{12,4},{13,5},{14,6},{15,7},{0,8},{1,9},... | collective-permute-start | bytes 1572872 | tf_op jit(solution)/shard_map/ppermute | solution.py:420
  71.8 14.8 %collective-permute-start.16 = (f32[1024,128]{1,0:T(8,128)S(1)}, f32[1024,128]{1,0:T(8,128)S(1)}, u32[]{:S(2)}, u32[]{:S(2)}) collective-permute-start(f32[1024,128]{1,0:T(8,128)S(1)} %get-tuple-element.112), channel_id=1, source_target_pairs={{0,0},{1,1},{2,2},{3,3},{4,4},{5,5},{6,6},{7,7},{16,8},{17,9},{18,... | collective-permute-start | bytes 1572872 | tf_op jit(solution)/shard_map/ppermute | solution.py:420
  74.3 6.6 %collective-permute-start.17 = (f32[128,128]{1,0:T(8,128)S(1)}, f32[128,128]{1,0:T(8,128)S(1)}, u32[]{:S(2)}, u32[]{:S(2)}) collective-permute-start(f32[128,128]{1,0:T(8,128)S(1)} %get-tuple-element.114), channel_id=1, source_target_pairs={{0,0},{8,1},{2,2},{10,3},{4,4},{12,5},{6,6},{14,7},{1,8},{16,9},{3... | collective-permute-start | bytes 196616 | tf_op jit(solution)/shard_map/ppermute | solution.py:420
  75.0 13.3 %collective-permute-start.19 = (f32[256,128]{1,0:T(8,128)S(1)}, f32[256,128]{1,0:T(8,128)S(1)}, u32[]{:S(2)}, u32[]{:S(2)}) collective-permute-start(f32[256,128]{1,0:T(8,128)S(1)} %get-tuple-element.122), channel_id=1, source_target_pairs={{8,0},{9,1},{10,2},{11,3},{12,4},{13,5},{14,6},{15,7},{0,8},{1,9},... | collective-permute-start | bytes 393224 | tf_op jit(solution)/shard_map/ppermute | solution.py:420
  80.3 8.0 %collective-permute-start.20 = (f32[256,128]{1,0:T(8,128)S(1)}, f32[256,128]{1,0:T(8,128)S(1)}, u32[]{:S(2)}, u32[]{:S(2)}) collective-permute-start(f32[256,128]{1,0:T(8,128)S(1)} %get-tuple-element.123), channel_id=1, source_target_pairs={{0,0},{1,1},{2,2},{3,3},{4,4},{5,5},{6,6},{7,7},{16,8},{17,9},{18,... | collective-permute-start | bytes 393224 | tf_op jit(solution)/shard_map/ppermute | solution.py:420
  81.0 5.7 %collective-permute-start.18 = (f32[128,128]{1,0:T(8,128)S(1)}, f32[128,128]{1,0:T(8,128)S(1)}, u32[]{:S(2)}, u32[]{:S(2)}) collective-permute-start(f32[128,128]{1,0:T(8,128)S(1)} %get-tuple-element.115), channel_id=1, source_target_pairs={{1,0},{0,1},{3,2},{2,3},{5,4},{4,5},{7,6},{6,7},{9,8},{8,9},{11,10... | collective-permute-start | bytes 196616 | tf_op jit(solution)/shard_map/ppermute | solution.py:420
  89.7 5.5 %collective-permute-start.24 = (f32[128,128]{1,0:T(8,128)S(1)}, f32[128,128]{1,0:T(8,128)S(1)}, u32[]{:S(2)}, u32[]{:S(2)}) collective-permute-start(f32[128,128]{1,0:T(8,128)S(1)} %add.40.refs_0_), channel_id=1, source_target_pairs={{6,0},{7,1},{4,2},{5,3},{2,4},{3,5},{0,6},{1,7},{14,8},{15,9},{12,... | collective-permute-start | bytes 196616 | tf_op jit(solution)/shard_map/ppermute | solution.py:420
  91.4 4.3 %collective-permute-start.23 = (f32[128,128]{1,0:T(8,128)S(1)}, f32[128,128]{1,0:T(8,128)S(1)}, u32[]{:S(2)}, u32[]{:S(2)}) collective-permute-start(f32[128,128]{1,0:T(8,128)S(1)} %add.40.refs_0_), channel_id=1, source_target_pairs={{4,0},{5,1},{6,2},{7,3},{0,4},{1,5},{2,6},{3,7},{12,8},{13,9},{14,... | collective-permute-start | bytes 196616 | tf_op jit(solution)/shard_map/ppermute | solution.py:420
  92.0 4.4 %collective-permute-start.22 = (f32[128,128]{1,0:T(8,128)S(1)}, f32[128,128]{1,0:T(8,128)S(1)}, u32[]{:S(2)}, u32[]{:S(2)}) collective-permute-start(f32[128,128]{1,0:T(8,128)S(1)} %add.40.refs_0_), channel_id=1, source_target_pairs={{2,0},{3,1},{0,2},{1,3},{6,4},{7,5},{4,6},{5,7},{10,8},{11,9},{8,1... | collective-permute-start | bytes 196616 | tf_op jit(solution)/shard_map/ppermute | solution.py:420
  102.8 20.4 %collective-permute-start.30 = (f32[1280,128]{1,0:T(8,128)S(1)}, f32[1280,128]{1,0:T(8,128)S(1)}, u32[]{:S(2)}, u32[]{:S(2)}) collective-permute-start(f32[1280,128]{1,0:T(8,128)S(1)} %get-tuple-element.141), channel_id=1, source_target_pairs={{4,0},{5,1},{6,2},{7,3},{0,4},{1,5},{2,6},{3,7},{12,8},{13,9},{14,... | collective-permute-start | bytes 1966088 | tf_op jit(solution)/shard_map/ppermute | solution.py:420
  104.4 18.3 %collective-permute-start.26 = (f32[1024,128]{1,0:T(8,128)S(1)}, f32[1024,128]{1,0:T(8,128)S(1)}, u32[]{:S(2)}, u32[]{:S(2)}) collective-permute-start(f32[1024,128]{1,0:T(8,128)S(1)} %get-tuple-element.134), channel_id=1, source_target_pairs={{8,0},{9,1},{10,2},{11,3},{12,4},{13,5},{14,6},{15,7},{0,8},{1,9},... | collective-permute-start | bytes 1572872 | tf_op jit(solution)/shard_map/ppermute | solution.py:420
  108.0 14.7 %collective-permute-start.27 = (f32[1024,128]{1,0:T(8,128)S(1)}, f32[1024,128]{1,0:T(8,128)S(1)}, u32[]{:S(2)}, u32[]{:S(2)}) collective-permute-start(f32[1024,128]{1,0:T(8,128)S(1)} %get-tuple-element.135), channel_id=1, source_target_pairs={{0,0},{1,1},{2,2},{3,3},{4,4},{5,5},{6,6},{7,7},{16,8},{17,9},{18,... | collective-permute-start | bytes 1572872 | tf_op jit(solution)/shard_map/ppermute | solution.py:420
  111.0 11.0 %collective-permute-start.29 = (f32[128,128]{1,0:T(8,128)S(1)}, f32[128,128]{1,0:T(8,128)S(1)}, u32[]{:S(2)}, u32[]{:S(2)}) collective-permute-start(f32[128,128]{1,0:T(8,128)S(1)} %get-tuple-element.138), channel_id=1, source_target_pairs={{1,0},{0,1},{3,2},{2,3},{5,4},{4,5},{7,6},{6,7},{9,8},{8,9},{11,10... | collective-permute-start | bytes 196616 | tf_op jit(solution)/shard_map/ppermute | solution.py:420
  114.0 12.6 %collective-permute-start.31 = (f32[256,128]{1,0:T(8,128)S(1)}, f32[256,128]{1,0:T(8,128)S(1)}, u32[]{:S(2)}, u32[]{:S(2)}) collective-permute-start(f32[256,128]{1,0:T(8,128)S(1)} %get-tuple-element.148), channel_id=1, source_target_pairs={{8,0},{9,1},{10,2},{11,3},{12,4},{13,5},{14,6},{15,7},{0,8},{1,9},... | collective-permute-start | bytes 393224 | tf_op jit(solution)/shard_map/ppermute | solution.py:420
  122.0 4.5 %collective-permute-start.32 = (f32[256,128]{1,0:T(8,128)S(1)}, f32[256,128]{1,0:T(8,128)S(1)}, u32[]{:S(2)}, u32[]{:S(2)}) collective-permute-start(f32[256,128]{1,0:T(8,128)S(1)} %get-tuple-element.149), channel_id=1, source_target_pairs={{0,0},{1,1},{2,2},{3,3},{4,4},{5,5},{6,6},{7,7},{16,8},{17,9},{18,... | collective-permute-start | bytes 393224 | tf_op jit(solution)/shard_map/ppermute | solution.py:420
  123.3 12.2 %collective-permute-start.37 = (f32[512,128]{1,0:T(8,128)S(1)}, f32[512,128]{1,0:T(8,128)S(1)}, u32[]{:S(2)}, u32[]{:S(2)}) collective-permute-start(f32[512,128]{1,0:T(8,128)S(1)} %shard_map.63), channel_id=1, source_target_pairs={{4,0},{5,1},{6,2},{7,3},{0,4},{1,5},{2,6},{3,7},{12,8},{13,9},{14,... | collective-permute-start | bytes 786440 | tf_op jit(solution)/shard_map/ppermute | solution.py:420
  129.1 6.0 %collective-permute-start.36 = (f32[128,128]{1,0:T(8,128)S(1)}, f32[128,128]{1,0:T(8,128)S(1)}, u32[]{:S(2)}, u32[]{:S(2)}) collective-permute-start(f32[128,128]{1,0:T(8,128)S(1)} %add.41.refs_0_), channel_id=1, source_target_pairs={{6,0},{7,1},{4,2},{5,3},{2,4},{3,5},{0,6},{1,7},{14,8},{15,9},{12,... | collective-permute-start | bytes 196616 | tf_op jit(solution)/shard_map/ppermute | solution.py:420
  130.5 5.0 %collective-permute-start.35 = (f32[128,128]{1,0:T(8,128)S(1)}, f32[128,128]{1,0:T(8,128)S(1)}, u32[]{:S(2)}, u32[]{:S(2)}) collective-permute-start(f32[128,128]{1,0:T(8,128)S(1)} %add.41.refs_0_), channel_id=1, source_target_pairs={{4,0},{5,1},{6,2},{7,3},{0,4},{1,5},{2,6},{3,7},{12,8},{13,9},{14,... | collective-permute-start | bytes 196616 | tf_op jit(solution)/shard_map/ppermute | solution.py:420
  135.5 10.7 %collective-permute-start.39 = (f32[768,128]{1,0:T(8,128)S(1)}, f32[768,128]{1,0:T(8,128)S(1)}, u32[]{:S(2)}, u32[]{:S(2)}) collective-permute-start(f32[768,128]{1,0:T(8,128)S(1)} %shard_map.65), channel_id=1, source_target_pairs={{4,0},{5,1},{6,2},{7,3},{0,4},{1,5},{2,6},{3,7},{12,8},{13,9},{14,... | collective-permute-start | bytes 1179656 | tf_op jit(solution)/shard_map/ppermute | solution.py:420
  136.8 4.3 %collective-permute-start.34 = (f32[128,128]{1,0:T(8,128)S(1)}, f32[128,128]{1,0:T(8,128)S(1)}, u32[]{:S(2)}, u32[]{:S(2)}) collective-permute-start(f32[128,128]{1,0:T(8,128)S(1)} %add.41.refs_0_), channel_id=1, source_target_pairs={{2,0},{3,1},{0,2},{1,3},{6,4},{7,5},{4,6},{5,7},{10,8},{11,9},{8,1... | collective-permute-start | bytes 196616 | tf_op jit(solution)/shard_map/ppermute | solution.py:420
  (10 other events, 26.0 us)

commit v6 on v5

--- a/solution.py
+++ b/solution.py
@@ -501,10 +501,12 @@
             other_rotation = exchange(rotation, 1, 0)
             stay, leave = turn_rows(facts, other_rotation, got, half, False)
             other_rows = [stay, leave, shift(leave, 2)]
-            vectors = first_vectors(
-                facts, rotation, other_rotation, vector_rows, half
-            )
-            own_rows[2], *diagonals = together(own_rows[2], *diagonals)
+            vectors = list(
+                first_vectors(facts, rotation, other_rotation, vector_rows, half)
+            )
+            vectors[0], vectors[1], diagonals[1] = together(
+                vectors[0], vectors[1], diagonals[1]
+            )
             *grams, up_0, nat_l, nat_u, low_1 = first_cross_gram(
                 facts, own_rows, other_rows, half
             )
@@ -516,18 +518,24 @@
             got = [swap(leave_a, 0), swap(leave_b, 1)]
             leave, stay = turned_gram(facts, gram, rotation, CORE)
             diagonals = [pass_diagonal(leave), exchange(stay, 0, 1)]
-            *got, diagonals[0], diagonals[1] = together(*got, *diagonals)
+            vectors[0], vectors[1], diagonals[1] = together(
+                vectors[0], vectors[1], diagonals[1]
+            )
             if last_move:
                 native = exchange(vectors.pop(), 1, 0)
                 top = part // 2
                 top_give = give(facts, [(got, 0, top)], half)
-                *got, native, top_give = together(*got, native, top_give)
+                *got, top_give = together(*got, top_give)
                 got_top = exchange(top_give, 1, 0)
             *grams, up_0, low_1 = cross_gram(facts, got, [nat_l, nat_u], half)
+            if last_move:
+                grams[1], native = together(grams[1], native)
         blocks = [up_0, nat_l, nat_u, low_1]
         vector_a, vector_b, *kept = vectors
         vectors = [swap(vector_a, 0), swap(vector_b, 1)] + kept
-        grams[1], vectors[0], vectors[1] = together(grams[1], *vectors[:2])
+        grams[1], vectors[0], vectors[1], diagonals[0] = together(
+            grams[1], *vectors[:2], diagonals[0]
+        )
         own = sum_rows(grams[0] + exchange(grams[1], 0, 1))
         if last_move:
             rest = give(

time: 150 us -> 152 us (1.013)
  waiting for transfers between devices: 44.4 us -> 59.7 us
  starting transfers between devices: 64.1 us -> 50.6 us
    ppermute x40, waiting for transfers between devices: 44.4 us -> 59.7 us  [permute(): return lax.ppermute(block, ('pair', 'row'), moves)]
    ppermute x40, starting transfers between devices: 64.1 us -> 50.6 us  [permute(): return lax.ppermute(block, ('pair', 'row'), moves)]
  transfers between devices with their start and end apart: 40 -> 40, of which waited for: 20 -> 26; matrix products, arithmetic and copies ran while one was open for 0% -> 0% of each run, Pallas kernels for 16% -> 16%
where the time goes in v6:
time: 152 us; the launch traced here: 151 us
  waiting for transfers between devices  59.7 us (39%)
  starting transfers between devices  50.6 us (33%)
  Pallas kernels  37.2 us (24%)
  local copies, waits for them, and re-layouts  2.57 us (2%)
    ppermute x40, waiting for transfers between devices, permute(): return lax.ppermute(block, ('pair', 'row'), moves)  59.7 us
    ppermute x40, starting transfers between devices, permute(): return lax.ppermute(block, ('pair', 'row'), moves)  50.6 us
    pallas_call x19, Pallas kernels, call(): pl.pallas_call(body, out_shape=outs, in_specs=[pl.BlockSpec(memory_space=...  37.2 us
  transfers between devices with their start and end apart: 40, of which 26 were waited for; matrix products, arithmetic and copies ran while one was open for 0% of the time, Pallas kernels for 16%

profile of v6, /device:TPU:0, one launch (start us, length us, event | category | flops | bytes accessed | tf_op | source)
XLA Modules:
  0.0 151.2 jit_solution(10703274038803286169)
XLA Ops:
  0.7 2.4 %constant_dynamic-slice_fusion = f32[1024,256]{1,0:T(8,128)} fusion(f32[2048,256]{1,0:T(8,128)} %x_ref.3, s32[]{:T(128)S(6)} %select_n.55), kind=kLoop, calls=%fused_computation.7 | loop fusion | bytes 2097156 | tf_op jit(solution)/shard_map/dynamic_slice | solution.py:489
  3.1 2.9 %collective-permute-start.4 = (f32[1024,256]{1,0:T(8,128)}, f32[1024,256]{1,0:T(8,128)S(1)}, u32[]{:S(2)}, u32[]{:S(2)}) collective-permute-start(f32[1024,256]{1,0:T(8,128)} %constant_dynamic-slice_fusion), channel_id=1, source_target_pairs={{4,0},{5,1},{6,2},{7,3},{0,4},{1,5},{2,6},{3,7},{12,8},{13,9},{14,... | collective-permute-start | bytes 3145736 | tf_op jit(solution)/shard_map/ppermute | solution.py:420
  6.2 2.6 %shard_map.49 = f32[384,128]{1,0:T(8,128)S(1)} custom-call(s32[16]{0:T(128)S(1)} %constant_dynamic-update-slice_fusion.f, f32[2048,256]{1,0:T(8,128)S(1)} %copy-done), custom_call_target="tpu_custom_call" | custom-call | tf_op jit(solution)/shard_map/pallas_call | solution.py:52
  12.0 5.4 %collective-permute-done.1.other_ref = f32[384,128]{1,0:T(8,128)S(1)} collective-permute-done((f32[384,128]{1,0:T(8,128)S(1)}, f32[384,128]{1,0:T(8,128)S(1)}, u32[]{:S(2)}, u32[]{:S(2)}) %collective-permute-start.1) | collective-permute-done | bytes 196640 | tf_op jit(solution)/shard_map/ppermute | solution.py:420
  17.4 3.4 %shard_map.50 = (f32[256,256]{1,0:T(8,128)S(1)}, f32[256,256]{1,0:T(8,128)S(1)}) custom-call(s32[16]{0:T(128)S(1)} %constant_dynamic-update-slice_fusion.f, f32[384,128]{1,0:T(8,128)S(1)} %add.37.own_ref, f32[384,128]{1,0:T(8,128)S(1)} %collective-permute-done.1.other_ref), custom_call_target="tpu_custom_call" | custom-call | tf_op jit(solution)/shard_map/pallas_call | solution.py:52
  23.6 11.4 %collective-permute-done.3.rotation_ref.other_ref = f32[256,256]{1,0:T(8,128)S(1)} collective-permute-done((f32[256,256]{1,0:T(8,128)S(1)}, f32[256,256]{1,0:T(8,128)S(1)}, u32[]{:S(2)}, u32[]{:S(2)}) %collective-permute-start.3) | collective-permute-done | bytes 262176 | tf_op jit(solution)/shard_map/ppermute | solution.py:420
  36.1 3.8 %collective-permute-start.5 = (f32[1024,128]{1,0:T(8,128)S(1)}, f32[1024,128]{1,0:T(8,128)S(1)}, u32[]{:S(2)}, u32[]{:S(2)}) collective-permute-start(f32[1024,128]{1,0:T(8,128)S(1)} %get-tuple-element.92.refs_4_), channel_id=1, source_target_pairs={{12,4},{13,5},{14,6},{15,7},{0,8},{1,9},{2,10},{3,11},{20,12},{21,... | collective-permute-start | bytes 1572872 | tf_op jit(solution)/shard_map/ppermute | solution.py:420
  42.6 3.3 %collective-permute-done.6.refs_5_ = f32[128,128]{1,0:T(8,128)S(1)} collective-permute-done((f32[128,128]{1,0:T(8,128)S(1)}, f32[128,128]{1,0:T(8,128)S(1)}, u32[]{:S(2)}, u32[]{:S(2)}) %collective-permute-start.6) | collective-permute-done | bytes 65568 | tf_op jit(solution)/shard_map/ppermute | solution.py:420
  48.7 2.9 %collective-permute-done.5.refs_5_ = f32[1024,128]{1,0:T(8,128)S(1)} collective-permute-done((f32[1024,128]{1,0:T(8,128)S(1)}, f32[1024,128]{1,0:T(8,128)S(1)}, u32[]{:S(2)}, u32[]{:S(2)}) %collective-permute-start.5) | collective-permute-done | bytes 524320 | tf_op jit(solution)/shard_map/ppermute | solution.py:420
  51.6 1.8 %shard_map.53 = (f32[128,128]{1,0:T(8,128)S(1)}, f32[128,128]{1,0:T(8,128)S(1)}, f32[1024,128]{1,0:T(8,128)S(1)}, f32[1024,128]{1,0:T(8,128)S(1)}, f32[1024,128]{1,0:T(8,128)S(1)}, /*index=5*/f32[1024,128]{1,0:T(8,128)S(1)}) custom-call(s32[16]{0:T(128)S(1)} %constant_dynamic-update-slice_fusion.f, f32[1024,128]{1,0:T(8,128)S(1)} %get-tuple-element.89.refs_0_, ...), custom_call_target="tpu_custom_call" | custom-call | tf_op jit(solution)/shard_map/pallas_call | solution.py:52
  55.8 2.7 %collective-permute-start.13 = (f32[128,128]{1,0:T(8,128)S(1)}, f32[128,128]{1,0:T(8,128)S(1)}, u32[]{:S(2)}, u32[]{:S(2)}) collective-permute-start(f32[128,128]{1,0:T(8,128)S(1)} %add.39.refs_0_), channel_id=1, source_target_pairs={{6,0},{7,1},{4,2},{5,3},{2,4},{3,5},{0,6},{1,7},{14,8},{15,9},{12,... | collective-permute-start | bytes 196616 | tf_op jit(solution)/shard_map/ppermute | solution.py:420
  59.3 2.0 %collective-permute-done.13.refs_3_ = f32[128,128]{1,0:T(8,128)S(1)} collective-permute-done((f32[128,128]{1,0:T(8,128)S(1)}, f32[128,128]{1,0:T(8,128)S(1)}, u32[]{:S(2)}, u32[]{:S(2)}) %collective-permute-start.13) | collective-permute-done | bytes 65568 | tf_op jit(solution)/shard_map/ppermute | solution.py:420
  63.1 3.4 %shard_map.56 = (f32[256,256]{1,0:T(8,128)S(1)}, f32[256,256]{1,0:T(8,128)S(1)}) custom-call(s32[16]{0:T(128)S(1)} %constant_dynamic-update-slice_fusion.f, f32[128,128]{1,0:T(8,128)S(1)} %add.39.refs_0_, f32[128,128]{1,0:T(8,128)S(1)} %collective-permute-done.11.refs_1_, f32[128,128]{1,0:T(8,128)S(1)} %collective-permute-done.12.refs_2_, ...), custom_call_target="tpu_custom_call" | custom-call | tf_op jit(solution)/shard_map/pallas_call | solution.py:52
  68.1 1.8 %shard_map.57 = (f32[1024,128]{1,0:T(8,128)S(1)}, f32[1024,128]{1,0:T(8,128)S(1)}, f32[1024,128]{1,0:T(8,128)S(1)}, f32[1024,128]{1,0:T(8,128)S(1)}, f32[256,128...) custom-call(s32[16]{0:T(128)S(1)} %constant_dynamic-update-slice_fusion.f, ...), custom_call_target="tpu_custom_call" | custom-call | tf_op jit(solution)/shard_map/pallas_call | solution.py:52
  69.9 3.5 %collective-permute-start.15 = (f32[1024,128]{1,0:T(8,128)S(1)}, f32[1024,128]{1,0:T(8,128)S(1)}, u32[]{:S(2)}, u32[]{:S(2)}) collective-permute-start(f32[1024,128]{1,0:T(8,128)S(1)} %get-tuple-element.114), channel_id=1, source_target_pairs={{8,0},{9,1},{10,2},{11,3},{12,4},{13,5},{14,6},{15,7},{0,8},{1,9},... | collective-permute-start | bytes 1572872 | tf_op jit(solution)/shard_map/ppermute | solution.py:420
  77.2 2.4 %collective-permute-start.18 = (f32[256,128]{1,0:T(8,128)S(1)}, f32[256,128]{1,0:T(8,128)S(1)}, u32[]{:S(2)}, u32[]{:S(2)}) collective-permute-start(f32[256,128]{1,0:T(8,128)S(1)} %get-tuple-element.124), channel_id=1, source_target_pairs={{8,0},{9,1},{10,2},{11,3},{12,4},{13,5},{14,6},{15,7},{0,8},{1,9},... | collective-permute-start | bytes 393224 | tf_op jit(solution)/shard_map/ppermute | solution.py:420
  81.0 5.1 %collective-permute-done.15.refs_0_ = f32[1024,128]{1,0:T(8,128)S(1)} collective-permute-done((f32[1024,128]{1,0:T(8,128)S(1)}, f32[1024,128]{1,0:T(8,128)S(1)}, u32[]{:S(2)}, u32[]{:S(2)}) %collective-permute-start.15) | collective-permute-done | bytes 524320 | tf_op jit(solution)/shard_map/ppermute | solution.py:420
  86.1 1.7 %shard_map.58 = (f32[128,128]{1,0:T(8,128)S(1)}, f32[128,128]{1,0:T(8,128)S(1)}, f32[1024,128]{1,0:T(8,128)S(1)}, f32[1024,128]{1,0:T(8,128)S(1)}) custom-call(s32[16]{0:T(128)S(1)} %constant_dynamic-update-slice_fusion.f, f32[1024,128]{1,0:T(8,128)S(1)} %collective-permute-done.15.refs_0_, f32[1024,128]{1,0:T(8,128)S(1)} %collective-permute-done.16.refs_1_, ...), custom_call_target="tpu_custom_call" | custom-call | tf_op jit(solution)/shard_map/pallas_call | solution.py:52
  90.1 2.1 %collective-permute-start.23 = (f32[128,128]{1,0:T(8,128)S(1)}, f32[128,128]{1,0:T(8,128)S(1)}, u32[]{:S(2)}, u32[]{:S(2)}) collective-permute-start(f32[128,128]{1,0:T(8,128)S(1)} %add.40.refs_0_), channel_id=1, source_target_pairs={{4,0},{5,1},{6,2},{7,3},{0,4},{1,5},{2,6},{3,7},{12,8},{13,9},{14,... | collective-permute-start | bytes 196616 | tf_op jit(solution)/shard_map/ppermute | solution.py:420
  93.4 2.3 %collective-permute-done.24.refs_3_ = f32[128,128]{1,0:T(8,128)S(1)} collective-permute-done((f32[128,128]{1,0:T(8,128)S(1)}, f32[128,128]{1,0:T(8,128)S(1)}, u32[]{:S(2)}, u32[]{:S(2)}) %collective-permute-start.24) | collective-permute-done | bytes 65568 | tf_op jit(solution)/shard_map/ppermute | solution.py:420
  96.6 3.0 %shard_map.60 = (f32[256,256]{1,0:T(8,128)S(1)}, f32[256,256]{1,0:T(8,128)S(1)}) custom-call(s32[16]{0:T(128)S(1)} %constant_dynamic-update-slice_fusion.f, f32[128,128]{1,0:T(8,128)S(1)} %add.40.refs_0_, f32[128,128]{1,0:T(8,128)S(1)} %collective-permute-done.22.refs_1_, f32[128,128]{1,0:T(8,128)S(1)} %collective-permute-done.23.refs_2_, ...), custom_call_target="tpu_custom_call" | custom-call | tf_op jit(solution)/shard_map/pallas_call | solution.py:52
  101.3 1.8 %shard_map.61 = (f32[1024,128]{1,0:T(8,128)S(1)}, f32[1024,128]{1,0:T(8,128)S(1)}, f32[1024,128]{1,0:T(8,128)S(1)}, f32[1024,128]{1,0:T(8,128)S(1)}, f32[256,128...) custom-call(s32[16]{0:T(128)S(1)} %constant_dynamic-update-slice_fus, ...), custom_call_target="tpu_custom_call" | custom-call | tf_op jit(solution)/shard_map/pallas_call | solution.py:52
  103.1 3.7 %collective-permute-start.26 = (f32[1024,128]{1,0:T(8,128)S(1)}, f32[1024,128]{1,0:T(8,128)S(1)}, u32[]{:S(2)}, u32[]{:S(2)}) collective-permute-start(f32[1024,128]{1,0:T(8,128)S(1)} %get-tuple-element.137), channel_id=1, source_target_pairs={{8,0},{9,1},{10,2},{11,3},{12,4},{13,5},{14,6},{15,7},{0,8},{1,9},... | collective-permute-start | bytes 1572872 | tf_op jit(solution)/shard_map/ppermute | solution.py:420
  110.5 2.7 %collective-permute-start.30 = (f32[256,128]{1,0:T(8,128)S(1)}, f32[256,128]{1,0:T(8,128)S(1)}, u32[]{:S(2)}, u32[]{:S(2)}) collective-permute-start(f32[256,128]{1,0:T(8,128)S(1)} %get-tuple-element.151), channel_id=1, source_target_pairs={{8,0},{9,1},{10,2},{11,3},{12,4},{13,5},{14,6},{15,7},{0,8},{1,9},... | collective-permute-start | bytes 393224 | tf_op jit(solution)/shard_map/ppermute | solution.py:420
  113.9 5.7 %collective-permute-done.26.refs_0_ = f32[1024,128]{1,0:T(8,128)S(1)} collective-permute-done((f32[1024,128]{1,0:T(8,128)S(1)}, f32[1024,128]{1,0:T(8,128)S(1)}, u32[]{:S(2)}, u32[]{:S(2)}) %collective-permute-start.26) | collective-permute-done | bytes 524320 | tf_op jit(solution)/shard_map/ppermute | solution.py:420
  120.1 2.0 %collective-permute-start.37 = (f32[512,128]{1,0:T(8,128)S(1)}, f32[512,128]{1,0:T(8,128)S(1)}, u32[]{:S(2)}, u32[]{:S(2)}) collective-permute-start(f32[512,128]{1,0:T(8,128)S(1)} %shard_map.62), channel_id=1, source_target_pairs={{4,0},{5,1},{6,2},{7,3},{0,4},{1,5},{2,6},{3,7},{12,8},{13,9},{14,... | collective-permute-start | bytes 786440 | tf_op jit(solution)/shard_map/ppermute | solution.py:420
  124.6 5.5 %collective-permute-start.33 = (f32[128,128]{1,0:T(8,128)S(1)}, f32[128,128]{1,0:T(8,128)S(1)}, u32[]{:S(2)}, u32[]{:S(2)}) collective-permute-start(f32[128,128]{1,0:T(8,128)S(1)} %get-tuple-element.154), channel_id=1, source_target_pairs={{1,0},{0,1},{3,2},{2,3},{5,4},{4,5},{7,6},{6,7},{9,8},{8,9},{11,10... | collective-permute-start | bytes 196616 | tf_op jit(solution)/shard_map/ppermute | solution.py:420
  131.7 2.0 %collective-permute-start.35 = (f32[128,128]{1,0:T(8,128)S(1)}, f32[128,128]{1,0:T(8,128)S(1)}, u32[]{:S(2)}, u32[]{:S(2)}) collective-permute-start(f32[128,128]{1,0:T(8,128)S(1)} %add.41.refs_0_), channel_id=1, source_target_pairs={{4,0},{5,1},{6,2},{7,3},{0,4},{1,5},{2,6},{3,7},{12,8},{13,9},{14,... | collective-permute-start | bytes 196616 | tf_op jit(solution)/shard_map/ppermute | solution.py:420
  134.2 2.7 %collective-permute-done.36.refs_3_ = f32[128,128]{1,0:T(8,128)S(1)} collective-permute-done((f32[128,128]{1,0:T(8,128)S(1)}, f32[128,128]{1,0:T(8,128)S(1)}, u32[]{:S(2)}, u32[]{:S(2)}) %collective-permute-start.36) | collective-permute-done | bytes 65568 | tf_op jit(solution)/shard_map/ppermute | solution.py:420
  138.8 3.3 %collective-permute-done.34.refs_1_ = f32[128,128]{1,0:T(8,128)S(1)} collective-permute-done((f32[128,128]{1,0:T(8,128)S(1)}, f32[128,128]{1,0:T(8,128)S(1)}, u32[]{:S(2)}, u32[]{:S(2)}) %collective-permute-start.34) | collective-permute-done | bytes 65568 | tf_op jit(solution)/shard_map/ppermute | solution.py:420
  142.2 3.4 %shard_map.66 = (f32[264,256]{1,0:T(8,128)S(1)}, f32[256,256]{1,0:T(8,128)}) custom-call(s32[16]{0:T(128)S(1)} %constant_dynamic-update-slice_fusion.f, f32[128,128]{1,0:T(8,128)S(1)} %add.41.refs_0_, f32[128,128]{1,0:T(8,128)S(1)} %collective-permute-done.34.refs_1_, f32[128,128]{1,0:T(8,128)S(1)} %collective-permute-done.35.refs_2_, ...), custom_call_target="tpu_custom_call" | custom-call | tf_op jit(solution)/shard_map/pallas_call | solution.py:52
  147.9 3.2 %shard_map.67 = (f32[2048,256]{1,0:T(8,128)}, f32[512,256]{1,0:T(8,128)}, f32[1,256]{1,0:T(1,128)}) custom-call(s32[16]{0:T(128)S(1)} %constant_dynamic-update-slice_fusion.f, f32[264,256]{1,0:T(8,128)S(1)} %get-tuple-element.162.refs_0_, f32[264,256]{1,0:T(8,128)S(1)} %collective-permute-done.38.refs_1_, f32[1024,128]{1,0:T(8,128)S(1)} %get-tuple-element.163.refs_2_, ...), custom_call_target="tpu_custom_call" | custom-call | tf_op jit(solution)/shard_map/pallas_call | solution.py:52
  (78 shorter events, 44.1 us)
Async XLA Ops:
  3.1 31.9 %collective-permute-start.4 = (f32[1024,256]{1,0:T(8,128)}, f32[1024,256]{1,0:T(8,128)S(1)}, u32[]{:S(2)}, u32[]{:S(2)}) collective-permute-start(f32[1024,256]{1,0:T(8,128)} %constant_dynamic-slice_fusion), channel_id=1, source_target_pairs={{4,0},{5,1},{6,2},{7,3},{0,4},{1,5},{2,6},{3,7},{12,8},{13,9},{14,... | collective-permute-start | bytes 3145736 | tf_op jit(solution)/shard_map/ppermute | solution.py:420
  10.4 7.0 %collective-permute-start.1 = (f32[384,128]{1,0:T(8,128)S(1)}, f32[384,128]{1,0:T(8,128)S(1)}, u32[]{:S(2)}, u32[]{:S(2)}) collective-permute-start(f32[384,128]{1,0:T(8,128)S(1)} %add.37.own_ref), channel_id=1, source_target_pairs={{2,0},{3,1},{0,2},{1,3},{6,4},{7,5},{4,6},{5,7},{10,8},{11,9},{8,1... | collective-permute-start | bytes 589832 | tf_op jit(solution)/shard_map/ppermute | solution.py:420
  20.8 14.2 %collective-permute-start.3 = (f32[256,256]{1,0:T(8,128)S(1)}, f32[256,256]{1,0:T(8,128)S(1)}, u32[]{:S(2)}, u32[]{:S(2)}) collective-permute-start(f32[256,256]{1,0:T(8,128)S(1)} %get-tuple-element.88.rotation_ref.own_ref), channel_id=1, source_target_pairs={{4,0},{5,1},{6,2},{7,3},{0,4},{1,5},{2,6},{3,7},{12,8},{13,9},{14,... | collective-permute-start | bytes 786440 | tf_op jit(solution)/shard_map/ppermute | solution.py:420
  22.3 26.4 %collective-permute-start.2 = (f32[1024,128]{1,0:T(8,128)S(1)}, f32[1024,128]{1,0:T(8,128)S(1)}, u32[]{:S(2)}, u32[]{:S(2)}) collective-permute-start(f32[1024,128]{1,0:T(8,128)S(1)} %get-tuple-element.90.refs_1_), channel_id=1, source_target_pairs={{8,0},{9,1},{10,2},{11,3},{16,8},{17,9},{18,10},{19,11},{4,12},{5,... | collective-permute-start | bytes 1572872 | tf_op jit(solution)/shard_map/ppermute | solution.py:420
  36.1 15.4 %collective-permute-start.5 = (f32[1024,128]{1,0:T(8,128)S(1)}, f32[1024,128]{1,0:T(8,128)S(1)}, u32[]{:S(2)}, u32[]{:S(2)}) collective-permute-start(f32[1024,128]{1,0:T(8,128)S(1)} %get-tuple-element.92.refs_4_), channel_id=1, source_target_pairs={{12,4},{13,5},{14,6},{15,7},{0,8},{1,9},{2,10},{3,11},{20,12},{21,... | collective-permute-start | bytes 1572872 | tf_op jit(solution)/shard_map/ppermute | solution.py:420
  41.6 4.3 %collective-permute-start.6 = (f32[128,128]{1,0:T(8,128)S(1)}, f32[128,128]{1,0:T(8,128)S(1)}, u32[]{:S(2)}, u32[]{:S(2)}) collective-permute-start(f32[128,128]{1,0:T(8,128)S(1)} %get-tuple-element.98), channel_id=1, source_target_pairs={{4,0},{0,1},{6,2},{2,3},{5,4},{1,5},{7,6},{3,7},{12,8},{8,9},{14,1... | collective-permute-start | bytes 196616 | tf_op jit(solution)/shard_map/ppermute | solution.py:420
  45.8 7.6 %collective-permute-start.7 = (f32[256,128]{1,0:T(8,128)S(1)}, f32[256,128]{1,0:T(8,128)S(1)}, u32[]{:S(2)}, u32[]{:S(2)}) collective-permute-start(f32[256,128]{1,0:T(8,128)S(1)} %get-tuple-element.99), channel_id=1, source_target_pairs={{8,0},{9,1},{10,2},{11,3},{12,4},{13,5},{14,6},{15,7},{0,8},{1,9},... | collective-permute-start | bytes 393224 | tf_op jit(solution)/shard_map/ppermute | solution.py:420
  47.4 6.0 %collective-permute-start.8 = (f32[256,128]{1,0:T(8,128)S(1)}, f32[256,128]{1,0:T(8,128)S(1)}, u32[]{:S(2)}, u32[]{:S(2)}) collective-permute-start(f32[256,128]{1,0:T(8,128)S(1)} %get-tuple-element.100), channel_id=1, source_target_pairs={{0,0},{1,1},{2,2},{3,3},{4,4},{5,5},{6,6},{7,7},{16,8},{17,9},{18,... | collective-permute-start | bytes 393224 | tf_op jit(solution)/shard_map/ppermute | solution.py:420
  48.0 5.4 %collective-permute-start.9 = (f32[128,128]{1,0:T(8,128)S(1)}, f32[128,128]{1,0:T(8,128)S(1)}, u32[]{:S(2)}, u32[]{:S(2)}) collective-permute-start(f32[128,128]{1,0:T(8,128)S(1)} %get-tuple-element.101), channel_id=1, source_target_pairs={{0,0},{8,1},{2,2},{10,3},{1,4},{9,5},{3,6},{11,7},{4,8},{16,9},{6,... | collective-permute-start | bytes 196616 | tf_op jit(solution)/shard_map/ppermute | solution.py:420
  55.8 5.5 %collective-permute-start.13 = (f32[128,128]{1,0:T(8,128)S(1)}, f32[128,128]{1,0:T(8,128)S(1)}, u32[]{:S(2)}, u32[]{:S(2)}) collective-permute-start(f32[128,128]{1,0:T(8,128)S(1)} %add.39.refs_0_), channel_id=1, source_target_pairs={{6,0},{7,1},{4,2},{5,3},{2,4},{3,5},{0,6},{1,7},{14,8},{15,9},{12,... | collective-permute-start | bytes 196616 | tf_op jit(solution)/shard_map/ppermute | solution.py:420
  58.5 4.3 %collective-permute-start.12 = (f32[128,128]{1,0:T(8,128)S(1)}, f32[128,128]{1,0:T(8,128)S(1)}, u32[]{:S(2)}, u32[]{:S(2)}) collective-permute-start(f32[128,128]{1,0:T(8,128)S(1)} %add.39.refs_0_), channel_id=1, source_target_pairs={{4,0},{5,1},{6,2},{7,3},{0,4},{1,5},{2,6},{3,7},{12,8},{13,9},{14,... | collective-permute-start | bytes 196616 | tf_op jit(solution)/shard_map/ppermute | solution.py:420
  58.8 4.3 %collective-permute-start.11 = (f32[128,128]{1,0:T(8,128)S(1)}, f32[128,128]{1,0:T(8,128)S(1)}, u32[]{:S(2)}, u32[]{:S(2)}) collective-permute-start(f32[128,128]{1,0:T(8,128)S(1)} %add.39.refs_0_), channel_id=1, source_target_pairs={{2,0},{3,1},{0,2},{1,3},{6,4},{7,5},{4,6},{5,7},{10,8},{11,9},{8,1... | collective-permute-start | bytes 196616 | tf_op jit(solution)/shard_map/ppermute | solution.py:420
  69.9 16.2 %collective-permute-start.15 = (f32[1024,128]{1,0:T(8,128)S(1)}, f32[1024,128]{1,0:T(8,128)S(1)}, u32[]{:S(2)}, u32[]{:S(2)}) collective-permute-start(f32[1024,128]{1,0:T(8,128)S(1)} %get-tuple-element.114), channel_id=1, source_target_pairs={{8,0},{9,1},{10,2},{11,3},{12,4},{13,5},{14,6},{15,7},{0,8},{1,9},... | collective-permute-start | bytes 1572872 | tf_op jit(solution)/shard_map/ppermute | solution.py:420
  73.4 12.7 %collective-permute-start.16 = (f32[1024,128]{1,0:T(8,128)S(1)}, f32[1024,128]{1,0:T(8,128)S(1)}, u32[]{:S(2)}, u32[]{:S(2)}) collective-permute-start(f32[1024,128]{1,0:T(8,128)S(1)} %get-tuple-element.115), channel_id=1, source_target_pairs={{0,0},{1,1},{2,2},{3,3},{4,4},{5,5},{6,6},{7,7},{16,8},{17,9},{18,... | collective-permute-start | bytes 1572872 | tf_op jit(solution)/shard_map/ppermute | solution.py:420
  77.2 11.2 %collective-permute-start.18 = (f32[256,128]{1,0:T(8,128)S(1)}, f32[256,128]{1,0:T(8,128)S(1)}, u32[]{:S(2)}, u32[]{:S(2)}) collective-permute-start(f32[256,128]{1,0:T(8,128)S(1)} %get-tuple-element.124), channel_id=1, source_target_pairs={{8,0},{9,1},{10,2},{11,3},{12,4},{13,5},{14,6},{15,7},{0,8},{1,9},... | collective-permute-start | bytes 393224 | tf_op jit(solution)/shard_map/ppermute | solution.py:420
  79.6 8.8 %collective-permute-start.19 = (f32[256,128]{1,0:T(8,128)S(1)}, f32[256,128]{1,0:T(8,128)S(1)}, u32[]{:S(2)}, u32[]{:S(2)}) collective-permute-start(f32[256,128]{1,0:T(8,128)S(1)} %get-tuple-element.125), channel_id=1, source_target_pairs={{0,0},{1,1},{2,2},{3,3},{4,4},{5,5},{6,6},{7,7},{16,8},{17,9},{18,... | collective-permute-start | bytes 393224 | tf_op jit(solution)/shard_map/ppermute | solution.py:420
  80.3 7.5 %collective-permute-start.20 = (f32[128,128]{1,0:T(8,128)S(1)}, f32[128,128]{1,0:T(8,128)S(1)}, u32[]{:S(2)}, u32[]{:S(2)}) collective-permute-start(f32[128,128]{1,0:T(8,128)S(1)} %get-tuple-element.126), channel_id=1, source_target_pairs={{0,0},{8,1},{2,2},{10,3},{4,4},{12,5},{6,6},{14,7},{1,8},{16,9},{3... | collective-permute-start | bytes 196616 | tf_op jit(solution)/shard_map/ppermute | solution.py:420
  89.9 5.9 %collective-permute-start.24 = (f32[128,128]{1,0:T(8,128)S(1)}, f32[128,128]{1,0:T(8,128)S(1)}, u32[]{:S(2)}, u32[]{:S(2)}) collective-permute-start(f32[128,128]{1,0:T(8,128)S(1)} %add.40.refs_0_), channel_id=1, source_target_pairs={{6,0},{7,1},{4,2},{5,3},{2,4},{3,5},{0,6},{1,7},{14,8},{15,9},{12,... | collective-permute-start | bytes 196616 | tf_op jit(solution)/shard_map/ppermute | solution.py:420
  90.1 5.8 %collective-permute-start.23 = (f32[128,128]{1,0:T(8,128)S(1)}, f32[128,128]{1,0:T(8,128)S(1)}, u32[]{:S(2)}, u32[]{:S(2)}) collective-permute-start(f32[128,128]{1,0:T(8,128)S(1)} %add.40.refs_0_), channel_id=1, source_target_pairs={{4,0},{5,1},{6,2},{7,3},{0,4},{1,5},{2,6},{3,7},{12,8},{13,9},{14,... | collective-permute-start | bytes 196616 | tf_op jit(solution)/shard_map/ppermute | solution.py:420
  92.2 4.4 %collective-permute-start.22 = (f32[128,128]{1,0:T(8,128)S(1)}, f32[128,128]{1,0:T(8,128)S(1)}, u32[]{:S(2)}, u32[]{:S(2)}) collective-permute-start(f32[128,128]{1,0:T(8,128)S(1)} %add.40.refs_0_), channel_id=1, source_target_pairs={{2,0},{3,1},{0,2},{1,3},{6,4},{7,5},{4,6},{5,7},{10,8},{11,9},{8,1... | collective-permute-start | bytes 196616 | tf_op jit(solution)/shard_map/ppermute | solution.py:420
  103.0 21.5 %collective-permute-start.28 = (f32[1280,128]{1,0:T(8,128)S(1)}, f32[1280,128]{1,0:T(8,128)S(1)}, u32[]{:S(2)}, u32[]{:S(2)}) collective-permute-start(f32[1280,128]{1,0:T(8,128)S(1)} %get-tuple-element.145), channel_id=1, source_target_pairs={{4,0},{5,1},{6,2},{7,3},{0,4},{1,5},{2,6},{3,7},{12,8},{13,9},{14,... | collective-permute-start | bytes 1966088 | tf_op jit(solution)/shard_map/ppermute | solution.py:420
  103.1 16.4 %collective-permute-start.26 = (f32[1024,128]{1,0:T(8,128)S(1)}, f32[1024,128]{1,0:T(8,128)S(1)}, u32[]{:S(2)}, u32[]{:S(2)}) collective-permute-start(f32[1024,128]{1,0:T(8,128)S(1)} %get-tuple-element.137), channel_id=1, source_target_pairs={{8,0},{9,1},{10,2},{11,3},{12,4},{13,5},{14,6},{15,7},{0,8},{1,9},... | collective-permute-start | bytes 1572872 | tf_op jit(solution)/shard_map/ppermute | solution.py:420
  106.8 12.7 %collective-permute-start.27 = (f32[1024,128]{1,0:T(8,128)S(1)}, f32[1024,128]{1,0:T(8,128)S(1)}, u32[]{:S(2)}, u32[]{:S(2)}) collective-permute-start(f32[1024,128]{1,0:T(8,128)S(1)} %get-tuple-element.138), channel_id=1, source_target_pairs={{0,0},{1,1},{2,2},{3,3},{4,4},{5,5},{6,6},{7,7},{16,8},{17,9},{18,... | collective-permute-start | bytes 1572872 | tf_op jit(solution)/shard_map/ppermute | solution.py:420
  110.5 14.1 %collective-permute-start.30 = (f32[256,128]{1,0:T(8,128)S(1)}, f32[256,128]{1,0:T(8,128)S(1)}, u32[]{:S(2)}, u32[]{:S(2)}) collective-permute-start(f32[256,128]{1,0:T(8,128)S(1)} %get-tuple-element.151), channel_id=1, source_target_pairs={{8,0},{9,1},{10,2},{11,3},{12,4},{13,5},{14,6},{15,7},{0,8},{1,9},... | collective-permute-start | bytes 393224 | tf_op jit(solution)/shard_map/ppermute | solution.py:420
  113.2 11.4 %collective-permute-start.31 = (f32[256,128]{1,0:T(8,128)S(1)}, f32[256,128]{1,0:T(8,128)S(1)}, u32[]{:S(2)}, u32[]{:S(2)}) collective-permute-start(f32[256,128]{1,0:T(8,128)S(1)} %get-tuple-element.152), channel_id=1, source_target_pairs={{0,0},{1,1},{2,2},{3,3},{4,4},{5,5},{6,6},{7,7},{16,8},{17,9},{18,... | collective-permute-start | bytes 393224 | tf_op jit(solution)/shard_map/ppermute | solution.py:420
  120.1 14.1 %collective-permute-start.37 = (f32[512,128]{1,0:T(8,128)S(1)}, f32[512,128]{1,0:T(8,128)S(1)}, u32[]{:S(2)}, u32[]{:S(2)}) collective-permute-start(f32[512,128]{1,0:T(8,128)S(1)} %shard_map.62), channel_id=1, source_target_pairs={{4,0},{5,1},{6,2},{7,3},{0,4},{1,5},{2,6},{3,7},{12,8},{13,9},{14,... | collective-permute-start | bytes 786440 | tf_op jit(solution)/shard_map/ppermute | solution.py:420
  122.2 2.3 %collective-permute-start.32 = (f32[128,128]{1,0:T(8,128)S(1)}, f32[128,128]{1,0:T(8,128)S(1)}, u32[]{:S(2)}, u32[]{:S(2)}) collective-permute-start(f32[128,128]{1,0:T(8,128)S(1)} %get-tuple-element.153), channel_id=1, source_target_pairs={{0,0},{8,1},{2,2},{10,3},{4,4},{12,5},{6,6},{14,7},{1,8},{16,9},{3... | collective-permute-start | bytes 196616 | tf_op jit(solution)/shard_map/ppermute | solution.py:420
  124.6 6.4 %collective-permute-start.33 = (f32[128,128]{1,0:T(8,128)S(1)}, f32[128,128]{1,0:T(8,128)S(1)}, u32[]{:S(2)}, u32[]{:S(2)}) collective-permute-start(f32[128,128]{1,0:T(8,128)S(1)} %get-tuple-element.154), channel_id=1, source_target_pairs={{1,0},{0,1},{3,2},{2,3},{5,4},{4,5},{7,6},{6,7},{9,8},{8,9},{11,10... | collective-permute-start | bytes 196616 | tf_op jit(solution)/shard_map/ppermute | solution.py:420
  131.0 5.9 %collective-permute-start.36 = (f32[128,128]{1,0:T(8,128)S(1)}, f32[128,128]{1,0:T(8,128)S(1)}, u32[]{:S(2)}, u32[]{:S(2)}) collective-permute-start(f32[128,128]{1,0:T(8,128)S(1)} %add.41.refs_0_), channel_id=1, source_target_pairs={{6,0},{7,1},{4,2},{5,3},{2,4},{3,5},{0,6},{1,7},{14,8},{15,9},{12,... | collective-permute-start | bytes 196616 | tf_op jit(solution)/shard_map/ppermute | solution.py:420
  131.7 5.7 %collective-permute-start.35 = (f32[128,128]{1,0:T(8,128)S(1)}, f32[128,128]{1,0:T(8,128)S(1)}, u32[]{:S(2)}, u32[]{:S(2)}) collective-permute-start(f32[128,128]{1,0:T(8,128)S(1)} %add.41.refs_0_), channel_id=1, source_target_pairs={{4,0},{5,1},{6,2},{7,3},{0,4},{1,5},{2,6},{3,7},{12,8},{13,9},{14,... | collective-permute-start | bytes 196616 | tf_op jit(solution)/shard_map/ppermute | solution.py:420
  137.4 10.6 %collective-permute-start.39 = (f32[768,128]{1,0:T(8,128)S(1)}, f32[768,128]{1,0:T(8,128)S(1)}, u32[]{:S(2)}, u32[]{:S(2)}) collective-permute-start(f32[768,128]{1,0:T(8,128)S(1)} %shard_map.65), channel_id=1, source_target_pairs={{4,0},{5,1},{6,2},{7,3},{0,4},{1,5},{2,6},{3,7},{12,8},{13,9},{14,... | collective-permute-start | bytes 1179656 | tf_op jit(solution)/shard_map/ppermute | solution.py:420
  137.9 4.3 %collective-permute-start.34 = (f32[128,128]{1,0:T(8,128)S(1)}, f32[128,128]{1,0:T(8,128)S(1)}, u32[]{:S(2)}, u32[]{:S(2)}) collective-permute-start(f32[128,128]{1,0:T(8,128)S(1)} %add.41.refs_0_), channel_id=1, source_target_pairs={{2,0},{3,1},{0,2},{1,3},{6,4},{7,5},{4,6},{5,7},{10,8},{11,9},{8,1... | collective-permute-start | bytes 196616 | tf_op jit(solution)/shard_map/ppermute | solution.py:420
  (10 other events, 23.6 us)

commit v7 on v6

--- a/solution.py
+++ b/solution.py
@@ -71,6 +71,36 @@
         out_ref[2 * half :] = g[half:, half:]
 
     return call(body, facts, [sector], shape(3 * half, half))
+
+
+def give_rows(facts, sector, top):
+    rows, width = sector.shape
+    part = rows // 2
+
+    def body(f, x_ref, top_ref, rest_ref, sems):
+        start = pl.multiple_of((1 - f[X]) * part, 8)
+        copies = [
+            pltpu.make_async_copy(
+                x_ref.at[pl.ds(start, top)], top_ref, sems.at[0]
+            ),
+            pltpu.make_async_copy(
+                x_ref.at[pl.ds(start + top, part - top)], rest_ref, sems.at[1]
+            ),
+        ]
+        for copy in copies:
+            copy.start()
+        for copy in copies:
+            copy.wait()
+
+    return pl.pallas_call(
+        body,
+        out_shape=(shape(top, width), shape(part - top, width)),
+        in_specs=[
+            pl.BlockSpec(memory_space=pltpu.SMEM), pl.BlockSpec(memory_space=pl.ANY)
+        ],
+        out_specs=(pl.BlockSpec(memory_space=pltpu.VMEM),) * 2,
+        scratch_shapes=[pltpu.SemaphoreType.DMA((2,))],
+    )(facts, sector)
 
 
 def rotate_of(gram, x_ref, e_ref):
@@ -202,14 +232,17 @@
     )
 
 
-def put_turned(f, refs, zero, one, half):
-    a_ref, b_ref, nat_l_ref, nat_u_ref = refs
+def put_turned(f, refs, zero, one, half, at=0):
+    a_ref, b_ref, nat_l_ref, nat_u_ref = refs[:4]
     even = f[EVEN] == 1
+    rows = slice(at, at + zero.shape[0])
     to_left, to_right = zero[:, half:], one[:, :half]
-    a_ref[...] = jnp.where(even, to_right, to_left)
-    b_ref[...] = jnp.where(even, to_left, to_right)
-    nat_l_ref[...] = one[:, half:]
-    nat_u_ref[...] = zero[:, :half]
+    a_ref[rows] = jnp.where(even, to_right, to_left)
+    b_ref[rows] = jnp.where(even, to_left, to_right)
+    nat_l_ref[rows] = one[:, half:]
+    nat_u_ref[rows] = zero[:, :half]
+    if len(refs) > 4:
+        refs[4][rows] = jnp.where(f[X] == 0, zero[:, :half], one[:, half:])
 
 
 def turns_of(f, own_ref, other_ref):
@@ -261,21 +294,19 @@
         turn_0, turn_1 = split(turn_0), split(turn_1)
         columns = [r[...] for r in refs[:4]]
         rows = blocks_of(f, *[r[...] for r in refs[4:8]])
-        at = 0
-        for (up_0, low_0, up_1, low_1), outs in (
-            (columns, refs[8:12]), (rows, refs[12:16])
-        ):
+        outs = refs[8:]
+        for (up_0, low_0, up_1, low_1), at in ((columns, 0), (rows, part)):
             zero = dot3(lax.concatenate([up_0, low_0], 1), turn_0)
             one = dot3(lax.concatenate([up_1, low_1], 1), turn_1)
-            put_turned(f, outs, zero, one, half)
             if last_move:
-                given = jnp.where(f[X] == 0, zero[:, :half], one[:, half:])
-                refs[16][at : at + given.shape[0]] = given
-                at += given.shape[0]
-
-    outs = (shape(part, half),) * 4 + (shape(vector_rows, half),) * 4
+                put_turned(f, outs, zero, one, half, at)
+            else:
+                put_turned(f, outs[4 if at else 0 :][:4], zero, one, half)
+
     if last_move:
-        outs = outs + (shape(part + vector_rows, half),)
+        outs = (shape(part + vector_rows, half),) * 5
+    else:
+        outs = (shape(part, half),) * 4 + (shape(vector_rows, half),) * 4
     return call(body, facts, packs + blocks + vectors, outs)
 
 
@@ -285,53 +316,68 @@
     refs[1][...] = jnp.where(core, one, zero)
 
 
-def first_cross_gram(facts, own, other, half):
+def first_cross_gram(facts, own, others, half):
     rows = own[0].shape[0]
+    pieces = len(others)
 
     def body(f, *refs):
-        up_0, low_0, up_1, low_1 = refs[8:]
+        own_refs = [[r] for r in refs[:3]]
+        other_refs = [refs[3 + k : 3 + 3 * pieces : 3] for k in range(3)]
+        up_0, low_0, up_1, low_1 = refs[5 + 3 * pieces :]
+
+        def fill(target, sources):
+            at = 0
+            for ref in sources:
+                target[at : at + ref.shape[0]] = ref[...]
+                at += ref.shape[0]
+
         first, last = f[FIRST] == 1, f[LAST] == 1
-        for x, near, far in ((0, refs[:3], refs[3:6]), (1, refs[3:6], refs[:3])):
+        for x, near, far in ((0, own_refs, other_refs), (1, other_refs, own_refs)):
             here = f[X] == x
 
             @pl.when(here)
             def _():
-                up_1[...] = near[0][...]
-                low_0[...] = far[0][...]
+                fill(up_1, near[0])
+                fill(low_0, far[0])
 
             @pl.when(here & first)
             def _():
-                up_0[...] = near[1][...]
+                fill(up_0, near[1])
 
             @pl.when(here & ~first)
             def _():
-                up_0[...] = far[2][...]
+                fill(up_0, far[2])
 
             @pl.when(here & last)
             def _():
-                low_1[...] = far[1][...]
+                fill(low_1, far[1])
 
             @pl.when(here & ~last)
             def _():
-                low_1[...] = near[2][...]
+                fill(low_1, near[2])
 
         put_cross(
             f,
-            refs[6:],
+            refs[3 + 3 * pieces :],
             dot_tn(up_0[...], low_0[...]),
             dot_tn(up_1[...], low_1[...]),
         )
 
     outs = (shape(half, half),) * 2 + (shape(rows, half),) * 4
-    return call(body, facts, own + other, outs)
-
-
-def cross_gram(facts, got, natives, half):
+    return call(body, facts, own + sum(others, []), outs)
+
+
+def cross_gram(facts, got, natives, part, half):
     rows = got[0].shape[0]
 
     def body(f, *refs):
         up_0, low_0, up_1, low_1 = blocks_of(f, *[r[...] for r in refs[:4]])
-        put_cross(f, refs[4:], dot_tn(up_0, low_0), dot_tn(up_1, low_1))
+        put_cross(
+            f,
+            refs[4:],
+            dot_tn(up_0[:part], low_0[:part]),
+            dot_tn(up_1[:part], low_1[:part]),
+        )
         refs[6][...] = up_0
         refs[7][...] = low_1
 
@@ -339,27 +385,17 @@
     return call(body, facts, got + natives, outs)
 
 
-def give(facts, pieces, half):
-    total = sum(stop - start for _, start, stop in pieces)
-
-    def body(f, *refs):
+def give(facts, got, start, stop, half):
+    def body(f, a_ref, b_ref, out_ref):
         mine = f[X] != f[EVEN]
-        at = 0
-        for k, (_, start, stop) in enumerate(pieces):
-            a_ref, b_ref = refs[2 * k : 2 * k + 2]
-            refs[-1][at : at + stop - start] = jnp.where(
-                mine, a_ref[start:stop], b_ref[start:stop]
-            )
-            at += stop - start
-
-    return call(
-        body, facts, sum([list(got) for got, _, _ in pieces], []), shape(total, half)
-    )
-
-
-def finish(facts, packs, blocks, vectors, native, got_top, got_rest, half):
+        out_ref[...] = jnp.where(mine, a_ref[start:stop], b_ref[start:stop])
+
+    return call(body, facts, got, shape(stop - start, half))
+
+
+def finish(facts, packs, blocks, native, got_top, got_rest, part, half):
     size = 2 * half
-    part, vector_rows = blocks[0].shape[0], vectors[0].shape[0]
+    vector_rows = blocks[0].shape[0] - part
     top = got_top.shape[0]
 
     def body(f, *refs):
@@ -367,37 +403,68 @@
         mine = f[CORE] == x
         pack = jnp.where(mine, refs[0][...], refs[1][...])
         turned = split(swapped(x == 1, pack[:size], 0))
-        native_ref, top_ref, rest_ref = refs[10:13]
-        out_ref, vectors_ref, singular_ref = refs[13:]
+        native_ref, top_ref, rest_ref = refs[6:9]
+        out_ref, vectors_ref, singular_ref, out, vectors, sems = refs[9:]
+        copies = []
+
+        def put(source, target, here, there, value):
+            rows = value.shape[0]
+            source[here : here + rows] = value
+            there = pl.multiple_of(there, 8)
+            copies.append(
+                pltpu.make_async_copy(
+                    source.at[here : here + rows],
+                    target.at[pl.ds(there, rows)],
+                    sems.at[len(copies)],
+                )
+            )
+            copies[-1].start()
 
         def product(moved, native):
             return dot3(lax.concatenate([moved, native], 1), turned)
 
-        def own(up_0, low_0, up_1, low_1):
+        def kept(rows):
+            up_0, low_0, up_1, low_1 = [r[rows] for r in refs[2:6]]
             return product(
                 jnp.where(x == 0, up_0, low_1), jnp.where(x == 0, low_0, up_1)
             )
 
-        def put(ref, at, value):
-            ref[pl.ds(pl.multiple_of(at, 8), value.shape[0])] = value
-
-        put(out_ref, x * part, own(*[r[...] for r in refs[2:6]]))
-        rows = blocks_of(f, *[r[...] for r in refs[6:10]])
-        put(vectors_ref, x * vector_rows, own(*rows))
-        there = (1 - x) * part
-        put(out_ref, there, product(top_ref[...], native_ref[:top]))
-        rest = product(rest_ref[...], native_ref[top:])
-        put(out_ref, there + top, rest[: part - top])
-        put(vectors_ref, (1 - x) * vector_rows, rest[part - top :])
         squares = pack[size : size + 1]
         singular_ref[...] = jnp.sqrt(jnp.maximum(squares, 0.0) + 1e-06)
-
-    return call(
+        other = (1 - x) * part
+        middle = part // 2
+        put(out, out_ref, 0, x * part, kept(slice(0, middle)))
+        put(out, out_ref, middle, x * part + middle, kept(slice(middle, part)))
+        put(out, out_ref, part, other, product(top_ref[...], native_ref[:top]))
+        put(
+            out, out_ref, part + top, other + top,
+            product(rest_ref[: part - top], native_ref[top:part]),
+        )
+        put(vectors, vectors_ref, 0, x * vector_rows, kept(slice(part, None)))
+        put(
+            vectors, vectors_ref, vector_rows, (1 - x) * vector_rows,
+            product(rest_ref[part - top :], native_ref[part:]),
+        )
+        for copy in copies:
+            copy.wait()
+
+    vmem = pl.BlockSpec(memory_space=pltpu.VMEM)
+    hbm = pl.BlockSpec(memory_space=pl.ANY)
+    inputs = packs + blocks + [native, got_top, got_rest]
+    return pl.pallas_call(
         body,
-        facts,
-        packs + blocks + vectors + [native, got_top, got_rest],
-        (shape(2 * part, size), shape(2 * vector_rows, size), shape(1, size)),
-    )
+        out_shape=(
+            shape(2 * part, size), shape(2 * vector_rows, size), shape(1, size)
+        ),
+        in_specs=[pl.BlockSpec(memory_space=pltpu.SMEM)] + [vmem] * len(inputs),
+        out_specs=(hbm, hbm, vmem),
+        scratch_shapes=[
+            pltpu.VMEM((2 * part, size), jnp.float32),
+            pltpu.VMEM((2 * vector_rows, size), jnp.float32),
+            pltpu.SemaphoreType.DMA((6,)),
+        ],
+        compiler_params=pltpu.CompilerParams(vmem_limit_bytes=24 << 20),
+    )(facts, *inputs)
 
 
 def per_device(sector, block_label):
@@ -486,7 +553,8 @@
     def together(*arrays):
         return lax.optimization_barrier(arrays)
 
-    got = exchange(lax.dynamic_slice_in_dim(sector, (1 - x) * part, part), 1, 0)
+    top_give, rest_give = give_rows(facts, sector, part * 3 // 4)
+    got_top = exchange(top_give, 1, 0)
     own = first_gram(facts, sector, half)
     own = sum_rows(own + exchange(own, 0, 1))
     rotation, gram = first_rotation(facts, own, exchange(own, 0, 2), half)
@@ -494,13 +562,17 @@
     for sweep_round in range(ROUNDS - 1):
         last_move = sweep_round == ROUNDS - 2
         if sweep_round == 0:
+            other_rotation = exchange(rotation, 1, 0)
             stay, leave = turn_rows(facts, rotation, sector, half, True)
+            leave, rest_give = together(leave, rest_give)
+            got_rest = exchange(rest_give, 1, 0)
             own_rows = [stay, leave, shift(leave, -2)]
+            other_rows = []
+            for got in (got_top, got_rest):
+                stay, leave = turn_rows(facts, other_rotation, got, half, False)
+                other_rows.append([stay, leave, shift(leave, 2)])
             leave, stay = turned_gram(facts, gram, rotation, X)
             diagonals = [first_diagonal(leave, True), first_diagonal(stay, False)]
-            other_rotation = exchange(rotation, 1, 0)
-            stay, leave = turn_rows(facts, other_rotation, got, half, False)
-            other_rows = [stay, leave, shift(leave, 2)]
             vectors = list(
                 first_vectors(facts, rotation, other_rotation, vector_rows, half)
             )
@@ -518,37 +590,40 @@
             got = [swap(leave_a, 0), swap(leave_b, 1)]
             leave, stay = turned_gram(facts, gram, rotation, CORE)
             diagonals = [pass_diagonal(leave), exchange(stay, 0, 1)]
-            vectors[0], vectors[1], diagonals[1] = together(
-                vectors[0], vectors[1], diagonals[1]
-            )
             if last_move:
                 native = exchange(vectors.pop(), 1, 0)
                 top = part // 2
-                top_give = give(facts, [(got, 0, top)], half)
-                *got, top_give = together(*got, top_give)
+                top_give = give(facts, got, 0, top, half)
+                *got, top_give, diagonals[0], diagonals[1] = together(
+                    *got, top_give, *diagonals
+                )
                 got_top = exchange(top_give, 1, 0)
-            *grams, up_0, low_1 = cross_gram(facts, got, [nat_l, nat_u], half)
-            if last_move:
-                grams[1], native = together(grams[1], native)
+            else:
+                vectors[0], vectors[1], diagonals[1] = together(
+                    vectors[0], vectors[1], diagonals[1]
+                )
+            *grams, up_0, low_1 = cross_gram(facts, got, [nat_l, nat_u], part, half)
         blocks = [up_0, nat_l, nat_u, low_1]
-        vector_a, vector_b, *kept = vectors
-        vectors = [swap(vector_a, 0), swap(vector_b, 1)] + kept
-        grams[1], vectors[0], vectors[1], diagonals[0] = together(
-            grams[1], *vectors[:2], diagonals[0]
-        )
+        if last_move:
+            grams[1], native = together(grams[1], native)
+        else:
+            vector_a, vector_b, *kept = vectors
+            grams[1], vector_a, vector_b, diagonals[0] = together(
+                grams[1], swap(vector_a, 0), swap(vector_b, 1), diagonals[0]
+            )
+            vectors = [vector_a, vector_b] + kept
         own = sum_rows(grams[0] + exchange(grams[1], 0, 1))
-        if last_move:
-            rest = give(
-                facts, [(got, top, part), (vectors[:2], 0, vector_rows)], half
-            )
         parts = [own, exchange(own, 0, 2), exchange(own, 1, 0), exchange(own, 1, 2)]
         if last_move:
-            parts[2], parts[3], got_top, rest = together(*parts[2:], got_top, rest)
-            got_rest = exchange(rest, 1, 0)
+            rest_give = give(facts, got, top, part + vector_rows, half)
+            parts[2], parts[3], got_top, rest_give = together(
+                *parts[2:], got_top, rest_give
+            )
+            got_rest = exchange(rest_give, 1, 0)
         rotation, gram = later_rotation(facts, parts, diagonals, half, last_move)
     packs = [rotation, exchange(rotation, 0, 1)]
     rotated, vectors_out, singular = finish(
-        facts, packs, blocks, vectors, native, got_top, got_rest, half
+        facts, packs, blocks, native, got_top, got_rest, part, half
     )
     return rotated, vectors_out, singular.reshape(size)
 

time: 152 us -> 150 us (0.987)
  waiting for transfers between devices: 59.7 us -> 46.4 us
  starting transfers between devices: 50.6 us -> 57.5 us
  Pallas kernels: 37.2 us -> 40.9 us
    ppermute x40, waiting for transfers between devices: 59.7 us -> 46.4 us  [permute(): return lax.ppermute(block, ('pair', 'row'), moves)]
    ppermute x40, starting transfers between devices: 50.6 us -> 57.5 us  [permute(): return lax.ppermute(block, ('pair', 'row'), moves)]
    pallas_call x0 -> x2, Pallas kernels: none -> 6.22 us  [the longest x1 3.39 us: finish(): pl.pallas_call(body, out_shape=(shape(2 * part, size), shape(2 * vector_r...]
    pallas_call x19, Pallas kernels: 37.2 us -> 34.7 us  [call(): pl.pallas_call(body, out_shape=outs, in_specs=[pl.BlockSpec(memory_space=...]
    dynamic_slice x1 -> x0, local copies, waits for them, and re-layouts: 2.41 us -> none  [per_device(): got = exchange(lax.dynamic_slice_in_dim(sector, (1 - x) * part, part), 1, 0)]
  transfers between devices with their start and end apart: 40 -> 40, of which waited for: 26 -> 24; matrix products, arithmetic and copies ran while one was open for 0% -> 0% of each run, Pallas kernels for 16% -> 17%
where the time goes in v7:
time: 150 us; the launch traced here: 148 us
  starting transfers between devices  57.5 us (38%)
  waiting for transfers between devices  46.4 us (31%)
  Pallas kernels  40.9 us (27%)
  local copies, waits for them, and re-layouts  2.12 us (1%)
    ppermute x40, starting transfers between devices, permute(): return lax.ppermute(block, ('pair', 'row'), moves)  57.5 us
    ppermute x40, waiting for transfers between devices, permute(): return lax.ppermute(block, ('pair', 'row'), moves)  46.4 us
    pallas_call x19, Pallas kernels, call(): pl.pallas_call(body, out_shape=outs, in_specs=[pl.BlockSpec(memory_space=...  34.7 us
    pallas_call x1, Pallas kernels, finish(): pl.pallas_call(body, out_shape=(shape(2 * part, size), shape(2 * vector_r...  3.39 us
  transfers between devices with their start and end apart: 40, of which 24 were waited for; matrix products, arithmetic and copies ran while one was open for 0% of the time, Pallas kernels for 17%

profile of v7, /device:TPU:0, one launch (start us, length us, event | category | flops | bytes accessed | tf_op | source)
XLA Modules:
  0.0 148.3 jit_solution(574460282714362623)
XLA Ops:
  2.2 2.8 %shard_map.52 = (f32[768,256]{1,0:T(8,128)}, f32[256,256]{1,0:T(8,128)}) custom-call(s32[16]{0:T(128)} %copy-done.1, f32[2048,256]{1,0:T(8,128)} %x_ref.5), custom_call_target="tpu_custom_call" | custom-call | tf_op jit(solution)/shard_map/pallas_call | solution.py:95
  5.0 3.0 %collective-permute-start.4 = (f32[768,256]{1,0:T(8,128)}, f32[768,256]{1,0:T(8,128)S(1)}, u32[]{:S(2)}, u32[]{:S(2)}) collective-permute-start(f32[768,256]{1,0:T(8,128)} %get-tuple-element.90), channel_id=1, source_target_pairs={{4,0},{5,1},{6,2},{7,3},{0,4},{1,5},{2,6},{3,7},{12,8},{13,9},{14,... | collective-permute-start | bytes 2359304 | tf_op jit(solution)/shard_map/ppermute | solution.py:487
  8.7 2.6 %shard_map.49 = f32[384,128]{1,0:T(8,128)S(1)} custom-call(s32[16]{0:T(128)S(1)} %copy-done.2, f32[2048,256]{1,0:T(8,128)S(1)} %copy-done), custom_call_target="tpu_custom_call" | custom-call | tf_op jit(solution)/shard_map/pallas_call | solution.py:52
  14.4 5.4 %collective-permute-done.1.other_ref = f32[384,128]{1,0:T(8,128)S(1)} collective-permute-done((f32[384,128]{1,0:T(8,128)S(1)}, f32[384,128]{1,0:T(8,128)S(1)}, u32[]{:S(2)}, u32[]{:S(2)}) %collective-permute-start.1) | collective-permute-done | bytes 196640 | tf_op jit(solution)/shard_map/ppermute | solution.py:487
  19.9 3.4 %shard_map.50 = (f32[256,256]{1,0:T(8,128)S(1)}, f32[256,256]{1,0:T(8,128)S(1)}) custom-call(s32[16]{0:T(128)S(1)} %copy-done.2, f32[384,128]{1,0:T(8,128)S(1)} %add.34.own_ref, f32[384,128]{1,0:T(8,128)S(1)} %collective-permute-done.1.other_ref), custom_call_target="tpu_custom_call" | custom-call | tf_op jit(solution)/shard_map/pallas_call | solution.py:52
  26.1 4.0 %collective-permute-start.6 = (f32[256,256]{1,0:T(8,128)S(1)}, f32[256,256]{1,0:T(8,128)S(1)}, u32[]{:S(2)}, u32[]{:S(2)}) collective-permute-start(f32[256,256]{1,0:T(8,128)S(1)} %copy-done.3), channel_id=1, source_target_pairs={{4,0},{5,1},{6,2},{7,3},{0,4},{1,5},{2,6},{3,7},{12,8},{13,9},{14,... | collective-permute-start | bytes 786440 | tf_op jit(solution)/shard_map/ppermute | solution.py:487
  30.1 2.5 %collective-permute-done.3.rotation_ref.other_ref = f32[256,256]{1,0:T(8,128)S(1)} collective-permute-done((f32[256,256]{1,0:T(8,128)S(1)}, f32[256,256]{1,0:T(8,128)S(1)}, u32[]{:S(2)}, u32[]{:S(2)}) %collective-permute-start.3) | collective-permute-done | bytes 262176 | tf_op jit(solution)/shard_map/ppermute | solution.py:487
  33.6 3.5 %collective-permute-start.5 = (f32[768,128]{1,0:T(8,128)S(1)}, f32[768,128]{1,0:T(8,128)S(1)}, u32[]{:S(2)}, u32[]{:S(2)}) collective-permute-start(f32[768,128]{1,0:T(8,128)S(1)} %get-tuple-element.92.refs_4_), channel_id=1, source_target_pairs={{12,4},{13,5},{14,6},{15,7},{0,8},{1,9},{2,10},{3,11},{20,12},{21,... | collective-permute-start | bytes 1179656 | tf_op jit(solution)/shard_map/ppermute | solution.py:487
  39.7 3.5 %collective-permute-start.7 = (f32[256,128]{1,0:T(8,128)S(1)}, f32[256,128]{1,0:T(8,128)S(1)}, u32[]{:S(2)}, u32[]{:S(2)}) collective-permute-start(f32[256,128]{1,0:T(8,128)S(1)} %get-tuple-element.95.refs_7_), channel_id=1, source_target_pairs={{12,4},{13,5},{14,6},{15,7},{0,8},{1,9},{2,10},{3,11},{20,12},{21,... | collective-permute-start | bytes 393224 | tf_op jit(solution)/shard_map/ppermute | solution.py:487
  48.7 1.8 %shard_map.55 = (f32[128,128]{1,0:T(8,128)S(1)}, f32[128,128]{1,0:T(8,128)S(1)}, f32[1024,128]{1,0:T(8,128)S(1)}, f32[1024,128]{1,0:T(8,128)S(1)}, f32[1024,128]{1,0:T(8,128)S(1)}, /*index=5*/f32[1024,128]{1,0:T(8,128)S(1)}) custom-call(s32[16]{0:T(128)S(1)} %copy-done.2, f32[1024,128]{1,0:T(8,128)S(1)} %get-tuple-element.86.refs_0_, ...), custom_call_target="tpu_custom_call" | custom-call | tf_op jit(solution)/shard_map/pallas_call | solution.py:52
  50.6 3.9 %collective-permute-start.12 = (f32[128,128]{1,0:T(8,128)S(1)}, f32[128,128]{1,0:T(8,128)S(1)}, u32[]{:S(2)}, u32[]{:S(2)}) collective-permute-start(f32[128,128]{1,0:T(8,128)S(1)} %get-tuple-element.105), channel_id=1, source_target_pairs={{1,0},{0,1},{3,2},{2,3},{5,4},{4,5},{7,6},{6,7},{9,8},{8,9},{11,10... | collective-permute-start | bytes 196616 | tf_op jit(solution)/shard_map/ppermute | solution.py:487
  55.4 2.7 %collective-permute-start.15 = (f32[128,128]{1,0:T(8,128)S(1)}, f32[128,128]{1,0:T(8,128)S(1)}, u32[]{:S(2)}, u32[]{:S(2)}) collective-permute-start(f32[128,128]{1,0:T(8,128)S(1)} %add.35.refs_0_), channel_id=1, source_target_pairs={{6,0},{7,1},{4,2},{5,3},{2,4},{3,5},{0,6},{1,7},{14,8},{15,9},{12,... | collective-permute-start | bytes 196616 | tf_op jit(solution)/shard_map/ppermute | solution.py:487
  59.0 2.0 %collective-permute-done.15.refs_3_ = f32[128,128]{1,0:T(8,128)S(1)} collective-permute-done((f32[128,128]{1,0:T(8,128)S(1)}, f32[128,128]{1,0:T(8,128)S(1)}, u32[]{:S(2)}, u32[]{:S(2)}) %collective-permute-start.15) | collective-permute-done | bytes 65568 | tf_op jit(solution)/shard_map/ppermute | solution.py:487
  62.7 3.4 %shard_map.58 = (f32[256,256]{1,0:T(8,128)S(1)}, f32[256,256]{1,0:T(8,128)S(1)}) custom-call(s32[16]{0:T(128)S(1)} %copy-done.2, f32[128,128]{1,0:T(8,128)S(1)} %add.35.refs_0_, f32[128,128]{1,0:T(8,128)S(1)} %collective-permute-done.13.refs_1_, f32[128,128]{1,0:T(8,128)S(1)} %collective-permute-done.14.refs_2_, ...), custom_call_target="tpu_custom_call" | custom-call | tf_op jit(solution)/shard_map/pallas_call | solution.py:52
  67.8 1.8 %shard_map.59 = (f32[1024,128]{1,0:T(8,128)S(1)}, f32[1024,128]{1,0:T(8,128)S(1)}, f32[1024,128]{1,0:T(8,128)S(1)}, f32[1024,128]{1,0:T(8,128)S(1)}, f32[256,128...) custom-call(s32[16]{0:T(128)S(1)} %copy-done.2, ...), custom_call_target="tpu_custom_call" | custom-call | tf_op jit(solution)/shard_map/pallas_call | solution.py:52
  69.5 3.5 %collective-permute-start.17 = (f32[1024,128]{1,0:T(8,128)S(1)}, f32[1024,128]{1,0:T(8,128)S(1)}, u32[]{:S(2)}, u32[]{:S(2)}) collective-permute-start(f32[1024,128]{1,0:T(8,128)S(1)} %get-tuple-element.117), channel_id=1, source_target_pairs={{8,0},{9,1},{10,2},{11,3},{12,4},{13,5},{14,6},{15,7},{0,8},{1,9},... | collective-permute-start | bytes 1572872 | tf_op jit(solution)/shard_map/ppermute | solution.py:487
  76.9 4.4 %collective-permute-start.20 = (f32[256,128]{1,0:T(8,128)S(1)}, f32[256,128]{1,0:T(8,128)S(1)}, u32[]{:S(2)}, u32[]{:S(2)}) collective-permute-start(f32[256,128]{1,0:T(8,128)S(1)} %get-tuple-element.127), channel_id=1, source_target_pairs={{8,0},{9,1},{10,2},{11,3},{12,4},{13,5},{14,6},{15,7},{0,8},{1,9},... | collective-permute-start | bytes 393224 | tf_op jit(solution)/shard_map/ppermute | solution.py:487
  82.6 3.2 %collective-permute-done.17.refs_0_ = f32[1024,128]{1,0:T(8,128)S(1)} collective-permute-done((f32[1024,128]{1,0:T(8,128)S(1)}, f32[1024,128]{1,0:T(8,128)S(1)}, u32[]{:S(2)}, u32[]{:S(2)}) %collective-permute-start.17) | collective-permute-done | bytes 524320 | tf_op jit(solution)/shard_map/ppermute | solution.py:487
  85.7 1.7 %shard_map.60 = (f32[128,128]{1,0:T(8,128)S(1)}, f32[128,128]{1,0:T(8,128)S(1)}, f32[1024,128]{1,0:T(8,128)S(1)}, f32[1024,128]{1,0:T(8,128)S(1)}) custom-call(s32[16]{0:T(128)S(1)} %copy-done.2, f32[1024,128]{1,0:T(8,128)S(1)} %collective-permute-done.17.refs_0_, f32[1024,128]{1,0:T(8,128)S(1)} %collective-permute-done.18.refs_1_, ...), custom_call_target="tpu_custom_call" | custom-call | tf_op jit(solution)/shard_map/pallas_call | solution.py:52
  89.7 2.0 %collective-permute-start.25 = (f32[128,128]{1,0:T(8,128)S(1)}, f32[128,128]{1,0:T(8,128)S(1)}, u32[]{:S(2)}, u32[]{:S(2)}) collective-permute-start(f32[128,128]{1,0:T(8,128)S(1)} %add.36.refs_0_), channel_id=1, source_target_pairs={{4,0},{5,1},{6,2},{7,3},{0,4},{1,5},{2,6},{3,7},{12,8},{13,9},{14,... | collective-permute-start | bytes 196616 | tf_op jit(solution)/shard_map/ppermute | solution.py:487
  93.1 2.3 %collective-permute-done.26.refs_3_ = f32[128,128]{1,0:T(8,128)S(1)} collective-permute-done((f32[128,128]{1,0:T(8,128)S(1)}, f32[128,128]{1,0:T(8,128)S(1)}, u32[]{:S(2)}, u32[]{:S(2)}) %collective-permute-start.26) | collective-permute-done | bytes 65568 | tf_op jit(solution)/shard_map/ppermute | solution.py:487
  96.2 3.1 %shard_map.62 = (f32[256,256]{1,0:T(8,128)S(1)}, f32[256,256]{1,0:T(8,128)S(1)}) custom-call(s32[16]{0:T(128)S(1)} %copy-done.2, f32[128,128]{1,0:T(8,128)S(1)} %add.36.refs_0_, f32[128,128]{1,0:T(8,128)S(1)} %collective-permute-done.24.refs_1_, f32[128,128]{1,0:T(8,128)S(1)} %collective-permute-done.25.refs_2_, ...), custom_call_target="tpu_custom_call" | custom-call | tf_op jit(solution)/shard_map/pallas_call | solution.py:52
  100.9 1.8 %shard_map.63 = (f32[1280,128]{1,0:T(8,128)S(1)}, f32[1280,128]{1,0:T(8,128)S(1)}, f32[1280,128]{1,0:T(8,128)S(1)}, f32[1280,128]{1,0:T(8,128)S(1)}, f32[1280,128]{1,0:T(8,128)S(1)}) custom-call(s32[16]{0:T(128)S(1)} %copy-done.2, f32[256,256]{1,0:T(8,128)S(1)} %get-tuple-element.133.own_ref.rotation_ref, f32[256,256]{1,0:T(8,128)S(1)} %collective-permute-done.27.other_ref, ...), custom_call_target="tpu_custom_call" | custom-call | tf_op jit(solution)/shard_map/pallas_call | solution.py:52
  102.7 4.8 %collective-permute-start.28 = (f32[1280,128]{1,0:T(8,128)S(1)}, f32[1280,128]{1,0:T(8,128)S(1)}, u32[]{:S(2)}, u32[]{:S(2)}) collective-permute-start(f32[1280,128]{1,0:T(8,128)S(1)} %get-tuple-element.140), channel_id=1, source_target_pairs={{8,0},{9,1},{10,2},{11,3},{12,4},{13,5},{14,6},{15,7},{0,8},{1,9},... | collective-permute-start | bytes 1966088 | tf_op jit(solution)/shard_map/ppermute | solution.py:487
  110.6 4.8 %collective-permute-start.31 = (f32[128,128]{1,0:T(8,128)S(1)}, f32[128,128]{1,0:T(8,128)S(1)}, u32[]{:S(2)}, u32[]{:S(2)}) collective-permute-start(f32[128,128]{1,0:T(8,128)S(1)} %get-tuple-element.144), channel_id=1, source_target_pairs={{1,0},{0,1},{3,2},{2,3},{5,4},{4,5},{7,6},{6,7},{9,8},{8,9},{11,10... | collective-permute-start | bytes 196616 | tf_op jit(solution)/shard_map/ppermute | solution.py:487
  115.4 7.1 %collective-permute-done.28.a_ref.refs_0_ = f32[1280,128]{1,0:T(8,128)S(1)} collective-permute-done((f32[1280,128]{1,0:T(8,128)S(1)}, f32[1280,128]{1,0:T(8,128)S(1)}, u32[]{:S(2)}, u32[]{:S(2)}) %collective-permute-start.28) | collective-permute-done | bytes 655392 | tf_op jit(solution)/shard_map/ppermute | solution.py:487
  123.2 1.7 %shard_map.66 = (f32[128,128]{1,0:T(8,128)S(1)}, f32[128,128]{1,0:T(8,128)S(1)}, f32[1280,128]{1,0:T(8,128)S(1)}, f32[1280,128]{1,0:T(8,128)S(1)}) custom-call(s32[16]{0:T(128)S(1)} %copy-done.2, f32[1280,128]{1,0:T(8,128)S(1)} %collective-permute-done.28.a_ref.refs_0_, f32[1280,128]{1,0:T(8,128)S(1)} %collective-permute-done.29.b_ref.refs_1_, ...), custom_call_target="tpu_custom_call" | custom-call | tf_op jit(solution)/shard_map/pallas_call | solution.py:52
  126.2 2.6 %collective-permute-start.36 = (f32[128,128]{1,0:T(8,128)S(1)}, f32[128,128]{1,0:T(8,128)S(1)}, u32[]{:S(2)}, u32[]{:S(2)}) collective-permute-start(f32[128,128]{1,0:T(8,128)S(1)} %add.37.refs_0_), channel_id=1, source_target_pairs={{6,0},{7,1},{4,2},{5,3},{2,4},{3,5},{0,6},{1,7},{14,8},{15,9},{12,... | collective-permute-start | bytes 196616 | tf_op jit(solution)/shard_map/ppermute | solution.py:487
  129.5 4.8 %collective-permute-done.36.refs_3_ = f32[128,128]{1,0:T(8,128)S(1)} collective-permute-done((f32[128,128]{1,0:T(8,128)S(1)}, f32[128,128]{1,0:T(8,128)S(1)}, u32[]{:S(2)}, u32[]{:S(2)}) %collective-permute-start.36) | collective-permute-done | bytes 65568 | tf_op jit(solution)/shard_map/ppermute | solution.py:487
  135.8 3.2 %collective-permute-done.34.refs_1_ = f32[128,128]{1,0:T(8,128)S(1)} collective-permute-done((f32[128,128]{1,0:T(8,128)S(1)}, f32[128,128]{1,0:T(8,128)S(1)}, u32[]{:S(2)}, u32[]{:S(2)}) %collective-permute-start.34) | collective-permute-done | bytes 65568 | tf_op jit(solution)/shard_map/ppermute | solution.py:487
  138.9 3.4 %shard_map.68 = (f32[264,256]{1,0:T(8,128)S(1)}, f32[256,256]{1,0:T(8,128)}) custom-call(s32[16]{0:T(128)S(1)} %copy-done.2, f32[128,128]{1,0:T(8,128)S(1)} %add.37.refs_0_, f32[128,128]{1,0:T(8,128)S(1)} %collective-permute-done.34.refs_1_, f32[128,128]{1,0:T(8,128)S(1)} %collective-permute-done.35.refs_2_, f32[128,128]{1,0:T(8,128)S(1)} %collective-permute-done.36.refs_3_, ...), custom_call_target="tpu_custom_call" | custom-call | tf_op jit(solution)/shard_map/pallas_call | solution.py:52
  144.7 3.4 %shard_map.69 = (f32[2048,256]{1,0:T(8,128)}, f32[512,256]{1,0:T(8,128)}, f32[1,256]{1,0:T(1,128)}) custom-call(s32[16]{0:T(128)S(1)} %copy-done.2, f32[264,256]{1,0:T(8,128)S(1)} %get-tuple-element.158.refs_0_, f32[264,256]{1,0:T(8,128)S(1)} %collective-permute-done.38.refs_1_, f32[1280,128]{1,0:T(8,128)S(1)} %get-tuple-element.159.refs_2_, ...), custom_call_target="tpu_custom_call" | custom-call | tf_op jit(solution)/shard_map/pallas_call | solution.py:454
  (83 shorter events, 42.9 us)
Async XLA Ops:
  5.0 27.6 %collective-permute-start.4 = (f32[768,256]{1,0:T(8,128)}, f32[768,256]{1,0:T(8,128)S(1)}, u32[]{:S(2)}, u32[]{:S(2)}) collective-permute-start(f32[768,256]{1,0:T(8,128)} %get-tuple-element.90), channel_id=1, source_target_pairs={{4,0},{5,1},{6,2},{7,3},{0,4},{1,5},{2,6},{3,7},{12,8},{13,9},{14,... | collective-permute-start | bytes 2359304 | tf_op jit(solution)/shard_map/ppermute | solution.py:487
  12.9 7.0 %collective-permute-start.1 = (f32[384,128]{1,0:T(8,128)S(1)}, f32[384,128]{1,0:T(8,128)S(1)}, u32[]{:S(2)}, u32[]{:S(2)}) collective-permute-start(f32[384,128]{1,0:T(8,128)S(1)} %add.34.own_ref), channel_id=1, source_target_pairs={{2,0},{3,1},{0,2},{1,3},{6,4},{7,5},{4,6},{5,7},{10,8},{11,9},{8,1... | collective-permute-start | bytes 589832 | tf_op jit(solution)/shard_map/ppermute | solution.py:487
  23.3 9.3 %collective-permute-start.3 = (f32[256,256]{1,0:T(8,128)S(1)}, f32[256,256]{1,0:T(8,128)S(1)}, u32[]{:S(2)}, u32[]{:S(2)}) collective-permute-start(f32[256,256]{1,0:T(8,128)S(1)} %get-tuple-element.85.rotation_ref.own_ref), channel_id=1, source_target_pairs={{4,0},{5,1},{6,2},{7,3},{0,4},{1,5},{2,6},{3,7},{12,8},{13,9},{14,... | collective-permute-start | bytes 786440 | tf_op jit(solution)/shard_map/ppermute | solution.py:487
  24.8 23.9 %collective-permute-start.2 = (f32[1024,128]{1,0:T(8,128)S(1)}, f32[1024,128]{1,0:T(8,128)S(1)}, u32[]{:S(2)}, u32[]{:S(2)}) collective-permute-start(f32[1024,128]{1,0:T(8,128)S(1)} %get-tuple-element.89.refs_1_), channel_id=1, source_target_pairs={{8,0},{9,1},{10,2},{11,3},{16,8},{17,9},{18,10},{19,11},{4,12},{5,... | collective-permute-start | bytes 1572872 | tf_op jit(solution)/shard_map/ppermute | solution.py:487
  26.1 12.7 %collective-permute-start.6 = (f32[256,256]{1,0:T(8,128)S(1)}, f32[256,256]{1,0:T(8,128)S(1)}, u32[]{:S(2)}, u32[]{:S(2)}) collective-permute-start(f32[256,256]{1,0:T(8,128)S(1)} %copy-done.3), channel_id=1, source_target_pairs={{4,0},{5,1},{6,2},{7,3},{0,4},{1,5},{2,6},{3,7},{12,8},{13,9},{14,... | collective-permute-start | bytes 786440 | tf_op jit(solution)/shard_map/ppermute | solution.py:487
  33.6 15.1 %collective-permute-start.5 = (f32[768,128]{1,0:T(8,128)S(1)}, f32[768,128]{1,0:T(8,128)S(1)}, u32[]{:S(2)}, u32[]{:S(2)}) collective-permute-start(f32[768,128]{1,0:T(8,128)S(1)} %get-tuple-element.92.refs_4_), channel_id=1, source_target_pairs={{12,4},{13,5},{14,6},{15,7},{0,8},{1,9},{2,10},{3,11},{20,12},{21,... | collective-permute-start | bytes 1179656 | tf_op jit(solution)/shard_map/ppermute | solution.py:487
  38.8 5.3 %collective-permute-start.8 = (f32[128,128]{1,0:T(8,128)S(1)}, f32[128,128]{1,0:T(8,128)S(1)}, u32[]{:S(2)}, u32[]{:S(2)}) collective-permute-start(f32[128,128]{1,0:T(8,128)S(1)} %get-tuple-element.101), channel_id=1, source_target_pairs={{4,0},{0,1},{6,2},{2,3},{5,4},{1,5},{7,6},{3,7},{12,8},{8,9},{14,1... | collective-permute-start | bytes 196616 | tf_op jit(solution)/shard_map/ppermute | solution.py:487
  39.7 8.4 %collective-permute-start.7 = (f32[256,128]{1,0:T(8,128)S(1)}, f32[256,128]{1,0:T(8,128)S(1)}, u32[]{:S(2)}, u32[]{:S(2)}) collective-permute-start(f32[256,128]{1,0:T(8,128)S(1)} %get-tuple-element.95.refs_7_), channel_id=1, source_target_pairs={{12,4},{13,5},{14,6},{15,7},{0,8},{1,9},{2,10},{3,11},{20,12},{21,... | collective-permute-start | bytes 393224 | tf_op jit(solution)/shard_map/ppermute | solution.py:487
  44.1 6.4 %collective-permute-start.9 = (f32[256,128]{1,0:T(8,128)S(1)}, f32[256,128]{1,0:T(8,128)S(1)}, u32[]{:S(2)}, u32[]{:S(2)}) collective-permute-start(f32[256,128]{1,0:T(8,128)S(1)} %get-tuple-element.102), channel_id=1, source_target_pairs={{8,0},{9,1},{10,2},{11,3},{12,4},{13,5},{14,6},{15,7},{0,8},{1,9},... | collective-permute-start | bytes 393224 | tf_op jit(solution)/shard_map/ppermute | solution.py:487
  45.8 4.8 %collective-permute-start.10 = (f32[256,128]{1,0:T(8,128)S(1)}, f32[256,128]{1,0:T(8,128)S(1)}, u32[]{:S(2)}, u32[]{:S(2)}) collective-permute-start(f32[256,128]{1,0:T(8,128)S(1)} %get-tuple-element.103), channel_id=1, source_target_pairs={{0,0},{1,1},{2,2},{3,3},{4,4},{5,5},{6,6},{7,7},{16,8},{17,9},{18,... | collective-permute-start | bytes 393224 | tf_op jit(solution)/shard_map/ppermute | solution.py:487
  50.6 4.8 %collective-permute-start.12 = (f32[128,128]{1,0:T(8,128)S(1)}, f32[128,128]{1,0:T(8,128)S(1)}, u32[]{:S(2)}, u32[]{:S(2)}) collective-permute-start(f32[128,128]{1,0:T(8,128)S(1)} %get-tuple-element.105), channel_id=1, source_target_pairs={{1,0},{0,1},{3,2},{2,3},{5,4},{4,5},{7,6},{6,7},{9,8},{8,9},{11,10... | collective-permute-start | bytes 196616 | tf_op jit(solution)/shard_map/ppermute | solution.py:487
  55.4 5.6 %collective-permute-start.15 = (f32[128,128]{1,0:T(8,128)S(1)}, f32[128,128]{1,0:T(8,128)S(1)}, u32[]{:S(2)}, u32[]{:S(2)}) collective-permute-start(f32[128,128]{1,0:T(8,128)S(1)} %add.35.refs_0_), channel_id=1, source_target_pairs={{6,0},{7,1},{4,2},{5,3},{2,4},{3,5},{0,6},{1,7},{14,8},{15,9},{12,... | collective-permute-start | bytes 196616 | tf_op jit(solution)/shard_map/ppermute | solution.py:487
  58.1 4.3 %collective-permute-start.14 = (f32[128,128]{1,0:T(8,128)S(1)}, f32[128,128]{1,0:T(8,128)S(1)}, u32[]{:S(2)}, u32[]{:S(2)}) collective-permute-start(f32[128,128]{1,0:T(8,128)S(1)} %add.35.refs_0_), channel_id=1, source_target_pairs={{4,0},{5,1},{6,2},{7,3},{0,4},{1,5},{2,6},{3,7},{12,8},{13,9},{14,... | collective-permute-start | bytes 196616 | tf_op jit(solution)/shard_map/ppermute | solution.py:487
  58.4 4.3 %collective-permute-start.13 = (f32[128,128]{1,0:T(8,128)S(1)}, f32[128,128]{1,0:T(8,128)S(1)}, u32[]{:S(2)}, u32[]{:S(2)}) collective-permute-start(f32[128,128]{1,0:T(8,128)S(1)} %add.35.refs_0_), channel_id=1, source_target_pairs={{2,0},{3,1},{0,2},{1,3},{6,4},{7,5},{4,6},{5,7},{10,8},{11,9},{8,1... | collective-permute-start | bytes 196616 | tf_op jit(solution)/shard_map/ppermute | solution.py:487
  69.5 16.2 %collective-permute-start.17 = (f32[1024,128]{1,0:T(8,128)S(1)}, f32[1024,128]{1,0:T(8,128)S(1)}, u32[]{:S(2)}, u32[]{:S(2)}) collective-permute-start(f32[1024,128]{1,0:T(8,128)S(1)} %get-tuple-element.117), channel_id=1, source_target_pairs={{8,0},{9,1},{10,2},{11,3},{12,4},{13,5},{14,6},{15,7},{0,8},{1,9},... | collective-permute-start | bytes 1572872 | tf_op jit(solution)/shard_map/ppermute | solution.py:487
  73.0 12.7 %collective-permute-start.18 = (f32[1024,128]{1,0:T(8,128)S(1)}, f32[1024,128]{1,0:T(8,128)S(1)}, u32[]{:S(2)}, u32[]{:S(2)}) collective-permute-start(f32[1024,128]{1,0:T(8,128)S(1)} %get-tuple-element.118), channel_id=1, source_target_pairs={{0,0},{1,1},{2,2},{3,3},{4,4},{5,5},{6,6},{7,7},{16,8},{17,9},{18,... | collective-permute-start | bytes 1572872 | tf_op jit(solution)/shard_map/ppermute | solution.py:487
  76.9 11.2 %collective-permute-start.20 = (f32[256,128]{1,0:T(8,128)S(1)}, f32[256,128]{1,0:T(8,128)S(1)}, u32[]{:S(2)}, u32[]{:S(2)}) collective-permute-start(f32[256,128]{1,0:T(8,128)S(1)} %get-tuple-element.127), channel_id=1, source_target_pairs={{8,0},{9,1},{10,2},{11,3},{12,4},{13,5},{14,6},{15,7},{0,8},{1,9},... | collective-permute-start | bytes 393224 | tf_op jit(solution)/shard_map/ppermute | solution.py:487
  81.2 6.8 %collective-permute-start.21 = (f32[256,128]{1,0:T(8,128)S(1)}, f32[256,128]{1,0:T(8,128)S(1)}, u32[]{:S(2)}, u32[]{:S(2)}) collective-permute-start(f32[256,128]{1,0:T(8,128)S(1)} %get-tuple-element.128), channel_id=1, source_target_pairs={{0,0},{1,1},{2,2},{3,3},{4,4},{5,5},{6,6},{7,7},{16,8},{17,9},{18,... | collective-permute-start | bytes 393224 | tf_op jit(solution)/shard_map/ppermute | solution.py:487
  81.9 5.5 %collective-permute-start.22 = (f32[128,128]{1,0:T(8,128)S(1)}, f32[128,128]{1,0:T(8,128)S(1)}, u32[]{:S(2)}, u32[]{:S(2)}) collective-permute-start(f32[128,128]{1,0:T(8,128)S(1)} %get-tuple-element.129), channel_id=1, source_target_pairs={{0,0},{8,1},{2,2},{10,3},{4,4},{12,5},{6,6},{14,7},{1,8},{16,9},{3... | collective-permute-start | bytes 196616 | tf_op jit(solution)/shard_map/ppermute | solution.py:487
  89.5 5.9 %collective-permute-start.26 = (f32[128,128]{1,0:T(8,128)S(1)}, f32[128,128]{1,0:T(8,128)S(1)}, u32[]{:S(2)}, u32[]{:S(2)}) collective-permute-start(f32[128,128]{1,0:T(8,128)S(1)} %add.36.refs_0_), channel_id=1, source_target_pairs={{6,0},{7,1},{4,2},{5,3},{2,4},{3,5},{0,6},{1,7},{14,8},{15,9},{12,... | collective-permute-start | bytes 196616 | tf_op jit(solution)/shard_map/ppermute | solution.py:487
  89.7 5.8 %collective-permute-start.25 = (f32[128,128]{1,0:T(8,128)S(1)}, f32[128,128]{1,0:T(8,128)S(1)}, u32[]{:S(2)}, u32[]{:S(2)}) collective-permute-start(f32[128,128]{1,0:T(8,128)S(1)} %add.36.refs_0_), channel_id=1, source_target_pairs={{4,0},{5,1},{6,2},{7,3},{0,4},{1,5},{2,6},{3,7},{12,8},{13,9},{14,... | collective-permute-start | bytes 196616 | tf_op jit(solution)/shard_map/ppermute | solution.py:487
  91.8 4.4 %collective-permute-start.24 = (f32[128,128]{1,0:T(8,128)S(1)}, f32[128,128]{1,0:T(8,128)S(1)}, u32[]{:S(2)}, u32[]{:S(2)}) collective-permute-start(f32[128,128]{1,0:T(8,128)S(1)} %add.36.refs_0_), channel_id=1, source_target_pairs={{2,0},{3,1},{0,2},{1,3},{6,4},{7,5},{4,6},{5,7},{10,8},{11,9},{8,1... | collective-permute-start | bytes 196616 | tf_op jit(solution)/shard_map/ppermute | solution.py:487
  102.7 19.9 %collective-permute-start.28 = (f32[1280,128]{1,0:T(8,128)S(1)}, f32[1280,128]{1,0:T(8,128)S(1)}, u32[]{:S(2)}, u32[]{:S(2)}) collective-permute-start(f32[1280,128]{1,0:T(8,128)S(1)} %get-tuple-element.140), channel_id=1, source_target_pairs={{8,0},{9,1},{10,2},{11,3},{12,4},{13,5},{14,6},{15,7},{0,8},{1,9},... | collective-permute-start | bytes 1966088 | tf_op jit(solution)/shard_map/ppermute | solution.py:487
  107.5 15.0 %collective-permute-start.29 = (f32[1280,128]{1,0:T(8,128)S(1)}, f32[1280,128]{1,0:T(8,128)S(1)}, u32[]{:S(2)}, u32[]{:S(2)}) collective-permute-start(f32[1280,128]{1,0:T(8,128)S(1)} %get-tuple-element.141), channel_id=1, source_target_pairs={{0,0},{1,1},{2,2},{3,3},{4,4},{5,5},{6,6},{7,7},{16,8},{17,9},{18,... | collective-permute-start | bytes 1966088 | tf_op jit(solution)/shard_map/ppermute | solution.py:487
  108.2 16.7 %collective-permute-start.32 = (f32[1280,128]{1,0:T(8,128)S(1)}, f32[1280,128]{1,0:T(8,128)S(1)}, u32[]{:S(2)}, u32[]{:S(2)}) collective-permute-start(f32[1280,128]{1,0:T(8,128)S(1)} %get-tuple-element.151), channel_id=1, source_target_pairs={{4,0},{5,1},{6,2},{7,3},{0,4},{1,5},{2,6},{3,7},{12,8},{13,9},{14,... | collective-permute-start | bytes 1966088 | tf_op jit(solution)/shard_map/ppermute | solution.py:487
  109.9 13.2 %collective-permute-start.30 = (f32[128,128]{1,0:T(8,128)S(1)}, f32[128,128]{1,0:T(8,128)S(1)}, u32[]{:S(2)}, u32[]{:S(2)}) collective-permute-start(f32[128,128]{1,0:T(8,128)S(1)} %get-tuple-element.143), channel_id=1, source_target_pairs={{0,0},{8,1},{2,2},{10,3},{4,4},{12,5},{6,6},{14,7},{1,8},{16,9},{3... | collective-permute-start | bytes 196616 | tf_op jit(solution)/shard_map/ppermute | solution.py:487
  110.6 12.5 %collective-permute-start.31 = (f32[128,128]{1,0:T(8,128)S(1)}, f32[128,128]{1,0:T(8,128)S(1)}, u32[]{:S(2)}, u32[]{:S(2)}) collective-permute-start(f32[128,128]{1,0:T(8,128)S(1)} %get-tuple-element.144), channel_id=1, source_target_pairs={{1,0},{0,1},{3,2},{2,3},{5,4},{4,5},{7,6},{6,7},{9,8},{8,9},{11,10... | collective-permute-start | bytes 196616 | tf_op jit(solution)/shard_map/ppermute | solution.py:487
  123.1 11.2 %collective-permute-start.37 = (f32[512,128]{1,0:T(8,128)S(1)}, f32[512,128]{1,0:T(8,128)S(1)}, u32[]{:S(2)}, u32[]{:S(2)}) collective-permute-start(f32[512,128]{1,0:T(8,128)S(1)} %shard_map.64), channel_id=1, source_target_pairs={{4,0},{5,1},{6,2},{7,3},{0,4},{1,5},{2,6},{3,7},{12,8},{13,9},{14,... | collective-permute-start | bytes 786440 | tf_op jit(solution)/shard_map/ppermute | solution.py:487
  126.2 8.0 %collective-permute-start.36 = (f32[128,128]{1,0:T(8,128)S(1)}, f32[128,128]{1,0:T(8,128)S(1)}, u32[]{:S(2)}, u32[]{:S(2)}) collective-permute-start(f32[128,128]{1,0:T(8,128)S(1)} %add.37.refs_0_), channel_id=1, source_target_pairs={{6,0},{7,1},{4,2},{5,3},{2,4},{3,5},{0,6},{1,7},{14,8},{15,9},{12,... | collective-permute-start | bytes 196616 | tf_op jit(solution)/shard_map/ppermute | solution.py:487
  128.8 5.5 %collective-permute-start.35 = (f32[128,128]{1,0:T(8,128)S(1)}, f32[128,128]{1,0:T(8,128)S(1)}, u32[]{:S(2)}, u32[]{:S(2)}) collective-permute-start(f32[128,128]{1,0:T(8,128)S(1)} %add.37.refs_0_), channel_id=1, source_target_pairs={{4,0},{5,1},{6,2},{7,3},{0,4},{1,5},{2,6},{3,7},{12,8},{13,9},{14,... | collective-permute-start | bytes 196616 | tf_op jit(solution)/shard_map/ppermute | solution.py:487
  134.4 10.3 %collective-permute-start.39 = (f32[768,128]{1,0:T(8,128)S(1)}, f32[768,128]{1,0:T(8,128)S(1)}, u32[]{:S(2)}, u32[]{:S(2)}) collective-permute-start(f32[768,128]{1,0:T(8,128)S(1)} %shard_map.67), channel_id=1, source_target_pairs={{4,0},{5,1},{6,2},{7,3},{0,4},{1,5},{2,6},{3,7},{12,8},{13,9},{14,... | collective-permute-start | bytes 1179656 | tf_op jit(solution)/shard_map/ppermute | solution.py:487
  134.7 4.3 %collective-permute-start.34 = (f32[128,128]{1,0:T(8,128)S(1)}, f32[128,128]{1,0:T(8,128)S(1)}, u32[]{:S(2)}, u32[]{:S(2)}) collective-permute-start(f32[128,128]{1,0:T(8,128)S(1)} %add.37.refs_0_), channel_id=1, source_target_pairs={{2,0},{3,1},{0,2},{1,3},{6,4},{7,5},{4,6},{5,7},{10,8},{11,9},{8,1... | collective-permute-start | bytes 196616 | tf_op jit(solution)/shard_map/ppermute | solution.py:487
  (12 other events, 36.3 us)

commit v8 on v7

--- a/solution.py
+++ b/solution.py
@@ -592,7 +592,7 @@
             diagonals = [pass_diagonal(leave), exchange(stay, 0, 1)]
             if last_move:
                 native = exchange(vectors.pop(), 1, 0)
-                top = part // 2
+                top = part * 3 // 4
                 top_give = give(facts, got, 0, top, half)
                 *got, top_give, diagonals[0], diagonals[1] = together(
                     *got, top_give, *diagonals
@@ -616,9 +616,7 @@
         parts = [own, exchange(own, 0, 2), exchange(own, 1, 0), exchange(own, 1, 2)]
         if last_move:
             rest_give = give(facts, got, top, part + vector_rows, half)
-            parts[2], parts[3], got_top, rest_give = together(
-                *parts[2:], got_top, rest_give
-            )
+            *parts, got_top, rest_give = together(*parts, got_top, rest_give)
             got_rest = exchange(rest_give, 1, 0)
         rotation, gram = later_rotation(facts, parts, diagonals, half, last_move)
     packs = [rotation, exchange(rotation, 0, 1)]

time: 150 us -> 155 us (1.033)
  waiting for transfers between devices: 46.4 us -> 51.2 us
    ppermute x40, waiting for transfers between devices: 46.4 us -> 51.2 us  [permute(): return lax.ppermute(block, ('pair', 'row'), moves)]
  transfers between devices with their start and end apart: 40 -> 40, of which waited for: 24 -> 22; matrix products, arithmetic and copies ran while one was open for 0% -> 0% of each run, Pallas kernels for 17% -> 14%
where the time goes in v8:
time: 155 us; the launch traced here: 153 us
  starting transfers between devices  57.4 us (37%)
  waiting for transfers between devices  51.2 us (33%)
  Pallas kernels  41.1 us (27%)
  local copies, waits for them, and re-layouts  2.12 us (1%)
    ppermute x40, starting transfers between devices, permute(): return lax.ppermute(block, ('pair', 'row'), moves)  57.4 us
    ppermute x40, waiting for transfers between devices, permute(): return lax.ppermute(block, ('pair', 'row'), moves)  51.2 us
    pallas_call x19, Pallas kernels, call(): pl.pallas_call(body, out_shape=outs, in_specs=[pl.BlockSpec(memory_space=...  34.7 us
    pallas_call x1, Pallas kernels, finish(): pl.pallas_call(body, out_shape=(shape(2 * part, size), shape(2 * vector_r...  3.58 us
  transfers between devices with their start and end apart: 40, of which 22 were waited for; matrix products, arithmetic and copies ran while one was open for 0% of the time, Pallas kernels for 14%

profile of v8, /device:TPU:0, one launch (start us, length us, event | category | flops | bytes accessed | tf_op | source)
XLA Modules:
  0.0 153.2 jit_solution(3745751497497121887)
XLA Ops:
  2.2 2.8 %shard_map.52 = (f32[768,256]{1,0:T(8,128)}, f32[256,256]{1,0:T(8,128)}) custom-call(s32[16]{0:T(128)} %copy-done.1, f32[2048,256]{1,0:T(8,128)} %x_ref.5), custom_call_target="tpu_custom_call" | custom-call | tf_op jit(solution)/shard_map/pallas_call | solution.py:95
  5.0 3.0 %collective-permute-start.4 = (f32[768,256]{1,0:T(8,128)}, f32[768,256]{1,0:T(8,128)S(1)}, u32[]{:S(2)}, u32[]{:S(2)}) collective-permute-start(f32[768,256]{1,0:T(8,128)} %get-tuple-element.92), channel_id=1, source_target_pairs={{4,0},{5,1},{6,2},{7,3},{0,4},{1,5},{2,6},{3,7},{12,8},{13,9},{14,... | collective-permute-start | bytes 2359304 | tf_op jit(solution)/shard_map/ppermute | solution.py:487
  8.7 2.6 %shard_map.49 = f32[384,128]{1,0:T(8,128)S(1)} custom-call(s32[16]{0:T(128)S(1)} %copy-done.2, f32[2048,256]{1,0:T(8,128)S(1)} %copy-done), custom_call_target="tpu_custom_call" | custom-call | tf_op jit(solution)/shard_map/pallas_call | solution.py:52
  14.4 5.4 %collective-permute-done.1.other_ref = f32[384,128]{1,0:T(8,128)S(1)} collective-permute-done((f32[384,128]{1,0:T(8,128)S(1)}, f32[384,128]{1,0:T(8,128)S(1)}, u32[]{:S(2)}, u32[]{:S(2)}) %collective-permute-start.1) | collective-permute-done | bytes 196640 | tf_op jit(solution)/shard_map/ppermute | solution.py:487
  19.9 3.4 %shard_map.50 = (f32[256,256]{1,0:T(8,128)S(1)}, f32[256,256]{1,0:T(8,128)S(1)}) custom-call(s32[16]{0:T(128)S(1)} %copy-done.2, f32[384,128]{1,0:T(8,128)S(1)} %add.34.own_ref, f32[384,128]{1,0:T(8,128)S(1)} %collective-permute-done.1.other_ref), custom_call_target="tpu_custom_call" | custom-call | tf_op jit(solution)/shard_map/pallas_call | solution.py:52
  26.1 4.0 %collective-permute-start.6 = (f32[256,256]{1,0:T(8,128)S(1)}, f32[256,256]{1,0:T(8,128)S(1)}, u32[]{:S(2)}, u32[]{:S(2)}) collective-permute-start(f32[256,256]{1,0:T(8,128)S(1)} %copy-done.3), channel_id=1, source_target_pairs={{4,0},{5,1},{6,2},{7,3},{0,4},{1,5},{2,6},{3,7},{12,8},{13,9},{14,... | collective-permute-start | bytes 786440 | tf_op jit(solution)/shard_map/ppermute | solution.py:487
  30.1 2.5 %collective-permute-done.3.rotation_ref.other_ref = f32[256,256]{1,0:T(8,128)S(1)} collective-permute-done((f32[256,256]{1,0:T(8,128)S(1)}, f32[256,256]{1,0:T(8,128)S(1)}, u32[]{:S(2)}, u32[]{:S(2)}) %collective-permute-start.3) | collective-permute-done | bytes 262176 | tf_op jit(solution)/shard_map/ppermute | solution.py:487
  33.6 3.5 %collective-permute-start.5 = (f32[768,128]{1,0:T(8,128)S(1)}, f32[768,128]{1,0:T(8,128)S(1)}, u32[]{:S(2)}, u32[]{:S(2)}) collective-permute-start(f32[768,128]{1,0:T(8,128)S(1)} %get-tuple-element.94.refs_4_), channel_id=1, source_target_pairs={{12,4},{13,5},{14,6},{15,7},{0,8},{1,9},{2,10},{3,11},{20,12},{21,... | collective-permute-start | bytes 1179656 | tf_op jit(solution)/shard_map/ppermute | solution.py:487
  39.7 3.5 %collective-permute-start.7 = (f32[256,128]{1,0:T(8,128)S(1)}, f32[256,128]{1,0:T(8,128)S(1)}, u32[]{:S(2)}, u32[]{:S(2)}) collective-permute-start(f32[256,128]{1,0:T(8,128)S(1)} %get-tuple-element.97.refs_7_), channel_id=1, source_target_pairs={{12,4},{13,5},{14,6},{15,7},{0,8},{1,9},{2,10},{3,11},{20,12},{21,... | collective-permute-start | bytes 393224 | tf_op jit(solution)/shard_map/ppermute | solution.py:487
  48.7 1.8 %shard_map.55 = (f32[128,128]{1,0:T(8,128)S(1)}, f32[128,128]{1,0:T(8,128)S(1)}, f32[1024,128]{1,0:T(8,128)S(1)}, f32[1024,128]{1,0:T(8,128)S(1)}, f32[1024,128]{1,0:T(8,128)S(1)}, /*index=5*/f32[1024,128]{1,0:T(8,128)S(1)}) custom-call(s32[16]{0:T(128)S(1)} %copy-done.2, f32[1024,128]{1,0:T(8,128)S(1)} %get-tuple-element.88.refs_0_, ...), custom_call_target="tpu_custom_call" | custom-call | tf_op jit(solution)/shard_map/pallas_call | solution.py:52
  50.6 3.9 %collective-permute-start.12 = (f32[128,128]{1,0:T(8,128)S(1)}, f32[128,128]{1,0:T(8,128)S(1)}, u32[]{:S(2)}, u32[]{:S(2)}) collective-permute-start(f32[128,128]{1,0:T(8,128)S(1)} %get-tuple-element.107), channel_id=1, source_target_pairs={{1,0},{0,1},{3,2},{2,3},{5,4},{4,5},{7,6},{6,7},{9,8},{8,9},{11,10... | collective-permute-start | bytes 196616 | tf_op jit(solution)/shard_map/ppermute | solution.py:487
  55.4 2.7 %collective-permute-start.15 = (f32[128,128]{1,0:T(8,128)S(1)}, f32[128,128]{1,0:T(8,128)S(1)}, u32[]{:S(2)}, u32[]{:S(2)}) collective-permute-start(f32[128,128]{1,0:T(8,128)S(1)} %add.35.refs_0_), channel_id=1, source_target_pairs={{6,0},{7,1},{4,2},{5,3},{2,4},{3,5},{0,6},{1,7},{14,8},{15,9},{12,... | collective-permute-start | bytes 196616 | tf_op jit(solution)/shard_map/ppermute | solution.py:487
  59.0 2.0 %collective-permute-done.15.refs_3_ = f32[128,128]{1,0:T(8,128)S(1)} collective-permute-done((f32[128,128]{1,0:T(8,128)S(1)}, f32[128,128]{1,0:T(8,128)S(1)}, u32[]{:S(2)}, u32[]{:S(2)}) %collective-permute-start.15) | collective-permute-done | bytes 65568 | tf_op jit(solution)/shard_map/ppermute | solution.py:487
  62.7 3.4 %shard_map.58 = (f32[256,256]{1,0:T(8,128)S(1)}, f32[256,256]{1,0:T(8,128)S(1)}) custom-call(s32[16]{0:T(128)S(1)} %copy-done.2, f32[128,128]{1,0:T(8,128)S(1)} %add.35.refs_0_, f32[128,128]{1,0:T(8,128)S(1)} %collective-permute-done.13.refs_1_, f32[128,128]{1,0:T(8,128)S(1)} %collective-permute-done.14.refs_2_, ...), custom_call_target="tpu_custom_call" | custom-call | tf_op jit(solution)/shard_map/pallas_call | solution.py:52
  67.8 1.8 %shard_map.59 = (f32[1024,128]{1,0:T(8,128)S(1)}, f32[1024,128]{1,0:T(8,128)S(1)}, f32[1024,128]{1,0:T(8,128)S(1)}, f32[1024,128]{1,0:T(8,128)S(1)}, f32[256,128...) custom-call(s32[16]{0:T(128)S(1)} %copy-done.2, ...), custom_call_target="tpu_custom_call" | custom-call | tf_op jit(solution)/shard_map/pallas_call | solution.py:52
  69.5 3.5 %collective-permute-start.17 = (f32[1024,128]{1,0:T(8,128)S(1)}, f32[1024,128]{1,0:T(8,128)S(1)}, u32[]{:S(2)}, u32[]{:S(2)}) collective-permute-start(f32[1024,128]{1,0:T(8,128)S(1)} %get-tuple-element.119), channel_id=1, source_target_pairs={{8,0},{9,1},{10,2},{11,3},{12,4},{13,5},{14,6},{15,7},{0,8},{1,9},... | collective-permute-start | bytes 1572872 | tf_op jit(solution)/shard_map/ppermute | solution.py:487
  76.9 4.4 %collective-permute-start.20 = (f32[256,128]{1,0:T(8,128)S(1)}, f32[256,128]{1,0:T(8,128)S(1)}, u32[]{:S(2)}, u32[]{:S(2)}) collective-permute-start(f32[256,128]{1,0:T(8,128)S(1)} %get-tuple-element.129), channel_id=1, source_target_pairs={{8,0},{9,1},{10,2},{11,3},{12,4},{13,5},{14,6},{15,7},{0,8},{1,9},... | collective-permute-start | bytes 393224 | tf_op jit(solution)/shard_map/ppermute | solution.py:487
  82.6 3.2 %collective-permute-done.17.refs_0_ = f32[1024,128]{1,0:T(8,128)S(1)} collective-permute-done((f32[1024,128]{1,0:T(8,128)S(1)}, f32[1024,128]{1,0:T(8,128)S(1)}, u32[]{:S(2)}, u32[]{:S(2)}) %collective-permute-start.17) | collective-permute-done | bytes 524320 | tf_op jit(solution)/shard_map/ppermute | solution.py:487
  85.7 1.7 %shard_map.60 = (f32[128,128]{1,0:T(8,128)S(1)}, f32[128,128]{1,0:T(8,128)S(1)}, f32[1024,128]{1,0:T(8,128)S(1)}, f32[1024,128]{1,0:T(8,128)S(1)}) custom-call(s32[16]{0:T(128)S(1)} %copy-done.2, f32[1024,128]{1,0:T(8,128)S(1)} %collective-permute-done.17.refs_0_, f32[1024,128]{1,0:T(8,128)S(1)} %collective-permute-done.18.refs_1_, ...), custom_call_target="tpu_custom_call" | custom-call | tf_op jit(solution)/shard_map/pallas_call | solution.py:52
  89.7 2.0 %collective-permute-start.25 = (f32[128,128]{1,0:T(8,128)S(1)}, f32[128,128]{1,0:T(8,128)S(1)}, u32[]{:S(2)}, u32[]{:S(2)}) collective-permute-start(f32[128,128]{1,0:T(8,128)S(1)} %add.36.refs_0_), channel_id=1, source_target_pairs={{4,0},{5,1},{6,2},{7,3},{0,4},{1,5},{2,6},{3,7},{12,8},{13,9},{14,... | collective-permute-start | bytes 196616 | tf_op jit(solution)/shard_map/ppermute | solution.py:487
  93.1 2.3 %collective-permute-done.26.refs_3_ = f32[128,128]{1,0:T(8,128)S(1)} collective-permute-done((f32[128,128]{1,0:T(8,128)S(1)}, f32[128,128]{1,0:T(8,128)S(1)}, u32[]{:S(2)}, u32[]{:S(2)}) %collective-permute-start.26) | collective-permute-done | bytes 65568 | tf_op jit(solution)/shard_map/ppermute | solution.py:487
  96.2 3.1 %shard_map.62 = (f32[256,256]{1,0:T(8,128)S(1)}, f32[256,256]{1,0:T(8,128)S(1)}) custom-call(s32[16]{0:T(128)S(1)} %copy-done.2, f32[128,128]{1,0:T(8,128)S(1)} %add.36.refs_0_, f32[128,128]{1,0:T(8,128)S(1)} %collective-permute-done.24.refs_1_, f32[128,128]{1,0:T(8,128)S(1)} %collective-permute-done.25.refs_2_, ...), custom_call_target="tpu_custom_call" | custom-call | tf_op jit(solution)/shard_map/pallas_call | solution.py:52
  100.9 1.8 %shard_map.63 = (f32[1280,128]{1,0:T(8,128)S(1)}, f32[1280,128]{1,0:T(8,128)S(1)}, f32[1280,128]{1,0:T(8,128)S(1)}, f32[1280,128]{1,0:T(8,128)S(1)}, f32[1280,128]{1,0:T(8,128)S(1)}) custom-call(s32[16]{0:T(128)S(1)} %copy-done.2, f32[256,256]{1,0:T(8,128)S(1)} %get-tuple-element.135.own_ref.rotation_ref, f32[256,256]{1,0:T(8,128)S(1)} %collective-permute-done.27.other_ref, ...), custom_call_target="tpu_custom_call" | custom-call | tf_op jit(solution)/shard_map/pallas_call | solution.py:52
  102.7 4.8 %collective-permute-start.28 = (f32[1280,128]{1,0:T(8,128)S(1)}, f32[1280,128]{1,0:T(8,128)S(1)}, u32[]{:S(2)}, u32[]{:S(2)}) collective-permute-start(f32[1280,128]{1,0:T(8,128)S(1)} %get-tuple-element.142), channel_id=1, source_target_pairs={{8,0},{9,1},{10,2},{11,3},{12,4},{13,5},{14,6},{15,7},{0,8},{1,9},... | collective-permute-start | bytes 1966088 | tf_op jit(solution)/shard_map/ppermute | solution.py:487
  110.6 4.8 %collective-permute-start.31 = (f32[128,128]{1,0:T(8,128)S(1)}, f32[128,128]{1,0:T(8,128)S(1)}, u32[]{:S(2)}, u32[]{:S(2)}) collective-permute-start(f32[128,128]{1,0:T(8,128)S(1)} %get-tuple-element.146), channel_id=1, source_target_pairs={{1,0},{0,1},{3,2},{2,3},{5,4},{4,5},{7,6},{6,7},{9,8},{8,9},{11,10... | collective-permute-start | bytes 196616 | tf_op jit(solution)/shard_map/ppermute | solution.py:487
  115.4 7.1 %collective-permute-done.28.a_ref.refs_0_ = f32[1280,128]{1,0:T(8,128)S(1)} collective-permute-done((f32[1280,128]{1,0:T(8,128)S(1)}, f32[1280,128]{1,0:T(8,128)S(1)}, u32[]{:S(2)}, u32[]{:S(2)}) %collective-permute-start.28) | collective-permute-done | bytes 655392 | tf_op jit(solution)/shard_map/ppermute | solution.py:487
  123.2 1.7 %shard_map.66 = (f32[128,128]{1,0:T(8,128)S(1)}, f32[128,128]{1,0:T(8,128)S(1)}, f32[1280,128]{1,0:T(8,128)S(1)}, f32[1280,128]{1,0:T(8,128)S(1)}) custom-call(s32[16]{0:T(128)S(1)} %copy-done.2, f32[1280,128]{1,0:T(8,128)S(1)} %collective-permute-done.28.a_ref.refs_0_, f32[1280,128]{1,0:T(8,128)S(1)} %collective-permute-done.29.b_ref.refs_1_, ...), custom_call_target="tpu_custom_call" | custom-call | tf_op jit(solution)/shard_map/pallas_call | solution.py:52
  126.3 2.6 %collective-permute-start.36 = (f32[128,128]{1,0:T(8,128)S(1)}, f32[128,128]{1,0:T(8,128)S(1)}, u32[]{:S(2)}, u32[]{:S(2)}) collective-permute-start(f32[128,128]{1,0:T(8,128)S(1)} %add.37.refs_0_), channel_id=1, source_target_pairs={{6,0},{7,1},{4,2},{5,3},{2,4},{3,5},{0,6},{1,7},{14,8},{15,9},{12,... | collective-permute-start | bytes 196616 | tf_op jit(solution)/shard_map/ppermute | solution.py:487
  130.4 6.6 %collective-permute-done.36.refs_3_ = f32[128,128]{1,0:T(8,128)S(1)} collective-permute-done((f32[128,128]{1,0:T(8,128)S(1)}, f32[128,128]{1,0:T(8,128)S(1)}, u32[]{:S(2)}, u32[]{:S(2)}) %collective-permute-start.36) | collective-permute-done | bytes 65568 | tf_op jit(solution)/shard_map/ppermute | solution.py:487
  137.2 3.4 %shard_map.68 = (f32[264,256]{1,0:T(8,128)S(1)}, f32[256,256]{1,0:T(8,128)}) custom-call(s32[16]{0:T(128)S(1)} %copy-done.2, f32[128,128]{1,0:T(8,128)S(1)} %add.37.refs_0_, f32[128,128]{1,0:T(8,128)S(1)} %collective-permute-done.34.refs_1_, f32[128,128]{1,0:T(8,128)S(1)} %collective-permute-done.35.refs_2_, f32[128,128]{1,0:T(8,128)S(1)} %collective-permute-done.36.refs_3_, ...), custom_call_target="tpu_custom_call" | custom-call | tf_op jit(solution)/shard_map/pallas_call | solution.py:52
  141.1 8.4 %collective-permute-done.39.refs_8_ = f32[512,128]{1,0:T(8,128)S(1)} collective-permute-done((f32[512,128]{1,0:T(8,128)S(1)}, f32[512,128]{1,0:T(8,128)S(1)}, u32[]{:S(2)}, u32[]{:S(2)}) %collective-permute-start.39) | collective-permute-done | bytes 262176 | tf_op jit(solution)/shard_map/ppermute | solution.py:487
  149.4 3.6 %shard_map.69 = (f32[2048,256]{1,0:T(8,128)}, f32[512,256]{1,0:T(8,128)}, f32[1,256]{1,0:T(1,128)}) custom-call(s32[16]{0:T(128)S(1)} %copy-done.2, f32[264,256]{1,0:T(8,128)S(1)} %get-tuple-element.162.refs_0_, f32[264,256]{1,0:T(8,128)S(1)} %collective-permute-done.38.refs_1_, f32[1280,128]{1,0:T(8,128)S(1)} %get-tuple-element.163.refs_2_, ...), custom_call_target="tpu_custom_call" | custom-call | tf_op jit(solution)/shard_map/pallas_call | solution.py:454
  (83 shorter events, 40.5 us)
Async XLA Ops:
  5.0 27.6 %collective-permute-start.4 = (f32[768,256]{1,0:T(8,128)}, f32[768,256]{1,0:T(8,128)S(1)}, u32[]{:S(2)}, u32[]{:S(2)}) collective-permute-start(f32[768,256]{1,0:T(8,128)} %get-tuple-element.92), channel_id=1, source_target_pairs={{4,0},{5,1},{6,2},{7,3},{0,4},{1,5},{2,6},{3,7},{12,8},{13,9},{14,... | collective-permute-start | bytes 2359304 | tf_op jit(solution)/shard_map/ppermute | solution.py:487
  12.9 7.0 %collective-permute-start.1 = (f32[384,128]{1,0:T(8,128)S(1)}, f32[384,128]{1,0:T(8,128)S(1)}, u32[]{:S(2)}, u32[]{:S(2)}) collective-permute-start(f32[384,128]{1,0:T(8,128)S(1)} %add.34.own_ref), channel_id=1, source_target_pairs={{2,0},{3,1},{0,2},{1,3},{6,4},{7,5},{4,6},{5,7},{10,8},{11,9},{8,1... | collective-permute-start | bytes 589832 | tf_op jit(solution)/shard_map/ppermute | solution.py:487
  23.3 9.3 %collective-permute-start.3 = (f32[256,256]{1,0:T(8,128)S(1)}, f32[256,256]{1,0:T(8,128)S(1)}, u32[]{:S(2)}, u32[]{:S(2)}) collective-permute-start(f32[256,256]{1,0:T(8,128)S(1)} %get-tuple-element.87.rotation_ref.own_ref), channel_id=1, source_target_pairs={{4,0},{5,1},{6,2},{7,3},{0,4},{1,5},{2,6},{3,7},{12,8},{13,9},{14,... | collective-permute-start | bytes 786440 | tf_op jit(solution)/shard_map/ppermute | solution.py:487
  24.8 23.9 %collective-permute-start.2 = (f32[1024,128]{1,0:T(8,128)S(1)}, f32[1024,128]{1,0:T(8,128)S(1)}, u32[]{:S(2)}, u32[]{:S(2)}) collective-permute-start(f32[1024,128]{1,0:T(8,128)S(1)} %get-tuple-element.91.refs_1_), channel_id=1, source_target_pairs={{8,0},{9,1},{10,2},{11,3},{16,8},{17,9},{18,10},{19,11},{4,12},{5,... | collective-permute-start | bytes 1572872 | tf_op jit(solution)/shard_map/ppermute | solution.py:487
  26.1 12.7 %collective-permute-start.6 = (f32[256,256]{1,0:T(8,128)S(1)}, f32[256,256]{1,0:T(8,128)S(1)}, u32[]{:S(2)}, u32[]{:S(2)}) collective-permute-start(f32[256,256]{1,0:T(8,128)S(1)} %copy-done.3), channel_id=1, source_target_pairs={{4,0},{5,1},{6,2},{7,3},{0,4},{1,5},{2,6},{3,7},{12,8},{13,9},{14,... | collective-permute-start | bytes 786440 | tf_op jit(solution)/shard_map/ppermute | solution.py:487
  33.6 15.1 %collective-permute-start.5 = (f32[768,128]{1,0:T(8,128)S(1)}, f32[768,128]{1,0:T(8,128)S(1)}, u32[]{:S(2)}, u32[]{:S(2)}) collective-permute-start(f32[768,128]{1,0:T(8,128)S(1)} %get-tuple-element.94.refs_4_), channel_id=1, source_target_pairs={{12,4},{13,5},{14,6},{15,7},{0,8},{1,9},{2,10},{3,11},{20,12},{21,... | collective-permute-start | bytes 1179656 | tf_op jit(solution)/shard_map/ppermute | solution.py:487
  38.8 5.3 %collective-permute-start.8 = (f32[128,128]{1,0:T(8,128)S(1)}, f32[128,128]{1,0:T(8,128)S(1)}, u32[]{:S(2)}, u32[]{:S(2)}) collective-permute-start(f32[128,128]{1,0:T(8,128)S(1)} %get-tuple-element.103), channel_id=1, source_target_pairs={{4,0},{0,1},{6,2},{2,3},{5,4},{1,5},{7,6},{3,7},{12,8},{8,9},{14,1... | collective-permute-start | bytes 196616 | tf_op jit(solution)/shard_map/ppermute | solution.py:487
  39.7 8.4 %collective-permute-start.7 = (f32[256,128]{1,0:T(8,128)S(1)}, f32[256,128]{1,0:T(8,128)S(1)}, u32[]{:S(2)}, u32[]{:S(2)}) collective-permute-start(f32[256,128]{1,0:T(8,128)S(1)} %get-tuple-element.97.refs_7_), channel_id=1, source_target_pairs={{12,4},{13,5},{14,6},{15,7},{0,8},{1,9},{2,10},{3,11},{20,12},{21,... | collective-permute-start | bytes 393224 | tf_op jit(solution)/shard_map/ppermute | solution.py:487
  44.1 6.4 %collective-permute-start.9 = (f32[256,128]{1,0:T(8,128)S(1)}, f32[256,128]{1,0:T(8,128)S(1)}, u32[]{:S(2)}, u32[]{:S(2)}) collective-permute-start(f32[256,128]{1,0:T(8,128)S(1)} %get-tuple-element.104), channel_id=1, source_target_pairs={{8,0},{9,1},{10,2},{11,3},{12,4},{13,5},{14,6},{15,7},{0,8},{1,9},... | collective-permute-start | bytes 393224 | tf_op jit(solution)/shard_map/ppermute | solution.py:487
  45.8 4.8 %collective-permute-start.10 = (f32[256,128]{1,0:T(8,128)S(1)}, f32[256,128]{1,0:T(8,128)S(1)}, u32[]{:S(2)}, u32[]{:S(2)}) collective-permute-start(f32[256,128]{1,0:T(8,128)S(1)} %get-tuple-element.105), channel_id=1, source_target_pairs={{0,0},{1,1},{2,2},{3,3},{4,4},{5,5},{6,6},{7,7},{16,8},{17,9},{18,... | collective-permute-start | bytes 393224 | tf_op jit(solution)/shard_map/ppermute | solution.py:487
  50.6 4.8 %collective-permute-start.12 = (f32[128,128]{1,0:T(8,128)S(1)}, f32[128,128]{1,0:T(8,128)S(1)}, u32[]{:S(2)}, u32[]{:S(2)}) collective-permute-start(f32[128,128]{1,0:T(8,128)S(1)} %get-tuple-element.107), channel_id=1, source_target_pairs={{1,0},{0,1},{3,2},{2,3},{5,4},{4,5},{7,6},{6,7},{9,8},{8,9},{11,10... | collective-permute-start | bytes 196616 | tf_op jit(solution)/shard_map/ppermute | solution.py:487
  55.4 5.6 %collective-permute-start.15 = (f32[128,128]{1,0:T(8,128)S(1)}, f32[128,128]{1,0:T(8,128)S(1)}, u32[]{:S(2)}, u32[]{:S(2)}) collective-permute-start(f32[128,128]{1,0:T(8,128)S(1)} %add.35.refs_0_), channel_id=1, source_target_pairs={{6,0},{7,1},{4,2},{5,3},{2,4},{3,5},{0,6},{1,7},{14,8},{15,9},{12,... | collective-permute-start | bytes 196616 | tf_op jit(solution)/shard_map/ppermute | solution.py:487
  58.4 4.3 %collective-permute-start.13 = (f32[128,128]{1,0:T(8,128)S(1)}, f32[128,128]{1,0:T(8,128)S(1)}, u32[]{:S(2)}, u32[]{:S(2)}) collective-permute-start(f32[128,128]{1,0:T(8,128)S(1)} %add.35.refs_0_), channel_id=1, source_target_pairs={{2,0},{3,1},{0,2},{1,3},{6,4},{7,5},{4,6},{5,7},{10,8},{11,9},{8,1... | collective-permute-start | bytes 196616 | tf_op jit(solution)/shard_map/ppermute | solution.py:487
  69.5 16.2 %collective-permute-start.17 = (f32[1024,128]{1,0:T(8,128)S(1)}, f32[1024,128]{1,0:T(8,128)S(1)}, u32[]{:S(2)}, u32[]{:S(2)}) collective-permute-start(f32[1024,128]{1,0:T(8,128)S(1)} %get-tuple-element.119), channel_id=1, source_target_pairs={{8,0},{9,1},{10,2},{11,3},{12,4},{13,5},{14,6},{15,7},{0,8},{1,9},... | collective-permute-start | bytes 1572872 | tf_op jit(solution)/shard_map/ppermute | solution.py:487
  73.0 12.7 %collective-permute-start.18 = (f32[1024,128]{1,0:T(8,128)S(1)}, f32[1024,128]{1,0:T(8,128)S(1)}, u32[]{:S(2)}, u32[]{:S(2)}) collective-permute-start(f32[1024,128]{1,0:T(8,128)S(1)} %get-tuple-element.120), channel_id=1, source_target_pairs={{0,0},{1,1},{2,2},{3,3},{4,4},{5,5},{6,6},{7,7},{16,8},{17,9},{18,... | collective-permute-start | bytes 1572872 | tf_op jit(solution)/shard_map/ppermute | solution.py:487
  76.9 11.2 %collective-permute-start.20 = (f32[256,128]{1,0:T(8,128)S(1)}, f32[256,128]{1,0:T(8,128)S(1)}, u32[]{:S(2)}, u32[]{:S(2)}) collective-permute-start(f32[256,128]{1,0:T(8,128)S(1)} %get-tuple-element.129), channel_id=1, source_target_pairs={{8,0},{9,1},{10,2},{11,3},{12,4},{13,5},{14,6},{15,7},{0,8},{1,9},... | collective-permute-start | bytes 393224 | tf_op jit(solution)/shard_map/ppermute | solution.py:487
  81.2 6.8 %collective-permute-start.21 = (f32[256,128]{1,0:T(8,128)S(1)}, f32[256,128]{1,0:T(8,128)S(1)}, u32[]{:S(2)}, u32[]{:S(2)}) collective-permute-start(f32[256,128]{1,0:T(8,128)S(1)} %get-tuple-element.130), channel_id=1, source_target_pairs={{0,0},{1,1},{2,2},{3,3},{4,4},{5,5},{6,6},{7,7},{16,8},{17,9},{18,... | collective-permute-start | bytes 393224 | tf_op jit(solution)/shard_map/ppermute | solution.py:487
  81.9 5.5 %collective-permute-start.22 = (f32[128,128]{1,0:T(8,128)S(1)}, f32[128,128]{1,0:T(8,128)S(1)}, u32[]{:S(2)}, u32[]{:S(2)}) collective-permute-start(f32[128,128]{1,0:T(8,128)S(1)} %get-tuple-element.131), channel_id=1, source_target_pairs={{0,0},{8,1},{2,2},{10,3},{4,4},{12,5},{6,6},{14,7},{1,8},{16,9},{3... | collective-permute-start | bytes 196616 | tf_op jit(solution)/shard_map/ppermute | solution.py:487
  89.5 5.9 %collective-permute-start.26 = (f32[128,128]{1,0:T(8,128)S(1)}, f32[128,128]{1,0:T(8,128)S(1)}, u32[]{:S(2)}, u32[]{:S(2)}) collective-permute-start(f32[128,128]{1,0:T(8,128)S(1)} %add.36.refs_0_), channel_id=1, source_target_pairs={{6,0},{7,1},{4,2},{5,3},{2,4},{3,5},{0,6},{1,7},{14,8},{15,9},{12,... | collective-permute-start | bytes 196616 | tf_op jit(solution)/shard_map/ppermute | solution.py:487
  89.7 5.8 %collective-permute-start.25 = (f32[128,128]{1,0:T(8,128)S(1)}, f32[128,128]{1,0:T(8,128)S(1)}, u32[]{:S(2)}, u32[]{:S(2)}) collective-permute-start(f32[128,128]{1,0:T(8,128)S(1)} %add.36.refs_0_), channel_id=1, source_target_pairs={{4,0},{5,1},{6,2},{7,3},{0,4},{1,5},{2,6},{3,7},{12,8},{13,9},{14,... | collective-permute-start | bytes 196616 | tf_op jit(solution)/shard_map/ppermute | solution.py:487
  91.8 4.4 %collective-permute-start.24 = (f32[128,128]{1,0:T(8,128)S(1)}, f32[128,128]{1,0:T(8,128)S(1)}, u32[]{:S(2)}, u32[]{:S(2)}) collective-permute-start(f32[128,128]{1,0:T(8,128)S(1)} %add.36.refs_0_), channel_id=1, source_target_pairs={{2,0},{3,1},{0,2},{1,3},{6,4},{7,5},{4,6},{5,7},{10,8},{11,9},{8,1... | collective-permute-start | bytes 196616 | tf_op jit(solution)/shard_map/ppermute | solution.py:487
  102.7 19.9 %collective-permute-start.28 = (f32[1280,128]{1,0:T(8,128)S(1)}, f32[1280,128]{1,0:T(8,128)S(1)}, u32[]{:S(2)}, u32[]{:S(2)}) collective-permute-start(f32[1280,128]{1,0:T(8,128)S(1)} %get-tuple-element.142), channel_id=1, source_target_pairs={{8,0},{9,1},{10,2},{11,3},{12,4},{13,5},{14,6},{15,7},{0,8},{1,9},... | collective-permute-start | bytes 1966088 | tf_op jit(solution)/shard_map/ppermute | solution.py:487
  107.5 15.0 %collective-permute-start.29 = (f32[1280,128]{1,0:T(8,128)S(1)}, f32[1280,128]{1,0:T(8,128)S(1)}, u32[]{:S(2)}, u32[]{:S(2)}) collective-permute-start(f32[1280,128]{1,0:T(8,128)S(1)} %get-tuple-element.143), channel_id=1, source_target_pairs={{0,0},{1,1},{2,2},{3,3},{4,4},{5,5},{6,6},{7,7},{16,8},{17,9},{18,... | collective-permute-start | bytes 1966088 | tf_op jit(solution)/shard_map/ppermute | solution.py:487
  108.2 16.7 %collective-permute-start.32 = (f32[1280,128]{1,0:T(8,128)S(1)}, f32[1280,128]{1,0:T(8,128)S(1)}, u32[]{:S(2)}, u32[]{:S(2)}) collective-permute-start(f32[1280,128]{1,0:T(8,128)S(1)} %get-tuple-element.153), channel_id=1, source_target_pairs={{4,0},{5,1},{6,2},{7,3},{0,4},{1,5},{2,6},{3,7},{12,8},{13,9},{14,... | collective-permute-start | bytes 1966088 | tf_op jit(solution)/shard_map/ppermute | solution.py:487
  109.9 13.2 %collective-permute-start.30 = (f32[128,128]{1,0:T(8,128)S(1)}, f32[128,128]{1,0:T(8,128)S(1)}, u32[]{:S(2)}, u32[]{:S(2)}) collective-permute-start(f32[128,128]{1,0:T(8,128)S(1)} %get-tuple-element.145), channel_id=1, source_target_pairs={{0,0},{8,1},{2,2},{10,3},{4,4},{12,5},{6,6},{14,7},{1,8},{16,9},{3... | collective-permute-start | bytes 196616 | tf_op jit(solution)/shard_map/ppermute | solution.py:487
  110.6 12.6 %collective-permute-start.31 = (f32[128,128]{1,0:T(8,128)S(1)}, f32[128,128]{1,0:T(8,128)S(1)}, u32[]{:S(2)}, u32[]{:S(2)}) collective-permute-start(f32[128,128]{1,0:T(8,128)S(1)} %get-tuple-element.146), channel_id=1, source_target_pairs={{1,0},{0,1},{3,2},{2,3},{5,4},{4,5},{7,6},{6,7},{9,8},{8,9},{11,10... | collective-permute-start | bytes 196616 | tf_op jit(solution)/shard_map/ppermute | solution.py:487
  123.2 14.0 %collective-permute-start.37 = (f32[768,128]{1,0:T(8,128)S(1)}, f32[768,128]{1,0:T(8,128)S(1)}, u32[]{:S(2)}, u32[]{:S(2)}) collective-permute-start(f32[768,128]{1,0:T(8,128)S(1)} %shard_map.64), channel_id=1, source_target_pairs={{4,0},{5,1},{6,2},{7,3},{0,4},{1,5},{2,6},{3,7},{12,8},{13,9},{14,... | collective-permute-start | bytes 1179656 | tf_op jit(solution)/shard_map/ppermute | solution.py:487
  126.3 10.8 %collective-permute-start.36 = (f32[128,128]{1,0:T(8,128)S(1)}, f32[128,128]{1,0:T(8,128)S(1)}, u32[]{:S(2)}, u32[]{:S(2)}) collective-permute-start(f32[128,128]{1,0:T(8,128)S(1)} %add.37.refs_0_), channel_id=1, source_target_pairs={{6,0},{7,1},{4,2},{5,3},{2,4},{3,5},{0,6},{1,7},{14,8},{15,9},{12,... | collective-permute-start | bytes 196616 | tf_op jit(solution)/shard_map/ppermute | solution.py:487
  128.9 8.3 %collective-permute-start.35 = (f32[128,128]{1,0:T(8,128)S(1)}, f32[128,128]{1,0:T(8,128)S(1)}, u32[]{:S(2)}, u32[]{:S(2)}) collective-permute-start(f32[128,128]{1,0:T(8,128)S(1)} %add.37.refs_0_), channel_id=1, source_target_pairs={{4,0},{5,1},{6,2},{7,3},{0,4},{1,5},{2,6},{3,7},{12,8},{13,9},{14,... | collective-permute-start | bytes 196616 | tf_op jit(solution)/shard_map/ppermute | solution.py:487
  128.9 8.3 %collective-permute-start.34 = (f32[128,128]{1,0:T(8,128)S(1)}, f32[128,128]{1,0:T(8,128)S(1)}, u32[]{:S(2)}, u32[]{:S(2)}) collective-permute-start(f32[128,128]{1,0:T(8,128)S(1)} %add.37.refs_0_), channel_id=1, source_target_pairs={{2,0},{3,1},{0,2},{1,3},{6,4},{7,5},{4,6},{5,7},{10,8},{11,9},{8,1... | collective-permute-start | bytes 196616 | tf_op jit(solution)/shard_map/ppermute | solution.py:487
  140.6 8.8 %collective-permute-start.38 = (f32[264,256]{1,0:T(8,128)S(1)}, f32[264,256]{1,0:T(8,128)S(1)}, u32[]{:S(2)}, u32[]{:S(2)}) collective-permute-start(f32[264,256]{1,0:T(8,128)S(1)} %get-tuple-element.162.refs_0_), channel_id=1, source_target_pairs={{1,0},{0,1},{3,2},{2,3},{5,4},{4,5},{7,6},{6,7},{9,8},{8,9},{11,10... | collective-permute-start | bytes 811016 | tf_op jit(solution)/shard_map/ppermute | solution.py:487
  140.7 8.7 %collective-permute-start.39 = (f32[512,128]{1,0:T(8,128)S(1)}, f32[512,128]{1,0:T(8,128)S(1)}, u32[]{:S(2)}, u32[]{:S(2)}) collective-permute-start(f32[512,128]{1,0:T(8,128)S(1)} %shard_map.67), channel_id=1, source_target_pairs={{4,0},{5,1},{6,2},{7,3},{0,4},{1,5},{2,6},{3,7},{12,8},{13,9},{14,... | collective-permute-start | bytes 786440 | tf_op jit(solution)/shard_map/ppermute | solution.py:487
  (12 other events, 38.9 us)

commit v9 on v8

--- a/solution.py
+++ b/solution.py
@@ -393,78 +393,113 @@
     return call(body, facts, got, shape(stop - start, half))
 
 
-def finish(facts, packs, blocks, native, got_top, got_rest, part, half):
+def final_turn(f, own_ref, other_ref, size):
+    pack = jnp.where(f[CORE] == f[X], own_ref[...], other_ref[...])
+    return split(swapped(f[X] == 1, pack[:size], 0)), pack[size : size + 1]
+
+
+def final_product(moved, native, turned):
+    return dot3(lax.concatenate([moved, native], 1), turned)
+
+
+def put_rows(copies, sems, source, target, here, there, value):
+    rows = value.shape[0]
+    source[here : here + rows] = value
+    copy = pltpu.make_async_copy(
+        source.at[here : here + rows],
+        target.at[pl.ds(pl.multiple_of(there, 8), rows)],
+        sems.at[len(copies)],
+    )
+    copies.append(copy)
+    copy.start()
+
+
+def finish_call(body, facts, inputs, outputs, outs, rows, vector_rows, size):
+    vmem = pl.BlockSpec(memory_space=pltpu.VMEM)
+    hbm = pl.BlockSpec(memory_space=pl.ANY)
+    first = 1 + len(inputs)
+    return pl.pallas_call(
+        body,
+        out_shape=outs,
+        in_specs=[pl.BlockSpec(memory_space=pltpu.SMEM)]
+        + [vmem] * len(inputs)
+        + [hbm] * len(outputs),
+        out_specs=(hbm, hbm, vmem)[: len(outs)],
+        input_output_aliases={first + k: k for k in range(len(outputs))},
+        cost_estimate=pl.CostEstimate(flops=1, transcendentals=0, bytes_accessed=1),
+        scratch_shapes=[
+            pltpu.VMEM((rows, size), jnp.float32),
+            pltpu.VMEM((vector_rows, size), jnp.float32),
+            pltpu.SemaphoreType.DMA((4,)),
+        ],
+        compiler_params=pltpu.CompilerParams(vmem_limit_bytes=24 << 20),
+    )(facts, *inputs, *outputs)
+
+
+def finish_kept(facts, packs, blocks, native, got_top, part, half):
     size = 2 * half
     vector_rows = blocks[0].shape[0] - part
     top = got_top.shape[0]
 
-    def body(f, *refs):
+    def body(f, own_ref, other_ref, *refs):
         x = f[X]
-        mine = f[CORE] == x
-        pack = jnp.where(mine, refs[0][...], refs[1][...])
-        turned = split(swapped(x == 1, pack[:size], 0))
-        native_ref, top_ref, rest_ref = refs[6:9]
-        out_ref, vectors_ref, singular_ref, out, vectors, sems = refs[9:]
+        turned, squares = final_turn(f, own_ref, other_ref, size)
+        native_ref, top_ref, out_ref, vectors_ref, singular_ref, out, vectors, sems = (
+            refs[4:]
+        )
         copies = []
 
-        def put(source, target, here, there, value):
-            rows = value.shape[0]
-            source[here : here + rows] = value
-            there = pl.multiple_of(there, 8)
-            copies.append(
-                pltpu.make_async_copy(
-                    source.at[here : here + rows],
-                    target.at[pl.ds(there, rows)],
-                    sems.at[len(copies)],
-                )
+        def kept(rows):
+            up_0, low_0, up_1, low_1 = [r[rows] for r in refs[:4]]
+            return final_product(
+                jnp.where(x == 0, up_0, low_1),
+                jnp.where(x == 0, low_0, up_1),
+                turned,
             )
-            copies[-1].start()
-
-        def product(moved, native):
-            return dot3(lax.concatenate([moved, native], 1), turned)
-
-        def kept(rows):
-            up_0, low_0, up_1, low_1 = [r[rows] for r in refs[2:6]]
-            return product(
-                jnp.where(x == 0, up_0, low_1), jnp.where(x == 0, low_0, up_1)
-            )
-
-        squares = pack[size : size + 1]
-        singular_ref[...] = jnp.sqrt(jnp.maximum(squares, 0.0) + 1e-06)
-        other = (1 - x) * part
+
+        def put(*args):
+            put_rows(copies, sems, *args)
+
         middle = part // 2
         put(out, out_ref, 0, x * part, kept(slice(0, middle)))
         put(out, out_ref, middle, x * part + middle, kept(slice(middle, part)))
-        put(out, out_ref, part, other, product(top_ref[...], native_ref[:top]))
-        put(
-            out, out_ref, part + top, other + top,
-            product(rest_ref[: part - top], native_ref[top:part]),
-        )
+        value = final_product(top_ref[...], native_ref[:top], turned)
+        put(out, out_ref, part, (1 - x) * part, value)
         put(vectors, vectors_ref, 0, x * vector_rows, kept(slice(part, None)))
-        put(
-            vectors, vectors_ref, vector_rows, (1 - x) * vector_rows,
-            product(rest_ref[part - top :], native_ref[part:]),
-        )
+        singular_ref[...] = jnp.sqrt(jnp.maximum(squares, 0.0) + 1e-06)
         for copy in copies:
             copy.wait()
 
-    vmem = pl.BlockSpec(memory_space=pltpu.VMEM)
-    hbm = pl.BlockSpec(memory_space=pl.ANY)
-    inputs = packs + blocks + [native, got_top, got_rest]
-    return pl.pallas_call(
-        body,
-        out_shape=(
-            shape(2 * part, size), shape(2 * vector_rows, size), shape(1, size)
-        ),
-        in_specs=[pl.BlockSpec(memory_space=pltpu.SMEM)] + [vmem] * len(inputs),
-        out_specs=(hbm, hbm, vmem),
-        scratch_shapes=[
-            pltpu.VMEM((2 * part, size), jnp.float32),
-            pltpu.VMEM((2 * vector_rows, size), jnp.float32),
-            pltpu.SemaphoreType.DMA((6,)),
-        ],
-        compiler_params=pltpu.CompilerParams(vmem_limit_bytes=24 << 20),
-    )(facts, *inputs)
+    outs = (shape(2 * part, size), shape(2 * vector_rows, size), shape(1, size))
+    inputs = packs + blocks + [native, got_top]
+    return finish_call(
+        body, facts, inputs, [], outs, part + top, vector_rows, size
+    )
+
+
+def finish_rest(facts, packs, outputs, native, got_rest, part, half):
+    size = 2 * half
+    vector_rows = native.shape[0] - part
+    rest = got_rest.shape[0] - vector_rows
+    top = part - rest
+
+    def body(f, own_ref, other_ref, native_ref, rest_ref, *refs):
+        x = f[X]
+        turned, _ = final_turn(f, own_ref, other_ref, size)
+        out_ref, vectors_ref, out, vectors, sems = refs[2:]
+        copies = []
+        value = final_product(rest_ref[:rest], native_ref[top:part], turned)
+        put_rows(copies, sems, out, out_ref, 0, (1 - x) * part + top, value)
+        value = final_product(rest_ref[rest:], native_ref[part:], turned)
+        put_rows(copies, sems, vectors, vectors_ref, 0, (1 - x) * vector_rows, value)
+        for copy in copies:
+            copy.wait()
+
+    outs = (shape(2 * part, size), shape(2 * vector_rows, size))
+    inputs = packs + [native, got_rest]
+    return finish_call(
+        body, facts, inputs, outputs, outs, rest, vector_rows, size
+    )
 
 
 def per_device(sector, block_label):
@@ -592,7 +627,7 @@
             diagonals = [pass_diagonal(leave), exchange(stay, 0, 1)]
             if last_move:
                 native = exchange(vectors.pop(), 1, 0)
-                top = part * 3 // 4
+                top = part // 2
                 top_give = give(facts, got, 0, top, half)
                 *got, top_give, diagonals[0], diagonals[1] = together(
                     *got, top_give, *diagonals
@@ -620,8 +655,11 @@
             got_rest = exchange(rest_give, 1, 0)
         rotation, gram = later_rotation(facts, parts, diagonals, half, last_move)
     packs = [rotation, exchange(rotation, 0, 1)]
-    rotated, vectors_out, singular = finish(
-        facts, packs, blocks, native, got_top, got_rest, part, half
+    *outputs, singular = finish_kept(
+        facts, packs, blocks, native, got_top, part, half
+    )
+    rotated, vectors_out = finish_rest(
+        facts, packs, outputs, native, got_rest, part, half
     )
     return rotated, vectors_out, singular.reshape(size)
 

time: 155 us -> 149 us (0.961)
  waiting for transfers between devices: 51.2 us -> 43.1 us
    ppermute x40, waiting for transfers between devices: 51.2 us -> 43.1 us  [permute(): return lax.ppermute(block, ('pair', 'row'), moves)]
    pallas_call x1 -> x2, Pallas kernels: 3.58 us -> 4.94 us  [finish_call(): pl.pallas_call(body, out_shape=outs, in_specs=[pl.BlockSpec(memory_space=...]
  transfers between devices with their start and end apart: 40 -> 40, of which waited for: 22 -> 23; matrix products, arithmetic and copies ran while one was open for 0% -> 0% of each run, Pallas kernels for 14% -> 19%
where the time goes in v9:
time: 149 us; the launch traced here: 147 us
  starting transfers between devices  57.8 us (39%)
  waiting for transfers between devices  43.1 us (29%)
  Pallas kernels  42.5 us (29%)
  local copies, waits for them, and re-layouts  2.12 us (1%)
    ppermute x40, starting transfers between devices, permute(): return lax.ppermute(block, ('pair', 'row'), moves)  57.8 us
    ppermute x40, waiting for transfers between devices, permute(): return lax.ppermute(block, ('pair', 'row'), moves)  43.1 us
    pallas_call x19, Pallas kernels, call(): pl.pallas_call(body, out_shape=outs, in_specs=[pl.BlockSpec(memory_space=...  34.7 us
    pallas_call x2, Pallas kernels, finish_call(): pl.pallas_call(body, out_shape=outs, in_specs=[pl.BlockSpec(memory_space=...  4.94 us
  transfers between devices with their start and end apart: 40, of which 23 were waited for; matrix products, arithmetic and copies ran while one was open for 0% of the time, Pallas kernels for 19%

profile of v9, /device:TPU:0, one launch (start us, length us, event | category | flops | bytes accessed | tf_op | source)
XLA Modules:
  0.0 146.9 jit_solution(11355848349360368716)
XLA Ops:
  2.2 2.8 %shard_map.52 = (f32[768,256]{1,0:T(8,128)}, f32[256,256]{1,0:T(8,128)}) custom-call(s32[16]{0:T(128)} %copy-done.1, f32[2048,256]{1,0:T(8,128)} %x_ref.5), custom_call_target="tpu_custom_call" | custom-call | tf_op jit(solution)/shard_map/pallas_call | solution.py:95
  5.0 3.0 %collective-permute-start.4 = (f32[768,256]{1,0:T(8,128)}, f32[768,256]{1,0:T(8,128)S(1)}, u32[]{:S(2)}, u32[]{:S(2)}) collective-permute-start(f32[768,256]{1,0:T(8,128)} %get-tuple-element.94), channel_id=1, source_target_pairs={{4,0},{5,1},{6,2},{7,3},{0,4},{1,5},{2,6},{3,7},{12,8},{13,9},{14,... | collective-permute-start | bytes 2359304 | tf_op jit(solution)/shard_map/ppermute | solution.py:522
  8.7 2.6 %shard_map.49 = f32[384,128]{1,0:T(8,128)S(1)} custom-call(s32[16]{0:T(128)S(1)} %copy-done.2, f32[2048,256]{1,0:T(8,128)S(1)} %copy-done), custom_call_target="tpu_custom_call" | custom-call | tf_op jit(solution)/shard_map/pallas_call | solution.py:52
  14.4 5.4 %collective-permute-done.1.other_ref = f32[384,128]{1,0:T(8,128)S(1)} collective-permute-done((f32[384,128]{1,0:T(8,128)S(1)}, f32[384,128]{1,0:T(8,128)S(1)}, u32[]{:S(2)}, u32[]{:S(2)}) %collective-permute-start.1) | collective-permute-done | bytes 196640 | tf_op jit(solution)/shard_map/ppermute | solution.py:522
  19.9 3.4 %shard_map.50 = (f32[256,256]{1,0:T(8,128)S(1)}, f32[256,256]{1,0:T(8,128)S(1)}) custom-call(s32[16]{0:T(128)S(1)} %copy-done.2, f32[384,128]{1,0:T(8,128)S(1)} %add.34.own_ref, f32[384,128]{1,0:T(8,128)S(1)} %collective-permute-done.1.other_ref), custom_call_target="tpu_custom_call" | custom-call | tf_op jit(solution)/shard_map/pallas_call | solution.py:52
  26.1 4.0 %collective-permute-start.6 = (f32[256,256]{1,0:T(8,128)S(1)}, f32[256,256]{1,0:T(8,128)S(1)}, u32[]{:S(2)}, u32[]{:S(2)}) collective-permute-start(f32[256,256]{1,0:T(8,128)S(1)} %copy-done.3), channel_id=1, source_target_pairs={{4,0},{5,1},{6,2},{7,3},{0,4},{1,5},{2,6},{3,7},{12,8},{13,9},{14,... | collective-permute-start | bytes 786440 | tf_op jit(solution)/shard_map/ppermute | solution.py:522
  30.1 2.5 %collective-permute-done.3.rotation_ref.other_ref = f32[256,256]{1,0:T(8,128)S(1)} collective-permute-done((f32[256,256]{1,0:T(8,128)S(1)}, f32[256,256]{1,0:T(8,128)S(1)}, u32[]{:S(2)}, u32[]{:S(2)}) %collective-permute-start.3) | collective-permute-done | bytes 262176 | tf_op jit(solution)/shard_map/ppermute | solution.py:522
  33.6 3.5 %collective-permute-start.5 = (f32[768,128]{1,0:T(8,128)S(1)}, f32[768,128]{1,0:T(8,128)S(1)}, u32[]{:S(2)}, u32[]{:S(2)}) collective-permute-start(f32[768,128]{1,0:T(8,128)S(1)} %get-tuple-element.96.refs_4_), channel_id=1, source_target_pairs={{12,4},{13,5},{14,6},{15,7},{0,8},{1,9},{2,10},{3,11},{20,12},{21,... | collective-permute-start | bytes 1179656 | tf_op jit(solution)/shard_map/ppermute | solution.py:522
  39.7 3.5 %collective-permute-start.7 = (f32[256,128]{1,0:T(8,128)S(1)}, f32[256,128]{1,0:T(8,128)S(1)}, u32[]{:S(2)}, u32[]{:S(2)}) collective-permute-start(f32[256,128]{1,0:T(8,128)S(1)} %get-tuple-element.99.refs_7_), channel_id=1, source_target_pairs={{12,4},{13,5},{14,6},{15,7},{0,8},{1,9},{2,10},{3,11},{20,12},{21,... | collective-permute-start | bytes 393224 | tf_op jit(solution)/shard_map/ppermute | solution.py:522
  48.7 1.8 %shard_map.55 = (f32[128,128]{1,0:T(8,128)S(1)}, f32[128,128]{1,0:T(8,128)S(1)}, f32[1024,128]{1,0:T(8,128)S(1)}, f32[1024,128]{1,0:T(8,128)S(1)}, f32[1024,128]{1,0:T(8,128)S(1)}, /*index=5*/f32[1024,128]{1,0:T(8,128)S(1)}) custom-call(s32[16]{0:T(128)S(1)} %copy-done.2, f32[1024,128]{1,0:T(8,128)S(1)} %get-tuple-element.90.refs_0_, ...), custom_call_target="tpu_custom_call" | custom-call | tf_op jit(solution)/shard_map/pallas_call | solution.py:52
  50.6 3.9 %collective-permute-start.12 = (f32[128,128]{1,0:T(8,128)S(1)}, f32[128,128]{1,0:T(8,128)S(1)}, u32[]{:S(2)}, u32[]{:S(2)}) collective-permute-start(f32[128,128]{1,0:T(8,128)S(1)} %get-tuple-element.109), channel_id=1, source_target_pairs={{1,0},{0,1},{3,2},{2,3},{5,4},{4,5},{7,6},{6,7},{9,8},{8,9},{11,10... | collective-permute-start | bytes 196616 | tf_op jit(solution)/shard_map/ppermute | solution.py:522
  55.4 2.7 %collective-permute-start.15 = (f32[128,128]{1,0:T(8,128)S(1)}, f32[128,128]{1,0:T(8,128)S(1)}, u32[]{:S(2)}, u32[]{:S(2)}) collective-permute-start(f32[128,128]{1,0:T(8,128)S(1)} %add.35.refs_0_), channel_id=1, source_target_pairs={{6,0},{7,1},{4,2},{5,3},{2,4},{3,5},{0,6},{1,7},{14,8},{15,9},{12,... | collective-permute-start | bytes 196616 | tf_op jit(solution)/shard_map/ppermute | solution.py:522
  59.0 2.0 %collective-permute-done.15.refs_3_ = f32[128,128]{1,0:T(8,128)S(1)} collective-permute-done((f32[128,128]{1,0:T(8,128)S(1)}, f32[128,128]{1,0:T(8,128)S(1)}, u32[]{:S(2)}, u32[]{:S(2)}) %collective-permute-start.15) | collective-permute-done | bytes 65568 | tf_op jit(solution)/shard_map/ppermute | solution.py:522
  62.7 3.4 %shard_map.58 = (f32[256,256]{1,0:T(8,128)S(1)}, f32[256,256]{1,0:T(8,128)S(1)}) custom-call(s32[16]{0:T(128)S(1)} %copy-done.2, f32[128,128]{1,0:T(8,128)S(1)} %add.35.refs_0_, f32[128,128]{1,0:T(8,128)S(1)} %collective-permute-done.13.refs_1_, f32[128,128]{1,0:T(8,128)S(1)} %collective-permute-done.14.refs_2_, ...), custom_call_target="tpu_custom_call" | custom-call | tf_op jit(solution)/shard_map/pallas_call | solution.py:52
  67.8 1.8 %shard_map.59 = (f32[1024,128]{1,0:T(8,128)S(1)}, f32[1024,128]{1,0:T(8,128)S(1)}, f32[1024,128]{1,0:T(8,128)S(1)}, f32[1024,128]{1,0:T(8,128)S(1)}, f32[256,128...) custom-call(s32[16]{0:T(128)S(1)} %copy-done.2, ...), custom_call_target="tpu_custom_call" | custom-call | tf_op jit(solution)/shard_map/pallas_call | solution.py:52
  69.5 3.5 %collective-permute-start.17 = (f32[1024,128]{1,0:T(8,128)S(1)}, f32[1024,128]{1,0:T(8,128)S(1)}, u32[]{:S(2)}, u32[]{:S(2)}) collective-permute-start(f32[1024,128]{1,0:T(8,128)S(1)} %get-tuple-element.121), channel_id=1, source_target_pairs={{8,0},{9,1},{10,2},{11,3},{12,4},{13,5},{14,6},{15,7},{0,8},{1,9},... | collective-permute-start | bytes 1572872 | tf_op jit(solution)/shard_map/ppermute | solution.py:522
  76.9 4.4 %collective-permute-start.20 = (f32[256,128]{1,0:T(8,128)S(1)}, f32[256,128]{1,0:T(8,128)S(1)}, u32[]{:S(2)}, u32[]{:S(2)}) collective-permute-start(f32[256,128]{1,0:T(8,128)S(1)} %get-tuple-element.131), channel_id=1, source_target_pairs={{8,0},{9,1},{10,2},{11,3},{12,4},{13,5},{14,6},{15,7},{0,8},{1,9},... | collective-permute-start | bytes 393224 | tf_op jit(solution)/shard_map/ppermute | solution.py:522
  82.6 3.2 %collective-permute-done.17.refs_0_ = f32[1024,128]{1,0:T(8,128)S(1)} collective-permute-done((f32[1024,128]{1,0:T(8,128)S(1)}, f32[1024,128]{1,0:T(8,128)S(1)}, u32[]{:S(2)}, u32[]{:S(2)}) %collective-permute-start.17) | collective-permute-done | bytes 524320 | tf_op jit(solution)/shard_map/ppermute | solution.py:522
  85.7 1.7 %shard_map.60 = (f32[128,128]{1,0:T(8,128)S(1)}, f32[128,128]{1,0:T(8,128)S(1)}, f32[1024,128]{1,0:T(8,128)S(1)}, f32[1024,128]{1,0:T(8,128)S(1)}) custom-call(s32[16]{0:T(128)S(1)} %copy-done.2, f32[1024,128]{1,0:T(8,128)S(1)} %collective-permute-done.17.refs_0_, f32[1024,128]{1,0:T(8,128)S(1)} %collective-permute-done.18.refs_1_, ...), custom_call_target="tpu_custom_call" | custom-call | tf_op jit(solution)/shard_map/pallas_call | solution.py:52
  89.7 2.0 %collective-permute-start.25 = (f32[128,128]{1,0:T(8,128)S(1)}, f32[128,128]{1,0:T(8,128)S(1)}, u32[]{:S(2)}, u32[]{:S(2)}) collective-permute-start(f32[128,128]{1,0:T(8,128)S(1)} %add.36.refs_0_), channel_id=1, source_target_pairs={{4,0},{5,1},{6,2},{7,3},{0,4},{1,5},{2,6},{3,7},{12,8},{13,9},{14,... | collective-permute-start | bytes 196616 | tf_op jit(solution)/shard_map/ppermute | solution.py:522
  93.1 2.3 %collective-permute-done.26.refs_3_ = f32[128,128]{1,0:T(8,128)S(1)} collective-permute-done((f32[128,128]{1,0:T(8,128)S(1)}, f32[128,128]{1,0:T(8,128)S(1)}, u32[]{:S(2)}, u32[]{:S(2)}) %collective-permute-start.26) | collective-permute-done | bytes 65568 | tf_op jit(solution)/shard_map/ppermute | solution.py:522
  96.2 3.1 %shard_map.62 = (f32[256,256]{1,0:T(8,128)S(1)}, f32[256,256]{1,0:T(8,128)S(1)}) custom-call(s32[16]{0:T(128)S(1)} %copy-done.2, f32[128,128]{1,0:T(8,128)S(1)} %add.36.refs_0_, f32[128,128]{1,0:T(8,128)S(1)} %collective-permute-done.24.refs_1_, f32[128,128]{1,0:T(8,128)S(1)} %collective-permute-done.25.refs_2_, ...), custom_call_target="tpu_custom_call" | custom-call | tf_op jit(solution)/shard_map/pallas_call | solution.py:52
  100.9 1.8 %shard_map.63 = (f32[1280,128]{1,0:T(8,128)S(1)}, f32[1280,128]{1,0:T(8,128)S(1)}, f32[1280,128]{1,0:T(8,128)S(1)}, f32[1280,128]{1,0:T(8,128)S(1)}, f32[1280,128]{1,0:T(8,128)S(1)}) custom-call(s32[16]{0:T(128)S(1)} %copy-done.2, f32[256,256]{1,0:T(8,128)S(1)} %get-tuple-element.137.own_ref.rotation_ref, f32[256,256]{1,0:T(8,128)S(1)} %collective-permute-done.27.other_ref, ...), custom_call_target="tpu_custom_call" | custom-call | tf_op jit(solution)/shard_map/pallas_call | solution.py:52
  102.7 4.8 %collective-permute-start.28 = (f32[1280,128]{1,0:T(8,128)S(1)}, f32[1280,128]{1,0:T(8,128)S(1)}, u32[]{:S(2)}, u32[]{:S(2)}) collective-permute-start(f32[1280,128]{1,0:T(8,128)S(1)} %get-tuple-element.144), channel_id=1, source_target_pairs={{8,0},{9,1},{10,2},{11,3},{12,4},{13,5},{14,6},{15,7},{0,8},{1,9},... | collective-permute-start | bytes 1966088 | tf_op jit(solution)/shard_map/ppermute | solution.py:522
  110.6 4.8 %collective-permute-start.31 = (f32[128,128]{1,0:T(8,128)S(1)}, f32[128,128]{1,0:T(8,128)S(1)}, u32[]{:S(2)}, u32[]{:S(2)}) collective-permute-start(f32[128,128]{1,0:T(8,128)S(1)} %get-tuple-element.148), channel_id=1, source_target_pairs={{1,0},{0,1},{3,2},{2,3},{5,4},{4,5},{7,6},{6,7},{9,8},{8,9},{11,10... | collective-permute-start | bytes 196616 | tf_op jit(solution)/shard_map/ppermute | solution.py:522
  115.4 7.1 %collective-permute-done.28.a_ref.refs_0_ = f32[1280,128]{1,0:T(8,128)S(1)} collective-permute-done((f32[1280,128]{1,0:T(8,128)S(1)}, f32[1280,128]{1,0:T(8,128)S(1)}, u32[]{:S(2)}, u32[]{:S(2)}) %collective-permute-start.28) | collective-permute-done | bytes 655392 | tf_op jit(solution)/shard_map/ppermute | solution.py:522
  123.2 1.7 %shard_map.66 = (f32[128,128]{1,0:T(8,128)S(1)}, f32[128,128]{1,0:T(8,128)S(1)}, f32[1280,128]{1,0:T(8,128)S(1)}, f32[1280,128]{1,0:T(8,128)S(1)}) custom-call(s32[16]{0:T(128)S(1)} %copy-done.2, f32[1280,128]{1,0:T(8,128)S(1)} %collective-permute-done.28.a_ref.refs_0_, f32[1280,128]{1,0:T(8,128)S(1)} %collective-permute-done.29.b_ref.refs_1_, ...), custom_call_target="tpu_custom_call" | custom-call | tf_op jit(solution)/shard_map/pallas_call | solution.py:52
  126.2 2.6 %collective-permute-start.36 = (f32[128,128]{1,0:T(8,128)S(1)}, f32[128,128]{1,0:T(8,128)S(1)}, u32[]{:S(2)}, u32[]{:S(2)}) collective-permute-start(f32[128,128]{1,0:T(8,128)S(1)} %add.37.refs_0_), channel_id=1, source_target_pairs={{6,0},{7,1},{4,2},{5,3},{2,4},{3,5},{0,6},{1,7},{14,8},{15,9},{12,... | collective-permute-start | bytes 196616 | tf_op jit(solution)/shard_map/ppermute | solution.py:522
  130.4 3.8 %collective-permute-done.36.refs_3_ = f32[128,128]{1,0:T(8,128)S(1)} collective-permute-done((f32[128,128]{1,0:T(8,128)S(1)}, f32[128,128]{1,0:T(8,128)S(1)}, u32[]{:S(2)}, u32[]{:S(2)}) %collective-permute-start.36) | collective-permute-done | bytes 65568 | tf_op jit(solution)/shard_map/ppermute | solution.py:522
  135.2 3.4 %shard_map.68 = (f32[264,256]{1,0:T(8,128)S(1)}, f32[256,256]{1,0:T(8,128)}) custom-call(s32[16]{0:T(128)S(1)} %copy-done.2, f32[128,128]{1,0:T(8,128)S(1)} %add.37.refs_0_, f32[128,128]{1,0:T(8,128)S(1)} %collective-permute-done.34.refs_1_, f32[128,128]{1,0:T(8,128)S(1)} %collective-permute-done.35.refs_2_, f32[128,128]{1,0:T(8,128)S(1)} %collective-permute-done.36.refs_3_, ...), custom_call_target="tpu_custom_call" | custom-call | tf_op jit(solution)/shard_map/pallas_call | solution.py:52
  140.2 3.0 %shard_map.69 = (f32[2048,256]{1,0:T(8,128)}, f32[512,256]{1,0:T(8,128)}, f32[1,256]{1,0:T(1,128)}) custom-call(s32[16]{0:T(128)S(1)} %copy-done.2, f32[264,256]{1,0:T(8,128)S(1)} %get-tuple-element.164.own_ref, f32[264,256]{1,0:T(8,128)S(1)} %collective-permute-done.38.other_ref, f32[1280,128]{1,0:T(8,128)S(1)} %get-tuple-element.167.refs_0_, ...), custom_call_target="tpu_custom_call" | custom-call | flops 1 | bytes 1 | tf_op jit(solution)/shard_map/pallas_call | solution.py:421
  144.7 2.0 %shard_map.70 = (f32[2048,256]{1,0:T(8,128)}, f32[512,256]{1,0:T(8,128)}) custom-call(s32[16]{0:T(128)S(1)} %copy-done.2, f32[264,256]{1,0:T(8,128)S(1)} %get-tuple-element.164.own_ref, f32[264,256]{1,0:T(8,128)S(1)} %collective-permute-done.38.other_ref, ...), custom_call_target="tpu_custom_call", output_to_operand_aliasing={{0}: (5, {}), {1}: (6, {})} | custom-call | flops 1 | bytes 1 | tf_op jit(solution)/shard_map/pallas_call | solution.py:421
  (84 shorter events, 44.0 us)
Async XLA Ops:
  5.0 27.6 %collective-permute-start.4 = (f32[768,256]{1,0:T(8,128)}, f32[768,256]{1,0:T(8,128)S(1)}, u32[]{:S(2)}, u32[]{:S(2)}) collective-permute-start(f32[768,256]{1,0:T(8,128)} %get-tuple-element.94), channel_id=1, source_target_pairs={{4,0},{5,1},{6,2},{7,3},{0,4},{1,5},{2,6},{3,7},{12,8},{13,9},{14,... | collective-permute-start | bytes 2359304 | tf_op jit(solution)/shard_map/ppermute | solution.py:522
  12.9 7.0 %collective-permute-start.1 = (f32[384,128]{1,0:T(8,128)S(1)}, f32[384,128]{1,0:T(8,128)S(1)}, u32[]{:S(2)}, u32[]{:S(2)}) collective-permute-start(f32[384,128]{1,0:T(8,128)S(1)} %add.34.own_ref), channel_id=1, source_target_pairs={{2,0},{3,1},{0,2},{1,3},{6,4},{7,5},{4,6},{5,7},{10,8},{11,9},{8,1... | collective-permute-start | bytes 589832 | tf_op jit(solution)/shard_map/ppermute | solution.py:522
  23.3 9.3 %collective-permute-start.3 = (f32[256,256]{1,0:T(8,128)S(1)}, f32[256,256]{1,0:T(8,128)S(1)}, u32[]{:S(2)}, u32[]{:S(2)}) collective-permute-start(f32[256,256]{1,0:T(8,128)S(1)} %get-tuple-element.89.rotation_ref.own_ref), channel_id=1, source_target_pairs={{4,0},{5,1},{6,2},{7,3},{0,4},{1,5},{2,6},{3,7},{12,8},{13,9},{14,... | collective-permute-start | bytes 786440 | tf_op jit(solution)/shard_map/ppermute | solution.py:522
  24.8 23.9 %collective-permute-start.2 = (f32[1024,128]{1,0:T(8,128)S(1)}, f32[1024,128]{1,0:T(8,128)S(1)}, u32[]{:S(2)}, u32[]{:S(2)}) collective-permute-start(f32[1024,128]{1,0:T(8,128)S(1)} %get-tuple-element.93.refs_1_), channel_id=1, source_target_pairs={{8,0},{9,1},{10,2},{11,3},{16,8},{17,9},{18,10},{19,11},{4,12},{5,... | collective-permute-start | bytes 1572872 | tf_op jit(solution)/shard_map/ppermute | solution.py:522
  26.1 12.7 %collective-permute-start.6 = (f32[256,256]{1,0:T(8,128)S(1)}, f32[256,256]{1,0:T(8,128)S(1)}, u32[]{:S(2)}, u32[]{:S(2)}) collective-permute-start(f32[256,256]{1,0:T(8,128)S(1)} %copy-done.3), channel_id=1, source_target_pairs={{4,0},{5,1},{6,2},{7,3},{0,4},{1,5},{2,6},{3,7},{12,8},{13,9},{14,... | collective-permute-start | bytes 786440 | tf_op jit(solution)/shard_map/ppermute | solution.py:522
  33.6 15.1 %collective-permute-start.5 = (f32[768,128]{1,0:T(8,128)S(1)}, f32[768,128]{1,0:T(8,128)S(1)}, u32[]{:S(2)}, u32[]{:S(2)}) collective-permute-start(f32[768,128]{1,0:T(8,128)S(1)} %get-tuple-element.96.refs_4_), channel_id=1, source_target_pairs={{12,4},{13,5},{14,6},{15,7},{0,8},{1,9},{2,10},{3,11},{20,12},{21,... | collective-permute-start | bytes 1179656 | tf_op jit(solution)/shard_map/ppermute | solution.py:522
  38.8 5.3 %collective-permute-start.8 = (f32[128,128]{1,0:T(8,128)S(1)}, f32[128,128]{1,0:T(8,128)S(1)}, u32[]{:S(2)}, u32[]{:S(2)}) collective-permute-start(f32[128,128]{1,0:T(8,128)S(1)} %get-tuple-element.105), channel_id=1, source_target_pairs={{4,0},{0,1},{6,2},{2,3},{5,4},{1,5},{7,6},{3,7},{12,8},{8,9},{14,1... | collective-permute-start | bytes 196616 | tf_op jit(solution)/shard_map/ppermute | solution.py:522
  39.7 8.4 %collective-permute-start.7 = (f32[256,128]{1,0:T(8,128)S(1)}, f32[256,128]{1,0:T(8,128)S(1)}, u32[]{:S(2)}, u32[]{:S(2)}) collective-permute-start(f32[256,128]{1,0:T(8,128)S(1)} %get-tuple-element.99.refs_7_), channel_id=1, source_target_pairs={{12,4},{13,5},{14,6},{15,7},{0,8},{1,9},{2,10},{3,11},{20,12},{21,... | collective-permute-start | bytes 393224 | tf_op jit(solution)/shard_map/ppermute | solution.py:522
  44.1 6.4 %collective-permute-start.9 = (f32[256,128]{1,0:T(8,128)S(1)}, f32[256,128]{1,0:T(8,128)S(1)}, u32[]{:S(2)}, u32[]{:S(2)}) collective-permute-start(f32[256,128]{1,0:T(8,128)S(1)} %get-tuple-element.106), channel_id=1, source_target_pairs={{8,0},{9,1},{10,2},{11,3},{12,4},{13,5},{14,6},{15,7},{0,8},{1,9},... | collective-permute-start | bytes 393224 | tf_op jit(solution)/shard_map/ppermute | solution.py:522
  45.8 4.8 %collective-permute-start.10 = (f32[256,128]{1,0:T(8,128)S(1)}, f32[256,128]{1,0:T(8,128)S(1)}, u32[]{:S(2)}, u32[]{:S(2)}) collective-permute-start(f32[256,128]{1,0:T(8,128)S(1)} %get-tuple-element.107), channel_id=1, source_target_pairs={{0,0},{1,1},{2,2},{3,3},{4,4},{5,5},{6,6},{7,7},{16,8},{17,9},{18,... | collective-permute-start | bytes 393224 | tf_op jit(solution)/shard_map/ppermute | solution.py:522
  50.6 4.8 %collective-permute-start.12 = (f32[128,128]{1,0:T(8,128)S(1)}, f32[128,128]{1,0:T(8,128)S(1)}, u32[]{:S(2)}, u32[]{:S(2)}) collective-permute-start(f32[128,128]{1,0:T(8,128)S(1)} %get-tuple-element.109), channel_id=1, source_target_pairs={{1,0},{0,1},{3,2},{2,3},{5,4},{4,5},{7,6},{6,7},{9,8},{8,9},{11,10... | collective-permute-start | bytes 196616 | tf_op jit(solution)/shard_map/ppermute | solution.py:522
  55.4 5.6 %collective-permute-start.15 = (f32[128,128]{1,0:T(8,128)S(1)}, f32[128,128]{1,0:T(8,128)S(1)}, u32[]{:S(2)}, u32[]{:S(2)}) collective-permute-start(f32[128,128]{1,0:T(8,128)S(1)} %add.35.refs_0_), channel_id=1, source_target_pairs={{6,0},{7,1},{4,2},{5,3},{2,4},{3,5},{0,6},{1,7},{14,8},{15,9},{12,... | collective-permute-start | bytes 196616 | tf_op jit(solution)/shard_map/ppermute | solution.py:522
  58.1 4.3 %collective-permute-start.14 = (f32[128,128]{1,0:T(8,128)S(1)}, f32[128,128]{1,0:T(8,128)S(1)}, u32[]{:S(2)}, u32[]{:S(2)}) collective-permute-start(f32[128,128]{1,0:T(8,128)S(1)} %add.35.refs_0_), channel_id=1, source_target_pairs={{4,0},{5,1},{6,2},{7,3},{0,4},{1,5},{2,6},{3,7},{12,8},{13,9},{14,... | collective-permute-start | bytes 196616 | tf_op jit(solution)/shard_map/ppermute | solution.py:522
  58.4 4.3 %collective-permute-start.13 = (f32[128,128]{1,0:T(8,128)S(1)}, f32[128,128]{1,0:T(8,128)S(1)}, u32[]{:S(2)}, u32[]{:S(2)}) collective-permute-start(f32[128,128]{1,0:T(8,128)S(1)} %add.35.refs_0_), channel_id=1, source_target_pairs={{2,0},{3,1},{0,2},{1,3},{6,4},{7,5},{4,6},{5,7},{10,8},{11,9},{8,1... | collective-permute-start | bytes 196616 | tf_op jit(solution)/shard_map/ppermute | solution.py:522
  69.5 16.2 %collective-permute-start.17 = (f32[1024,128]{1,0:T(8,128)S(1)}, f32[1024,128]{1,0:T(8,128)S(1)}, u32[]{:S(2)}, u32[]{:S(2)}) collective-permute-start(f32[1024,128]{1,0:T(8,128)S(1)} %get-tuple-element.121), channel_id=1, source_target_pairs={{8,0},{9,1},{10,2},{11,3},{12,4},{13,5},{14,6},{15,7},{0,8},{1,9},... | collective-permute-start | bytes 1572872 | tf_op jit(solution)/shard_map/ppermute | solution.py:522
  73.0 12.7 %collective-permute-start.18 = (f32[1024,128]{1,0:T(8,128)S(1)}, f32[1024,128]{1,0:T(8,128)S(1)}, u32[]{:S(2)}, u32[]{:S(2)}) collective-permute-start(f32[1024,128]{1,0:T(8,128)S(1)} %get-tuple-element.122), channel_id=1, source_target_pairs={{0,0},{1,1},{2,2},{3,3},{4,4},{5,5},{6,6},{7,7},{16,8},{17,9},{18,... | collective-permute-start | bytes 1572872 | tf_op jit(solution)/shard_map/ppermute | solution.py:522
  76.9 11.2 %collective-permute-start.20 = (f32[256,128]{1,0:T(8,128)S(1)}, f32[256,128]{1,0:T(8,128)S(1)}, u32[]{:S(2)}, u32[]{:S(2)}) collective-permute-start(f32[256,128]{1,0:T(8,128)S(1)} %get-tuple-element.131), channel_id=1, source_target_pairs={{8,0},{9,1},{10,2},{11,3},{12,4},{13,5},{14,6},{15,7},{0,8},{1,9},... | collective-permute-start | bytes 393224 | tf_op jit(solution)/shard_map/ppermute | solution.py:522
  81.2 6.8 %collective-permute-start.21 = (f32[256,128]{1,0:T(8,128)S(1)}, f32[256,128]{1,0:T(8,128)S(1)}, u32[]{:S(2)}, u32[]{:S(2)}) collective-permute-start(f32[256,128]{1,0:T(8,128)S(1)} %get-tuple-element.132), channel_id=1, source_target_pairs={{0,0},{1,1},{2,2},{3,3},{4,4},{5,5},{6,6},{7,7},{16,8},{17,9},{18,... | collective-permute-start | bytes 393224 | tf_op jit(solution)/shard_map/ppermute | solution.py:522
  81.9 5.5 %collective-permute-start.22 = (f32[128,128]{1,0:T(8,128)S(1)}, f32[128,128]{1,0:T(8,128)S(1)}, u32[]{:S(2)}, u32[]{:S(2)}) collective-permute-start(f32[128,128]{1,0:T(8,128)S(1)} %get-tuple-element.133), channel_id=1, source_target_pairs={{0,0},{8,1},{2,2},{10,3},{4,4},{12,5},{6,6},{14,7},{1,8},{16,9},{3... | collective-permute-start | bytes 196616 | tf_op jit(solution)/shard_map/ppermute | solution.py:522
  89.5 5.9 %collective-permute-start.26 = (f32[128,128]{1,0:T(8,128)S(1)}, f32[128,128]{1,0:T(8,128)S(1)}, u32[]{:S(2)}, u32[]{:S(2)}) collective-permute-start(f32[128,128]{1,0:T(8,128)S(1)} %add.36.refs_0_), channel_id=1, source_target_pairs={{6,0},{7,1},{4,2},{5,3},{2,4},{3,5},{0,6},{1,7},{14,8},{15,9},{12,... | collective-permute-start | bytes 196616 | tf_op jit(solution)/shard_map/ppermute | solution.py:522
  89.7 5.8 %collective-permute-start.25 = (f32[128,128]{1,0:T(8,128)S(1)}, f32[128,128]{1,0:T(8,128)S(1)}, u32[]{:S(2)}, u32[]{:S(2)}) collective-permute-start(f32[128,128]{1,0:T(8,128)S(1)} %add.36.refs_0_), channel_id=1, source_target_pairs={{4,0},{5,1},{6,2},{7,3},{0,4},{1,5},{2,6},{3,7},{12,8},{13,9},{14,... | collective-permute-start | bytes 196616 | tf_op jit(solution)/shard_map/ppermute | solution.py:522
  91.8 4.4 %collective-permute-start.24 = (f32[128,128]{1,0:T(8,128)S(1)}, f32[128,128]{1,0:T(8,128)S(1)}, u32[]{:S(2)}, u32[]{:S(2)}) collective-permute-start(f32[128,128]{1,0:T(8,128)S(1)} %add.36.refs_0_), channel_id=1, source_target_pairs={{2,0},{3,1},{0,2},{1,3},{6,4},{7,5},{4,6},{5,7},{10,8},{11,9},{8,1... | collective-permute-start | bytes 196616 | tf_op jit(solution)/shard_map/ppermute | solution.py:522
  102.7 19.9 %collective-permute-start.28 = (f32[1280,128]{1,0:T(8,128)S(1)}, f32[1280,128]{1,0:T(8,128)S(1)}, u32[]{:S(2)}, u32[]{:S(2)}) collective-permute-start(f32[1280,128]{1,0:T(8,128)S(1)} %get-tuple-element.144), channel_id=1, source_target_pairs={{8,0},{9,1},{10,2},{11,3},{12,4},{13,5},{14,6},{15,7},{0,8},{1,9},... | collective-permute-start | bytes 1966088 | tf_op jit(solution)/shard_map/ppermute | solution.py:522
  107.5 15.0 %collective-permute-start.29 = (f32[1280,128]{1,0:T(8,128)S(1)}, f32[1280,128]{1,0:T(8,128)S(1)}, u32[]{:S(2)}, u32[]{:S(2)}) collective-permute-start(f32[1280,128]{1,0:T(8,128)S(1)} %get-tuple-element.145), channel_id=1, source_target_pairs={{0,0},{1,1},{2,2},{3,3},{4,4},{5,5},{6,6},{7,7},{16,8},{17,9},{18,... | collective-permute-start | bytes 1966088 | tf_op jit(solution)/shard_map/ppermute | solution.py:522
  108.2 16.7 %collective-permute-start.32 = (f32[1280,128]{1,0:T(8,128)S(1)}, f32[1280,128]{1,0:T(8,128)S(1)}, u32[]{:S(2)}, u32[]{:S(2)}) collective-permute-start(f32[1280,128]{1,0:T(8,128)S(1)} %get-tuple-element.155), channel_id=1, source_target_pairs={{4,0},{5,1},{6,2},{7,3},{0,4},{1,5},{2,6},{3,7},{12,8},{13,9},{14,... | collective-permute-start | bytes 1966088 | tf_op jit(solution)/shard_map/ppermute | solution.py:522
  109.9 13.2 %collective-permute-start.30 = (f32[128,128]{1,0:T(8,128)S(1)}, f32[128,128]{1,0:T(8,128)S(1)}, u32[]{:S(2)}, u32[]{:S(2)}) collective-permute-start(f32[128,128]{1,0:T(8,128)S(1)} %get-tuple-element.147), channel_id=1, source_target_pairs={{0,0},{8,1},{2,2},{10,3},{4,4},{12,5},{6,6},{14,7},{1,8},{16,9},{3... | collective-permute-start | bytes 196616 | tf_op jit(solution)/shard_map/ppermute | solution.py:522
  110.6 12.5 %collective-permute-start.31 = (f32[128,128]{1,0:T(8,128)S(1)}, f32[128,128]{1,0:T(8,128)S(1)}, u32[]{:S(2)}, u32[]{:S(2)}) collective-permute-start(f32[128,128]{1,0:T(8,128)S(1)} %get-tuple-element.148), channel_id=1, source_target_pairs={{1,0},{0,1},{3,2},{2,3},{5,4},{4,5},{7,6},{6,7},{9,8},{8,9},{11,10... | collective-permute-start | bytes 196616 | tf_op jit(solution)/shard_map/ppermute | solution.py:522
  123.1 11.2 %collective-permute-start.37 = (f32[512,128]{1,0:T(8,128)S(1)}, f32[512,128]{1,0:T(8,128)S(1)}, u32[]{:S(2)}, u32[]{:S(2)}) collective-permute-start(f32[512,128]{1,0:T(8,128)S(1)} %shard_map.64), channel_id=1, source_target_pairs={{4,0},{5,1},{6,2},{7,3},{0,4},{1,5},{2,6},{3,7},{12,8},{13,9},{14,... | collective-permute-start | bytes 786440 | tf_op jit(solution)/shard_map/ppermute | solution.py:522
  126.2 8.0 %collective-permute-start.36 = (f32[128,128]{1,0:T(8,128)S(1)}, f32[128,128]{1,0:T(8,128)S(1)}, u32[]{:S(2)}, u32[]{:S(2)}) collective-permute-start(f32[128,128]{1,0:T(8,128)S(1)} %add.37.refs_0_), channel_id=1, source_target_pairs={{6,0},{7,1},{4,2},{5,3},{2,4},{3,5},{0,6},{1,7},{14,8},{15,9},{12,... | collective-permute-start | bytes 196616 | tf_op jit(solution)/shard_map/ppermute | solution.py:522
  128.8 5.5 %collective-permute-start.35 = (f32[128,128]{1,0:T(8,128)S(1)}, f32[128,128]{1,0:T(8,128)S(1)}, u32[]{:S(2)}, u32[]{:S(2)}) collective-permute-start(f32[128,128]{1,0:T(8,128)S(1)} %add.37.refs_0_), channel_id=1, source_target_pairs={{4,0},{5,1},{6,2},{7,3},{0,4},{1,5},{2,6},{3,7},{12,8},{13,9},{14,... | collective-permute-start | bytes 196616 | tf_op jit(solution)/shard_map/ppermute | solution.py:522
  128.9 5.5 %collective-permute-start.34 = (f32[128,128]{1,0:T(8,128)S(1)}, f32[128,128]{1,0:T(8,128)S(1)}, u32[]{:S(2)}, u32[]{:S(2)}) collective-permute-start(f32[128,128]{1,0:T(8,128)S(1)} %add.37.refs_0_), channel_id=1, source_target_pairs={{2,0},{3,1},{0,2},{1,3},{6,4},{7,5},{4,6},{5,7},{10,8},{11,9},{8,1... | collective-permute-start | bytes 196616 | tf_op jit(solution)/shard_map/ppermute | solution.py:522
  134.4 10.3 %collective-permute-start.39 = (f32[768,128]{1,0:T(8,128)S(1)}, f32[768,128]{1,0:T(8,128)S(1)}, u32[]{:S(2)}, u32[]{:S(2)}) collective-permute-start(f32[768,128]{1,0:T(8,128)S(1)} %shard_map.67), channel_id=1, source_target_pairs={{4,0},{5,1},{6,2},{7,3},{0,4},{1,5},{2,6},{3,7},{12,8},{13,9},{14,... | collective-permute-start | bytes 1179656 | tf_op jit(solution)/shard_map/ppermute | solution.py:522
  (12 other events, 36.3 us)

commit v10 on v9

--- a/solution.py
+++ b/solution.py
@@ -62,45 +62,52 @@
     )(facts, *inputs)
 
 
-def first_gram(facts, sector, half):
-    def body(f, x_ref, out_ref):
+def first_gram(sector, half):
+    def body(x_ref, out_ref):
         x = x_ref[...]
         g = dot_tn(x, x)
         out_ref[:half] = g[:half, :half]
         out_ref[half : 2 * half] = g[:half, half:]
         out_ref[2 * half :] = g[half:, half:]
 
-    return call(body, facts, [sector], shape(3 * half, half))
-
-
-def give_rows(facts, sector, top):
+    vmem = pl.BlockSpec(memory_space=pltpu.VMEM)
+    return pl.pallas_call(
+        body,
+        out_shape=shape(3 * half, half),
+        in_specs=[vmem],
+        out_specs=vmem,
+        compiler_params=pltpu.CompilerParams(vmem_limit_bytes=24 << 20),
+    )(sector)
+
+
+def give_rows(sector, top, pieces=8):
     rows, width = sector.shape
     part = rows // 2
-
-    def body(f, x_ref, top_ref, rest_ref, sems):
-        start = pl.multiple_of((1 - f[X]) * part, 8)
-        copies = [
-            pltpu.make_async_copy(
-                x_ref.at[pl.ds(start, top)], top_ref, sems.at[0]
-            ),
-            pltpu.make_async_copy(
-                x_ref.at[pl.ds(start + top, part - top)], rest_ref, sems.at[1]
-            ),
-        ]
-        for copy in copies:
-            copy.start()
+    step = part // pieces
+
+    def body(x_ref, top_ref, rest_ref, sems):
+        start = (1 - lax.axis_index("pair") % 2) * part
+        copies = []
+        for k in range(pieces):
+            at = k * step
+            target, here = (top_ref, at) if at < top else (rest_ref, at - top)
+            source = x_ref.at[pl.ds(pl.multiple_of(start + at, 8), step)]
+            copies.append(
+                pltpu.make_async_copy(
+                    source, target.at[here : here + step], sems.at[k]
+                )
+            )
+            copies[-1].start()
         for copy in copies:
             copy.wait()
 
     return pl.pallas_call(
         body,
         out_shape=(shape(top, width), shape(part - top, width)),
-        in_specs=[
-            pl.BlockSpec(memory_space=pltpu.SMEM), pl.BlockSpec(memory_space=pl.ANY)
-        ],
+        in_specs=[pl.BlockSpec(memory_space=pl.ANY)],
         out_specs=(pl.BlockSpec(memory_space=pltpu.VMEM),) * 2,
-        scratch_shapes=[pltpu.SemaphoreType.DMA((2,))],
-    )(facts, sector)
+        scratch_shapes=[pltpu.SemaphoreType.DMA((pieces,))],
+    )(sector)
 
 
 def rotate_of(gram, x_ref, e_ref):
@@ -588,9 +595,9 @@
     def together(*arrays):
         return lax.optimization_barrier(arrays)
 
-    top_give, rest_give = give_rows(facts, sector, part * 3 // 4)
+    top_give, rest_give = give_rows(sector, part * 3 // 4)
     got_top = exchange(top_give, 1, 0)
-    own = first_gram(facts, sector, half)
+    own = first_gram(sector, half)
     own = sum_rows(own + exchange(own, 0, 1))
     rotation, gram = first_rotation(facts, own, exchange(own, 0, 2), half)
 

time: 149 us -> 146 us (0.980)
  local copies, waits for them, and re-layouts: 2.12 us -> 0.17 us
    pallas_call x19 -> x18, Pallas kernels: 34.7 us -> 32.1 us  [call(): pl.pallas_call(body, out_shape=outs, in_specs=[pl.BlockSpec(memory_space=...]
    pallas_call x0 -> x1, Pallas kernels: none -> 2.15 us  [first_gram(): pl.pallas_call(body, out_shape=shape(3 * half, half), in_specs=[vmem], ou...]
where the time goes in v10:
time: 146 us; the launch traced here: 145 us
  starting transfers between devices  58.2 us (40%)
  waiting for transfers between devices  43.4 us (30%)
  Pallas kernels  41.6 us (28%)
    ppermute x40, starting transfers between devices, permute(): return lax.ppermute(block, ('pair', 'row'), moves)  58.2 us
    ppermute x40, waiting for transfers between devices, permute(): return lax.ppermute(block, ('pair', 'row'), moves)  43.4 us
    pallas_call x18, Pallas kernels, call(): pl.pallas_call(body, out_shape=outs, in_specs=[pl.BlockSpec(memory_space=...  32.1 us
    pallas_call x2, Pallas kernels, finish_call(): pl.pallas_call(body, out_shape=outs, in_specs=[pl.BlockSpec(memory_space=...  4.95 us
  transfers between devices with their start and end apart: 40, of which 23 were waited for; matrix products, arithmetic and copies ran while one was open for 0% of the time, Pallas kernels for 19%

profile of v10, /device:TPU:0, one launch (start us, length us, event | category | flops | bytes accessed | tf_op | source)
XLA Modules:
  0.0 144.8 jit_solution(11451108309890760819)
XLA Ops:
  0.6 2.5 %shard_map.52 = (f32[768,256]{1,0:T(8,128)}, f32[256,256]{1,0:T(8,128)}) custom-call(f32[2048,256]{1,0:T(8,128)} %x_ref.5), custom_call_target="tpu_custom_call" | custom-call | tf_op jit(solution)/shard_map/pallas_call | solution.py:104
  3.1 3.0 %collective-permute-start.4 = (f32[768,256]{1,0:T(8,128)}, f32[768,256]{1,0:T(8,128)S(1)}, u32[]{:S(2)}, u32[]{:S(2)}) collective-permute-start(f32[768,256]{1,0:T(8,128)} %get-tuple-element.94), channel_id=1, source_target_pairs={{4,0},{5,1},{6,2},{7,3},{0,4},{1,5},{2,6},{3,7},{12,8},{13,9},{14,... | collective-permute-start | bytes 2359304 | tf_op jit(solution)/shard_map/ppermute | solution.py:529
  6.1 2.2 %shard_map.49 = f32[384,128]{1,0:T(8,128)S(1)} custom-call(f32[2048,256]{1,0:T(8,128)S(1)} %copy-done), custom_call_target="tpu_custom_call" | custom-call | tf_op jit(solution)/shard_map/pallas_call | solution.py:74
  11.6 5.3 %collective-permute-done.1.other_ref = f32[384,128]{1,0:T(8,128)S(1)} collective-permute-done((f32[384,128]{1,0:T(8,128)S(1)}, f32[384,128]{1,0:T(8,128)S(1)}, u32[]{:S(2)}, u32[]{:S(2)}) %collective-permute-start.1) | collective-permute-done | bytes 196640 | tf_op jit(solution)/shard_map/ppermute | solution.py:529
  16.8 3.4 %shard_map.50 = (f32[256,256]{1,0:T(8,128)S(1)}, f32[256,256]{1,0:T(8,128)S(1)}) custom-call(s32[16]{0:T(128)S(1)} %constant_dynamic-update-slice_fusion.f, f32[384,128]{1,0:T(8,128)S(1)} %add.34.own_ref, f32[384,128]{1,0:T(8,128)S(1)} %collective-permute-done.1.other_ref), custom_call_target="tpu_custom_call" | custom-call | tf_op jit(solution)/shard_map/pallas_call | solution.py:52
  23.1 4.0 %collective-permute-start.6 = (f32[256,256]{1,0:T(8,128)S(1)}, f32[256,256]{1,0:T(8,128)S(1)}, u32[]{:S(2)}, u32[]{:S(2)}) collective-permute-start(f32[256,256]{1,0:T(8,128)S(1)} %copy-done.1), channel_id=1, source_target_pairs={{4,0},{5,1},{6,2},{7,3},{0,4},{1,5},{2,6},{3,7},{12,8},{13,9},{14,... | collective-permute-start | bytes 786440 | tf_op jit(solution)/shard_map/ppermute | solution.py:529
  27.1 3.2 %collective-permute-done.3.rotation_ref.other_ref = f32[256,256]{1,0:T(8,128)S(1)} collective-permute-done((f32[256,256]{1,0:T(8,128)S(1)}, f32[256,256]{1,0:T(8,128)S(1)}, u32[]{:S(2)}, u32[]{:S(2)}) %collective-permute-start.3) | collective-permute-done | bytes 262176 | tf_op jit(solution)/shard_map/ppermute | solution.py:529
  31.4 4.1 %collective-permute-start.5 = (f32[768,128]{1,0:T(8,128)S(1)}, f32[768,128]{1,0:T(8,128)S(1)}, u32[]{:S(2)}, u32[]{:S(2)}) collective-permute-start(f32[768,128]{1,0:T(8,128)S(1)} %get-tuple-element.96.refs_4_), channel_id=1, source_target_pairs={{12,4},{13,5},{14,6},{15,7},{0,8},{1,9},{2,10},{3,11},{20,12},{21,... | collective-permute-start | bytes 1179656 | tf_op jit(solution)/shard_map/ppermute | solution.py:529
  38.0 3.5 %collective-permute-start.7 = (f32[256,128]{1,0:T(8,128)S(1)}, f32[256,128]{1,0:T(8,128)S(1)}, u32[]{:S(2)}, u32[]{:S(2)}) collective-permute-start(f32[256,128]{1,0:T(8,128)S(1)} %get-tuple-element.99.refs_7_), channel_id=1, source_target_pairs={{12,4},{13,5},{14,6},{15,7},{0,8},{1,9},{2,10},{3,11},{20,12},{21,... | collective-permute-start | bytes 393224 | tf_op jit(solution)/shard_map/ppermute | solution.py:529
  46.7 1.8 %shard_map.55 = (f32[128,128]{1,0:T(8,128)S(1)}, f32[128,128]{1,0:T(8,128)S(1)}, f32[1024,128]{1,0:T(8,128)S(1)}, f32[1024,128]{1,0:T(8,128)S(1)}, f32[1024,128]{1,0:T(8,128)S(1)}, /*index=5*/f32[1024,128]{1,0:T(8,128)S(1)}) custom-call(s32[16]{0:T(128)S(1)} %constant_dynamic-update-slice_fusion.f, f32[1024,128]{1,0:T(8,128)S(1)} %get-tuple-element.90.refs_0_, ...), custom_call_target="tpu_custom_call" | custom-call | tf_op jit(solution)/shard_map/pallas_call | solution.py:52
  48.5 3.9 %collective-permute-start.12 = (f32[128,128]{1,0:T(8,128)S(1)}, f32[128,128]{1,0:T(8,128)S(1)}, u32[]{:S(2)}, u32[]{:S(2)}) collective-permute-start(f32[128,128]{1,0:T(8,128)S(1)} %get-tuple-element.109), channel_id=1, source_target_pairs={{1,0},{0,1},{3,2},{2,3},{5,4},{4,5},{7,6},{6,7},{9,8},{8,9},{11,10... | collective-permute-start | bytes 196616 | tf_op jit(solution)/shard_map/ppermute | solution.py:529
  53.3 2.8 %collective-permute-start.15 = (f32[128,128]{1,0:T(8,128)S(1)}, f32[128,128]{1,0:T(8,128)S(1)}, u32[]{:S(2)}, u32[]{:S(2)}) collective-permute-start(f32[128,128]{1,0:T(8,128)S(1)} %add.35.refs_0_), channel_id=1, source_target_pairs={{6,0},{7,1},{4,2},{5,3},{2,4},{3,5},{0,6},{1,7},{14,8},{15,9},{12,... | collective-permute-start | bytes 196616 | tf_op jit(solution)/shard_map/ppermute | solution.py:529
  56.9 1.9 %collective-permute-done.15.refs_3_ = f32[128,128]{1,0:T(8,128)S(1)} collective-permute-done((f32[128,128]{1,0:T(8,128)S(1)}, f32[128,128]{1,0:T(8,128)S(1)}, u32[]{:S(2)}, u32[]{:S(2)}) %collective-permute-start.15) | collective-permute-done | bytes 65568 | tf_op jit(solution)/shard_map/ppermute | solution.py:529
  60.6 3.4 %shard_map.58 = (f32[256,256]{1,0:T(8,128)S(1)}, f32[256,256]{1,0:T(8,128)S(1)}) custom-call(s32[16]{0:T(128)S(1)} %constant_dynamic-update-slice_fusion.f, f32[128,128]{1,0:T(8,128)S(1)} %add.35.refs_0_, f32[128,128]{1,0:T(8,128)S(1)} %collective-permute-done.13.refs_1_, f32[128,128]{1,0:T(8,128)S(1)} %collective-permute-done.14.refs_2_, ...), custom_call_target="tpu_custom_call" | custom-call | tf_op jit(solution)/shard_map/pallas_call | solution.py:52
  65.7 1.8 %shard_map.59 = (f32[1024,128]{1,0:T(8,128)S(1)}, f32[1024,128]{1,0:T(8,128)S(1)}, f32[1024,128]{1,0:T(8,128)S(1)}, f32[1024,128]{1,0:T(8,128)S(1)}, f32[256,128...) custom-call(s32[16]{0:T(128)S(1)} %constant_dynamic-update-slice_fusion.f, ...), custom_call_target="tpu_custom_call" | custom-call | tf_op jit(solution)/shard_map/pallas_call | solution.py:52
  67.5 3.8 %collective-permute-start.17 = (f32[1024,128]{1,0:T(8,128)S(1)}, f32[1024,128]{1,0:T(8,128)S(1)}, u32[]{:S(2)}, u32[]{:S(2)}) collective-permute-start(f32[1024,128]{1,0:T(8,128)S(1)} %get-tuple-element.121), channel_id=1, source_target_pairs={{8,0},{9,1},{10,2},{11,3},{12,4},{13,5},{14,6},{15,7},{0,8},{1,9},... | collective-permute-start | bytes 1572872 | tf_op jit(solution)/shard_map/ppermute | solution.py:529
  75.0 4.1 %collective-permute-start.20 = (f32[256,128]{1,0:T(8,128)S(1)}, f32[256,128]{1,0:T(8,128)S(1)}, u32[]{:S(2)}, u32[]{:S(2)}) collective-permute-start(f32[256,128]{1,0:T(8,128)S(1)} %get-tuple-element.131), channel_id=1, source_target_pairs={{8,0},{9,1},{10,2},{11,3},{12,4},{13,5},{14,6},{15,7},{0,8},{1,9},... | collective-permute-start | bytes 393224 | tf_op jit(solution)/shard_map/ppermute | solution.py:529
  80.5 3.4 %collective-permute-done.17.refs_0_ = f32[1024,128]{1,0:T(8,128)S(1)} collective-permute-done((f32[1024,128]{1,0:T(8,128)S(1)}, f32[1024,128]{1,0:T(8,128)S(1)}, u32[]{:S(2)}, u32[]{:S(2)}) %collective-permute-start.17) | collective-permute-done | bytes 524320 | tf_op jit(solution)/shard_map/ppermute | solution.py:529
  83.9 1.7 %shard_map.60 = (f32[128,128]{1,0:T(8,128)S(1)}, f32[128,128]{1,0:T(8,128)S(1)}, f32[1024,128]{1,0:T(8,128)S(1)}, f32[1024,128]{1,0:T(8,128)S(1)}) custom-call(s32[16]{0:T(128)S(1)} %constant_dynamic-update-slice_fusion.f, f32[1024,128]{1,0:T(8,128)S(1)} %collective-permute-done.17.refs_0_, f32[1024,128]{1,0:T(8,128)S(1)} %collective-permute-done.18.refs_1_, ...), custom_call_target="tpu_custom_call" | custom-call | tf_op jit(solution)/shard_map/pallas_call | solution.py:52
  88.2 1.8 %collective-permute-start.25 = (f32[128,128]{1,0:T(8,128)S(1)}, f32[128,128]{1,0:T(8,128)S(1)}, u32[]{:S(2)}, u32[]{:S(2)}) collective-permute-start(f32[128,128]{1,0:T(8,128)S(1)} %add.36.refs_0_), channel_id=1, source_target_pairs={{4,0},{5,1},{6,2},{7,3},{0,4},{1,5},{2,6},{3,7},{12,8},{13,9},{14,... | collective-permute-start | bytes 196616 | tf_op jit(solution)/shard_map/ppermute | solution.py:529
  91.3 2.3 %collective-permute-done.26.refs_3_ = f32[128,128]{1,0:T(8,128)S(1)} collective-permute-done((f32[128,128]{1,0:T(8,128)S(1)}, f32[128,128]{1,0:T(8,128)S(1)}, u32[]{:S(2)}, u32[]{:S(2)}) %collective-permute-start.26) | collective-permute-done | bytes 65568 | tf_op jit(solution)/shard_map/ppermute | solution.py:529
  94.4 3.0 %shard_map.62 = (f32[256,256]{1,0:T(8,128)S(1)}, f32[256,256]{1,0:T(8,128)S(1)}) custom-call(s32[16]{0:T(128)S(1)} %constant_dynamic-update-slice_fusion.f, f32[128,128]{1,0:T(8,128)S(1)} %add.36.refs_0_, f32[128,128]{1,0:T(8,128)S(1)} %collective-permute-done.24.refs_1_, f32[128,128]{1,0:T(8,128)S(1)} %collective-permute-done.25.refs_2_, ...), custom_call_target="tpu_custom_call" | custom-call | tf_op jit(solution)/shard_map/pallas_call | solution.py:52
  99.1 1.8 %shard_map.63 = (f32[1280,128]{1,0:T(8,128)S(1)}, f32[1280,128]{1,0:T(8,128)S(1)}, f32[1280,128]{1,0:T(8,128)S(1)}, f32[1280,128]{1,0:T(8,128)S(1)}, f32[1280,128]{1,0:T(8,128)S(1)}) custom-call(s32[16]{0:T(128)S(1)} %constant_dynamic-update-slice_fusion.f, f32[256,256]{1,0:T(8,128)S(1)} %get-tuple-element.137.own_ref.rotation_ref, ...), custom_call_target="tpu_custom_call" | custom-call | tf_op jit(solution)/shard_map/pallas_call | solution.py:52
  100.9 4.6 %collective-permute-start.28 = (f32[1280,128]{1,0:T(8,128)S(1)}, f32[1280,128]{1,0:T(8,128)S(1)}, u32[]{:S(2)}, u32[]{:S(2)}) collective-permute-start(f32[1280,128]{1,0:T(8,128)S(1)} %get-tuple-element.144), channel_id=1, source_target_pairs={{8,0},{9,1},{10,2},{11,3},{12,4},{13,5},{14,6},{15,7},{0,8},{1,9},... | collective-permute-start | bytes 1966088 | tf_op jit(solution)/shard_map/ppermute | solution.py:529
  108.5 4.8 %collective-permute-start.31 = (f32[128,128]{1,0:T(8,128)S(1)}, f32[128,128]{1,0:T(8,128)S(1)}, u32[]{:S(2)}, u32[]{:S(2)}) collective-permute-start(f32[128,128]{1,0:T(8,128)S(1)} %get-tuple-element.148), channel_id=1, source_target_pairs={{1,0},{0,1},{3,2},{2,3},{5,4},{4,5},{7,6},{6,7},{9,8},{8,9},{11,10... | collective-permute-start | bytes 196616 | tf_op jit(solution)/shard_map/ppermute | solution.py:529
  113.4 7.1 %collective-permute-done.28.a_ref.refs_0_ = f32[1280,128]{1,0:T(8,128)S(1)} collective-permute-done((f32[1280,128]{1,0:T(8,128)S(1)}, f32[1280,128]{1,0:T(8,128)S(1)}, u32[]{:S(2)}, u32[]{:S(2)}) %collective-permute-start.28) | collective-permute-done | bytes 655392 | tf_op jit(solution)/shard_map/ppermute | solution.py:529
  121.2 1.7 %shard_map.66 = (f32[128,128]{1,0:T(8,128)S(1)}, f32[128,128]{1,0:T(8,128)S(1)}, f32[1280,128]{1,0:T(8,128)S(1)}, f32[1280,128]{1,0:T(8,128)S(1)}) custom-call(s32[16]{0:T(128)S(1)} %constant_dynamic-update-slice_fusion.f, f32[1280,128]{1,0:T(8,128)S(1)} %collective-permute-done.28.a_ref.refs_0_, f32[1280,128]{1,0:T(8,128)S(1)} %collective-permute-done.29.b_ref.refs_1_, ...), custom_call_target="tpu_custom_call" | custom-call | tf_op jit(solution)/shard_map/pallas_call | solution.py:52
  124.2 2.6 %collective-permute-start.36 = (f32[128,128]{1,0:T(8,128)S(1)}, f32[128,128]{1,0:T(8,128)S(1)}, u32[]{:S(2)}, u32[]{:S(2)}) collective-permute-start(f32[128,128]{1,0:T(8,128)S(1)} %add.37.refs_0_), channel_id=1, source_target_pairs={{6,0},{7,1},{4,2},{5,3},{2,4},{3,5},{0,6},{1,7},{14,8},{15,9},{12,... | collective-permute-start | bytes 196616 | tf_op jit(solution)/shard_map/ppermute | solution.py:529
  128.4 3.8 %collective-permute-done.36.refs_3_ = f32[128,128]{1,0:T(8,128)S(1)} collective-permute-done((f32[128,128]{1,0:T(8,128)S(1)}, f32[128,128]{1,0:T(8,128)S(1)}, u32[]{:S(2)}, u32[]{:S(2)}) %collective-permute-start.36) | collective-permute-done | bytes 65568 | tf_op jit(solution)/shard_map/ppermute | solution.py:529
  133.2 3.4 %shard_map.68 = (f32[264,256]{1,0:T(8,128)S(1)}, f32[256,256]{1,0:T(8,128)}) custom-call(s32[16]{0:T(128)S(1)} %constant_dynamic-update-slice_fusion.f, f32[128,128]{1,0:T(8,128)S(1)} %add.37.refs_0_, f32[128,128]{1,0:T(8,128)S(1)} %collective-permute-done.34.refs_1_, f32[128,128]{1,0:T(8,128)S(1)} %collective-permute-done.35.refs_2_, ...), custom_call_target="tpu_custom_call" | custom-call | tf_op jit(solution)/shard_map/pallas_call | solution.py:52
  138.2 3.0 %shard_map.69 = (f32[2048,256]{1,0:T(8,128)}, f32[512,256]{1,0:T(8,128)}, f32[1,256]{1,0:T(1,128)}) custom-call(s32[16]{0:T(128)S(1)} %constant_dynamic-update-slice_fusion.f, f32[264,256]{1,0:T(8,128)S(1)} %get-tuple-element.164.own_ref, f32[264,256]{1,0:T(8,128)S(1)} %collective-permute-done.38.other_ref, f32[1280,128]{1,0:T(8,128)S(1)} %get-tuple-element.167.refs_0_, ...), custom_call_target="tpu_custom_call" | custom-call | flops 1 | bytes 1 | tf_op jit(solution)/shard_map/pallas_call | solution.py:428
  142.7 2.0 %shard_map.70 = (f32[2048,256]{1,0:T(8,128)}, f32[512,256]{1,0:T(8,128)}) custom-call(s32[16]{0:T(128)S(1)} %constant_dynamic-update-slice_fusion.f, f32[264,256]{1,0:T(8,128)S(1)} %get-tuple-element.164.own_ref, f32[264,256]{1,0:T(8,128)S(1)} %collective-permute-done.38.other_ref, ...), custom_call_target="tpu_custom_call", output_to_operand_aliasing={{0}: (5, {}), {1}: (6, {})} | custom-call | flops 1 | bytes 1 | tf_op jit(solution)/shard_map/pallas_call | solution.py:428
  (82 shorter events, 41.9 us)
Async XLA Ops:
  3.1 27.2 %collective-permute-start.4 = (f32[768,256]{1,0:T(8,128)}, f32[768,256]{1,0:T(8,128)S(1)}, u32[]{:S(2)}, u32[]{:S(2)}) collective-permute-start(f32[768,256]{1,0:T(8,128)} %get-tuple-element.94), channel_id=1, source_target_pairs={{4,0},{5,1},{6,2},{7,3},{0,4},{1,5},{2,6},{3,7},{12,8},{13,9},{14,... | collective-permute-start | bytes 2359304 | tf_op jit(solution)/shard_map/ppermute | solution.py:529
  9.8 7.0 %collective-permute-start.1 = (f32[384,128]{1,0:T(8,128)S(1)}, f32[384,128]{1,0:T(8,128)S(1)}, u32[]{:S(2)}, u32[]{:S(2)}) collective-permute-start(f32[384,128]{1,0:T(8,128)S(1)} %add.34.own_ref), channel_id=1, source_target_pairs={{2,0},{3,1},{0,2},{1,3},{6,4},{7,5},{4,6},{5,7},{10,8},{11,9},{8,1... | collective-permute-start | bytes 589832 | tf_op jit(solution)/shard_map/ppermute | solution.py:529
  20.3 10.0 %collective-permute-start.3 = (f32[256,256]{1,0:T(8,128)S(1)}, f32[256,256]{1,0:T(8,128)S(1)}, u32[]{:S(2)}, u32[]{:S(2)}) collective-permute-start(f32[256,256]{1,0:T(8,128)S(1)} %get-tuple-element.89.rotation_ref.own_ref), channel_id=1, source_target_pairs={{4,0},{5,1},{6,2},{7,3},{0,4},{1,5},{2,6},{3,7},{12,8},{13,9},{14,... | collective-permute-start | bytes 786440 | tf_op jit(solution)/shard_map/ppermute | solution.py:529
  21.8 24.8 %collective-permute-start.2 = (f32[1024,128]{1,0:T(8,128)S(1)}, f32[1024,128]{1,0:T(8,128)S(1)}, u32[]{:S(2)}, u32[]{:S(2)}) collective-permute-start(f32[1024,128]{1,0:T(8,128)S(1)} %get-tuple-element.93.refs_1_), channel_id=1, source_target_pairs={{8,0},{9,1},{10,2},{11,3},{16,8},{17,9},{18,10},{19,11},{4,12},{5,... | collective-permute-start | bytes 1572872 | tf_op jit(solution)/shard_map/ppermute | solution.py:529
  23.1 14.0 %collective-permute-start.6 = (f32[256,256]{1,0:T(8,128)S(1)}, f32[256,256]{1,0:T(8,128)S(1)}, u32[]{:S(2)}, u32[]{:S(2)}) collective-permute-start(f32[256,256]{1,0:T(8,128)S(1)} %copy-done.1), channel_id=1, source_target_pairs={{4,0},{5,1},{6,2},{7,3},{0,4},{1,5},{2,6},{3,7},{12,8},{13,9},{14,... | collective-permute-start | bytes 786440 | tf_op jit(solution)/shard_map/ppermute | solution.py:529
  31.4 15.3 %collective-permute-start.5 = (f32[768,128]{1,0:T(8,128)S(1)}, f32[768,128]{1,0:T(8,128)S(1)}, u32[]{:S(2)}, u32[]{:S(2)}) collective-permute-start(f32[768,128]{1,0:T(8,128)S(1)} %get-tuple-element.96.refs_4_), channel_id=1, source_target_pairs={{12,4},{13,5},{14,6},{15,7},{0,8},{1,9},{2,10},{3,11},{20,12},{21,... | collective-permute-start | bytes 1179656 | tf_op jit(solution)/shard_map/ppermute | solution.py:529
  37.1 5.4 %collective-permute-start.8 = (f32[128,128]{1,0:T(8,128)S(1)}, f32[128,128]{1,0:T(8,128)S(1)}, u32[]{:S(2)}, u32[]{:S(2)}) collective-permute-start(f32[128,128]{1,0:T(8,128)S(1)} %get-tuple-element.105), channel_id=1, source_target_pairs={{4,0},{0,1},{6,2},{2,3},{5,4},{1,5},{7,6},{3,7},{12,8},{8,9},{14,1... | collective-permute-start | bytes 196616 | tf_op jit(solution)/shard_map/ppermute | solution.py:529
  38.0 8.0 %collective-permute-start.7 = (f32[256,128]{1,0:T(8,128)S(1)}, f32[256,128]{1,0:T(8,128)S(1)}, u32[]{:S(2)}, u32[]{:S(2)}) collective-permute-start(f32[256,128]{1,0:T(8,128)S(1)} %get-tuple-element.99.refs_7_), channel_id=1, source_target_pairs={{12,4},{13,5},{14,6},{15,7},{0,8},{1,9},{2,10},{3,11},{20,12},{21,... | collective-permute-start | bytes 393224 | tf_op jit(solution)/shard_map/ppermute | solution.py:529
  42.4 6.1 %collective-permute-start.9 = (f32[256,128]{1,0:T(8,128)S(1)}, f32[256,128]{1,0:T(8,128)S(1)}, u32[]{:S(2)}, u32[]{:S(2)}) collective-permute-start(f32[256,128]{1,0:T(8,128)S(1)} %get-tuple-element.106), channel_id=1, source_target_pairs={{8,0},{9,1},{10,2},{11,3},{12,4},{13,5},{14,6},{15,7},{0,8},{1,9},... | collective-permute-start | bytes 393224 | tf_op jit(solution)/shard_map/ppermute | solution.py:529
  44.1 4.4 %collective-permute-start.10 = (f32[256,128]{1,0:T(8,128)S(1)}, f32[256,128]{1,0:T(8,128)S(1)}, u32[]{:S(2)}, u32[]{:S(2)}) collective-permute-start(f32[256,128]{1,0:T(8,128)S(1)} %get-tuple-element.107), channel_id=1, source_target_pairs={{0,0},{1,1},{2,2},{3,3},{4,4},{5,5},{6,6},{7,7},{16,8},{17,9},{18,... | collective-permute-start | bytes 393224 | tf_op jit(solution)/shard_map/ppermute | solution.py:529
  48.5 4.8 %collective-permute-start.12 = (f32[128,128]{1,0:T(8,128)S(1)}, f32[128,128]{1,0:T(8,128)S(1)}, u32[]{:S(2)}, u32[]{:S(2)}) collective-permute-start(f32[128,128]{1,0:T(8,128)S(1)} %get-tuple-element.109), channel_id=1, source_target_pairs={{1,0},{0,1},{3,2},{2,3},{5,4},{4,5},{7,6},{6,7},{9,8},{8,9},{11,10... | collective-permute-start | bytes 196616 | tf_op jit(solution)/shard_map/ppermute | solution.py:529
  53.3 5.4 %collective-permute-start.15 = (f32[128,128]{1,0:T(8,128)S(1)}, f32[128,128]{1,0:T(8,128)S(1)}, u32[]{:S(2)}, u32[]{:S(2)}) collective-permute-start(f32[128,128]{1,0:T(8,128)S(1)} %add.35.refs_0_), channel_id=1, source_target_pairs={{6,0},{7,1},{4,2},{5,3},{2,4},{3,5},{0,6},{1,7},{14,8},{15,9},{12,... | collective-permute-start | bytes 196616 | tf_op jit(solution)/shard_map/ppermute | solution.py:529
  56.2 4.3 %collective-permute-start.14 = (f32[128,128]{1,0:T(8,128)S(1)}, f32[128,128]{1,0:T(8,128)S(1)}, u32[]{:S(2)}, u32[]{:S(2)}) collective-permute-start(f32[128,128]{1,0:T(8,128)S(1)} %add.35.refs_0_), channel_id=1, source_target_pairs={{4,0},{5,1},{6,2},{7,3},{0,4},{1,5},{2,6},{3,7},{12,8},{13,9},{14,... | collective-permute-start | bytes 196616 | tf_op jit(solution)/shard_map/ppermute | solution.py:529
  56.4 4.3 %collective-permute-start.13 = (f32[128,128]{1,0:T(8,128)S(1)}, f32[128,128]{1,0:T(8,128)S(1)}, u32[]{:S(2)}, u32[]{:S(2)}) collective-permute-start(f32[128,128]{1,0:T(8,128)S(1)} %add.35.refs_0_), channel_id=1, source_target_pairs={{2,0},{3,1},{0,2},{1,3},{6,4},{7,5},{4,6},{5,7},{10,8},{11,9},{8,1... | collective-permute-start | bytes 196616 | tf_op jit(solution)/shard_map/ppermute | solution.py:529
  67.5 16.5 %collective-permute-start.17 = (f32[1024,128]{1,0:T(8,128)S(1)}, f32[1024,128]{1,0:T(8,128)S(1)}, u32[]{:S(2)}, u32[]{:S(2)}) collective-permute-start(f32[1024,128]{1,0:T(8,128)S(1)} %get-tuple-element.121), channel_id=1, source_target_pairs={{8,0},{9,1},{10,2},{11,3},{12,4},{13,5},{14,6},{15,7},{0,8},{1,9},... | collective-permute-start | bytes 1572872 | tf_op jit(solution)/shard_map/ppermute | solution.py:529
  71.2 12.7 %collective-permute-start.18 = (f32[1024,128]{1,0:T(8,128)S(1)}, f32[1024,128]{1,0:T(8,128)S(1)}, u32[]{:S(2)}, u32[]{:S(2)}) collective-permute-start(f32[1024,128]{1,0:T(8,128)S(1)} %get-tuple-element.122), channel_id=1, source_target_pairs={{0,0},{1,1},{2,2},{3,3},{4,4},{5,5},{6,6},{7,7},{16,8},{17,9},{18,... | collective-permute-start | bytes 1572872 | tf_op jit(solution)/shard_map/ppermute | solution.py:529
  75.0 11.2 %collective-permute-start.20 = (f32[256,128]{1,0:T(8,128)S(1)}, f32[256,128]{1,0:T(8,128)S(1)}, u32[]{:S(2)}, u32[]{:S(2)}) collective-permute-start(f32[256,128]{1,0:T(8,128)S(1)} %get-tuple-element.131), channel_id=1, source_target_pairs={{8,0},{9,1},{10,2},{11,3},{12,4},{13,5},{14,6},{15,7},{0,8},{1,9},... | collective-permute-start | bytes 393224 | tf_op jit(solution)/shard_map/ppermute | solution.py:529
  79.2 7.1 %collective-permute-start.21 = (f32[256,128]{1,0:T(8,128)S(1)}, f32[256,128]{1,0:T(8,128)S(1)}, u32[]{:S(2)}, u32[]{:S(2)}) collective-permute-start(f32[256,128]{1,0:T(8,128)S(1)} %get-tuple-element.132), channel_id=1, source_target_pairs={{0,0},{1,1},{2,2},{3,3},{4,4},{5,5},{6,6},{7,7},{16,8},{17,9},{18,... | collective-permute-start | bytes 393224 | tf_op jit(solution)/shard_map/ppermute | solution.py:529
  79.8 5.8 %collective-permute-start.22 = (f32[128,128]{1,0:T(8,128)S(1)}, f32[128,128]{1,0:T(8,128)S(1)}, u32[]{:S(2)}, u32[]{:S(2)}) collective-permute-start(f32[128,128]{1,0:T(8,128)S(1)} %get-tuple-element.133), channel_id=1, source_target_pairs={{0,0},{8,1},{2,2},{10,3},{4,4},{12,5},{6,6},{14,7},{1,8},{16,9},{3... | collective-permute-start | bytes 196616 | tf_op jit(solution)/shard_map/ppermute | solution.py:529
  87.7 5.9 %collective-permute-start.26 = (f32[128,128]{1,0:T(8,128)S(1)}, f32[128,128]{1,0:T(8,128)S(1)}, u32[]{:S(2)}, u32[]{:S(2)}) collective-permute-start(f32[128,128]{1,0:T(8,128)S(1)} %add.36.refs_0_), channel_id=1, source_target_pairs={{6,0},{7,1},{4,2},{5,3},{2,4},{3,5},{0,6},{1,7},{14,8},{15,9},{12,... | collective-permute-start | bytes 196616 | tf_op jit(solution)/shard_map/ppermute | solution.py:529
  88.2 5.5 %collective-permute-start.25 = (f32[128,128]{1,0:T(8,128)S(1)}, f32[128,128]{1,0:T(8,128)S(1)}, u32[]{:S(2)}, u32[]{:S(2)}) collective-permute-start(f32[128,128]{1,0:T(8,128)S(1)} %add.36.refs_0_), channel_id=1, source_target_pairs={{4,0},{5,1},{6,2},{7,3},{0,4},{1,5},{2,6},{3,7},{12,8},{13,9},{14,... | collective-permute-start | bytes 196616 | tf_op jit(solution)/shard_map/ppermute | solution.py:529
  90.0 4.5 %collective-permute-start.24 = (f32[128,128]{1,0:T(8,128)S(1)}, f32[128,128]{1,0:T(8,128)S(1)}, u32[]{:S(2)}, u32[]{:S(2)}) collective-permute-start(f32[128,128]{1,0:T(8,128)S(1)} %add.36.refs_0_), channel_id=1, source_target_pairs={{2,0},{3,1},{0,2},{1,3},{6,4},{7,5},{4,6},{5,7},{10,8},{11,9},{8,1... | collective-permute-start | bytes 196616 | tf_op jit(solution)/shard_map/ppermute | solution.py:529
  100.9 19.6 %collective-permute-start.28 = (f32[1280,128]{1,0:T(8,128)S(1)}, f32[1280,128]{1,0:T(8,128)S(1)}, u32[]{:S(2)}, u32[]{:S(2)}) collective-permute-start(f32[1280,128]{1,0:T(8,128)S(1)} %get-tuple-element.144), channel_id=1, source_target_pairs={{8,0},{9,1},{10,2},{11,3},{12,4},{13,5},{14,6},{15,7},{0,8},{1,9},... | collective-permute-start | bytes 1966088 | tf_op jit(solution)/shard_map/ppermute | solution.py:529
  105.5 15.0 %collective-permute-start.29 = (f32[1280,128]{1,0:T(8,128)S(1)}, f32[1280,128]{1,0:T(8,128)S(1)}, u32[]{:S(2)}, u32[]{:S(2)}) collective-permute-start(f32[1280,128]{1,0:T(8,128)S(1)} %get-tuple-element.145), channel_id=1, source_target_pairs={{0,0},{1,1},{2,2},{3,3},{4,4},{5,5},{6,6},{7,7},{16,8},{17,9},{18,... | collective-permute-start | bytes 1966088 | tf_op jit(solution)/shard_map/ppermute | solution.py:529
  106.2 16.7 %collective-permute-start.32 = (f32[1280,128]{1,0:T(8,128)S(1)}, f32[1280,128]{1,0:T(8,128)S(1)}, u32[]{:S(2)}, u32[]{:S(2)}) collective-permute-start(f32[1280,128]{1,0:T(8,128)S(1)} %get-tuple-element.155), channel_id=1, source_target_pairs={{4,0},{5,1},{6,2},{7,3},{0,4},{1,5},{2,6},{3,7},{12,8},{13,9},{14,... | collective-permute-start | bytes 1966088 | tf_op jit(solution)/shard_map/ppermute | solution.py:529
  107.9 13.2 %collective-permute-start.30 = (f32[128,128]{1,0:T(8,128)S(1)}, f32[128,128]{1,0:T(8,128)S(1)}, u32[]{:S(2)}, u32[]{:S(2)}) collective-permute-start(f32[128,128]{1,0:T(8,128)S(1)} %get-tuple-element.147), channel_id=1, source_target_pairs={{0,0},{8,1},{2,2},{10,3},{4,4},{12,5},{6,6},{14,7},{1,8},{16,9},{3... | collective-permute-start | bytes 196616 | tf_op jit(solution)/shard_map/ppermute | solution.py:529
  108.5 12.5 %collective-permute-start.31 = (f32[128,128]{1,0:T(8,128)S(1)}, f32[128,128]{1,0:T(8,128)S(1)}, u32[]{:S(2)}, u32[]{:S(2)}) collective-permute-start(f32[128,128]{1,0:T(8,128)S(1)} %get-tuple-element.148), channel_id=1, source_target_pairs={{1,0},{0,1},{3,2},{2,3},{5,4},{4,5},{7,6},{6,7},{9,8},{8,9},{11,10... | collective-permute-start | bytes 196616 | tf_op jit(solution)/shard_map/ppermute | solution.py:529
  121.1 11.2 %collective-permute-start.37 = (f32[512,128]{1,0:T(8,128)S(1)}, f32[512,128]{1,0:T(8,128)S(1)}, u32[]{:S(2)}, u32[]{:S(2)}) collective-permute-start(f32[512,128]{1,0:T(8,128)S(1)} %shard_map.64), channel_id=1, source_target_pairs={{4,0},{5,1},{6,2},{7,3},{0,4},{1,5},{2,6},{3,7},{12,8},{13,9},{14,... | collective-permute-start | bytes 786440 | tf_op jit(solution)/shard_map/ppermute | solution.py:529
  124.2 8.0 %collective-permute-start.36 = (f32[128,128]{1,0:T(8,128)S(1)}, f32[128,128]{1,0:T(8,128)S(1)}, u32[]{:S(2)}, u32[]{:S(2)}) collective-permute-start(f32[128,128]{1,0:T(8,128)S(1)} %add.37.refs_0_), channel_id=1, source_target_pairs={{6,0},{7,1},{4,2},{5,3},{2,4},{3,5},{0,6},{1,7},{14,8},{15,9},{12,... | collective-permute-start | bytes 196616 | tf_op jit(solution)/shard_map/ppermute | solution.py:529
  126.8 5.5 %collective-permute-start.35 = (f32[128,128]{1,0:T(8,128)S(1)}, f32[128,128]{1,0:T(8,128)S(1)}, u32[]{:S(2)}, u32[]{:S(2)}) collective-permute-start(f32[128,128]{1,0:T(8,128)S(1)} %add.37.refs_0_), channel_id=1, source_target_pairs={{4,0},{5,1},{6,2},{7,3},{0,4},{1,5},{2,6},{3,7},{12,8},{13,9},{14,... | collective-permute-start | bytes 196616 | tf_op jit(solution)/shard_map/ppermute | solution.py:529
  126.8 5.5 %collective-permute-start.34 = (f32[128,128]{1,0:T(8,128)S(1)}, f32[128,128]{1,0:T(8,128)S(1)}, u32[]{:S(2)}, u32[]{:S(2)}) collective-permute-start(f32[128,128]{1,0:T(8,128)S(1)} %add.37.refs_0_), channel_id=1, source_target_pairs={{2,0},{3,1},{0,2},{1,3},{6,4},{7,5},{4,6},{5,7},{10,8},{11,9},{8,1... | collective-permute-start | bytes 196616 | tf_op jit(solution)/shard_map/ppermute | solution.py:529
  132.3 10.3 %collective-permute-start.39 = (f32[768,128]{1,0:T(8,128)S(1)}, f32[768,128]{1,0:T(8,128)S(1)}, u32[]{:S(2)}, u32[]{:S(2)}) collective-permute-start(f32[768,128]{1,0:T(8,128)S(1)} %shard_map.67), channel_id=1, source_target_pairs={{4,0},{5,1},{6,2},{7,3},{0,4},{1,5},{2,6},{3,7},{12,8},{13,9},{14,... | collective-permute-start | bytes 1179656 | tf_op jit(solution)/shard_map/ppermute | solution.py:529
  (11 other events, 44.0 us)

commit v11 on v10

--- a/solution.py
+++ b/solution.py
@@ -618,9 +618,7 @@
             vectors = list(
                 first_vectors(facts, rotation, other_rotation, vector_rows, half)
             )
-            vectors[0], vectors[1], diagonals[1] = together(
-                vectors[0], vectors[1], diagonals[1]
-            )
+            own_rows[2], *diagonals = together(own_rows[2], *diagonals)
             *grams, up_0, nat_l, nat_u, low_1 = first_cross_gram(
                 facts, own_rows, other_rows, half
             )
@@ -641,20 +639,17 @@
                 )
                 got_top = exchange(top_give, 1, 0)
             else:
-                vectors[0], vectors[1], diagonals[1] = together(
-                    vectors[0], vectors[1], diagonals[1]
-                )
+                *got, diagonals[0], diagonals[1] = together(*got, *diagonals)
             *grams, up_0, low_1 = cross_gram(facts, got, [nat_l, nat_u], part, half)
         blocks = [up_0, nat_l, nat_u, low_1]
         if last_move:
             grams[1], native = together(grams[1], native)
         else:
             vector_a, vector_b, *kept = vectors
-            grams[1], vector_a, vector_b, diagonals[0] = together(
-                grams[1], swap(vector_a, 0), swap(vector_b, 1), diagonals[0]
-            )
-            vectors = [vector_a, vector_b] + kept
+            vectors = [swap(vector_a, 0), swap(vector_b, 1)] + kept
         own = sum_rows(grams[0] + exchange(grams[1], 0, 1))
+        if not last_move:
+            own, vectors[0], vectors[1] = together(own, vectors[0], vectors[1])
         parts = [own, exchange(own, 0, 2), exchange(own, 1, 0), exchange(own, 1, 2)]
         if last_move:
             rest_give = give(facts, got, top, part + vector_rows, half)

time: 146 us -> 148 us (1.014)
  starting transfers between devices: 58.2 us -> 62.9 us
  waiting for transfers between devices: 43.4 us -> 41.2 us
    ppermute x40, starting transfers between devices: 58.2 us -> 62.9 us  [permute(): return lax.ppermute(block, ('pair', 'row'), moves)]
    ppermute x40, waiting for transfers between devices: 43.4 us -> 41.2 us  [permute(): return lax.ppermute(block, ('pair', 'row'), moves)]
  transfers between devices with their start and end apart: 40 -> 40, of which waited for: 23 -> 19; matrix products, arithmetic and copies ran while one was open for 0% -> 0% of each run, Pallas kernels for 19% -> 18%
where the time goes in v11:
time: 148 us; the launch traced here: 147 us
  starting transfers between devices  62.9 us (42%)
  Pallas kernels  41.6 us (28%)
  waiting for transfers between devices  41.2 us (28%)
    ppermute x40, starting transfers between devices, permute(): return lax.ppermute(block, ('pair', 'row'), moves)  62.9 us
    ppermute x40, waiting for transfers between devices, permute(): return lax.ppermute(block, ('pair', 'row'), moves)  41.2 us
    pallas_call x18, Pallas kernels, call(): pl.pallas_call(body, out_shape=outs, in_specs=[pl.BlockSpec(memory_space=...  32.1 us
    pallas_call x2, Pallas kernels, finish_call(): pl.pallas_call(body, out_shape=outs, in_specs=[pl.BlockSpec(memory_space=...  4.95 us
  transfers between devices with their start and end apart: 40, of which 19 were waited for; matrix products, arithmetic and copies ran while one was open for 0% of the time, Pallas kernels for 18%

profile of v11, /device:TPU:0, one launch (start us, length us, event | category | flops | bytes accessed | tf_op | source)
XLA Modules:
  0.0 147.3 jit_solution(17815626679584972874)
XLA Ops:
  0.6 2.5 %shard_map.52 = (f32[768,256]{1,0:T(8,128)}, f32[256,256]{1,0:T(8,128)}) custom-call(f32[2048,256]{1,0:T(8,128)} %x_ref.5), custom_call_target="tpu_custom_call" | custom-call | tf_op jit(solution)/shard_map/pallas_call | solution.py:104
  3.1 3.0 %collective-permute-start.6 = (f32[768,256]{1,0:T(8,128)}, f32[768,256]{1,0:T(8,128)S(1)}, u32[]{:S(2)}, u32[]{:S(2)}) collective-permute-start(f32[768,256]{1,0:T(8,128)} %get-tuple-element.97), channel_id=1, source_target_pairs={{4,0},{5,1},{6,2},{7,3},{0,4},{1,5},{2,6},{3,7},{12,8},{13,9},{14,... | collective-permute-start | bytes 2359304 | tf_op jit(solution)/shard_map/ppermute | solution.py:529
  6.1 2.2 %shard_map.49 = f32[384,128]{1,0:T(8,128)S(1)} custom-call(f32[2048,256]{1,0:T(8,128)S(1)} %copy-done), custom_call_target="tpu_custom_call" | custom-call | tf_op jit(solution)/shard_map/pallas_call | solution.py:74
  11.6 5.3 %collective-permute-done.1.other_ref = f32[384,128]{1,0:T(8,128)S(1)} collective-permute-done((f32[384,128]{1,0:T(8,128)S(1)}, f32[384,128]{1,0:T(8,128)S(1)}, u32[]{:S(2)}, u32[]{:S(2)}) %collective-permute-start.1) | collective-permute-done | bytes 196640 | tf_op jit(solution)/shard_map/ppermute | solution.py:529
  16.8 3.4 %shard_map.50 = (f32[256,256]{1,0:T(8,128)S(1)}, f32[256,256]{1,0:T(8,128)S(1)}) custom-call(s32[16]{0:T(128)S(1)} %constant_dynamic-update-slice_fusion.f, f32[384,128]{1,0:T(8,128)S(1)} %add.34.own_ref, f32[384,128]{1,0:T(8,128)S(1)} %collective-permute-done.1.other_ref), custom_call_target="tpu_custom_call" | custom-call | tf_op jit(solution)/shard_map/pallas_call | solution.py:52
  23.1 4.0 %collective-permute-start.8 = (f32[256,256]{1,0:T(8,128)S(1)}, f32[256,256]{1,0:T(8,128)S(1)}, u32[]{:S(2)}, u32[]{:S(2)}) collective-permute-start(f32[256,256]{1,0:T(8,128)S(1)} %copy-done.1), channel_id=1, source_target_pairs={{4,0},{5,1},{6,2},{7,3},{0,4},{1,5},{2,6},{3,7},{12,8},{13,9},{14,... | collective-permute-start | bytes 786440 | tf_op jit(solution)/shard_map/ppermute | solution.py:529
  27.1 3.2 %collective-permute-done.5.rotation_ref.other_ref = f32[256,256]{1,0:T(8,128)S(1)} collective-permute-done((f32[256,256]{1,0:T(8,128)S(1)}, f32[256,256]{1,0:T(8,128)S(1)}, u32[]{:S(2)}, u32[]{:S(2)}) %collective-permute-start.5) | collective-permute-done | bytes 262176 | tf_op jit(solution)/shard_map/ppermute | solution.py:529
  31.4 4.1 %collective-permute-start.7 = (f32[768,128]{1,0:T(8,128)S(1)}, f32[768,128]{1,0:T(8,128)S(1)}, u32[]{:S(2)}, u32[]{:S(2)}) collective-permute-start(f32[768,128]{1,0:T(8,128)S(1)} %get-tuple-element.99.refs_4_), channel_id=1, source_target_pairs={{12,4},{13,5},{14,6},{15,7},{0,8},{1,9},{2,10},{3,11},{20,12},{21,... | collective-permute-start | bytes 1179656 | tf_op jit(solution)/shard_map/ppermute | solution.py:529
  36.3 3.5 %collective-permute-start.9 = (f32[256,128]{1,0:T(8,128)S(1)}, f32[256,128]{1,0:T(8,128)S(1)}, u32[]{:S(2)}, u32[]{:S(2)}) collective-permute-start(f32[256,128]{1,0:T(8,128)S(1)} %get-tuple-element.102.refs_7_), channel_id=1, source_target_pairs={{12,4},{13,5},{14,6},{15,7},{0,8},{1,9},{2,10},{3,11},{20,12},{21,... | collective-permute-start | bytes 393224 | tf_op jit(solution)/shard_map/ppermute | solution.py:529
  43.7 6.4 %collective-permute-start.11 = (f32[256,128]{1,0:T(8,128)S(1)}, f32[256,128]{1,0:T(8,128)S(1)}, u32[]{:S(2)}, u32[]{:S(2)}) collective-permute-start(f32[256,128]{1,0:T(8,128)S(1)} %get-tuple-element.105), channel_id=1, source_target_pairs={{8,0},{9,1},{10,2},{11,3},{12,4},{13,5},{14,6},{15,7},{0,8},{1,9},... | collective-permute-start | bytes 393224 | tf_op jit(solution)/shard_map/ppermute | solution.py:529
  50.8 1.8 %shard_map.56 = (f32[128,128]{1,0:T(8,128)S(1)}, f32[128,128]{1,0:T(8,128)S(1)}, f32[1024,128]{1,0:T(8,128)S(1)}, f32[1024,128]{1,0:T(8,128)S(1)}, f32[1024,128]{1,0:T(8,128)S(1)}, /*index=5*/f32[1024,128]{1,0:T(8,128)S(1)}) custom-call(s32[16]{0:T(128)S(1)} %constant_dynamic-update-slice_fusion.f, f32[1024,128]{1,0:T(8,128)S(1)} %get-tuple-element.89.refs_0_, ...), custom_call_target="tpu_custom_call" | custom-call | tf_op jit(solution)/shard_map/pallas_call | solution.py:52
  54.6 2.4 %collective-permute-start.14 = (f32[128,128]{1,0:T(8,128)S(1)}, f32[128,128]{1,0:T(8,128)S(1)}, u32[]{:S(2)}, u32[]{:S(2)}) collective-permute-start(f32[128,128]{1,0:T(8,128)S(1)} %add.35.refs_0_), channel_id=1, source_target_pairs={{4,0},{5,1},{6,2},{7,3},{0,4},{1,5},{2,6},{3,7},{12,8},{13,9},{14,... | collective-permute-start | bytes 196616 | tf_op jit(solution)/shard_map/ppermute | solution.py:529
  57.5 2.4 %collective-permute-done.15.refs_3_ = f32[128,128]{1,0:T(8,128)S(1)} collective-permute-done((f32[128,128]{1,0:T(8,128)S(1)}, f32[128,128]{1,0:T(8,128)S(1)}, u32[]{:S(2)}, u32[]{:S(2)}) %collective-permute-start.15) | collective-permute-done | bytes 65568 | tf_op jit(solution)/shard_map/ppermute | solution.py:529
  61.3 3.4 %shard_map.58 = (f32[256,256]{1,0:T(8,128)S(1)}, f32[256,256]{1,0:T(8,128)S(1)}) custom-call(s32[16]{0:T(128)S(1)} %constant_dynamic-update-slice_fusion.f, f32[128,128]{1,0:T(8,128)S(1)} %add.35.refs_0_, f32[128,128]{1,0:T(8,128)S(1)} %collective-permute-done.13.refs_1_, f32[128,128]{1,0:T(8,128)S(1)} %collective-permute-done.14.refs_2_, ...), custom_call_target="tpu_custom_call" | custom-call | tf_op jit(solution)/shard_map/pallas_call | solution.py:52
  66.3 1.8 %shard_map.59 = (f32[1024,128]{1,0:T(8,128)S(1)}, f32[1024,128]{1,0:T(8,128)S(1)}, f32[1024,128]{1,0:T(8,128)S(1)}, f32[1024,128]{1,0:T(8,128)S(1)}, f32[256,128...) custom-call(s32[16]{0:T(128)S(1)} %constant_dynamic-update-slice_fusion.f, ...), custom_call_target="tpu_custom_call" | custom-call | tf_op jit(solution)/shard_map/pallas_call | solution.py:52
  68.1 3.6 %collective-permute-start.17 = (f32[1024,128]{1,0:T(8,128)S(1)}, f32[1024,128]{1,0:T(8,128)S(1)}, u32[]{:S(2)}, u32[]{:S(2)}) collective-permute-start(f32[1024,128]{1,0:T(8,128)S(1)} %get-tuple-element.119), channel_id=1, source_target_pairs={{8,0},{9,1},{10,2},{11,3},{12,4},{13,5},{14,6},{15,7},{0,8},{1,9},... | collective-permute-start | bytes 1572872 | tf_op jit(solution)/shard_map/ppermute | solution.py:529
  74.9 3.5 %collective-permute-start.20 = (f32[128,128]{1,0:T(8,128)S(1)}, f32[128,128]{1,0:T(8,128)S(1)}, u32[]{:S(2)}, u32[]{:S(2)}) collective-permute-start(f32[128,128]{1,0:T(8,128)S(1)} %get-tuple-element.123), channel_id=1, source_target_pairs={{1,0},{0,1},{3,2},{2,3},{5,4},{4,5},{7,6},{6,7},{9,8},{8,9},{11,10... | collective-permute-start | bytes 196616 | tf_op jit(solution)/shard_map/ppermute | solution.py:529
  80.3 4.2 %collective-permute-done.17.refs_0_ = f32[1024,128]{1,0:T(8,128)S(1)} collective-permute-done((f32[1024,128]{1,0:T(8,128)S(1)}, f32[1024,128]{1,0:T(8,128)S(1)}, u32[]{:S(2)}, u32[]{:S(2)}) %collective-permute-start.17) | collective-permute-done | bytes 524320 | tf_op jit(solution)/shard_map/ppermute | solution.py:529
  86.1 2.0 %collective-permute-start.21 = (f32[128,128]{1,0:T(8,128)S(1)}, f32[128,128]{1,0:T(8,128)S(1)}, u32[]{:S(2)}, u32[]{:S(2)}) collective-permute-start(f32[128,128]{1,0:T(8,128)S(1)} %get-tuple-element.129), channel_id=1, source_target_pairs={{1,0},{0,1},{3,2},{2,3},{5,4},{4,5},{7,6},{6,7},{9,8},{8,9},{11,10... | collective-permute-start | bytes 196616 | tf_op jit(solution)/shard_map/ppermute | solution.py:529
  89.1 2.0 %collective-permute-start.25 = (f32[128,128]{1,0:T(8,128)S(1)}, f32[128,128]{1,0:T(8,128)S(1)}, u32[]{:S(2)}, u32[]{:S(2)}) collective-permute-start(f32[128,128]{1,0:T(8,128)S(1)} %add.36.refs_0_), channel_id=1, source_target_pairs={{4,0},{5,1},{6,2},{7,3},{0,4},{1,5},{2,6},{3,7},{12,8},{13,9},{14,... | collective-permute-start | bytes 196616 | tf_op jit(solution)/shard_map/ppermute | solution.py:529
  92.6 2.3 %collective-permute-done.26.refs_3_ = f32[128,128]{1,0:T(8,128)S(1)} collective-permute-done((f32[128,128]{1,0:T(8,128)S(1)}, f32[128,128]{1,0:T(8,128)S(1)}, u32[]{:S(2)}, u32[]{:S(2)}) %collective-permute-start.26) | collective-permute-done | bytes 65568 | tf_op jit(solution)/shard_map/ppermute | solution.py:529
  95.8 3.0 %shard_map.62 = (f32[256,256]{1,0:T(8,128)S(1)}, f32[256,256]{1,0:T(8,128)S(1)}) custom-call(s32[16]{0:T(128)S(1)} %constant_dynamic-update-slice_fusion.f, f32[128,128]{1,0:T(8,128)S(1)} %add.36.refs_0_, f32[128,128]{1,0:T(8,128)S(1)} %collective-permute-done.24.refs_1_, f32[128,128]{1,0:T(8,128)S(1)} %collective-permute-done.25.refs_2_, ...), custom_call_target="tpu_custom_call" | custom-call | tf_op jit(solution)/shard_map/pallas_call | solution.py:52
  100.4 1.8 %shard_map.63 = (f32[1280,128]{1,0:T(8,128)S(1)}, f32[1280,128]{1,0:T(8,128)S(1)}, f32[1280,128]{1,0:T(8,128)S(1)}, f32[1280,128]{1,0:T(8,128)S(1)}, f32[1280,128]{1,0:T(8,128)S(1)}) custom-call(s32[16]{0:T(128)S(1)} %constant_dynamic-update-slice_fusion.f, f32[256,256]{1,0:T(8,128)S(1)} %get-tuple-element.135.own_ref.rotation_ref, ...), custom_call_target="tpu_custom_call" | custom-call | tf_op jit(solution)/shard_map/pallas_call | solution.py:52
  102.2 5.7 %collective-permute-start.28 = (f32[1280,128]{1,0:T(8,128)S(1)}, f32[1280,128]{1,0:T(8,128)S(1)}, u32[]{:S(2)}, u32[]{:S(2)}) collective-permute-start(f32[1280,128]{1,0:T(8,128)S(1)} %get-tuple-element.142), channel_id=1, source_target_pairs={{8,0},{9,1},{10,2},{11,3},{12,4},{13,5},{14,6},{15,7},{0,8},{1,9},... | collective-permute-start | bytes 1966088 | tf_op jit(solution)/shard_map/ppermute | solution.py:529
  111.6 3.7 %collective-permute-start.31 = (f32[128,128]{1,0:T(8,128)S(1)}, f32[128,128]{1,0:T(8,128)S(1)}, u32[]{:S(2)}, u32[]{:S(2)}) collective-permute-start(f32[128,128]{1,0:T(8,128)S(1)} %get-tuple-element.146), channel_id=1, source_target_pairs={{1,0},{0,1},{3,2},{2,3},{5,4},{4,5},{7,6},{6,7},{9,8},{8,9},{11,10... | collective-permute-start | bytes 196616 | tf_op jit(solution)/shard_map/ppermute | solution.py:529
  115.3 7.6 %collective-permute-done.28.a_ref.refs_0_ = f32[1280,128]{1,0:T(8,128)S(1)} collective-permute-done((f32[1280,128]{1,0:T(8,128)S(1)}, f32[1280,128]{1,0:T(8,128)S(1)}, u32[]{:S(2)}, u32[]{:S(2)}) %collective-permute-start.28) | collective-permute-done | bytes 655392 | tf_op jit(solution)/shard_map/ppermute | solution.py:529
  124.3 1.7 %shard_map.66 = (f32[128,128]{1,0:T(8,128)S(1)}, f32[128,128]{1,0:T(8,128)S(1)}, f32[1280,128]{1,0:T(8,128)S(1)}, f32[1280,128]{1,0:T(8,128)S(1)}) custom-call(s32[16]{0:T(128)S(1)} %constant_dynamic-update-slice_fusion.f, f32[1280,128]{1,0:T(8,128)S(1)} %collective-permute-done.28.a_ref.refs_0_, f32[1280,128]{1,0:T(8,128)S(1)} %collective-permute-done.29.b_ref.refs_1_, ...), custom_call_target="tpu_custom_call" | custom-call | tf_op jit(solution)/shard_map/pallas_call | solution.py:52
  127.3 2.1 %collective-permute-start.36 = (f32[128,128]{1,0:T(8,128)S(1)}, f32[128,128]{1,0:T(8,128)S(1)}, u32[]{:S(2)}, u32[]{:S(2)}) collective-permute-start(f32[128,128]{1,0:T(8,128)S(1)} %add.37.refs_0_), channel_id=1, source_target_pairs={{6,0},{7,1},{4,2},{5,3},{2,4},{3,5},{0,6},{1,7},{14,8},{15,9},{12,... | collective-permute-start | bytes 196616 | tf_op jit(solution)/shard_map/ppermute | solution.py:529
  131.4 3.4 %collective-permute-done.36.refs_3_ = f32[128,128]{1,0:T(8,128)S(1)} collective-permute-done((f32[128,128]{1,0:T(8,128)S(1)}, f32[128,128]{1,0:T(8,128)S(1)}, u32[]{:S(2)}, u32[]{:S(2)}) %collective-permute-start.36) | collective-permute-done | bytes 65568 | tf_op jit(solution)/shard_map/ppermute | solution.py:529
  136.0 3.4 %shard_map.68 = (f32[264,256]{1,0:T(8,128)S(1)}, f32[256,256]{1,0:T(8,128)}) custom-call(s32[16]{0:T(128)S(1)} %constant_dynamic-update-slice_fusion.f, f32[128,128]{1,0:T(8,128)S(1)} %add.37.refs_0_, f32[128,128]{1,0:T(8,128)S(1)} %collective-permute-done.34.refs_1_, f32[128,128]{1,0:T(8,128)S(1)} %collective-permute-done.35.refs_2_, ...), custom_call_target="tpu_custom_call" | custom-call | tf_op jit(solution)/shard_map/pallas_call | solution.py:52
  141.1 3.0 %shard_map.69 = (f32[2048,256]{1,0:T(8,128)}, f32[512,256]{1,0:T(8,128)}, f32[1,256]{1,0:T(1,128)}) custom-call(s32[16]{0:T(128)S(1)} %constant_dynamic-update-slice_fusion.f, f32[264,256]{1,0:T(8,128)S(1)} %get-tuple-element.162.own_ref, f32[264,256]{1,0:T(8,128)S(1)} %collective-permute-done.38.other_ref, f32[1280,128]{1,0:T(8,128)S(1)} %get-tuple-element.165.refs_0_, ...), custom_call_target="tpu_custom_call" | custom-call | flops 1 | bytes 1 | tf_op jit(solution)/shard_map/pallas_call | solution.py:428
  145.1 2.0 %shard_map.70 = (f32[2048,256]{1,0:T(8,128)}, f32[512,256]{1,0:T(8,128)}) custom-call(s32[16]{0:T(128)S(1)} %constant_dynamic-update-slice_fusion.f, f32[264,256]{1,0:T(8,128)S(1)} %get-tuple-element.162.own_ref, f32[264,256]{1,0:T(8,128)S(1)} %collective-permute-done.38.other_ref, ...), custom_call_target="tpu_custom_call", output_to_operand_aliasing={{0}: (5, {}), {1}: (6, {})} | custom-call | flops 1 | bytes 1 | tf_op jit(solution)/shard_map/pallas_call | solution.py:428
  (82 shorter events, 41.8 us)
Async XLA Ops:
  3.1 27.2 %collective-permute-start.6 = (f32[768,256]{1,0:T(8,128)}, f32[768,256]{1,0:T(8,128)S(1)}, u32[]{:S(2)}, u32[]{:S(2)}) collective-permute-start(f32[768,256]{1,0:T(8,128)} %get-tuple-element.97), channel_id=1, source_target_pairs={{4,0},{5,1},{6,2},{7,3},{0,4},{1,5},{2,6},{3,7},{12,8},{13,9},{14,... | collective-permute-start | bytes 2359304 | tf_op jit(solution)/shard_map/ppermute | solution.py:529
  9.8 7.0 %collective-permute-start.1 = (f32[384,128]{1,0:T(8,128)S(1)}, f32[384,128]{1,0:T(8,128)S(1)}, u32[]{:S(2)}, u32[]{:S(2)}) collective-permute-start(f32[384,128]{1,0:T(8,128)S(1)} %add.34.own_ref), channel_id=1, source_target_pairs={{2,0},{3,1},{0,2},{1,3},{6,4},{7,5},{4,6},{5,7},{10,8},{11,9},{8,1... | collective-permute-start | bytes 589832 | tf_op jit(solution)/shard_map/ppermute | solution.py:529
  20.3 10.0 %collective-permute-start.5 = (f32[256,256]{1,0:T(8,128)S(1)}, f32[256,256]{1,0:T(8,128)S(1)}, u32[]{:S(2)}, u32[]{:S(2)}) collective-permute-start(f32[256,256]{1,0:T(8,128)S(1)} %get-tuple-element.88.rotation_ref.own_ref), channel_id=1, source_target_pairs={{4,0},{5,1},{6,2},{7,3},{0,4},{1,5},{2,6},{3,7},{12,8},{13,9},{14,... | collective-permute-start | bytes 786440 | tf_op jit(solution)/shard_map/ppermute | solution.py:529
  21.8 29.0 %collective-permute-start.2 = (f32[1024,128]{1,0:T(8,128)S(1)}, f32[1024,128]{1,0:T(8,128)S(1)}, u32[]{:S(2)}, u32[]{:S(2)}) collective-permute-start(f32[1024,128]{1,0:T(8,128)S(1)} %get-tuple-element.92.refs_1_), channel_id=1, source_target_pairs={{8,0},{9,1},{10,2},{11,3},{16,8},{17,9},{18,10},{19,11},{4,12},{5,... | collective-permute-start | bytes 1572872 | tf_op jit(solution)/shard_map/ppermute | solution.py:529
  23.1 12.3 %collective-permute-start.8 = (f32[256,256]{1,0:T(8,128)S(1)}, f32[256,256]{1,0:T(8,128)S(1)}, u32[]{:S(2)}, u32[]{:S(2)}) collective-permute-start(f32[256,256]{1,0:T(8,128)S(1)} %copy-done.1), channel_id=1, source_target_pairs={{4,0},{5,1},{6,2},{7,3},{0,4},{1,5},{2,6},{3,7},{12,8},{13,9},{14,... | collective-permute-start | bytes 786440 | tf_op jit(solution)/shard_map/ppermute | solution.py:529
  31.4 19.4 %collective-permute-start.7 = (f32[768,128]{1,0:T(8,128)S(1)}, f32[768,128]{1,0:T(8,128)S(1)}, u32[]{:S(2)}, u32[]{:S(2)}) collective-permute-start(f32[768,128]{1,0:T(8,128)S(1)} %get-tuple-element.99.refs_4_), channel_id=1, source_target_pairs={{12,4},{13,5},{14,6},{15,7},{0,8},{1,9},{2,10},{3,11},{20,12},{21,... | collective-permute-start | bytes 1179656 | tf_op jit(solution)/shard_map/ppermute | solution.py:529
  36.3 14.5 %collective-permute-start.9 = (f32[256,128]{1,0:T(8,128)S(1)}, f32[256,128]{1,0:T(8,128)S(1)}, u32[]{:S(2)}, u32[]{:S(2)}) collective-permute-start(f32[256,128]{1,0:T(8,128)S(1)} %get-tuple-element.102.refs_7_), channel_id=1, source_target_pairs={{12,4},{13,5},{14,6},{15,7},{0,8},{1,9},{2,10},{3,11},{20,12},{21,... | collective-permute-start | bytes 393224 | tf_op jit(solution)/shard_map/ppermute | solution.py:529
  42.1 8.0 %collective-permute-start.4 = (f32[128,128]{1,0:T(8,128)S(1)}, f32[128,128]{1,0:T(8,128)S(1)}, u32[]{:S(2)}, u32[]{:S(2)}) collective-permute-start(f32[128,128]{1,0:T(8,128)S(1)} %get-tuple-element.95), channel_id=1, source_target_pairs={{4,0},{0,1},{6,2},{2,3},{5,4},{1,5},{7,6},{3,7},{12,8},{8,9},{14,1... | collective-permute-start | bytes 196616 | tf_op jit(solution)/shard_map/ppermute | solution.py:529
  43.7 10.3 %collective-permute-start.11 = (f32[256,128]{1,0:T(8,128)S(1)}, f32[256,128]{1,0:T(8,128)S(1)}, u32[]{:S(2)}, u32[]{:S(2)}) collective-permute-start(f32[256,128]{1,0:T(8,128)S(1)} %get-tuple-element.105), channel_id=1, source_target_pairs={{8,0},{9,1},{10,2},{11,3},{12,4},{13,5},{14,6},{15,7},{0,8},{1,9},... | collective-permute-start | bytes 393224 | tf_op jit(solution)/shard_map/ppermute | solution.py:529
  50.1 3.9 %collective-permute-start.12 = (f32[256,128]{1,0:T(8,128)S(1)}, f32[256,128]{1,0:T(8,128)S(1)}, u32[]{:S(2)}, u32[]{:S(2)}) collective-permute-start(f32[256,128]{1,0:T(8,128)S(1)} %get-tuple-element.106), channel_id=1, source_target_pairs={{0,0},{1,1},{2,2},{3,3},{4,4},{5,5},{6,6},{7,7},{16,8},{17,9},{18,... | collective-permute-start | bytes 393224 | tf_op jit(solution)/shard_map/ppermute | solution.py:529
  54.0 5.9 %collective-permute-start.15 = (f32[128,128]{1,0:T(8,128)S(1)}, f32[128,128]{1,0:T(8,128)S(1)}, u32[]{:S(2)}, u32[]{:S(2)}) collective-permute-start(f32[128,128]{1,0:T(8,128)S(1)} %add.35.refs_0_), channel_id=1, source_target_pairs={{6,0},{7,1},{4,2},{5,3},{2,4},{3,5},{0,6},{1,7},{14,8},{15,9},{12,... | collective-permute-start | bytes 196616 | tf_op jit(solution)/shard_map/ppermute | solution.py:529
  54.6 5.9 %collective-permute-start.14 = (f32[128,128]{1,0:T(8,128)S(1)}, f32[128,128]{1,0:T(8,128)S(1)}, u32[]{:S(2)}, u32[]{:S(2)}) collective-permute-start(f32[128,128]{1,0:T(8,128)S(1)} %add.35.refs_0_), channel_id=1, source_target_pairs={{4,0},{5,1},{6,2},{7,3},{0,4},{1,5},{2,6},{3,7},{12,8},{13,9},{14,... | collective-permute-start | bytes 196616 | tf_op jit(solution)/shard_map/ppermute | solution.py:529
  57.0 4.3 %collective-permute-start.13 = (f32[128,128]{1,0:T(8,128)S(1)}, f32[128,128]{1,0:T(8,128)S(1)}, u32[]{:S(2)}, u32[]{:S(2)}) collective-permute-start(f32[128,128]{1,0:T(8,128)S(1)} %add.35.refs_0_), channel_id=1, source_target_pairs={{2,0},{3,1},{0,2},{1,3},{6,4},{7,5},{4,6},{5,7},{10,8},{11,9},{8,1... | collective-permute-start | bytes 196616 | tf_op jit(solution)/shard_map/ppermute | solution.py:529
  68.1 16.3 %collective-permute-start.17 = (f32[1024,128]{1,0:T(8,128)S(1)}, f32[1024,128]{1,0:T(8,128)S(1)}, u32[]{:S(2)}, u32[]{:S(2)}) collective-permute-start(f32[1024,128]{1,0:T(8,128)S(1)} %get-tuple-element.119), channel_id=1, source_target_pairs={{8,0},{9,1},{10,2},{11,3},{12,4},{13,5},{14,6},{15,7},{0,8},{1,9},... | collective-permute-start | bytes 1572872 | tf_op jit(solution)/shard_map/ppermute | solution.py:529
  71.7 12.7 %collective-permute-start.18 = (f32[1024,128]{1,0:T(8,128)S(1)}, f32[1024,128]{1,0:T(8,128)S(1)}, u32[]{:S(2)}, u32[]{:S(2)}) collective-permute-start(f32[1024,128]{1,0:T(8,128)S(1)} %get-tuple-element.120), channel_id=1, source_target_pairs={{0,0},{1,1},{2,2},{3,3},{4,4},{5,5},{6,6},{7,7},{16,8},{17,9},{18,... | collective-permute-start | bytes 1572872 | tf_op jit(solution)/shard_map/ppermute | solution.py:529
  74.2 5.4 %collective-permute-start.19 = (f32[128,128]{1,0:T(8,128)S(1)}, f32[128,128]{1,0:T(8,128)S(1)}, u32[]{:S(2)}, u32[]{:S(2)}) collective-permute-start(f32[128,128]{1,0:T(8,128)S(1)} %get-tuple-element.122), channel_id=1, source_target_pairs={{0,0},{8,1},{2,2},{10,3},{4,4},{12,5},{6,6},{14,7},{1,8},{16,9},{3... | collective-permute-start | bytes 196616 | tf_op jit(solution)/shard_map/ppermute | solution.py:529
  74.9 5.4 %collective-permute-start.20 = (f32[128,128]{1,0:T(8,128)S(1)}, f32[128,128]{1,0:T(8,128)S(1)}, u32[]{:S(2)}, u32[]{:S(2)}) collective-permute-start(f32[128,128]{1,0:T(8,128)S(1)} %get-tuple-element.123), channel_id=1, source_target_pairs={{1,0},{0,1},{3,2},{2,3},{5,4},{4,5},{7,6},{6,7},{9,8},{8,9},{11,10... | collective-permute-start | bytes 196616 | tf_op jit(solution)/shard_map/ppermute | solution.py:529
  78.4 10.6 %collective-permute-start.22 = (f32[256,128]{1,0:T(8,128)S(1)}, f32[256,128]{1,0:T(8,128)S(1)}, u32[]{:S(2)}, u32[]{:S(2)}) collective-permute-start(f32[256,128]{1,0:T(8,128)S(1)} %get-tuple-element.130), channel_id=1, source_target_pairs={{8,0},{9,1},{10,2},{11,3},{12,4},{13,5},{14,6},{15,7},{0,8},{1,9},... | collective-permute-start | bytes 393224 | tf_op jit(solution)/shard_map/ppermute | solution.py:529
  79.6 9.4 %collective-permute-start.23 = (f32[256,128]{1,0:T(8,128)S(1)}, f32[256,128]{1,0:T(8,128)S(1)}, u32[]{:S(2)}, u32[]{:S(2)}) collective-permute-start(f32[256,128]{1,0:T(8,128)S(1)} %get-tuple-element.131), channel_id=1, source_target_pairs={{0,0},{1,1},{2,2},{3,3},{4,4},{5,5},{6,6},{7,7},{16,8},{17,9},{18,... | collective-permute-start | bytes 393224 | tf_op jit(solution)/shard_map/ppermute | solution.py:529
  89.0 5.9 %collective-permute-start.26 = (f32[128,128]{1,0:T(8,128)S(1)}, f32[128,128]{1,0:T(8,128)S(1)}, u32[]{:S(2)}, u32[]{:S(2)}) collective-permute-start(f32[128,128]{1,0:T(8,128)S(1)} %add.36.refs_0_), channel_id=1, source_target_pairs={{6,0},{7,1},{4,2},{5,3},{2,4},{3,5},{0,6},{1,7},{14,8},{15,9},{12,... | collective-permute-start | bytes 196616 | tf_op jit(solution)/shard_map/ppermute | solution.py:529
  89.1 5.8 %collective-permute-start.25 = (f32[128,128]{1,0:T(8,128)S(1)}, f32[128,128]{1,0:T(8,128)S(1)}, u32[]{:S(2)}, u32[]{:S(2)}) collective-permute-start(f32[128,128]{1,0:T(8,128)S(1)} %add.36.refs_0_), channel_id=1, source_target_pairs={{4,0},{5,1},{6,2},{7,3},{0,4},{1,5},{2,6},{3,7},{12,8},{13,9},{14,... | collective-permute-start | bytes 196616 | tf_op jit(solution)/shard_map/ppermute | solution.py:529
  91.1 4.7 %collective-permute-start.24 = (f32[128,128]{1,0:T(8,128)S(1)}, f32[128,128]{1,0:T(8,128)S(1)}, u32[]{:S(2)}, u32[]{:S(2)}) collective-permute-start(f32[128,128]{1,0:T(8,128)S(1)} %add.36.refs_0_), channel_id=1, source_target_pairs={{2,0},{3,1},{0,2},{1,3},{6,4},{7,5},{4,6},{5,7},{10,8},{11,9},{8,1... | collective-permute-start | bytes 196616 | tf_op jit(solution)/shard_map/ppermute | solution.py:529
  102.2 20.7 %collective-permute-start.28 = (f32[1280,128]{1,0:T(8,128)S(1)}, f32[1280,128]{1,0:T(8,128)S(1)}, u32[]{:S(2)}, u32[]{:S(2)}) collective-permute-start(f32[1280,128]{1,0:T(8,128)S(1)} %get-tuple-element.142), channel_id=1, source_target_pairs={{8,0},{9,1},{10,2},{11,3},{12,4},{13,5},{14,6},{15,7},{0,8},{1,9},... | collective-permute-start | bytes 1966088 | tf_op jit(solution)/shard_map/ppermute | solution.py:529
  107.9 15.0 %collective-permute-start.29 = (f32[1280,128]{1,0:T(8,128)S(1)}, f32[1280,128]{1,0:T(8,128)S(1)}, u32[]{:S(2)}, u32[]{:S(2)}) collective-permute-start(f32[1280,128]{1,0:T(8,128)S(1)} %get-tuple-element.143), channel_id=1, source_target_pairs={{0,0},{1,1},{2,2},{3,3},{4,4},{5,5},{6,6},{7,7},{16,8},{17,9},{18,... | collective-permute-start | bytes 1966088 | tf_op jit(solution)/shard_map/ppermute | solution.py:529
  108.6 17.4 %collective-permute-start.32 = (f32[1280,128]{1,0:T(8,128)S(1)}, f32[1280,128]{1,0:T(8,128)S(1)}, u32[]{:S(2)}, u32[]{:S(2)}) collective-permute-start(f32[1280,128]{1,0:T(8,128)S(1)} %get-tuple-element.153), channel_id=1, source_target_pairs={{4,0},{5,1},{6,2},{7,3},{0,4},{1,5},{2,6},{3,7},{12,8},{13,9},{14,... | collective-permute-start | bytes 1966088 | tf_op jit(solution)/shard_map/ppermute | solution.py:529
  111.0 12.5 %collective-permute-start.30 = (f32[128,128]{1,0:T(8,128)S(1)}, f32[128,128]{1,0:T(8,128)S(1)}, u32[]{:S(2)}, u32[]{:S(2)}) collective-permute-start(f32[128,128]{1,0:T(8,128)S(1)} %get-tuple-element.145), channel_id=1, source_target_pairs={{0,0},{8,1},{2,2},{10,3},{4,4},{12,5},{6,6},{14,7},{1,8},{16,9},{3... | collective-permute-start | bytes 196616 | tf_op jit(solution)/shard_map/ppermute | solution.py:529
  111.6 11.9 %collective-permute-start.31 = (f32[128,128]{1,0:T(8,128)S(1)}, f32[128,128]{1,0:T(8,128)S(1)}, u32[]{:S(2)}, u32[]{:S(2)}) collective-permute-start(f32[128,128]{1,0:T(8,128)S(1)} %get-tuple-element.146), channel_id=1, source_target_pairs={{1,0},{0,1},{3,2},{2,3},{5,4},{4,5},{7,6},{6,7},{9,8},{8,9},{11,10... | collective-permute-start | bytes 196616 | tf_op jit(solution)/shard_map/ppermute | solution.py:529
  123.5 11.5 %collective-permute-start.37 = (f32[512,128]{1,0:T(8,128)S(1)}, f32[512,128]{1,0:T(8,128)S(1)}, u32[]{:S(2)}, u32[]{:S(2)}) collective-permute-start(f32[512,128]{1,0:T(8,128)S(1)} %shard_map.64), channel_id=1, source_target_pairs={{4,0},{5,1},{6,2},{7,3},{0,4},{1,5},{2,6},{3,7},{12,8},{13,9},{14,... | collective-permute-start | bytes 786440 | tf_op jit(solution)/shard_map/ppermute | solution.py:529
  127.3 7.5 %collective-permute-start.36 = (f32[128,128]{1,0:T(8,128)S(1)}, f32[128,128]{1,0:T(8,128)S(1)}, u32[]{:S(2)}, u32[]{:S(2)}) collective-permute-start(f32[128,128]{1,0:T(8,128)S(1)} %add.37.refs_0_), channel_id=1, source_target_pairs={{6,0},{7,1},{4,2},{5,3},{2,4},{3,5},{0,6},{1,7},{14,8},{15,9},{12,... | collective-permute-start | bytes 196616 | tf_op jit(solution)/shard_map/ppermute | solution.py:529
  129.4 5.5 %collective-permute-start.35 = (f32[128,128]{1,0:T(8,128)S(1)}, f32[128,128]{1,0:T(8,128)S(1)}, u32[]{:S(2)}, u32[]{:S(2)}) collective-permute-start(f32[128,128]{1,0:T(8,128)S(1)} %add.37.refs_0_), channel_id=1, source_target_pairs={{4,0},{5,1},{6,2},{7,3},{0,4},{1,5},{2,6},{3,7},{12,8},{13,9},{14,... | collective-permute-start | bytes 196616 | tf_op jit(solution)/shard_map/ppermute | solution.py:529
  130.2 4.8 %collective-permute-start.34 = (f32[128,128]{1,0:T(8,128)S(1)}, f32[128,128]{1,0:T(8,128)S(1)}, u32[]{:S(2)}, u32[]{:S(2)}) collective-permute-start(f32[128,128]{1,0:T(8,128)S(1)} %add.37.refs_0_), channel_id=1, source_target_pairs={{2,0},{3,1},{0,2},{1,3},{6,4},{7,5},{4,6},{5,7},{10,8},{11,9},{8,1... | collective-permute-start | bytes 196616 | tf_op jit(solution)/shard_map/ppermute | solution.py:529
  135.0 10.1 %collective-permute-start.39 = (f32[768,128]{1,0:T(8,128)S(1)}, f32[768,128]{1,0:T(8,128)S(1)}, u32[]{:S(2)}, u32[]{:S(2)}) collective-permute-start(f32[768,128]{1,0:T(8,128)S(1)} %shard_map.67), channel_id=1, source_target_pairs={{4,0},{5,1},{6,2},{7,3},{0,4},{1,5},{2,6},{3,7},{12,8},{13,9},{14,... | collective-permute-start | bytes 1179656 | tf_op jit(solution)/shard_map/ppermute | solution.py:529
  (11 other events, 45.2 us)

commit v12 on v10

--- a/solution.py
+++ b/solution.py
@@ -258,50 +258,46 @@
     return swapped(f[FIRST] == 1, turn_0, 1), turn_1
 
 
-def turn_rows(facts, rotation, rows_of, half, own):
+def turn_rows(facts, rotation, rows_of, vector_rows, half, own):
     rows = rows_of.shape[0] // 2 if own else rows_of.shape[0]
 
     def body(f, rotation_ref, x_ref, stay_ref, leave_ref):
         zero = f[X] == (0 if own else 1)
         upper_leaves = jnp.where(zero, f[FIRST], 1) == 1
-        turn = swapped(upper_leaves, rotation_ref[...], 1)
+        turn = split(swapped(upper_leaves, rotation_ref[...], 1))
         here = pl.multiple_of(f[X] * rows, 8)
         out = dot3(x_ref[pl.ds(here, rows)] if own else x_ref[...], turn)
-        stay_ref[...] = out[:, :half]
-        leave_ref[...] = out[:, half:]
-
-    return call(body, facts, [rotation, rows_of], (shape(rows, half),) * 2)
-
-
-def first_vectors(facts, rotation, other_rotation, vector_rows, half):
-    def body(f, own_ref, other_ref, *refs):
-        even = f[X] == 0
-        own, other = own_ref[...], other_ref[...]
-        turn_0 = swapped(f[FIRST] == 1, jnp.where(even, own, other), 1)
-        turn_1 = jnp.where(even, other, own)
-        ids = f[VROW] + lax.broadcasted_iota(jnp.int32, (vector_rows, half), 0)
-        cols = lax.broadcasted_iota(jnp.int32, (vector_rows, half), 1)
-        up_0, low_0, up_1, low_1 = [
-            (ids == f[LABEL + k] * half + cols).astype(jnp.float32) for k in range(4)
-        ]
-        zero = dot3(lax.concatenate([up_0, low_0], 1), turn_0)
-        one = dot3(lax.concatenate([up_1, low_1], 1), turn_1)
-        put_turned(f, refs, zero, one, half)
+        stay_ref[:rows] = out[:, :half]
+        leave_ref[:rows] = out[:, half:]
+        if vector_rows:
+            ids = f[VROW] + lax.broadcasted_iota(jnp.int32, (vector_rows, half), 0)
+            cols = lax.broadcasted_iota(jnp.int32, (vector_rows, half), 1)
+            position = jnp.where(zero, 0, 2)
+            vectors = [
+                (ids == f[LABEL + position + k] * half + cols).astype(jnp.float32)
+                for k in range(2)
+            ]
+            out = dot3(lax.concatenate(vectors, 1), turn)
+            stay_ref[rows:] = out[:, :half]
+            leave_ref[rows:] = out[:, half:]
 
     return call(
-        body, facts, [rotation, other_rotation], (shape(vector_rows, half),) * 4
-    )
-
-
-def turn(facts, packs, blocks, vectors, half, last_move):
-    part, vector_rows = blocks[0].shape[0], vectors[0].shape[0]
+        body, facts, [rotation, rows_of], (shape(rows + vector_rows, half),) * 2
+    )
+
+
+def turn(facts, packs, blocks, vectors, part, vector_rows, half, last_move):
+    inputs = packs + blocks + vectors
 
     def body(f, own_ref, other_ref, *refs):
         turn_0, turn_1 = turns_of(f, own_ref, other_ref)
         turn_0, turn_1 = split(turn_0), split(turn_1)
-        columns = [r[...] for r in refs[:4]]
-        rows = blocks_of(f, *[r[...] for r in refs[4:8]])
-        outs = refs[8:]
+        columns = [r[:part] for r in refs[:4]]
+        if vectors:
+            rows = blocks_of(f, *[r[...] for r in refs[4:8]])
+        else:
+            rows = [r[part:] for r in refs[:4]]
+        outs = refs[len(inputs) - 2 :]
         for (up_0, low_0, up_1, low_1), at in ((columns, 0), (rows, part)):
             zero = dot3(lax.concatenate([up_0, low_0], 1), turn_0)
             one = dot3(lax.concatenate([up_1, low_1], 1), turn_1)
@@ -314,7 +310,7 @@
         outs = (shape(part + vector_rows, half),) * 5
     else:
         outs = (shape(part, half),) * 4 + (shape(vector_rows, half),) * 4
-    return call(body, facts, packs + blocks + vectors, outs)
+    return call(body, facts, inputs, outs)
 
 
 def put_cross(f, refs, zero, one):
@@ -323,7 +319,7 @@
     refs[1][...] = jnp.where(core, one, zero)
 
 
-def first_cross_gram(facts, own, others, half):
+def first_cross_gram(facts, own, others, part, half):
     rows = own[0].shape[0]
     pieces = len(others)
 
@@ -366,8 +362,8 @@
         put_cross(
             f,
             refs[3 + 3 * pieces :],
-            dot_tn(up_0[...], low_0[...]),
-            dot_tn(up_1[...], low_1[...]),
+            dot_tn(up_0[:part], low_0[:part]),
+            dot_tn(up_1[:part], low_1[:part]),
         )
 
     outs = (shape(half, half),) * 2 + (shape(rows, half),) * 4
@@ -601,33 +597,28 @@
     own = sum_rows(own + exchange(own, 0, 1))
     rotation, gram = first_rotation(facts, own, exchange(own, 0, 2), half)
 
+    vectors = []
     for sweep_round in range(ROUNDS - 1):
         last_move = sweep_round == ROUNDS - 2
         if sweep_round == 0:
             other_rotation = exchange(rotation, 1, 0)
-            stay, leave = turn_rows(facts, rotation, sector, half, True)
+            stay, leave = turn_rows(facts, rotation, sector, vector_rows, half, True)
             leave, rest_give = together(leave, rest_give)
             got_rest = exchange(rest_give, 1, 0)
             own_rows = [stay, leave, shift(leave, -2)]
             other_rows = []
-            for got in (got_top, got_rest):
-                stay, leave = turn_rows(facts, other_rotation, got, half, False)
+            for got, below in ((got_top, 0), (got_rest, vector_rows)):
+                stay, leave = turn_rows(facts, other_rotation, got, below, half, False)
                 other_rows.append([stay, leave, shift(leave, 2)])
             leave, stay = turned_gram(facts, gram, rotation, X)
             diagonals = [first_diagonal(leave, True), first_diagonal(stay, False)]
-            vectors = list(
-                first_vectors(facts, rotation, other_rotation, vector_rows, half)
-            )
-            vectors[0], vectors[1], diagonals[1] = together(
-                vectors[0], vectors[1], diagonals[1]
-            )
             *grams, up_0, nat_l, nat_u, low_1 = first_cross_gram(
-                facts, own_rows, other_rows, half
+                facts, own_rows, other_rows, part, half
             )
         else:
             packs = [rotation, exchange(rotation, 0, 1)]
             leave_a, leave_b, nat_l, nat_u, *vectors = turn(
-                facts, packs, blocks, vectors, half, last_move
+                facts, packs, blocks, vectors, part, vector_rows, half, last_move
             )
             got = [swap(leave_a, 0), swap(leave_b, 1)]
             leave, stay = turned_gram(facts, gram, rotation, CORE)
@@ -648,6 +639,8 @@
         blocks = [up_0, nat_l, nat_u, low_1]
         if last_move:
             grams[1], native = together(grams[1], native)
+        elif sweep_round == 0:
+            grams[1], *diagonals = together(grams[1], *diagonals)
         else:
             vector_a, vector_b, *kept = vectors
             grams[1], vector_a, vector_b, diagonals[0] = together(

time: 146 us -> 143 us (0.979)
  starting transfers between devices: 58.2 us -> 52.8 us
  waiting for transfers between devices: 43.4 us -> 45.9 us
    ppermute x40 -> x38, starting transfers between devices: 58.2 us -> 52.8 us  [permute(): return lax.ppermute(block, ('pair', 'row'), moves)]
    ppermute x40 -> x38, waiting for transfers between devices: 43.4 us -> 45.9 us  [permute(): return lax.ppermute(block, ('pair', 'row'), moves)]
    pallas_call x18 -> x17, Pallas kernels: 32.1 us -> 31.3 us  [call(): pl.pallas_call(body, out_shape=outs, in_specs=[pl.BlockSpec(memory_space=...]
  transfers between devices with their start and end apart: 40 -> 38, of which waited for: 23 -> 22; matrix products, arithmetic and copies ran while one was open for 0% -> 0% of each run, Pallas kernels for 19% -> 19%
where the time goes in v12:
time: 143 us; the launch traced here: 141 us
  starting transfers between devices  52.8 us (37%)
  waiting for transfers between devices  45.9 us (32%)
  Pallas kernels  40.9 us (29%)
    ppermute x38, starting transfers between devices, permute(): return lax.ppermute(block, ('pair', 'row'), moves)  52.8 us
    ppermute x38, waiting for transfers between devices, permute(): return lax.ppermute(block, ('pair', 'row'), moves)  45.9 us
    pallas_call x17, Pallas kernels, call(): pl.pallas_call(body, out_shape=outs, in_specs=[pl.BlockSpec(memory_space=...  31.3 us
    pallas_call x2, Pallas kernels, finish_call(): pl.pallas_call(body, out_shape=outs, in_specs=[pl.BlockSpec(memory_space=...  4.93 us
  transfers between devices with their start and end apart: 38, of which 22 were waited for; matrix products, arithmetic and copies ran while one was open for 0% of the time, Pallas kernels for 19%

profile of v12, /device:TPU:0, one launch (start us, length us, event | category | flops | bytes accessed | tf_op | source)
XLA Modules:
  0.0 141.1 jit_solution(3762567561801646264)
XLA Ops:
  0.6 2.5 %shard_map.52 = (f32[768,256]{1,0:T(8,128)}, f32[256,256]{1,0:T(8,128)}) custom-call(f32[2048,256]{1,0:T(8,128)} %x_ref.5), custom_call_target="tpu_custom_call" | custom-call | tf_op jit(solution)/shard_map/pallas_call | solution.py:104
  3.1 3.0 %collective-permute-start.4 = (f32[768,256]{1,0:T(8,128)}, f32[768,256]{1,0:T(8,128)S(1)}, u32[]{:S(2)}, u32[]{:S(2)}) collective-permute-start(f32[768,256]{1,0:T(8,128)} %get-tuple-element.86), channel_id=1, source_target_pairs={{4,0},{5,1},{6,2},{7,3},{0,4},{1,5},{2,6},{3,7},{12,8},{13,9},{14,... | collective-permute-start | bytes 2359304 | tf_op jit(solution)/shard_map/ppermute | solution.py:525
  6.1 2.2 %shard_map.49 = f32[384,128]{1,0:T(8,128)S(1)} custom-call(f32[2048,256]{1,0:T(8,128)S(1)} %copy-done), custom_call_target="tpu_custom_call" | custom-call | tf_op jit(solution)/shard_map/pallas_call | solution.py:74
  11.6 5.3 %collective-permute-done.1.other_ref = f32[384,128]{1,0:T(8,128)S(1)} collective-permute-done((f32[384,128]{1,0:T(8,128)S(1)}, f32[384,128]{1,0:T(8,128)S(1)}, u32[]{:S(2)}, u32[]{:S(2)}) %collective-permute-start.1) | collective-permute-done | bytes 196640 | tf_op jit(solution)/shard_map/ppermute | solution.py:525
  16.8 3.4 %shard_map.50 = (f32[256,256]{1,0:T(8,128)S(1)}, f32[256,256]{1,0:T(8,128)S(1)}) custom-call(s32[16]{0:T(128)S(1)} %constant_dynamic-update-slice_fusion.f, f32[384,128]{1,0:T(8,128)S(1)} %add.34.own_ref, f32[384,128]{1,0:T(8,128)S(1)} %collective-permute-done.1.other_ref), custom_call_target="tpu_custom_call" | custom-call | tf_op jit(solution)/shard_map/pallas_call | solution.py:52
  23.2 4.0 %collective-permute-start.6 = (f32[256,256]{1,0:T(8,128)S(1)}, f32[256,256]{1,0:T(8,128)S(1)}, u32[]{:S(2)}, u32[]{:S(2)}) collective-permute-start(f32[256,256]{1,0:T(8,128)S(1)} %copy-done.1), channel_id=1, source_target_pairs={{4,0},{5,1},{6,2},{7,3},{0,4},{1,5},{2,6},{3,7},{12,8},{13,9},{14,... | collective-permute-start | bytes 786440 | tf_op jit(solution)/shard_map/ppermute | solution.py:525
  27.2 3.1 %collective-permute-done.3.rotation_ref = f32[256,256]{1,0:T(8,128)S(1)} collective-permute-done((f32[256,256]{1,0:T(8,128)S(1)}, f32[256,256]{1,0:T(8,128)S(1)}, u32[]{:S(2)}, u32[]{:S(2)}) %collective-permute-start.3) | collective-permute-done | bytes 262176 | tf_op jit(solution)/shard_map/ppermute | solution.py:525
  31.4 4.1 %collective-permute-start.5 = (f32[768,128]{1,0:T(8,128)S(1)}, f32[768,128]{1,0:T(8,128)S(1)}, u32[]{:S(2)}, u32[]{:S(2)}) collective-permute-start(f32[768,128]{1,0:T(8,128)S(1)} %get-tuple-element.88.refs_4_), channel_id=1, source_target_pairs={{12,4},{13,5},{14,6},{15,7},{0,8},{1,9},{2,10},{3,11},{20,12},{21,... | collective-permute-start | bytes 1179656 | tf_op jit(solution)/shard_map/ppermute | solution.py:525
  36.4 3.5 %collective-permute-start.7 = (f32[512,128]{1,0:T(8,128)S(1)}, f32[512,128]{1,0:T(8,128)S(1)}, u32[]{:S(2)}, u32[]{:S(2)}) collective-permute-start(f32[512,128]{1,0:T(8,128)S(1)} %get-tuple-element.91.refs_7_), channel_id=1, source_target_pairs={{12,4},{13,5},{14,6},{15,7},{0,8},{1,9},{2,10},{3,11},{20,12},{21,... | collective-permute-start | bytes 786440 | tf_op jit(solution)/shard_map/ppermute | solution.py:525
  42.8 4.6 %collective-permute-done.7.refs_8_ = f32[512,128]{1,0:T(8,128)S(1)} collective-permute-done((f32[512,128]{1,0:T(8,128)S(1)}, f32[512,128]{1,0:T(8,128)S(1)}, u32[]{:S(2)}, u32[]{:S(2)}) %collective-permute-start.7) | collective-permute-done | bytes 262176 | tf_op jit(solution)/shard_map/ppermute | solution.py:525
  47.4 1.9 %shard_map.55 = (f32[128,128]{1,0:T(8,128)S(1)}, f32[128,128]{1,0:T(8,128)S(1)}, f32[1280,128]{1,0:T(8,128)S(1)}, f32[1280,128]{1,0:T(8,128)S(1)}, f32[1280,128]{1,0:T(8,128)S(1)}, /*index=5*/f32[1280,128]{1,0:T(8,128)S(1)}) custom-call(s32[16]{0:T(128)S(1)} %constant_dynamic-update-slice_fusion.f, f32[1280,128]{1,0:T(8,128)S(1)} %get-tuple-element.82.refs_0_, ...), custom_call_target="tpu_custom_call" | custom-call | tf_op jit(solution)/shard_map/pallas_call | solution.py:52
  50.6 3.4 %collective-permute-start.13 = (f32[128,128]{1,0:T(8,128)S(1)}, f32[128,128]{1,0:T(8,128)S(1)}, u32[]{:S(2)}, u32[]{:S(2)}) collective-permute-start(f32[128,128]{1,0:T(8,128)S(1)} %add.35.refs_0_), channel_id=1, source_target_pairs={{6,0},{7,1},{4,2},{5,3},{2,4},{3,5},{0,6},{1,7},{14,8},{15,9},{12,... | collective-permute-start | bytes 196616 | tf_op jit(solution)/shard_map/ppermute | solution.py:525
  54.7 1.8 %collective-permute-done.13.refs_3_ = f32[128,128]{1,0:T(8,128)S(1)} collective-permute-done((f32[128,128]{1,0:T(8,128)S(1)}, f32[128,128]{1,0:T(8,128)S(1)}, u32[]{:S(2)}, u32[]{:S(2)}) %collective-permute-start.13) | collective-permute-done | bytes 65568 | tf_op jit(solution)/shard_map/ppermute | solution.py:525
  56.4 1.9 %collective-permute-done.12.refs_2_ = f32[128,128]{1,0:T(8,128)S(1)} collective-permute-done((f32[128,128]{1,0:T(8,128)S(1)}, f32[128,128]{1,0:T(8,128)S(1)}, u32[]{:S(2)}, u32[]{:S(2)}) %collective-permute-start.12) | collective-permute-done | bytes 65568 | tf_op jit(solution)/shard_map/ppermute | solution.py:525
  58.3 3.4 %shard_map.57 = (f32[256,256]{1,0:T(8,128)S(1)}, f32[256,256]{1,0:T(8,128)S(1)}) custom-call(s32[16]{0:T(128)S(1)} %constant_dynamic-update-slice_fusion.f, f32[128,128]{1,0:T(8,128)S(1)} %add.35.refs_0_, f32[128,128]{1,0:T(8,128)S(1)} %collective-permute-done.11.refs_1_, f32[128,128]{1,0:T(8,128)S(1)} %collective-permute-done.12.refs_2_, ...), custom_call_target="tpu_custom_call" | custom-call | tf_op jit(solution)/shard_map/pallas_call | solution.py:52
  63.3 1.8 %shard_map.58 = (f32[1024,128]{1,0:T(8,128)S(1)}, f32[1024,128]{1,0:T(8,128)S(1)}, f32[1024,128]{1,0:T(8,128)S(1)}, f32[1024,128]{1,0:T(8,128)S(1)}, f32[256,128...) custom-call(s32[16]{0:T(128)S(1)} %constant_dynamic-update-slice_fusion.f, ...), custom_call_target="tpu_custom_call" | custom-call | tf_op jit(solution)/shard_map/pallas_call | solution.py:52
  65.1 2.2 %collective-permute-start.15 = (f32[1024,128]{1,0:T(8,128)S(1)}, f32[1024,128]{1,0:T(8,128)S(1)}, u32[]{:S(2)}, u32[]{:S(2)}) collective-permute-start(f32[1024,128]{1,0:T(8,128)S(1)} %get-tuple-element.105), channel_id=1, source_target_pairs={{8,0},{9,1},{10,2},{11,3},{12,4},{13,5},{14,6},{15,7},{0,8},{1,9},... | collective-permute-start | bytes 1572872 | tf_op jit(solution)/shard_map/ppermute | solution.py:525
  71.1 4.4 %collective-permute-start.18 = (f32[256,128]{1,0:T(8,128)S(1)}, f32[256,128]{1,0:T(8,128)S(1)}, u32[]{:S(2)}, u32[]{:S(2)}) collective-permute-start(f32[256,128]{1,0:T(8,128)S(1)} %get-tuple-element.115), channel_id=1, source_target_pairs={{8,0},{9,1},{10,2},{11,3},{12,4},{13,5},{14,6},{15,7},{0,8},{1,9},... | collective-permute-start | bytes 393224 | tf_op jit(solution)/shard_map/ppermute | solution.py:525
  76.8 3.2 %collective-permute-done.15.refs_0_ = f32[1024,128]{1,0:T(8,128)S(1)} collective-permute-done((f32[1024,128]{1,0:T(8,128)S(1)}, f32[1024,128]{1,0:T(8,128)S(1)}, u32[]{:S(2)}, u32[]{:S(2)}) %collective-permute-start.15) | collective-permute-done | bytes 524320 | tf_op jit(solution)/shard_map/ppermute | solution.py:525
  83.7 1.9 %collective-permute-start.24 = (f32[128,128]{1,0:T(8,128)S(1)}, f32[128,128]{1,0:T(8,128)S(1)}, u32[]{:S(2)}, u32[]{:S(2)}) collective-permute-start(f32[128,128]{1,0:T(8,128)S(1)} %add.36.refs_0_), channel_id=1, source_target_pairs={{6,0},{7,1},{4,2},{5,3},{2,4},{3,5},{0,6},{1,7},{14,8},{15,9},{12,... | collective-permute-start | bytes 196616 | tf_op jit(solution)/shard_map/ppermute | solution.py:525
  87.3 1.8 %collective-permute-done.24.refs_3_ = f32[128,128]{1,0:T(8,128)S(1)} collective-permute-done((f32[128,128]{1,0:T(8,128)S(1)}, f32[128,128]{1,0:T(8,128)S(1)}, u32[]{:S(2)}, u32[]{:S(2)}) %collective-permute-start.24) | collective-permute-done | bytes 65568 | tf_op jit(solution)/shard_map/ppermute | solution.py:525
  90.5 3.0 %shard_map.61 = (f32[256,256]{1,0:T(8,128)S(1)}, f32[256,256]{1,0:T(8,128)S(1)}) custom-call(s32[16]{0:T(128)S(1)} %constant_dynamic-update-slice_fusion.f, f32[128,128]{1,0:T(8,128)S(1)} %add.36.refs_0_, f32[128,128]{1,0:T(8,128)S(1)} %collective-permute-done.22.refs_1_, f32[128,128]{1,0:T(8,128)S(1)} %collective-permute-done.23.refs_2_, ...), custom_call_target="tpu_custom_call" | custom-call | tf_op jit(solution)/shard_map/pallas_call | solution.py:52
  95.1 1.8 %shard_map.62 = (f32[1280,128]{1,0:T(8,128)S(1)}, f32[1280,128]{1,0:T(8,128)S(1)}, f32[1280,128]{1,0:T(8,128)S(1)}, f32[1280,128]{1,0:T(8,128)S(1)}, f32[1280,128]{1,0:T(8,128)S(1)}) custom-call(s32[16]{0:T(128)S(1)} %constant_dynamic-update-slice_fusion.f, f32[256,256]{1,0:T(8,128)S(1)} %get-tuple-element.121.own_ref.rotation_ref, ...), custom_call_target="tpu_custom_call" | custom-call | tf_op jit(solution)/shard_map/pallas_call | solution.py:52
  96.9 4.8 %collective-permute-start.26 = (f32[1280,128]{1,0:T(8,128)S(1)}, f32[1280,128]{1,0:T(8,128)S(1)}, u32[]{:S(2)}, u32[]{:S(2)}) collective-permute-start(f32[1280,128]{1,0:T(8,128)S(1)} %get-tuple-element.128), channel_id=1, source_target_pairs={{8,0},{9,1},{10,2},{11,3},{12,4},{13,5},{14,6},{15,7},{0,8},{1,9},... | collective-permute-start | bytes 1966088 | tf_op jit(solution)/shard_map/ppermute | solution.py:525
  105.3 4.5 %collective-permute-start.29 = (f32[128,128]{1,0:T(8,128)S(1)}, f32[128,128]{1,0:T(8,128)S(1)}, u32[]{:S(2)}, u32[]{:S(2)}) collective-permute-start(f32[128,128]{1,0:T(8,128)S(1)} %get-tuple-element.132), channel_id=1, source_target_pairs={{1,0},{0,1},{3,2},{2,3},{5,4},{4,5},{7,6},{6,7},{9,8},{8,9},{11,10... | collective-permute-start | bytes 196616 | tf_op jit(solution)/shard_map/ppermute | solution.py:525
  109.8 6.9 %collective-permute-done.26.a_ref.refs_0_ = f32[1280,128]{1,0:T(8,128)S(1)} collective-permute-done((f32[1280,128]{1,0:T(8,128)S(1)}, f32[1280,128]{1,0:T(8,128)S(1)}, u32[]{:S(2)}, u32[]{:S(2)}) %collective-permute-start.26) | collective-permute-done | bytes 655392 | tf_op jit(solution)/shard_map/ppermute | solution.py:525
  118.0 1.7 %shard_map.65 = (f32[128,128]{1,0:T(8,128)S(1)}, f32[128,128]{1,0:T(8,128)S(1)}, f32[1280,128]{1,0:T(8,128)S(1)}, f32[1280,128]{1,0:T(8,128)S(1)}) custom-call(s32[16]{0:T(128)S(1)} %constant_dynamic-update-slice_fusion.f, f32[1280,128]{1,0:T(8,128)S(1)} %collective-permute-done.26.a_ref.refs_0_, f32[1280,128]{1,0:T(8,128)S(1)} %collective-permute-done.27.b_ref.refs_1_, ...), custom_call_target="tpu_custom_call" | custom-call | tf_op jit(solution)/shard_map/pallas_call | solution.py:52
  121.0 2.1 %collective-permute-start.34 = (f32[128,128]{1,0:T(8,128)S(1)}, f32[128,128]{1,0:T(8,128)S(1)}, u32[]{:S(2)}, u32[]{:S(2)}) collective-permute-start(f32[128,128]{1,0:T(8,128)S(1)} %add.37.refs_0_), channel_id=1, source_target_pairs={{6,0},{7,1},{4,2},{5,3},{2,4},{3,5},{0,6},{1,7},{14,8},{15,9},{12,... | collective-permute-start | bytes 196616 | tf_op jit(solution)/shard_map/ppermute | solution.py:525
  125.1 3.4 %collective-permute-done.34.refs_3_ = f32[128,128]{1,0:T(8,128)S(1)} collective-permute-done((f32[128,128]{1,0:T(8,128)S(1)}, f32[128,128]{1,0:T(8,128)S(1)}, u32[]{:S(2)}, u32[]{:S(2)}) %collective-permute-start.34) | collective-permute-done | bytes 65568 | tf_op jit(solution)/shard_map/ppermute | solution.py:525
  129.6 3.4 %shard_map.67 = (f32[264,256]{1,0:T(8,128)S(1)}, f32[256,256]{1,0:T(8,128)}) custom-call(s32[16]{0:T(128)S(1)} %constant_dynamic-update-slice_fusion.f, f32[128,128]{1,0:T(8,128)S(1)} %add.37.refs_0_, f32[128,128]{1,0:T(8,128)S(1)} %collective-permute-done.32.refs_1_, f32[128,128]{1,0:T(8,128)S(1)} %collective-permute-done.33.refs_2_, ...), custom_call_target="tpu_custom_call" | custom-call | tf_op jit(solution)/shard_map/pallas_call | solution.py:52
  134.7 3.0 %shard_map.68 = (f32[2048,256]{1,0:T(8,128)}, f32[512,256]{1,0:T(8,128)}, f32[1,256]{1,0:T(1,128)}) custom-call(s32[16]{0:T(128)S(1)} %constant_dynamic-update-slice_fusion.f, f32[264,256]{1,0:T(8,128)S(1)} %get-tuple-element.148.own_ref, f32[264,256]{1,0:T(8,128)S(1)} %collective-permute-done.36.other_ref, f32[1280,128]{1,0:T(8,128)S(1)} %get-tuple-element.151.refs_0_, ...), custom_call_target="tpu_custom_call" | custom-call | flops 1 | bytes 1 | tf_op jit(solution)/shard_map/pallas_call | solution.py:424
  139.0 2.0 %shard_map.69 = (f32[2048,256]{1,0:T(8,128)}, f32[512,256]{1,0:T(8,128)}) custom-call(s32[16]{0:T(128)S(1)} %constant_dynamic-update-slice_fusion.f, f32[264,256]{1,0:T(8,128)S(1)} %get-tuple-element.148.own_ref, f32[264,256]{1,0:T(8,128)S(1)} %collective-permute-done.36.other_ref, ...), custom_call_target="tpu_custom_call", output_to_operand_aliasing={{0}: (5, {}), {1}: (6, {})} | custom-call | flops 1 | bytes 1 | tf_op jit(solution)/shard_map/pallas_call | solution.py:424
  (77 shorter events, 40.1 us)
Async XLA Ops:
  3.1 27.2 %collective-permute-start.4 = (f32[768,256]{1,0:T(8,128)}, f32[768,256]{1,0:T(8,128)S(1)}, u32[]{:S(2)}, u32[]{:S(2)}) collective-permute-start(f32[768,256]{1,0:T(8,128)} %get-tuple-element.86), channel_id=1, source_target_pairs={{4,0},{5,1},{6,2},{7,3},{0,4},{1,5},{2,6},{3,7},{12,8},{13,9},{14,... | collective-permute-start | bytes 2359304 | tf_op jit(solution)/shard_map/ppermute | solution.py:525
  9.8 7.0 %collective-permute-start.1 = (f32[384,128]{1,0:T(8,128)S(1)}, f32[384,128]{1,0:T(8,128)S(1)}, u32[]{:S(2)}, u32[]{:S(2)}) collective-permute-start(f32[384,128]{1,0:T(8,128)S(1)} %add.34.own_ref), channel_id=1, source_target_pairs={{2,0},{3,1},{0,2},{1,3},{6,4},{7,5},{4,6},{5,7},{10,8},{11,9},{8,1... | collective-permute-start | bytes 589832 | tf_op jit(solution)/shard_map/ppermute | solution.py:525
  20.3 10.0 %collective-permute-start.3 = (f32[256,256]{1,0:T(8,128)S(1)}, f32[256,256]{1,0:T(8,128)S(1)}, u32[]{:S(2)}, u32[]{:S(2)}) collective-permute-start(f32[256,256]{1,0:T(8,128)S(1)} %get-tuple-element.81.rotation_ref), channel_id=1, source_target_pairs={{4,0},{5,1},{6,2},{7,3},{0,4},{1,5},{2,6},{3,7},{12,8},{13,9},{14,... | collective-permute-start | bytes 786440 | tf_op jit(solution)/shard_map/ppermute | solution.py:525
  21.9 25.5 %collective-permute-start.2 = (f32[1280,128]{1,0:T(8,128)S(1)}, f32[1280,128]{1,0:T(8,128)S(1)}, u32[]{:S(2)}, u32[]{:S(2)}) collective-permute-start(f32[1280,128]{1,0:T(8,128)S(1)} %get-tuple-element.85.refs_1_), channel_id=1, source_target_pairs={{8,0},{9,1},{10,2},{11,3},{16,8},{17,9},{18,10},{19,11},{4,12},{5,... | collective-permute-start | bytes 1966088 | tf_op jit(solution)/shard_map/ppermute | solution.py:525
  23.2 12.2 %collective-permute-start.6 = (f32[256,256]{1,0:T(8,128)S(1)}, f32[256,256]{1,0:T(8,128)S(1)}, u32[]{:S(2)}, u32[]{:S(2)}) collective-permute-start(f32[256,256]{1,0:T(8,128)S(1)} %copy-done.1), channel_id=1, source_target_pairs={{4,0},{5,1},{6,2},{7,3},{0,4},{1,5},{2,6},{3,7},{12,8},{13,9},{14,... | collective-permute-start | bytes 786440 | tf_op jit(solution)/shard_map/ppermute | solution.py:525
  31.4 16.0 %collective-permute-start.5 = (f32[768,128]{1,0:T(8,128)S(1)}, f32[768,128]{1,0:T(8,128)S(1)}, u32[]{:S(2)}, u32[]{:S(2)}) collective-permute-start(f32[768,128]{1,0:T(8,128)S(1)} %get-tuple-element.88.refs_4_), channel_id=1, source_target_pairs={{12,4},{13,5},{14,6},{15,7},{0,8},{1,9},{2,10},{3,11},{20,12},{21,... | collective-permute-start | bytes 1179656 | tf_op jit(solution)/shard_map/ppermute | solution.py:525
  36.4 11.0 %collective-permute-start.7 = (f32[512,128]{1,0:T(8,128)S(1)}, f32[512,128]{1,0:T(8,128)S(1)}, u32[]{:S(2)}, u32[]{:S(2)}) collective-permute-start(f32[512,128]{1,0:T(8,128)S(1)} %get-tuple-element.91.refs_7_), channel_id=1, source_target_pairs={{12,4},{13,5},{14,6},{15,7},{0,8},{1,9},{2,10},{3,11},{20,12},{21,... | collective-permute-start | bytes 786440 | tf_op jit(solution)/shard_map/ppermute | solution.py:525
  41.5 7.7 %collective-permute-start.8 = (f32[128,128]{1,0:T(8,128)S(1)}, f32[128,128]{1,0:T(8,128)S(1)}, u32[]{:S(2)}, u32[]{:S(2)}) collective-permute-start(f32[128,128]{1,0:T(8,128)S(1)} %get-tuple-element.95), channel_id=1, source_target_pairs={{0,0},{8,1},{2,2},{10,3},{1,4},{9,5},{3,6},{11,7},{4,8},{16,9},{6,... | collective-permute-start | bytes 196616 | tf_op jit(solution)/shard_map/ppermute | solution.py:525
  42.2 7.1 %collective-permute-start.9 = (f32[128,128]{1,0:T(8,128)S(1)}, f32[128,128]{1,0:T(8,128)S(1)}, u32[]{:S(2)}, u32[]{:S(2)}) collective-permute-start(f32[128,128]{1,0:T(8,128)S(1)} %get-tuple-element.96), channel_id=1, source_target_pairs={{4,0},{0,1},{6,2},{2,3},{5,4},{1,5},{7,6},{3,7},{12,8},{8,9},{14,1... | collective-permute-start | bytes 196616 | tf_op jit(solution)/shard_map/ppermute | solution.py:525
  50.6 5.8 %collective-permute-start.13 = (f32[128,128]{1,0:T(8,128)S(1)}, f32[128,128]{1,0:T(8,128)S(1)}, u32[]{:S(2)}, u32[]{:S(2)}) collective-permute-start(f32[128,128]{1,0:T(8,128)S(1)} %add.35.refs_0_), channel_id=1, source_target_pairs={{6,0},{7,1},{4,2},{5,3},{2,4},{3,5},{0,6},{1,7},{14,8},{15,9},{12,... | collective-permute-start | bytes 196616 | tf_op jit(solution)/shard_map/ppermute | solution.py:525
  54.0 4.3 %collective-permute-start.12 = (f32[128,128]{1,0:T(8,128)S(1)}, f32[128,128]{1,0:T(8,128)S(1)}, u32[]{:S(2)}, u32[]{:S(2)}) collective-permute-start(f32[128,128]{1,0:T(8,128)S(1)} %add.35.refs_0_), channel_id=1, source_target_pairs={{4,0},{5,1},{6,2},{7,3},{0,4},{1,5},{2,6},{3,7},{12,8},{13,9},{14,... | collective-permute-start | bytes 196616 | tf_op jit(solution)/shard_map/ppermute | solution.py:525
  54.0 4.3 %collective-permute-start.11 = (f32[128,128]{1,0:T(8,128)S(1)}, f32[128,128]{1,0:T(8,128)S(1)}, u32[]{:S(2)}, u32[]{:S(2)}) collective-permute-start(f32[128,128]{1,0:T(8,128)S(1)} %add.35.refs_0_), channel_id=1, source_target_pairs={{2,0},{3,1},{0,2},{1,3},{6,4},{7,5},{4,6},{5,7},{10,8},{11,9},{8,1... | collective-permute-start | bytes 196616 | tf_op jit(solution)/shard_map/ppermute | solution.py:525
  65.1 14.9 %collective-permute-start.15 = (f32[1024,128]{1,0:T(8,128)S(1)}, f32[1024,128]{1,0:T(8,128)S(1)}, u32[]{:S(2)}, u32[]{:S(2)}) collective-permute-start(f32[1024,128]{1,0:T(8,128)S(1)} %get-tuple-element.105), channel_id=1, source_target_pairs={{8,0},{9,1},{10,2},{11,3},{12,4},{13,5},{14,6},{15,7},{0,8},{1,9},... | collective-permute-start | bytes 1572872 | tf_op jit(solution)/shard_map/ppermute | solution.py:525
  67.3 12.7 %collective-permute-start.16 = (f32[1024,128]{1,0:T(8,128)S(1)}, f32[1024,128]{1,0:T(8,128)S(1)}, u32[]{:S(2)}, u32[]{:S(2)}) collective-permute-start(f32[1024,128]{1,0:T(8,128)S(1)} %get-tuple-element.106), channel_id=1, source_target_pairs={{0,0},{1,1},{2,2},{3,3},{4,4},{5,5},{6,6},{7,7},{16,8},{17,9},{18,... | collective-permute-start | bytes 1572872 | tf_op jit(solution)/shard_map/ppermute | solution.py:525
  71.1 11.2 %collective-permute-start.18 = (f32[256,128]{1,0:T(8,128)S(1)}, f32[256,128]{1,0:T(8,128)S(1)}, u32[]{:S(2)}, u32[]{:S(2)}) collective-permute-start(f32[256,128]{1,0:T(8,128)S(1)} %get-tuple-element.115), channel_id=1, source_target_pairs={{8,0},{9,1},{10,2},{11,3},{12,4},{13,5},{14,6},{15,7},{0,8},{1,9},... | collective-permute-start | bytes 393224 | tf_op jit(solution)/shard_map/ppermute | solution.py:525
  75.5 6.9 %collective-permute-start.19 = (f32[256,128]{1,0:T(8,128)S(1)}, f32[256,128]{1,0:T(8,128)S(1)}, u32[]{:S(2)}, u32[]{:S(2)}) collective-permute-start(f32[256,128]{1,0:T(8,128)S(1)} %get-tuple-element.116), channel_id=1, source_target_pairs={{0,0},{1,1},{2,2},{3,3},{4,4},{5,5},{6,6},{7,7},{16,8},{17,9},{18,... | collective-permute-start | bytes 393224 | tf_op jit(solution)/shard_map/ppermute | solution.py:525
  76.1 5.5 %collective-permute-start.20 = (f32[128,128]{1,0:T(8,128)S(1)}, f32[128,128]{1,0:T(8,128)S(1)}, u32[]{:S(2)}, u32[]{:S(2)}) collective-permute-start(f32[128,128]{1,0:T(8,128)S(1)} %get-tuple-element.117), channel_id=1, source_target_pairs={{0,0},{8,1},{2,2},{10,3},{4,4},{12,5},{6,6},{14,7},{1,8},{16,9},{3... | collective-permute-start | bytes 196616 | tf_op jit(solution)/shard_map/ppermute | solution.py:525
  83.7 5.4 %collective-permute-start.24 = (f32[128,128]{1,0:T(8,128)S(1)}, f32[128,128]{1,0:T(8,128)S(1)}, u32[]{:S(2)}, u32[]{:S(2)}) collective-permute-start(f32[128,128]{1,0:T(8,128)S(1)} %add.36.refs_0_), channel_id=1, source_target_pairs={{6,0},{7,1},{4,2},{5,3},{2,4},{3,5},{0,6},{1,7},{14,8},{15,9},{12,... | collective-permute-start | bytes 196616 | tf_op jit(solution)/shard_map/ppermute | solution.py:525
  85.6 4.3 %collective-permute-start.23 = (f32[128,128]{1,0:T(8,128)S(1)}, f32[128,128]{1,0:T(8,128)S(1)}, u32[]{:S(2)}, u32[]{:S(2)}) collective-permute-start(f32[128,128]{1,0:T(8,128)S(1)} %add.36.refs_0_), channel_id=1, source_target_pairs={{4,0},{5,1},{6,2},{7,3},{0,4},{1,5},{2,6},{3,7},{12,8},{13,9},{14,... | collective-permute-start | bytes 196616 | tf_op jit(solution)/shard_map/ppermute | solution.py:525
  86.0 4.5 %collective-permute-start.22 = (f32[128,128]{1,0:T(8,128)S(1)}, f32[128,128]{1,0:T(8,128)S(1)}, u32[]{:S(2)}, u32[]{:S(2)}) collective-permute-start(f32[128,128]{1,0:T(8,128)S(1)} %add.36.refs_0_), channel_id=1, source_target_pairs={{2,0},{3,1},{0,2},{1,3},{6,4},{7,5},{4,6},{5,7},{10,8},{11,9},{8,1... | collective-permute-start | bytes 196616 | tf_op jit(solution)/shard_map/ppermute | solution.py:525
  93.5 1.6 %collective-permute-start.25 = (f32[256,256]{1,0:T(8,128)S(1)}, f32[256,256]{1,0:T(8,128)S(1)}, u32[]{:S(2)}, u32[]{:S(2)}) collective-permute-start(f32[256,256]{1,0:T(8,128)S(1)} %get-tuple-element.121.own_ref.rotation_ref), channel_id=1, source_target_pairs={{1,0},{0,1},{3,2},{2,3},{5,4},{4,5},{7,6},{6,7},{9,8},{8,9},{11,10... | collective-permute-start | bytes 786440 | tf_op jit(solution)/shard_map/ppermute | solution.py:525
  96.9 19.9 %collective-permute-start.26 = (f32[1280,128]{1,0:T(8,128)S(1)}, f32[1280,128]{1,0:T(8,128)S(1)}, u32[]{:S(2)}, u32[]{:S(2)}) collective-permute-start(f32[1280,128]{1,0:T(8,128)S(1)} %get-tuple-element.128), channel_id=1, source_target_pairs={{8,0},{9,1},{10,2},{11,3},{12,4},{13,5},{14,6},{15,7},{0,8},{1,9},... | collective-permute-start | bytes 1966088 | tf_op jit(solution)/shard_map/ppermute | solution.py:525
  101.7 15.0 %collective-permute-start.27 = (f32[1280,128]{1,0:T(8,128)S(1)}, f32[1280,128]{1,0:T(8,128)S(1)}, u32[]{:S(2)}, u32[]{:S(2)}) collective-permute-start(f32[1280,128]{1,0:T(8,128)S(1)} %get-tuple-element.129), channel_id=1, source_target_pairs={{0,0},{1,1},{2,2},{3,3},{4,4},{5,5},{6,6},{7,7},{16,8},{17,9},{18,... | collective-permute-start | bytes 1966088 | tf_op jit(solution)/shard_map/ppermute | solution.py:525
  102.4 17.2 %collective-permute-start.30 = (f32[1280,128]{1,0:T(8,128)S(1)}, f32[1280,128]{1,0:T(8,128)S(1)}, u32[]{:S(2)}, u32[]{:S(2)}) collective-permute-start(f32[1280,128]{1,0:T(8,128)S(1)} %get-tuple-element.139), channel_id=1, source_target_pairs={{4,0},{5,1},{6,2},{7,3},{0,4},{1,5},{2,6},{3,7},{12,8},{13,9},{14,... | collective-permute-start | bytes 1966088 | tf_op jit(solution)/shard_map/ppermute | solution.py:525
  104.7 12.7 %collective-permute-start.28 = (f32[128,128]{1,0:T(8,128)S(1)}, f32[128,128]{1,0:T(8,128)S(1)}, u32[]{:S(2)}, u32[]{:S(2)}) collective-permute-start(f32[128,128]{1,0:T(8,128)S(1)} %get-tuple-element.131), channel_id=1, source_target_pairs={{0,0},{8,1},{2,2},{10,3},{4,4},{12,5},{6,6},{14,7},{1,8},{16,9},{3... | collective-permute-start | bytes 196616 | tf_op jit(solution)/shard_map/ppermute | solution.py:525
  105.3 12.0 %collective-permute-start.29 = (f32[128,128]{1,0:T(8,128)S(1)}, f32[128,128]{1,0:T(8,128)S(1)}, u32[]{:S(2)}, u32[]{:S(2)}) collective-permute-start(f32[128,128]{1,0:T(8,128)S(1)} %get-tuple-element.132), channel_id=1, source_target_pairs={{1,0},{0,1},{3,2},{2,3},{5,4},{4,5},{7,6},{6,7},{9,8},{8,9},{11,10... | collective-permute-start | bytes 196616 | tf_op jit(solution)/shard_map/ppermute | solution.py:525
  117.4 11.2 %collective-permute-start.35 = (f32[512,128]{1,0:T(8,128)S(1)}, f32[512,128]{1,0:T(8,128)S(1)}, u32[]{:S(2)}, u32[]{:S(2)}) collective-permute-start(f32[512,128]{1,0:T(8,128)S(1)} %shard_map.63), channel_id=1, source_target_pairs={{4,0},{5,1},{6,2},{7,3},{0,4},{1,5},{2,6},{3,7},{12,8},{13,9},{14,... | collective-permute-start | bytes 786440 | tf_op jit(solution)/shard_map/ppermute | solution.py:525
  121.0 7.6 %collective-permute-start.34 = (f32[128,128]{1,0:T(8,128)S(1)}, f32[128,128]{1,0:T(8,128)S(1)}, u32[]{:S(2)}, u32[]{:S(2)}) collective-permute-start(f32[128,128]{1,0:T(8,128)S(1)} %add.37.refs_0_), channel_id=1, source_target_pairs={{6,0},{7,1},{4,2},{5,3},{2,4},{3,5},{0,6},{1,7},{14,8},{15,9},{12,... | collective-permute-start | bytes 196616 | tf_op jit(solution)/shard_map/ppermute | solution.py:525
  123.1 5.5 %collective-permute-start.33 = (f32[128,128]{1,0:T(8,128)S(1)}, f32[128,128]{1,0:T(8,128)S(1)}, u32[]{:S(2)}, u32[]{:S(2)}) collective-permute-start(f32[128,128]{1,0:T(8,128)S(1)} %add.37.refs_0_), channel_id=1, source_target_pairs={{4,0},{5,1},{6,2},{7,3},{0,4},{1,5},{2,6},{3,7},{12,8},{13,9},{14,... | collective-permute-start | bytes 196616 | tf_op jit(solution)/shard_map/ppermute | solution.py:525
  123.6 5.0 %collective-permute-start.32 = (f32[128,128]{1,0:T(8,128)S(1)}, f32[128,128]{1,0:T(8,128)S(1)}, u32[]{:S(2)}, u32[]{:S(2)}) collective-permute-start(f32[128,128]{1,0:T(8,128)S(1)} %add.37.refs_0_), channel_id=1, source_target_pairs={{2,0},{3,1},{0,2},{1,3},{6,4},{7,5},{4,6},{5,7},{10,8},{11,9},{8,1... | collective-permute-start | bytes 196616 | tf_op jit(solution)/shard_map/ppermute | solution.py:525
  128.6 10.3 %collective-permute-start.37 = (f32[768,128]{1,0:T(8,128)S(1)}, f32[768,128]{1,0:T(8,128)S(1)}, u32[]{:S(2)}, u32[]{:S(2)}) collective-permute-start(f32[768,128]{1,0:T(8,128)S(1)} %shard_map.66), channel_id=1, source_target_pairs={{4,0},{5,1},{6,2},{7,3},{0,4},{1,5},{2,6},{3,7},{12,8},{13,9},{14,... | collective-permute-start | bytes 1179656 | tf_op jit(solution)/shard_map/ppermute | solution.py:525
  133.0 1.6 %collective-permute-start.36 = (f32[264,256]{1,0:T(8,128)S(1)}, f32[264,256]{1,0:T(8,128)S(1)}, u32[]{:S(2)}, u32[]{:S(2)}) collective-permute-start(f32[264,256]{1,0:T(8,128)S(1)} %get-tuple-element.148.own_ref), channel_id=1, source_target_pairs={{1,0},{0,1},{3,2},{2,3},{5,4},{4,5},{7,6},{6,7},{9,8},{8,9},{11,10... | collective-permute-start | bytes 811016 | tf_op jit(solution)/shard_map/ppermute | solution.py:525
  (9 other events, 39.7 us)

commit v13 on v12

--- a/solution.py
+++ b/solution.py
@@ -220,42 +220,11 @@
     return call(body, facts, [gram, rotation], (shape(half, half),) * 2)
 
 
-def two_packs(f, own, other):
-    core = f[CORE] == 0
-    return jnp.where(core, own, other), jnp.where(core, other, own)
-
-
 def swapped(flag, matrix, axis):
     half = matrix.shape[axis] // 2
     a = lax.slice_in_dim(matrix, 0, half, axis=axis)
     b = lax.slice_in_dim(matrix, half, 2 * half, axis=axis)
     return jnp.where(flag, lax.concatenate([b, a], axis), matrix)
-
-
-def blocks_of(f, got_a, got_b, low_0, up_1):
-    even = f[EVEN] == 1
-    return (
-        jnp.where(even, got_b, got_a), low_0, up_1, jnp.where(even, got_a, got_b)
-    )
-
-
-def put_turned(f, refs, zero, one, half, at=0):
-    a_ref, b_ref, nat_l_ref, nat_u_ref = refs[:4]
-    even = f[EVEN] == 1
-    rows = slice(at, at + zero.shape[0])
-    to_left, to_right = zero[:, half:], one[:, :half]
-    a_ref[rows] = jnp.where(even, to_right, to_left)
-    b_ref[rows] = jnp.where(even, to_left, to_right)
-    nat_l_ref[rows] = one[:, half:]
-    nat_u_ref[rows] = zero[:, :half]
-    if len(refs) > 4:
-        refs[4][rows] = jnp.where(f[X] == 0, zero[:, :half], one[:, half:])
-
-
-def turns_of(f, own_ref, other_ref):
-    size = other_ref.shape[1]
-    turn_0, turn_1 = two_packs(f, own_ref[:size], other_ref[:size])
-    return swapped(f[FIRST] == 1, turn_0, 1), turn_1
 
 
 def turn_rows(facts, rotation, rows_of, vector_rows, half, own):
@@ -286,31 +255,30 @@
     )
 
 
-def turn(facts, packs, blocks, vectors, part, vector_rows, half, last_move):
-    inputs = packs + blocks + vectors
-
-    def body(f, own_ref, other_ref, *refs):
-        turn_0, turn_1 = turns_of(f, own_ref, other_ref)
-        turn_0, turn_1 = split(turn_0), split(turn_1)
-        columns = [r[:part] for r in refs[:4]]
-        if vectors:
-            rows = blocks_of(f, *[r[...] for r in refs[4:8]])
-        else:
-            rows = [r[part:] for r in refs[:4]]
-        outs = refs[len(inputs) - 2 :]
-        for (up_0, low_0, up_1, low_1), at in ((columns, 0), (rows, part)):
-            zero = dot3(lax.concatenate([up_0, low_0], 1), turn_0)
-            one = dot3(lax.concatenate([up_1, low_1], 1), turn_1)
-            if last_move:
-                put_turned(f, outs, zero, one, half, at)
-            else:
-                put_turned(f, outs[4 if at else 0 :][:4], zero, one, half)
-
-    if last_move:
-        outs = (shape(part + vector_rows, half),) * 5
-    else:
-        outs = (shape(part, half),) * 4 + (shape(vector_rows, half),) * 4
-    return call(body, facts, inputs, outs)
+def turn(facts, rotation, blocks, own, own_stay=None):
+    rows, half = blocks[0].shape
+    size = 2 * half
+    extra = [] if own_stay is None else [own_stay]
+
+    def body(f, rotation_ref, *refs):
+        up_0, low_0, up_1, low_1 = [r[...] for r in refs[:4]]
+        zero = f[CORE] == (0 if own else 1)
+        upper_leaves = jnp.where(zero, f[FIRST], 1) == 1
+        turned = swapped(upper_leaves, rotation_ref[:size], 1)
+        columns = lax.concatenate(
+            [jnp.where(zero, up_0, up_1), jnp.where(zero, low_0, low_1)], 1
+        )
+        out = dot3(columns, turned)
+        outs = refs[4 + len(extra) :]
+        outs[0][...] = out[:, :half]
+        outs[1][...] = out[:, half:]
+        if extra:
+            outs[2][...] = jnp.where(f[CORE] == f[X], refs[4][...], out[:, :half])
+
+    return call(
+        body, facts, [rotation] + blocks + extra,
+        (shape(rows, half),) * (2 + len(extra)),
+    )
 
 
 def put_cross(f, refs, zero, one):
@@ -319,7 +287,7 @@
     refs[1][...] = jnp.where(core, one, zero)
 
 
-def first_cross_gram(facts, own, others, part, half):
+def cross_gram(facts, own, others, position, part, half):
     rows = own[0].shape[0]
     pieces = len(others)
 
@@ -336,7 +304,7 @@
 
         first, last = f[FIRST] == 1, f[LAST] == 1
         for x, near, far in ((0, own_refs, other_refs), (1, other_refs, own_refs)):
-            here = f[X] == x
+            here = f[position] == x
 
             @pl.when(here)
             def _():
@@ -370,30 +338,15 @@
     return call(body, facts, own + sum(others, []), outs)
 
 
-def cross_gram(facts, got, natives, part, half):
-    rows = got[0].shape[0]
-
-    def body(f, *refs):
-        up_0, low_0, up_1, low_1 = blocks_of(f, *[r[...] for r in refs[:4]])
-        put_cross(
-            f,
-            refs[4:],
-            dot_tn(up_0[:part], low_0[:part]),
-            dot_tn(up_1[:part], low_1[:part]),
+def give(facts, blocks, start, stop, half):
+    def body(f, up_0_ref, low_1_ref, out_ref):
+        out_ref[...] = jnp.where(
+            f[X] == 0, low_1_ref[start:stop], up_0_ref[start:stop]
         )
-        refs[6][...] = up_0
-        refs[7][...] = low_1
-
-    outs = (shape(half, half),) * 2 + (shape(rows, half),) * 2
-    return call(body, facts, got + natives, outs)
-
-
-def give(facts, got, start, stop, half):
-    def body(f, a_ref, b_ref, out_ref):
-        mine = f[X] != f[EVEN]
-        out_ref[...] = jnp.where(mine, a_ref[start:stop], b_ref[start:stop])
-
-    return call(body, facts, got, shape(stop - start, half))
+
+    return call(
+        body, facts, [blocks[0], blocks[3]], shape(stop - start, half)
+    )
 
 
 def final_turn(f, own_ref, other_ref, size):
@@ -531,19 +484,12 @@
             block, [((p ^ over_pair, r ^ over_row), (p, r)) for p, r in devices]
         )
 
-    def shift(block, even_by):
+    def shift(block, leftward):
         moves = []
         for p, r in devices:
-            source = p - even_by if p % 2 == 0 else p + even_by
+            source = p + 2 if leftward(p, r) else p - 2
             if 0 <= source < pairs:
                 moves.append(((source, r), (p, r)))
-        return permute(block, moves)
-
-    def swap(block, odd):
-        moves = []
-        for p, r in devices:
-            other = p + 2 if p // 2 % 2 == odd else p - 2
-            moves.append(((other if 0 <= other < pairs else p, r), (p, r)))
         return permute(block, moves)
 
     def pass_diagonal(block):
@@ -597,7 +543,6 @@
     own = sum_rows(own + exchange(own, 0, 1))
     rotation, gram = first_rotation(facts, own, exchange(own, 0, 2), half)
 
-    vectors = []
     for sweep_round in range(ROUNDS - 1):
         last_move = sweep_round == ROUNDS - 2
         if sweep_round == 0:
@@ -605,52 +550,42 @@
             stay, leave = turn_rows(facts, rotation, sector, vector_rows, half, True)
             leave, rest_give = together(leave, rest_give)
             got_rest = exchange(rest_give, 1, 0)
-            own_rows = [stay, leave, shift(leave, -2)]
-            other_rows = []
+            own = [stay, leave, shift(leave, lambda p, r: p % 2 == 0)]
+            others = []
             for got, below in ((got_top, 0), (got_rest, vector_rows)):
                 stay, leave = turn_rows(facts, other_rotation, got, below, half, False)
-                other_rows.append([stay, leave, shift(leave, 2)])
+                others.append([stay, leave, shift(leave, lambda p, r: p % 2 == 1)])
             leave, stay = turned_gram(facts, gram, rotation, X)
             diagonals = [first_diagonal(leave, True), first_diagonal(stay, False)]
-            *grams, up_0, nat_l, nat_u, low_1 = first_cross_gram(
-                facts, own_rows, other_rows, part, half
+            *grams, up_0, low_0, up_1, low_1 = cross_gram(
+                facts, own, others, X, part, half
             )
         else:
-            packs = [rotation, exchange(rotation, 0, 1)]
-            leave_a, leave_b, nat_l, nat_u, *vectors = turn(
-                facts, packs, blocks, vectors, part, vector_rows, half, last_move
+            other_rotation = exchange(rotation, 0, 1)
+            stay, leave = turn(facts, rotation, blocks, True)
+            own = [stay, leave, shift(leave, lambda p, r: r % 2 == 0)]
+            stay, leave, *native = turn(
+                facts, other_rotation, blocks, False, stay if last_move else None
             )
-            got = [swap(leave_a, 0), swap(leave_b, 1)]
+            others = [[stay, leave, shift(leave, lambda p, r: r % 2 == 1)]]
             leave, stay = turned_gram(facts, gram, rotation, CORE)
             diagonals = [pass_diagonal(leave), exchange(stay, 0, 1)]
             if last_move:
-                native = exchange(vectors.pop(), 1, 0)
-                top = part // 2
-                top_give = give(facts, got, 0, top, half)
-                *got, top_give, diagonals[0], diagonals[1] = together(
-                    *got, top_give, *diagonals
-                )
-                got_top = exchange(top_give, 1, 0)
-            else:
-                vectors[0], vectors[1], diagonals[1] = together(
-                    vectors[0], vectors[1], diagonals[1]
-                )
-            *grams, up_0, low_1 = cross_gram(facts, got, [nat_l, nat_u], part, half)
-        blocks = [up_0, nat_l, nat_u, low_1]
+                native = exchange(native[0], 1, 0)
+            *grams, up_0, low_0, up_1, low_1 = cross_gram(
+                facts, own, others, CORE, part, half
+            )
+        blocks = [up_0, low_0, up_1, low_1]
+        grams[1], *diagonals = together(grams[1], *diagonals)
+        own = sum_rows(grams[0] + exchange(grams[1], 0, 1))
         if last_move:
-            grams[1], native = together(grams[1], native)
-        elif sweep_round == 0:
-            grams[1], *diagonals = together(grams[1], *diagonals)
-        else:
-            vector_a, vector_b, *kept = vectors
-            grams[1], vector_a, vector_b, diagonals[0] = together(
-                grams[1], swap(vector_a, 0), swap(vector_b, 1), diagonals[0]
-            )
-            vectors = [vector_a, vector_b] + kept
-        own = sum_rows(grams[0] + exchange(grams[1], 0, 1))
+            top = part // 2
+            top_give = give(facts, blocks, 0, top, half)
+            own, native, top_give = together(own, native, top_give)
+            got_top = exchange(top_give, 1, 0)
         parts = [own, exchange(own, 0, 2), exchange(own, 1, 0), exchange(own, 1, 2)]
         if last_move:
-            rest_give = give(facts, got, top, part + vector_rows, half)
+            rest_give = give(facts, blocks, top, part + vector_rows, half)
             *parts, got_top, rest_give = together(*parts, got_top, rest_give)
             got_rest = exchange(rest_give, 1, 0)
         rotation, gram = later_rotation(facts, parts, diagonals, half, last_move)

time: 143 us -> 145 us (1.014); the launches traced: 141 us -> 145 us
  starting transfers between devices: 52.8 us -> 57.7 us
  waiting for transfers between devices: 45.9 us -> 42.6 us
  Pallas kernels: 40.9 us -> 42.9 us
    ppermute x38 -> x36, starting transfers between devices: 52.8 us -> 57.7 us  [permute(): return lax.ppermute(block, ('pair', 'row'), moves)]
    ppermute x38 -> x36, waiting for transfers between devices: 45.9 us -> 42.6 us  [permute(): return lax.ppermute(block, ('pair', 'row'), moves)]
    pallas_call x17 -> x19, Pallas kernels: 31.3 us -> 33.4 us  [call(): pl.pallas_call(body, out_shape=outs, in_specs=[pl.BlockSpec(memory_space=...]
  transfers between devices with their start and end apart: 38 -> 36, of which waited for: 22 -> 21; matrix products, arithmetic and copies ran while one was open for 0% -> 0% of each run, Pallas kernels for 19% -> 22%
where the time goes in v13:
time: 145 us
  starting transfers between devices  57.7 us (40%)
  Pallas kernels  42.9 us (30%)
  waiting for transfers between devices  42.6 us (29%)
    ppermute x36, starting transfers between devices, permute(): return lax.ppermute(block, ('pair', 'row'), moves)  57.7 us
    ppermute x36, waiting for transfers between devices, permute(): return lax.ppermute(block, ('pair', 'row'), moves)  42.6 us
    pallas_call x19, Pallas kernels, call(): pl.pallas_call(body, out_shape=outs, in_specs=[pl.BlockSpec(memory_space=...  33.4 us
    pallas_call x2, Pallas kernels, finish_call(): pl.pallas_call(body, out_shape=outs, in_specs=[pl.BlockSpec(memory_space=...  4.94 us
  transfers between devices with their start and end apart: 36, of which 21 were waited for; matrix products, arithmetic and copies ran while one was open for 0% of the time, Pallas kernels for 22%

profile of v13, /device:TPU:0, one launch (start us, length us, event | category | flops | bytes accessed | tf_op | source)
XLA Modules:
  0.0 144.7 jit_solution(1572374519270251167)
XLA Ops:
  0.6 2.5 %shard_map.52 = (f32[768,256]{1,0:T(8,128)}, f32[256,256]{1,0:T(8,128)}) custom-call(f32[2048,256]{1,0:T(8,128)} %x_ref.5), custom_call_target="tpu_custom_call" | custom-call | tf_op jit(solution)/shard_map/pallas_call | solution.py:104
  3.1 3.0 %collective-permute-start.4 = (f32[768,256]{1,0:T(8,128)}, f32[768,256]{1,0:T(8,128)S(1)}, u32[]{:S(2)}, u32[]{:S(2)}) collective-permute-start(f32[768,256]{1,0:T(8,128)} %get-tuple-element.81), channel_id=1, source_target_pairs={{4,0},{5,1},{6,2},{7,3},{0,4},{1,5},{2,6},{3,7},{12,8},{13,9},{14,... | collective-permute-start | bytes 2359304 | tf_op jit(solution)/shard_map/ppermute | solution.py:478
  6.1 2.2 %shard_map.49 = f32[384,128]{1,0:T(8,128)S(1)} custom-call(f32[2048,256]{1,0:T(8,128)S(1)} %copy-done), custom_call_target="tpu_custom_call" | custom-call | tf_op jit(solution)/shard_map/pallas_call | solution.py:74
  11.6 5.3 %collective-permute-done.1.other_ref = f32[384,128]{1,0:T(8,128)S(1)} collective-permute-done((f32[384,128]{1,0:T(8,128)S(1)}, f32[384,128]{1,0:T(8,128)S(1)}, u32[]{:S(2)}, u32[]{:S(2)}) %collective-permute-start.1) | collective-permute-done | bytes 196640 | tf_op jit(solution)/shard_map/ppermute | solution.py:478
  16.8 3.4 %shard_map.50 = (f32[256,256]{1,0:T(8,128)S(1)}, f32[256,256]{1,0:T(8,128)S(1)}) custom-call(s32[16]{0:T(128)S(1)} %constant_dynamic-update-slice_fusion.f, f32[384,128]{1,0:T(8,128)S(1)} %add.34.own_ref, f32[384,128]{1,0:T(8,128)S(1)} %collective-permute-done.1.other_ref), custom_call_target="tpu_custom_call" | custom-call | tf_op jit(solution)/shard_map/pallas_call | solution.py:52
  23.2 4.0 %collective-permute-start.6 = (f32[256,256]{1,0:T(8,128)S(1)}, f32[256,256]{1,0:T(8,128)S(1)}, u32[]{:S(2)}, u32[]{:S(2)}) collective-permute-start(f32[256,256]{1,0:T(8,128)S(1)} %copy-done.1), channel_id=1, source_target_pairs={{4,0},{5,1},{6,2},{7,3},{0,4},{1,5},{2,6},{3,7},{12,8},{13,9},{14,... | collective-permute-start | bytes 786440 | tf_op jit(solution)/shard_map/ppermute | solution.py:478
  27.2 3.1 %collective-permute-done.3.rotation_ref = f32[256,256]{1,0:T(8,128)S(1)} collective-permute-done((f32[256,256]{1,0:T(8,128)S(1)}, f32[256,256]{1,0:T(8,128)S(1)}, u32[]{:S(2)}, u32[]{:S(2)}) %collective-permute-start.3) | collective-permute-done | bytes 262176 | tf_op jit(solution)/shard_map/ppermute | solution.py:478
  31.4 4.1 %collective-permute-start.5 = (f32[768,128]{1,0:T(8,128)S(1)}, f32[768,128]{1,0:T(8,128)S(1)}, u32[]{:S(2)}, u32[]{:S(2)}) collective-permute-start(f32[768,128]{1,0:T(8,128)S(1)} %get-tuple-element.83.refs_4_), channel_id=1, source_target_pairs={{12,4},{13,5},{14,6},{15,7},{0,8},{1,9},{2,10},{3,11},{20,12},{21,... | collective-permute-start | bytes 1179656 | tf_op jit(solution)/shard_map/ppermute | solution.py:478
  36.4 3.5 %collective-permute-start.7 = (f32[512,128]{1,0:T(8,128)S(1)}, f32[512,128]{1,0:T(8,128)S(1)}, u32[]{:S(2)}, u32[]{:S(2)}) collective-permute-start(f32[512,128]{1,0:T(8,128)S(1)} %get-tuple-element.86.refs_7_), channel_id=1, source_target_pairs={{12,4},{13,5},{14,6},{15,7},{0,8},{1,9},{2,10},{3,11},{20,12},{21,... | collective-permute-start | bytes 786440 | tf_op jit(solution)/shard_map/ppermute | solution.py:478
  42.8 4.6 %collective-permute-done.7.refs_8_ = f32[512,128]{1,0:T(8,128)S(1)} collective-permute-done((f32[512,128]{1,0:T(8,128)S(1)}, f32[512,128]{1,0:T(8,128)S(1)}, u32[]{:S(2)}, u32[]{:S(2)}) %collective-permute-start.7) | collective-permute-done | bytes 262176 | tf_op jit(solution)/shard_map/ppermute | solution.py:478
  47.4 1.9 %shard_map.55 = (f32[128,128]{1,0:T(8,128)S(1)}, f32[128,128]{1,0:T(8,128)S(1)}, f32[1280,128]{1,0:T(8,128)S(1)}, f32[1280,128]{1,0:T(8,128)S(1)}, f32[1280,128]{1,0:T(8,128)S(1)}, /*index=5*/f32[1280,128]{1,0:T(8,128)S(1)}) custom-call(s32[16]{0:T(128)S(1)} %constant_dynamic-update-slice_fusion.f, f32[1280,128]{1,0:T(8,128)S(1)} %get-tuple-element.77.refs_0_, ...), custom_call_target="tpu_custom_call" | custom-call | tf_op jit(solution)/shard_map/pallas_call | solution.py:52
  50.6 3.4 %collective-permute-start.13 = (f32[128,128]{1,0:T(8,128)S(1)}, f32[128,128]{1,0:T(8,128)S(1)}, u32[]{:S(2)}, u32[]{:S(2)}) collective-permute-start(f32[128,128]{1,0:T(8,128)S(1)} %add.35.refs_0_), channel_id=1, source_target_pairs={{6,0},{7,1},{4,2},{5,3},{2,4},{3,5},{0,6},{1,7},{14,8},{15,9},{12,... | collective-permute-start | bytes 196616 | tf_op jit(solution)/shard_map/ppermute | solution.py:478
  54.7 1.8 %collective-permute-done.13.refs_3_ = f32[128,128]{1,0:T(8,128)S(1)} collective-permute-done((f32[128,128]{1,0:T(8,128)S(1)}, f32[128,128]{1,0:T(8,128)S(1)}, u32[]{:S(2)}, u32[]{:S(2)}) %collective-permute-start.13) | collective-permute-done | bytes 65568 | tf_op jit(solution)/shard_map/ppermute | solution.py:478
  56.4 1.9 %collective-permute-done.12.refs_2_ = f32[128,128]{1,0:T(8,128)S(1)} collective-permute-done((f32[128,128]{1,0:T(8,128)S(1)}, f32[128,128]{1,0:T(8,128)S(1)}, u32[]{:S(2)}, u32[]{:S(2)}) %collective-permute-start.12) | collective-permute-done | bytes 65568 | tf_op jit(solution)/shard_map/ppermute | solution.py:478
  58.3 3.4 %shard_map.57 = (f32[256,256]{1,0:T(8,128)S(1)}, f32[256,256]{1,0:T(8,128)S(1)}) custom-call(s32[16]{0:T(128)S(1)} %constant_dynamic-update-slice_fusion.f, f32[128,128]{1,0:T(8,128)S(1)} %add.35.refs_0_, f32[128,128]{1,0:T(8,128)S(1)} %collective-permute-done.11.refs_1_, f32[128,128]{1,0:T(8,128)S(1)} %collective-permute-done.12.refs_2_, ...), custom_call_target="tpu_custom_call" | custom-call | tf_op jit(solution)/shard_map/pallas_call | solution.py:52
  65.8 4.7 %collective-permute-start.16 = (f32[1280,128]{1,0:T(8,128)S(1)}, f32[1280,128]{1,0:T(8,128)S(1)}, u32[]{:S(2)}, u32[]{:S(2)}) collective-permute-start(f32[1280,128]{1,0:T(8,128)S(1)} %get-tuple-element.103.refs_4_), channel_id=1, source_target_pairs={{9,1},{11,3},{13,5},{15,7},{0,8},{17,9},{2,10},{19,11},{4,12},{21,... | collective-permute-start | bytes 1966088 | tf_op jit(solution)/shard_map/ppermute | solution.py:478
  72.8 3.4 %collective-permute-start.18 = (f32[128,128]{1,0:T(8,128)S(1)}, f32[128,128]{1,0:T(8,128)S(1)}, u32[]{:S(2)}, u32[]{:S(2)}) collective-permute-start(f32[128,128]{1,0:T(8,128)S(1)} %get-tuple-element.108), channel_id=1, source_target_pairs={{1,0},{0,1},{3,2},{2,3},{5,4},{4,5},{7,6},{6,7},{9,8},{8,9},{11,10... | collective-permute-start | bytes 196616 | tf_op jit(solution)/shard_map/ppermute | solution.py:478
  77.9 4.5 %collective-permute-done.16.refs_5_ = f32[1280,128]{1,0:T(8,128)S(1)} collective-permute-done((f32[1280,128]{1,0:T(8,128)S(1)}, f32[1280,128]{1,0:T(8,128)S(1)}, u32[]{:S(2)}, u32[]{:S(2)}) %collective-permute-start.16) | collective-permute-done | bytes 655392 | tf_op jit(solution)/shard_map/ppermute | solution.py:478
  82.4 1.9 %shard_map.60 = (f32[128,128]{1,0:T(8,128)S(1)}, f32[128,128]{1,0:T(8,128)S(1)}, f32[1280,128]{1,0:T(8,128)S(1)}, f32[1280,128]{1,0:T(8,128)S(1)}, f32[1280,128]{1,0:T(8,128)S(1)}, /*index=5*/f32[1280,128]{1,0:T(8,128)S(1)}) custom-call(s32[16]{0:T(128)S(1)} %constant_dynamic-update-slice_fusion.f, f32[1280,128]{1,0:T(8,128)S(1)} %get-tuple-element.100.refs_0_, ...), custom_call_target="tpu_custom_call" | custom-call | tf_op jit(solution)/shard_map/pallas_call | solution.py:52
  86.0 2.2 %collective-permute-start.22 = (f32[128,128]{1,0:T(8,128)S(1)}, f32[128,128]{1,0:T(8,128)S(1)}, u32[]{:S(2)}, u32[]{:S(2)}) collective-permute-start(f32[128,128]{1,0:T(8,128)S(1)} %add.36.refs_0_), channel_id=1, source_target_pairs={{6,0},{7,1},{4,2},{5,3},{2,4},{3,5},{0,6},{1,7},{14,8},{15,9},{12,... | collective-permute-start | bytes 196616 | tf_op jit(solution)/shard_map/ppermute | solution.py:478
  89.6 1.8 %collective-permute-done.22.refs_3_ = f32[128,128]{1,0:T(8,128)S(1)} collective-permute-done((f32[128,128]{1,0:T(8,128)S(1)}, f32[128,128]{1,0:T(8,128)S(1)}, u32[]{:S(2)}, u32[]{:S(2)}) %collective-permute-start.22) | collective-permute-done | bytes 65568 | tf_op jit(solution)/shard_map/ppermute | solution.py:478
  92.7 3.1 %shard_map.62 = (f32[256,256]{1,0:T(8,128)S(1)}, f32[256,256]{1,0:T(8,128)S(1)}) custom-call(s32[16]{0:T(128)S(1)} %constant_dynamic-update-slice_fusion.f, f32[128,128]{1,0:T(8,128)S(1)} %add.36.refs_0_, f32[128,128]{1,0:T(8,128)S(1)} %collective-permute-done.20.refs_1_, f32[128,128]{1,0:T(8,128)S(1)} %collective-permute-done.21.refs_2_, ...), custom_call_target="tpu_custom_call" | custom-call | tf_op jit(solution)/shard_map/pallas_call | solution.py:52
  99.7 4.6 %collective-permute-start.25 = (f32[1280,128]{1,0:T(8,128)S(1)}, f32[1280,128]{1,0:T(8,128)S(1)}, u32[]{:S(2)}, u32[]{:S(2)}) collective-permute-start(f32[1280,128]{1,0:T(8,128)S(1)} %get-tuple-element.120.refs_4_), channel_id=1, source_target_pairs={{9,1},{11,3},{13,5},{15,7},{0,8},{17,9},{2,10},{19,11},{4,12},{21,... | collective-permute-start | bytes 1966088 | tf_op jit(solution)/shard_map/ppermute | solution.py:478
  104.3 2.0 %collective-permute-start.29 = (f32[1280,128]{1,0:T(8,128)S(1)}, f32[1280,128]{1,0:T(8,128)S(1)}, u32[]{:S(2)}, u32[]{:S(2)}) collective-permute-start(f32[1280,128]{1,0:T(8,128)S(1)} %get-tuple-element.127), channel_id=1, source_target_pairs={{4,0},{5,1},{6,2},{7,3},{0,4},{1,5},{2,6},{3,7},{12,8},{13,9},{14,... | collective-permute-start | bytes 1966088 | tf_op jit(solution)/shard_map/ppermute | solution.py:478
  108.6 3.0 %collective-permute-start.27 = (f32[128,128]{1,0:T(8,128)S(1)}, f32[128,128]{1,0:T(8,128)S(1)}, u32[]{:S(2)}, u32[]{:S(2)}) collective-permute-start(f32[128,128]{1,0:T(8,128)S(1)} %get-tuple-element.125), channel_id=1, source_target_pairs={{1,0},{0,1},{3,2},{2,3},{5,4},{4,5},{7,6},{6,7},{9,8},{8,9},{11,10... | collective-permute-start | bytes 196616 | tf_op jit(solution)/shard_map/ppermute | solution.py:478
  112.1 4.3 %collective-permute-done.25.refs_5_ = f32[1280,128]{1,0:T(8,128)S(1)} collective-permute-done((f32[1280,128]{1,0:T(8,128)S(1)}, f32[1280,128]{1,0:T(8,128)S(1)}, u32[]{:S(2)}, u32[]{:S(2)}) %collective-permute-start.25) | collective-permute-done | bytes 655392 | tf_op jit(solution)/shard_map/ppermute | solution.py:478
  116.4 1.8 %shard_map.65 = (f32[128,128]{1,0:T(8,128)S(1)}, f32[128,128]{1,0:T(8,128)S(1)}, f32[1280,128]{1,0:T(8,128)S(1)}, f32[1280,128]{1,0:T(8,128)S(1)}, f32[1280,128]{1,0:T(8,128)S(1)}, /*index=5*/f32[1280,128]{1,0:T(8,128)S(1)}) custom-call(s32[16]{0:T(128)S(1)} %constant_dynamic-update-slice_fusion.f, f32[1280,128]{1,0:T(8,128)S(1)} %get-tuple-element.117.refs_4_.refs_0_, ...), custom_call_target="tpu_custom_call" | custom-call | tf_op jit(solution)/shard_map/pallas_call | solution.py:52
  126.4 5.3 %collective-permute-done.32.refs_3_ = f32[128,128]{1,0:T(8,128)S(1)} collective-permute-done((f32[128,128]{1,0:T(8,128)S(1)}, f32[128,128]{1,0:T(8,128)S(1)}, u32[]{:S(2)}, u32[]{:S(2)}) %collective-permute-start.32) | collective-permute-done | bytes 65568 | tf_op jit(solution)/shard_map/ppermute | solution.py:478
  132.0 1.7 %collective-permute-start.35 = (f32[768,128]{1,0:T(8,128)S(1)}, f32[768,128]{1,0:T(8,128)S(1)}, u32[]{:S(2)}, u32[]{:S(2)}) collective-permute-start(f32[768,128]{1,0:T(8,128)S(1)} %shard_map.68), channel_id=1, source_target_pairs={{4,0},{5,1},{6,2},{7,3},{0,4},{1,5},{2,6},{3,7},{12,8},{13,9},{14,... | collective-permute-start | bytes 1179656 | tf_op jit(solution)/shard_map/ppermute | solution.py:478
  133.7 3.6 %shard_map.69 = (f32[264,256]{1,0:T(8,128)S(1)}, f32[256,256]{1,0:T(8,128)}) custom-call(s32[16]{0:T(128)S(1)} %constant_dynamic-update-slice_fusion.f, f32[128,128]{1,0:T(8,128)S(1)} %add.37.refs_0_, f32[128,128]{1,0:T(8,128)S(1)} %collective-permute-done.30.refs_1_, f32[128,128]{1,0:T(8,128)S(1)} %collective-permute-done.31.refs_2_, ...), custom_call_target="tpu_custom_call" | custom-call | tf_op jit(solution)/shard_map/pallas_call | solution.py:52
  139.0 3.0 %shard_map.70 = (f32[2048,256]{1,0:T(8,128)}, f32[512,256]{1,0:T(8,128)}, f32[1,256]{1,0:T(1,128)}) custom-call(s32[16]{0:T(128)S(1)} %constant_dynamic-update-slice_fusion.f, f32[264,256]{1,0:T(8,128)S(1)} %get-tuple-element.138.own_ref, f32[264,256]{1,0:T(8,128)S(1)} %collective-permute-done.34.other_ref, ...), custom_call_target="tpu_custom_call" | custom-call | flops 1 | bytes 1 | tf_op jit(solution)/shard_map/pallas_call | solution.py:377
  142.5 2.0 %shard_map.71 = (f32[2048,256]{1,0:T(8,128)}, f32[512,256]{1,0:T(8,128)}) custom-call(s32[16]{0:T(128)S(1)} %constant_dynamic-update-slice_fusion.f, f32[264,256]{1,0:T(8,128)S(1)} %get-tuple-element.138.own_ref, f32[264,256]{1,0:T(8,128)S(1)} %collective-permute-done.34.other_ref, ...), custom_call_target="tpu_custom_call", output_to_operand_aliasing={{0}: (5, {}), {1}: (6, {})} | custom-call | flops 1 | bytes 1 | tf_op jit(solution)/shard_map/pallas_call | solution.py:377
  (75 shorter events, 42.8 us)
Async XLA Ops:
  3.1 27.2 %collective-permute-start.4 = (f32[768,256]{1,0:T(8,128)}, f32[768,256]{1,0:T(8,128)S(1)}, u32[]{:S(2)}, u32[]{:S(2)}) collective-permute-start(f32[768,256]{1,0:T(8,128)} %get-tuple-element.81), channel_id=1, source_target_pairs={{4,0},{5,1},{6,2},{7,3},{0,4},{1,5},{2,6},{3,7},{12,8},{13,9},{14,... | collective-permute-start | bytes 2359304 | tf_op jit(solution)/shard_map/ppermute | solution.py:478
  9.8 7.0 %collective-permute-start.1 = (f32[384,128]{1,0:T(8,128)S(1)}, f32[384,128]{1,0:T(8,128)S(1)}, u32[]{:S(2)}, u32[]{:S(2)}) collective-permute-start(f32[384,128]{1,0:T(8,128)S(1)} %add.34.own_ref), channel_id=1, source_target_pairs={{2,0},{3,1},{0,2},{1,3},{6,4},{7,5},{4,6},{5,7},{10,8},{11,9},{8,1... | collective-permute-start | bytes 589832 | tf_op jit(solution)/shard_map/ppermute | solution.py:478
  20.3 10.0 %collective-permute-start.3 = (f32[256,256]{1,0:T(8,128)S(1)}, f32[256,256]{1,0:T(8,128)S(1)}, u32[]{:S(2)}, u32[]{:S(2)}) collective-permute-start(f32[256,256]{1,0:T(8,128)S(1)} %get-tuple-element.76.rotation_ref), channel_id=1, source_target_pairs={{4,0},{5,1},{6,2},{7,3},{0,4},{1,5},{2,6},{3,7},{12,8},{13,9},{14,... | collective-permute-start | bytes 786440 | tf_op jit(solution)/shard_map/ppermute | solution.py:478
  21.9 25.5 %collective-permute-start.2 = (f32[1280,128]{1,0:T(8,128)S(1)}, f32[1280,128]{1,0:T(8,128)S(1)}, u32[]{:S(2)}, u32[]{:S(2)}) collective-permute-start(f32[1280,128]{1,0:T(8,128)S(1)} %get-tuple-element.80.refs_1_), channel_id=1, source_target_pairs={{8,0},{9,1},{10,2},{11,3},{16,8},{17,9},{18,10},{19,11},{4,12},{5,... | collective-permute-start | bytes 1966088 | tf_op jit(solution)/shard_map/ppermute | solution.py:478
  23.2 12.2 %collective-permute-start.6 = (f32[256,256]{1,0:T(8,128)S(1)}, f32[256,256]{1,0:T(8,128)S(1)}, u32[]{:S(2)}, u32[]{:S(2)}) collective-permute-start(f32[256,256]{1,0:T(8,128)S(1)} %copy-done.1), channel_id=1, source_target_pairs={{4,0},{5,1},{6,2},{7,3},{0,4},{1,5},{2,6},{3,7},{12,8},{13,9},{14,... | collective-permute-start | bytes 786440 | tf_op jit(solution)/shard_map/ppermute | solution.py:478
  31.4 16.0 %collective-permute-start.5 = (f32[768,128]{1,0:T(8,128)S(1)}, f32[768,128]{1,0:T(8,128)S(1)}, u32[]{:S(2)}, u32[]{:S(2)}) collective-permute-start(f32[768,128]{1,0:T(8,128)S(1)} %get-tuple-element.83.refs_4_), channel_id=1, source_target_pairs={{12,4},{13,5},{14,6},{15,7},{0,8},{1,9},{2,10},{3,11},{20,12},{21,... | collective-permute-start | bytes 1179656 | tf_op jit(solution)/shard_map/ppermute | solution.py:478
  36.4 11.0 %collective-permute-start.7 = (f32[512,128]{1,0:T(8,128)S(1)}, f32[512,128]{1,0:T(8,128)S(1)}, u32[]{:S(2)}, u32[]{:S(2)}) collective-permute-start(f32[512,128]{1,0:T(8,128)S(1)} %get-tuple-element.86.refs_7_), channel_id=1, source_target_pairs={{12,4},{13,5},{14,6},{15,7},{0,8},{1,9},{2,10},{3,11},{20,12},{21,... | collective-permute-start | bytes 786440 | tf_op jit(solution)/shard_map/ppermute | solution.py:478
  41.5 7.7 %collective-permute-start.8 = (f32[128,128]{1,0:T(8,128)S(1)}, f32[128,128]{1,0:T(8,128)S(1)}, u32[]{:S(2)}, u32[]{:S(2)}) collective-permute-start(f32[128,128]{1,0:T(8,128)S(1)} %get-tuple-element.90), channel_id=1, source_target_pairs={{0,0},{8,1},{2,2},{10,3},{1,4},{9,5},{3,6},{11,7},{4,8},{16,9},{6,... | collective-permute-start | bytes 196616 | tf_op jit(solution)/shard_map/ppermute | solution.py:478
  42.2 7.1 %collective-permute-start.9 = (f32[128,128]{1,0:T(8,128)S(1)}, f32[128,128]{1,0:T(8,128)S(1)}, u32[]{:S(2)}, u32[]{:S(2)}) collective-permute-start(f32[128,128]{1,0:T(8,128)S(1)} %get-tuple-element.91), channel_id=1, source_target_pairs={{4,0},{0,1},{6,2},{2,3},{5,4},{1,5},{7,6},{3,7},{12,8},{8,9},{14,1... | collective-permute-start | bytes 196616 | tf_op jit(solution)/shard_map/ppermute | solution.py:478
  50.6 5.8 %collective-permute-start.13 = (f32[128,128]{1,0:T(8,128)S(1)}, f32[128,128]{1,0:T(8,128)S(1)}, u32[]{:S(2)}, u32[]{:S(2)}) collective-permute-start(f32[128,128]{1,0:T(8,128)S(1)} %add.35.refs_0_), channel_id=1, source_target_pairs={{6,0},{7,1},{4,2},{5,3},{2,4},{3,5},{0,6},{1,7},{14,8},{15,9},{12,... | collective-permute-start | bytes 196616 | tf_op jit(solution)/shard_map/ppermute | solution.py:478
  54.0 4.3 %collective-permute-start.12 = (f32[128,128]{1,0:T(8,128)S(1)}, f32[128,128]{1,0:T(8,128)S(1)}, u32[]{:S(2)}, u32[]{:S(2)}) collective-permute-start(f32[128,128]{1,0:T(8,128)S(1)} %add.35.refs_0_), channel_id=1, source_target_pairs={{4,0},{5,1},{6,2},{7,3},{0,4},{1,5},{2,6},{3,7},{12,8},{13,9},{14,... | collective-permute-start | bytes 196616 | tf_op jit(solution)/shard_map/ppermute | solution.py:478
  54.0 4.3 %collective-permute-start.11 = (f32[128,128]{1,0:T(8,128)S(1)}, f32[128,128]{1,0:T(8,128)S(1)}, u32[]{:S(2)}, u32[]{:S(2)}) collective-permute-start(f32[128,128]{1,0:T(8,128)S(1)} %add.35.refs_0_), channel_id=1, source_target_pairs={{2,0},{3,1},{0,2},{1,3},{6,4},{7,5},{4,6},{5,7},{10,8},{11,9},{8,1... | collective-permute-start | bytes 196616 | tf_op jit(solution)/shard_map/ppermute | solution.py:478
  61.7 2.8 %collective-permute-start.15 = (f32[256,256]{1,0:T(8,128)S(1)}, f32[256,256]{1,0:T(8,128)S(1)}, u32[]{:S(2)}, u32[]{:S(2)}) collective-permute-start(f32[256,256]{1,0:T(8,128)S(1)} %get-tuple-element.95.rotation_ref), channel_id=1, source_target_pairs={{1,0},{0,1},{3,2},{2,3},{5,4},{4,5},{7,6},{6,7},{9,8},{8,9},{11,10... | collective-permute-start | bytes 786440 | tf_op jit(solution)/shard_map/ppermute | solution.py:478
  63.1 14.9 %collective-permute-start.14 = (f32[1280,128]{1,0:T(8,128)S(1)}, f32[1280,128]{1,0:T(8,128)S(1)}, u32[]{:S(2)}, u32[]{:S(2)}) collective-permute-start(f32[1280,128]{1,0:T(8,128)S(1)} %get-tuple-element.101.refs_1_), channel_id=1, source_target_pairs={{8,0},{10,2},{12,4},{14,6},{16,8},{1,9},{18,10},{3,11},{20,12},{5,... | collective-permute-start | bytes 1966088 | tf_op jit(solution)/shard_map/ppermute | solution.py:478
  65.8 16.6 %collective-permute-start.16 = (f32[1280,128]{1,0:T(8,128)S(1)}, f32[1280,128]{1,0:T(8,128)S(1)}, u32[]{:S(2)}, u32[]{:S(2)}) collective-permute-start(f32[1280,128]{1,0:T(8,128)S(1)} %get-tuple-element.103.refs_4_), channel_id=1, source_target_pairs={{9,1},{11,3},{13,5},{15,7},{0,8},{17,9},{2,10},{19,11},{4,12},{21,... | collective-permute-start | bytes 1966088 | tf_op jit(solution)/shard_map/ppermute | solution.py:478
  72.1 12.1 %collective-permute-start.17 = (f32[128,128]{1,0:T(8,128)S(1)}, f32[128,128]{1,0:T(8,128)S(1)}, u32[]{:S(2)}, u32[]{:S(2)}) collective-permute-start(f32[128,128]{1,0:T(8,128)S(1)} %get-tuple-element.107), channel_id=1, source_target_pairs={{0,0},{8,1},{2,2},{10,3},{4,4},{12,5},{6,6},{14,7},{1,8},{16,9},{3... | collective-permute-start | bytes 196616 | tf_op jit(solution)/shard_map/ppermute | solution.py:478
  72.8 11.5 %collective-permute-start.18 = (f32[128,128]{1,0:T(8,128)S(1)}, f32[128,128]{1,0:T(8,128)S(1)}, u32[]{:S(2)}, u32[]{:S(2)}) collective-permute-start(f32[128,128]{1,0:T(8,128)S(1)} %get-tuple-element.108), channel_id=1, source_target_pairs={{1,0},{0,1},{3,2},{2,3},{5,4},{4,5},{7,6},{6,7},{9,8},{8,9},{11,10... | collective-permute-start | bytes 196616 | tf_op jit(solution)/shard_map/ppermute | solution.py:478
  86.0 5.4 %collective-permute-start.22 = (f32[128,128]{1,0:T(8,128)S(1)}, f32[128,128]{1,0:T(8,128)S(1)}, u32[]{:S(2)}, u32[]{:S(2)}) collective-permute-start(f32[128,128]{1,0:T(8,128)S(1)} %add.36.refs_0_), channel_id=1, source_target_pairs={{6,0},{7,1},{4,2},{5,3},{2,4},{3,5},{0,6},{1,7},{14,8},{15,9},{12,... | collective-permute-start | bytes 196616 | tf_op jit(solution)/shard_map/ppermute | solution.py:478
  88.2 4.3 %collective-permute-start.21 = (f32[128,128]{1,0:T(8,128)S(1)}, f32[128,128]{1,0:T(8,128)S(1)}, u32[]{:S(2)}, u32[]{:S(2)}) collective-permute-start(f32[128,128]{1,0:T(8,128)S(1)} %add.36.refs_0_), channel_id=1, source_target_pairs={{4,0},{5,1},{6,2},{7,3},{0,4},{1,5},{2,6},{3,7},{12,8},{13,9},{14,... | collective-permute-start | bytes 196616 | tf_op jit(solution)/shard_map/ppermute | solution.py:478
  88.3 4.5 %collective-permute-start.20 = (f32[128,128]{1,0:T(8,128)S(1)}, f32[128,128]{1,0:T(8,128)S(1)}, u32[]{:S(2)}, u32[]{:S(2)}) collective-permute-start(f32[128,128]{1,0:T(8,128)S(1)} %add.36.refs_0_), channel_id=1, source_target_pairs={{2,0},{3,1},{0,2},{1,3},{6,4},{7,5},{4,6},{5,7},{10,8},{11,9},{8,1... | collective-permute-start | bytes 196616 | tf_op jit(solution)/shard_map/ppermute | solution.py:478
  95.8 2.6 %collective-permute-start.24 = (f32[256,256]{1,0:T(8,128)S(1)}, f32[256,256]{1,0:T(8,128)S(1)}, u32[]{:S(2)}, u32[]{:S(2)}) collective-permute-start(f32[256,256]{1,0:T(8,128)S(1)} %get-tuple-element.112.rotation_ref), channel_id=1, source_target_pairs={{1,0},{0,1},{3,2},{2,3},{5,4},{4,5},{7,6},{6,7},{9,8},{8,9},{11,10... | collective-permute-start | bytes 786440 | tf_op jit(solution)/shard_map/ppermute | solution.py:478
  97.2 15.0 %collective-permute-start.23 = (f32[1280,128]{1,0:T(8,128)S(1)}, f32[1280,128]{1,0:T(8,128)S(1)}, u32[]{:S(2)}, u32[]{:S(2)}) collective-permute-start(f32[1280,128]{1,0:T(8,128)S(1)} %get-tuple-element.118.refs_1_), channel_id=1, source_target_pairs={{8,0},{10,2},{12,4},{14,6},{16,8},{1,9},{18,10},{3,11},{20,12},{5,... | collective-permute-start | bytes 1966088 | tf_op jit(solution)/shard_map/ppermute | solution.py:478
  99.7 16.7 %collective-permute-start.25 = (f32[1280,128]{1,0:T(8,128)S(1)}, f32[1280,128]{1,0:T(8,128)S(1)}, u32[]{:S(2)}, u32[]{:S(2)}) collective-permute-start(f32[1280,128]{1,0:T(8,128)S(1)} %get-tuple-element.120.refs_4_), channel_id=1, source_target_pairs={{9,1},{11,3},{13,5},{15,7},{0,8},{17,9},{2,10},{19,11},{4,12},{21,... | collective-permute-start | bytes 1966088 | tf_op jit(solution)/shard_map/ppermute | solution.py:478
  104.3 16.3 %collective-permute-start.29 = (f32[1280,128]{1,0:T(8,128)S(1)}, f32[1280,128]{1,0:T(8,128)S(1)}, u32[]{:S(2)}, u32[]{:S(2)}) collective-permute-start(f32[1280,128]{1,0:T(8,128)S(1)} %get-tuple-element.127), channel_id=1, source_target_pairs={{4,0},{5,1},{6,2},{7,3},{0,4},{1,5},{2,6},{3,7},{12,8},{13,9},{14,... | collective-permute-start | bytes 1966088 | tf_op jit(solution)/shard_map/ppermute | solution.py:478
  107.9 10.3 %collective-permute-start.26 = (f32[128,128]{1,0:T(8,128)S(1)}, f32[128,128]{1,0:T(8,128)S(1)}, u32[]{:S(2)}, u32[]{:S(2)}) collective-permute-start(f32[128,128]{1,0:T(8,128)S(1)} %get-tuple-element.124), channel_id=1, source_target_pairs={{0,0},{8,1},{2,2},{10,3},{4,4},{12,5},{6,6},{14,7},{1,8},{16,9},{3... | collective-permute-start | bytes 196616 | tf_op jit(solution)/shard_map/ppermute | solution.py:478
  108.6 9.7 %collective-permute-start.27 = (f32[128,128]{1,0:T(8,128)S(1)}, f32[128,128]{1,0:T(8,128)S(1)}, u32[]{:S(2)}, u32[]{:S(2)}) collective-permute-start(f32[128,128]{1,0:T(8,128)S(1)} %get-tuple-element.125), channel_id=1, source_target_pairs={{1,0},{0,1},{3,2},{2,3},{5,4},{4,5},{7,6},{6,7},{9,8},{8,9},{11,10... | collective-permute-start | bytes 196616 | tf_op jit(solution)/shard_map/ppermute | solution.py:478
  118.3 2.0 %collective-permute-start.28 = (f32[128,128]{1,0:T(8,128)S(1)}, f32[128,128]{1,0:T(8,128)S(1)}, u32[]{:S(2)}, u32[]{:S(2)}) collective-permute-start(f32[128,128]{1,0:T(8,128)S(1)} %get-tuple-element.126), channel_id=1, source_target_pairs={{1,0},{0,1},{3,2},{2,3},{5,4},{4,5},{7,6},{6,7},{9,8},{8,9},{11,10... | collective-permute-start | bytes 196616 | tf_op jit(solution)/shard_map/ppermute | solution.py:478
  120.6 11.4 %collective-permute-start.33 = (f32[512,128]{1,0:T(8,128)S(1)}, f32[512,128]{1,0:T(8,128)S(1)}, u32[]{:S(2)}, u32[]{:S(2)}) collective-permute-start(f32[512,128]{1,0:T(8,128)S(1)} %shard_map.67), channel_id=1, source_target_pairs={{4,0},{5,1},{6,2},{7,3},{0,4},{1,5},{2,6},{3,7},{12,8},{13,9},{14,... | collective-permute-start | bytes 786440 | tf_op jit(solution)/shard_map/ppermute | solution.py:478
  122.3 9.4 %collective-permute-start.32 = (f32[128,128]{1,0:T(8,128)S(1)}, f32[128,128]{1,0:T(8,128)S(1)}, u32[]{:S(2)}, u32[]{:S(2)}) collective-permute-start(f32[128,128]{1,0:T(8,128)S(1)} %add.37.refs_0_), channel_id=1, source_target_pairs={{6,0},{7,1},{4,2},{5,3},{2,4},{3,5},{0,6},{1,7},{14,8},{15,9},{12,... | collective-permute-start | bytes 196616 | tf_op jit(solution)/shard_map/ppermute | solution.py:478
  123.2 8.7 %collective-permute-start.31 = (f32[128,128]{1,0:T(8,128)S(1)}, f32[128,128]{1,0:T(8,128)S(1)}, u32[]{:S(2)}, u32[]{:S(2)}) collective-permute-start(f32[128,128]{1,0:T(8,128)S(1)} %add.37.refs_0_), channel_id=1, source_target_pairs={{4,0},{5,1},{6,2},{7,3},{0,4},{1,5},{2,6},{3,7},{12,8},{13,9},{14,... | collective-permute-start | bytes 196616 | tf_op jit(solution)/shard_map/ppermute | solution.py:478
  124.9 7.1 %collective-permute-start.30 = (f32[128,128]{1,0:T(8,128)S(1)}, f32[128,128]{1,0:T(8,128)S(1)}, u32[]{:S(2)}, u32[]{:S(2)}) collective-permute-start(f32[128,128]{1,0:T(8,128)S(1)} %add.37.refs_0_), channel_id=1, source_target_pairs={{2,0},{3,1},{0,2},{1,3},{6,4},{7,5},{4,6},{5,7},{10,8},{11,9},{8,1... | collective-permute-start | bytes 196616 | tf_op jit(solution)/shard_map/ppermute | solution.py:478
  132.0 10.6 %collective-permute-start.35 = (f32[768,128]{1,0:T(8,128)S(1)}, f32[768,128]{1,0:T(8,128)S(1)}, u32[]{:S(2)}, u32[]{:S(2)}) collective-permute-start(f32[768,128]{1,0:T(8,128)S(1)} %shard_map.68), channel_id=1, source_target_pairs={{4,0},{5,1},{6,2},{7,3},{0,4},{1,5},{2,6},{3,7},{12,8},{13,9},{14,... | collective-permute-start | bytes 1179656 | tf_op jit(solution)/shard_map/ppermute | solution.py:478
  (7 other events, 37.4 us)

commit v14 on v13

--- a/solution.py
+++ b/solution.py
@@ -336,6 +336,22 @@
 
     outs = (shape(half, half),) * 2 + (shape(rows, half),) * 4
     return call(body, facts, own + sum(others, []), outs)
+
+
+def give_arrived(facts, own, other, rows, half):
+    def body(f, *refs):
+        out_ref = refs[4]
+        near = f[CORE] == f[X]
+        edge = jnp.where(f[X] == 0, f[LAST], f[FIRST]) == 1
+        for ref, here in zip(
+            refs, (~near & edge, near & ~edge, near & edge, ~near & ~edge)
+        ):
+
+            @pl.when(here)
+            def _():
+                out_ref[...] = ref[:rows]
+
+    return call(body, facts, own[1:] + other[1:], shape(rows, half))
 
 
 def give(facts, blocks, start, stop, half):
@@ -572,17 +588,21 @@
             diagonals = [pass_diagonal(leave), exchange(stay, 0, 1)]
             if last_move:
                 native = exchange(native[0], 1, 0)
+                top = part // 2
+                top_give = give_arrived(facts, own, others[0], top, half)
+                own[2], others[0][2], top_give, *diagonals = together(
+                    own[2], others[0][2], top_give, *diagonals
+                )
+                got_top = exchange(top_give, 1, 0)
             *grams, up_0, low_0, up_1, low_1 = cross_gram(
                 facts, own, others, CORE, part, half
             )
         blocks = [up_0, low_0, up_1, low_1]
-        grams[1], *diagonals = together(grams[1], *diagonals)
+        if last_move:
+            grams[1], native = together(grams[1], native)
+        else:
+            grams[1], *diagonals = together(grams[1], *diagonals)
         own = sum_rows(grams[0] + exchange(grams[1], 0, 1))
-        if last_move:
-            top = part // 2
-            top_give = give(facts, blocks, 0, top, half)
-            own, native, top_give = together(own, native, top_give)
-            got_top = exchange(top_give, 1, 0)
         parts = [own, exchange(own, 0, 2), exchange(own, 1, 0), exchange(own, 1, 2)]
         if last_move:
             rest_give = give(facts, blocks, top, part + vector_rows, half)

time: 145 us -> 143 us (0.986)
  waiting for transfers between devices: 42.6 us -> 40.8 us
    ppermute x36, waiting for transfers between devices: 42.6 us -> 40.8 us  [permute(): return lax.ppermute(block, ('pair', 'row'), moves)]
  transfers between devices with their start and end apart: 36 -> 36, of which waited for: 21 -> 22; matrix products, arithmetic and copies ran while one was open for 0% -> 0% of each run, Pallas kernels for 22% -> 22%
where the time goes in v14:
time: 143 us; the launch traced here: 142 us
  starting transfers between devices  57.1 us (40%)
  Pallas kernels  42.9 us (30%)
  waiting for transfers between devices  40.8 us (29%)
    ppermute x36, starting transfers between devices, permute(): return lax.ppermute(block, ('pair', 'row'), moves)  57.1 us
    ppermute x36, waiting for transfers between devices, permute(): return lax.ppermute(block, ('pair', 'row'), moves)  40.8 us
    pallas_call x19, Pallas kernels, call(): pl.pallas_call(body, out_shape=outs, in_specs=[pl.BlockSpec(memory_space=...  33.4 us
    pallas_call x2, Pallas kernels, finish_call(): pl.pallas_call(body, out_shape=outs, in_specs=[pl.BlockSpec(memory_space=...  4.94 us
  transfers between devices with their start and end apart: 36, of which 22 were waited for; matrix products, arithmetic and copies ran while one was open for 0% of the time, Pallas kernels for 22%

profile of v14, /device:TPU:0, one launch (start us, length us, event | category | flops | bytes accessed | tf_op | source)
XLA Modules:
  0.0 142.3 jit_solution(7279776079764232965)
XLA Ops:
  0.6 2.5 %shard_map.52 = (f32[768,256]{1,0:T(8,128)}, f32[256,256]{1,0:T(8,128)}) custom-call(f32[2048,256]{1,0:T(8,128)} %x_ref.5), custom_call_target="tpu_custom_call" | custom-call | tf_op jit(solution)/shard_map/pallas_call | solution.py:104
  3.1 3.0 %collective-permute-start.4 = (f32[768,256]{1,0:T(8,128)}, f32[768,256]{1,0:T(8,128)S(1)}, u32[]{:S(2)}, u32[]{:S(2)}) collective-permute-start(f32[768,256]{1,0:T(8,128)} %get-tuple-element.82), channel_id=1, source_target_pairs={{4,0},{5,1},{6,2},{7,3},{0,4},{1,5},{2,6},{3,7},{12,8},{13,9},{14,... | collective-permute-start | bytes 2359304 | tf_op jit(solution)/shard_map/ppermute | solution.py:494
  6.1 2.2 %shard_map.49 = f32[384,128]{1,0:T(8,128)S(1)} custom-call(f32[2048,256]{1,0:T(8,128)S(1)} %copy-done), custom_call_target="tpu_custom_call" | custom-call | tf_op jit(solution)/shard_map/pallas_call | solution.py:74
  11.6 5.3 %collective-permute-done.1.other_ref = f32[384,128]{1,0:T(8,128)S(1)} collective-permute-done((f32[384,128]{1,0:T(8,128)S(1)}, f32[384,128]{1,0:T(8,128)S(1)}, u32[]{:S(2)}, u32[]{:S(2)}) %collective-permute-start.1) | collective-permute-done | bytes 196640 | tf_op jit(solution)/shard_map/ppermute | solution.py:494
  16.8 3.4 %shard_map.50 = (f32[256,256]{1,0:T(8,128)S(1)}, f32[256,256]{1,0:T(8,128)S(1)}) custom-call(s32[16]{0:T(128)S(1)} %constant_dynamic-update-slice_fusion.f, f32[384,128]{1,0:T(8,128)S(1)} %add.34.own_ref, f32[384,128]{1,0:T(8,128)S(1)} %collective-permute-done.1.other_ref), custom_call_target="tpu_custom_call" | custom-call | tf_op jit(solution)/shard_map/pallas_call | solution.py:52
  23.2 4.0 %collective-permute-start.6 = (f32[256,256]{1,0:T(8,128)S(1)}, f32[256,256]{1,0:T(8,128)S(1)}, u32[]{:S(2)}, u32[]{:S(2)}) collective-permute-start(f32[256,256]{1,0:T(8,128)S(1)} %copy-done.1), channel_id=1, source_target_pairs={{4,0},{5,1},{6,2},{7,3},{0,4},{1,5},{2,6},{3,7},{12,8},{13,9},{14,... | collective-permute-start | bytes 786440 | tf_op jit(solution)/shard_map/ppermute | solution.py:494
  27.2 3.1 %collective-permute-done.3.rotation_ref = f32[256,256]{1,0:T(8,128)S(1)} collective-permute-done((f32[256,256]{1,0:T(8,128)S(1)}, f32[256,256]{1,0:T(8,128)S(1)}, u32[]{:S(2)}, u32[]{:S(2)}) %collective-permute-start.3) | collective-permute-done | bytes 262176 | tf_op jit(solution)/shard_map/ppermute | solution.py:494
  31.4 4.1 %collective-permute-start.5 = (f32[768,128]{1,0:T(8,128)S(1)}, f32[768,128]{1,0:T(8,128)S(1)}, u32[]{:S(2)}, u32[]{:S(2)}) collective-permute-start(f32[768,128]{1,0:T(8,128)S(1)} %get-tuple-element.84.refs_4_), channel_id=1, source_target_pairs={{12,4},{13,5},{14,6},{15,7},{0,8},{1,9},{2,10},{3,11},{20,12},{21,... | collective-permute-start | bytes 1179656 | tf_op jit(solution)/shard_map/ppermute | solution.py:494
  36.4 3.5 %collective-permute-start.7 = (f32[512,128]{1,0:T(8,128)S(1)}, f32[512,128]{1,0:T(8,128)S(1)}, u32[]{:S(2)}, u32[]{:S(2)}) collective-permute-start(f32[512,128]{1,0:T(8,128)S(1)} %get-tuple-element.87.refs_7_), channel_id=1, source_target_pairs={{12,4},{13,5},{14,6},{15,7},{0,8},{1,9},{2,10},{3,11},{20,12},{21,... | collective-permute-start | bytes 786440 | tf_op jit(solution)/shard_map/ppermute | solution.py:494
  42.8 4.6 %collective-permute-done.7.refs_8_ = f32[512,128]{1,0:T(8,128)S(1)} collective-permute-done((f32[512,128]{1,0:T(8,128)S(1)}, f32[512,128]{1,0:T(8,128)S(1)}, u32[]{:S(2)}, u32[]{:S(2)}) %collective-permute-start.7) | collective-permute-done | bytes 262176 | tf_op jit(solution)/shard_map/ppermute | solution.py:494
  47.4 1.9 %shard_map.55 = (f32[128,128]{1,0:T(8,128)S(1)}, f32[128,128]{1,0:T(8,128)S(1)}, f32[1280,128]{1,0:T(8,128)S(1)}, f32[1280,128]{1,0:T(8,128)S(1)}, f32[1280,128]{1,0:T(8,128)S(1)}, /*index=5*/f32[1280,128]{1,0:T(8,128)S(1)}) custom-call(s32[16]{0:T(128)S(1)} %constant_dynamic-update-slice_fusion.f, f32[1280,128]{1,0:T(8,128)S(1)} %get-tuple-element.78.refs_0_, ...), custom_call_target="tpu_custom_call" | custom-call | tf_op jit(solution)/shard_map/pallas_call | solution.py:52
  50.6 3.4 %collective-permute-start.13 = (f32[128,128]{1,0:T(8,128)S(1)}, f32[128,128]{1,0:T(8,128)S(1)}, u32[]{:S(2)}, u32[]{:S(2)}) collective-permute-start(f32[128,128]{1,0:T(8,128)S(1)} %add.35.refs_0_), channel_id=1, source_target_pairs={{6,0},{7,1},{4,2},{5,3},{2,4},{3,5},{0,6},{1,7},{14,8},{15,9},{12,... | collective-permute-start | bytes 196616 | tf_op jit(solution)/shard_map/ppermute | solution.py:494
  54.7 1.8 %collective-permute-done.13.refs_3_ = f32[128,128]{1,0:T(8,128)S(1)} collective-permute-done((f32[128,128]{1,0:T(8,128)S(1)}, f32[128,128]{1,0:T(8,128)S(1)}, u32[]{:S(2)}, u32[]{:S(2)}) %collective-permute-start.13) | collective-permute-done | bytes 65568 | tf_op jit(solution)/shard_map/ppermute | solution.py:494
  56.4 1.9 %collective-permute-done.12.refs_2_ = f32[128,128]{1,0:T(8,128)S(1)} collective-permute-done((f32[128,128]{1,0:T(8,128)S(1)}, f32[128,128]{1,0:T(8,128)S(1)}, u32[]{:S(2)}, u32[]{:S(2)}) %collective-permute-start.12) | collective-permute-done | bytes 65568 | tf_op jit(solution)/shard_map/ppermute | solution.py:494
  58.3 3.4 %shard_map.57 = (f32[256,256]{1,0:T(8,128)S(1)}, f32[256,256]{1,0:T(8,128)S(1)}) custom-call(s32[16]{0:T(128)S(1)} %constant_dynamic-update-slice_fusion.f, f32[128,128]{1,0:T(8,128)S(1)} %add.35.refs_0_, f32[128,128]{1,0:T(8,128)S(1)} %collective-permute-done.11.refs_1_, f32[128,128]{1,0:T(8,128)S(1)} %collective-permute-done.12.refs_2_, ...), custom_call_target="tpu_custom_call" | custom-call | tf_op jit(solution)/shard_map/pallas_call | solution.py:52
  65.8 4.7 %collective-permute-start.16 = (f32[1280,128]{1,0:T(8,128)S(1)}, f32[1280,128]{1,0:T(8,128)S(1)}, u32[]{:S(2)}, u32[]{:S(2)}) collective-permute-start(f32[1280,128]{1,0:T(8,128)S(1)} %get-tuple-element.104.refs_4_), channel_id=1, source_target_pairs={{9,1},{11,3},{13,5},{15,7},{0,8},{17,9},{2,10},{19,11},{4,12},{21,... | collective-permute-start | bytes 1966088 | tf_op jit(solution)/shard_map/ppermute | solution.py:494
  72.8 3.4 %collective-permute-start.18 = (f32[128,128]{1,0:T(8,128)S(1)}, f32[128,128]{1,0:T(8,128)S(1)}, u32[]{:S(2)}, u32[]{:S(2)}) collective-permute-start(f32[128,128]{1,0:T(8,128)S(1)} %get-tuple-element.109), channel_id=1, source_target_pairs={{1,0},{0,1},{3,2},{2,3},{5,4},{4,5},{7,6},{6,7},{9,8},{8,9},{11,10... | collective-permute-start | bytes 196616 | tf_op jit(solution)/shard_map/ppermute | solution.py:494
  76.2 1.7 %collective-permute-done.14.refs_2_ = f32[1280,128]{1,0:T(8,128)S(1)} collective-permute-done((f32[1280,128]{1,0:T(8,128)S(1)}, f32[1280,128]{1,0:T(8,128)S(1)}, u32[]{:S(2)}, u32[]{:S(2)}) %collective-permute-start.14) | collective-permute-done | bytes 655392 | tf_op jit(solution)/shard_map/ppermute | solution.py:494
  77.9 4.5 %collective-permute-done.16.refs_5_ = f32[1280,128]{1,0:T(8,128)S(1)} collective-permute-done((f32[1280,128]{1,0:T(8,128)S(1)}, f32[1280,128]{1,0:T(8,128)S(1)}, u32[]{:S(2)}, u32[]{:S(2)}) %collective-permute-start.16) | collective-permute-done | bytes 655392 | tf_op jit(solution)/shard_map/ppermute | solution.py:494
  82.4 1.9 %shard_map.60 = (f32[128,128]{1,0:T(8,128)S(1)}, f32[128,128]{1,0:T(8,128)S(1)}, f32[1280,128]{1,0:T(8,128)S(1)}, f32[1280,128]{1,0:T(8,128)S(1)}, f32[1280,128]{1,0:T(8,128)S(1)}, /*index=5*/f32[1280,128]{1,0:T(8,128)S(1)}) custom-call(s32[16]{0:T(128)S(1)} %constant_dynamic-update-slice_fusion.f, f32[1280,128]{1,0:T(8,128)S(1)} %get-tuple-element.101.refs_0_, ...), custom_call_target="tpu_custom_call" | custom-call | tf_op jit(solution)/shard_map/pallas_call | solution.py:52
  86.0 2.2 %collective-permute-start.22 = (f32[128,128]{1,0:T(8,128)S(1)}, f32[128,128]{1,0:T(8,128)S(1)}, u32[]{:S(2)}, u32[]{:S(2)}) collective-permute-start(f32[128,128]{1,0:T(8,128)S(1)} %add.36.refs_0_), channel_id=1, source_target_pairs={{6,0},{7,1},{4,2},{5,3},{2,4},{3,5},{0,6},{1,7},{14,8},{15,9},{12,... | collective-permute-start | bytes 196616 | tf_op jit(solution)/shard_map/ppermute | solution.py:494
  89.6 1.8 %collective-permute-done.22.refs_3_ = f32[128,128]{1,0:T(8,128)S(1)} collective-permute-done((f32[128,128]{1,0:T(8,128)S(1)}, f32[128,128]{1,0:T(8,128)S(1)}, u32[]{:S(2)}, u32[]{:S(2)}) %collective-permute-start.22) | collective-permute-done | bytes 65568 | tf_op jit(solution)/shard_map/ppermute | solution.py:494
  92.7 3.1 %shard_map.62 = (f32[256,256]{1,0:T(8,128)S(1)}, f32[256,256]{1,0:T(8,128)S(1)}) custom-call(s32[16]{0:T(128)S(1)} %constant_dynamic-update-slice_fusion.f, f32[128,128]{1,0:T(8,128)S(1)} %add.36.refs_0_, f32[128,128]{1,0:T(8,128)S(1)} %collective-permute-done.20.refs_1_, f32[128,128]{1,0:T(8,128)S(1)} %collective-permute-done.21.refs_2_, ...), custom_call_target="tpu_custom_call" | custom-call | tf_op jit(solution)/shard_map/pallas_call | solution.py:52
  99.7 4.6 %collective-permute-start.25 = (f32[1280,128]{1,0:T(8,128)S(1)}, f32[1280,128]{1,0:T(8,128)S(1)}, u32[]{:S(2)}, u32[]{:S(2)}) collective-permute-start(f32[1280,128]{1,0:T(8,128)S(1)} %get-tuple-element.120.refs_2_.refs_4_), channel_id=1, source_target_pairs={{9,1},{11,3},{13,5},{15,7},{0,8},{17,9},{2,10},{19,11},{4,12},{21,... | collective-permute-start | bytes 1966088 | tf_op jit(solution)/shard_map/ppermute | solution.py:494
  104.3 2.0 %collective-permute-start.28 = (f32[1280,128]{1,0:T(8,128)S(1)}, f32[1280,128]{1,0:T(8,128)S(1)}, u32[]{:S(2)}, u32[]{:S(2)}) collective-permute-start(f32[1280,128]{1,0:T(8,128)S(1)} %get-tuple-element.129), channel_id=1, source_target_pairs={{4,0},{5,1},{6,2},{7,3},{0,4},{1,5},{2,6},{3,7},{12,8},{13,9},{14,... | collective-permute-start | bytes 1966088 | tf_op jit(solution)/shard_map/ppermute | solution.py:494
  108.6 3.0 %collective-permute-start.27 = (f32[128,128]{1,0:T(8,128)S(1)}, f32[128,128]{1,0:T(8,128)S(1)}, u32[]{:S(2)}, u32[]{:S(2)}) collective-permute-start(f32[128,128]{1,0:T(8,128)S(1)} %get-tuple-element.123), channel_id=1, source_target_pairs={{1,0},{0,1},{3,2},{2,3},{5,4},{4,5},{7,6},{6,7},{9,8},{8,9},{11,10... | collective-permute-start | bytes 196616 | tf_op jit(solution)/shard_map/ppermute | solution.py:494
  112.1 4.3 %collective-permute-done.25.refs_3_.refs_5_ = f32[1280,128]{1,0:T(8,128)S(1)} collective-permute-done((f32[1280,128]{1,0:T(8,128)S(1)}, f32[1280,128]{1,0:T(8,128)S(1)}, u32[]{:S(2)}, u32[]{:S(2)}) %collective-permute-start.25) | collective-permute-done | bytes 655392 | tf_op jit(solution)/shard_map/ppermute | solution.py:494
  118.6 1.9 %shard_map.67 = (f32[128,128]{1,0:T(8,128)S(1)}, f32[128,128]{1,0:T(8,128)S(1)}, f32[1280,128]{1,0:T(8,128)S(1)}, f32[1280,128]{1,0:T(8,128)S(1)}, f32[1280,128]{1,0:T(8,128)S(1)}, /*index=5*/f32[1280,128]{1,0:T(8,128)S(1)}) custom-call(s32[16]{0:T(128)S(1)} %constant_dynamic-update-slice_fusion.f, f32[1280,128]{1,0:T(8,128)S(1)} %get-tuple-element.118.refs_4_.refs_0_, ...), custom_call_target="tpu_custom_call" | custom-call | tf_op jit(solution)/shard_map/pallas_call | solution.py:52
  126.8 1.9 %collective-permute-done.32.refs_3_ = f32[128,128]{1,0:T(8,128)S(1)} collective-permute-done((f32[128,128]{1,0:T(8,128)S(1)}, f32[128,128]{1,0:T(8,128)S(1)}, u32[]{:S(2)}, u32[]{:S(2)}) %collective-permute-start.32) | collective-permute-done | bytes 65568 | tf_op jit(solution)/shard_map/ppermute | solution.py:494
  130.9 3.6 %shard_map.69 = (f32[264,256]{1,0:T(8,128)S(1)}, f32[256,256]{1,0:T(8,128)}) custom-call(s32[16]{0:T(128)S(1)} %constant_dynamic-update-slice_fusion.f, f32[128,128]{1,0:T(8,128)S(1)} %add.37.refs_0_, f32[128,128]{1,0:T(8,128)S(1)} %collective-permute-done.30.refs_1_, f32[128,128]{1,0:T(8,128)S(1)} %collective-permute-done.31.refs_2_, ...), custom_call_target="tpu_custom_call" | custom-call | tf_op jit(solution)/shard_map/pallas_call | solution.py:52
  136.2 3.0 %shard_map.70 = (f32[2048,256]{1,0:T(8,128)}, f32[512,256]{1,0:T(8,128)}, f32[1,256]{1,0:T(1,128)}) custom-call(s32[16]{0:T(128)S(1)} %constant_dynamic-update-slice_fusion.f, f32[264,256]{1,0:T(8,128)S(1)} %get-tuple-element.140.own_ref, f32[264,256]{1,0:T(8,128)S(1)} %collective-permute-done.34.other_ref, ...), custom_call_target="tpu_custom_call" | custom-call | flops 1 | bytes 1 | tf_op jit(solution)/shard_map/pallas_call | solution.py:393
  140.2 2.0 %shard_map.71 = (f32[2048,256]{1,0:T(8,128)}, f32[512,256]{1,0:T(8,128)}) custom-call(s32[16]{0:T(128)S(1)} %constant_dynamic-update-slice_fusion.f, f32[264,256]{1,0:T(8,128)S(1)} %get-tuple-element.140.own_ref, f32[264,256]{1,0:T(8,128)S(1)} %collective-permute-done.34.other_ref, ...), custom_call_target="tpu_custom_call", output_to_operand_aliasing={{0}: (5, {}), {1}: (6, {})} | custom-call | flops 1 | bytes 1 | tf_op jit(solution)/shard_map/pallas_call | solution.py:393
  (75 shorter events, 43.9 us)
Async XLA Ops:
  3.1 27.2 %collective-permute-start.4 = (f32[768,256]{1,0:T(8,128)}, f32[768,256]{1,0:T(8,128)S(1)}, u32[]{:S(2)}, u32[]{:S(2)}) collective-permute-start(f32[768,256]{1,0:T(8,128)} %get-tuple-element.82), channel_id=1, source_target_pairs={{4,0},{5,1},{6,2},{7,3},{0,4},{1,5},{2,6},{3,7},{12,8},{13,9},{14,... | collective-permute-start | bytes 2359304 | tf_op jit(solution)/shard_map/ppermute | solution.py:494
  9.8 7.0 %collective-permute-start.1 = (f32[384,128]{1,0:T(8,128)S(1)}, f32[384,128]{1,0:T(8,128)S(1)}, u32[]{:S(2)}, u32[]{:S(2)}) collective-permute-start(f32[384,128]{1,0:T(8,128)S(1)} %add.34.own_ref), channel_id=1, source_target_pairs={{2,0},{3,1},{0,2},{1,3},{6,4},{7,5},{4,6},{5,7},{10,8},{11,9},{8,1... | collective-permute-start | bytes 589832 | tf_op jit(solution)/shard_map/ppermute | solution.py:494
  20.3 10.0 %collective-permute-start.3 = (f32[256,256]{1,0:T(8,128)S(1)}, f32[256,256]{1,0:T(8,128)S(1)}, u32[]{:S(2)}, u32[]{:S(2)}) collective-permute-start(f32[256,256]{1,0:T(8,128)S(1)} %get-tuple-element.77.rotation_ref), channel_id=1, source_target_pairs={{4,0},{5,1},{6,2},{7,3},{0,4},{1,5},{2,6},{3,7},{12,8},{13,9},{14,... | collective-permute-start | bytes 786440 | tf_op jit(solution)/shard_map/ppermute | solution.py:494
  21.9 25.5 %collective-permute-start.2 = (f32[1280,128]{1,0:T(8,128)S(1)}, f32[1280,128]{1,0:T(8,128)S(1)}, u32[]{:S(2)}, u32[]{:S(2)}) collective-permute-start(f32[1280,128]{1,0:T(8,128)S(1)} %get-tuple-element.81.refs_1_), channel_id=1, source_target_pairs={{8,0},{9,1},{10,2},{11,3},{16,8},{17,9},{18,10},{19,11},{4,12},{5,... | collective-permute-start | bytes 1966088 | tf_op jit(solution)/shard_map/ppermute | solution.py:494
  23.2 12.2 %collective-permute-start.6 = (f32[256,256]{1,0:T(8,128)S(1)}, f32[256,256]{1,0:T(8,128)S(1)}, u32[]{:S(2)}, u32[]{:S(2)}) collective-permute-start(f32[256,256]{1,0:T(8,128)S(1)} %copy-done.1), channel_id=1, source_target_pairs={{4,0},{5,1},{6,2},{7,3},{0,4},{1,5},{2,6},{3,7},{12,8},{13,9},{14,... | collective-permute-start | bytes 786440 | tf_op jit(solution)/shard_map/ppermute | solution.py:494
  31.4 16.0 %collective-permute-start.5 = (f32[768,128]{1,0:T(8,128)S(1)}, f32[768,128]{1,0:T(8,128)S(1)}, u32[]{:S(2)}, u32[]{:S(2)}) collective-permute-start(f32[768,128]{1,0:T(8,128)S(1)} %get-tuple-element.84.refs_4_), channel_id=1, source_target_pairs={{12,4},{13,5},{14,6},{15,7},{0,8},{1,9},{2,10},{3,11},{20,12},{21,... | collective-permute-start | bytes 1179656 | tf_op jit(solution)/shard_map/ppermute | solution.py:494
  36.4 11.0 %collective-permute-start.7 = (f32[512,128]{1,0:T(8,128)S(1)}, f32[512,128]{1,0:T(8,128)S(1)}, u32[]{:S(2)}, u32[]{:S(2)}) collective-permute-start(f32[512,128]{1,0:T(8,128)S(1)} %get-tuple-element.87.refs_7_), channel_id=1, source_target_pairs={{12,4},{13,5},{14,6},{15,7},{0,8},{1,9},{2,10},{3,11},{20,12},{21,... | collective-permute-start | bytes 786440 | tf_op jit(solution)/shard_map/ppermute | solution.py:494
  41.5 7.7 %collective-permute-start.8 = (f32[128,128]{1,0:T(8,128)S(1)}, f32[128,128]{1,0:T(8,128)S(1)}, u32[]{:S(2)}, u32[]{:S(2)}) collective-permute-start(f32[128,128]{1,0:T(8,128)S(1)} %get-tuple-element.91), channel_id=1, source_target_pairs={{0,0},{8,1},{2,2},{10,3},{1,4},{9,5},{3,6},{11,7},{4,8},{16,9},{6,... | collective-permute-start | bytes 196616 | tf_op jit(solution)/shard_map/ppermute | solution.py:494
  42.2 7.1 %collective-permute-start.9 = (f32[128,128]{1,0:T(8,128)S(1)}, f32[128,128]{1,0:T(8,128)S(1)}, u32[]{:S(2)}, u32[]{:S(2)}) collective-permute-start(f32[128,128]{1,0:T(8,128)S(1)} %get-tuple-element.92), channel_id=1, source_target_pairs={{4,0},{0,1},{6,2},{2,3},{5,4},{1,5},{7,6},{3,7},{12,8},{8,9},{14,1... | collective-permute-start | bytes 196616 | tf_op jit(solution)/shard_map/ppermute | solution.py:494
  50.6 5.8 %collective-permute-start.13 = (f32[128,128]{1,0:T(8,128)S(1)}, f32[128,128]{1,0:T(8,128)S(1)}, u32[]{:S(2)}, u32[]{:S(2)}) collective-permute-start(f32[128,128]{1,0:T(8,128)S(1)} %add.35.refs_0_), channel_id=1, source_target_pairs={{6,0},{7,1},{4,2},{5,3},{2,4},{3,5},{0,6},{1,7},{14,8},{15,9},{12,... | collective-permute-start | bytes 196616 | tf_op jit(solution)/shard_map/ppermute | solution.py:494
  54.0 4.3 %collective-permute-start.12 = (f32[128,128]{1,0:T(8,128)S(1)}, f32[128,128]{1,0:T(8,128)S(1)}, u32[]{:S(2)}, u32[]{:S(2)}) collective-permute-start(f32[128,128]{1,0:T(8,128)S(1)} %add.35.refs_0_), channel_id=1, source_target_pairs={{4,0},{5,1},{6,2},{7,3},{0,4},{1,5},{2,6},{3,7},{12,8},{13,9},{14,... | collective-permute-start | bytes 196616 | tf_op jit(solution)/shard_map/ppermute | solution.py:494
  54.0 4.3 %collective-permute-start.11 = (f32[128,128]{1,0:T(8,128)S(1)}, f32[128,128]{1,0:T(8,128)S(1)}, u32[]{:S(2)}, u32[]{:S(2)}) collective-permute-start(f32[128,128]{1,0:T(8,128)S(1)} %add.35.refs_0_), channel_id=1, source_target_pairs={{2,0},{3,1},{0,2},{1,3},{6,4},{7,5},{4,6},{5,7},{10,8},{11,9},{8,1... | collective-permute-start | bytes 196616 | tf_op jit(solution)/shard_map/ppermute | solution.py:494
  61.7 2.8 %collective-permute-start.15 = (f32[256,256]{1,0:T(8,128)S(1)}, f32[256,256]{1,0:T(8,128)S(1)}, u32[]{:S(2)}, u32[]{:S(2)}) collective-permute-start(f32[256,256]{1,0:T(8,128)S(1)} %get-tuple-element.96.rotation_ref), channel_id=1, source_target_pairs={{1,0},{0,1},{3,2},{2,3},{5,4},{4,5},{7,6},{6,7},{9,8},{8,9},{11,10... | collective-permute-start | bytes 786440 | tf_op jit(solution)/shard_map/ppermute | solution.py:494
  63.1 14.9 %collective-permute-start.14 = (f32[1280,128]{1,0:T(8,128)S(1)}, f32[1280,128]{1,0:T(8,128)S(1)}, u32[]{:S(2)}, u32[]{:S(2)}) collective-permute-start(f32[1280,128]{1,0:T(8,128)S(1)} %get-tuple-element.102.refs_1_), channel_id=1, source_target_pairs={{8,0},{10,2},{12,4},{14,6},{16,8},{1,9},{18,10},{3,11},{20,12},{5,... | collective-permute-start | bytes 1966088 | tf_op jit(solution)/shard_map/ppermute | solution.py:494
  65.8 16.6 %collective-permute-start.16 = (f32[1280,128]{1,0:T(8,128)S(1)}, f32[1280,128]{1,0:T(8,128)S(1)}, u32[]{:S(2)}, u32[]{:S(2)}) collective-permute-start(f32[1280,128]{1,0:T(8,128)S(1)} %get-tuple-element.104.refs_4_), channel_id=1, source_target_pairs={{9,1},{11,3},{13,5},{15,7},{0,8},{17,9},{2,10},{19,11},{4,12},{21,... | collective-permute-start | bytes 1966088 | tf_op jit(solution)/shard_map/ppermute | solution.py:494
  72.1 12.1 %collective-permute-start.17 = (f32[128,128]{1,0:T(8,128)S(1)}, f32[128,128]{1,0:T(8,128)S(1)}, u32[]{:S(2)}, u32[]{:S(2)}) collective-permute-start(f32[128,128]{1,0:T(8,128)S(1)} %get-tuple-element.108), channel_id=1, source_target_pairs={{0,0},{8,1},{2,2},{10,3},{4,4},{12,5},{6,6},{14,7},{1,8},{16,9},{3... | collective-permute-start | bytes 196616 | tf_op jit(solution)/shard_map/ppermute | solution.py:494
  72.8 11.5 %collective-permute-start.18 = (f32[128,128]{1,0:T(8,128)S(1)}, f32[128,128]{1,0:T(8,128)S(1)}, u32[]{:S(2)}, u32[]{:S(2)}) collective-permute-start(f32[128,128]{1,0:T(8,128)S(1)} %get-tuple-element.109), channel_id=1, source_target_pairs={{1,0},{0,1},{3,2},{2,3},{5,4},{4,5},{7,6},{6,7},{9,8},{8,9},{11,10... | collective-permute-start | bytes 196616 | tf_op jit(solution)/shard_map/ppermute | solution.py:494
  86.0 5.4 %collective-permute-start.22 = (f32[128,128]{1,0:T(8,128)S(1)}, f32[128,128]{1,0:T(8,128)S(1)}, u32[]{:S(2)}, u32[]{:S(2)}) collective-permute-start(f32[128,128]{1,0:T(8,128)S(1)} %add.36.refs_0_), channel_id=1, source_target_pairs={{6,0},{7,1},{4,2},{5,3},{2,4},{3,5},{0,6},{1,7},{14,8},{15,9},{12,... | collective-permute-start | bytes 196616 | tf_op jit(solution)/shard_map/ppermute | solution.py:494
  88.2 4.3 %collective-permute-start.21 = (f32[128,128]{1,0:T(8,128)S(1)}, f32[128,128]{1,0:T(8,128)S(1)}, u32[]{:S(2)}, u32[]{:S(2)}) collective-permute-start(f32[128,128]{1,0:T(8,128)S(1)} %add.36.refs_0_), channel_id=1, source_target_pairs={{4,0},{5,1},{6,2},{7,3},{0,4},{1,5},{2,6},{3,7},{12,8},{13,9},{14,... | collective-permute-start | bytes 196616 | tf_op jit(solution)/shard_map/ppermute | solution.py:494
  88.3 4.5 %collective-permute-start.20 = (f32[128,128]{1,0:T(8,128)S(1)}, f32[128,128]{1,0:T(8,128)S(1)}, u32[]{:S(2)}, u32[]{:S(2)}) collective-permute-start(f32[128,128]{1,0:T(8,128)S(1)} %add.36.refs_0_), channel_id=1, source_target_pairs={{2,0},{3,1},{0,2},{1,3},{6,4},{7,5},{4,6},{5,7},{10,8},{11,9},{8,1... | collective-permute-start | bytes 196616 | tf_op jit(solution)/shard_map/ppermute | solution.py:494
  95.8 2.6 %collective-permute-start.24 = (f32[256,256]{1,0:T(8,128)S(1)}, f32[256,256]{1,0:T(8,128)S(1)}, u32[]{:S(2)}, u32[]{:S(2)}) collective-permute-start(f32[256,256]{1,0:T(8,128)S(1)} %get-tuple-element.113.rotation_ref), channel_id=1, source_target_pairs={{1,0},{0,1},{3,2},{2,3},{5,4},{4,5},{7,6},{6,7},{9,8},{8,9},{11,10... | collective-permute-start | bytes 786440 | tf_op jit(solution)/shard_map/ppermute | solution.py:494
  97.2 15.0 %collective-permute-start.23 = (f32[1280,128]{1,0:T(8,128)S(1)}, f32[1280,128]{1,0:T(8,128)S(1)}, u32[]{:S(2)}, u32[]{:S(2)}) collective-permute-start(f32[1280,128]{1,0:T(8,128)S(1)} %get-tuple-element.119.refs_0_.refs_1_), channel_id=1, source_target_pairs={{8,0},{10,2},{12,4},{14,6},{16,8},{1,9},{18,10},{3,11},{20,12},{5,... | collective-permute-start | bytes 1966088 | tf_op jit(solution)/shard_map/ppermute | solution.py:494
  99.7 16.7 %collective-permute-start.25 = (f32[1280,128]{1,0:T(8,128)S(1)}, f32[1280,128]{1,0:T(8,128)S(1)}, u32[]{:S(2)}, u32[]{:S(2)}) collective-permute-start(f32[1280,128]{1,0:T(8,128)S(1)} %get-tuple-element.120.refs_2_.refs_4_), channel_id=1, source_target_pairs={{9,1},{11,3},{13,5},{15,7},{0,8},{17,9},{2,10},{19,11},{4,12},{21,... | collective-permute-start | bytes 1966088 | tf_op jit(solution)/shard_map/ppermute | solution.py:494
  104.3 16.3 %collective-permute-start.28 = (f32[1280,128]{1,0:T(8,128)S(1)}, f32[1280,128]{1,0:T(8,128)S(1)}, u32[]{:S(2)}, u32[]{:S(2)}) collective-permute-start(f32[1280,128]{1,0:T(8,128)S(1)} %get-tuple-element.129), channel_id=1, source_target_pairs={{4,0},{5,1},{6,2},{7,3},{0,4},{1,5},{2,6},{3,7},{12,8},{13,9},{14,... | collective-permute-start | bytes 1966088 | tf_op jit(solution)/shard_map/ppermute | solution.py:494
  107.9 9.1 %collective-permute-start.26 = (f32[128,128]{1,0:T(8,128)S(1)}, f32[128,128]{1,0:T(8,128)S(1)}, u32[]{:S(2)}, u32[]{:S(2)}) collective-permute-start(f32[128,128]{1,0:T(8,128)S(1)} %get-tuple-element.122), channel_id=1, source_target_pairs={{0,0},{8,1},{2,2},{10,3},{4,4},{12,5},{6,6},{14,7},{1,8},{16,9},{3... | collective-permute-start | bytes 196616 | tf_op jit(solution)/shard_map/ppermute | solution.py:494
  108.6 8.4 %collective-permute-start.27 = (f32[128,128]{1,0:T(8,128)S(1)}, f32[128,128]{1,0:T(8,128)S(1)}, u32[]{:S(2)}, u32[]{:S(2)}) collective-permute-start(f32[128,128]{1,0:T(8,128)S(1)} %get-tuple-element.123), channel_id=1, source_target_pairs={{1,0},{0,1},{3,2},{2,3},{5,4},{4,5},{7,6},{6,7},{9,8},{8,9},{11,10... | collective-permute-start | bytes 196616 | tf_op jit(solution)/shard_map/ppermute | solution.py:494
  117.0 12.6 %collective-permute-start.33 = (f32[512,128]{1,0:T(8,128)S(1)}, f32[512,128]{1,0:T(8,128)S(1)}, u32[]{:S(2)}, u32[]{:S(2)}) collective-permute-start(f32[512,128]{1,0:T(8,128)S(1)} %shard_map.65), channel_id=1, source_target_pairs={{4,0},{5,1},{6,2},{7,3},{0,4},{1,5},{2,6},{3,7},{12,8},{13,9},{14,... | collective-permute-start | bytes 786440 | tf_op jit(solution)/shard_map/ppermute | solution.py:494
  120.6 2.0 %collective-permute-start.29 = (f32[128,128]{1,0:T(8,128)S(1)}, f32[128,128]{1,0:T(8,128)S(1)}, u32[]{:S(2)}, u32[]{:S(2)}) collective-permute-start(f32[128,128]{1,0:T(8,128)S(1)} %get-tuple-element.130), channel_id=1, source_target_pairs={{1,0},{0,1},{3,2},{2,3},{5,4},{4,5},{7,6},{6,7},{9,8},{8,9},{11,10... | collective-permute-start | bytes 196616 | tf_op jit(solution)/shard_map/ppermute | solution.py:494
  122.6 6.0 %collective-permute-start.32 = (f32[128,128]{1,0:T(8,128)S(1)}, f32[128,128]{1,0:T(8,128)S(1)}, u32[]{:S(2)}, u32[]{:S(2)}) collective-permute-start(f32[128,128]{1,0:T(8,128)S(1)} %add.37.refs_0_), channel_id=1, source_target_pairs={{6,0},{7,1},{4,2},{5,3},{2,4},{3,5},{0,6},{1,7},{14,8},{15,9},{12,... | collective-permute-start | bytes 196616 | tf_op jit(solution)/shard_map/ppermute | solution.py:494
  124.0 5.0 %collective-permute-start.31 = (f32[128,128]{1,0:T(8,128)S(1)}, f32[128,128]{1,0:T(8,128)S(1)}, u32[]{:S(2)}, u32[]{:S(2)}) collective-permute-start(f32[128,128]{1,0:T(8,128)S(1)} %add.37.refs_0_), channel_id=1, source_target_pairs={{4,0},{5,1},{6,2},{7,3},{0,4},{1,5},{2,6},{3,7},{12,8},{13,9},{14,... | collective-permute-start | bytes 196616 | tf_op jit(solution)/shard_map/ppermute | solution.py:494
  125.3 4.4 %collective-permute-start.30 = (f32[128,128]{1,0:T(8,128)S(1)}, f32[128,128]{1,0:T(8,128)S(1)}, u32[]{:S(2)}, u32[]{:S(2)}) collective-permute-start(f32[128,128]{1,0:T(8,128)S(1)} %add.37.refs_0_), channel_id=1, source_target_pairs={{2,0},{3,1},{0,2},{1,3},{6,4},{7,5},{4,6},{5,7},{10,8},{11,9},{8,1... | collective-permute-start | bytes 196616 | tf_op jit(solution)/shard_map/ppermute | solution.py:494
  129.6 10.5 %collective-permute-start.35 = (f32[768,128]{1,0:T(8,128)S(1)}, f32[768,128]{1,0:T(8,128)S(1)}, u32[]{:S(2)}, u32[]{:S(2)}) collective-permute-start(f32[768,128]{1,0:T(8,128)S(1)} %shard_map.68), channel_id=1, source_target_pairs={{4,0},{5,1},{6,2},{7,3},{0,4},{1,5},{2,6},{3,7},{12,8},{13,9},{14,... | collective-permute-start | bytes 1179656 | tf_op jit(solution)/shard_map/ppermute | solution.py:494
  (7 other events, 37.4 us)

commit v15 on v14

--- a/solution.py
+++ b/solution.py
@@ -168,16 +168,19 @@
 def first_rotation(facts, own, other_y, half):
     size = 2 * half
 
-    def body(f, own_ref, other_ref, rotation_ref, g_ref, x_ref, e_ref):
+    def body(f, own_ref, other_ref, rotation_ref, g_ref, half_ref, x_ref, e_ref):
         total = own_ref[...] + other_ref[...]
         g_ref[:half, :half] = total[:half]
         g_ref[:half, half:] = total[half : 2 * half]
         g_ref[half:, :half] = total[half : 2 * half].T
         g_ref[half:, half:] = total[2 * half :]
         put_rotation(rotation_ref, g_ref[...], x_ref, e_ref, False)
+        rotation = rotation_ref[...]
+        half_ref[...] = jnp.where(f[CORE] == 0, rotation[:half], rotation[half:])
 
     square = pltpu.VMEM((size, size), jnp.float32)
-    return call(body, facts, [own, other_y], (shape(size, size),) * 2, [square] * 2)
+    outs = (shape(size, size),) * 2 + (shape(half, size),)
+    return call(body, facts, [own, other_y], outs, [square] * 2)
 
 
 def later_rotation(facts, parts, diagonals, half, last_round):
@@ -230,10 +233,14 @@
 def turn_rows(facts, rotation, rows_of, vector_rows, half, own):
     rows = rows_of.shape[0] // 2 if own else rows_of.shape[0]
 
-    def body(f, rotation_ref, x_ref, stay_ref, leave_ref):
+    def body(f, *refs):
+        x_ref, stay_ref, leave_ref = refs[-3:]
+        matrix = lax.concatenate([r[...] for r in refs[:-3]], 0)
+        if not own:
+            matrix = swapped(f[CORE] == 1, matrix, 0)
         zero = f[X] == (0 if own else 1)
         upper_leaves = jnp.where(zero, f[FIRST], 1) == 1
-        turn = split(swapped(upper_leaves, rotation_ref[...], 1))
+        turn = split(swapped(upper_leaves, matrix, 1))
         here = pl.multiple_of(f[X] * rows, 8)
         out = dot3(x_ref[pl.ds(here, rows)] if own else x_ref[...], turn)
         stay_ref[:rows] = out[:, :half]
@@ -251,7 +258,7 @@
             leave_ref[rows:] = out[:, half:]
 
     return call(
-        body, facts, [rotation, rows_of], (shape(rows + vector_rows, half),) * 2
+        body, facts, rotation + [rows_of], (shape(rows + vector_rows, half),) * 2
     )
 
 
@@ -557,13 +564,16 @@
     got_top = exchange(top_give, 1, 0)
     own = first_gram(sector, half)
     own = sum_rows(own + exchange(own, 0, 1))
-    rotation, gram = first_rotation(facts, own, exchange(own, 0, 2), half)
+    rotation, gram, rotation_half = first_rotation(facts, own, exchange(own, 0, 2), half)
 
     for sweep_round in range(ROUNDS - 1):
         last_move = sweep_round == ROUNDS - 2
         if sweep_round == 0:
-            other_rotation = exchange(rotation, 1, 0)
-            stay, leave = turn_rows(facts, rotation, sector, vector_rows, half, True)
+            other_half = exchange(rotation_half, 1, 0)
+            other_rotation = [other_half, exchange(other_half, 0, 1)]
+            stay, leave = turn_rows(
+                facts, [rotation], sector, vector_rows, half, True
+            )
             leave, rest_give = together(leave, rest_give)
             got_rest = exchange(rest_give, 1, 0)
             own = [stay, leave, shift(leave, lambda p, r: p % 2 == 0)]
@@ -588,7 +598,7 @@
             diagonals = [pass_diagonal(leave), exchange(stay, 0, 1)]
             if last_move:
                 native = exchange(native[0], 1, 0)
-                top = part // 2
+                top = part * 5 // 8
                 top_give = give_arrived(facts, own, others[0], top, half)
                 own[2], others[0][2], top_give, *diagonals = together(
                     own[2], others[0][2], top_give, *diagonals

time: 143 us -> 143 us (level)
  starting transfers between devices: 57.1 us -> 55.6 us
    ppermute x36 -> x37, starting transfers between devices: 57.1 us -> 55.6 us  [permute(): return lax.ppermute(block, ('pair', 'row'), moves)]
    ppermute x36 -> x37, waiting for transfers between devices: 40.8 us -> 42.1 us  [permute(): return lax.ppermute(block, ('pair', 'row'), moves)]
  transfers between devices with their start and end apart: 36 -> 37, of which waited for: 22 -> 21; matrix products, arithmetic and copies ran while one was open for 0% -> 0% of each run, Pallas kernels for 22% -> 23%
where the time goes in v15:
time: 143 us; the launch traced here: 142 us
  starting transfers between devices  55.6 us (39%)
  Pallas kernels  43 us (30%)
  waiting for transfers between devices  42.1 us (29%)
    ppermute x37, starting transfers between devices, permute(): return lax.ppermute(block, ('pair', 'row'), moves)  55.6 us
    ppermute x37, waiting for transfers between devices, permute(): return lax.ppermute(block, ('pair', 'row'), moves)  42.1 us
    pallas_call x19, Pallas kernels, call(): pl.pallas_call(body, out_shape=outs, in_specs=[pl.BlockSpec(memory_space=...  33.4 us
    pallas_call x2, Pallas kernels, finish_call(): pl.pallas_call(body, out_shape=outs, in_specs=[pl.BlockSpec(memory_space=...  4.98 us
  transfers between devices with their start and end apart: 37, of which 21 were waited for; matrix products, arithmetic and copies ran while one was open for 0% of the time, Pallas kernels for 23%

profile of v15, /device:TPU:0, one launch (start us, length us, event | category | flops | bytes accessed | tf_op | source)
XLA Modules:
  0.0 142.2 jit_solution(2350360558747902663)
XLA Ops:
  0.6 2.5 %shard_map.52 = (f32[768,256]{1,0:T(8,128)}, f32[256,256]{1,0:T(8,128)}) custom-call(f32[2048,256]{1,0:T(8,128)} %x_ref.3), custom_call_target="tpu_custom_call" | custom-call | tf_op jit(solution)/shard_map/pallas_call | solution.py:104
  3.1 3.0 %collective-permute-start.5 = (f32[768,256]{1,0:T(8,128)}, f32[768,256]{1,0:T(8,128)S(1)}, u32[]{:S(2)}, u32[]{:S(2)}) collective-permute-start(f32[768,256]{1,0:T(8,128)} %get-tuple-element.84), channel_id=1, source_target_pairs={{4,0},{5,1},{6,2},{7,3},{0,4},{1,5},{2,6},{3,7},{12,8},{13,9},{14,... | collective-permute-start | bytes 2359304 | tf_op jit(solution)/shard_map/ppermute | solution.py:501
  6.1 2.2 %shard_map.49 = f32[384,128]{1,0:T(8,128)S(1)} custom-call(f32[2048,256]{1,0:T(8,128)S(1)} %copy-done), custom_call_target="tpu_custom_call" | custom-call | tf_op jit(solution)/shard_map/pallas_call | solution.py:74
  11.6 5.3 %collective-permute-done.1.other_ref = f32[384,128]{1,0:T(8,128)S(1)} collective-permute-done((f32[384,128]{1,0:T(8,128)S(1)}, f32[384,128]{1,0:T(8,128)S(1)}, u32[]{:S(2)}, u32[]{:S(2)}) %collective-permute-start.1) | collective-permute-done | bytes 196640 | tf_op jit(solution)/shard_map/ppermute | solution.py:501
  16.8 3.4 %shard_map.50 = (f32[256,256]{1,0:T(8,128)S(1)}, f32[256,256]{1,0:T(8,128)S(1)}, f32[128,256]{1,0:T(8,128)S(1)}) custom-call(s32[16]{0:T(128)S(1)} %constant_dynamic-update-slice_fusion.f, f32[384,128]{1,0:T(8,128)S(1)} %add.34.own_ref, f32[384,128]{1,0:T(8,128)S(1)} %collective-permute-done.1.other_ref), custom_call_target="tpu_custom_call" | custom-call | tf_op jit(solution)/shard_map/pallas_call | solution.py:52
  23.2 4.0 %collective-permute-start.7 = (f32[256,256]{1,0:T(8,128)S(1)}, f32[256,256]{1,0:T(8,128)S(1)}, u32[]{:S(2)}, u32[]{:S(2)}) collective-permute-start(f32[256,256]{1,0:T(8,128)S(1)} %copy-done.1), channel_id=1, source_target_pairs={{4,0},{5,1},{6,2},{7,3},{0,4},{1,5},{2,6},{3,7},{12,8},{13,9},{14,... | collective-permute-start | bytes 786440 | tf_op jit(solution)/shard_map/ppermute | solution.py:501
  29.6 3.5 %collective-permute-start.6 = (f32[768,128]{1,0:T(8,128)S(1)}, f32[768,128]{1,0:T(8,128)S(1)}, u32[]{:S(2)}, u32[]{:S(2)}) collective-permute-start(f32[768,128]{1,0:T(8,128)S(1)} %get-tuple-element.86.refs_4_), channel_id=1, source_target_pairs={{12,4},{13,5},{14,6},{15,7},{0,8},{1,9},{2,10},{3,11},{20,12},{21,... | collective-permute-start | bytes 1179656 | tf_op jit(solution)/shard_map/ppermute | solution.py:501
  34.1 3.5 %collective-permute-start.8 = (f32[512,128]{1,0:T(8,128)S(1)}, f32[512,128]{1,0:T(8,128)S(1)}, u32[]{:S(2)}, u32[]{:S(2)}) collective-permute-start(f32[512,128]{1,0:T(8,128)S(1)} %get-tuple-element.89.refs_7_), channel_id=1, source_target_pairs={{12,4},{13,5},{14,6},{15,7},{0,8},{1,9},{2,10},{3,11},{20,12},{21,... | collective-permute-start | bytes 786440 | tf_op jit(solution)/shard_map/ppermute | solution.py:501
  37.5 1.6 %shard_map.56 = (f32[128,128]{1,0:T(8,128)S(1)}, f32[128,128]{1,0:T(8,128)S(1)}) custom-call(s32[16]{0:T(128)S(1)} %constant_dynamic-update-slice_fusion.f, f32[256,256]{1,0:T(8,128)S(1)} %get-tuple-element.92.gram_ref, f32[256,256]{1,0:T(8,128)S(1)} %get-tuple-element.78.refs_0_.rotation_ref), custom_call_target="tpu_custom_call" | custom-call | tf_op jit(solution)/shard_map/pallas_call | solution.py:52
  40.7 6.6 %collective-permute-done.8.refs_8_ = f32[512,128]{1,0:T(8,128)S(1)} collective-permute-done((f32[512,128]{1,0:T(8,128)S(1)}, f32[512,128]{1,0:T(8,128)S(1)}, u32[]{:S(2)}, u32[]{:S(2)}) %collective-permute-start.8) | collective-permute-done | bytes 262176 | tf_op jit(solution)/shard_map/ppermute | solution.py:501
  47.4 1.9 %shard_map.55 = (f32[128,128]{1,0:T(8,128)S(1)}, f32[128,128]{1,0:T(8,128)S(1)}, f32[1280,128]{1,0:T(8,128)S(1)}, f32[1280,128]{1,0:T(8,128)S(1)}, f32[1280,128]{1,0:T(8,128)S(1)}, /*index=5*/f32[1280,128]{1,0:T(8,128)S(1)}) custom-call(s32[16]{0:T(128)S(1)} %constant_dynamic-update-slice_fusion.f, f32[1280,128]{1,0:T(8,128)S(1)} %get-tuple-element.79.refs_0_, ...), custom_call_target="tpu_custom_call" | custom-call | tf_op jit(solution)/shard_map/pallas_call | solution.py:52
  50.6 3.2 %collective-permute-start.14 = (f32[128,128]{1,0:T(8,128)S(1)}, f32[128,128]{1,0:T(8,128)S(1)}, u32[]{:S(2)}, u32[]{:S(2)}) collective-permute-start(f32[128,128]{1,0:T(8,128)S(1)} %add.35.refs_0_), channel_id=1, source_target_pairs={{6,0},{7,1},{4,2},{5,3},{2,4},{3,5},{0,6},{1,7},{14,8},{15,9},{12,... | collective-permute-start | bytes 196616 | tf_op jit(solution)/shard_map/ppermute | solution.py:501
  54.4 1.8 %collective-permute-done.14.refs_3_ = f32[128,128]{1,0:T(8,128)S(1)} collective-permute-done((f32[128,128]{1,0:T(8,128)S(1)}, f32[128,128]{1,0:T(8,128)S(1)}, u32[]{:S(2)}, u32[]{:S(2)}) %collective-permute-start.14) | collective-permute-done | bytes 65568 | tf_op jit(solution)/shard_map/ppermute | solution.py:501
  56.2 1.9 %collective-permute-done.13.refs_2_ = f32[128,128]{1,0:T(8,128)S(1)} collective-permute-done((f32[128,128]{1,0:T(8,128)S(1)}, f32[128,128]{1,0:T(8,128)S(1)}, u32[]{:S(2)}, u32[]{:S(2)}) %collective-permute-start.13) | collective-permute-done | bytes 65568 | tf_op jit(solution)/shard_map/ppermute | solution.py:501
  58.0 3.4 %shard_map.57 = (f32[256,256]{1,0:T(8,128)S(1)}, f32[256,256]{1,0:T(8,128)S(1)}) custom-call(s32[16]{0:T(128)S(1)} %constant_dynamic-update-slice_fusion.f, f32[128,128]{1,0:T(8,128)S(1)} %add.35.refs_0_, f32[128,128]{1,0:T(8,128)S(1)} %collective-permute-done.12.refs_1_, f32[128,128]{1,0:T(8,128)S(1)} %collective-permute-done.13.refs_2_, ...), custom_call_target="tpu_custom_call" | custom-call | tf_op jit(solution)/shard_map/pallas_call | solution.py:52
  65.5 4.9 %collective-permute-start.17 = (f32[1280,128]{1,0:T(8,128)S(1)}, f32[1280,128]{1,0:T(8,128)S(1)}, u32[]{:S(2)}, u32[]{:S(2)}) collective-permute-start(f32[1280,128]{1,0:T(8,128)S(1)} %get-tuple-element.106.refs_4_), channel_id=1, source_target_pairs={{9,1},{11,3},{13,5},{15,7},{0,8},{17,9},{2,10},{19,11},{4,12},{21,... | collective-permute-start | bytes 1966088 | tf_op jit(solution)/shard_map/ppermute | solution.py:501
  72.8 3.4 %collective-permute-start.19 = (f32[128,128]{1,0:T(8,128)S(1)}, f32[128,128]{1,0:T(8,128)S(1)}, u32[]{:S(2)}, u32[]{:S(2)}) collective-permute-start(f32[128,128]{1,0:T(8,128)S(1)} %get-tuple-element.111), channel_id=1, source_target_pairs={{1,0},{0,1},{3,2},{2,3},{5,4},{4,5},{7,6},{6,7},{9,8},{8,9},{11,10... | collective-permute-start | bytes 196616 | tf_op jit(solution)/shard_map/ppermute | solution.py:501
  76.2 1.7 %collective-permute-done.15.refs_2_ = f32[1280,128]{1,0:T(8,128)S(1)} collective-permute-done((f32[1280,128]{1,0:T(8,128)S(1)}, f32[1280,128]{1,0:T(8,128)S(1)}, u32[]{:S(2)}, u32[]{:S(2)}) %collective-permute-start.15) | collective-permute-done | bytes 655392 | tf_op jit(solution)/shard_map/ppermute | solution.py:501
  77.9 4.5 %collective-permute-done.17.refs_5_ = f32[1280,128]{1,0:T(8,128)S(1)} collective-permute-done((f32[1280,128]{1,0:T(8,128)S(1)}, f32[1280,128]{1,0:T(8,128)S(1)}, u32[]{:S(2)}, u32[]{:S(2)}) %collective-permute-start.17) | collective-permute-done | bytes 655392 | tf_op jit(solution)/shard_map/ppermute | solution.py:501
  82.4 1.9 %shard_map.60 = (f32[128,128]{1,0:T(8,128)S(1)}, f32[128,128]{1,0:T(8,128)S(1)}, f32[1280,128]{1,0:T(8,128)S(1)}, f32[1280,128]{1,0:T(8,128)S(1)}, f32[1280,128]{1,0:T(8,128)S(1)}, /*index=5*/f32[1280,128]{1,0:T(8,128)S(1)}) custom-call(s32[16]{0:T(128)S(1)} %constant_dynamic-update-slice_fusion.f, f32[1280,128]{1,0:T(8,128)S(1)} %get-tuple-element.103.refs_0_, ...), custom_call_target="tpu_custom_call" | custom-call | tf_op jit(solution)/shard_map/pallas_call | solution.py:52
  86.0 1.9 %collective-permute-start.23 = (f32[128,128]{1,0:T(8,128)S(1)}, f32[128,128]{1,0:T(8,128)S(1)}, u32[]{:S(2)}, u32[]{:S(2)}) collective-permute-start(f32[128,128]{1,0:T(8,128)S(1)} %add.36.refs_0_), channel_id=1, source_target_pairs={{6,0},{7,1},{4,2},{5,3},{2,4},{3,5},{0,6},{1,7},{14,8},{15,9},{12,... | collective-permute-start | bytes 196616 | tf_op jit(solution)/shard_map/ppermute | solution.py:501
  89.6 1.8 %collective-permute-done.23.refs_3_ = f32[128,128]{1,0:T(8,128)S(1)} collective-permute-done((f32[128,128]{1,0:T(8,128)S(1)}, f32[128,128]{1,0:T(8,128)S(1)}, u32[]{:S(2)}, u32[]{:S(2)}) %collective-permute-start.23) | collective-permute-done | bytes 65568 | tf_op jit(solution)/shard_map/ppermute | solution.py:501
  92.7 3.0 %shard_map.62 = (f32[256,256]{1,0:T(8,128)S(1)}, f32[256,256]{1,0:T(8,128)S(1)}) custom-call(s32[16]{0:T(128)S(1)} %constant_dynamic-update-slice_fusion.f, f32[128,128]{1,0:T(8,128)S(1)} %add.36.refs_0_, f32[128,128]{1,0:T(8,128)S(1)} %collective-permute-done.21.refs_1_, f32[128,128]{1,0:T(8,128)S(1)} %collective-permute-done.22.refs_2_, ...), custom_call_target="tpu_custom_call" | custom-call | tf_op jit(solution)/shard_map/pallas_call | solution.py:52
  99.7 4.6 %collective-permute-start.26 = (f32[1280,128]{1,0:T(8,128)S(1)}, f32[1280,128]{1,0:T(8,128)S(1)}, u32[]{:S(2)}, u32[]{:S(2)}) collective-permute-start(f32[1280,128]{1,0:T(8,128)S(1)} %get-tuple-element.122.refs_2_.refs_4_), channel_id=1, source_target_pairs={{9,1},{11,3},{13,5},{15,7},{0,8},{17,9},{2,10},{19,11},{4,12},{21,... | collective-permute-start | bytes 1966088 | tf_op jit(solution)/shard_map/ppermute | solution.py:501
  104.3 1.7 %collective-permute-start.29 = (f32[1280,128]{1,0:T(8,128)S(1)}, f32[1280,128]{1,0:T(8,128)S(1)}, u32[]{:S(2)}, u32[]{:S(2)}) collective-permute-start(f32[1280,128]{1,0:T(8,128)S(1)} %get-tuple-element.131), channel_id=1, source_target_pairs={{4,0},{5,1},{6,2},{7,3},{0,4},{1,5},{2,6},{3,7},{12,8},{13,9},{14,... | collective-permute-start | bytes 1966088 | tf_op jit(solution)/shard_map/ppermute | solution.py:501
  108.3 3.0 %collective-permute-start.28 = (f32[128,128]{1,0:T(8,128)S(1)}, f32[128,128]{1,0:T(8,128)S(1)}, u32[]{:S(2)}, u32[]{:S(2)}) collective-permute-start(f32[128,128]{1,0:T(8,128)S(1)} %get-tuple-element.125), channel_id=1, source_target_pairs={{1,0},{0,1},{3,2},{2,3},{5,4},{4,5},{7,6},{6,7},{9,8},{8,9},{11,10... | collective-permute-start | bytes 196616 | tf_op jit(solution)/shard_map/ppermute | solution.py:501
  112.1 4.3 %collective-permute-done.26.refs_3_.refs_5_ = f32[1280,128]{1,0:T(8,128)S(1)} collective-permute-done((f32[1280,128]{1,0:T(8,128)S(1)}, f32[1280,128]{1,0:T(8,128)S(1)}, u32[]{:S(2)}, u32[]{:S(2)}) %collective-permute-start.26) | collective-permute-done | bytes 655392 | tf_op jit(solution)/shard_map/ppermute | solution.py:501
  118.3 1.9 %shard_map.67 = (f32[128,128]{1,0:T(8,128)S(1)}, f32[128,128]{1,0:T(8,128)S(1)}, f32[1280,128]{1,0:T(8,128)S(1)}, f32[1280,128]{1,0:T(8,128)S(1)}, f32[1280,128]{1,0:T(8,128)S(1)}, /*index=5*/f32[1280,128]{1,0:T(8,128)S(1)}) custom-call(s32[16]{0:T(128)S(1)} %constant_dynamic-update-slice_fusion.f, f32[1280,128]{1,0:T(8,128)S(1)} %get-tuple-element.120.refs_4_.refs_0_, ...), custom_call_target="tpu_custom_call" | custom-call | tf_op jit(solution)/shard_map/pallas_call | solution.py:52
  126.5 3.2 %collective-permute-done.33.refs_3_ = f32[128,128]{1,0:T(8,128)S(1)} collective-permute-done((f32[128,128]{1,0:T(8,128)S(1)}, f32[128,128]{1,0:T(8,128)S(1)}, u32[]{:S(2)}, u32[]{:S(2)}) %collective-permute-start.33) | collective-permute-done | bytes 65568 | tf_op jit(solution)/shard_map/ppermute | solution.py:501
  131.3 3.6 %shard_map.69 = (f32[264,256]{1,0:T(8,128)S(1)}, f32[256,256]{1,0:T(8,128)}) custom-call(s32[16]{0:T(128)S(1)} %constant_dynamic-update-slice_fusion.f, f32[128,128]{1,0:T(8,128)S(1)} %add.37.refs_0_, f32[128,128]{1,0:T(8,128)S(1)} %collective-permute-done.31.refs_1_, f32[128,128]{1,0:T(8,128)S(1)} %collective-permute-done.32.refs_2_, ...), custom_call_target="tpu_custom_call" | custom-call | tf_op jit(solution)/shard_map/pallas_call | solution.py:52
  136.6 3.1 %shard_map.70 = (f32[2048,256]{1,0:T(8,128)}, f32[512,256]{1,0:T(8,128)}, f32[1,256]{1,0:T(1,128)}) custom-call(s32[16]{0:T(128)S(1)} %constant_dynamic-update-slice_fusion.f, f32[264,256]{1,0:T(8,128)S(1)} %get-tuple-element.142.own_ref, f32[264,256]{1,0:T(8,128)S(1)} %collective-permute-done.35.other_ref, ...), custom_call_target="tpu_custom_call" | custom-call | flops 1 | bytes 1 | tf_op jit(solution)/shard_map/pallas_call | solution.py:400
  140.1 1.9 %shard_map.71 = (f32[2048,256]{1,0:T(8,128)}, f32[512,256]{1,0:T(8,128)}) custom-call(s32[16]{0:T(128)S(1)} %constant_dynamic-update-slice_fusion.f, f32[264,256]{1,0:T(8,128)S(1)} %get-tuple-element.142.own_ref, f32[264,256]{1,0:T(8,128)S(1)} %collective-permute-done.35.other_ref, ...), custom_call_target="tpu_custom_call", output_to_operand_aliasing={{0}: (5, {}), {1}: (6, {})} | custom-call | flops 1 | bytes 1 | tf_op jit(solution)/shard_map/pallas_call | solution.py:400
  (77 shorter events, 42.9 us)
Async XLA Ops:
  3.1 25.5 %collective-permute-start.5 = (f32[768,256]{1,0:T(8,128)}, f32[768,256]{1,0:T(8,128)S(1)}, u32[]{:S(2)}, u32[]{:S(2)}) collective-permute-start(f32[768,256]{1,0:T(8,128)} %get-tuple-element.84), channel_id=1, source_target_pairs={{4,0},{5,1},{6,2},{7,3},{0,4},{1,5},{2,6},{3,7},{12,8},{13,9},{14,... | collective-permute-start | bytes 2359304 | tf_op jit(solution)/shard_map/ppermute | solution.py:501
  9.8 7.0 %collective-permute-start.1 = (f32[384,128]{1,0:T(8,128)S(1)}, f32[384,128]{1,0:T(8,128)S(1)}, u32[]{:S(2)}, u32[]{:S(2)}) collective-permute-start(f32[384,128]{1,0:T(8,128)S(1)} %add.34.own_ref), channel_id=1, source_target_pairs={{2,0},{3,1},{0,2},{1,3},{6,4},{7,5},{4,6},{5,7},{10,8},{11,9},{8,1... | collective-permute-start | bytes 589832 | tf_op jit(solution)/shard_map/ppermute | solution.py:501
  20.3 6.9 %collective-permute-start.3 = (f32[128,256]{1,0:T(8,128)S(1)}, f32[128,256]{1,0:T(8,128)S(1)}, u32[]{:S(2)}, u32[]{:S(2)}) collective-permute-start(f32[128,256]{1,0:T(8,128)S(1)} %get-tuple-element.83), channel_id=1, source_target_pairs={{4,0},{5,1},{6,2},{7,3},{0,4},{1,5},{2,6},{3,7},{12,8},{13,9},{14,... | collective-permute-start | bytes 393224 | tf_op jit(solution)/shard_map/ppermute | solution.py:501
  21.9 25.5 %collective-permute-start.2 = (f32[1280,128]{1,0:T(8,128)S(1)}, f32[1280,128]{1,0:T(8,128)S(1)}, u32[]{:S(2)}, u32[]{:S(2)}) collective-permute-start(f32[1280,128]{1,0:T(8,128)S(1)} %get-tuple-element.82.refs_1_), channel_id=1, source_target_pairs={{8,0},{9,1},{10,2},{11,3},{16,8},{17,9},{18,10},{19,11},{4,12},{5,... | collective-permute-start | bytes 1966088 | tf_op jit(solution)/shard_map/ppermute | solution.py:501
  23.2 9.9 %collective-permute-start.7 = (f32[256,256]{1,0:T(8,128)S(1)}, f32[256,256]{1,0:T(8,128)S(1)}, u32[]{:S(2)}, u32[]{:S(2)}) collective-permute-start(f32[256,256]{1,0:T(8,128)S(1)} %copy-done.1), channel_id=1, source_target_pairs={{4,0},{5,1},{6,2},{7,3},{0,4},{1,5},{2,6},{3,7},{12,8},{13,9},{14,... | collective-permute-start | bytes 786440 | tf_op jit(solution)/shard_map/ppermute | solution.py:501
  29.6 17.7 %collective-permute-start.6 = (f32[768,128]{1,0:T(8,128)S(1)}, f32[768,128]{1,0:T(8,128)S(1)}, u32[]{:S(2)}, u32[]{:S(2)}) collective-permute-start(f32[768,128]{1,0:T(8,128)S(1)} %get-tuple-element.86.refs_4_), channel_id=1, source_target_pairs={{12,4},{13,5},{14,6},{15,7},{0,8},{1,9},{2,10},{3,11},{20,12},{21,... | collective-permute-start | bytes 1179656 | tf_op jit(solution)/shard_map/ppermute | solution.py:501
  34.1 13.3 %collective-permute-start.8 = (f32[512,128]{1,0:T(8,128)S(1)}, f32[512,128]{1,0:T(8,128)S(1)}, u32[]{:S(2)}, u32[]{:S(2)}) collective-permute-start(f32[512,128]{1,0:T(8,128)S(1)} %get-tuple-element.89.refs_7_), channel_id=1, source_target_pairs={{12,4},{13,5},{14,6},{15,7},{0,8},{1,9},{2,10},{3,11},{20,12},{21,... | collective-permute-start | bytes 786440 | tf_op jit(solution)/shard_map/ppermute | solution.py:501
  39.2 10.0 %collective-permute-start.9 = (f32[128,128]{1,0:T(8,128)S(1)}, f32[128,128]{1,0:T(8,128)S(1)}, u32[]{:S(2)}, u32[]{:S(2)}) collective-permute-start(f32[128,128]{1,0:T(8,128)S(1)} %get-tuple-element.93), channel_id=1, source_target_pairs={{0,0},{8,1},{2,2},{10,3},{1,4},{9,5},{3,6},{11,7},{4,8},{16,9},{6,... | collective-permute-start | bytes 196616 | tf_op jit(solution)/shard_map/ppermute | solution.py:501
  39.8 9.4 %collective-permute-start.10 = (f32[128,128]{1,0:T(8,128)S(1)}, f32[128,128]{1,0:T(8,128)S(1)}, u32[]{:S(2)}, u32[]{:S(2)}) collective-permute-start(f32[128,128]{1,0:T(8,128)S(1)} %get-tuple-element.94), channel_id=1, source_target_pairs={{4,0},{0,1},{6,2},{2,3},{5,4},{1,5},{7,6},{3,7},{12,8},{8,9},{14,1... | collective-permute-start | bytes 196616 | tf_op jit(solution)/shard_map/ppermute | solution.py:501
  50.6 5.6 %collective-permute-start.14 = (f32[128,128]{1,0:T(8,128)S(1)}, f32[128,128]{1,0:T(8,128)S(1)}, u32[]{:S(2)}, u32[]{:S(2)}) collective-permute-start(f32[128,128]{1,0:T(8,128)S(1)} %add.35.refs_0_), channel_id=1, source_target_pairs={{6,0},{7,1},{4,2},{5,3},{2,4},{3,5},{0,6},{1,7},{14,8},{15,9},{12,... | collective-permute-start | bytes 196616 | tf_op jit(solution)/shard_map/ppermute | solution.py:501
  53.7 4.3 %collective-permute-start.13 = (f32[128,128]{1,0:T(8,128)S(1)}, f32[128,128]{1,0:T(8,128)S(1)}, u32[]{:S(2)}, u32[]{:S(2)}) collective-permute-start(f32[128,128]{1,0:T(8,128)S(1)} %add.35.refs_0_), channel_id=1, source_target_pairs={{4,0},{5,1},{6,2},{7,3},{0,4},{1,5},{2,6},{3,7},{12,8},{13,9},{14,... | collective-permute-start | bytes 196616 | tf_op jit(solution)/shard_map/ppermute | solution.py:501
  53.7 4.3 %collective-permute-start.12 = (f32[128,128]{1,0:T(8,128)S(1)}, f32[128,128]{1,0:T(8,128)S(1)}, u32[]{:S(2)}, u32[]{:S(2)}) collective-permute-start(f32[128,128]{1,0:T(8,128)S(1)} %add.35.refs_0_), channel_id=1, source_target_pairs={{2,0},{3,1},{0,2},{1,3},{6,4},{7,5},{4,6},{5,7},{10,8},{11,9},{8,1... | collective-permute-start | bytes 196616 | tf_op jit(solution)/shard_map/ppermute | solution.py:501
  61.4 2.8 %collective-permute-start.16 = (f32[256,256]{1,0:T(8,128)S(1)}, f32[256,256]{1,0:T(8,128)S(1)}, u32[]{:S(2)}, u32[]{:S(2)}) collective-permute-start(f32[256,256]{1,0:T(8,128)S(1)} %get-tuple-element.98.rotation_ref), channel_id=1, source_target_pairs={{1,0},{0,1},{3,2},{2,3},{5,4},{4,5},{7,6},{6,7},{9,8},{8,9},{11,10... | collective-permute-start | bytes 786440 | tf_op jit(solution)/shard_map/ppermute | solution.py:501
  62.8 15.1 %collective-permute-start.15 = (f32[1280,128]{1,0:T(8,128)S(1)}, f32[1280,128]{1,0:T(8,128)S(1)}, u32[]{:S(2)}, u32[]{:S(2)}) collective-permute-start(f32[1280,128]{1,0:T(8,128)S(1)} %get-tuple-element.104.refs_1_), channel_id=1, source_target_pairs={{8,0},{10,2},{12,4},{14,6},{16,8},{1,9},{18,10},{3,11},{20,12},{5,... | collective-permute-start | bytes 1966088 | tf_op jit(solution)/shard_map/ppermute | solution.py:501
  65.5 16.9 %collective-permute-start.17 = (f32[1280,128]{1,0:T(8,128)S(1)}, f32[1280,128]{1,0:T(8,128)S(1)}, u32[]{:S(2)}, u32[]{:S(2)}) collective-permute-start(f32[1280,128]{1,0:T(8,128)S(1)} %get-tuple-element.106.refs_4_), channel_id=1, source_target_pairs={{9,1},{11,3},{13,5},{15,7},{0,8},{17,9},{2,10},{19,11},{4,12},{21,... | collective-permute-start | bytes 1966088 | tf_op jit(solution)/shard_map/ppermute | solution.py:501
  72.1 12.1 %collective-permute-start.18 = (f32[128,128]{1,0:T(8,128)S(1)}, f32[128,128]{1,0:T(8,128)S(1)}, u32[]{:S(2)}, u32[]{:S(2)}) collective-permute-start(f32[128,128]{1,0:T(8,128)S(1)} %get-tuple-element.110), channel_id=1, source_target_pairs={{0,0},{8,1},{2,2},{10,3},{4,4},{12,5},{6,6},{14,7},{1,8},{16,9},{3... | collective-permute-start | bytes 196616 | tf_op jit(solution)/shard_map/ppermute | solution.py:501
  72.8 11.5 %collective-permute-start.19 = (f32[128,128]{1,0:T(8,128)S(1)}, f32[128,128]{1,0:T(8,128)S(1)}, u32[]{:S(2)}, u32[]{:S(2)}) collective-permute-start(f32[128,128]{1,0:T(8,128)S(1)} %get-tuple-element.111), channel_id=1, source_target_pairs={{1,0},{0,1},{3,2},{2,3},{5,4},{4,5},{7,6},{6,7},{9,8},{8,9},{11,10... | collective-permute-start | bytes 196616 | tf_op jit(solution)/shard_map/ppermute | solution.py:501
  86.0 5.4 %collective-permute-start.23 = (f32[128,128]{1,0:T(8,128)S(1)}, f32[128,128]{1,0:T(8,128)S(1)}, u32[]{:S(2)}, u32[]{:S(2)}) collective-permute-start(f32[128,128]{1,0:T(8,128)S(1)} %add.36.refs_0_), channel_id=1, source_target_pairs={{6,0},{7,1},{4,2},{5,3},{2,4},{3,5},{0,6},{1,7},{14,8},{15,9},{12,... | collective-permute-start | bytes 196616 | tf_op jit(solution)/shard_map/ppermute | solution.py:501
  87.9 4.3 %collective-permute-start.22 = (f32[128,128]{1,0:T(8,128)S(1)}, f32[128,128]{1,0:T(8,128)S(1)}, u32[]{:S(2)}, u32[]{:S(2)}) collective-permute-start(f32[128,128]{1,0:T(8,128)S(1)} %add.36.refs_0_), channel_id=1, source_target_pairs={{4,0},{5,1},{6,2},{7,3},{0,4},{1,5},{2,6},{3,7},{12,8},{13,9},{14,... | collective-permute-start | bytes 196616 | tf_op jit(solution)/shard_map/ppermute | solution.py:501
  88.3 4.5 %collective-permute-start.21 = (f32[128,128]{1,0:T(8,128)S(1)}, f32[128,128]{1,0:T(8,128)S(1)}, u32[]{:S(2)}, u32[]{:S(2)}) collective-permute-start(f32[128,128]{1,0:T(8,128)S(1)} %add.36.refs_0_), channel_id=1, source_target_pairs={{2,0},{3,1},{0,2},{1,3},{6,4},{7,5},{4,6},{5,7},{10,8},{11,9},{8,1... | collective-permute-start | bytes 196616 | tf_op jit(solution)/shard_map/ppermute | solution.py:501
  95.8 2.6 %collective-permute-start.25 = (f32[256,256]{1,0:T(8,128)S(1)}, f32[256,256]{1,0:T(8,128)S(1)}, u32[]{:S(2)}, u32[]{:S(2)}) collective-permute-start(f32[256,256]{1,0:T(8,128)S(1)} %get-tuple-element.115.rotation_ref), channel_id=1, source_target_pairs={{1,0},{0,1},{3,2},{2,3},{5,4},{4,5},{7,6},{6,7},{9,8},{8,9},{11,10... | collective-permute-start | bytes 786440 | tf_op jit(solution)/shard_map/ppermute | solution.py:501
  97.1 14.9 %collective-permute-start.24 = (f32[1280,128]{1,0:T(8,128)S(1)}, f32[1280,128]{1,0:T(8,128)S(1)}, u32[]{:S(2)}, u32[]{:S(2)}) collective-permute-start(f32[1280,128]{1,0:T(8,128)S(1)} %get-tuple-element.121.refs_0_.refs_1_), channel_id=1, source_target_pairs={{8,0},{10,2},{12,4},{14,6},{16,8},{1,9},{18,10},{3,11},{20,12},{5,... | collective-permute-start | bytes 1966088 | tf_op jit(solution)/shard_map/ppermute | solution.py:501
  99.7 16.7 %collective-permute-start.26 = (f32[1280,128]{1,0:T(8,128)S(1)}, f32[1280,128]{1,0:T(8,128)S(1)}, u32[]{:S(2)}, u32[]{:S(2)}) collective-permute-start(f32[1280,128]{1,0:T(8,128)S(1)} %get-tuple-element.122.refs_2_.refs_4_), channel_id=1, source_target_pairs={{9,1},{11,3},{13,5},{15,7},{0,8},{17,9},{2,10},{19,11},{4,12},{21,... | collective-permute-start | bytes 1966088 | tf_op jit(solution)/shard_map/ppermute | solution.py:501
  104.3 16.3 %collective-permute-start.29 = (f32[1280,128]{1,0:T(8,128)S(1)}, f32[1280,128]{1,0:T(8,128)S(1)}, u32[]{:S(2)}, u32[]{:S(2)}) collective-permute-start(f32[1280,128]{1,0:T(8,128)S(1)} %get-tuple-element.131), channel_id=1, source_target_pairs={{4,0},{5,1},{6,2},{7,3},{0,4},{1,5},{2,6},{3,7},{12,8},{13,9},{14,... | collective-permute-start | bytes 1966088 | tf_op jit(solution)/shard_map/ppermute | solution.py:501
  107.7 9.3 %collective-permute-start.27 = (f32[128,128]{1,0:T(8,128)S(1)}, f32[128,128]{1,0:T(8,128)S(1)}, u32[]{:S(2)}, u32[]{:S(2)}) collective-permute-start(f32[128,128]{1,0:T(8,128)S(1)} %get-tuple-element.124), channel_id=1, source_target_pairs={{0,0},{8,1},{2,2},{10,3},{4,4},{12,5},{6,6},{14,7},{1,8},{16,9},{3... | collective-permute-start | bytes 196616 | tf_op jit(solution)/shard_map/ppermute | solution.py:501
  108.3 8.6 %collective-permute-start.28 = (f32[128,128]{1,0:T(8,128)S(1)}, f32[128,128]{1,0:T(8,128)S(1)}, u32[]{:S(2)}, u32[]{:S(2)}) collective-permute-start(f32[128,128]{1,0:T(8,128)S(1)} %get-tuple-element.125), channel_id=1, source_target_pairs={{1,0},{0,1},{3,2},{2,3},{5,4},{4,5},{7,6},{6,7},{9,8},{8,9},{11,10... | collective-permute-start | bytes 196616 | tf_op jit(solution)/shard_map/ppermute | solution.py:501
  117.0 13.4 %collective-permute-start.34 = (f32[640,128]{1,0:T(8,128)S(1)}, f32[640,128]{1,0:T(8,128)S(1)}, u32[]{:S(2)}, u32[]{:S(2)}) collective-permute-start(f32[640,128]{1,0:T(8,128)S(1)} %shard_map.65), channel_id=1, source_target_pairs={{4,0},{5,1},{6,2},{7,3},{0,4},{1,5},{2,6},{3,7},{12,8},{13,9},{14,... | collective-permute-start | bytes 983048 | tf_op jit(solution)/shard_map/ppermute | solution.py:501
  120.6 1.8 %collective-permute-start.30 = (f32[128,128]{1,0:T(8,128)S(1)}, f32[128,128]{1,0:T(8,128)S(1)}, u32[]{:S(2)}, u32[]{:S(2)}) collective-permute-start(f32[128,128]{1,0:T(8,128)S(1)} %get-tuple-element.132), channel_id=1, source_target_pairs={{1,0},{0,1},{3,2},{2,3},{5,4},{4,5},{7,6},{6,7},{9,8},{8,9},{11,10... | collective-permute-start | bytes 196616 | tf_op jit(solution)/shard_map/ppermute | solution.py:501
  122.4 7.3 %collective-permute-start.33 = (f32[128,128]{1,0:T(8,128)S(1)}, f32[128,128]{1,0:T(8,128)S(1)}, u32[]{:S(2)}, u32[]{:S(2)}) collective-permute-start(f32[128,128]{1,0:T(8,128)S(1)} %add.37.refs_0_), channel_id=1, source_target_pairs={{6,0},{7,1},{4,2},{5,3},{2,4},{3,5},{0,6},{1,7},{14,8},{15,9},{12,... | collective-permute-start | bytes 196616 | tf_op jit(solution)/shard_map/ppermute | solution.py:501
  123.7 6.6 %collective-permute-start.32 = (f32[128,128]{1,0:T(8,128)S(1)}, f32[128,128]{1,0:T(8,128)S(1)}, u32[]{:S(2)}, u32[]{:S(2)}) collective-permute-start(f32[128,128]{1,0:T(8,128)S(1)} %add.37.refs_0_), channel_id=1, source_target_pairs={{4,0},{5,1},{6,2},{7,3},{0,4},{1,5},{2,6},{3,7},{12,8},{13,9},{14,... | collective-permute-start | bytes 196616 | tf_op jit(solution)/shard_map/ppermute | solution.py:501
  125.0 5.4 %collective-permute-start.31 = (f32[128,128]{1,0:T(8,128)S(1)}, f32[128,128]{1,0:T(8,128)S(1)}, u32[]{:S(2)}, u32[]{:S(2)}) collective-permute-start(f32[128,128]{1,0:T(8,128)S(1)} %add.37.refs_0_), channel_id=1, source_target_pairs={{2,0},{3,1},{0,2},{1,3},{6,4},{7,5},{4,6},{5,7},{10,8},{11,9},{8,1... | collective-permute-start | bytes 196616 | tf_op jit(solution)/shard_map/ppermute | solution.py:501
  130.4 9.7 %collective-permute-start.36 = (f32[640,128]{1,0:T(8,128)S(1)}, f32[640,128]{1,0:T(8,128)S(1)}, u32[]{:S(2)}, u32[]{:S(2)}) collective-permute-start(f32[640,128]{1,0:T(8,128)S(1)} %shard_map.68), channel_id=1, source_target_pairs={{4,0},{5,1},{6,2},{7,3},{0,4},{1,5},{2,6},{3,7},{12,8},{13,9},{14,... | collective-permute-start | bytes 983048 | tf_op jit(solution)/shard_map/ppermute | solution.py:501
  (8 other events, 38.7 us)

commit v16 on v15

--- a/solution.py
+++ b/solution.py
@@ -42,6 +42,19 @@
         a, b, (((0,), (0,)), ((), ())), precision=highest,
         preferred_element_type=jnp.float32,
     )
+
+
+def dot3_tn(a, b):
+    def product(left, right):
+        return lax.dot_general(
+            left, right, (((0,), (0,)), ((), ())),
+            preferred_element_type=jnp.float32,
+        )
+
+    a_high, a_low = split(a)
+    b_high, b_low = split(b)
+    small = product(a_high, b_low) + product(a_low, b_high)
+    return product(a_high, b_high) + small
 
 
 def shape(*dims):
@@ -65,7 +78,7 @@
 def first_gram(sector, half):
     def body(x_ref, out_ref):
         x = x_ref[...]
-        g = dot_tn(x, x)
+        g = dot3_tn(x, x)
         out_ref[:half] = g[:half, :half]
         out_ref[half : 2 * half] = g[:half, half:]
         out_ref[2 * half :] = g[half:, half:]
@@ -156,13 +169,17 @@
     return 2.0 * x_ref[...] - identity
 
 
-def put_rotation(rotation_ref, gram, x_ref, e_ref, last_round):
+def squares_of(facts, gram, rotation):
     size = gram.shape[0]
-    rotation = rotate_of(gram, x_ref, e_ref)
-    rotation_ref[:size] = rotation
-    if last_round:
-        squares = jnp.sum(rotation * dot(gram, rotation), axis=0, keepdims=True)
-        rotation_ref[size:] = jnp.broadcast_to(squares, (8, size))
+
+    def body(f, gram_ref, rotation_ref, out_ref):
+        rotation = rotation_ref[...]
+        squares = rotation * dot(gram_ref[...], rotation)
+        out_ref[...] = jnp.broadcast_to(
+            jnp.sum(squares, axis=0, keepdims=True), (8, size)
+        )
+
+    return call(body, facts, [gram, rotation], shape(8, size))
 
 
 def first_rotation(facts, own, other_y, half):
@@ -174,7 +191,7 @@
         g_ref[:half, half:] = total[half : 2 * half]
         g_ref[half:, :half] = total[half : 2 * half].T
         g_ref[half:, half:] = total[2 * half :]
-        put_rotation(rotation_ref, g_ref[...], x_ref, e_ref, False)
+        rotation_ref[...] = rotate_of(g_ref[...], x_ref, e_ref)
         rotation = rotation_ref[...]
         half_ref[...] = jnp.where(f[CORE] == 0, rotation[:half], rotation[half:])
 
@@ -183,7 +200,7 @@
     return call(body, facts, [own, other_y], outs, [square] * 2)
 
 
-def later_rotation(facts, parts, diagonals, half, last_round):
+def later_rotation(facts, parts, diagonals, half):
     size = 2 * half
 
     def body(f, *refs):
@@ -195,14 +212,14 @@
         g_ref[:half, half:] = cross
         g_ref[half:, :half] = cross.T
         g_ref[half:, half:] = jnp.where(core, native, foreign)
-        put_rotation(rotation_ref, g_ref[...], x_ref, e_ref, last_round)
+        rotation_ref[...] = rotate_of(g_ref[...], x_ref, e_ref)
 
     square = pltpu.VMEM((size, size), jnp.float32)
     return call(
         body,
         facts,
         parts + diagonals,
-        (shape(size + 8 if last_round else size, size), shape(size, size)),
+        (shape(size, size),) * 2,
         [square] * 2,
     )
 
@@ -337,8 +354,8 @@
         put_cross(
             f,
             refs[3 + 3 * pieces :],
-            dot_tn(up_0[:part], low_0[:part]),
-            dot_tn(up_1[:part], low_1[:part]),
+            dot3_tn(up_0[:part], low_0[:part]),
+            dot3_tn(up_1[:part], low_1[:part]),
         )
 
     outs = (shape(half, half),) * 2 + (shape(rows, half),) * 4
@@ -372,9 +389,9 @@
     )
 
 
-def final_turn(f, own_ref, other_ref, size):
-    pack = jnp.where(f[CORE] == f[X], own_ref[...], other_ref[...])
-    return split(swapped(f[X] == 1, pack[:size], 0)), pack[size : size + 1]
+def final_turn(f, own_ref, other_ref):
+    rotation = jnp.where(f[CORE] == f[X], own_ref[...], other_ref[...])
+    return split(swapped(f[X] == 1, rotation, 0))
 
 
 def final_product(moved, native, turned):
@@ -422,10 +439,8 @@
 
     def body(f, own_ref, other_ref, *refs):
         x = f[X]
-        turned, squares = final_turn(f, own_ref, other_ref, size)
-        native_ref, top_ref, out_ref, vectors_ref, singular_ref, out, vectors, sems = (
-            refs[4:]
-        )
+        turned = final_turn(f, own_ref, other_ref)
+        native_ref, top_ref, out_ref, vectors_ref, out, vectors, sems = refs[4:]
         copies = []
 
         def kept(rows):
@@ -445,18 +460,17 @@
         value = final_product(top_ref[...], native_ref[:top], turned)
         put(out, out_ref, part, (1 - x) * part, value)
         put(vectors, vectors_ref, 0, x * vector_rows, kept(slice(part, None)))
-        singular_ref[...] = jnp.sqrt(jnp.maximum(squares, 0.0) + 1e-06)
         for copy in copies:
             copy.wait()
 
-    outs = (shape(2 * part, size), shape(2 * vector_rows, size), shape(1, size))
+    outs = (shape(2 * part, size), shape(2 * vector_rows, size))
     inputs = packs + blocks + [native, got_top]
     return finish_call(
         body, facts, inputs, [], outs, part + top, vector_rows, size
     )
 
 
-def finish_rest(facts, packs, outputs, native, got_rest, part, half):
+def finish_rest(facts, packs, squares, outputs, native, got_rest, part, half):
     size = 2 * half
     vector_rows = native.shape[0] - part
     rest = got_rest.shape[0] - vector_rows
@@ -464,8 +478,10 @@
 
     def body(f, own_ref, other_ref, native_ref, rest_ref, *refs):
         x = f[X]
-        turned, _ = final_turn(f, own_ref, other_ref, size)
-        out_ref, vectors_ref, out, vectors, sems = refs[2:]
+        turned = final_turn(f, own_ref, other_ref)
+        total = jnp.where(f[CORE] == x, refs[0][:1], refs[1][:1])
+        out_ref, vectors_ref, singular_ref, out, vectors, sems = refs[4:]
+        singular_ref[...] = jnp.sqrt(jnp.maximum(total, 0.0) + 1e-06)
         copies = []
         value = final_product(rest_ref[:rest], native_ref[top:part], turned)
         put_rows(copies, sems, out, out_ref, 0, (1 - x) * part + top, value)
@@ -474,8 +490,8 @@
         for copy in copies:
             copy.wait()
 
-    outs = (shape(2 * part, size), shape(2 * vector_rows, size))
-    inputs = packs + [native, got_rest]
+    outs = (shape(2 * part, size), shape(2 * vector_rows, size), shape(1, size))
+    inputs = packs + [native, got_rest] + squares
     return finish_call(
         body, facts, inputs, outputs, outs, rest, vector_rows, size
     )
@@ -618,13 +634,13 @@
             rest_give = give(facts, blocks, top, part + vector_rows, half)
             *parts, got_top, rest_give = together(*parts, got_top, rest_give)
             got_rest = exchange(rest_give, 1, 0)
-        rotation, gram = later_rotation(facts, parts, diagonals, half, last_move)
+        rotation, gram = later_rotation(facts, parts, diagonals, half)
     packs = [rotation, exchange(rotation, 0, 1)]
-    *outputs, singular = finish_kept(
-        facts, packs, blocks, native, got_top, part, half
-    )
-    rotated, vectors_out = finish_rest(
-        facts, packs, outputs, native, got_rest, part, half
+    squares = squares_of(facts, gram, rotation)
+    squares = [squares, exchange(squares, 0, 1)]
+    outputs = list(finish_kept(facts, packs, blocks, native, got_top, part, half))
+    rotated, vectors_out, singular = finish_rest(
+        facts, packs, squares, outputs, native, got_rest, part, half
     )
     return rotated, vectors_out, singular.reshape(size)
 

time: 143 us -> 143 us (level)
  Pallas kernels: 43 us -> 41 us
  waiting for transfers between devices: 42.1 us -> 44.1 us
    ppermute x37 -> x38, waiting for transfers between devices: 42.1 us -> 44.1 us  [permute(): return lax.ppermute(block, ('pair', 'row'), moves)]
    pallas_call x19 -> x20, Pallas kernels: 33.4 us -> 32.5 us  [call(): pl.pallas_call(body, out_shape=outs, in_specs=[pl.BlockSpec(memory_space=...]
    ppermute x37 -> x38, starting transfers between devices: 55.6 us -> 56.3 us  [permute(): return lax.ppermute(block, ('pair', 'row'), moves)]
  transfers between devices with their start and end apart: 37 -> 38, of which waited for: 21 -> 21; matrix products, arithmetic and copies ran while one was open for 0% -> 0% of each run, Pallas kernels for 23% -> 21%
where the time goes in v16:
time: 143 us
  starting transfers between devices  56.3 us (39%)
  waiting for transfers between devices  44.1 us (31%)
  Pallas kernels  41 us (29%)
    ppermute x38, starting transfers between devices, permute(): return lax.ppermute(block, ('pair', 'row'), moves)  56.3 us
    ppermute x38, waiting for transfers between devices, permute(): return lax.ppermute(block, ('pair', 'row'), moves)  44.1 us
    pallas_call x20, Pallas kernels, call(): pl.pallas_call(body, out_shape=outs, in_specs=[pl.BlockSpec(memory_space=...  32.5 us
    pallas_call x2, Pallas kernels, finish_call(): pl.pallas_call(body, out_shape=outs, in_specs=[pl.BlockSpec(memory_space=...  4.97 us
  transfers between devices with their start and end apart: 38, of which 21 were waited for; matrix products, arithmetic and copies ran while one was open for 0% of the time, Pallas kernels for 21%

profile of v16, /device:TPU:0, one launch (start us, length us, event | category | flops | bytes accessed | tf_op | source)
XLA Modules:
  0.0 142.9 jit_solution(14113497048604947682)
XLA Ops:
  0.6 2.5 %shard_map.52 = (f32[768,256]{1,0:T(8,128)}, f32[256,256]{1,0:T(8,128)}) custom-call(f32[2048,256]{1,0:T(8,128)} %x_ref.3), custom_call_target="tpu_custom_call" | custom-call | tf_op jit(solution)/shard_map/pallas_call | solution.py:117
  3.1 3.0 %collective-permute-start.5 = (f32[768,256]{1,0:T(8,128)}, f32[768,256]{1,0:T(8,128)S(1)}, u32[]{:S(2)}, u32[]{:S(2)}) collective-permute-start(f32[768,256]{1,0:T(8,128)} %get-tuple-element.85), channel_id=1, source_target_pairs={{4,0},{5,1},{6,2},{7,3},{0,4},{1,5},{2,6},{3,7},{12,8},{13,9},{14,... | collective-permute-start | bytes 2359304 | tf_op jit(solution)/shard_map/ppermute | solution.py:517
  8.7 1.6 %collective-permute-start.1 = (f32[384,128]{1,0:T(8,128)S(1)}, f32[384,128]{1,0:T(8,128)S(1)}, u32[]{:S(2)}, u32[]{:S(2)}) collective-permute-start(f32[384,128]{1,0:T(8,128)S(1)} %add.34.own_ref), channel_id=1, source_target_pairs={{2,0},{3,1},{0,2},{1,3},{6,4},{7,5},{4,6},{5,7},{10,8},{11,9},{8,1... | collective-permute-start | bytes 589832 | tf_op jit(solution)/shard_map/ppermute | solution.py:517
  10.5 5.3 %collective-permute-done.1.other_ref = f32[384,128]{1,0:T(8,128)S(1)} collective-permute-done((f32[384,128]{1,0:T(8,128)S(1)}, f32[384,128]{1,0:T(8,128)S(1)}, u32[]{:S(2)}, u32[]{:S(2)}) %collective-permute-start.1) | collective-permute-done | bytes 196640 | tf_op jit(solution)/shard_map/ppermute | solution.py:517
  15.7 3.4 %shard_map.50 = (f32[256,256]{1,0:T(8,128)S(1)}, f32[256,256]{1,0:T(8,128)S(1)}, f32[128,256]{1,0:T(8,128)S(1)}) custom-call(s32[16]{0:T(128)S(1)} %constant_dynamic-update-slice_fusion.f, f32[384,128]{1,0:T(8,128)S(1)} %add.34.own_ref, f32[384,128]{1,0:T(8,128)S(1)} %collective-permute-done.1.other_ref), custom_call_target="tpu_custom_call" | custom-call | tf_op jit(solution)/shard_map/pallas_call | solution.py:65
  22.1 4.0 %collective-permute-start.7 = (f32[256,256]{1,0:T(8,128)S(1)}, f32[256,256]{1,0:T(8,128)S(1)}, u32[]{:S(2)}, u32[]{:S(2)}) collective-permute-start(f32[256,256]{1,0:T(8,128)S(1)} %copy-done.1), channel_id=1, source_target_pairs={{4,0},{5,1},{6,2},{7,3},{0,4},{1,5},{2,6},{3,7},{12,8},{13,9},{14,... | collective-permute-start | bytes 786440 | tf_op jit(solution)/shard_map/ppermute | solution.py:517
  29.9 4.1 %collective-permute-start.6 = (f32[768,128]{1,0:T(8,128)S(1)}, f32[768,128]{1,0:T(8,128)S(1)}, u32[]{:S(2)}, u32[]{:S(2)}) collective-permute-start(f32[768,128]{1,0:T(8,128)S(1)} %get-tuple-element.87.refs_4_), channel_id=1, source_target_pairs={{12,4},{13,5},{14,6},{15,7},{0,8},{1,9},{2,10},{3,11},{20,12},{21,... | collective-permute-start | bytes 1179656 | tf_op jit(solution)/shard_map/ppermute | solution.py:517
  35.0 3.5 %collective-permute-start.8 = (f32[512,128]{1,0:T(8,128)S(1)}, f32[512,128]{1,0:T(8,128)S(1)}, u32[]{:S(2)}, u32[]{:S(2)}) collective-permute-start(f32[512,128]{1,0:T(8,128)S(1)} %get-tuple-element.90.refs_7_), channel_id=1, source_target_pairs={{12,4},{13,5},{14,6},{15,7},{0,8},{1,9},{2,10},{3,11},{20,12},{21,... | collective-permute-start | bytes 786440 | tf_op jit(solution)/shard_map/ppermute | solution.py:517
  38.4 1.6 %shard_map.56 = (f32[128,128]{1,0:T(8,128)S(1)}, f32[128,128]{1,0:T(8,128)S(1)}) custom-call(s32[16]{0:T(128)S(1)} %constant_dynamic-update-slice_fusion.f, f32[256,256]{1,0:T(8,128)S(1)} %get-tuple-element.93.gram_ref, f32[256,256]{1,0:T(8,128)S(1)} %get-tuple-element.79.refs_0_.rotation_ref), custom_call_target="tpu_custom_call" | custom-call | tf_op jit(solution)/shard_map/pallas_call | solution.py:65
  41.6 6.6 %collective-permute-done.8.refs_8_ = f32[512,128]{1,0:T(8,128)S(1)} collective-permute-done((f32[512,128]{1,0:T(8,128)S(1)}, f32[512,128]{1,0:T(8,128)S(1)}, u32[]{:S(2)}, u32[]{:S(2)}) %collective-permute-start.8) | collective-permute-done | bytes 262176 | tf_op jit(solution)/shard_map/ppermute | solution.py:517
  51.0 3.2 %collective-permute-start.14 = (f32[128,128]{1,0:T(8,128)S(1)}, f32[128,128]{1,0:T(8,128)S(1)}, u32[]{:S(2)}, u32[]{:S(2)}) collective-permute-start(f32[128,128]{1,0:T(8,128)S(1)} %add.35.refs_0_), channel_id=1, source_target_pairs={{6,0},{7,1},{4,2},{5,3},{2,4},{3,5},{0,6},{1,7},{14,8},{15,9},{12,... | collective-permute-start | bytes 196616 | tf_op jit(solution)/shard_map/ppermute | solution.py:517
  54.8 1.8 %collective-permute-done.14.refs_3_ = f32[128,128]{1,0:T(8,128)S(1)} collective-permute-done((f32[128,128]{1,0:T(8,128)S(1)}, f32[128,128]{1,0:T(8,128)S(1)}, u32[]{:S(2)}, u32[]{:S(2)}) %collective-permute-start.14) | collective-permute-done | bytes 65568 | tf_op jit(solution)/shard_map/ppermute | solution.py:517
  56.6 1.8 %collective-permute-done.13.refs_2_ = f32[128,128]{1,0:T(8,128)S(1)} collective-permute-done((f32[128,128]{1,0:T(8,128)S(1)}, f32[128,128]{1,0:T(8,128)S(1)}, u32[]{:S(2)}, u32[]{:S(2)}) %collective-permute-start.13) | collective-permute-done | bytes 65568 | tf_op jit(solution)/shard_map/ppermute | solution.py:517
  58.5 3.4 %shard_map.57 = (f32[256,256]{1,0:T(8,128)S(1)}, f32[256,256]{1,0:T(8,128)S(1)}) custom-call(s32[16]{0:T(128)S(1)} %constant_dynamic-update-slice_fusion.f, f32[128,128]{1,0:T(8,128)S(1)} %add.35.refs_0_, f32[128,128]{1,0:T(8,128)S(1)} %collective-permute-done.12.refs_1_, f32[128,128]{1,0:T(8,128)S(1)} %collective-permute-done.13.refs_2_, ...), custom_call_target="tpu_custom_call" | custom-call | tf_op jit(solution)/shard_map/pallas_call | solution.py:65
  65.8 4.9 %collective-permute-start.17 = (f32[1280,128]{1,0:T(8,128)S(1)}, f32[1280,128]{1,0:T(8,128)S(1)}, u32[]{:S(2)}, u32[]{:S(2)}) collective-permute-start(f32[1280,128]{1,0:T(8,128)S(1)} %get-tuple-element.107.refs_4_), channel_id=1, source_target_pairs={{9,1},{11,3},{13,5},{15,7},{0,8},{17,9},{2,10},{19,11},{4,12},{21,... | collective-permute-start | bytes 1966088 | tf_op jit(solution)/shard_map/ppermute | solution.py:517
  70.7 1.6 %shard_map.61 = (f32[128,128]{1,0:T(8,128)S(1)}, f32[128,128]{1,0:T(8,128)S(1)}) custom-call(s32[16]{0:T(128)S(1)} %constant_dynamic-update-slice_fusion.f, f32[256,256]{1,0:T(8,128)S(1)} %get-tuple-element.110.gram_ref, f32[256,256]{1,0:T(8,128)S(1)} %get-tuple-element.99.rotation_ref), custom_call_target="tpu_custom_call" | custom-call | tf_op jit(solution)/shard_map/pallas_call | solution.py:65
  73.1 3.4 %collective-permute-start.19 = (f32[128,128]{1,0:T(8,128)S(1)}, f32[128,128]{1,0:T(8,128)S(1)}, u32[]{:S(2)}, u32[]{:S(2)}) collective-permute-start(f32[128,128]{1,0:T(8,128)S(1)} %get-tuple-element.112), channel_id=1, source_target_pairs={{1,0},{0,1},{3,2},{2,3},{5,4},{4,5},{7,6},{6,7},{9,8},{8,9},{11,10... | collective-permute-start | bytes 196616 | tf_op jit(solution)/shard_map/ppermute | solution.py:517
  76.5 2.1 %collective-permute-done.15.refs_2_ = f32[1280,128]{1,0:T(8,128)S(1)} collective-permute-done((f32[1280,128]{1,0:T(8,128)S(1)}, f32[1280,128]{1,0:T(8,128)S(1)}, u32[]{:S(2)}, u32[]{:S(2)}) %collective-permute-start.15) | collective-permute-done | bytes 655392 | tf_op jit(solution)/shard_map/ppermute | solution.py:517
  78.5 4.3 %collective-permute-done.17.refs_5_ = f32[1280,128]{1,0:T(8,128)S(1)} collective-permute-done((f32[1280,128]{1,0:T(8,128)S(1)}, f32[1280,128]{1,0:T(8,128)S(1)}, u32[]{:S(2)}, u32[]{:S(2)}) %collective-permute-start.17) | collective-permute-done | bytes 655392 | tf_op jit(solution)/shard_map/ppermute | solution.py:517
  86.2 1.9 %collective-permute-start.23 = (f32[128,128]{1,0:T(8,128)S(1)}, f32[128,128]{1,0:T(8,128)S(1)}, u32[]{:S(2)}, u32[]{:S(2)}) collective-permute-start(f32[128,128]{1,0:T(8,128)S(1)} %add.36.refs_0_), channel_id=1, source_target_pairs={{6,0},{7,1},{4,2},{5,3},{2,4},{3,5},{0,6},{1,7},{14,8},{15,9},{12,... | collective-permute-start | bytes 196616 | tf_op jit(solution)/shard_map/ppermute | solution.py:517
  89.7 1.8 %collective-permute-done.23.refs_3_ = f32[128,128]{1,0:T(8,128)S(1)} collective-permute-done((f32[128,128]{1,0:T(8,128)S(1)}, f32[128,128]{1,0:T(8,128)S(1)}, u32[]{:S(2)}, u32[]{:S(2)}) %collective-permute-start.23) | collective-permute-done | bytes 65568 | tf_op jit(solution)/shard_map/ppermute | solution.py:517
  92.9 3.0 %shard_map.62 = (f32[256,256]{1,0:T(8,128)S(1)}, f32[256,256]{1,0:T(8,128)S(1)}) custom-call(s32[16]{0:T(128)S(1)} %constant_dynamic-update-slice_fusion.f, f32[128,128]{1,0:T(8,128)S(1)} %add.36.refs_0_, f32[128,128]{1,0:T(8,128)S(1)} %collective-permute-done.21.refs_1_, f32[128,128]{1,0:T(8,128)S(1)} %collective-permute-done.22.refs_2_, ...), custom_call_target="tpu_custom_call" | custom-call | tf_op jit(solution)/shard_map/pallas_call | solution.py:65
  99.9 4.6 %collective-permute-start.26 = (f32[1280,128]{1,0:T(8,128)S(1)}, f32[1280,128]{1,0:T(8,128)S(1)}, u32[]{:S(2)}, u32[]{:S(2)}) collective-permute-start(f32[1280,128]{1,0:T(8,128)S(1)} %get-tuple-element.123.refs_2_.refs_4_), channel_id=1, source_target_pairs={{9,1},{11,3},{13,5},{15,7},{0,8},{17,9},{2,10},{19,11},{4,12},{21,... | collective-permute-start | bytes 1966088 | tf_op jit(solution)/shard_map/ppermute | solution.py:517
  104.5 1.7 %collective-permute-start.29 = (f32[1280,128]{1,0:T(8,128)S(1)}, f32[1280,128]{1,0:T(8,128)S(1)}, u32[]{:S(2)}, u32[]{:S(2)}) collective-permute-start(f32[1280,128]{1,0:T(8,128)S(1)} %get-tuple-element.132), channel_id=1, source_target_pairs={{4,0},{5,1},{6,2},{7,3},{0,4},{1,5},{2,6},{3,7},{12,8},{13,9},{14,... | collective-permute-start | bytes 1966088 | tf_op jit(solution)/shard_map/ppermute | solution.py:517
  106.2 1.6 %shard_map.66 = (f32[128,128]{1,0:T(8,128)S(1)}, f32[128,128]{1,0:T(8,128)S(1)}) custom-call(s32[16]{0:T(128)S(1)} %constant_dynamic-update-slice_fusion.f, f32[256,256]{1,0:T(8,128)S(1)} %get-tuple-element.124.gram_ref, f32[256,256]{1,0:T(8,128)S(1)} %get-tuple-element.116.rotation_ref), custom_call_target="tpu_custom_call" | custom-call | tf_op jit(solution)/shard_map/pallas_call | solution.py:65
  108.5 3.0 %collective-permute-start.28 = (f32[128,128]{1,0:T(8,128)S(1)}, f32[128,128]{1,0:T(8,128)S(1)}, u32[]{:S(2)}, u32[]{:S(2)}) collective-permute-start(f32[128,128]{1,0:T(8,128)S(1)} %get-tuple-element.126), channel_id=1, source_target_pairs={{1,0},{0,1},{3,2},{2,3},{5,4},{4,5},{7,6},{6,7},{9,8},{8,9},{11,10... | collective-permute-start | bytes 196616 | tf_op jit(solution)/shard_map/ppermute | solution.py:517
  112.2 4.3 %collective-permute-done.26.refs_3_.refs_5_ = f32[1280,128]{1,0:T(8,128)S(1)} collective-permute-done((f32[1280,128]{1,0:T(8,128)S(1)}, f32[1280,128]{1,0:T(8,128)S(1)}, u32[]{:S(2)}, u32[]{:S(2)}) %collective-permute-start.26) | collective-permute-done | bytes 655392 | tf_op jit(solution)/shard_map/ppermute | solution.py:517
  122.1 1.9 %collective-permute-start.33 = (f32[128,128]{1,0:T(8,128)S(1)}, f32[128,128]{1,0:T(8,128)S(1)}, u32[]{:S(2)}, u32[]{:S(2)}) collective-permute-start(f32[128,128]{1,0:T(8,128)S(1)} %add.37.refs_0_), channel_id=1, source_target_pairs={{6,0},{7,1},{4,2},{5,3},{2,4},{3,5},{0,6},{1,7},{14,8},{15,9},{12,... | collective-permute-start | bytes 196616 | tf_op jit(solution)/shard_map/ppermute | solution.py:517
  126.2 3.6 %collective-permute-done.33.refs_3_ = f32[128,128]{1,0:T(8,128)S(1)} collective-permute-done((f32[128,128]{1,0:T(8,128)S(1)}, f32[128,128]{1,0:T(8,128)S(1)}, u32[]{:S(2)}, u32[]{:S(2)}) %collective-permute-start.33) | collective-permute-done | bytes 65568 | tf_op jit(solution)/shard_map/ppermute | solution.py:517
  131.6 3.1 %shard_map.69 = (f32[256,256]{1,0:T(8,128)S(1)}, f32[256,256]{1,0:T(8,128)S(1)}) custom-call(s32[16]{0:T(128)S(1)} %constant_dynamic-update-slice_fusion.f, f32[128,128]{1,0:T(8,128)S(1)} %add.37.refs_0_, f32[128,128]{1,0:T(8,128)S(1)} %collective-permute-done.31.refs_1_, f32[128,128]{1,0:T(8,128)S(1)} %collective-permute-done.32.refs_2_, ...), custom_call_target="tpu_custom_call" | custom-call | tf_op jit(solution)/shard_map/pallas_call | solution.py:65
  136.2 2.5 %shard_map.71 = (f32[2048,256]{1,0:T(8,128)}, f32[512,256]{1,0:T(8,128)}) custom-call(s32[16]{0:T(128)S(1)} %constant_dynamic-update-slice_fusion.f, f32[256,256]{1,0:T(8,128)S(1)} %get-tuple-element.143.rotation_ref.own_ref, f32[256,256]{1,0:T(8,128)S(1)} %collective-permute-done.35.other_ref, f32[1280,128]{1,0:T(8,128)S(1)} %get-tuple-element.135.up_0_ref.refs_0_, ...), custom_call_target="tpu_custom_call" | custom-call | flops 1 | bytes 1 | tf_op jit(solution)/shard_map/pallas_call | solution.py:417
  140.3 2.4 %shard_map.72 = (f32[2048,256]{1,0:T(8,128)}, f32[512,256]{1,0:T(8,128)}, f32[1,256]{1,0:T(1,128)}) custom-call(s32[16]{0:T(128)S(1)} %constant_dynamic-update-slice_fusion.f, f32[256,256]{1,0:T(8,128)S(1)} %get-tuple-element.143.rotation_ref.own_ref, ...), custom_call_target="tpu_custom_call", output_to_operand_aliasing={{0}: (7, {}), {1}: (8, {})} | custom-call | flops 1 | bytes 1 | tf_op jit(solution)/shard_map/pallas_call | solution.py:417
  (80 shorter events, 43.9 us)
Async XLA Ops:
  3.1 25.7 %collective-permute-start.5 = (f32[768,256]{1,0:T(8,128)}, f32[768,256]{1,0:T(8,128)S(1)}, u32[]{:S(2)}, u32[]{:S(2)}) collective-permute-start(f32[768,256]{1,0:T(8,128)} %get-tuple-element.85), channel_id=1, source_target_pairs={{4,0},{5,1},{6,2},{7,3},{0,4},{1,5},{2,6},{3,7},{12,8},{13,9},{14,... | collective-permute-start | bytes 2359304 | tf_op jit(solution)/shard_map/ppermute | solution.py:517
  8.7 7.0 %collective-permute-start.1 = (f32[384,128]{1,0:T(8,128)S(1)}, f32[384,128]{1,0:T(8,128)S(1)}, u32[]{:S(2)}, u32[]{:S(2)}) collective-permute-start(f32[384,128]{1,0:T(8,128)S(1)} %add.34.own_ref), channel_id=1, source_target_pairs={{2,0},{3,1},{0,2},{1,3},{6,4},{7,5},{4,6},{5,7},{10,8},{11,9},{8,1... | collective-permute-start | bytes 589832 | tf_op jit(solution)/shard_map/ppermute | solution.py:517
  19.2 8.3 %collective-permute-start.3 = (f32[128,256]{1,0:T(8,128)S(1)}, f32[128,256]{1,0:T(8,128)S(1)}, u32[]{:S(2)}, u32[]{:S(2)}) collective-permute-start(f32[128,256]{1,0:T(8,128)S(1)} %get-tuple-element.84), channel_id=1, source_target_pairs={{4,0},{5,1},{6,2},{7,3},{0,4},{1,5},{2,6},{3,7},{12,8},{13,9},{14,... | collective-permute-start | bytes 393224 | tf_op jit(solution)/shard_map/ppermute | solution.py:517
  20.8 27.4 %collective-permute-start.2 = (f32[1280,128]{1,0:T(8,128)S(1)}, f32[1280,128]{1,0:T(8,128)S(1)}, u32[]{:S(2)}, u32[]{:S(2)}) collective-permute-start(f32[1280,128]{1,0:T(8,128)S(1)} %get-tuple-element.83.refs_1_), channel_id=1, source_target_pairs={{8,0},{9,1},{10,2},{11,3},{16,8},{17,9},{18,10},{19,11},{4,12},{5,... | collective-permute-start | bytes 1966088 | tf_op jit(solution)/shard_map/ppermute | solution.py:517
  22.1 11.9 %collective-permute-start.7 = (f32[256,256]{1,0:T(8,128)S(1)}, f32[256,256]{1,0:T(8,128)S(1)}, u32[]{:S(2)}, u32[]{:S(2)}) collective-permute-start(f32[256,256]{1,0:T(8,128)S(1)} %copy-done.1), channel_id=1, source_target_pairs={{4,0},{5,1},{6,2},{7,3},{0,4},{1,5},{2,6},{3,7},{12,8},{13,9},{14,... | collective-permute-start | bytes 786440 | tf_op jit(solution)/shard_map/ppermute | solution.py:517
  29.9 18.4 %collective-permute-start.6 = (f32[768,128]{1,0:T(8,128)S(1)}, f32[768,128]{1,0:T(8,128)S(1)}, u32[]{:S(2)}, u32[]{:S(2)}) collective-permute-start(f32[768,128]{1,0:T(8,128)S(1)} %get-tuple-element.87.refs_4_), channel_id=1, source_target_pairs={{12,4},{13,5},{14,6},{15,7},{0,8},{1,9},{2,10},{3,11},{20,12},{21,... | collective-permute-start | bytes 1179656 | tf_op jit(solution)/shard_map/ppermute | solution.py:517
  35.0 13.3 %collective-permute-start.8 = (f32[512,128]{1,0:T(8,128)S(1)}, f32[512,128]{1,0:T(8,128)S(1)}, u32[]{:S(2)}, u32[]{:S(2)}) collective-permute-start(f32[512,128]{1,0:T(8,128)S(1)} %get-tuple-element.90.refs_7_), channel_id=1, source_target_pairs={{12,4},{13,5},{14,6},{15,7},{0,8},{1,9},{2,10},{3,11},{20,12},{21,... | collective-permute-start | bytes 786440 | tf_op jit(solution)/shard_map/ppermute | solution.py:517
  40.1 9.6 %collective-permute-start.9 = (f32[128,128]{1,0:T(8,128)S(1)}, f32[128,128]{1,0:T(8,128)S(1)}, u32[]{:S(2)}, u32[]{:S(2)}) collective-permute-start(f32[128,128]{1,0:T(8,128)S(1)} %get-tuple-element.94), channel_id=1, source_target_pairs={{0,0},{8,1},{2,2},{10,3},{1,4},{9,5},{3,6},{11,7},{4,8},{16,9},{6,... | collective-permute-start | bytes 196616 | tf_op jit(solution)/shard_map/ppermute | solution.py:517
  40.8 8.9 %collective-permute-start.10 = (f32[128,128]{1,0:T(8,128)S(1)}, f32[128,128]{1,0:T(8,128)S(1)}, u32[]{:S(2)}, u32[]{:S(2)}) collective-permute-start(f32[128,128]{1,0:T(8,128)S(1)} %get-tuple-element.95), channel_id=1, source_target_pairs={{4,0},{0,1},{6,2},{2,3},{5,4},{1,5},{7,6},{3,7},{12,8},{8,9},{14,1... | collective-permute-start | bytes 196616 | tf_op jit(solution)/shard_map/ppermute | solution.py:517
  51.0 5.6 %collective-permute-start.14 = (f32[128,128]{1,0:T(8,128)S(1)}, f32[128,128]{1,0:T(8,128)S(1)}, u32[]{:S(2)}, u32[]{:S(2)}) collective-permute-start(f32[128,128]{1,0:T(8,128)S(1)} %add.35.refs_0_), channel_id=1, source_target_pairs={{6,0},{7,1},{4,2},{5,3},{2,4},{3,5},{0,6},{1,7},{14,8},{15,9},{12,... | collective-permute-start | bytes 196616 | tf_op jit(solution)/shard_map/ppermute | solution.py:517
  54.2 4.3 %collective-permute-start.13 = (f32[128,128]{1,0:T(8,128)S(1)}, f32[128,128]{1,0:T(8,128)S(1)}, u32[]{:S(2)}, u32[]{:S(2)}) collective-permute-start(f32[128,128]{1,0:T(8,128)S(1)} %add.35.refs_0_), channel_id=1, source_target_pairs={{4,0},{5,1},{6,2},{7,3},{0,4},{1,5},{2,6},{3,7},{12,8},{13,9},{14,... | collective-permute-start | bytes 196616 | tf_op jit(solution)/shard_map/ppermute | solution.py:517
  54.2 4.3 %collective-permute-start.12 = (f32[128,128]{1,0:T(8,128)S(1)}, f32[128,128]{1,0:T(8,128)S(1)}, u32[]{:S(2)}, u32[]{:S(2)}) collective-permute-start(f32[128,128]{1,0:T(8,128)S(1)} %add.35.refs_0_), channel_id=1, source_target_pairs={{2,0},{3,1},{0,2},{1,3},{6,4},{7,5},{4,6},{5,7},{10,8},{11,9},{8,1... | collective-permute-start | bytes 196616 | tf_op jit(solution)/shard_map/ppermute | solution.py:517
  61.9 2.6 %collective-permute-start.16 = (f32[256,256]{1,0:T(8,128)S(1)}, f32[256,256]{1,0:T(8,128)S(1)}, u32[]{:S(2)}, u32[]{:S(2)}) collective-permute-start(f32[256,256]{1,0:T(8,128)S(1)} %get-tuple-element.99.rotation_ref), channel_id=1, source_target_pairs={{1,0},{0,1},{3,2},{2,3},{5,4},{4,5},{7,6},{6,7},{9,8},{8,9},{11,10... | collective-permute-start | bytes 786440 | tf_op jit(solution)/shard_map/ppermute | solution.py:517
  63.2 15.3 %collective-permute-start.15 = (f32[1280,128]{1,0:T(8,128)S(1)}, f32[1280,128]{1,0:T(8,128)S(1)}, u32[]{:S(2)}, u32[]{:S(2)}) collective-permute-start(f32[1280,128]{1,0:T(8,128)S(1)} %get-tuple-element.105.refs_1_), channel_id=1, source_target_pairs={{8,0},{10,2},{12,4},{14,6},{16,8},{1,9},{18,10},{3,11},{20,12},{5,... | collective-permute-start | bytes 1966088 | tf_op jit(solution)/shard_map/ppermute | solution.py:517
  65.8 17.0 %collective-permute-start.17 = (f32[1280,128]{1,0:T(8,128)S(1)}, f32[1280,128]{1,0:T(8,128)S(1)}, u32[]{:S(2)}, u32[]{:S(2)}) collective-permute-start(f32[1280,128]{1,0:T(8,128)S(1)} %get-tuple-element.107.refs_4_), channel_id=1, source_target_pairs={{9,1},{11,3},{13,5},{15,7},{0,8},{17,9},{2,10},{19,11},{4,12},{21,... | collective-permute-start | bytes 1966088 | tf_op jit(solution)/shard_map/ppermute | solution.py:517
  72.4 12.0 %collective-permute-start.18 = (f32[128,128]{1,0:T(8,128)S(1)}, f32[128,128]{1,0:T(8,128)S(1)}, u32[]{:S(2)}, u32[]{:S(2)}) collective-permute-start(f32[128,128]{1,0:T(8,128)S(1)} %get-tuple-element.111), channel_id=1, source_target_pairs={{0,0},{8,1},{2,2},{10,3},{4,4},{12,5},{6,6},{14,7},{1,8},{16,9},{3... | collective-permute-start | bytes 196616 | tf_op jit(solution)/shard_map/ppermute | solution.py:517
  73.1 11.4 %collective-permute-start.19 = (f32[128,128]{1,0:T(8,128)S(1)}, f32[128,128]{1,0:T(8,128)S(1)}, u32[]{:S(2)}, u32[]{:S(2)}) collective-permute-start(f32[128,128]{1,0:T(8,128)S(1)} %get-tuple-element.112), channel_id=1, source_target_pairs={{1,0},{0,1},{3,2},{2,3},{5,4},{4,5},{7,6},{6,7},{9,8},{8,9},{11,10... | collective-permute-start | bytes 196616 | tf_op jit(solution)/shard_map/ppermute | solution.py:517
  86.2 5.4 %collective-permute-start.23 = (f32[128,128]{1,0:T(8,128)S(1)}, f32[128,128]{1,0:T(8,128)S(1)}, u32[]{:S(2)}, u32[]{:S(2)}) collective-permute-start(f32[128,128]{1,0:T(8,128)S(1)} %add.36.refs_0_), channel_id=1, source_target_pairs={{6,0},{7,1},{4,2},{5,3},{2,4},{3,5},{0,6},{1,7},{14,8},{15,9},{12,... | collective-permute-start | bytes 196616 | tf_op jit(solution)/shard_map/ppermute | solution.py:517
  88.1 4.3 %collective-permute-start.22 = (f32[128,128]{1,0:T(8,128)S(1)}, f32[128,128]{1,0:T(8,128)S(1)}, u32[]{:S(2)}, u32[]{:S(2)}) collective-permute-start(f32[128,128]{1,0:T(8,128)S(1)} %add.36.refs_0_), channel_id=1, source_target_pairs={{4,0},{5,1},{6,2},{7,3},{0,4},{1,5},{2,6},{3,7},{12,8},{13,9},{14,... | collective-permute-start | bytes 196616 | tf_op jit(solution)/shard_map/ppermute | solution.py:517
  88.4 4.5 %collective-permute-start.21 = (f32[128,128]{1,0:T(8,128)S(1)}, f32[128,128]{1,0:T(8,128)S(1)}, u32[]{:S(2)}, u32[]{:S(2)}) collective-permute-start(f32[128,128]{1,0:T(8,128)S(1)} %add.36.refs_0_), channel_id=1, source_target_pairs={{2,0},{3,1},{0,2},{1,3},{6,4},{7,5},{4,6},{5,7},{10,8},{11,9},{8,1... | collective-permute-start | bytes 196616 | tf_op jit(solution)/shard_map/ppermute | solution.py:517
  96.0 2.6 %collective-permute-start.25 = (f32[256,256]{1,0:T(8,128)S(1)}, f32[256,256]{1,0:T(8,128)S(1)}, u32[]{:S(2)}, u32[]{:S(2)}) collective-permute-start(f32[256,256]{1,0:T(8,128)S(1)} %get-tuple-element.116.rotation_ref), channel_id=1, source_target_pairs={{1,0},{0,1},{3,2},{2,3},{5,4},{4,5},{7,6},{6,7},{9,8},{8,9},{11,10... | collective-permute-start | bytes 786440 | tf_op jit(solution)/shard_map/ppermute | solution.py:517
  97.3 14.9 %collective-permute-start.24 = (f32[1280,128]{1,0:T(8,128)S(1)}, f32[1280,128]{1,0:T(8,128)S(1)}, u32[]{:S(2)}, u32[]{:S(2)}) collective-permute-start(f32[1280,128]{1,0:T(8,128)S(1)} %get-tuple-element.122.refs_0_.refs_1_), channel_id=1, source_target_pairs={{8,0},{10,2},{12,4},{14,6},{16,8},{1,9},{18,10},{3,11},{20,12},{5,... | collective-permute-start | bytes 1966088 | tf_op jit(solution)/shard_map/ppermute | solution.py:517
  99.9 16.7 %collective-permute-start.26 = (f32[1280,128]{1,0:T(8,128)S(1)}, f32[1280,128]{1,0:T(8,128)S(1)}, u32[]{:S(2)}, u32[]{:S(2)}) collective-permute-start(f32[1280,128]{1,0:T(8,128)S(1)} %get-tuple-element.123.refs_2_.refs_4_), channel_id=1, source_target_pairs={{9,1},{11,3},{13,5},{15,7},{0,8},{17,9},{2,10},{19,11},{4,12},{21,... | collective-permute-start | bytes 1966088 | tf_op jit(solution)/shard_map/ppermute | solution.py:517
  104.5 16.3 %collective-permute-start.29 = (f32[1280,128]{1,0:T(8,128)S(1)}, f32[1280,128]{1,0:T(8,128)S(1)}, u32[]{:S(2)}, u32[]{:S(2)}) collective-permute-start(f32[1280,128]{1,0:T(8,128)S(1)} %get-tuple-element.132), channel_id=1, source_target_pairs={{4,0},{5,1},{6,2},{7,3},{0,4},{1,5},{2,6},{3,7},{12,8},{13,9},{14,... | collective-permute-start | bytes 1966088 | tf_op jit(solution)/shard_map/ppermute | solution.py:517
  107.8 9.3 %collective-permute-start.27 = (f32[128,128]{1,0:T(8,128)S(1)}, f32[128,128]{1,0:T(8,128)S(1)}, u32[]{:S(2)}, u32[]{:S(2)}) collective-permute-start(f32[128,128]{1,0:T(8,128)S(1)} %get-tuple-element.125), channel_id=1, source_target_pairs={{0,0},{8,1},{2,2},{10,3},{4,4},{12,5},{6,6},{14,7},{1,8},{16,9},{3... | collective-permute-start | bytes 196616 | tf_op jit(solution)/shard_map/ppermute | solution.py:517
  108.5 8.6 %collective-permute-start.28 = (f32[128,128]{1,0:T(8,128)S(1)}, f32[128,128]{1,0:T(8,128)S(1)}, u32[]{:S(2)}, u32[]{:S(2)}) collective-permute-start(f32[128,128]{1,0:T(8,128)S(1)} %get-tuple-element.126), channel_id=1, source_target_pairs={{1,0},{0,1},{3,2},{2,3},{5,4},{4,5},{7,6},{6,7},{9,8},{8,9},{11,10... | collective-permute-start | bytes 196616 | tf_op jit(solution)/shard_map/ppermute | solution.py:517
  117.2 13.4 %collective-permute-start.34 = (f32[640,128]{1,0:T(8,128)S(1)}, f32[640,128]{1,0:T(8,128)S(1)}, u32[]{:S(2)}, u32[]{:S(2)}) collective-permute-start(f32[640,128]{1,0:T(8,128)S(1)} %shard_map.65), channel_id=1, source_target_pairs={{4,0},{5,1},{6,2},{7,3},{0,4},{1,5},{2,6},{3,7},{12,8},{13,9},{14,... | collective-permute-start | bytes 983048 | tf_op jit(solution)/shard_map/ppermute | solution.py:517
  122.1 7.8 %collective-permute-start.33 = (f32[128,128]{1,0:T(8,128)S(1)}, f32[128,128]{1,0:T(8,128)S(1)}, u32[]{:S(2)}, u32[]{:S(2)}) collective-permute-start(f32[128,128]{1,0:T(8,128)S(1)} %add.37.refs_0_), channel_id=1, source_target_pairs={{6,0},{7,1},{4,2},{5,3},{2,4},{3,5},{0,6},{1,7},{14,8},{15,9},{12,... | collective-permute-start | bytes 196616 | tf_op jit(solution)/shard_map/ppermute | solution.py:517
  124.0 6.6 %collective-permute-start.32 = (f32[128,128]{1,0:T(8,128)S(1)}, f32[128,128]{1,0:T(8,128)S(1)}, u32[]{:S(2)}, u32[]{:S(2)}) collective-permute-start(f32[128,128]{1,0:T(8,128)S(1)} %add.37.refs_0_), channel_id=1, source_target_pairs={{4,0},{5,1},{6,2},{7,3},{0,4},{1,5},{2,6},{3,7},{12,8},{13,9},{14,... | collective-permute-start | bytes 196616 | tf_op jit(solution)/shard_map/ppermute | solution.py:517
  124.7 5.8 %collective-permute-start.31 = (f32[128,128]{1,0:T(8,128)S(1)}, f32[128,128]{1,0:T(8,128)S(1)}, u32[]{:S(2)}, u32[]{:S(2)}) collective-permute-start(f32[128,128]{1,0:T(8,128)S(1)} %add.37.refs_0_), channel_id=1, source_target_pairs={{2,0},{3,1},{0,2},{1,3},{6,4},{7,5},{4,6},{5,7},{10,8},{11,9},{8,1... | collective-permute-start | bytes 196616 | tf_op jit(solution)/shard_map/ppermute | solution.py:517
  130.6 9.7 %collective-permute-start.36 = (f32[640,128]{1,0:T(8,128)S(1)}, f32[640,128]{1,0:T(8,128)S(1)}, u32[]{:S(2)}, u32[]{:S(2)}) collective-permute-start(f32[640,128]{1,0:T(8,128)S(1)} %shard_map.68), channel_id=1, source_target_pairs={{4,0},{5,1},{6,2},{7,3},{0,4},{1,5},{2,6},{3,7},{12,8},{13,9},{14,... | collective-permute-start | bytes 983048 | tf_op jit(solution)/shard_map/ppermute | solution.py:517
  135.6 3.1 %collective-permute-start.37 = (f32[8,256]{1,0:T(8,128)S(1)}, f32[8,256]{1,0:T(8,128)S(1)}, u32[]{:S(2)}, u32[]{:S(2)}) collective-permute-start(f32[8,256]{1,0:T(8,128)S(1)} %shard_map.70.refs_0_), channel_id=1, source_target_pairs={{1,0},{0,1},{3,2},{2,3},{5,4},{4,5},{7,6},{6,7},{9,8},{8,9},{11,10... | collective-permute-start | bytes 24584 | tf_op jit(solution)/shard_map/ppermute | solution.py:517
  (9 other events, 38.9 us)

commit v17 on v16

--- a/solution.py
+++ b/solution.py
@@ -432,7 +432,7 @@
     )(facts, *inputs, *outputs)
 
 
-def finish_kept(facts, packs, blocks, native, got_top, part, half):
+def finish_kept(facts, packs, squares, blocks, native, got_top, part, half):
     size = 2 * half
     vector_rows = blocks[0].shape[0] - part
     top = got_top.shape[0]
@@ -440,7 +440,10 @@
     def body(f, own_ref, other_ref, *refs):
         x = f[X]
         turned = final_turn(f, own_ref, other_ref)
-        native_ref, top_ref, out_ref, vectors_ref, out, vectors, sems = refs[4:]
+        native_ref, top_ref = refs[4:6]
+        total = jnp.where(f[CORE] == x, refs[6][:1], refs[7][:1])
+        out_ref, vectors_ref, singular_ref, out, vectors, sems = refs[8:]
+        singular_ref[...] = jnp.sqrt(jnp.maximum(total, 0.0) + 1e-06)
         copies = []
 
         def kept(rows):
@@ -463,14 +466,14 @@
         for copy in copies:
             copy.wait()
 
-    outs = (shape(2 * part, size), shape(2 * vector_rows, size))
-    inputs = packs + blocks + [native, got_top]
+    outs = (shape(2 * part, size), shape(2 * vector_rows, size), shape(1, size))
+    inputs = packs + blocks + [native, got_top] + squares
     return finish_call(
         body, facts, inputs, [], outs, part + top, vector_rows, size
     )
 
 
-def finish_rest(facts, packs, squares, outputs, native, got_rest, part, half):
+def finish_rest(facts, packs, outputs, native, got_rest, part, half):
     size = 2 * half
     vector_rows = native.shape[0] - part
     rest = got_rest.shape[0] - vector_rows
@@ -479,9 +482,7 @@
     def body(f, own_ref, other_ref, native_ref, rest_ref, *refs):
         x = f[X]
         turned = final_turn(f, own_ref, other_ref)
-        total = jnp.where(f[CORE] == x, refs[0][:1], refs[1][:1])
-        out_ref, vectors_ref, singular_ref, out, vectors, sems = refs[4:]
-        singular_ref[...] = jnp.sqrt(jnp.maximum(total, 0.0) + 1e-06)
+        out_ref, vectors_ref, out, vectors, sems = refs[2:]
         copies = []
         value = final_product(rest_ref[:rest], native_ref[top:part], turned)
         put_rows(copies, sems, out, out_ref, 0, (1 - x) * part + top, value)
@@ -490,8 +491,8 @@
         for copy in copies:
             copy.wait()
 
-    outs = (shape(2 * part, size), shape(2 * vector_rows, size), shape(1, size))
-    inputs = packs + [native, got_rest] + squares
+    outs = (shape(2 * part, size), shape(2 * vector_rows, size))
+    inputs = packs + [native, got_rest]
     return finish_call(
         body, facts, inputs, outputs, outs, rest, vector_rows, size
     )
@@ -638,9 +639,11 @@
     packs = [rotation, exchange(rotation, 0, 1)]
     squares = squares_of(facts, gram, rotation)
     squares = [squares, exchange(squares, 0, 1)]
-    outputs = list(finish_kept(facts, packs, blocks, native, got_top, part, half))
-    rotated, vectors_out, singular = finish_rest(
-        facts, packs, squares, outputs, native, got_rest, part, half
+    *outputs, singular = finish_kept(
+        facts, packs, squares, blocks, native, got_top, part, half
+    )
+    rotated, vectors_out = finish_rest(
+        facts, packs, outputs, native, got_rest, part, half
     )
     return rotated, vectors_out, singular.reshape(size)
 

time: 143 us -> 143 us (level)
  transfers between devices with their start and end apart: 38 -> 38, of which waited for: 21 -> 22; matrix products, arithmetic and copies ran while one was open for 0% -> 0% of each run, Pallas kernels for 21% -> 21%
where the time goes in v17:
time: 143 us; the launch traced here: 142 us
  starting transfers between devices  56.3 us (39%)
  waiting for transfers between devices  43.5 us (30%)
  Pallas kernels  41 us (29%)
    ppermute x38, starting transfers between devices, permute(): return lax.ppermute(block, ('pair', 'row'), moves)  56.3 us
    ppermute x38, waiting for transfers between devices, permute(): return lax.ppermute(block, ('pair', 'row'), moves)  43.5 us
    pallas_call x20, Pallas kernels, call(): pl.pallas_call(body, out_shape=outs, in_specs=[pl.BlockSpec(memory_space=...  32.5 us
    pallas_call x2, Pallas kernels, finish_call(): pl.pallas_call(body, out_shape=outs, in_specs=[pl.BlockSpec(memory_space=...  4.97 us
  transfers between devices with their start and end apart: 38, of which 22 were waited for; matrix products, arithmetic and copies ran while one was open for 0% of the time, Pallas kernels for 21%

profile of v17, /device:TPU:0, one launch (start us, length us, event | category | flops | bytes accessed | tf_op | source)
XLA Modules:
  0.0 142.3 jit_solution(4493240884794905598)
XLA Ops:
  0.6 2.5 %shard_map.52 = (f32[768,256]{1,0:T(8,128)}, f32[256,256]{1,0:T(8,128)}) custom-call(f32[2048,256]{1,0:T(8,128)} %x_ref.3), custom_call_target="tpu_custom_call" | custom-call | tf_op jit(solution)/shard_map/pallas_call | solution.py:117
  3.1 3.0 %collective-permute-start.5 = (f32[768,256]{1,0:T(8,128)}, f32[768,256]{1,0:T(8,128)S(1)}, u32[]{:S(2)}, u32[]{:S(2)}) collective-permute-start(f32[768,256]{1,0:T(8,128)} %get-tuple-element.85), channel_id=1, source_target_pairs={{4,0},{5,1},{6,2},{7,3},{0,4},{1,5},{2,6},{3,7},{12,8},{13,9},{14,... | collective-permute-start | bytes 2359304 | tf_op jit(solution)/shard_map/ppermute | solution.py:518
  8.7 1.6 %collective-permute-start.1 = (f32[384,128]{1,0:T(8,128)S(1)}, f32[384,128]{1,0:T(8,128)S(1)}, u32[]{:S(2)}, u32[]{:S(2)}) collective-permute-start(f32[384,128]{1,0:T(8,128)S(1)} %add.34.own_ref), channel_id=1, source_target_pairs={{2,0},{3,1},{0,2},{1,3},{6,4},{7,5},{4,6},{5,7},{10,8},{11,9},{8,1... | collective-permute-start | bytes 589832 | tf_op jit(solution)/shard_map/ppermute | solution.py:518
  10.5 5.3 %collective-permute-done.1.other_ref = f32[384,128]{1,0:T(8,128)S(1)} collective-permute-done((f32[384,128]{1,0:T(8,128)S(1)}, f32[384,128]{1,0:T(8,128)S(1)}, u32[]{:S(2)}, u32[]{:S(2)}) %collective-permute-start.1) | collective-permute-done | bytes 196640 | tf_op jit(solution)/shard_map/ppermute | solution.py:518
  15.7 3.4 %shard_map.50 = (f32[256,256]{1,0:T(8,128)S(1)}, f32[256,256]{1,0:T(8,128)S(1)}, f32[128,256]{1,0:T(8,128)S(1)}) custom-call(s32[16]{0:T(128)S(1)} %constant_dynamic-update-slice_fusion.f, f32[384,128]{1,0:T(8,128)S(1)} %add.34.own_ref, f32[384,128]{1,0:T(8,128)S(1)} %collective-permute-done.1.other_ref), custom_call_target="tpu_custom_call" | custom-call | tf_op jit(solution)/shard_map/pallas_call | solution.py:65
  22.1 4.0 %collective-permute-start.7 = (f32[256,256]{1,0:T(8,128)S(1)}, f32[256,256]{1,0:T(8,128)S(1)}, u32[]{:S(2)}, u32[]{:S(2)}) collective-permute-start(f32[256,256]{1,0:T(8,128)S(1)} %copy-done.1), channel_id=1, source_target_pairs={{4,0},{5,1},{6,2},{7,3},{0,4},{1,5},{2,6},{3,7},{12,8},{13,9},{14,... | collective-permute-start | bytes 786440 | tf_op jit(solution)/shard_map/ppermute | solution.py:518
  29.9 4.1 %collective-permute-start.6 = (f32[768,128]{1,0:T(8,128)S(1)}, f32[768,128]{1,0:T(8,128)S(1)}, u32[]{:S(2)}, u32[]{:S(2)}) collective-permute-start(f32[768,128]{1,0:T(8,128)S(1)} %get-tuple-element.87.refs_4_), channel_id=1, source_target_pairs={{12,4},{13,5},{14,6},{15,7},{0,8},{1,9},{2,10},{3,11},{20,12},{21,... | collective-permute-start | bytes 1179656 | tf_op jit(solution)/shard_map/ppermute | solution.py:518
  35.0 3.5 %collective-permute-start.8 = (f32[512,128]{1,0:T(8,128)S(1)}, f32[512,128]{1,0:T(8,128)S(1)}, u32[]{:S(2)}, u32[]{:S(2)}) collective-permute-start(f32[512,128]{1,0:T(8,128)S(1)} %get-tuple-element.90.refs_7_), channel_id=1, source_target_pairs={{12,4},{13,5},{14,6},{15,7},{0,8},{1,9},{2,10},{3,11},{20,12},{21,... | collective-permute-start | bytes 786440 | tf_op jit(solution)/shard_map/ppermute | solution.py:518
  38.4 1.6 %shard_map.56 = (f32[128,128]{1,0:T(8,128)S(1)}, f32[128,128]{1,0:T(8,128)S(1)}) custom-call(s32[16]{0:T(128)S(1)} %constant_dynamic-update-slice_fusion.f, f32[256,256]{1,0:T(8,128)S(1)} %get-tuple-element.93.gram_ref, f32[256,256]{1,0:T(8,128)S(1)} %get-tuple-element.79.refs_0_.rotation_ref), custom_call_target="tpu_custom_call" | custom-call | tf_op jit(solution)/shard_map/pallas_call | solution.py:65
  41.6 6.6 %collective-permute-done.8.refs_8_ = f32[512,128]{1,0:T(8,128)S(1)} collective-permute-done((f32[512,128]{1,0:T(8,128)S(1)}, f32[512,128]{1,0:T(8,128)S(1)}, u32[]{:S(2)}, u32[]{:S(2)}) %collective-permute-start.8) | collective-permute-done | bytes 262176 | tf_op jit(solution)/shard_map/ppermute | solution.py:518
  51.0 3.2 %collective-permute-start.14 = (f32[128,128]{1,0:T(8,128)S(1)}, f32[128,128]{1,0:T(8,128)S(1)}, u32[]{:S(2)}, u32[]{:S(2)}) collective-permute-start(f32[128,128]{1,0:T(8,128)S(1)} %add.35.refs_0_), channel_id=1, source_target_pairs={{6,0},{7,1},{4,2},{5,3},{2,4},{3,5},{0,6},{1,7},{14,8},{15,9},{12,... | collective-permute-start | bytes 196616 | tf_op jit(solution)/shard_map/ppermute | solution.py:518
  54.8 1.8 %collective-permute-done.14.refs_3_ = f32[128,128]{1,0:T(8,128)S(1)} collective-permute-done((f32[128,128]{1,0:T(8,128)S(1)}, f32[128,128]{1,0:T(8,128)S(1)}, u32[]{:S(2)}, u32[]{:S(2)}) %collective-permute-start.14) | collective-permute-done | bytes 65568 | tf_op jit(solution)/shard_map/ppermute | solution.py:518
  56.6 1.8 %collective-permute-done.13.refs_2_ = f32[128,128]{1,0:T(8,128)S(1)} collective-permute-done((f32[128,128]{1,0:T(8,128)S(1)}, f32[128,128]{1,0:T(8,128)S(1)}, u32[]{:S(2)}, u32[]{:S(2)}) %collective-permute-start.13) | collective-permute-done | bytes 65568 | tf_op jit(solution)/shard_map/ppermute | solution.py:518
  58.5 3.4 %shard_map.57 = (f32[256,256]{1,0:T(8,128)S(1)}, f32[256,256]{1,0:T(8,128)S(1)}) custom-call(s32[16]{0:T(128)S(1)} %constant_dynamic-update-slice_fusion.f, f32[128,128]{1,0:T(8,128)S(1)} %add.35.refs_0_, f32[128,128]{1,0:T(8,128)S(1)} %collective-permute-done.12.refs_1_, f32[128,128]{1,0:T(8,128)S(1)} %collective-permute-done.13.refs_2_, ...), custom_call_target="tpu_custom_call" | custom-call | tf_op jit(solution)/shard_map/pallas_call | solution.py:65
  65.8 4.9 %collective-permute-start.17 = (f32[1280,128]{1,0:T(8,128)S(1)}, f32[1280,128]{1,0:T(8,128)S(1)}, u32[]{:S(2)}, u32[]{:S(2)}) collective-permute-start(f32[1280,128]{1,0:T(8,128)S(1)} %get-tuple-element.107.refs_4_), channel_id=1, source_target_pairs={{9,1},{11,3},{13,5},{15,7},{0,8},{17,9},{2,10},{19,11},{4,12},{21,... | collective-permute-start | bytes 1966088 | tf_op jit(solution)/shard_map/ppermute | solution.py:518
  70.7 1.6 %shard_map.61 = (f32[128,128]{1,0:T(8,128)S(1)}, f32[128,128]{1,0:T(8,128)S(1)}) custom-call(s32[16]{0:T(128)S(1)} %constant_dynamic-update-slice_fusion.f, f32[256,256]{1,0:T(8,128)S(1)} %get-tuple-element.110.gram_ref, f32[256,256]{1,0:T(8,128)S(1)} %get-tuple-element.99.rotation_ref), custom_call_target="tpu_custom_call" | custom-call | tf_op jit(solution)/shard_map/pallas_call | solution.py:65
  73.1 3.4 %collective-permute-start.19 = (f32[128,128]{1,0:T(8,128)S(1)}, f32[128,128]{1,0:T(8,128)S(1)}, u32[]{:S(2)}, u32[]{:S(2)}) collective-permute-start(f32[128,128]{1,0:T(8,128)S(1)} %get-tuple-element.112), channel_id=1, source_target_pairs={{1,0},{0,1},{3,2},{2,3},{5,4},{4,5},{7,6},{6,7},{9,8},{8,9},{11,10... | collective-permute-start | bytes 196616 | tf_op jit(solution)/shard_map/ppermute | solution.py:518
  76.5 2.1 %collective-permute-done.15.refs_2_ = f32[1280,128]{1,0:T(8,128)S(1)} collective-permute-done((f32[1280,128]{1,0:T(8,128)S(1)}, f32[1280,128]{1,0:T(8,128)S(1)}, u32[]{:S(2)}, u32[]{:S(2)}) %collective-permute-start.15) | collective-permute-done | bytes 655392 | tf_op jit(solution)/shard_map/ppermute | solution.py:518
  78.5 4.3 %collective-permute-done.17.refs_5_ = f32[1280,128]{1,0:T(8,128)S(1)} collective-permute-done((f32[1280,128]{1,0:T(8,128)S(1)}, f32[1280,128]{1,0:T(8,128)S(1)}, u32[]{:S(2)}, u32[]{:S(2)}) %collective-permute-start.17) | collective-permute-done | bytes 655392 | tf_op jit(solution)/shard_map/ppermute | solution.py:518
  86.2 1.9 %collective-permute-start.23 = (f32[128,128]{1,0:T(8,128)S(1)}, f32[128,128]{1,0:T(8,128)S(1)}, u32[]{:S(2)}, u32[]{:S(2)}) collective-permute-start(f32[128,128]{1,0:T(8,128)S(1)} %add.36.refs_0_), channel_id=1, source_target_pairs={{6,0},{7,1},{4,2},{5,3},{2,4},{3,5},{0,6},{1,7},{14,8},{15,9},{12,... | collective-permute-start | bytes 196616 | tf_op jit(solution)/shard_map/ppermute | solution.py:518
  89.7 1.8 %collective-permute-done.23.refs_3_ = f32[128,128]{1,0:T(8,128)S(1)} collective-permute-done((f32[128,128]{1,0:T(8,128)S(1)}, f32[128,128]{1,0:T(8,128)S(1)}, u32[]{:S(2)}, u32[]{:S(2)}) %collective-permute-start.23) | collective-permute-done | bytes 65568 | tf_op jit(solution)/shard_map/ppermute | solution.py:518
  92.9 3.0 %shard_map.62 = (f32[256,256]{1,0:T(8,128)S(1)}, f32[256,256]{1,0:T(8,128)S(1)}) custom-call(s32[16]{0:T(128)S(1)} %constant_dynamic-update-slice_fusion.f, f32[128,128]{1,0:T(8,128)S(1)} %add.36.refs_0_, f32[128,128]{1,0:T(8,128)S(1)} %collective-permute-done.21.refs_1_, f32[128,128]{1,0:T(8,128)S(1)} %collective-permute-done.22.refs_2_, ...), custom_call_target="tpu_custom_call" | custom-call | tf_op jit(solution)/shard_map/pallas_call | solution.py:65
  99.9 4.6 %collective-permute-start.26 = (f32[1280,128]{1,0:T(8,128)S(1)}, f32[1280,128]{1,0:T(8,128)S(1)}, u32[]{:S(2)}, u32[]{:S(2)}) collective-permute-start(f32[1280,128]{1,0:T(8,128)S(1)} %get-tuple-element.123.refs_2_.refs_4_), channel_id=1, source_target_pairs={{9,1},{11,3},{13,5},{15,7},{0,8},{17,9},{2,10},{19,11},{4,12},{21,... | collective-permute-start | bytes 1966088 | tf_op jit(solution)/shard_map/ppermute | solution.py:518
  104.5 1.7 %collective-permute-start.29 = (f32[1280,128]{1,0:T(8,128)S(1)}, f32[1280,128]{1,0:T(8,128)S(1)}, u32[]{:S(2)}, u32[]{:S(2)}) collective-permute-start(f32[1280,128]{1,0:T(8,128)S(1)} %get-tuple-element.132), channel_id=1, source_target_pairs={{4,0},{5,1},{6,2},{7,3},{0,4},{1,5},{2,6},{3,7},{12,8},{13,9},{14,... | collective-permute-start | bytes 1966088 | tf_op jit(solution)/shard_map/ppermute | solution.py:518
  106.2 1.6 %shard_map.66 = (f32[128,128]{1,0:T(8,128)S(1)}, f32[128,128]{1,0:T(8,128)S(1)}) custom-call(s32[16]{0:T(128)S(1)} %constant_dynamic-update-slice_fusion.f, f32[256,256]{1,0:T(8,128)S(1)} %get-tuple-element.124.gram_ref, f32[256,256]{1,0:T(8,128)S(1)} %get-tuple-element.116.rotation_ref), custom_call_target="tpu_custom_call" | custom-call | tf_op jit(solution)/shard_map/pallas_call | solution.py:65
  108.5 3.0 %collective-permute-start.28 = (f32[128,128]{1,0:T(8,128)S(1)}, f32[128,128]{1,0:T(8,128)S(1)}, u32[]{:S(2)}, u32[]{:S(2)}) collective-permute-start(f32[128,128]{1,0:T(8,128)S(1)} %get-tuple-element.126), channel_id=1, source_target_pairs={{1,0},{0,1},{3,2},{2,3},{5,4},{4,5},{7,6},{6,7},{9,8},{8,9},{11,10... | collective-permute-start | bytes 196616 | tf_op jit(solution)/shard_map/ppermute | solution.py:518
  112.2 4.3 %collective-permute-done.26.refs_3_.refs_5_ = f32[1280,128]{1,0:T(8,128)S(1)} collective-permute-done((f32[1280,128]{1,0:T(8,128)S(1)}, f32[1280,128]{1,0:T(8,128)S(1)}, u32[]{:S(2)}, u32[]{:S(2)}) %collective-permute-start.26) | collective-permute-done | bytes 655392 | tf_op jit(solution)/shard_map/ppermute | solution.py:518
  122.1 1.9 %collective-permute-start.33 = (f32[128,128]{1,0:T(8,128)S(1)}, f32[128,128]{1,0:T(8,128)S(1)}, u32[]{:S(2)}, u32[]{:S(2)}) collective-permute-start(f32[128,128]{1,0:T(8,128)S(1)} %add.37.refs_0_), channel_id=1, source_target_pairs={{6,0},{7,1},{4,2},{5,3},{2,4},{3,5},{0,6},{1,7},{14,8},{15,9},{12,... | collective-permute-start | bytes 196616 | tf_op jit(solution)/shard_map/ppermute | solution.py:518
  126.2 3.6 %collective-permute-done.33.refs_3_ = f32[128,128]{1,0:T(8,128)S(1)} collective-permute-done((f32[128,128]{1,0:T(8,128)S(1)}, f32[128,128]{1,0:T(8,128)S(1)}, u32[]{:S(2)}, u32[]{:S(2)}) %collective-permute-start.33) | collective-permute-done | bytes 65568 | tf_op jit(solution)/shard_map/ppermute | solution.py:518
  131.6 3.1 %shard_map.69 = (f32[256,256]{1,0:T(8,128)S(1)}, f32[256,256]{1,0:T(8,128)S(1)}) custom-call(s32[16]{0:T(128)S(1)} %constant_dynamic-update-slice_fusion.f, f32[128,128]{1,0:T(8,128)S(1)} %add.37.refs_0_, f32[128,128]{1,0:T(8,128)S(1)} %collective-permute-done.31.refs_1_, f32[128,128]{1,0:T(8,128)S(1)} %collective-permute-done.32.refs_2_, ...), custom_call_target="tpu_custom_call" | custom-call | tf_op jit(solution)/shard_map/pallas_call | solution.py:65
  137.0 3.1 %shard_map.71 = (f32[2048,256]{1,0:T(8,128)}, f32[512,256]{1,0:T(8,128)}, f32[1,256]{1,0:T(1,128)}) custom-call(s32[16]{0:T(128)S(1)} %constant_dynamic-update-slice_fusion.f, f32[256,256]{1,0:T(8,128)S(1)} %get-tuple-element.143.rotation_ref.own_ref, f32[256,256]{1,0:T(8,128)S(1)} %collective-permute-done.35.other_ref, ...), custom_call_target="tpu_custom_call" | custom-call | flops 1 | bytes 1 | tf_op jit(solution)/shard_map/pallas_call | solution.py:417
  140.3 1.9 %shard_map.72 = (f32[2048,256]{1,0:T(8,128)}, f32[512,256]{1,0:T(8,128)}) custom-call(s32[16]{0:T(128)S(1)} %constant_dynamic-update-slice_fusion.f, f32[256,256]{1,0:T(8,128)S(1)} %get-tuple-element.143.rotation_ref.own_ref, f32[256,256]{1,0:T(8,128)S(1)} %collective-permute-done.35.other_ref, ...), custom_call_target="tpu_custom_call", output_to_operand_aliasing={{0}: (5, {}), {1}: (6, {})} | custom-call | flops 1 | bytes 1 | tf_op jit(solution)/shard_map/pallas_call | solution.py:417
  (80 shorter events, 43.4 us)
Async XLA Ops:
  3.1 25.7 %collective-permute-start.5 = (f32[768,256]{1,0:T(8,128)}, f32[768,256]{1,0:T(8,128)S(1)}, u32[]{:S(2)}, u32[]{:S(2)}) collective-permute-start(f32[768,256]{1,0:T(8,128)} %get-tuple-element.85), channel_id=1, source_target_pairs={{4,0},{5,1},{6,2},{7,3},{0,4},{1,5},{2,6},{3,7},{12,8},{13,9},{14,... | collective-permute-start | bytes 2359304 | tf_op jit(solution)/shard_map/ppermute | solution.py:518
  8.7 7.0 %collective-permute-start.1 = (f32[384,128]{1,0:T(8,128)S(1)}, f32[384,128]{1,0:T(8,128)S(1)}, u32[]{:S(2)}, u32[]{:S(2)}) collective-permute-start(f32[384,128]{1,0:T(8,128)S(1)} %add.34.own_ref), channel_id=1, source_target_pairs={{2,0},{3,1},{0,2},{1,3},{6,4},{7,5},{4,6},{5,7},{10,8},{11,9},{8,1... | collective-permute-start | bytes 589832 | tf_op jit(solution)/shard_map/ppermute | solution.py:518
  19.2 8.3 %collective-permute-start.3 = (f32[128,256]{1,0:T(8,128)S(1)}, f32[128,256]{1,0:T(8,128)S(1)}, u32[]{:S(2)}, u32[]{:S(2)}) collective-permute-start(f32[128,256]{1,0:T(8,128)S(1)} %get-tuple-element.84), channel_id=1, source_target_pairs={{4,0},{5,1},{6,2},{7,3},{0,4},{1,5},{2,6},{3,7},{12,8},{13,9},{14,... | collective-permute-start | bytes 393224 | tf_op jit(solution)/shard_map/ppermute | solution.py:518
  20.8 27.4 %collective-permute-start.2 = (f32[1280,128]{1,0:T(8,128)S(1)}, f32[1280,128]{1,0:T(8,128)S(1)}, u32[]{:S(2)}, u32[]{:S(2)}) collective-permute-start(f32[1280,128]{1,0:T(8,128)S(1)} %get-tuple-element.83.refs_1_), channel_id=1, source_target_pairs={{8,0},{9,1},{10,2},{11,3},{16,8},{17,9},{18,10},{19,11},{4,12},{5,... | collective-permute-start | bytes 1966088 | tf_op jit(solution)/shard_map/ppermute | solution.py:518
  22.1 11.9 %collective-permute-start.7 = (f32[256,256]{1,0:T(8,128)S(1)}, f32[256,256]{1,0:T(8,128)S(1)}, u32[]{:S(2)}, u32[]{:S(2)}) collective-permute-start(f32[256,256]{1,0:T(8,128)S(1)} %copy-done.1), channel_id=1, source_target_pairs={{4,0},{5,1},{6,2},{7,3},{0,4},{1,5},{2,6},{3,7},{12,8},{13,9},{14,... | collective-permute-start | bytes 786440 | tf_op jit(solution)/shard_map/ppermute | solution.py:518
  29.9 18.4 %collective-permute-start.6 = (f32[768,128]{1,0:T(8,128)S(1)}, f32[768,128]{1,0:T(8,128)S(1)}, u32[]{:S(2)}, u32[]{:S(2)}) collective-permute-start(f32[768,128]{1,0:T(8,128)S(1)} %get-tuple-element.87.refs_4_), channel_id=1, source_target_pairs={{12,4},{13,5},{14,6},{15,7},{0,8},{1,9},{2,10},{3,11},{20,12},{21,... | collective-permute-start | bytes 1179656 | tf_op jit(solution)/shard_map/ppermute | solution.py:518
  35.0 13.3 %collective-permute-start.8 = (f32[512,128]{1,0:T(8,128)S(1)}, f32[512,128]{1,0:T(8,128)S(1)}, u32[]{:S(2)}, u32[]{:S(2)}) collective-permute-start(f32[512,128]{1,0:T(8,128)S(1)} %get-tuple-element.90.refs_7_), channel_id=1, source_target_pairs={{12,4},{13,5},{14,6},{15,7},{0,8},{1,9},{2,10},{3,11},{20,12},{21,... | collective-permute-start | bytes 786440 | tf_op jit(solution)/shard_map/ppermute | solution.py:518
  40.1 9.6 %collective-permute-start.9 = (f32[128,128]{1,0:T(8,128)S(1)}, f32[128,128]{1,0:T(8,128)S(1)}, u32[]{:S(2)}, u32[]{:S(2)}) collective-permute-start(f32[128,128]{1,0:T(8,128)S(1)} %get-tuple-element.94), channel_id=1, source_target_pairs={{0,0},{8,1},{2,2},{10,3},{1,4},{9,5},{3,6},{11,7},{4,8},{16,9},{6,... | collective-permute-start | bytes 196616 | tf_op jit(solution)/shard_map/ppermute | solution.py:518
  40.8 8.9 %collective-permute-start.10 = (f32[128,128]{1,0:T(8,128)S(1)}, f32[128,128]{1,0:T(8,128)S(1)}, u32[]{:S(2)}, u32[]{:S(2)}) collective-permute-start(f32[128,128]{1,0:T(8,128)S(1)} %get-tuple-element.95), channel_id=1, source_target_pairs={{4,0},{0,1},{6,2},{2,3},{5,4},{1,5},{7,6},{3,7},{12,8},{8,9},{14,1... | collective-permute-start | bytes 196616 | tf_op jit(solution)/shard_map/ppermute | solution.py:518
  51.0 5.6 %collective-permute-start.14 = (f32[128,128]{1,0:T(8,128)S(1)}, f32[128,128]{1,0:T(8,128)S(1)}, u32[]{:S(2)}, u32[]{:S(2)}) collective-permute-start(f32[128,128]{1,0:T(8,128)S(1)} %add.35.refs_0_), channel_id=1, source_target_pairs={{6,0},{7,1},{4,2},{5,3},{2,4},{3,5},{0,6},{1,7},{14,8},{15,9},{12,... | collective-permute-start | bytes 196616 | tf_op jit(solution)/shard_map/ppermute | solution.py:518
  54.2 4.3 %collective-permute-start.13 = (f32[128,128]{1,0:T(8,128)S(1)}, f32[128,128]{1,0:T(8,128)S(1)}, u32[]{:S(2)}, u32[]{:S(2)}) collective-permute-start(f32[128,128]{1,0:T(8,128)S(1)} %add.35.refs_0_), channel_id=1, source_target_pairs={{4,0},{5,1},{6,2},{7,3},{0,4},{1,5},{2,6},{3,7},{12,8},{13,9},{14,... | collective-permute-start | bytes 196616 | tf_op jit(solution)/shard_map/ppermute | solution.py:518
  54.2 4.3 %collective-permute-start.12 = (f32[128,128]{1,0:T(8,128)S(1)}, f32[128,128]{1,0:T(8,128)S(1)}, u32[]{:S(2)}, u32[]{:S(2)}) collective-permute-start(f32[128,128]{1,0:T(8,128)S(1)} %add.35.refs_0_), channel_id=1, source_target_pairs={{2,0},{3,1},{0,2},{1,3},{6,4},{7,5},{4,6},{5,7},{10,8},{11,9},{8,1... | collective-permute-start | bytes 196616 | tf_op jit(solution)/shard_map/ppermute | solution.py:518
  61.9 2.6 %collective-permute-start.16 = (f32[256,256]{1,0:T(8,128)S(1)}, f32[256,256]{1,0:T(8,128)S(1)}, u32[]{:S(2)}, u32[]{:S(2)}) collective-permute-start(f32[256,256]{1,0:T(8,128)S(1)} %get-tuple-element.99.rotation_ref), channel_id=1, source_target_pairs={{1,0},{0,1},{3,2},{2,3},{5,4},{4,5},{7,6},{6,7},{9,8},{8,9},{11,10... | collective-permute-start | bytes 786440 | tf_op jit(solution)/shard_map/ppermute | solution.py:518
  63.2 15.3 %collective-permute-start.15 = (f32[1280,128]{1,0:T(8,128)S(1)}, f32[1280,128]{1,0:T(8,128)S(1)}, u32[]{:S(2)}, u32[]{:S(2)}) collective-permute-start(f32[1280,128]{1,0:T(8,128)S(1)} %get-tuple-element.105.refs_1_), channel_id=1, source_target_pairs={{8,0},{10,2},{12,4},{14,6},{16,8},{1,9},{18,10},{3,11},{20,12},{5,... | collective-permute-start | bytes 1966088 | tf_op jit(solution)/shard_map/ppermute | solution.py:518
  65.8 17.0 %collective-permute-start.17 = (f32[1280,128]{1,0:T(8,128)S(1)}, f32[1280,128]{1,0:T(8,128)S(1)}, u32[]{:S(2)}, u32[]{:S(2)}) collective-permute-start(f32[1280,128]{1,0:T(8,128)S(1)} %get-tuple-element.107.refs_4_), channel_id=1, source_target_pairs={{9,1},{11,3},{13,5},{15,7},{0,8},{17,9},{2,10},{19,11},{4,12},{21,... | collective-permute-start | bytes 1966088 | tf_op jit(solution)/shard_map/ppermute | solution.py:518
  72.4 12.0 %collective-permute-start.18 = (f32[128,128]{1,0:T(8,128)S(1)}, f32[128,128]{1,0:T(8,128)S(1)}, u32[]{:S(2)}, u32[]{:S(2)}) collective-permute-start(f32[128,128]{1,0:T(8,128)S(1)} %get-tuple-element.111), channel_id=1, source_target_pairs={{0,0},{8,1},{2,2},{10,3},{4,4},{12,5},{6,6},{14,7},{1,8},{16,9},{3... | collective-permute-start | bytes 196616 | tf_op jit(solution)/shard_map/ppermute | solution.py:518
  73.1 11.4 %collective-permute-start.19 = (f32[128,128]{1,0:T(8,128)S(1)}, f32[128,128]{1,0:T(8,128)S(1)}, u32[]{:S(2)}, u32[]{:S(2)}) collective-permute-start(f32[128,128]{1,0:T(8,128)S(1)} %get-tuple-element.112), channel_id=1, source_target_pairs={{1,0},{0,1},{3,2},{2,3},{5,4},{4,5},{7,6},{6,7},{9,8},{8,9},{11,10... | collective-permute-start | bytes 196616 | tf_op jit(solution)/shard_map/ppermute | solution.py:518
  86.2 5.4 %collective-permute-start.23 = (f32[128,128]{1,0:T(8,128)S(1)}, f32[128,128]{1,0:T(8,128)S(1)}, u32[]{:S(2)}, u32[]{:S(2)}) collective-permute-start(f32[128,128]{1,0:T(8,128)S(1)} %add.36.refs_0_), channel_id=1, source_target_pairs={{6,0},{7,1},{4,2},{5,3},{2,4},{3,5},{0,6},{1,7},{14,8},{15,9},{12,... | collective-permute-start | bytes 196616 | tf_op jit(solution)/shard_map/ppermute | solution.py:518
  88.1 4.3 %collective-permute-start.22 = (f32[128,128]{1,0:T(8,128)S(1)}, f32[128,128]{1,0:T(8,128)S(1)}, u32[]{:S(2)}, u32[]{:S(2)}) collective-permute-start(f32[128,128]{1,0:T(8,128)S(1)} %add.36.refs_0_), channel_id=1, source_target_pairs={{4,0},{5,1},{6,2},{7,3},{0,4},{1,5},{2,6},{3,7},{12,8},{13,9},{14,... | collective-permute-start | bytes 196616 | tf_op jit(solution)/shard_map/ppermute | solution.py:518
  88.4 4.5 %collective-permute-start.21 = (f32[128,128]{1,0:T(8,128)S(1)}, f32[128,128]{1,0:T(8,128)S(1)}, u32[]{:S(2)}, u32[]{:S(2)}) collective-permute-start(f32[128,128]{1,0:T(8,128)S(1)} %add.36.refs_0_), channel_id=1, source_target_pairs={{2,0},{3,1},{0,2},{1,3},{6,4},{7,5},{4,6},{5,7},{10,8},{11,9},{8,1... | collective-permute-start | bytes 196616 | tf_op jit(solution)/shard_map/ppermute | solution.py:518
  96.0 2.6 %collective-permute-start.25 = (f32[256,256]{1,0:T(8,128)S(1)}, f32[256,256]{1,0:T(8,128)S(1)}, u32[]{:S(2)}, u32[]{:S(2)}) collective-permute-start(f32[256,256]{1,0:T(8,128)S(1)} %get-tuple-element.116.rotation_ref), channel_id=1, source_target_pairs={{1,0},{0,1},{3,2},{2,3},{5,4},{4,5},{7,6},{6,7},{9,8},{8,9},{11,10... | collective-permute-start | bytes 786440 | tf_op jit(solution)/shard_map/ppermute | solution.py:518
  97.3 14.9 %collective-permute-start.24 = (f32[1280,128]{1,0:T(8,128)S(1)}, f32[1280,128]{1,0:T(8,128)S(1)}, u32[]{:S(2)}, u32[]{:S(2)}) collective-permute-start(f32[1280,128]{1,0:T(8,128)S(1)} %get-tuple-element.122.refs_0_.refs_1_), channel_id=1, source_target_pairs={{8,0},{10,2},{12,4},{14,6},{16,8},{1,9},{18,10},{3,11},{20,12},{5,... | collective-permute-start | bytes 1966088 | tf_op jit(solution)/shard_map/ppermute | solution.py:518
  99.9 16.7 %collective-permute-start.26 = (f32[1280,128]{1,0:T(8,128)S(1)}, f32[1280,128]{1,0:T(8,128)S(1)}, u32[]{:S(2)}, u32[]{:S(2)}) collective-permute-start(f32[1280,128]{1,0:T(8,128)S(1)} %get-tuple-element.123.refs_2_.refs_4_), channel_id=1, source_target_pairs={{9,1},{11,3},{13,5},{15,7},{0,8},{17,9},{2,10},{19,11},{4,12},{21,... | collective-permute-start | bytes 1966088 | tf_op jit(solution)/shard_map/ppermute | solution.py:518
  104.5 16.3 %collective-permute-start.29 = (f32[1280,128]{1,0:T(8,128)S(1)}, f32[1280,128]{1,0:T(8,128)S(1)}, u32[]{:S(2)}, u32[]{:S(2)}) collective-permute-start(f32[1280,128]{1,0:T(8,128)S(1)} %get-tuple-element.132), channel_id=1, source_target_pairs={{4,0},{5,1},{6,2},{7,3},{0,4},{1,5},{2,6},{3,7},{12,8},{13,9},{14,... | collective-permute-start | bytes 1966088 | tf_op jit(solution)/shard_map/ppermute | solution.py:518
  107.8 9.3 %collective-permute-start.27 = (f32[128,128]{1,0:T(8,128)S(1)}, f32[128,128]{1,0:T(8,128)S(1)}, u32[]{:S(2)}, u32[]{:S(2)}) collective-permute-start(f32[128,128]{1,0:T(8,128)S(1)} %get-tuple-element.125), channel_id=1, source_target_pairs={{0,0},{8,1},{2,2},{10,3},{4,4},{12,5},{6,6},{14,7},{1,8},{16,9},{3... | collective-permute-start | bytes 196616 | tf_op jit(solution)/shard_map/ppermute | solution.py:518
  108.5 8.6 %collective-permute-start.28 = (f32[128,128]{1,0:T(8,128)S(1)}, f32[128,128]{1,0:T(8,128)S(1)}, u32[]{:S(2)}, u32[]{:S(2)}) collective-permute-start(f32[128,128]{1,0:T(8,128)S(1)} %get-tuple-element.126), channel_id=1, source_target_pairs={{1,0},{0,1},{3,2},{2,3},{5,4},{4,5},{7,6},{6,7},{9,8},{8,9},{11,10... | collective-permute-start | bytes 196616 | tf_op jit(solution)/shard_map/ppermute | solution.py:518
  117.2 13.4 %collective-permute-start.34 = (f32[640,128]{1,0:T(8,128)S(1)}, f32[640,128]{1,0:T(8,128)S(1)}, u32[]{:S(2)}, u32[]{:S(2)}) collective-permute-start(f32[640,128]{1,0:T(8,128)S(1)} %shard_map.65), channel_id=1, source_target_pairs={{4,0},{5,1},{6,2},{7,3},{0,4},{1,5},{2,6},{3,7},{12,8},{13,9},{14,... | collective-permute-start | bytes 983048 | tf_op jit(solution)/shard_map/ppermute | solution.py:518
  122.1 7.8 %collective-permute-start.33 = (f32[128,128]{1,0:T(8,128)S(1)}, f32[128,128]{1,0:T(8,128)S(1)}, u32[]{:S(2)}, u32[]{:S(2)}) collective-permute-start(f32[128,128]{1,0:T(8,128)S(1)} %add.37.refs_0_), channel_id=1, source_target_pairs={{6,0},{7,1},{4,2},{5,3},{2,4},{3,5},{0,6},{1,7},{14,8},{15,9},{12,... | collective-permute-start | bytes 196616 | tf_op jit(solution)/shard_map/ppermute | solution.py:518
  124.0 6.6 %collective-permute-start.32 = (f32[128,128]{1,0:T(8,128)S(1)}, f32[128,128]{1,0:T(8,128)S(1)}, u32[]{:S(2)}, u32[]{:S(2)}) collective-permute-start(f32[128,128]{1,0:T(8,128)S(1)} %add.37.refs_0_), channel_id=1, source_target_pairs={{4,0},{5,1},{6,2},{7,3},{0,4},{1,5},{2,6},{3,7},{12,8},{13,9},{14,... | collective-permute-start | bytes 196616 | tf_op jit(solution)/shard_map/ppermute | solution.py:518
  124.7 5.8 %collective-permute-start.31 = (f32[128,128]{1,0:T(8,128)S(1)}, f32[128,128]{1,0:T(8,128)S(1)}, u32[]{:S(2)}, u32[]{:S(2)}) collective-permute-start(f32[128,128]{1,0:T(8,128)S(1)} %add.37.refs_0_), channel_id=1, source_target_pairs={{2,0},{3,1},{0,2},{1,3},{6,4},{7,5},{4,6},{5,7},{10,8},{11,9},{8,1... | collective-permute-start | bytes 196616 | tf_op jit(solution)/shard_map/ppermute | solution.py:518
  130.6 9.7 %collective-permute-start.36 = (f32[640,128]{1,0:T(8,128)S(1)}, f32[640,128]{1,0:T(8,128)S(1)}, u32[]{:S(2)}, u32[]{:S(2)}) collective-permute-start(f32[640,128]{1,0:T(8,128)S(1)} %shard_map.68), channel_id=1, source_target_pairs={{4,0},{5,1},{6,2},{7,3},{0,4},{1,5},{2,6},{3,7},{12,8},{13,9},{14,... | collective-permute-start | bytes 983048 | tf_op jit(solution)/shard_map/ppermute | solution.py:518
  134.6 2.4 %collective-permute-start.35 = (f32[256,256]{1,0:T(8,128)S(1)}, f32[256,256]{1,0:T(8,128)S(1)}, u32[]{:S(2)}, u32[]{:S(2)}) collective-permute-start(f32[256,256]{1,0:T(8,128)S(1)} %get-tuple-element.143.rotation_ref.own_ref), channel_id=1, source_target_pairs={{1,0},{0,1},{3,2},{2,3},{5,4},{4,5},{7,6},{6,7},{9,8},{8,9},{11,10... | collective-permute-start | bytes 786440 | tf_op jit(solution)/shard_map/ppermute | solution.py:518
  (9 other events, 38.7 us)

commit v18 on v17

--- a/solution.py
+++ b/solution.py
@@ -615,7 +615,7 @@
             diagonals = [pass_diagonal(leave), exchange(stay, 0, 1)]
             if last_move:
                 native = exchange(native[0], 1, 0)
-                top = part * 5 // 8
+                top = part // 2
                 top_give = give_arrived(facts, own, others[0], top, half)
                 own[2], others[0][2], top_give, *diagonals = together(
                     own[2], others[0][2], top_give, *diagonals

time: 143 us -> 143 us (level)
  transfers between devices with their start and end apart: 38 -> 38, of which waited for: 22 -> 23; matrix products, arithmetic and copies ran while one was open for 0% -> 0% of each run, Pallas kernels for 21% -> 21%
where the time goes in v18:
time: 143 us
  starting transfers between devices  56.3 us (39%)
  waiting for transfers between devices  44.1 us (31%)
  Pallas kernels  41 us (29%)
    ppermute x38, starting transfers between devices, permute(): return lax.ppermute(block, ('pair', 'row'), moves)  56.3 us
    ppermute x38, waiting for transfers between devices, permute(): return lax.ppermute(block, ('pair', 'row'), moves)  44.1 us
    pallas_call x20, Pallas kernels, call(): pl.pallas_call(body, out_shape=outs, in_specs=[pl.BlockSpec(memory_space=...  32.5 us
    pallas_call x2, Pallas kernels, finish_call(): pl.pallas_call(body, out_shape=outs, in_specs=[pl.BlockSpec(memory_space=...  4.95 us
  transfers between devices with their start and end apart: 38, of which 23 were waited for; matrix products, arithmetic and copies ran while one was open for 0% of the time, Pallas kernels for 21%

profile of v18, /device:TPU:0, one launch (start us, length us, event | category | flops | bytes accessed | tf_op | source)
XLA Modules:
  0.0 143.0 jit_solution(16158074986610148196)
XLA Ops:
  0.6 2.5 %shard_map.52 = (f32[768,256]{1,0:T(8,128)}, f32[256,256]{1,0:T(8,128)}) custom-call(f32[2048,256]{1,0:T(8,128)} %x_ref.3), custom_call_target="tpu_custom_call" | custom-call | tf_op jit(solution)/shard_map/pallas_call | solution.py:117
  3.1 3.0 %collective-permute-start.5 = (f32[768,256]{1,0:T(8,128)}, f32[768,256]{1,0:T(8,128)S(1)}, u32[]{:S(2)}, u32[]{:S(2)}) collective-permute-start(f32[768,256]{1,0:T(8,128)} %get-tuple-element.85), channel_id=1, source_target_pairs={{4,0},{5,1},{6,2},{7,3},{0,4},{1,5},{2,6},{3,7},{12,8},{13,9},{14,... | collective-permute-start | bytes 2359304 | tf_op jit(solution)/shard_map/ppermute | solution.py:518
  8.7 1.6 %collective-permute-start.1 = (f32[384,128]{1,0:T(8,128)S(1)}, f32[384,128]{1,0:T(8,128)S(1)}, u32[]{:S(2)}, u32[]{:S(2)}) collective-permute-start(f32[384,128]{1,0:T(8,128)S(1)} %add.34.own_ref), channel_id=1, source_target_pairs={{2,0},{3,1},{0,2},{1,3},{6,4},{7,5},{4,6},{5,7},{10,8},{11,9},{8,1... | collective-permute-start | bytes 589832 | tf_op jit(solution)/shard_map/ppermute | solution.py:518
  10.5 5.3 %collective-permute-done.1.other_ref = f32[384,128]{1,0:T(8,128)S(1)} collective-permute-done((f32[384,128]{1,0:T(8,128)S(1)}, f32[384,128]{1,0:T(8,128)S(1)}, u32[]{:S(2)}, u32[]{:S(2)}) %collective-permute-start.1) | collective-permute-done | bytes 196640 | tf_op jit(solution)/shard_map/ppermute | solution.py:518
  15.7 3.4 %shard_map.50 = (f32[256,256]{1,0:T(8,128)S(1)}, f32[256,256]{1,0:T(8,128)S(1)}, f32[128,256]{1,0:T(8,128)S(1)}) custom-call(s32[16]{0:T(128)S(1)} %constant_dynamic-update-slice_fusion.f, f32[384,128]{1,0:T(8,128)S(1)} %add.34.own_ref, f32[384,128]{1,0:T(8,128)S(1)} %collective-permute-done.1.other_ref), custom_call_target="tpu_custom_call" | custom-call | tf_op jit(solution)/shard_map/pallas_call | solution.py:65
  22.1 4.0 %collective-permute-start.7 = (f32[256,256]{1,0:T(8,128)S(1)}, f32[256,256]{1,0:T(8,128)S(1)}, u32[]{:S(2)}, u32[]{:S(2)}) collective-permute-start(f32[256,256]{1,0:T(8,128)S(1)} %copy-done.1), channel_id=1, source_target_pairs={{4,0},{5,1},{6,2},{7,3},{0,4},{1,5},{2,6},{3,7},{12,8},{13,9},{14,... | collective-permute-start | bytes 786440 | tf_op jit(solution)/shard_map/ppermute | solution.py:518
  29.9 4.1 %collective-permute-start.6 = (f32[768,128]{1,0:T(8,128)S(1)}, f32[768,128]{1,0:T(8,128)S(1)}, u32[]{:S(2)}, u32[]{:S(2)}) collective-permute-start(f32[768,128]{1,0:T(8,128)S(1)} %get-tuple-element.87.refs_4_), channel_id=1, source_target_pairs={{12,4},{13,5},{14,6},{15,7},{0,8},{1,9},{2,10},{3,11},{20,12},{21,... | collective-permute-start | bytes 1179656 | tf_op jit(solution)/shard_map/ppermute | solution.py:518
  35.0 3.5 %collective-permute-start.8 = (f32[512,128]{1,0:T(8,128)S(1)}, f32[512,128]{1,0:T(8,128)S(1)}, u32[]{:S(2)}, u32[]{:S(2)}) collective-permute-start(f32[512,128]{1,0:T(8,128)S(1)} %get-tuple-element.90.refs_7_), channel_id=1, source_target_pairs={{12,4},{13,5},{14,6},{15,7},{0,8},{1,9},{2,10},{3,11},{20,12},{21,... | collective-permute-start | bytes 786440 | tf_op jit(solution)/shard_map/ppermute | solution.py:518
  38.4 1.6 %shard_map.56 = (f32[128,128]{1,0:T(8,128)S(1)}, f32[128,128]{1,0:T(8,128)S(1)}) custom-call(s32[16]{0:T(128)S(1)} %constant_dynamic-update-slice_fusion.f, f32[256,256]{1,0:T(8,128)S(1)} %get-tuple-element.93.gram_ref, f32[256,256]{1,0:T(8,128)S(1)} %get-tuple-element.79.refs_0_.rotation_ref), custom_call_target="tpu_custom_call" | custom-call | tf_op jit(solution)/shard_map/pallas_call | solution.py:65
  41.6 6.6 %collective-permute-done.8.refs_8_ = f32[512,128]{1,0:T(8,128)S(1)} collective-permute-done((f32[512,128]{1,0:T(8,128)S(1)}, f32[512,128]{1,0:T(8,128)S(1)}, u32[]{:S(2)}, u32[]{:S(2)}) %collective-permute-start.8) | collective-permute-done | bytes 262176 | tf_op jit(solution)/shard_map/ppermute | solution.py:518
  51.0 3.2 %collective-permute-start.14 = (f32[128,128]{1,0:T(8,128)S(1)}, f32[128,128]{1,0:T(8,128)S(1)}, u32[]{:S(2)}, u32[]{:S(2)}) collective-permute-start(f32[128,128]{1,0:T(8,128)S(1)} %add.35.refs_0_), channel_id=1, source_target_pairs={{6,0},{7,1},{4,2},{5,3},{2,4},{3,5},{0,6},{1,7},{14,8},{15,9},{12,... | collective-permute-start | bytes 196616 | tf_op jit(solution)/shard_map/ppermute | solution.py:518
  54.8 1.8 %collective-permute-done.14.refs_3_ = f32[128,128]{1,0:T(8,128)S(1)} collective-permute-done((f32[128,128]{1,0:T(8,128)S(1)}, f32[128,128]{1,0:T(8,128)S(1)}, u32[]{:S(2)}, u32[]{:S(2)}) %collective-permute-start.14) | collective-permute-done | bytes 65568 | tf_op jit(solution)/shard_map/ppermute | solution.py:518
  56.6 1.8 %collective-permute-done.13.refs_2_ = f32[128,128]{1,0:T(8,128)S(1)} collective-permute-done((f32[128,128]{1,0:T(8,128)S(1)}, f32[128,128]{1,0:T(8,128)S(1)}, u32[]{:S(2)}, u32[]{:S(2)}) %collective-permute-start.13) | collective-permute-done | bytes 65568 | tf_op jit(solution)/shard_map/ppermute | solution.py:518
  58.5 3.4 %shard_map.57 = (f32[256,256]{1,0:T(8,128)S(1)}, f32[256,256]{1,0:T(8,128)S(1)}) custom-call(s32[16]{0:T(128)S(1)} %constant_dynamic-update-slice_fusion.f, f32[128,128]{1,0:T(8,128)S(1)} %add.35.refs_0_, f32[128,128]{1,0:T(8,128)S(1)} %collective-permute-done.12.refs_1_, f32[128,128]{1,0:T(8,128)S(1)} %collective-permute-done.13.refs_2_, ...), custom_call_target="tpu_custom_call" | custom-call | tf_op jit(solution)/shard_map/pallas_call | solution.py:65
  65.8 4.9 %collective-permute-start.17 = (f32[1280,128]{1,0:T(8,128)S(1)}, f32[1280,128]{1,0:T(8,128)S(1)}, u32[]{:S(2)}, u32[]{:S(2)}) collective-permute-start(f32[1280,128]{1,0:T(8,128)S(1)} %get-tuple-element.107.refs_4_), channel_id=1, source_target_pairs={{9,1},{11,3},{13,5},{15,7},{0,8},{17,9},{2,10},{19,11},{4,12},{21,... | collective-permute-start | bytes 1966088 | tf_op jit(solution)/shard_map/ppermute | solution.py:518
  70.7 1.6 %shard_map.61 = (f32[128,128]{1,0:T(8,128)S(1)}, f32[128,128]{1,0:T(8,128)S(1)}) custom-call(s32[16]{0:T(128)S(1)} %constant_dynamic-update-slice_fusion.f, f32[256,256]{1,0:T(8,128)S(1)} %get-tuple-element.110.gram_ref, f32[256,256]{1,0:T(8,128)S(1)} %get-tuple-element.99.rotation_ref), custom_call_target="tpu_custom_call" | custom-call | tf_op jit(solution)/shard_map/pallas_call | solution.py:65
  73.1 3.4 %collective-permute-start.19 = (f32[128,128]{1,0:T(8,128)S(1)}, f32[128,128]{1,0:T(8,128)S(1)}, u32[]{:S(2)}, u32[]{:S(2)}) collective-permute-start(f32[128,128]{1,0:T(8,128)S(1)} %get-tuple-element.112), channel_id=1, source_target_pairs={{1,0},{0,1},{3,2},{2,3},{5,4},{4,5},{7,6},{6,7},{9,8},{8,9},{11,10... | collective-permute-start | bytes 196616 | tf_op jit(solution)/shard_map/ppermute | solution.py:518
  76.5 2.1 %collective-permute-done.15.refs_2_ = f32[1280,128]{1,0:T(8,128)S(1)} collective-permute-done((f32[1280,128]{1,0:T(8,128)S(1)}, f32[1280,128]{1,0:T(8,128)S(1)}, u32[]{:S(2)}, u32[]{:S(2)}) %collective-permute-start.15) | collective-permute-done | bytes 655392 | tf_op jit(solution)/shard_map/ppermute | solution.py:518
  78.5 4.3 %collective-permute-done.17.refs_5_ = f32[1280,128]{1,0:T(8,128)S(1)} collective-permute-done((f32[1280,128]{1,0:T(8,128)S(1)}, f32[1280,128]{1,0:T(8,128)S(1)}, u32[]{:S(2)}, u32[]{:S(2)}) %collective-permute-start.17) | collective-permute-done | bytes 655392 | tf_op jit(solution)/shard_map/ppermute | solution.py:518
  86.2 1.9 %collective-permute-start.23 = (f32[128,128]{1,0:T(8,128)S(1)}, f32[128,128]{1,0:T(8,128)S(1)}, u32[]{:S(2)}, u32[]{:S(2)}) collective-permute-start(f32[128,128]{1,0:T(8,128)S(1)} %add.36.refs_0_), channel_id=1, source_target_pairs={{6,0},{7,1},{4,2},{5,3},{2,4},{3,5},{0,6},{1,7},{14,8},{15,9},{12,... | collective-permute-start | bytes 196616 | tf_op jit(solution)/shard_map/ppermute | solution.py:518
  89.7 1.8 %collective-permute-done.23.refs_3_ = f32[128,128]{1,0:T(8,128)S(1)} collective-permute-done((f32[128,128]{1,0:T(8,128)S(1)}, f32[128,128]{1,0:T(8,128)S(1)}, u32[]{:S(2)}, u32[]{:S(2)}) %collective-permute-start.23) | collective-permute-done | bytes 65568 | tf_op jit(solution)/shard_map/ppermute | solution.py:518
  92.9 3.0 %shard_map.62 = (f32[256,256]{1,0:T(8,128)S(1)}, f32[256,256]{1,0:T(8,128)S(1)}) custom-call(s32[16]{0:T(128)S(1)} %constant_dynamic-update-slice_fusion.f, f32[128,128]{1,0:T(8,128)S(1)} %add.36.refs_0_, f32[128,128]{1,0:T(8,128)S(1)} %collective-permute-done.21.refs_1_, f32[128,128]{1,0:T(8,128)S(1)} %collective-permute-done.22.refs_2_, ...), custom_call_target="tpu_custom_call" | custom-call | tf_op jit(solution)/shard_map/pallas_call | solution.py:65
  99.9 4.6 %collective-permute-start.26 = (f32[1280,128]{1,0:T(8,128)S(1)}, f32[1280,128]{1,0:T(8,128)S(1)}, u32[]{:S(2)}, u32[]{:S(2)}) collective-permute-start(f32[1280,128]{1,0:T(8,128)S(1)} %get-tuple-element.123.refs_2_.refs_4_), channel_id=1, source_target_pairs={{9,1},{11,3},{13,5},{15,7},{0,8},{17,9},{2,10},{19,11},{4,12},{21,... | collective-permute-start | bytes 1966088 | tf_op jit(solution)/shard_map/ppermute | solution.py:518
  104.5 1.7 %collective-permute-start.29 = (f32[1280,128]{1,0:T(8,128)S(1)}, f32[1280,128]{1,0:T(8,128)S(1)}, u32[]{:S(2)}, u32[]{:S(2)}) collective-permute-start(f32[1280,128]{1,0:T(8,128)S(1)} %get-tuple-element.132), channel_id=1, source_target_pairs={{4,0},{5,1},{6,2},{7,3},{0,4},{1,5},{2,6},{3,7},{12,8},{13,9},{14,... | collective-permute-start | bytes 1966088 | tf_op jit(solution)/shard_map/ppermute | solution.py:518
  106.2 1.6 %shard_map.66 = (f32[128,128]{1,0:T(8,128)S(1)}, f32[128,128]{1,0:T(8,128)S(1)}) custom-call(s32[16]{0:T(128)S(1)} %constant_dynamic-update-slice_fusion.f, f32[256,256]{1,0:T(8,128)S(1)} %get-tuple-element.124.gram_ref, f32[256,256]{1,0:T(8,128)S(1)} %get-tuple-element.116.rotation_ref), custom_call_target="tpu_custom_call" | custom-call | tf_op jit(solution)/shard_map/pallas_call | solution.py:65
  108.5 3.0 %collective-permute-start.28 = (f32[128,128]{1,0:T(8,128)S(1)}, f32[128,128]{1,0:T(8,128)S(1)}, u32[]{:S(2)}, u32[]{:S(2)}) collective-permute-start(f32[128,128]{1,0:T(8,128)S(1)} %get-tuple-element.126), channel_id=1, source_target_pairs={{1,0},{0,1},{3,2},{2,3},{5,4},{4,5},{7,6},{6,7},{9,8},{8,9},{11,10... | collective-permute-start | bytes 196616 | tf_op jit(solution)/shard_map/ppermute | solution.py:518
  112.2 4.3 %collective-permute-done.26.refs_3_.refs_5_ = f32[1280,128]{1,0:T(8,128)S(1)} collective-permute-done((f32[1280,128]{1,0:T(8,128)S(1)}, f32[1280,128]{1,0:T(8,128)S(1)}, u32[]{:S(2)}, u32[]{:S(2)}) %collective-permute-start.26) | collective-permute-done | bytes 655392 | tf_op jit(solution)/shard_map/ppermute | solution.py:518
  122.1 1.9 %collective-permute-start.33 = (f32[128,128]{1,0:T(8,128)S(1)}, f32[128,128]{1,0:T(8,128)S(1)}, u32[]{:S(2)}, u32[]{:S(2)}) collective-permute-start(f32[128,128]{1,0:T(8,128)S(1)} %add.37.refs_0_), channel_id=1, source_target_pairs={{6,0},{7,1},{4,2},{5,3},{2,4},{3,5},{0,6},{1,7},{14,8},{15,9},{12,... | collective-permute-start | bytes 196616 | tf_op jit(solution)/shard_map/ppermute | solution.py:518
  126.2 2.2 %collective-permute-done.33.refs_3_ = f32[128,128]{1,0:T(8,128)S(1)} collective-permute-done((f32[128,128]{1,0:T(8,128)S(1)}, f32[128,128]{1,0:T(8,128)S(1)}, u32[]{:S(2)}, u32[]{:S(2)}) %collective-permute-start.33) | collective-permute-done | bytes 65568 | tf_op jit(solution)/shard_map/ppermute | solution.py:518
  130.9 3.1 %shard_map.69 = (f32[256,256]{1,0:T(8,128)S(1)}, f32[256,256]{1,0:T(8,128)S(1)}) custom-call(s32[16]{0:T(128)S(1)} %constant_dynamic-update-slice_fusion.f, f32[128,128]{1,0:T(8,128)S(1)} %add.37.refs_0_, f32[128,128]{1,0:T(8,128)S(1)} %collective-permute-done.31.refs_1_, f32[128,128]{1,0:T(8,128)S(1)} %collective-permute-done.32.refs_2_, ...), custom_call_target="tpu_custom_call" | custom-call | tf_op jit(solution)/shard_map/pallas_call | solution.py:65
  136.3 3.0 %shard_map.71 = (f32[2048,256]{1,0:T(8,128)}, f32[512,256]{1,0:T(8,128)}, f32[1,256]{1,0:T(1,128)}) custom-call(s32[16]{0:T(128)S(1)} %constant_dynamic-update-slice_fusion.f, f32[256,256]{1,0:T(8,128)S(1)} %get-tuple-element.143.rotation_ref.own_ref, f32[256,256]{1,0:T(8,128)S(1)} %collective-permute-done.35.other_ref, ...), custom_call_target="tpu_custom_call" | custom-call | flops 1 | bytes 1 | tf_op jit(solution)/shard_map/pallas_call | solution.py:417
  140.9 2.0 %shard_map.72 = (f32[2048,256]{1,0:T(8,128)}, f32[512,256]{1,0:T(8,128)}) custom-call(s32[16]{0:T(128)S(1)} %constant_dynamic-update-slice_fusion.f, f32[256,256]{1,0:T(8,128)S(1)} %get-tuple-element.143.rotation_ref.own_ref, f32[256,256]{1,0:T(8,128)S(1)} %collective-permute-done.35.other_ref, ...), custom_call_target="tpu_custom_call", output_to_operand_aliasing={{0}: (5, {}), {1}: (6, {})} | custom-call | flops 1 | bytes 1 | tf_op jit(solution)/shard_map/pallas_call | solution.py:417
  (80 shorter events, 45.4 us)
Async XLA Ops:
  3.1 25.7 %collective-permute-start.5 = (f32[768,256]{1,0:T(8,128)}, f32[768,256]{1,0:T(8,128)S(1)}, u32[]{:S(2)}, u32[]{:S(2)}) collective-permute-start(f32[768,256]{1,0:T(8,128)} %get-tuple-element.85), channel_id=1, source_target_pairs={{4,0},{5,1},{6,2},{7,3},{0,4},{1,5},{2,6},{3,7},{12,8},{13,9},{14,... | collective-permute-start | bytes 2359304 | tf_op jit(solution)/shard_map/ppermute | solution.py:518
  8.7 7.0 %collective-permute-start.1 = (f32[384,128]{1,0:T(8,128)S(1)}, f32[384,128]{1,0:T(8,128)S(1)}, u32[]{:S(2)}, u32[]{:S(2)}) collective-permute-start(f32[384,128]{1,0:T(8,128)S(1)} %add.34.own_ref), channel_id=1, source_target_pairs={{2,0},{3,1},{0,2},{1,3},{6,4},{7,5},{4,6},{5,7},{10,8},{11,9},{8,1... | collective-permute-start | bytes 589832 | tf_op jit(solution)/shard_map/ppermute | solution.py:518
  19.2 8.3 %collective-permute-start.3 = (f32[128,256]{1,0:T(8,128)S(1)}, f32[128,256]{1,0:T(8,128)S(1)}, u32[]{:S(2)}, u32[]{:S(2)}) collective-permute-start(f32[128,256]{1,0:T(8,128)S(1)} %get-tuple-element.84), channel_id=1, source_target_pairs={{4,0},{5,1},{6,2},{7,3},{0,4},{1,5},{2,6},{3,7},{12,8},{13,9},{14,... | collective-permute-start | bytes 393224 | tf_op jit(solution)/shard_map/ppermute | solution.py:518
  20.8 27.4 %collective-permute-start.2 = (f32[1280,128]{1,0:T(8,128)S(1)}, f32[1280,128]{1,0:T(8,128)S(1)}, u32[]{:S(2)}, u32[]{:S(2)}) collective-permute-start(f32[1280,128]{1,0:T(8,128)S(1)} %get-tuple-element.83.refs_1_), channel_id=1, source_target_pairs={{8,0},{9,1},{10,2},{11,3},{16,8},{17,9},{18,10},{19,11},{4,12},{5,... | collective-permute-start | bytes 1966088 | tf_op jit(solution)/shard_map/ppermute | solution.py:518
  22.1 11.9 %collective-permute-start.7 = (f32[256,256]{1,0:T(8,128)S(1)}, f32[256,256]{1,0:T(8,128)S(1)}, u32[]{:S(2)}, u32[]{:S(2)}) collective-permute-start(f32[256,256]{1,0:T(8,128)S(1)} %copy-done.1), channel_id=1, source_target_pairs={{4,0},{5,1},{6,2},{7,3},{0,4},{1,5},{2,6},{3,7},{12,8},{13,9},{14,... | collective-permute-start | bytes 786440 | tf_op jit(solution)/shard_map/ppermute | solution.py:518
  29.9 18.4 %collective-permute-start.6 = (f32[768,128]{1,0:T(8,128)S(1)}, f32[768,128]{1,0:T(8,128)S(1)}, u32[]{:S(2)}, u32[]{:S(2)}) collective-permute-start(f32[768,128]{1,0:T(8,128)S(1)} %get-tuple-element.87.refs_4_), channel_id=1, source_target_pairs={{12,4},{13,5},{14,6},{15,7},{0,8},{1,9},{2,10},{3,11},{20,12},{21,... | collective-permute-start | bytes 1179656 | tf_op jit(solution)/shard_map/ppermute | solution.py:518
  35.0 13.3 %collective-permute-start.8 = (f32[512,128]{1,0:T(8,128)S(1)}, f32[512,128]{1,0:T(8,128)S(1)}, u32[]{:S(2)}, u32[]{:S(2)}) collective-permute-start(f32[512,128]{1,0:T(8,128)S(1)} %get-tuple-element.90.refs_7_), channel_id=1, source_target_pairs={{12,4},{13,5},{14,6},{15,7},{0,8},{1,9},{2,10},{3,11},{20,12},{21,... | collective-permute-start | bytes 786440 | tf_op jit(solution)/shard_map/ppermute | solution.py:518
  40.1 9.6 %collective-permute-start.9 = (f32[128,128]{1,0:T(8,128)S(1)}, f32[128,128]{1,0:T(8,128)S(1)}, u32[]{:S(2)}, u32[]{:S(2)}) collective-permute-start(f32[128,128]{1,0:T(8,128)S(1)} %get-tuple-element.94), channel_id=1, source_target_pairs={{0,0},{8,1},{2,2},{10,3},{1,4},{9,5},{3,6},{11,7},{4,8},{16,9},{6,... | collective-permute-start | bytes 196616 | tf_op jit(solution)/shard_map/ppermute | solution.py:518
  40.8 8.9 %collective-permute-start.10 = (f32[128,128]{1,0:T(8,128)S(1)}, f32[128,128]{1,0:T(8,128)S(1)}, u32[]{:S(2)}, u32[]{:S(2)}) collective-permute-start(f32[128,128]{1,0:T(8,128)S(1)} %get-tuple-element.95), channel_id=1, source_target_pairs={{4,0},{0,1},{6,2},{2,3},{5,4},{1,5},{7,6},{3,7},{12,8},{8,9},{14,1... | collective-permute-start | bytes 196616 | tf_op jit(solution)/shard_map/ppermute | solution.py:518
  51.0 5.6 %collective-permute-start.14 = (f32[128,128]{1,0:T(8,128)S(1)}, f32[128,128]{1,0:T(8,128)S(1)}, u32[]{:S(2)}, u32[]{:S(2)}) collective-permute-start(f32[128,128]{1,0:T(8,128)S(1)} %add.35.refs_0_), channel_id=1, source_target_pairs={{6,0},{7,1},{4,2},{5,3},{2,4},{3,5},{0,6},{1,7},{14,8},{15,9},{12,... | collective-permute-start | bytes 196616 | tf_op jit(solution)/shard_map/ppermute | solution.py:518
  54.2 4.3 %collective-permute-start.13 = (f32[128,128]{1,0:T(8,128)S(1)}, f32[128,128]{1,0:T(8,128)S(1)}, u32[]{:S(2)}, u32[]{:S(2)}) collective-permute-start(f32[128,128]{1,0:T(8,128)S(1)} %add.35.refs_0_), channel_id=1, source_target_pairs={{4,0},{5,1},{6,2},{7,3},{0,4},{1,5},{2,6},{3,7},{12,8},{13,9},{14,... | collective-permute-start | bytes 196616 | tf_op jit(solution)/shard_map/ppermute | solution.py:518
  54.2 4.3 %collective-permute-start.12 = (f32[128,128]{1,0:T(8,128)S(1)}, f32[128,128]{1,0:T(8,128)S(1)}, u32[]{:S(2)}, u32[]{:S(2)}) collective-permute-start(f32[128,128]{1,0:T(8,128)S(1)} %add.35.refs_0_), channel_id=1, source_target_pairs={{2,0},{3,1},{0,2},{1,3},{6,4},{7,5},{4,6},{5,7},{10,8},{11,9},{8,1... | collective-permute-start | bytes 196616 | tf_op jit(solution)/shard_map/ppermute | solution.py:518
  61.9 2.6 %collective-permute-start.16 = (f32[256,256]{1,0:T(8,128)S(1)}, f32[256,256]{1,0:T(8,128)S(1)}, u32[]{:S(2)}, u32[]{:S(2)}) collective-permute-start(f32[256,256]{1,0:T(8,128)S(1)} %get-tuple-element.99.rotation_ref), channel_id=1, source_target_pairs={{1,0},{0,1},{3,2},{2,3},{5,4},{4,5},{7,6},{6,7},{9,8},{8,9},{11,10... | collective-permute-start | bytes 786440 | tf_op jit(solution)/shard_map/ppermute | solution.py:518
  63.2 15.3 %collective-permute-start.15 = (f32[1280,128]{1,0:T(8,128)S(1)}, f32[1280,128]{1,0:T(8,128)S(1)}, u32[]{:S(2)}, u32[]{:S(2)}) collective-permute-start(f32[1280,128]{1,0:T(8,128)S(1)} %get-tuple-element.105.refs_1_), channel_id=1, source_target_pairs={{8,0},{10,2},{12,4},{14,6},{16,8},{1,9},{18,10},{3,11},{20,12},{5,... | collective-permute-start | bytes 1966088 | tf_op jit(solution)/shard_map/ppermute | solution.py:518
  65.8 17.0 %collective-permute-start.17 = (f32[1280,128]{1,0:T(8,128)S(1)}, f32[1280,128]{1,0:T(8,128)S(1)}, u32[]{:S(2)}, u32[]{:S(2)}) collective-permute-start(f32[1280,128]{1,0:T(8,128)S(1)} %get-tuple-element.107.refs_4_), channel_id=1, source_target_pairs={{9,1},{11,3},{13,5},{15,7},{0,8},{17,9},{2,10},{19,11},{4,12},{21,... | collective-permute-start | bytes 1966088 | tf_op jit(solution)/shard_map/ppermute | solution.py:518
  72.4 12.0 %collective-permute-start.18 = (f32[128,128]{1,0:T(8,128)S(1)}, f32[128,128]{1,0:T(8,128)S(1)}, u32[]{:S(2)}, u32[]{:S(2)}) collective-permute-start(f32[128,128]{1,0:T(8,128)S(1)} %get-tuple-element.111), channel_id=1, source_target_pairs={{0,0},{8,1},{2,2},{10,3},{4,4},{12,5},{6,6},{14,7},{1,8},{16,9},{3... | collective-permute-start | bytes 196616 | tf_op jit(solution)/shard_map/ppermute | solution.py:518
  73.1 11.4 %collective-permute-start.19 = (f32[128,128]{1,0:T(8,128)S(1)}, f32[128,128]{1,0:T(8,128)S(1)}, u32[]{:S(2)}, u32[]{:S(2)}) collective-permute-start(f32[128,128]{1,0:T(8,128)S(1)} %get-tuple-element.112), channel_id=1, source_target_pairs={{1,0},{0,1},{3,2},{2,3},{5,4},{4,5},{7,6},{6,7},{9,8},{8,9},{11,10... | collective-permute-start | bytes 196616 | tf_op jit(solution)/shard_map/ppermute | solution.py:518
  86.2 5.4 %collective-permute-start.23 = (f32[128,128]{1,0:T(8,128)S(1)}, f32[128,128]{1,0:T(8,128)S(1)}, u32[]{:S(2)}, u32[]{:S(2)}) collective-permute-start(f32[128,128]{1,0:T(8,128)S(1)} %add.36.refs_0_), channel_id=1, source_target_pairs={{6,0},{7,1},{4,2},{5,3},{2,4},{3,5},{0,6},{1,7},{14,8},{15,9},{12,... | collective-permute-start | bytes 196616 | tf_op jit(solution)/shard_map/ppermute | solution.py:518
  88.1 4.3 %collective-permute-start.22 = (f32[128,128]{1,0:T(8,128)S(1)}, f32[128,128]{1,0:T(8,128)S(1)}, u32[]{:S(2)}, u32[]{:S(2)}) collective-permute-start(f32[128,128]{1,0:T(8,128)S(1)} %add.36.refs_0_), channel_id=1, source_target_pairs={{4,0},{5,1},{6,2},{7,3},{0,4},{1,5},{2,6},{3,7},{12,8},{13,9},{14,... | collective-permute-start | bytes 196616 | tf_op jit(solution)/shard_map/ppermute | solution.py:518
  88.4 4.5 %collective-permute-start.21 = (f32[128,128]{1,0:T(8,128)S(1)}, f32[128,128]{1,0:T(8,128)S(1)}, u32[]{:S(2)}, u32[]{:S(2)}) collective-permute-start(f32[128,128]{1,0:T(8,128)S(1)} %add.36.refs_0_), channel_id=1, source_target_pairs={{2,0},{3,1},{0,2},{1,3},{6,4},{7,5},{4,6},{5,7},{10,8},{11,9},{8,1... | collective-permute-start | bytes 196616 | tf_op jit(solution)/shard_map/ppermute | solution.py:518
  96.0 2.6 %collective-permute-start.25 = (f32[256,256]{1,0:T(8,128)S(1)}, f32[256,256]{1,0:T(8,128)S(1)}, u32[]{:S(2)}, u32[]{:S(2)}) collective-permute-start(f32[256,256]{1,0:T(8,128)S(1)} %get-tuple-element.116.rotation_ref), channel_id=1, source_target_pairs={{1,0},{0,1},{3,2},{2,3},{5,4},{4,5},{7,6},{6,7},{9,8},{8,9},{11,10... | collective-permute-start | bytes 786440 | tf_op jit(solution)/shard_map/ppermute | solution.py:518
  97.3 14.9 %collective-permute-start.24 = (f32[1280,128]{1,0:T(8,128)S(1)}, f32[1280,128]{1,0:T(8,128)S(1)}, u32[]{:S(2)}, u32[]{:S(2)}) collective-permute-start(f32[1280,128]{1,0:T(8,128)S(1)} %get-tuple-element.122.refs_0_.refs_1_), channel_id=1, source_target_pairs={{8,0},{10,2},{12,4},{14,6},{16,8},{1,9},{18,10},{3,11},{20,12},{5,... | collective-permute-start | bytes 1966088 | tf_op jit(solution)/shard_map/ppermute | solution.py:518
  99.9 16.7 %collective-permute-start.26 = (f32[1280,128]{1,0:T(8,128)S(1)}, f32[1280,128]{1,0:T(8,128)S(1)}, u32[]{:S(2)}, u32[]{:S(2)}) collective-permute-start(f32[1280,128]{1,0:T(8,128)S(1)} %get-tuple-element.123.refs_2_.refs_4_), channel_id=1, source_target_pairs={{9,1},{11,3},{13,5},{15,7},{0,8},{17,9},{2,10},{19,11},{4,12},{21,... | collective-permute-start | bytes 1966088 | tf_op jit(solution)/shard_map/ppermute | solution.py:518
  104.5 16.3 %collective-permute-start.29 = (f32[1280,128]{1,0:T(8,128)S(1)}, f32[1280,128]{1,0:T(8,128)S(1)}, u32[]{:S(2)}, u32[]{:S(2)}) collective-permute-start(f32[1280,128]{1,0:T(8,128)S(1)} %get-tuple-element.132), channel_id=1, source_target_pairs={{4,0},{5,1},{6,2},{7,3},{0,4},{1,5},{2,6},{3,7},{12,8},{13,9},{14,... | collective-permute-start | bytes 1966088 | tf_op jit(solution)/shard_map/ppermute | solution.py:518
  107.8 9.3 %collective-permute-start.27 = (f32[128,128]{1,0:T(8,128)S(1)}, f32[128,128]{1,0:T(8,128)S(1)}, u32[]{:S(2)}, u32[]{:S(2)}) collective-permute-start(f32[128,128]{1,0:T(8,128)S(1)} %get-tuple-element.125), channel_id=1, source_target_pairs={{0,0},{8,1},{2,2},{10,3},{4,4},{12,5},{6,6},{14,7},{1,8},{16,9},{3... | collective-permute-start | bytes 196616 | tf_op jit(solution)/shard_map/ppermute | solution.py:518
  108.5 8.6 %collective-permute-start.28 = (f32[128,128]{1,0:T(8,128)S(1)}, f32[128,128]{1,0:T(8,128)S(1)}, u32[]{:S(2)}, u32[]{:S(2)}) collective-permute-start(f32[128,128]{1,0:T(8,128)S(1)} %get-tuple-element.126), channel_id=1, source_target_pairs={{1,0},{0,1},{3,2},{2,3},{5,4},{4,5},{7,6},{6,7},{9,8},{8,9},{11,10... | collective-permute-start | bytes 196616 | tf_op jit(solution)/shard_map/ppermute | solution.py:518
  117.2 12.7 %collective-permute-start.34 = (f32[512,128]{1,0:T(8,128)S(1)}, f32[512,128]{1,0:T(8,128)S(1)}, u32[]{:S(2)}, u32[]{:S(2)}) collective-permute-start(f32[512,128]{1,0:T(8,128)S(1)} %shard_map.65), channel_id=1, source_target_pairs={{4,0},{5,1},{6,2},{7,3},{0,4},{1,5},{2,6},{3,7},{12,8},{13,9},{14,... | collective-permute-start | bytes 786440 | tf_op jit(solution)/shard_map/ppermute | solution.py:518
  122.1 6.4 %collective-permute-start.33 = (f32[128,128]{1,0:T(8,128)S(1)}, f32[128,128]{1,0:T(8,128)S(1)}, u32[]{:S(2)}, u32[]{:S(2)}) collective-permute-start(f32[128,128]{1,0:T(8,128)S(1)} %add.37.refs_0_), channel_id=1, source_target_pairs={{6,0},{7,1},{4,2},{5,3},{2,4},{3,5},{0,6},{1,7},{14,8},{15,9},{12,... | collective-permute-start | bytes 196616 | tf_op jit(solution)/shard_map/ppermute | solution.py:518
  124.0 5.1 %collective-permute-start.32 = (f32[128,128]{1,0:T(8,128)S(1)}, f32[128,128]{1,0:T(8,128)S(1)}, u32[]{:S(2)}, u32[]{:S(2)}) collective-permute-start(f32[128,128]{1,0:T(8,128)S(1)} %add.37.refs_0_), channel_id=1, source_target_pairs={{4,0},{5,1},{6,2},{7,3},{0,4},{1,5},{2,6},{3,7},{12,8},{13,9},{14,... | collective-permute-start | bytes 196616 | tf_op jit(solution)/shard_map/ppermute | solution.py:518
  124.7 5.1 %collective-permute-start.31 = (f32[128,128]{1,0:T(8,128)S(1)}, f32[128,128]{1,0:T(8,128)S(1)}, u32[]{:S(2)}, u32[]{:S(2)}) collective-permute-start(f32[128,128]{1,0:T(8,128)S(1)} %add.37.refs_0_), channel_id=1, source_target_pairs={{2,0},{3,1},{0,2},{1,3},{6,4},{7,5},{4,6},{5,7},{10,8},{11,9},{8,1... | collective-permute-start | bytes 196616 | tf_op jit(solution)/shard_map/ppermute | solution.py:518
  129.8 11.0 %collective-permute-start.36 = (f32[768,128]{1,0:T(8,128)S(1)}, f32[768,128]{1,0:T(8,128)S(1)}, u32[]{:S(2)}, u32[]{:S(2)}) collective-permute-start(f32[768,128]{1,0:T(8,128)S(1)} %shard_map.68), channel_id=1, source_target_pairs={{4,0},{5,1},{6,2},{7,3},{0,4},{1,5},{2,6},{3,7},{12,8},{13,9},{14,... | collective-permute-start | bytes 1179656 | tf_op jit(solution)/shard_map/ppermute | solution.py:518
  133.9 2.4 %collective-permute-start.35 = (f32[256,256]{1,0:T(8,128)S(1)}, f32[256,256]{1,0:T(8,128)S(1)}, u32[]{:S(2)}, u32[]{:S(2)}) collective-permute-start(f32[256,256]{1,0:T(8,128)S(1)} %get-tuple-element.143.rotation_ref.own_ref), channel_id=1, source_target_pairs={{1,0},{0,1},{3,2},{2,3},{5,4},{4,5},{7,6},{6,7},{9,8},{8,9},{11,10... | collective-permute-start | bytes 786440 | tf_op jit(solution)/shard_map/ppermute | solution.py:518
  (9 other events, 38.7 us)

commit v19 on v17

--- a/solution.py
+++ b/solution.py
@@ -42,19 +42,6 @@
         a, b, (((0,), (0,)), ((), ())), precision=highest,
         preferred_element_type=jnp.float32,
     )
-
-
-def dot3_tn(a, b):
-    def product(left, right):
-        return lax.dot_general(
-            left, right, (((0,), (0,)), ((), ())),
-            preferred_element_type=jnp.float32,
-        )
-
-    a_high, a_low = split(a)
-    b_high, b_low = split(b)
-    small = product(a_high, b_low) + product(a_low, b_high)
-    return product(a_high, b_high) + small
 
 
 def shape(*dims):
@@ -78,7 +65,7 @@
 def first_gram(sector, half):
     def body(x_ref, out_ref):
         x = x_ref[...]
-        g = dot3_tn(x, x)
+        g = dot_tn(x, x)
         out_ref[:half] = g[:half, :half]
         out_ref[half : 2 * half] = g[:half, half:]
         out_ref[2 * half :] = g[half:, half:]
@@ -354,8 +341,8 @@
         put_cross(
             f,
             refs[3 + 3 * pieces :],
-            dot3_tn(up_0[:part], low_0[:part]),
-            dot3_tn(up_1[:part], low_1[:part]),
+            dot_tn(up_0[:part], low_0[:part]),
+            dot_tn(up_1[:part], low_1[:part]),
         )
 
     outs = (shape(half, half),) * 2 + (shape(rows, half),) * 4

time: 143 us -> 143 us (level)
  Pallas kernels: 41 us -> 43.5 us
  waiting for transfers between devices: 43.5 us -> 41 us
    ppermute x38, waiting for transfers between devices: 43.5 us -> 41 us  [permute(): return lax.ppermute(block, ('pair', 'row'), moves)]
  transfers between devices with their start and end apart: 38 -> 38, of which waited for: 22 -> 20; matrix products, arithmetic and copies ran while one was open for 0% -> 0% of each run, Pallas kernels for 21% -> 23%
where the time goes in v19:
time: 143 us; the launch traced here: 142 us
  starting transfers between devices  56.2 us (39%)
  Pallas kernels  43.5 us (30%)
  waiting for transfers between devices  41 us (29%)
    ppermute x38, starting transfers between devices, permute(): return lax.ppermute(block, ('pair', 'row'), moves)  56.2 us
    ppermute x38, waiting for transfers between devices, permute(): return lax.ppermute(block, ('pair', 'row'), moves)  41 us
    pallas_call x20, Pallas kernels, call(): pl.pallas_call(body, out_shape=outs, in_specs=[pl.BlockSpec(memory_space=...  33.9 us
    pallas_call x2, Pallas kernels, finish_call(): pl.pallas_call(body, out_shape=outs, in_specs=[pl.BlockSpec(memory_space=...  4.97 us
  transfers between devices with their start and end apart: 38, of which 20 were waited for; matrix products, arithmetic and copies ran while one was open for 0% of the time, Pallas kernels for 23%

profile of v19, /device:TPU:0, one launch (start us, length us, event | category | flops | bytes accessed | tf_op | source)
XLA Modules:
  0.0 142.2 jit_solution(17476382856471817284)
XLA Ops:
  0.6 2.5 %shard_map.52 = (f32[768,256]{1,0:T(8,128)}, f32[256,256]{1,0:T(8,128)}) custom-call(f32[2048,256]{1,0:T(8,128)} %x_ref.3), custom_call_target="tpu_custom_call" | custom-call | tf_op jit(solution)/shard_map/pallas_call | solution.py:104
  3.1 3.0 %collective-permute-start.5 = (f32[768,256]{1,0:T(8,128)}, f32[768,256]{1,0:T(8,128)S(1)}, u32[]{:S(2)}, u32[]{:S(2)}) collective-permute-start(f32[768,256]{1,0:T(8,128)} %get-tuple-element.85), channel_id=1, source_target_pairs={{4,0},{5,1},{6,2},{7,3},{0,4},{1,5},{2,6},{3,7},{12,8},{13,9},{14,... | collective-permute-start | bytes 2359304 | tf_op jit(solution)/shard_map/ppermute | solution.py:505
  6.1 2.2 %shard_map.49 = f32[384,128]{1,0:T(8,128)S(1)} custom-call(f32[2048,256]{1,0:T(8,128)S(1)} %copy-done), custom_call_target="tpu_custom_call" | custom-call | tf_op jit(solution)/shard_map/pallas_call | solution.py:74
  11.6 5.3 %collective-permute-done.1.other_ref = f32[384,128]{1,0:T(8,128)S(1)} collective-permute-done((f32[384,128]{1,0:T(8,128)S(1)}, f32[384,128]{1,0:T(8,128)S(1)}, u32[]{:S(2)}, u32[]{:S(2)}) %collective-permute-start.1) | collective-permute-done | bytes 196640 | tf_op jit(solution)/shard_map/ppermute | solution.py:505
  16.8 3.4 %shard_map.50 = (f32[256,256]{1,0:T(8,128)S(1)}, f32[256,256]{1,0:T(8,128)S(1)}, f32[128,256]{1,0:T(8,128)S(1)}) custom-call(s32[16]{0:T(128)S(1)} %constant_dynamic-update-slice_fusion.f, f32[384,128]{1,0:T(8,128)S(1)} %add.34.own_ref, f32[384,128]{1,0:T(8,128)S(1)} %collective-permute-done.1.other_ref), custom_call_target="tpu_custom_call" | custom-call | tf_op jit(solution)/shard_map/pallas_call | solution.py:52
  23.2 4.0 %collective-permute-start.7 = (f32[256,256]{1,0:T(8,128)S(1)}, f32[256,256]{1,0:T(8,128)S(1)}, u32[]{:S(2)}, u32[]{:S(2)}) collective-permute-start(f32[256,256]{1,0:T(8,128)S(1)} %copy-done.1), channel_id=1, source_target_pairs={{4,0},{5,1},{6,2},{7,3},{0,4},{1,5},{2,6},{3,7},{12,8},{13,9},{14,... | collective-permute-start | bytes 786440 | tf_op jit(solution)/shard_map/ppermute | solution.py:505
  29.6 3.5 %collective-permute-start.6 = (f32[768,128]{1,0:T(8,128)S(1)}, f32[768,128]{1,0:T(8,128)S(1)}, u32[]{:S(2)}, u32[]{:S(2)}) collective-permute-start(f32[768,128]{1,0:T(8,128)S(1)} %get-tuple-element.87.refs_4_), channel_id=1, source_target_pairs={{12,4},{13,5},{14,6},{15,7},{0,8},{1,9},{2,10},{3,11},{20,12},{21,... | collective-permute-start | bytes 1179656 | tf_op jit(solution)/shard_map/ppermute | solution.py:505
  34.1 3.5 %collective-permute-start.8 = (f32[512,128]{1,0:T(8,128)S(1)}, f32[512,128]{1,0:T(8,128)S(1)}, u32[]{:S(2)}, u32[]{:S(2)}) collective-permute-start(f32[512,128]{1,0:T(8,128)S(1)} %get-tuple-element.90.refs_7_), channel_id=1, source_target_pairs={{12,4},{13,5},{14,6},{15,7},{0,8},{1,9},{2,10},{3,11},{20,12},{21,... | collective-permute-start | bytes 786440 | tf_op jit(solution)/shard_map/ppermute | solution.py:505
  37.5 1.6 %shard_map.56 = (f32[128,128]{1,0:T(8,128)S(1)}, f32[128,128]{1,0:T(8,128)S(1)}) custom-call(s32[16]{0:T(128)S(1)} %constant_dynamic-update-slice_fusion.f, f32[256,256]{1,0:T(8,128)S(1)} %get-tuple-element.93.gram_ref, f32[256,256]{1,0:T(8,128)S(1)} %get-tuple-element.79.refs_0_.rotation_ref), custom_call_target="tpu_custom_call" | custom-call | tf_op jit(solution)/shard_map/pallas_call | solution.py:52
  40.7 6.6 %collective-permute-done.8.refs_8_ = f32[512,128]{1,0:T(8,128)S(1)} collective-permute-done((f32[512,128]{1,0:T(8,128)S(1)}, f32[512,128]{1,0:T(8,128)S(1)}, u32[]{:S(2)}, u32[]{:S(2)}) %collective-permute-start.8) | collective-permute-done | bytes 262176 | tf_op jit(solution)/shard_map/ppermute | solution.py:505
  47.4 1.9 %shard_map.55 = (f32[128,128]{1,0:T(8,128)S(1)}, f32[128,128]{1,0:T(8,128)S(1)}, f32[1280,128]{1,0:T(8,128)S(1)}, f32[1280,128]{1,0:T(8,128)S(1)}, f32[1280,128]{1,0:T(8,128)S(1)}, /*index=5*/f32[1280,128]{1,0:T(8,128)S(1)}) custom-call(s32[16]{0:T(128)S(1)} %constant_dynamic-update-slice_fusion.f, f32[1280,128]{1,0:T(8,128)S(1)} %get-tuple-element.80.refs_0_, ...), custom_call_target="tpu_custom_call" | custom-call | tf_op jit(solution)/shard_map/pallas_call | solution.py:52
  50.6 3.2 %collective-permute-start.14 = (f32[128,128]{1,0:T(8,128)S(1)}, f32[128,128]{1,0:T(8,128)S(1)}, u32[]{:S(2)}, u32[]{:S(2)}) collective-permute-start(f32[128,128]{1,0:T(8,128)S(1)} %add.35.refs_0_), channel_id=1, source_target_pairs={{6,0},{7,1},{4,2},{5,3},{2,4},{3,5},{0,6},{1,7},{14,8},{15,9},{12,... | collective-permute-start | bytes 196616 | tf_op jit(solution)/shard_map/ppermute | solution.py:505
  54.4 1.8 %collective-permute-done.14.refs_3_ = f32[128,128]{1,0:T(8,128)S(1)} collective-permute-done((f32[128,128]{1,0:T(8,128)S(1)}, f32[128,128]{1,0:T(8,128)S(1)}, u32[]{:S(2)}, u32[]{:S(2)}) %collective-permute-start.14) | collective-permute-done | bytes 65568 | tf_op jit(solution)/shard_map/ppermute | solution.py:505
  56.2 1.9 %collective-permute-done.13.refs_2_ = f32[128,128]{1,0:T(8,128)S(1)} collective-permute-done((f32[128,128]{1,0:T(8,128)S(1)}, f32[128,128]{1,0:T(8,128)S(1)}, u32[]{:S(2)}, u32[]{:S(2)}) %collective-permute-start.13) | collective-permute-done | bytes 65568 | tf_op jit(solution)/shard_map/ppermute | solution.py:505
  58.0 3.4 %shard_map.57 = (f32[256,256]{1,0:T(8,128)S(1)}, f32[256,256]{1,0:T(8,128)S(1)}) custom-call(s32[16]{0:T(128)S(1)} %constant_dynamic-update-slice_fusion.f, f32[128,128]{1,0:T(8,128)S(1)} %add.35.refs_0_, f32[128,128]{1,0:T(8,128)S(1)} %collective-permute-done.12.refs_1_, f32[128,128]{1,0:T(8,128)S(1)} %collective-permute-done.13.refs_2_, ...), custom_call_target="tpu_custom_call" | custom-call | tf_op jit(solution)/shard_map/pallas_call | solution.py:52
  65.5 4.9 %collective-permute-start.17 = (f32[1280,128]{1,0:T(8,128)S(1)}, f32[1280,128]{1,0:T(8,128)S(1)}, u32[]{:S(2)}, u32[]{:S(2)}) collective-permute-start(f32[1280,128]{1,0:T(8,128)S(1)} %get-tuple-element.107.refs_4_), channel_id=1, source_target_pairs={{9,1},{11,3},{13,5},{15,7},{0,8},{17,9},{2,10},{19,11},{4,12},{21,... | collective-permute-start | bytes 1966088 | tf_op jit(solution)/shard_map/ppermute | solution.py:505
  72.8 3.4 %collective-permute-start.19 = (f32[128,128]{1,0:T(8,128)S(1)}, f32[128,128]{1,0:T(8,128)S(1)}, u32[]{:S(2)}, u32[]{:S(2)}) collective-permute-start(f32[128,128]{1,0:T(8,128)S(1)} %get-tuple-element.112), channel_id=1, source_target_pairs={{1,0},{0,1},{3,2},{2,3},{5,4},{4,5},{7,6},{6,7},{9,8},{8,9},{11,10... | collective-permute-start | bytes 196616 | tf_op jit(solution)/shard_map/ppermute | solution.py:505
  76.2 1.7 %collective-permute-done.15.refs_2_ = f32[1280,128]{1,0:T(8,128)S(1)} collective-permute-done((f32[1280,128]{1,0:T(8,128)S(1)}, f32[1280,128]{1,0:T(8,128)S(1)}, u32[]{:S(2)}, u32[]{:S(2)}) %collective-permute-start.15) | collective-permute-done | bytes 655392 | tf_op jit(solution)/shard_map/ppermute | solution.py:505
  77.9 4.5 %collective-permute-done.17.refs_5_ = f32[1280,128]{1,0:T(8,128)S(1)} collective-permute-done((f32[1280,128]{1,0:T(8,128)S(1)}, f32[1280,128]{1,0:T(8,128)S(1)}, u32[]{:S(2)}, u32[]{:S(2)}) %collective-permute-start.17) | collective-permute-done | bytes 655392 | tf_op jit(solution)/shard_map/ppermute | solution.py:505
  82.4 1.9 %shard_map.60 = (f32[128,128]{1,0:T(8,128)S(1)}, f32[128,128]{1,0:T(8,128)S(1)}, f32[1280,128]{1,0:T(8,128)S(1)}, f32[1280,128]{1,0:T(8,128)S(1)}, f32[1280,128]{1,0:T(8,128)S(1)}, /*index=5*/f32[1280,128]{1,0:T(8,128)S(1)}) custom-call(s32[16]{0:T(128)S(1)} %constant_dynamic-update-slice_fusion.f, f32[1280,128]{1,0:T(8,128)S(1)} %get-tuple-element.104.refs_0_, ...), custom_call_target="tpu_custom_call" | custom-call | tf_op jit(solution)/shard_map/pallas_call | solution.py:52
  86.0 1.9 %collective-permute-start.23 = (f32[128,128]{1,0:T(8,128)S(1)}, f32[128,128]{1,0:T(8,128)S(1)}, u32[]{:S(2)}, u32[]{:S(2)}) collective-permute-start(f32[128,128]{1,0:T(8,128)S(1)} %add.36.refs_0_), channel_id=1, source_target_pairs={{6,0},{7,1},{4,2},{5,3},{2,4},{3,5},{0,6},{1,7},{14,8},{15,9},{12,... | collective-permute-start | bytes 196616 | tf_op jit(solution)/shard_map/ppermute | solution.py:505
  89.6 1.8 %collective-permute-done.23.refs_3_ = f32[128,128]{1,0:T(8,128)S(1)} collective-permute-done((f32[128,128]{1,0:T(8,128)S(1)}, f32[128,128]{1,0:T(8,128)S(1)}, u32[]{:S(2)}, u32[]{:S(2)}) %collective-permute-start.23) | collective-permute-done | bytes 65568 | tf_op jit(solution)/shard_map/ppermute | solution.py:505
  92.7 3.0 %shard_map.62 = (f32[256,256]{1,0:T(8,128)S(1)}, f32[256,256]{1,0:T(8,128)S(1)}) custom-call(s32[16]{0:T(128)S(1)} %constant_dynamic-update-slice_fusion.f, f32[128,128]{1,0:T(8,128)S(1)} %add.36.refs_0_, f32[128,128]{1,0:T(8,128)S(1)} %collective-permute-done.21.refs_1_, f32[128,128]{1,0:T(8,128)S(1)} %collective-permute-done.22.refs_2_, ...), custom_call_target="tpu_custom_call" | custom-call | tf_op jit(solution)/shard_map/pallas_call | solution.py:52
  99.7 4.6 %collective-permute-start.26 = (f32[1280,128]{1,0:T(8,128)S(1)}, f32[1280,128]{1,0:T(8,128)S(1)}, u32[]{:S(2)}, u32[]{:S(2)}) collective-permute-start(f32[1280,128]{1,0:T(8,128)S(1)} %get-tuple-element.123.refs_2_.refs_4_), channel_id=1, source_target_pairs={{9,1},{11,3},{13,5},{15,7},{0,8},{17,9},{2,10},{19,11},{4,12},{21,... | collective-permute-start | bytes 1966088 | tf_op jit(solution)/shard_map/ppermute | solution.py:505
  104.3 1.7 %collective-permute-start.29 = (f32[1280,128]{1,0:T(8,128)S(1)}, f32[1280,128]{1,0:T(8,128)S(1)}, u32[]{:S(2)}, u32[]{:S(2)}) collective-permute-start(f32[1280,128]{1,0:T(8,128)S(1)} %get-tuple-element.132), channel_id=1, source_target_pairs={{4,0},{5,1},{6,2},{7,3},{0,4},{1,5},{2,6},{3,7},{12,8},{13,9},{14,... | collective-permute-start | bytes 1966088 | tf_op jit(solution)/shard_map/ppermute | solution.py:505
  108.3 3.0 %collective-permute-start.28 = (f32[128,128]{1,0:T(8,128)S(1)}, f32[128,128]{1,0:T(8,128)S(1)}, u32[]{:S(2)}, u32[]{:S(2)}) collective-permute-start(f32[128,128]{1,0:T(8,128)S(1)} %get-tuple-element.126), channel_id=1, source_target_pairs={{1,0},{0,1},{3,2},{2,3},{5,4},{4,5},{7,6},{6,7},{9,8},{8,9},{11,10... | collective-permute-start | bytes 196616 | tf_op jit(solution)/shard_map/ppermute | solution.py:505
  112.1 4.3 %collective-permute-done.26.refs_3_.refs_5_ = f32[1280,128]{1,0:T(8,128)S(1)} collective-permute-done((f32[1280,128]{1,0:T(8,128)S(1)}, f32[1280,128]{1,0:T(8,128)S(1)}, u32[]{:S(2)}, u32[]{:S(2)}) %collective-permute-start.26) | collective-permute-done | bytes 655392 | tf_op jit(solution)/shard_map/ppermute | solution.py:505
  118.3 1.9 %shard_map.67 = (f32[128,128]{1,0:T(8,128)S(1)}, f32[128,128]{1,0:T(8,128)S(1)}, f32[1280,128]{1,0:T(8,128)S(1)}, f32[1280,128]{1,0:T(8,128)S(1)}, f32[1280,128]{1,0:T(8,128)S(1)}, /*index=5*/f32[1280,128]{1,0:T(8,128)S(1)}) custom-call(s32[16]{0:T(128)S(1)} %constant_dynamic-update-slice_fusion.f, f32[1280,128]{1,0:T(8,128)S(1)} %get-tuple-element.121.refs_4_.refs_0_, ...), custom_call_target="tpu_custom_call" | custom-call | tf_op jit(solution)/shard_map/pallas_call | solution.py:52
  126.5 3.2 %collective-permute-done.33.refs_3_ = f32[128,128]{1,0:T(8,128)S(1)} collective-permute-done((f32[128,128]{1,0:T(8,128)S(1)}, f32[128,128]{1,0:T(8,128)S(1)}, u32[]{:S(2)}, u32[]{:S(2)}) %collective-permute-start.33) | collective-permute-done | bytes 65568 | tf_op jit(solution)/shard_map/ppermute | solution.py:505
  131.3 3.3 %shard_map.69 = (f32[256,256]{1,0:T(8,128)S(1)}, f32[256,256]{1,0:T(8,128)S(1)}) custom-call(s32[16]{0:T(128)S(1)} %constant_dynamic-update-slice_fusion.f, f32[128,128]{1,0:T(8,128)S(1)} %add.37.refs_0_, f32[128,128]{1,0:T(8,128)S(1)} %collective-permute-done.31.refs_1_, f32[128,128]{1,0:T(8,128)S(1)} %collective-permute-done.32.refs_2_, ...), custom_call_target="tpu_custom_call" | custom-call | tf_op jit(solution)/shard_map/pallas_call | solution.py:52
  137.0 3.1 %shard_map.71 = (f32[2048,256]{1,0:T(8,128)}, f32[512,256]{1,0:T(8,128)}, f32[1,256]{1,0:T(1,128)}) custom-call(s32[16]{0:T(128)S(1)} %constant_dynamic-update-slice_fusion.f, f32[256,256]{1,0:T(8,128)S(1)} %get-tuple-element.143.rotation_ref.own_ref, f32[256,256]{1,0:T(8,128)S(1)} %collective-permute-done.35.other_ref, ...), custom_call_target="tpu_custom_call" | custom-call | flops 1 | bytes 1 | tf_op jit(solution)/shard_map/pallas_call | solution.py:404
  140.1 1.9 %shard_map.72 = (f32[2048,256]{1,0:T(8,128)}, f32[512,256]{1,0:T(8,128)}) custom-call(s32[16]{0:T(128)S(1)} %constant_dynamic-update-slice_fusion.f, f32[256,256]{1,0:T(8,128)S(1)} %get-tuple-element.143.rotation_ref.own_ref, f32[256,256]{1,0:T(8,128)S(1)} %collective-permute-done.35.other_ref, ...), custom_call_target="tpu_custom_call", output_to_operand_aliasing={{0}: (5, {}), {1}: (6, {})} | custom-call | flops 1 | bytes 1 | tf_op jit(solution)/shard_map/pallas_call | solution.py:404
  (80 shorter events, 43.2 us)
Async XLA Ops:
  3.1 25.5 %collective-permute-start.5 = (f32[768,256]{1,0:T(8,128)}, f32[768,256]{1,0:T(8,128)S(1)}, u32[]{:S(2)}, u32[]{:S(2)}) collective-permute-start(f32[768,256]{1,0:T(8,128)} %get-tuple-element.85), channel_id=1, source_target_pairs={{4,0},{5,1},{6,2},{7,3},{0,4},{1,5},{2,6},{3,7},{12,8},{13,9},{14,... | collective-permute-start | bytes 2359304 | tf_op jit(solution)/shard_map/ppermute | solution.py:505
  9.8 7.0 %collective-permute-start.1 = (f32[384,128]{1,0:T(8,128)S(1)}, f32[384,128]{1,0:T(8,128)S(1)}, u32[]{:S(2)}, u32[]{:S(2)}) collective-permute-start(f32[384,128]{1,0:T(8,128)S(1)} %add.34.own_ref), channel_id=1, source_target_pairs={{2,0},{3,1},{0,2},{1,3},{6,4},{7,5},{4,6},{5,7},{10,8},{11,9},{8,1... | collective-permute-start | bytes 589832 | tf_op jit(solution)/shard_map/ppermute | solution.py:505
  20.3 6.9 %collective-permute-start.3 = (f32[128,256]{1,0:T(8,128)S(1)}, f32[128,256]{1,0:T(8,128)S(1)}, u32[]{:S(2)}, u32[]{:S(2)}) collective-permute-start(f32[128,256]{1,0:T(8,128)S(1)} %get-tuple-element.84), channel_id=1, source_target_pairs={{4,0},{5,1},{6,2},{7,3},{0,4},{1,5},{2,6},{3,7},{12,8},{13,9},{14,... | collective-permute-start | bytes 393224 | tf_op jit(solution)/shard_map/ppermute | solution.py:505
  21.9 25.5 %collective-permute-start.2 = (f32[1280,128]{1,0:T(8,128)S(1)}, f32[1280,128]{1,0:T(8,128)S(1)}, u32[]{:S(2)}, u32[]{:S(2)}) collective-permute-start(f32[1280,128]{1,0:T(8,128)S(1)} %get-tuple-element.83.refs_1_), channel_id=1, source_target_pairs={{8,0},{9,1},{10,2},{11,3},{16,8},{17,9},{18,10},{19,11},{4,12},{5,... | collective-permute-start | bytes 1966088 | tf_op jit(solution)/shard_map/ppermute | solution.py:505
  23.2 9.9 %collective-permute-start.7 = (f32[256,256]{1,0:T(8,128)S(1)}, f32[256,256]{1,0:T(8,128)S(1)}, u32[]{:S(2)}, u32[]{:S(2)}) collective-permute-start(f32[256,256]{1,0:T(8,128)S(1)} %copy-done.1), channel_id=1, source_target_pairs={{4,0},{5,1},{6,2},{7,3},{0,4},{1,5},{2,6},{3,7},{12,8},{13,9},{14,... | collective-permute-start | bytes 786440 | tf_op jit(solution)/shard_map/ppermute | solution.py:505
  29.6 17.7 %collective-permute-start.6 = (f32[768,128]{1,0:T(8,128)S(1)}, f32[768,128]{1,0:T(8,128)S(1)}, u32[]{:S(2)}, u32[]{:S(2)}) collective-permute-start(f32[768,128]{1,0:T(8,128)S(1)} %get-tuple-element.87.refs_4_), channel_id=1, source_target_pairs={{12,4},{13,5},{14,6},{15,7},{0,8},{1,9},{2,10},{3,11},{20,12},{21,... | collective-permute-start | bytes 1179656 | tf_op jit(solution)/shard_map/ppermute | solution.py:505
  34.1 13.3 %collective-permute-start.8 = (f32[512,128]{1,0:T(8,128)S(1)}, f32[512,128]{1,0:T(8,128)S(1)}, u32[]{:S(2)}, u32[]{:S(2)}) collective-permute-start(f32[512,128]{1,0:T(8,128)S(1)} %get-tuple-element.90.refs_7_), channel_id=1, source_target_pairs={{12,4},{13,5},{14,6},{15,7},{0,8},{1,9},{2,10},{3,11},{20,12},{21,... | collective-permute-start | bytes 786440 | tf_op jit(solution)/shard_map/ppermute | solution.py:505
  39.2 10.0 %collective-permute-start.9 = (f32[128,128]{1,0:T(8,128)S(1)}, f32[128,128]{1,0:T(8,128)S(1)}, u32[]{:S(2)}, u32[]{:S(2)}) collective-permute-start(f32[128,128]{1,0:T(8,128)S(1)} %get-tuple-element.94), channel_id=1, source_target_pairs={{0,0},{8,1},{2,2},{10,3},{1,4},{9,5},{3,6},{11,7},{4,8},{16,9},{6,... | collective-permute-start | bytes 196616 | tf_op jit(solution)/shard_map/ppermute | solution.py:505
  39.8 9.4 %collective-permute-start.10 = (f32[128,128]{1,0:T(8,128)S(1)}, f32[128,128]{1,0:T(8,128)S(1)}, u32[]{:S(2)}, u32[]{:S(2)}) collective-permute-start(f32[128,128]{1,0:T(8,128)S(1)} %get-tuple-element.95), channel_id=1, source_target_pairs={{4,0},{0,1},{6,2},{2,3},{5,4},{1,5},{7,6},{3,7},{12,8},{8,9},{14,1... | collective-permute-start | bytes 196616 | tf_op jit(solution)/shard_map/ppermute | solution.py:505
  50.6 5.6 %collective-permute-start.14 = (f32[128,128]{1,0:T(8,128)S(1)}, f32[128,128]{1,0:T(8,128)S(1)}, u32[]{:S(2)}, u32[]{:S(2)}) collective-permute-start(f32[128,128]{1,0:T(8,128)S(1)} %add.35.refs_0_), channel_id=1, source_target_pairs={{6,0},{7,1},{4,2},{5,3},{2,4},{3,5},{0,6},{1,7},{14,8},{15,9},{12,... | collective-permute-start | bytes 196616 | tf_op jit(solution)/shard_map/ppermute | solution.py:505
  53.7 4.3 %collective-permute-start.13 = (f32[128,128]{1,0:T(8,128)S(1)}, f32[128,128]{1,0:T(8,128)S(1)}, u32[]{:S(2)}, u32[]{:S(2)}) collective-permute-start(f32[128,128]{1,0:T(8,128)S(1)} %add.35.refs_0_), channel_id=1, source_target_pairs={{4,0},{5,1},{6,2},{7,3},{0,4},{1,5},{2,6},{3,7},{12,8},{13,9},{14,... | collective-permute-start | bytes 196616 | tf_op jit(solution)/shard_map/ppermute | solution.py:505
  53.7 4.3 %collective-permute-start.12 = (f32[128,128]{1,0:T(8,128)S(1)}, f32[128,128]{1,0:T(8,128)S(1)}, u32[]{:S(2)}, u32[]{:S(2)}) collective-permute-start(f32[128,128]{1,0:T(8,128)S(1)} %add.35.refs_0_), channel_id=1, source_target_pairs={{2,0},{3,1},{0,2},{1,3},{6,4},{7,5},{4,6},{5,7},{10,8},{11,9},{8,1... | collective-permute-start | bytes 196616 | tf_op jit(solution)/shard_map/ppermute | solution.py:505
  61.4 2.8 %collective-permute-start.16 = (f32[256,256]{1,0:T(8,128)S(1)}, f32[256,256]{1,0:T(8,128)S(1)}, u32[]{:S(2)}, u32[]{:S(2)}) collective-permute-start(f32[256,256]{1,0:T(8,128)S(1)} %get-tuple-element.99.rotation_ref), channel_id=1, source_target_pairs={{1,0},{0,1},{3,2},{2,3},{5,4},{4,5},{7,6},{6,7},{9,8},{8,9},{11,10... | collective-permute-start | bytes 786440 | tf_op jit(solution)/shard_map/ppermute | solution.py:505
  62.8 15.1 %collective-permute-start.15 = (f32[1280,128]{1,0:T(8,128)S(1)}, f32[1280,128]{1,0:T(8,128)S(1)}, u32[]{:S(2)}, u32[]{:S(2)}) collective-permute-start(f32[1280,128]{1,0:T(8,128)S(1)} %get-tuple-element.105.refs_1_), channel_id=1, source_target_pairs={{8,0},{10,2},{12,4},{14,6},{16,8},{1,9},{18,10},{3,11},{20,12},{5,... | collective-permute-start | bytes 1966088 | tf_op jit(solution)/shard_map/ppermute | solution.py:505
  65.5 16.9 %collective-permute-start.17 = (f32[1280,128]{1,0:T(8,128)S(1)}, f32[1280,128]{1,0:T(8,128)S(1)}, u32[]{:S(2)}, u32[]{:S(2)}) collective-permute-start(f32[1280,128]{1,0:T(8,128)S(1)} %get-tuple-element.107.refs_4_), channel_id=1, source_target_pairs={{9,1},{11,3},{13,5},{15,7},{0,8},{17,9},{2,10},{19,11},{4,12},{21,... | collective-permute-start | bytes 1966088 | tf_op jit(solution)/shard_map/ppermute | solution.py:505
  72.1 12.1 %collective-permute-start.18 = (f32[128,128]{1,0:T(8,128)S(1)}, f32[128,128]{1,0:T(8,128)S(1)}, u32[]{:S(2)}, u32[]{:S(2)}) collective-permute-start(f32[128,128]{1,0:T(8,128)S(1)} %get-tuple-element.111), channel_id=1, source_target_pairs={{0,0},{8,1},{2,2},{10,3},{4,4},{12,5},{6,6},{14,7},{1,8},{16,9},{3... | collective-permute-start | bytes 196616 | tf_op jit(solution)/shard_map/ppermute | solution.py:505
  72.8 11.5 %collective-permute-start.19 = (f32[128,128]{1,0:T(8,128)S(1)}, f32[128,128]{1,0:T(8,128)S(1)}, u32[]{:S(2)}, u32[]{:S(2)}) collective-permute-start(f32[128,128]{1,0:T(8,128)S(1)} %get-tuple-element.112), channel_id=1, source_target_pairs={{1,0},{0,1},{3,2},{2,3},{5,4},{4,5},{7,6},{6,7},{9,8},{8,9},{11,10... | collective-permute-start | bytes 196616 | tf_op jit(solution)/shard_map/ppermute | solution.py:505
  86.0 5.4 %collective-permute-start.23 = (f32[128,128]{1,0:T(8,128)S(1)}, f32[128,128]{1,0:T(8,128)S(1)}, u32[]{:S(2)}, u32[]{:S(2)}) collective-permute-start(f32[128,128]{1,0:T(8,128)S(1)} %add.36.refs_0_), channel_id=1, source_target_pairs={{6,0},{7,1},{4,2},{5,3},{2,4},{3,5},{0,6},{1,7},{14,8},{15,9},{12,... | collective-permute-start | bytes 196616 | tf_op jit(solution)/shard_map/ppermute | solution.py:505
  87.9 4.3 %collective-permute-start.22 = (f32[128,128]{1,0:T(8,128)S(1)}, f32[128,128]{1,0:T(8,128)S(1)}, u32[]{:S(2)}, u32[]{:S(2)}) collective-permute-start(f32[128,128]{1,0:T(8,128)S(1)} %add.36.refs_0_), channel_id=1, source_target_pairs={{4,0},{5,1},{6,2},{7,3},{0,4},{1,5},{2,6},{3,7},{12,8},{13,9},{14,... | collective-permute-start | bytes 196616 | tf_op jit(solution)/shard_map/ppermute | solution.py:505
  88.3 4.5 %collective-permute-start.21 = (f32[128,128]{1,0:T(8,128)S(1)}, f32[128,128]{1,0:T(8,128)S(1)}, u32[]{:S(2)}, u32[]{:S(2)}) collective-permute-start(f32[128,128]{1,0:T(8,128)S(1)} %add.36.refs_0_), channel_id=1, source_target_pairs={{2,0},{3,1},{0,2},{1,3},{6,4},{7,5},{4,6},{5,7},{10,8},{11,9},{8,1... | collective-permute-start | bytes 196616 | tf_op jit(solution)/shard_map/ppermute | solution.py:505
  95.8 2.6 %collective-permute-start.25 = (f32[256,256]{1,0:T(8,128)S(1)}, f32[256,256]{1,0:T(8,128)S(1)}, u32[]{:S(2)}, u32[]{:S(2)}) collective-permute-start(f32[256,256]{1,0:T(8,128)S(1)} %get-tuple-element.116.rotation_ref), channel_id=1, source_target_pairs={{1,0},{0,1},{3,2},{2,3},{5,4},{4,5},{7,6},{6,7},{9,8},{8,9},{11,10... | collective-permute-start | bytes 786440 | tf_op jit(solution)/shard_map/ppermute | solution.py:505
  97.1 14.9 %collective-permute-start.24 = (f32[1280,128]{1,0:T(8,128)S(1)}, f32[1280,128]{1,0:T(8,128)S(1)}, u32[]{:S(2)}, u32[]{:S(2)}) collective-permute-start(f32[1280,128]{1,0:T(8,128)S(1)} %get-tuple-element.122.refs_0_.refs_1_), channel_id=1, source_target_pairs={{8,0},{10,2},{12,4},{14,6},{16,8},{1,9},{18,10},{3,11},{20,12},{5,... | collective-permute-start | bytes 1966088 | tf_op jit(solution)/shard_map/ppermute | solution.py:505
  99.7 16.7 %collective-permute-start.26 = (f32[1280,128]{1,0:T(8,128)S(1)}, f32[1280,128]{1,0:T(8,128)S(1)}, u32[]{:S(2)}, u32[]{:S(2)}) collective-permute-start(f32[1280,128]{1,0:T(8,128)S(1)} %get-tuple-element.123.refs_2_.refs_4_), channel_id=1, source_target_pairs={{9,1},{11,3},{13,5},{15,7},{0,8},{17,9},{2,10},{19,11},{4,12},{21,... | collective-permute-start | bytes 1966088 | tf_op jit(solution)/shard_map/ppermute | solution.py:505
  104.3 16.3 %collective-permute-start.29 = (f32[1280,128]{1,0:T(8,128)S(1)}, f32[1280,128]{1,0:T(8,128)S(1)}, u32[]{:S(2)}, u32[]{:S(2)}) collective-permute-start(f32[1280,128]{1,0:T(8,128)S(1)} %get-tuple-element.132), channel_id=1, source_target_pairs={{4,0},{5,1},{6,2},{7,3},{0,4},{1,5},{2,6},{3,7},{12,8},{13,9},{14,... | collective-permute-start | bytes 1966088 | tf_op jit(solution)/shard_map/ppermute | solution.py:505
  107.7 9.3 %collective-permute-start.27 = (f32[128,128]{1,0:T(8,128)S(1)}, f32[128,128]{1,0:T(8,128)S(1)}, u32[]{:S(2)}, u32[]{:S(2)}) collective-permute-start(f32[128,128]{1,0:T(8,128)S(1)} %get-tuple-element.125), channel_id=1, source_target_pairs={{0,0},{8,1},{2,2},{10,3},{4,4},{12,5},{6,6},{14,7},{1,8},{16,9},{3... | collective-permute-start | bytes 196616 | tf_op jit(solution)/shard_map/ppermute | solution.py:505
  108.3 8.6 %collective-permute-start.28 = (f32[128,128]{1,0:T(8,128)S(1)}, f32[128,128]{1,0:T(8,128)S(1)}, u32[]{:S(2)}, u32[]{:S(2)}) collective-permute-start(f32[128,128]{1,0:T(8,128)S(1)} %get-tuple-element.126), channel_id=1, source_target_pairs={{1,0},{0,1},{3,2},{2,3},{5,4},{4,5},{7,6},{6,7},{9,8},{8,9},{11,10... | collective-permute-start | bytes 196616 | tf_op jit(solution)/shard_map/ppermute | solution.py:505
  117.0 13.4 %collective-permute-start.34 = (f32[640,128]{1,0:T(8,128)S(1)}, f32[640,128]{1,0:T(8,128)S(1)}, u32[]{:S(2)}, u32[]{:S(2)}) collective-permute-start(f32[640,128]{1,0:T(8,128)S(1)} %shard_map.65), channel_id=1, source_target_pairs={{4,0},{5,1},{6,2},{7,3},{0,4},{1,5},{2,6},{3,7},{12,8},{13,9},{14,... | collective-permute-start | bytes 983048 | tf_op jit(solution)/shard_map/ppermute | solution.py:505
  122.4 7.3 %collective-permute-start.33 = (f32[128,128]{1,0:T(8,128)S(1)}, f32[128,128]{1,0:T(8,128)S(1)}, u32[]{:S(2)}, u32[]{:S(2)}) collective-permute-start(f32[128,128]{1,0:T(8,128)S(1)} %add.37.refs_0_), channel_id=1, source_target_pairs={{6,0},{7,1},{4,2},{5,3},{2,4},{3,5},{0,6},{1,7},{14,8},{15,9},{12,... | collective-permute-start | bytes 196616 | tf_op jit(solution)/shard_map/ppermute | solution.py:505
  123.7 6.6 %collective-permute-start.32 = (f32[128,128]{1,0:T(8,128)S(1)}, f32[128,128]{1,0:T(8,128)S(1)}, u32[]{:S(2)}, u32[]{:S(2)}) collective-permute-start(f32[128,128]{1,0:T(8,128)S(1)} %add.37.refs_0_), channel_id=1, source_target_pairs={{4,0},{5,1},{6,2},{7,3},{0,4},{1,5},{2,6},{3,7},{12,8},{13,9},{14,... | collective-permute-start | bytes 196616 | tf_op jit(solution)/shard_map/ppermute | solution.py:505
  125.0 5.4 %collective-permute-start.31 = (f32[128,128]{1,0:T(8,128)S(1)}, f32[128,128]{1,0:T(8,128)S(1)}, u32[]{:S(2)}, u32[]{:S(2)}) collective-permute-start(f32[128,128]{1,0:T(8,128)S(1)} %add.37.refs_0_), channel_id=1, source_target_pairs={{2,0},{3,1},{0,2},{1,3},{6,4},{7,5},{4,6},{5,7},{10,8},{11,9},{8,1... | collective-permute-start | bytes 196616 | tf_op jit(solution)/shard_map/ppermute | solution.py:505
  130.4 9.7 %collective-permute-start.36 = (f32[640,128]{1,0:T(8,128)S(1)}, f32[640,128]{1,0:T(8,128)S(1)}, u32[]{:S(2)}, u32[]{:S(2)}) collective-permute-start(f32[640,128]{1,0:T(8,128)S(1)} %shard_map.68), channel_id=1, source_target_pairs={{4,0},{5,1},{6,2},{7,3},{0,4},{1,5},{2,6},{3,7},{12,8},{13,9},{14,... | collective-permute-start | bytes 983048 | tf_op jit(solution)/shard_map/ppermute | solution.py:505
  134.6 2.4 %collective-permute-start.35 = (f32[256,256]{1,0:T(8,128)S(1)}, f32[256,256]{1,0:T(8,128)S(1)}, u32[]{:S(2)}, u32[]{:S(2)}) collective-permute-start(f32[256,256]{1,0:T(8,128)S(1)} %get-tuple-element.143.rotation_ref.own_ref), channel_id=1, source_target_pairs={{1,0},{0,1},{3,2},{2,3},{5,4},{4,5},{7,6},{6,7},{9,8},{8,9},{11,10... | collective-permute-start | bytes 786440 | tf_op jit(solution)/shard_map/ppermute | solution.py:505
  (9 other events, 40.3 us)
